TPU v7x, 32 devices: a whole 2x2x4 slice. The times are simulated.
32 devices in a mesh: groups: 2 (over y), tok: 4 (over z), mod: 2 (over x), fsdp: 2 (over core).
Axes of the slice: x: 2, y: 2, z: 4, core: 2. Of those that a mesh axis runs over, the one named last changes fastest.
Arguments:
- residual: bfloat16 [1024, 4096], P(('groups', 'tok'), ('fsdp', 'mod')), parts along dimension 0, may hold values from -30 to 30
- context: bfloat16 [1024, 4096], P(('groups', 'tok'), ('mod', 'fsdp')), parts along dimension 0, may hold values from -6 to 6
- out_proj: bfloat16 [4096, 4096], P('tok', ('fsdp', 'mod')), may hold values from -0.09375 to 0.09375
- norm_gain: bfloat16 [2, 4096], P(None, ('fsdp', 'mod')), may hold values from 0.099609375 to 1.8984375
- router_weight: bfloat16 [4096, 4], P(('fsdp', 'mod')), may hold values from -0.25 to 0.25
- block_modality: int32 [8], P(('groups', 'tok')), parts along dimension 0, may hold values from 0 to 1, as said below
- expert_rows: int32 [4, 128], P(None, ('groups', 'tok')), parts along dimension 1, may hold values from -1 to 127, as said below
- gate_weight: bfloat16 [4, 4096, 11008], P('mod', 'fsdp', 'tok'), may hold values from -0.09375 to 0.09375
- up_weight: bfloat16 [4, 4096, 11008], P('mod', 'fsdp', 'tok'), may hold values from -0.09375 to 0.09375
- down_weight: bfloat16 [4, 11008, 4096], P('mod', 'tok', 'fsdp'), may hold values from -0.0546875 to 0.0546875
Outputs:
- expert_out: bfloat16 [1024, 4096], P(('groups', 'tok'), ('fsdp', 'mod')), parts along dimension 0
There are 2 independent parts, one for each index of `groups`. A program takes and returns all parts, laid end to end along the dimension named above; an argument that names none is the same for every part. Nothing has to cross between parts.
Inputs may be any that keep to these rules, and one draw needn't show every extreme that they name: `block_modality`: both modalities occur in every window. `expert_rows`: slot s = t * 16 + j of expert e names a row among tokens t * 128 to (t + 1) * 128 - 1, or is -1 if unused. Experts below 2 take only text tokens, the others only image tokens; no expert takes a token twice; in each aligned block of 16 slots the used ones come first; every expert fills all 16 slots of at least one index of tok whose tokens have the expert's modality.
All inputs are finite; a program needn't handle non-finite values.
Results may differ from a plain program's by a relative error of at most 0.02.
Values may be sent and summed in bfloat16 or wider, within the bound.
No kernel may reach another device: no remote copies, remote signals or barrier semaphores. Data moves between devices by JAX's collectives and lax.ppermute only.
A program may use at most 192 MiB of HBM per device.

v0:
```python
import jax
import jax.numpy as jnp
from jax import lax
from jax.sharding import PartitionSpec as P

D = 4096
BLOCK = 128


def local(
    residual,
    context,
    out_proj,
    norm_gain,
    router_weight,
    block_modality,
    expert_rows,
    gate_weight,
    up_weight,
    down_weight,
):
    full_context = lax.all_gather(context, ("mod", "fsdp"), axis=1, tiled=True)
    token_count = residual.shape[0]
    projected = jnp.dot(
        full_context,
        lax.all_gather(out_proj, "tok", axis=0, tiled=True),
        preferred_element_type=jnp.float32,
    )
    hidden = residual.astype(jnp.float32) + projected
    token_mod = jnp.repeat(block_modality, BLOCK)
    gain_table = norm_gain.astype(jnp.float32)
    token_gain = jnp.where(token_mod[:, None] == 0, gain_table[0][None, :], gain_table[1][None, :])
    gained = hidden * token_gain
    router_table = router_weight.astype(jnp.float32)
    squares = jnp.sum(hidden * hidden, axis=1)
    square_total = lax.psum(squares, ("mod", "fsdp"))
    inverse = lax.rsqrt(square_total / D + 1e-05)
    normed = gained * inverse[:, None]
    logits = lax.psum(
        jnp.dot(normed, router_table, precision=lax.Precision.HIGHEST), ("mod", "fsdp")
    )
    score = jax.nn.sigmoid(logits)
    normed_rows = normed.astype(jnp.bfloat16)
    local_experts = gate_weight.shape[0]
    first_expert = lax.axis_index("mod") * local_experts
    row_ids = lax.iota(jnp.int32, token_count)
    own_rows = lax.dynamic_slice_in_dim(expert_rows, first_expert, local_experts, 0)
    own_pick = (own_rows[:, :, None] == row_ids[None, None, :]).astype(jnp.bfloat16)
    half_rows = lax.all_gather(normed_rows, "mod", axis=1, tiled=True)
    chosen = jnp.einsum(
        "ecr,rd->ecd", own_pick, half_rows, preferred_element_type=jnp.float32
    ).astype(jnp.bfloat16)
    unit_count = gate_weight.shape[2]
    piece = lax.all_gather(chosen, "tok", axis=1, tiled=True)
    gate_part = jnp.einsum("esd,edf->esf", piece, gate_weight, preferred_element_type=jnp.float32)
    up_part = jnp.einsum("esd,edf->esf", piece, up_weight, preferred_element_type=jnp.float32)
    partial_in = jnp.concatenate((gate_part, up_part), axis=2)
    summed_in = lax.psum(partial_in.astype(jnp.bfloat16), "fsdp").astype(jnp.float32)
    activation = (jax.nn.silu(summed_in[:, :, :unit_count]) * summed_in[:, :, unit_count:]).astype(
        jnp.bfloat16
    )
    expert_value = lax.psum_scatter(
        jnp.einsum(
            "esf,efd->sed", activation, down_weight, preferred_element_type=jnp.float32
        ).astype(jnp.bfloat16),
        "tok",
        scatter_dimension=0,
        tiled=True,
    ).astype(jnp.float32)
    own_score = lax.dynamic_slice_in_dim(score, first_expert, local_experts, 1)
    pick_table = own_pick.astype(jnp.float32)
    slot_score = jnp.einsum("ecr,re->ce", pick_table, own_score, precision=lax.Precision.HIGHEST)
    scaled = expert_value * slot_score[:, :, None]
    mixed_rows = jnp.einsum("ecr,ced->rd", pick_table, scaled, precision=lax.Precision.HIGHEST)
    combined = lax.psum_scatter(
        mixed_rows.astype(jnp.bfloat16), "mod", scatter_dimension=1, tiled=True
    )
    return combined


def solution(mesh):
    placed = (
        P(("groups", "tok"), ("fsdp", "mod")),
        P(("groups", "tok"), ("mod", "fsdp")),
        P("tok", ("fsdp", "mod")),
        P(None, ("fsdp", "mod")),
        P(("fsdp", "mod"), None),
        P(("groups", "tok")),
        P(None, ("groups", "tok")),
        P("mod", "fsdp", "tok"),
        P("mod", "fsdp", "tok"),
        P("mod", "tok", "fsdp"),
    )
    return jax.shard_map(
        local,
        mesh=mesh,
        in_specs=placed,
        out_specs=P(("groups", "tok"), ("fsdp", "mod")),
        check_vma=False,
    )
```

profile of v0, /device:TPU:0, one launch (start us, length us, event | category | flops | bytes accessed | tf_op | source)
XLA Modules:
  0.0 316.3 jit_solution(1377281258367514044)
XLA Ops:
  6.5 0.0 copy-start
  6.5 0.0 all-gather.3.cloned.1.call-start
  6.5 0.7 all-gather.3.cloned.1.call-update
  7.3 0.0 all-gather.5.cloned.1.call-start
  7.3 0.7 all-gather.5.cloned.1.call-update
  8.0 0.0 all-reduce.2.cloned.1.call-start
  8.7 0.7 convert_element_type.35
  9.4 0.7 constant_dynamic-slice_fusion.1
  10.1 18.3 %all-gather.3.cloned.1.call-done = bf16[128,4096]{1,0:T(8,128)(2,1)} async-done(((bf16[128,1024]{1,0:T(8,128)(2,1)}), bf16[128,4096]{1,0:T(8,128)(2,1)}) %all-gather.3.cloned.1.call-update) | async-done | bytes 1048592 | tf_op jit(solution)/shard_map/all_gather | solution.py:22
  28.4 151.2 %all-gather.5.cloned.1.call-done = bf16[4096,1024]{1,0:T(8,128)(2,1)} async-done(((bf16[1024,1024]{1,0:T(8,128)(2,1)}), bf16[4096,1024]{1,0:T(8,128)(2,1)}) %all-gather.5.cloned.1.call-update) | async-done | bytes 8388624 | tf_op jit(solution)/shard_map/all_gather | solution.py:26
  179.6 5.0 %multiply_reduce_fusion = (f32[128]{0:T(128)S(1)}, f32[128,1024]{1,0:T(8,128)S(1)}) fusion(bf16[128,4096]{1,0:T(8,128)(2,1)} %all-gather.3.cloned.1.call-done, bf16[4096,1024]{1,0:T(8,128)(2,1)} %all-gather.5.cloned.1.call-done, bf16[128,1024]{1,0:T(8,128)(2,1)} %param.10), kind=kOutput, calls=%fused_computation.13 | convolution fusion | flops 1074265984 | bytes 10224128 | tf_op jit(solution)/shard_map/dot_general | solution.py:24
  184.6 6.8 %psum.21 = f32[128]{0:T(128)S(1)} all-reduce(f32[128]{0:T(128)S(1)} %get-tuple-element.5), channel_id=1, replica_groups=mesh['groups'=2,'tok'=4,'mod'=2,'fsdp'=2] {'mod','fsdp'}, use_global_device_ids=true, to_apply=%region_1.2 | all-reduce | flops 128 | bytes 1024 | tf_op jit(solution)/shard_map/psum | solution.py:36
  191.5 0.1 fusion.7
  191.6 7.6 %all_gather.14 = bf16[128,2048]{1,0:T(8,128)(2,1)S(1)} all-gather(bf16[128,1024]{1,0:T(8,128)(2,1)S(1)} %fusion.7), channel_id=1, replica_groups=mesh['groups'=2,'tok'=4,'mod'=2,'fsdp'=2] {'mod'}, dimensions={1}, use_global_device_ids=true | all-gather | bytes 786432 | tf_op jit(solution)/shard_map/all_gather | solution.py:49
  199.1 0.2 convolution_convert_fusion.3
  199.4 14.7 %all_gather.15 = bf16[2,64,2048]{2,1,0:T(8,128)(2,1)S(1)} all-gather(bf16[2,16,2048]{2,1,0:T(8,128)(2,1)S(1)} %convolution_convert_fusion.3), channel_id=1, replica_groups=mesh['groups'=2,'tok'=4,'mod'=2,'fsdp'=2] {'tok'}, dimensions={1}, use_global_device_ids=true | all-gather | bytes 655360 | tf_op jit(solution)/shard_map/all_gather | solution.py:54
  214.1 11.3 %convolution_convert_fusion = bf16[2,64,2752]{2,1,0:T(8,128)(2,1)S(1)} fusion(bf16[2,64,2048]{2,1,0:T(8,128)(2,1)S(1)} %all_gather.15, bf16[2,2048,2752]{1,2,0:T(8,128)(2,1)} %param.18), kind=kOutput, calls=%fused_computation | convolution fusion | flops 1443192832 | bytes 23773184 | tf_op jit(solution)/shard_map/esd,edf->esf/dot_general | solution.py:56
  225.4 11.3 %convolution_convert_fusion.1 = bf16[2,64,2752]{2,1,0:T(8,128)(2,1)S(1)} fusion(bf16[2,64,2048]{2,1,0:T(8,128)(2,1)S(1)} %all_gather.15, bf16[2,2048,2752]{1,2,0:T(8,128)(2,1)} %param.17), kind=kOutput, calls=%fused_computation.1 | convolution fusion | flops 1443192832 | bytes 23773184 | tf_op jit(solution)/shard_map/esd,edf->esf/dot_general | solution.py:55
  236.7 1.4 pad_maximum_fusion
  238.1 0.0 all-reduce.2.cloned.1.call-update
  238.1 0.0 reduce-scatter.3.cloned.1.call-start
  238.2 19.4 %all-reduce.2.cloned.1.call-done = bf16[2,64,5504]{2,1,0:T(8,128)(2,1)} async-done(((bf16[2,64,5504]{2,1,0:T(8,128)(2,1)}), bf16[2,64,5504]{2,1,0:T(8,128)(2,1)}) %all-reduce.2.cloned.1.call-update) | async-done | bytes 1409040 | tf_op jit(solution)/shard_map/psum | solution.py:58
  257.6 1.5 convert_element_type.38
  259.1 12.3 %fusion.1 = bf16[64,2,2048]{2,0,1:T(8,128)(2,1)} fusion(bf16[2,2752,2048]{2,1,0:T(8,128)(2,1)} %param.19, f32[2,64,5504]{2,1,0:T(8,128)S(1)} %convert_element_type.38), kind=kOutput, calls=%fused_computation.5 | convolution fusion | flops 1445216256 | bytes 25952256 | tf_op jit(solution)/shard_map/esf,efd->sed/dot_general | solution.py:63
  271.4 0.0 reduce-scatter.3.cloned.1.call-update
  271.4 0.0 reduce-scatter.5.cloned.1.call-start
  271.5 0.0 copy-done
  271.5 0.4 fusion.6
  271.9 7.3 %psum.23 = f32[128,4]{0,1:T(4,128)S(1)} all-reduce(f32[128,4]{0,1:T(4,128)S(1)} %fusion.6), channel_id=1, replica_groups=mesh['groups'=2,'tok'=4,'mod'=2,'fsdp'=2] {'mod','fsdp'}, use_global_device_ids=true, to_apply=%region_4.5 | all-reduce | flops 512 | bytes 4096 | tf_op jit(solution)/shard_map/psum | solution.py:39
  279.2 0.2 fusion.13
  279.4 15.0 %reduce-scatter.3.cloned.1.call-done = bf16[16,2,2048]{2,0,1:T(8,128)(2,1)} async-done(((bf16[64,2,2048]{2,0,1:T(8,128)(2,1)}), bf16[16,2,2048]{2,0,1:T(8,128)(2,1)}) %reduce-scatter.3.cloned.1.call-update) | async-done | bytes 131088 | tf_op jit(solution)/shard_map/reduce_scatter | solution.py:62
  294.4 2.4 fusion
  296.8 0.0 reduce-scatter.5.cloned.1.call-update
  296.8 12.9 %reduce-scatter.5.cloned.1.call-done = bf16[128,1024]{1,0:T(8,128)(2,1)} async-done(((bf16[128,2048]{1,0:T(8,128)(2,1)}), bf16[128,1024]{1,0:T(8,128)(2,1)}) %reduce-scatter.5.cloned.1.call-update) | async-done | bytes 262160 | tf_op jit(solution)/shard_map/reduce_scatter | solution.py:75
  (4 shorter events, 0.0 us)
Async XLA Ops:
  6.5 264.9 %copy-start = (bf16[1024,4]{0,1:T(4,128)(2,1)S(1)}, bf16[1024,4]{0,1:T(4,128)(2,1)}, u32[]{:S(2)}) copy-start(bf16[1024,4]{0,1:T(4,128)(2,1)} %param.14) | copy-start | bytes 24580
  6.5 21.8 %all-gather.3.cloned.1.call-start = ((), (), s32[]{:S(2)}) async-start(), calls=%async_computation.2 | async-start | bytes 1310720 | tf_op jit(solution)/shard_map/all_gather | solution.py:22
  7.3 172.4 %all-gather.5.cloned.1.call-start = ((), (), s32[]{:S(2)}) async-start(), calls=%async_computation.3 | async-start | bytes 10485760 | tf_op jit(solution)/shard_map/all_gather | solution.py:26
  8.0 249.5 %all-reduce.2.cloned.1.call-start = ((), (), s32[]{:S(2)}) async-start(), calls=%async_computation.4 | async-start | bytes 2818048 | tf_op jit(solution)/shard_map/psum | solution.py:58
  238.1 56.3 %reduce-scatter.3.cloned.1.call-start = ((), (), s32[]{:S(2)}) async-start(), calls=%async_computation.5 | async-start | bytes 655360 | tf_op jit(solution)/shard_map/reduce_scatter | solution.py:62
  271.4 38.4 %reduce-scatter.5.cloned.1.call-start = ((), (), s32[]{:S(2)}) async-start(), calls=%async_computation.6 | async-start | bytes 786432 | tf_op jit(solution)/shard_map/reduce_scatter | solution.py:75
Sparse Core Ops, SparseCore 0:
  8.9 19.4 all-gather.2
  29.9 149.6 all-gather.4
  238.2 19.2 all-reduce.1
  271.5 22.8 reduce-scatter.2
  296.9 12.7 reduce-scatter.4
where the time goes:
time: 317 us; the launch traced here: 316 us
  waiting for transfers between devices  218 us (69%)
  matrix products  43.1 us (14%)
  blocking collectives  36.4 us (11%)
  between operations  13.8 us (4%)
  other arithmetic  3.74 us (1%)
    all_gather x1, waiting for transfers between devices, local(): lax.all_gather(out_proj, 'tok', axis=0, tiled=True)  151 us
    psum x1, waiting for transfers between devices, local(): lax.psum(partial_in.astype(jnp.bfloat16), 'fsdp').astype(jnp.float32)  19.4 us
    all_gather x1, waiting for transfers between devices, local(): full_context = lax.all_gather(context, ('mod', 'fsdp'), axis=1, tiled=True)  18.3 us
    reduce_scatter x1, waiting for transfers between devices, local(): lax.psum_scatter(jnp.einsum('esf,efd->sed', activation, down_weight, pref...  15 us
    all_gather x1, blocking collectives, local(): piece = lax.all_gather(chosen, 'tok', axis=1, tiled=True)  14.7 us
    reduce_scatter x1, waiting for transfers between devices, local(): lax.psum_scatter(mixed_rows.astype(jnp.bfloat16), 'mod', scatter_dimensio...  12.9 us
    dot_general x1, matrix products, local(): jnp.einsum('esf,efd->sed', activation, down_weight, preferred_element_typ...  12.3 us
    dot_general x1, matrix products, local(): jnp.einsum('esd,edf->esf', piece, gate_weight, preferred_element_type=jnp...  11.3 us
  transfers between devices with their start and end apart: 5, of which 5 were waited for; matrix products, arithmetic and copies ran while one was open for 1% of the time, Pallas kernels for 0%

commit v1 on v0

v1 whole, which is shorter than its diff:
```python
import functools

import jax
import jax.numpy as jnp
from jax import lax
from jax.sharding import PartitionSpec as P

D = 4096
STAT_COLS = 128
FEW = 4


def ring(size, step):
    return [(i, (i + step) % size) for i in range(size)]


def reduce_tok(blocks, n_tok):
    if n_tok > FEW:
        return lax.psum_scatter(blocks, "tok", scatter_dimension=0, tiled=False).astype(jnp.float32)
    own = lax.axis_index("tok")
    total = lax.dynamic_index_in_dim(blocks, own, 0, False).astype(jnp.float32)
    for step in range(1, n_tok):
        sent = lax.dynamic_index_in_dim(blocks, (own + step) % n_tok, 0, False)
        total = total + lax.ppermute(sent, "tok", ring(n_tok, step)).astype(jnp.float32)
    return total


def gather_tok(rows, n_tok):
    if n_tok > FEW:
        return lax.all_gather(rows, "tok", axis=0, tiled=False)
    own = lax.axis_index("tok")
    result = jnp.zeros((n_tok,) + rows.shape, rows.dtype)
    result = lax.dynamic_update_index_in_dim(result, rows, own, 0)
    for step in range(1, n_tok):
        got = lax.ppermute(rows, "tok", ring(n_tok, step))
        result = lax.dynamic_update_index_in_dim(result, got, (own - step) % n_tok, 0)
    return result


def spread_context(rows, n_tok, n_mod, n_fsdp):
    if n_tok > FEW or n_tok != n_mod * n_fsdp:
        full = lax.all_gather(rows, ("mod", "fsdp"), axis=1, tiled=True)
        split = full.reshape(full.shape[0], n_tok, full.shape[1] // n_tok).transpose(1, 0, 2)
        return lax.all_to_all(split, "tok", 0, 0, tiled=True)
    pairs = [(t * n_tok + q, q * n_tok + t) for t in range(n_tok) for q in range(n_tok)]
    swapped = lax.ppermute(rows, ("tok", "mod", "fsdp"), pairs)
    return lax.all_gather(swapped, ("mod", "fsdp"), axis=0, tiled=False)


def local(
    residual,
    context,
    out_proj,
    norm_gain,
    router_weight,
    block_modality,
    expert_rows,
    gate_weight,
    up_weight,
    down_weight,
    *,
    n_tok,
    n_mod,
    n_fsdp,
):
    token_count = residual.shape[0]
    experts, capacity = expert_rows.shape
    kind_experts = experts // 2
    slots = kind_experts * capacity
    local_experts = gate_weight.shape[0]
    columns = residual.shape[1]
    assert block_modality.shape == (1,) and n_mod * local_experts == experts
    modality = block_modality[0]
    first = modality * kind_experts
    mod_index = lax.axis_index("mod")

    own_rows = lax.dynamic_slice_in_dim(expert_rows, first, kind_experts, 0).reshape(slots)
    pick = own_rows[:, None] == lax.iota(jnp.int32, token_count)[None, :]
    pick_half = pick.astype(jnp.bfloat16)
    picked_context = jnp.dot(pick_half, context, preferred_element_type=jnp.float32).astype(jnp.bfloat16)
    picked_residual = jnp.dot(pick_half, residual, preferred_element_type=jnp.float32)

    spread = spread_context(picked_context, n_tok, n_mod, n_fsdp)
    partial = jnp.einsum("tsk,kc->tsc", spread, out_proj, preferred_element_type=jnp.float32)
    hidden = picked_residual + reduce_tok(partial.astype(jnp.bfloat16), n_tok)

    gain_table = norm_gain.astype(jnp.float32)
    gained = hidden * jnp.where(modality == 0, gain_table[0], gain_table[1])[None, :]
    router = lax.dynamic_slice_in_dim(router_weight.astype(jnp.float32), first, kind_experts, 1)
    slot_router = jnp.repeat(router.T, capacity, axis=0)
    squares = jnp.sum(hidden * hidden, axis=1, keepdims=True)
    logits = jnp.sum(gained * slot_router, axis=1, keepdims=True)
    flag = jnp.broadcast_to(modality.astype(jnp.bfloat16), (slots, 1))
    stat_list = []
    for stat in (squares, logits):
        high = lax.reduce_precision(stat, 8, 7)
        stat_list += [high.astype(jnp.bfloat16), (stat - high).astype(jnp.bfloat16)]
    packed = jnp.concatenate(
        [gained.astype(jnp.bfloat16)] + stat_list
        + [flag, jnp.zeros((slots, STAT_COLS - 5), jnp.bfloat16)],
        axis=1,
    )

    everyone = gather_tok(packed, n_tok)
    both = lax.all_gather(everyone, "mod", axis=0, tiled=False)
    kind_first = (mod_index * local_experts) % kind_experts
    both = both.reshape(n_mod, n_tok, kind_experts, capacity, columns + STAT_COLS)
    mine = lax.dynamic_slice_in_dim(both, kind_first, local_experts, 2)
    piece = mine[..., :columns].transpose(2, 1, 3, 0, 4).reshape(
        local_experts, n_tok * capacity, n_mod * columns
    )
    tail = mine[..., columns : columns + 5].astype(jnp.float32)
    half_stats = jnp.sum(
        jnp.stack([tail[..., 0] + tail[..., 1], tail[..., 2] + tail[..., 3]], axis=-1), axis=0
    )
    stats = lax.psum(half_stats, "fsdp")
    flags = tail[0, :, :, :, 4]
    by_expert = stats.transpose(1, 0, 2, 3).reshape(local_experts, n_tok * capacity, 2)
    inverse = lax.rsqrt(by_expert[..., 0:1] / D + 1e-05)
    score = jax.nn.sigmoid(by_expert[..., 1:2] * inverse)

    gate_part = jnp.einsum("esd,edf->esf", piece, gate_weight, preferred_element_type=jnp.float32)
    up_part = jnp.einsum("esd,edf->esf", piece, up_weight, preferred_element_type=jnp.float32)
    gate_half = gate_part.astype(jnp.bfloat16)
    up_half = up_part.astype(jnp.bfloat16)
    if n_fsdp == 2:
        swap = [(0, 1), (1, 0)]
        gate_sum = gate_half.astype(jnp.float32) + lax.ppermute(gate_half, "fsdp", swap).astype(jnp.float32)
        up_sum = up_half.astype(jnp.float32) + lax.ppermute(up_half, "fsdp", swap).astype(jnp.float32)
    else:
        gate_sum = lax.psum(gate_half, "fsdp").astype(jnp.float32)
        up_sum = lax.psum(up_half, "fsdp").astype(jnp.float32)
    activation = (jax.nn.silu(gate_sum * inverse) * (up_sum * inverse)).astype(jnp.bfloat16)
    value = jnp.einsum("esf,efd->esd", activation, down_weight, preferred_element_type=jnp.float32)
    value = (value * score).astype(jnp.bfloat16)
    value = value.reshape(local_experts, n_tok, capacity, n_mod * columns).transpose(1, 0, 2, 3)

    own_kind = (mod_index * local_experts) // kind_experts
    valid = (flags == own_kind.astype(jnp.float32))[..., None]
    if n_mod == 2:
        value = value.reshape(n_tok, local_experts, capacity, n_mod, columns)
        kept = lax.dynamic_index_in_dim(value, mod_index, 3, False)
        sent = lax.dynamic_index_in_dim(value, 1 - mod_index, 3, False)
        got = lax.ppermute(sent, "mod", [(0, 1), (1, 0)])
        merged = jnp.where(valid, kept, got).reshape(n_tok, slots, columns)
    else:
        value = jnp.where(valid, value, jnp.zeros((), jnp.bfloat16))
        wide = jnp.zeros((n_tok, kind_experts, capacity, n_mod * columns), jnp.bfloat16)
        wide = lax.dynamic_update_slice_in_dim(wide, value, kind_first, 1)
        wide = wide.reshape(n_tok, slots, n_mod * columns)
        merged = lax.psum_scatter(wide, "mod", scatter_dimension=2, tiled=True)
    summed = reduce_tok(merged, n_tok)
    return jnp.dot(
        pick.astype(jnp.float32).T, summed, precision=lax.Precision.HIGHEST
    ).astype(jnp.bfloat16)


def solution(mesh):
    placed = (
        P(("groups", "tok"), ("fsdp", "mod")),
        P(("groups", "tok"), ("mod", "fsdp")),
        P("tok", ("fsdp", "mod")),
        P(None, ("fsdp", "mod")),
        P(("fsdp", "mod"), None),
        P(("groups", "tok")),
        P(None, ("groups", "tok")),
        P("mod", "fsdp", "tok"),
        P("mod", "fsdp", "tok"),
        P("mod", "tok", "fsdp"),
    )
    sizes = dict(n_tok=mesh.shape["tok"], n_mod=mesh.shape["mod"], n_fsdp=mesh.shape["fsdp"])
    return jax.shard_map(
        functools.partial(local, **sizes),
        mesh=mesh,
        in_specs=placed,
        out_specs=P(("groups", "tok"), ("fsdp", "mod")),
        check_vma=False,
    )
```

time: 317 us -> 110 us (0.35)
  waiting for transfers between devices: 218 us -> 26 us
  between operations: 13.8 us -> 1.19 us
  starting transfers between devices: 0.16 us -> 12.3 us
  blocking collectives: 36.4 us -> 26.9 us
  matrix products: 43.1 us -> 38 us
  local copies, waits for them, and re-layouts: 0.7 us -> 4.53 us
    all_gather x2 -> x0, waiting for transfers between devices: 170 us -> none  [the longest x1 151 us: local(): lax.all_gather(out_proj, 'tok', axis=0, tiled=True)]
    reduce_scatter x2 -> x0, waiting for transfers between devices: 28 us -> none  [the longest x1 15 us: local(): lax.psum_scatter(jnp.einsum('esf,efd->sed', activation, down_weight, pref...]
    ppermute x0 -> x13, waiting for transfers between devices: none -> 26 us  [the longest x6 11.5 us: reduce_tok(): lax.ppermute(sent, 'tok', ring(n_tok, step)).astype(jnp.float32)]
    psum x1 -> x0, waiting for transfers between devices: 19.4 us -> none  [local(): lax.psum(partial_in.astype(jnp.bfloat16), 'fsdp').astype(jnp.float32)]
    ppermute x0 -> x13, starting transfers between devices: none -> 12.3 us  [the longest x6 7.75 us: reduce_tok(): lax.ppermute(sent, 'tok', ring(n_tok, step)).astype(jnp.float32)]
    psum x2 -> x1, blocking collectives: 14.1 us -> 2.63 us  [local(): stats = lax.psum(half_stats, 'fsdp')]
    dot_general x6 -> x5, matrix products: 20.5 us -> 15.4 us  [the longest x1 12.2 us: local(): jnp.einsum('esf,efd->esd', activation, down_weight, preferred_element_typ...]
  transfers between devices with their start and end apart: 5 -> 13, of which waited for: 5 -> 7; matrix products, arithmetic and copies ran while one was open for 1% -> 1% of each run, Pallas kernels for 0% -> 0%
where the time goes in v1:
time: 110 us
  matrix products  38 us (35%)
  blocking collectives  26.9 us (24%)
  waiting for transfers between devices  26 us (24%)
  starting transfers between devices  12.3 us (11%)
  local copies, waits for them, and re-layouts  4.53 us (4%)
  between operations  1.19 us (1%)
    all_gather x1, blocking collectives, spread_context(): return lax.all_gather(swapped, ('mod', 'fsdp'), axis=0, tiled=False)  15.3 us
    dot_general x1, matrix products, local(): jnp.einsum('esf,efd->esd', activation, down_weight, preferred_element_typ...  12.2 us
    ppermute x6, waiting for transfers between devices, reduce_tok(): lax.ppermute(sent, 'tok', ring(n_tok, step)).astype(jnp.float32)  11.5 us
    dot_general x1, matrix products, local(): jnp.einsum('esd,edf->esf', piece, gate_weight, preferred_element_type=jnp...  11.3 us
    dot_general x1, matrix products, local(): jnp.einsum('esd,edf->esf', piece, up_weight, preferred_element_type=jnp.f...  11.3 us
    all_gather x1, blocking collectives, local(): both = lax.all_gather(everyone, 'mod', axis=0, tiled=False)  8.99 us
    ppermute x1, waiting for transfers between devices, local(): got = lax.ppermute(sent, 'mod', [(0, 1), (1, 0)])  8.09 us
    ppermute x6, starting transfers between devices, reduce_tok(): lax.ppermute(sent, 'tok', ring(n_tok, step)).astype(jnp.float32)  7.75 us
  transfers between devices with their start and end apart: 13, of which 7 were waited for; matrix products, arithmetic and copies ran while one was open for 1% of the time, Pallas kernels for 0%

profile of v1, /device:TPU:0, one launch (start us, length us, event | category | flops | bytes accessed | tf_op | source)
XLA Modules:
  0.0 109.8 jit_solution(11024385152500869714)
XLA Ops:
  0.8 0.7 constant_dynamic-slice_fusion.2
  1.5 0.1 eq.45
  1.6 1.1 %convolution_convert_fusion.3 = bf16[32,1024]{1,0:T(8,128)(2,1)S(1)} fusion(bf16[128,1024]{1,0:T(8,128)(2,1)} %param.11, s32[32]{0:T(128)S(1)} %eq.45), kind=kOutput, calls=%fused_computation.9 | convolution fusion | flops 8425472 | bytes 327808 | tf_op jit(solution)/shard_map/dot_general | solution.py:80
  2.7 0.7 collective-permute-start
  3.4 0.7 convert_element_type.137
  4.2 0.0 collective-permute-done
  4.2 15.3 %all-gather = bf16[128,1024]{1,0:T(8,128)(2,1)S(1)} all-gather(bf16[32,1024]{1,0:T(8,128)(2,1)S(1)} %collective-permute-done), channel_id=2, replica_groups=mesh['groups'=2,'tok'=4,'mod'=2,'fsdp'=2] {'mod','fsdp'}, dimensions={0}, use_global_device_ids=true | all-gather | bytes 327680 | tf_op jit(solution)/shard_map/all_gather | solution.py:47
  19.5 0.5 fusion.3
  20.0 0.3 collective-permute-start.1
  20.3 3.6 %collective-permute-start.3 = (bf16[32,1024]{1,0:T(8,128)(2,1)S(1)}, bf16[32,1024]{1,0:T(8,128)(2,1)S(1)}, u32[]{:S(2)}, u32[]{:S(2)}) collective-permute-start(bf16[32,1024]{1,0:T(8,128)(2,1)S(1)} %get-tuple-element.16), channel_id=1, source_target_pairs={{0,12},{4,0},{8,4},{12,8},{1,13},{5,1},{9,5},{13,9},{2,14},{6,2},{... | collective-permute-start | bytes 196616 | tf_op jit(solution)/shard_map/ppermute | solution.py:24
  23.9 2.9 %collective-permute-done.1 = bf16[32,1024]{1,0:T(8,128)(2,1)S(1)} collective-permute-done((bf16[32,1024]{1,0:T(8,128)(2,1)S(1)}, bf16[32,1024]{1,0:T(8,128)(2,1)S(1)}, u32[]{:S(2)}, u32[]{:S(2)}) %collective-permute-start.1) | collective-permute-done | bytes 65568 | tf_op jit(solution)/shard_map/ppermute | solution.py:24
  26.8 3.1 %collective-permute-done.2 = bf16[32,1024]{1,0:T(8,128)(2,1)S(1)} collective-permute-done((bf16[32,1024]{1,0:T(8,128)(2,1)S(1)}, bf16[32,1024]{1,0:T(8,128)(2,1)S(1)}, u32[]{:S(2)}, u32[]{:S(2)}) %collective-permute-start.2) | collective-permute-done | bytes 65568 | tf_op jit(solution)/shard_map/ppermute | solution.py:24
  29.9 0.3 fusion.14
  30.3 0.1 copy.64
  30.4 0.1 copy.63
  30.5 0.1 copy.65
  30.6 0.1 copy.66
  30.7 0.1 concatenate.3
  30.8 2.3 %collective-permute-start.6 = (bf16[32,1152]{1,0:T(8,128)(2,1)S(1)}, bf16[32,1152]{1,0:T(8,128)(2,1)S(1)}, u32[]{:S(2)}, u32[]{:S(2)}) collective-permute-start(bf16[32,1152]{1,0:T(8,128)(2,1)S(1)} %concatenate.3), channel_id=1, source_target_pairs={{0,12},{4,0},{8,4},{12,8},{1,13},{5,1},{9,5},{13,9},{2,14},{6,2},{... | collective-permute-start | bytes 221192 | tf_op jit(solution)/shard_map/ppermute | solution.py:35
  33.1 0.6 collective-permute-start.4
  33.8 5.5 %collective-permute-done.4 = bf16[32,1152]{1,0:T(8,128)(2,1)S(1)} collective-permute-done((bf16[32,1152]{1,0:T(8,128)(2,1)S(1)}, bf16[32,1152]{1,0:T(8,128)(2,1)S(1)}, u32[]{:S(2)}, u32[]{:S(2)}) %collective-permute-start.4) | collective-permute-done | bytes 73760 | tf_op jit(solution)/shard_map/ppermute | solution.py:35
  39.3 0.9 collective-permute-done.5
  40.3 9.0 %all_gather.27 = bf16[2,4,32,1152]{3,2,1,0:T(8,128)(2,1)S(1)} all-gather(bf16[1,4,32,1152]{3,2,1,0:T(8,128)(2,1)S(1)} %bitcast_dynamic-update-slice_fusion), channel_id=1, replica_groups=mesh['groups'=2,'tok'=4,'mod'=2,'fsdp'=2] {'mod'}, dimensions={0}, use_global_device_ids=true | all-gather | bytes 884736 | tf_op jit(solution)/shard_map/all_gather | solution.py:105
  49.3 0.1 slice_bitcast_fusion
  49.3 0.5 copy.69
  49.9 0.4 reshape.100
  50.3 11.3 %convolution_convert_fusion = bf16[2,64,2752]{2,1,0:T(8,128)(2,1)S(1)} fusion(bf16[2,64,2048]{2,1,0:T(8,128)(2,1)S(1)} %reshape.100, bf16[2,2048,2752]{1,2,0:T(8,128)(2,1)} %param.18), kind=kOutput, calls=%fused_computation | convolution fusion | flops 1443192832 | bytes 23773184 | tf_op jit(solution)/shard_map/esd,edf->esf/dot_general | solution.py:123
  61.6 11.3 %convolution_convert_fusion.1 = bf16[2,64,2752]{2,1,0:T(8,128)(2,1)S(1)} fusion(bf16[2,64,2048]{2,1,0:T(8,128)(2,1)S(1)} %reshape.100, bf16[2,2048,2752]{1,2,0:T(8,128)(2,1)} %param.17), kind=kOutput, calls=%fused_computation.1 | convolution fusion | flops 1443192832 | bytes 23773184 | tf_op jit(solution)/shard_map/esd,edf->esf/dot_general | solution.py:122
  72.9 0.1 collective-permute-start.7
  73.0 0.5 collective-permute-start.8
  73.5 0.2 copy.76
  73.7 0.1 copy.75
  73.8 0.1 copy.71
  74.0 0.1 reshape.101
  74.0 2.6 %psum.7 = f32[2,64,2]{1,2,0:T(2,128)S(1)} all-reduce(f32[2,64,2]{1,2,0:T(2,128)S(1)} %reshape.101), channel_id=1, replica_groups=mesh['groups'=2,'tok'=4,'mod'=2,'fsdp'=2] {'fsdp'}, use_global_device_ids=true, to_apply=%region_3.4 | all-reduce | flops 256 | bytes 2048 | tf_op jit(solution)/shard_map/psum | solution.py:116
  76.7 12.2 %fusion = bf16[2,64,2048]{2,1,0:T(8,128)(2,1)S(1)} fusion(bf16[2,2752,2048]{2,1,0:T(8,128)(2,1)} %param.19, bf16[2,64,2752]{2,1,0:T(8,128)(2,1)} %collective-permute-done.8, bf16[2,64,2752]{2,1,0:T(8,128)(2,1)S(1)} %convolution_convert_fusion, bf16[2,64,2752]{2,1,0:T(8,128)(2,1)S(1)} %collective-permute-done.7, ...), kind=kOutput, calls=%fused_computation.3 | convolution fusion | flops 1448296448 | bytes 25887744 | tf_op jit(solution)/shard_map/esf,efd->esd/dot_general | solution.py:134
  89.0 0.4 reshape.103
  89.4 0.0 copy-start.1
  89.4 1.1 constant_dynamic-slice_fusion.1
  90.5 0.1 copy.81
  90.6 0.3 collective-permute-start.9
  90.9 8.1 %collective-permute-done.9 = bf16[4,2,16,1024]{3,2,1,0:T(8,128)(2,1)S(1)} collective-permute-done((bf16[4,2,16,1024]{3,2,1,0:T(8,128)(2,1)S(1)}, bf16[4,2,16,1024]{3,2,1,0:T(8,128)(2,1)S(1)}, u32[]{:S(2)}, u32[]{:S(2)}) %collective-permute-start.9) | collective-permute-done | bytes 262176 | tf_op jit(solution)/shard_map/ppermute | solution.py:144
  99.0 0.1 bitcast_select_fusion
  99.2 0.1 collective-permute-start.10
  99.3 3.8 %collective-permute-start.12 = (bf16[32,1024]{1,0:T(8,128)(2,1)S(1)}, bf16[32,1024]{1,0:T(8,128)(2,1)S(1)}, u32[]{:S(2)}, u32[]{:S(2)}) collective-permute-start(bf16[32,1024]{1,0:T(8,128)(2,1)S(1)} %get-tuple-element.13), channel_id=1, source_target_pairs={{0,12},{4,0},{8,4},{12,8},{1,13},{5,1},{9,5},{13,9},{2,14},{6,2},{... | collective-permute-start | bytes 196616 | tf_op jit(solution)/shard_map/ppermute | solution.py:24
  103.1 2.8 %collective-permute-done.10 = bf16[32,1024]{1,0:T(8,128)(2,1)S(1)} collective-permute-done((bf16[32,1024]{1,0:T(8,128)(2,1)S(1)}, bf16[32,1024]{1,0:T(8,128)(2,1)S(1)}, u32[]{:S(2)}, u32[]{:S(2)}) %collective-permute-start.10) | collective-permute-done | bytes 65568 | tf_op jit(solution)/shard_map/ppermute | solution.py:24
  105.9 2.7 %collective-permute-done.11 = bf16[32,1024]{1,0:T(8,128)(2,1)S(1)} collective-permute-done((bf16[32,1024]{1,0:T(8,128)(2,1)S(1)}, bf16[32,1024]{1,0:T(8,128)(2,1)S(1)}, u32[]{:S(2)}, u32[]{:S(2)}) %collective-permute-start.11) | collective-permute-done | bytes 65568 | tf_op jit(solution)/shard_map/ppermute | solution.py:24
  108.6 1.2 %convolution_convert_fusion.2 = bf16[128,1024]{1,0:T(8,128)(2,1)} fusion(bf16[32,1024]{1,0:T(8,128)(2,1)S(1)} %collective-permute-done.12, bf16[32,1024]{1,0:T(8,128)(2,1)S(1)} %collective-permute-done.11, bf16[32,1024]{1,0:T(8,128)(2,1)S(1)} %collective-permute-done.10, bf16[4,32,1024]{2,1,0:T(8,128)(2,1)S(1)} %bitcast.87, s32[]{:T(128)S(6)} %select_n.93, ...), kind=kOutput, calls=%fused_computation.8 | convolution fusion | flops 50696192 | bytes 524804 | tf_op jit(solution)/shard_map/dot_general | solution.py:153
  (36 shorter events, 0.3 us)
Async XLA Ops:
  0.0 19.5 %copy-start = (bf16[1024,1024]{1,0:T(8,128)(2,1)S(1)}, bf16[1024,1024]{1,0:T(8,128)(2,1)}, u32[]{:S(2)}) copy-start(bf16[1024,1024]{1,0:T(8,128)(2,1)} %param.12) | copy-start | bytes 6291460
  2.7 1.5 %collective-permute-start = (bf16[32,1024]{1,0:T(8,128)(2,1)S(1)}, bf16[32,1024]{1,0:T(8,128)(2,1)S(1)}, u32[]{:S(2)}, u32[]{:S(2)}) collective-permute-start(bf16[32,1024]{1,0:T(8,128)(2,1)S(1)} %convolution_convert_fusion.3), channel_id=1, source_target_pairs={{0,0},{1,4},{2,8},{3,12},{4,1},{5,5},{6,9},{7,13},{8,2},{9,6},{10,... | collective-permute-start | bytes 196616 | tf_op jit(solution)/shard_map/ppermute | solution.py:46
  19.5 4.4 %copy-start.3 = (bf16[1024,4]{0,1:T(4,128)(2,1)S(1)}, bf16[1024,4]{0,1:T(4,128)(2,1)}, u32[]{:S(2)}) copy-start(bf16[1024,4]{0,1:T(4,128)(2,1)} %param.14) | copy-start | bytes 24580
  19.5 10.4 %copy-start.2 = (bf16[128,1024]{1,0:T(8,128)(2,1)S(1)}, bf16[128,1024]{1,0:T(8,128)(2,1)}, u32[]{:S(2)}) copy-start(bf16[128,1024]{1,0:T(8,128)(2,1)} %param.10) | copy-start | bytes 786436
  20.0 6.8 %collective-permute-start.1 = (bf16[32,1024]{1,0:T(8,128)(2,1)S(1)}, bf16[32,1024]{1,0:T(8,128)(2,1)S(1)}, u32[]{:S(2)}, u32[]{:S(2)}) collective-permute-start(bf16[32,1024]{1,0:T(8,128)(2,1)S(1)} %get-tuple-element.15), channel_id=1, source_target_pairs={{0,4},{4,8},{8,12},{12,0},{1,5},{5,9},{9,13},{13,1},{2,6},{6,10},{... | collective-permute-start | bytes 196616 | tf_op jit(solution)/shard_map/ppermute | solution.py:24
  20.3 6.5 %collective-permute-start.3 = (bf16[32,1024]{1,0:T(8,128)(2,1)S(1)}, bf16[32,1024]{1,0:T(8,128)(2,1)S(1)}, u32[]{:S(2)}, u32[]{:S(2)}) collective-permute-start(bf16[32,1024]{1,0:T(8,128)(2,1)S(1)} %get-tuple-element.16), channel_id=1, source_target_pairs={{0,12},{4,0},{8,4},{12,8},{1,13},{5,1},{9,5},{13,9},{2,14},{6,2},{... | collective-permute-start | bytes 196616 | tf_op jit(solution)/shard_map/ppermute | solution.py:24
  23.9 6.0 %collective-permute-start.2 = (bf16[32,1024]{1,0:T(8,128)(2,1)S(1)}, bf16[32,1024]{1,0:T(8,128)(2,1)S(1)}, u32[]{:S(2)}, u32[]{:S(2)}) collective-permute-start(bf16[32,1024]{1,0:T(8,128)(2,1)S(1)} %get-tuple-element.17), channel_id=1, source_target_pairs={{0,8},{4,12},{8,0},{12,4},{1,9},{5,13},{9,1},{13,5},{2,10},{6,14},... | collective-permute-start | bytes 196616 | tf_op jit(solution)/shard_map/ppermute | solution.py:24
  30.8 9.4 %collective-permute-start.6 = (bf16[32,1152]{1,0:T(8,128)(2,1)S(1)}, bf16[32,1152]{1,0:T(8,128)(2,1)S(1)}, u32[]{:S(2)}, u32[]{:S(2)}) collective-permute-start(bf16[32,1152]{1,0:T(8,128)(2,1)S(1)} %concatenate.3), channel_id=1, source_target_pairs={{0,12},{4,0},{8,4},{12,8},{1,13},{5,1},{9,5},{13,9},{2,14},{6,2},{... | collective-permute-start | bytes 221192 | tf_op jit(solution)/shard_map/ppermute | solution.py:35
  33.1 7.1 %collective-permute-start.5 = (bf16[32,1152]{1,0:T(8,128)(2,1)S(1)}, bf16[32,1152]{1,0:T(8,128)(2,1)S(1)}, u32[]{:S(2)}, u32[]{:S(2)}) collective-permute-start(bf16[32,1152]{1,0:T(8,128)(2,1)S(1)} %concatenate.3), channel_id=1, source_target_pairs={{0,8},{4,12},{8,0},{12,4},{1,9},{5,13},{9,1},{13,5},{2,10},{6,14},... | collective-permute-start | bytes 221192 | tf_op jit(solution)/shard_map/ppermute | solution.py:35
  33.1 6.2 %collective-permute-start.4 = (bf16[32,1152]{1,0:T(8,128)(2,1)S(1)}, bf16[32,1152]{1,0:T(8,128)(2,1)S(1)}, u32[]{:S(2)}, u32[]{:S(2)}) collective-permute-start(bf16[32,1152]{1,0:T(8,128)(2,1)S(1)} %concatenate.3), channel_id=1, source_target_pairs={{0,4},{4,8},{8,12},{12,0},{1,5},{5,9},{9,13},{13,1},{2,6},{6,10},{... | collective-permute-start | bytes 221192 | tf_op jit(solution)/shard_map/ppermute | solution.py:35
  72.9 3.8 %collective-permute-start.7 = (bf16[2,64,2752]{2,1,0:T(8,128)(2,1)S(1)}, bf16[2,64,2752]{2,1,0:T(8,128)(2,1)S(1)}, u32[]{:S(2)}, u32[]{:S(2)}) collective-permute-start(bf16[2,64,2752]{2,1,0:T(8,128)(2,1)S(1)} %convolution_convert_fusion.1), channel_id=1, source_target_pairs={{0,1},{1,0},{2,3},{3,2},{4,5},{5,4},{6,7},{7,6},{8,9},{9,8},{10,11... | collective-permute-start | bytes 2113544 | tf_op jit(solution)/shard_map/ppermute | solution.py:128
  73.0 3.7 %collective-permute-start.8 = (bf16[2,64,2752]{2,1,0:T(8,128)(2,1)S(1)}, bf16[2,64,2752]{2,1,0:T(8,128)(2,1)}, u32[]{:S(2)}, u32[]{:S(2)}) collective-permute-start(bf16[2,64,2752]{2,1,0:T(8,128)(2,1)S(1)} %convolution_convert_fusion), channel_id=1, source_target_pairs={{0,1},{1,0},{2,3},{3,2},{4,5},{5,4},{6,7},{7,6},{8,9},{9,8},{10,11... | collective-permute-start | bytes 2113544 | tf_op jit(solution)/shard_map/ppermute | solution.py:129
  89.4 20.4 %copy-start.1 = (bf16[1024,1024]{1,0:T(8,128)(2,1)S(1)}, bf16[1024,1024]{1,0:T(8,128)(2,1)}, u32[]{:S(2)}) copy-start(bf16[1024,1024]{1,0:T(8,128)(2,1)} %param.12) | copy-start | bytes 6291460
  90.6 8.4 %collective-permute-start.9 = (bf16[4,2,16,1024]{3,2,1,0:T(8,128)(2,1)S(1)}, bf16[4,2,16,1024]{3,2,1,0:T(8,128)(2,1)S(1)}, u32[]{:S(2)}, u32[]{:S(2)}) collective-permute-start(bf16[4,2,16,1024]{3,2,1,0:T(8,128)(2,1)S(1)} %bitcast.89), channel_id=1, source_target_pairs={{0,2},{2,0},{1,3},{3,1},{4,6},{6,4},{5,7},{7,5},{8,10},{10,8},{9,1... | collective-permute-start | bytes 786440 | tf_op jit(solution)/shard_map/ppermute | solution.py:144
  99.2 6.7 %collective-permute-start.10 = (bf16[32,1024]{1,0:T(8,128)(2,1)S(1)}, bf16[32,1024]{1,0:T(8,128)(2,1)S(1)}, u32[]{:S(2)}, u32[]{:S(2)}) collective-permute-start(bf16[32,1024]{1,0:T(8,128)(2,1)S(1)} %get-tuple-element.12), channel_id=1, source_target_pairs={{0,4},{4,8},{8,12},{12,0},{1,5},{5,9},{9,13},{13,1},{2,6},{6,10},{... | collective-permute-start | bytes 196616 | tf_op jit(solution)/shard_map/ppermute | solution.py:24
  99.3 6.6 %collective-permute-start.12 = (bf16[32,1024]{1,0:T(8,128)(2,1)S(1)}, bf16[32,1024]{1,0:T(8,128)(2,1)S(1)}, u32[]{:S(2)}, u32[]{:S(2)}) collective-permute-start(bf16[32,1024]{1,0:T(8,128)(2,1)S(1)} %get-tuple-element.13), channel_id=1, source_target_pairs={{0,12},{4,0},{8,4},{12,8},{1,13},{5,1},{9,5},{13,9},{2,14},{6,2},{... | collective-permute-start | bytes 196616 | tf_op jit(solution)/shard_map/ppermute | solution.py:24
  103.1 5.5 %collective-permute-start.11 = (bf16[32,1024]{1,0:T(8,128)(2,1)S(1)}, bf16[32,1024]{1,0:T(8,128)(2,1)S(1)}, u32[]{:S(2)}, u32[]{:S(2)}) collective-permute-start(bf16[32,1024]{1,0:T(8,128)(2,1)S(1)} %get-tuple-element.14), channel_id=1, source_target_pairs={{0,8},{4,12},{8,0},{12,4},{1,9},{5,13},{9,1},{13,5},{2,10},{6,14},... | collective-permute-start | bytes 196616 | tf_op jit(solution)/shard_map/ppermute | solution.py:24

commit v2 on v1

--- a/solution.py
+++ b/solution.py
@@ -3,6 +3,8 @@
 import jax
 import jax.numpy as jnp
 from jax import lax
+from jax.experimental import pallas as pl
+from jax.experimental.pallas import tpu as pltpu
 from jax.sharding import PartitionSpec as P
 
 D = 4096
@@ -155,6 +157,249 @@
     ).astype(jnp.bfloat16)
 
 
+SWAP = [(0, 1), (1, 0)]
+CHUNK = 512
+
+
+def crossed(axis_sizes_bits, flip):
+    return [(i, i ^ flip) for i in range(1 << axis_sizes_bits)]
+
+
+def keep_kernel(index_ref, weight_ref, held_ref, semaphore):
+    copy = pltpu.make_async_copy(weight_ref.at[index_ref[0]], held_ref, semaphore)
+    copy.start()
+    copy.wait()
+
+
+def keep_on_chip(index, weight, name):
+    weight = pltpu.with_memory_space_constraint(weight, pltpu.HBM)
+    size = weight.shape[1] * weight.shape[2] * 2
+    return pl.pallas_call(
+        keep_kernel,
+        out_shape=pltpu.VMEM(weight.shape[1:], weight.dtype),
+        in_specs=[pl.BlockSpec(memory_space=pltpu.SMEM), pl.BlockSpec(memory_space=pltpu.HBM)],
+        out_specs=pl.BlockSpec(memory_space=pltpu.VMEM),
+        scratch_shapes=[pltpu.SemaphoreType.DMA(())],
+        compiler_params=pltpu.CompilerParams(vmem_limit_bytes=1 << 20),
+        cost_estimate=pl.CostEstimate(flops=0, transcendentals=0, bytes_accessed=size),
+        name=name,
+    )(index, weight)
+
+
+def project_kernel(flip_ref, *refs):
+    block_refs, weight_ref, out_ref, rows_ref = refs[:4], refs[4], refs[5], refs[6]
+    slots = block_refs[0].shape[0]
+    for u, block_ref in enumerate(block_refs):
+        rows_ref[u * slots : (u + 1) * slots, :] = block_ref[...]
+    product = jnp.dot(rows_ref[...], weight_ref[...], preferred_element_type=jnp.float32)
+    product = product.astype(jnp.bfloat16)
+    for u in range(len(block_refs)):
+        out_ref[flip_ref[0] ^ u] = product[u * slots : (u + 1) * slots, :]
+
+
+def project(flip, blocks, weight):
+    slots, depth = blocks[0].shape
+    return pl.pallas_call(
+        project_kernel,
+        out_shape=jax.ShapeDtypeStruct((len(blocks), slots, weight.shape[1]), jnp.bfloat16),
+        in_specs=[pl.BlockSpec(memory_space=pltpu.SMEM)]
+        + [pl.BlockSpec(memory_space=pltpu.VMEM)] * (len(blocks) + 1),
+        out_specs=pl.BlockSpec(memory_space=pltpu.VMEM),
+        scratch_shapes=[pltpu.VMEM((len(blocks) * slots, depth), jnp.bfloat16)],
+        compiler_params=pltpu.CompilerParams(vmem_limit_bytes=8 << 20),
+        name="project",
+    )(flip, *blocks, weight)
+
+
+def gate_up_kernel(side_ref, own_ref, far_ref, side_own_ref, side_far_ref, gate_ref, up_ref, out_ref, rows_ref):
+    half = own_ref.shape[0]
+    columns = rows_ref.shape[1] // 2
+    units = gate_ref.shape[0]
+    for side in range(2):
+
+        @pl.when(side_ref[0] == side)
+        def _():
+            here, there = side * columns, (1 - side) * columns
+            rows_ref[:half, here : here + columns] = own_ref[:, :columns]
+            rows_ref[half:, here : here + columns] = far_ref[:, :columns]
+            rows_ref[:half, there : there + columns] = side_own_ref[:, :columns]
+            rows_ref[half:, there : there + columns] = side_far_ref[:, :columns]
+
+    rows = rows_ref[...]
+    for which, weight_ref in enumerate((gate_ref, up_ref)):
+        for start in range(0, units, CHUNK):
+            stop = min(start + CHUNK, units)
+            product = lax.dot_general(
+                rows, weight_ref[start:stop, :], (((1,), (1,)), ((), ())),
+                preferred_element_type=jnp.float32,
+            )
+            out_ref[which, :, start:stop] = product.astype(jnp.bfloat16)
+
+
+def gate_up(side, blocks, gate, up):
+    half = blocks[0].shape[0]
+    units, depth = gate.shape
+    return pl.pallas_call(
+        gate_up_kernel,
+        out_shape=jax.ShapeDtypeStruct((2, 2 * half, units), jnp.bfloat16),
+        in_specs=[pl.BlockSpec(memory_space=pltpu.SMEM)] + [pl.BlockSpec(memory_space=pltpu.VMEM)] * 6,
+        out_specs=pl.BlockSpec(memory_space=pltpu.VMEM),
+        scratch_shapes=[pltpu.VMEM((2 * half, depth), jnp.bfloat16)],
+        compiler_params=pltpu.CompilerParams(vmem_limit_bytes=8 << 20),
+        cost_estimate=pl.CostEstimate(
+            flops=8 * half * units * depth, transcendentals=0, bytes_accessed=4 * half * units * 2
+        ),
+        name="gate_up",
+    )(side, *blocks, gate, up)
+
+
+def down_kernel(side_ref, mine_ref, other_ref, stat_ref, weight_ref, out_ref, act_ref):
+    units, width = weight_ref.shape
+    stat = stat_ref[...]
+    squares = stat[:, 0:1] + stat[:, 1:2]
+    inverse = lax.rsqrt(squares / D + 1e-05)
+    logits = (stat[:, 2:3] + stat[:, 3:4]) * inverse
+    score = 1.0 / (1.0 + jnp.exp(-logits))
+    for start in range(0, units, CHUNK):
+        stop = min(start + CHUNK, units)
+        gate, up = [
+            (
+                mine_ref[which, :, start:stop].astype(jnp.float32)
+                + other_ref[which, :, start:stop].astype(jnp.float32)
+            )
+            * inverse
+            for which in range(2)
+        ]
+        act_ref[:, start:stop] = (gate / (1.0 + jnp.exp(-gate)) * up).astype(jnp.bfloat16)
+    columns = width // 2
+    for start in range(0, width, CHUNK):
+        value = jnp.dot(
+            act_ref[...], weight_ref[:, start : start + CHUNK], preferred_element_type=jnp.float32
+        )
+        quarter = start // columns
+        at = start - quarter * columns
+        out_ref[side_ref[0] ^ quarter, :, at : at + CHUNK] = (value * score).astype(jnp.bfloat16)
+
+
+def down(side, mine, other, stat, weight):
+    rows = stat.shape[0]
+    units, width = weight.shape
+    return pl.pallas_call(
+        down_kernel,
+        out_shape=jax.ShapeDtypeStruct((2, rows, width // 2), jnp.bfloat16),
+        in_specs=[pl.BlockSpec(memory_space=pltpu.SMEM)] + [pl.BlockSpec(memory_space=pltpu.VMEM)] * 4,
+        out_specs=pl.BlockSpec(memory_space=pltpu.VMEM),
+        scratch_shapes=[pltpu.VMEM((rows, units), jnp.bfloat16)],
+        compiler_params=pltpu.CompilerParams(vmem_limit_bytes=8 << 20),
+        cost_estimate=pl.CostEstimate(
+            flops=2 * rows * units * width, transcendentals=2 * rows * units, bytes_accessed=rows * width * 2
+        ),
+        name="down",
+    )(side, mine, other, stat, weight)
+
+
+def paired_local(
+    residual,
+    context,
+    out_proj,
+    norm_gain,
+    router_weight,
+    block_modality,
+    expert_rows,
+    gate_weight,
+    up_weight,
+    down_weight,
+):
+    token_count, columns = residual.shape
+    experts, capacity = expert_rows.shape
+    kind_experts = experts // 2
+    slots = kind_experts * capacity
+    assert block_modality.shape == (1,) and kind_experts == 2 and gate_weight.shape[0] == 2
+    modality = block_modality[0]
+    first = modality * kind_experts
+    group = lax.axis_index("groups")
+    tok = lax.axis_index("tok")
+    side = lax.axis_index("mod")
+    group_list, side_list = group.reshape(1), side.reshape(1)
+
+    gate_held = keep_on_chip(group_list, gate_weight.swapaxes(1, 2), "keep_gate")
+    up_held = keep_on_chip(group_list, up_weight.swapaxes(1, 2), "keep_up")
+    down_held = keep_on_chip(group_list, down_weight, "keep_down")
+
+    kind_rows = lax.dynamic_slice_in_dim(expert_rows, first, kind_experts, 0)
+    own_rows = jnp.where(group == 0, kind_rows, kind_rows[::-1]).reshape(slots)
+    pick = own_rows[:, None] == lax.iota(jnp.int32, token_count)[None, :]
+    pick_half = pick.astype(jnp.bfloat16)
+    picked_context = jnp.dot(pick_half, context, preferred_element_type=jnp.float32).astype(jnp.bfloat16)
+    picked_residual = jnp.dot(pick_half, residual, preferred_element_type=jnp.float32)
+
+    plane = ("tok", "mod", "fsdp")
+    to_first = [(t * 4 + q, q * 4 + t) for t in range(4) for q in range(4)]
+    to_second = [(t * 4 + q, q * 4 + (t ^ 2)) for t in range(4) for q in range(4)]
+    near = lax.ppermute(picked_context, plane, to_first)
+    across = lax.ppermute(picked_context, plane, to_second)
+    near_core = lax.ppermute(near, "fsdp", SWAP)
+    across_core = lax.ppermute(across, "fsdp", SWAP)
+    corner = 2 * side + lax.axis_index("fsdp")
+    partial = project((tok ^ corner).reshape(1), [near, near_core, across, across_core], out_proj)
+    hidden = picked_residual + partial[0].astype(jnp.float32)
+    for v in (3, 2, 1):
+        hidden = hidden + lax.ppermute(partial[v], "tok", crossed(2, v)).astype(jnp.float32)
+
+    gain_table = norm_gain.astype(jnp.float32)
+    gained = hidden * jnp.where(modality == 0, gain_table[0], gain_table[1])[None, :]
+    router = lax.dynamic_slice_in_dim(router_weight.astype(jnp.float32), first, kind_experts, 1).T
+    router = jnp.where(group == 0, router, router[::-1])
+    slot_router = jnp.repeat(router, capacity, axis=0)
+    squares = jnp.sum(hidden * hidden, axis=1, keepdims=True)
+    logits = jnp.sum(gained * slot_router, axis=1, keepdims=True)
+    lane = lax.broadcasted_iota(jnp.int32, (slots, STAT_COLS), 1)
+    squares_high = lax.reduce_precision(squares, 8, 7)
+    logits_high = lax.reduce_precision(logits, 8, 7)
+    extra = jnp.where(lane == 0, squares_high, 0.0)
+    extra = jnp.where(lane == 1, squares - squares_high, extra)
+    extra = jnp.where(lane == 2, logits_high, extra)
+    extra = jnp.where(lane == 3, logits - logits_high, extra)
+    extra = jnp.where(lane == 4, modality.astype(jnp.float32), extra)
+    packed = jnp.concatenate([gained, extra], axis=1).astype(jnp.bfloat16)
+
+    everyone = jnp.stack([packed] + [lax.ppermute(packed, "tok", crossed(2, v)) for v in (1, 2, 3)])
+    packed_columns = columns + STAT_COLS
+    own = everyone[:, :capacity].reshape(4 * capacity, packed_columns)
+    given = everyone[:, capacity:].reshape(4 * capacity, packed_columns)
+    both_axes = ("groups", "mod")
+    side_far = lax.ppermute(given, both_axes, crossed(2, 3))
+    far = lax.ppermute(given, "groups", SWAP)
+    side_own = lax.ppermute(own, "mod", SWAP)
+    flags = own[:, columns + 4].astype(jnp.float32)
+    half_stat = jnp.concatenate(
+        [
+            own[:, columns:].astype(jnp.float32) + side_own[:, columns:].astype(jnp.float32),
+            far[:, columns:].astype(jnp.float32) + side_far[:, columns:].astype(jnp.float32),
+        ]
+    )
+    stat = half_stat + lax.ppermute(half_stat, "fsdp", SWAP)
+
+    mine = gate_up(side_list, [own, far, side_own, side_far], gate_held, up_held)
+    other = lax.ppermute(mine, "fsdp", SWAP)
+    value = down(side_list, mine, other, stat, down_held)
+
+    half = 4 * capacity
+    from_side_far = lax.ppermute(value[1, half:], both_axes, crossed(2, 3))
+    from_far = lax.ppermute(value[0, half:], "groups", SWAP)
+    from_side = lax.ppermute(value[1, :half], "mod", SWAP)
+    valid = (flags == side.astype(jnp.float32))[:, None]
+    first_expert = jnp.where(valid, value[0, :half], from_side).reshape(4, capacity, columns)
+    second_expert = jnp.where(valid, from_far, from_side_far).reshape(4, capacity, columns)
+    merged = jnp.concatenate([first_expert, second_expert], axis=1)
+    summed = merged[0].astype(jnp.float32)
+    for v in (3, 2, 1):
+        summed = summed + lax.ppermute(merged[v], "tok", crossed(2, v)).astype(jnp.float32)
+    return jnp.dot(
+        pick.astype(jnp.float32).T, summed, precision=lax.Precision.HIGHEST
+    ).astype(jnp.bfloat16)
+
+
 def solution(mesh):
     placed = (
         P(("groups", "tok"), ("fsdp", "mod")),
@@ -169,8 +414,13 @@
         P("mod", "tok", "fsdp"),
     )
     sizes = dict(n_tok=mesh.shape["tok"], n_mod=mesh.shape["mod"], n_fsdp=mesh.shape["fsdp"])
+    paired = (
+        mesh.shape["groups"] == 2
+        and sizes == dict(n_tok=4, n_mod=2, n_fsdp=2)
+    )
+    body = paired_local if paired else functools.partial(local, **sizes)
     return jax.shard_map(
-        functools.partial(local, **sizes),
+        body,
         mesh=mesh,
         in_specs=placed,
         out_specs=P(("groups", "tok"), ("fsdp", "mod")),

time: 110 us -> 96.4 us (0.88)
  matrix products: 38 us -> 2.53 us
  blocking collectives: 26.9 us -> 0 us
  Pallas kernels: 0 us -> 22.7 us
  starting transfers between devices: 12.3 us -> 28.6 us
  local copies, waits for them, and re-layouts: 4.53 us -> 15.1 us
  waiting for transfers between devices: 26 us -> 21.6 us
  other arithmetic: 0.93 us -> 4.36 us
    dot_general x7 -> x3, matrix products: 38 us -> 2.53 us  [the longest x1 1.18 us: paired_local(): jnp.dot(pick.astype(jnp.float32).T, summed, precision=lax.Precision.HIGHEST)]
    all_gather x2 -> x0, blocking collectives: 24.3 us -> none  [the longest x1 15.3 us: spread_context(): return lax.all_gather(swapped, ('mod', 'fsdp'), axis=0, tiled=False)]
    pallas_call x0 -> x6, Pallas kernels: none -> 22.7 us  [the longest x3 12.7 us: keep_on_chip(): pl.pallas_call(keep_kernel, out_shape=pltpu.VMEM(weight.shape[1:], weight...]
    ppermute x13 -> x21, starting transfers between devices: 12.3 us -> 28.6 us  [the longest x1 6.79 us: paired_local(): across = lax.ppermute(picked_context, plane, to_second)]
    unnamed x11 -> x12, local copies, waits for them, and re-layouts: 0.39 us -> 10.8 us
    ppermute x13 -> x21, waiting for transfers between devices: 26 us -> 21.6 us  [the longest x3 4.22 us: paired_local(): lax.ppermute(packed, 'tok', crossed(2, v))]
    psum x1 -> x0, blocking collectives: 2.63 us -> none  [local(): stats = lax.psum(half_stats, 'fsdp')]
    select_n x2 -> x4, other arithmetic: 0.13 us -> 2.4 us  [the longest x1 1 us: paired_local(): jnp.where(valid, value[0, :half], from_side).reshape(4, capacity, columns)]
  transfers between devices with their start and end apart: 13 -> 21, of which waited for: 7 -> 10; matrix products, arithmetic and copies ran while one was open for 1% -> 4% of each run, Pallas kernels for 0% -> 13%
where the time goes in v2:
time: 96.4 us; the launch traced here: 95.9 us
  starting transfers between devices  28.6 us (30%)
  Pallas kernels  22.7 us (24%)
  waiting for transfers between devices  21.6 us (22%)
  local copies, waits for them, and re-layouts  15.1 us (16%)
  other arithmetic  4.36 us (5%)
  matrix products  2.53 us (3%)
  between operations  0.97 us (1%)
    pallas_call x3, Pallas kernels, keep_on_chip(): pl.pallas_call(keep_kernel, out_shape=pltpu.VMEM(weight.shape[1:], weight...  12.7 us
    unnamed x12, local copies, waits for them, and re-layouts  10.8 us
    pallas_call x1, Pallas kernels, gate_up(): pl.pallas_call(gate_up_kernel, out_shape=jax.ShapeDtypeStruct((2, 2 * hal...  7.3 us
    ppermute x1, starting transfers between devices, paired_local(): across = lax.ppermute(picked_context, plane, to_second)  6.79 us
    ppermute x3, starting transfers between devices, paired_local(): lax.ppermute(partial[v], 'tok', crossed(2, v)).astype(jnp.float32)  4.45 us
    ppermute x3, starting transfers between devices, paired_local(): lax.ppermute(merged[v], 'tok', crossed(2, v)).astype(jnp.float32)  4.45 us
    ppermute x3, starting transfers between devices, paired_local(): lax.ppermute(packed, 'tok', crossed(2, v))  4.45 us
    ppermute x3, waiting for transfers between devices, paired_local(): lax.ppermute(packed, 'tok', crossed(2, v))  4.22 us
  transfers between devices with their start and end apart: 21, of which 10 were waited for; matrix products, arithmetic and copies ran while one was open for 4% of the time, Pallas kernels for 13%

profile of v2, /device:TPU:0, one launch (start us, length us, event | category | flops | bytes accessed | tf_op | source)
XLA Modules:
  0.0 95.9 jit_solution(9929974213807807208)
XLA Ops:
  0.7 0.7 constant_dynamic-slice_fusion
  1.4 0.7 broadcast_select_fusion.3
  2.2 0.2 convolution_convert_fusion.1
  2.4 0.7 collective-permute-start
  3.1 6.8 %collective-permute-start.2 = (bf16[32,1024]{1,0:T(8,128)(2,1)S(1)}, bf16[32,1024]{1,0:T(8,128)(2,1)S(1)}, u32[]{:S(2)}, u32[]{:S(2)}) collective-permute-start(bf16[32,1024]{1,0:T(8,128)(2,1)S(1)} %convolution_convert_fusion.1), channel_id=1, source_target_pairs={{0,2},{1,6},{2,10},{3,14},{4,3},{5,7},{6,11},{7,15},{8,0},{9,4},{1... | collective-permute-start | bytes 196616 | tf_op jit(solution)/shard_map/ppermute | solution.py:340
  9.9 1.1 %fusion.20 = f32[32,1024]{1,0:T(8,128)S(1)} fusion(bf16[128,1024]{1,0:T(8,128)(2,1)} %param.10, s32[32]{0:T(128)S(1)} %eq.68), kind=kOutput, calls=%fused_computation.49 | convolution fusion | flops 8392704 | bytes 393344 | tf_op jit(solution)/shard_map/dot_general | solution.py:334
  11.0 0.7 convert_element_type.83
  11.7 0.7 convert_bitcast_fusion
  12.4 0.2 rev.7
  12.6 0.7 broadcast_select_fusion.1
  13.5 2.8 %collective-permute-done.2.refs_2_ = bf16[32,1024]{1,0:T(8,128)(2,1)S(1)} collective-permute-done((bf16[32,1024]{1,0:T(8,128)(2,1)S(1)}, bf16[32,1024]{1,0:T(8,128)(2,1)S(1)}, u32[]{:S(2)}, u32[]{:S(2)}) %collective-permute-start.2) | collective-permute-done | bytes 65568 | tf_op jit(solution)/shard_map/ppermute | solution.py:340
  16.3 1.2 %collective-permute-done.3.refs_3_ = bf16[32,1024]{1,0:T(8,128)(2,1)S(1)} collective-permute-done((bf16[32,1024]{1,0:T(8,128)(2,1)S(1)}, bf16[32,1024]{1,0:T(8,128)(2,1)S(1)}, u32[]{:S(2)}, u32[]{:S(2)}) %collective-permute-start.3) | collective-permute-done | bytes 65568 | tf_op jit(solution)/shard_map/ppermute | solution.py:342
  17.6 1.6 %copy-done.5 = bf16[1024,1024]{1,0:T(8,128)(2,1)S(1)} copy-done((bf16[1024,1024]{1,0:T(8,128)(2,1)S(1)}, bf16[1024,1024]{1,0:T(8,128)(2,1)}, u32[]{:S(2)}) %copy-start.5) | copy-done | bytes 2097176
  19.1 0.5 project.1
  19.6 0.4 collective-permute-start.4
  20.0 1.3 %collective-permute-start.5 = (bf16[32,1024]{1,0:T(8,128)(2,1)S(1)}, bf16[32,1024]{1,0:T(8,128)(2,1)S(1)}, u32[]{:S(2)}, u32[]{:S(2)}) collective-permute-start(bf16[32,1024]{1,0:T(8,128)(2,1)S(1)} %get-tuple-element.19), channel_id=1, source_target_pairs={{0,8},{4,12},{8,0},{12,4},{1,9},{5,13},{9,1},{13,5},{2,10},{6,14},... | collective-permute-start | bytes 196616 | tf_op jit(solution)/shard_map/ppermute | solution.py:347
  21.4 2.7 %collective-permute-start.6 = (bf16[32,1024]{1,0:T(8,128)(2,1)S(1)}, bf16[32,1024]{1,0:T(8,128)(2,1)S(1)}, u32[]{:S(2)}, u32[]{:S(2)}) collective-permute-start(bf16[32,1024]{1,0:T(8,128)(2,1)S(1)} %get-tuple-element.18), channel_id=1, source_target_pairs={{0,4},{4,0},{8,12},{12,8},{1,5},{5,1},{9,13},{13,9},{2,6},{6,2},{1... | collective-permute-start | bytes 196616 | tf_op jit(solution)/shard_map/ppermute | solution.py:347
  24.1 2.4 %collective-permute-done.4 = bf16[32,1024]{1,0:T(8,128)(2,1)S(1)} collective-permute-done((bf16[32,1024]{1,0:T(8,128)(2,1)S(1)}, bf16[32,1024]{1,0:T(8,128)(2,1)S(1)}, u32[]{:S(2)}, u32[]{:S(2)}) %collective-permute-start.4) | collective-permute-done | bytes 65568 | tf_op jit(solution)/shard_map/ppermute | solution.py:347
  26.5 1.3 %collective-permute-done.5 = bf16[32,1024]{1,0:T(8,128)(2,1)S(1)} collective-permute-done((bf16[32,1024]{1,0:T(8,128)(2,1)S(1)}, bf16[32,1024]{1,0:T(8,128)(2,1)S(1)}, u32[]{:S(2)}, u32[]{:S(2)}) %collective-permute-start.5) | collective-permute-done | bytes 65568 | tf_op jit(solution)/shard_map/ppermute | solution.py:347
  28.1 0.6 collective-permute-start.7
  28.7 1.4 %collective-permute-start.8 = (bf16[32,1152]{1,0:T(8,128)(2,1)S(1)}, bf16[32,1152]{1,0:T(8,128)(2,1)S(1)}, u32[]{:S(2)}, u32[]{:S(2)}) collective-permute-start(bf16[32,1152]{1,0:T(8,128)(2,1)S(1)} %pad_maximum_fusion.1), channel_id=1, source_target_pairs={{0,8},{4,12},{8,0},{12,4},{1,9},{5,13},{9,1},{13,5},{2,10},{6,14},... | collective-permute-start | bytes 221192 | tf_op jit(solution)/shard_map/ppermute | solution.py:366
  30.1 2.5 %collective-permute-start.9 = (bf16[32,1152]{1,0:T(8,128)(2,1)S(1)}, bf16[32,1152]{1,0:T(8,128)(2,1)S(1)}, u32[]{:S(2)}, u32[]{:S(2)}) collective-permute-start(bf16[32,1152]{1,0:T(8,128)(2,1)S(1)} %pad_maximum_fusion.1), channel_id=1, source_target_pairs={{0,12},{4,8},{8,4},{12,0},{1,13},{5,9},{9,5},{13,1},{2,14},{6,10},... | collective-permute-start | bytes 221192 | tf_op jit(solution)/shard_map/ppermute | solution.py:366
  32.6 0.3 collective-permute-done.7
  32.8 3.9 %collective-permute-done.8 = bf16[32,1152]{1,0:T(8,128)(2,1)S(1)} collective-permute-done((bf16[32,1152]{1,0:T(8,128)(2,1)S(1)}, bf16[32,1152]{1,0:T(8,128)(2,1)S(1)}, u32[]{:S(2)}, u32[]{:S(2)}) %collective-permute-start.8) | collective-permute-done | bytes 73760 | tf_op jit(solution)/shard_map/ppermute | solution.py:366
  36.9 1.6 %collective-permute-start.10 = (bf16[64,1152]{1,0:T(8,128)(2,1)S(1)}, bf16[64,1152]{1,0:T(8,128)(2,1)S(1)}, u32[]{:S(2)}, u32[]{:S(2)}) collective-permute-start(bf16[64,1152]{1,0:T(8,128)(2,1)S(1)} %bitcast.74), channel_id=1, source_target_pairs={{0,16},{16,0},{1,17},{17,1},{2,18},{18,2},{3,19},{19,3},{4,20},{20... | collective-permute-start | bytes 442376 | tf_op jit(solution)/shard_map/ppermute | solution.py:372
  38.5 1.9 %collective-permute-start.11 = (bf16[64,1152]{1,0:T(8,128)(2,1)S(1)}, bf16[64,1152]{1,0:T(8,128)(2,1)S(1)}, u32[]{:S(2)}, u32[]{:S(2)}) collective-permute-start(bf16[64,1152]{1,0:T(8,128)(2,1)S(1)} %bitcast.63), channel_id=1, source_target_pairs={{0,2},{2,0},{1,3},{3,1},{4,6},{6,4},{5,7},{7,5},{8,10},{10,8},{9,1... | collective-permute-start | bytes 442376 | tf_op jit(solution)/shard_map/ppermute | solution.py:373
  40.4 4.2 %keep_gate.1.gate_ref = bf16[2752,2048]{1,0:T(8,128)(2,1)S(1)} custom-call(s32[1]{0:T(128)} %bitcast.19.index_ref, bf16[2,2752,2048]{2,1,0:T(8,128)(2,1)} %bitcast.67), custom_call_target="tpu_custom_call" | custom-call | bytes 11272192 | tf_op jit(solution)/shard_map/keep_gate/pallas_call | solution.py:177
  44.6 4.2 %keep_up.1.up_ref = bf16[2752,2048]{1,0:T(8,128)(2,1)S(1)} custom-call(s32[1]{0:T(128)} %bitcast.19.index_ref, bf16[2,2752,2048]{2,1,0:T(8,128)(2,1)} %bitcast.68), custom_call_target="tpu_custom_call" | custom-call | bytes 11272192 | tf_op jit(solution)/shard_map/keep_up/pallas_call | solution.py:177
  48.9 7.3 %gate_up.1.mine_ref = bf16[2,128,2752]{2,1,0:T(8,128)(2,1)S(1)} custom-call(s32[1]{0:T(128)} %bitcast.17.side_ref, bf16[64,1152]{1,0:T(8,128)(2,1)S(1)} %bitcast.64, bf16[64,1152]{1,0:T(8,128)(2,1)S(1)} %collective-permute-done.10.far_ref, bf16[64,1152]{1,0:T(8,128)(2,1)S(1)} %collective-permute-done.11.side_own_ref, ...), custom_call_target="tpu_custom_call" | custom-call | flops 2885681152 | bytes 1409024 | tf_op jit(solution)/shard_map/gate_up/pallas_call | solution.py:242
  56.2 1.5 %copy.11 = bf16[2,128,2752]{1,2,0:T(8,128)(2,1)} copy(bf16[2,128,2752]{2,1,0:T(8,128)(2,1)S(1)} %gate_up.1.mine_ref) | data formatting | bytes 2818048 | tf_op jit(solution)/shard_map/gate_up/pallas_call | solution.py:242
  57.8 0.6 collective-permute-start.14
  58.4 4.3 %keep_down.1.weight_ref = bf16[2752,2048]{1,0:T(8,128)(2,1)S(1)} custom-call(s32[1]{0:T(128)} %bitcast.19.index_ref, bf16[2,2752,2048]{2,1,0:T(8,128)(2,1)} %weight_ref.1), custom_call_target="tpu_custom_call" | custom-call | bytes 11272192 | tf_op jit(solution)/shard_map/keep_down/pallas_call | solution.py:177
  62.6 4.2 %copy-done.2 = bf16[2752,2048]{1,0:T(8,128)(2,1)} copy-done((bf16[2752,2048]{1,0:T(8,128)(2,1)}, bf16[2752,2048]{1,0:T(8,128)(2,1)S(1)}, u32[]{:S(2)}) %copy-start.2) | copy-done | bytes 11272216
  66.9 1.7 %copy.12.other_ref = bf16[2,128,2752]{2,1,0:T(8,128)(2,1)S(1)} copy(bf16[2,128,2752]{1,2,0:T(8,128)(2,1)} %collective-permute-done.13) | data formatting | bytes 2818048 | tf_op jit(solution)/shard_map/ppermute | solution.py:384
  68.6 4.2 %copy-done.3 = bf16[2752,2048]{1,0:T(8,128)(2,1)S(1)} copy-done((bf16[2752,2048]{1,0:T(8,128)(2,1)S(1)}, bf16[2752,2048]{1,0:T(8,128)(2,1)}, u32[]{:S(2)}) %copy-start.3) | copy-done | bytes 11272216
  72.8 2.3 %down.1 = bf16[2,128,1024]{2,1,0:T(8,128)(2,1)S(1)} custom-call(s32[1]{0:T(128)} %bitcast.17.side_ref, bf16[2,128,2752]{2,1,0:T(8,128)(2,1)S(1)} %gate_up.1.mine_ref, bf16[2,128,2752]{2,1,0:T(8,128)(2,1)S(1)} %copy.12.other_ref, f32[128,128]{1,0:T(8,128)S(1)} %fusion.26.stat_ref, bf16[2752,2048]{1,0:T(8,128)(2,1)S(1)} %copy-done.3), custom_call_target="tpu_custom_call" | custom-call | flops 1442840576 | bytes 524288 | tf_op jit(solution)/shard_map/down/pallas_call | solution.py:287
  75.0 0.8 copy-done.4
  75.9 2.0 %collective-permute-start.15 = (bf16[64,1024]{1,0:T(8,128)(2,1)S(1)}, bf16[64,1024]{1,0:T(8,128)(2,1)S(1)}, u32[]{:S(2)}, u32[]{:S(2)}) collective-permute-start(bf16[64,1024]{1,0:T(8,128)(2,1)S(1)} %get-tuple-element.9), channel_id=1, source_target_pairs={{0,2},{2,0},{1,3},{3,1},{4,6},{6,4},{5,7},{7,5},{8,10},{10,8},{9,1... | collective-permute-start | bytes 393224 | tf_op jit(solution)/shard_map/ppermute | solution.py:390
  77.9 1.6 %collective-permute-start.16 = (bf16[64,1024]{1,0:T(8,128)(2,1)S(1)}, bf16[64,1024]{1,0:T(8,128)(2,1)S(1)}, u32[]{:S(2)}, u32[]{:S(2)}) collective-permute-start(bf16[64,1024]{1,0:T(8,128)(2,1)S(1)} %get-tuple-element.11), channel_id=1, source_target_pairs={{0,16},{16,0},{1,17},{17,1},{2,18},{18,2},{3,19},{19,3},{4,20},{20... | collective-permute-start | bytes 393224 | tf_op jit(solution)/shard_map/ppermute | solution.py:389
  79.6 2.1 %collective-permute-done.15 = bf16[64,1024]{1,0:T(8,128)(2,1)S(1)} collective-permute-done((bf16[64,1024]{1,0:T(8,128)(2,1)S(1)}, bf16[64,1024]{1,0:T(8,128)(2,1)S(1)}, u32[]{:S(2)}, u32[]{:S(2)}) %collective-permute-start.15) | collective-permute-done | bytes 131104 | tf_op jit(solution)/shard_map/ppermute | solution.py:390
  81.8 4.1 %collective-permute-done.16 = bf16[64,1024]{1,0:T(8,128)(2,1)S(1)} collective-permute-done((bf16[64,1024]{1,0:T(8,128)(2,1)S(1)}, bf16[64,1024]{1,0:T(8,128)(2,1)S(1)}, u32[]{:S(2)}, u32[]{:S(2)}) %collective-permute-start.16) | collective-permute-done | bytes 131104 | tf_op jit(solution)/shard_map/ppermute | solution.py:389
  85.8 1.0 %fusion = (bf16[64,1024]{1,0:T(8,128)(2,1)S(1)}, bf16[64,1024]{1,0:T(8,128)(2,1)S(1)}) fusion(bf16[64,1024]{1,0:T(8,128)(2,1)S(1)} %collective-permute-done.15, bf16[2,128,1024]{2,1,0:T(8,128)(2,1)} %copy-done.4, pred[64]{0:T(512)(128)(4,1)S(1)} %fusion.19, bf16[64,1024]{1,0:T(8,128)(2,1)S(1)} %collective-permute-done.16, ...), kind=kLoop, calls=%fused_computation.13 | loop fusion | flops 131072 | bytes 786496 | tf_op jit(solution)/shard_map/jit(_where)/select_n | solution.py:392
  86.9 1.9 %collective-permute-start.18 = (bf16[32,1024]{1,0:T(8,128)(2,1)S(1)}, bf16[32,1024]{1,0:T(8,128)(2,1)S(1)}, u32[]{:S(2)}, u32[]{:S(2)}) collective-permute-start(bf16[32,1024]{1,0:T(8,128)(2,1)S(1)} %get-tuple-element.14), channel_id=1, source_target_pairs={{0,12},{4,8},{8,4},{12,0},{1,13},{5,9},{9,5},{13,1},{2,14},{6,10},... | collective-permute-start | bytes 196616 | tf_op jit(solution)/shard_map/ppermute | solution.py:397
  88.8 1.0 collective-permute-start.19
  89.7 1.6 %collective-permute-start.20 = (bf16[32,1024]{1,0:T(8,128)(2,1)S(1)}, bf16[32,1024]{1,0:T(8,128)(2,1)S(1)}, u32[]{:S(2)}, u32[]{:S(2)}) collective-permute-start(bf16[32,1024]{1,0:T(8,128)(2,1)S(1)} %get-tuple-element.15), channel_id=1, source_target_pairs={{0,4},{4,0},{8,12},{12,8},{1,5},{5,1},{9,13},{13,9},{2,6},{6,2},{1... | collective-permute-start | bytes 196616 | tf_op jit(solution)/shard_map/ppermute | solution.py:397
  91.3 1.8 %collective-permute-done.18 = bf16[32,1024]{1,0:T(8,128)(2,1)S(1)} collective-permute-done((bf16[32,1024]{1,0:T(8,128)(2,1)S(1)}, bf16[32,1024]{1,0:T(8,128)(2,1)S(1)}, u32[]{:S(2)}, u32[]{:S(2)}) %collective-permute-start.18) | collective-permute-done | bytes 65568 | tf_op jit(solution)/shard_map/ppermute | solution.py:397
  93.1 1.6 %collective-permute-done.19 = bf16[32,1024]{1,0:T(8,128)(2,1)S(1)} collective-permute-done((bf16[32,1024]{1,0:T(8,128)(2,1)S(1)}, bf16[32,1024]{1,0:T(8,128)(2,1)S(1)}, u32[]{:S(2)}, u32[]{:S(2)}) %collective-permute-start.19) | collective-permute-done | bytes 65568 | tf_op jit(solution)/shard_map/ppermute | solution.py:397
  94.7 1.2 %convolution_convert_fusion = bf16[128,1024]{1,0:T(8,128)(2,1)} fusion(bf16[32,1024]{1,0:T(8,128)(2,1)S(1)} %collective-permute-done.20, bf16[32,1024]{1,0:T(8,128)(2,1)S(1)} %collective-permute-done.19, bf16[32,1024]{1,0:T(8,128)(2,1)S(1)} %collective-permute-done.18, bf16[4,16,1024]{2,1,0:T(8,128)(2,1)S(1)} %bitcast.70, ...), kind=kOutput, calls=%fused_computation | convolution fusion | flops 50827264 | bytes 721024 | tf_op jit(solution)/shard_map/dot_general | solution.py:398
  (45 shorter events, 0.9 us)
Async XLA Ops:
  0.0 2.2 %copy-start = (bf16[128,1024]{1,0:T(8,128)(2,1)S(1)}, bf16[128,1024]{1,0:T(8,128)(2,1)}, u32[]{:S(2)}) copy-start(bf16[128,1024]{1,0:T(8,128)(2,1)} %param.11) | copy-start | bytes 786436
  2.4 11.0 %collective-permute-start = (bf16[32,1024]{1,0:T(8,128)(2,1)S(1)}, bf16[32,1024]{1,0:T(8,128)(2,1)S(1)}, u32[]{:S(2)}, u32[]{:S(2)}) collective-permute-start(bf16[32,1024]{1,0:T(8,128)(2,1)S(1)} %convolution_convert_fusion.1), channel_id=1, source_target_pairs={{0,0},{1,4},{2,8},{3,12},{4,1},{5,5},{6,9},{7,13},{8,2},{9,6},{10,... | collective-permute-start | bytes 196616 | tf_op jit(solution)/shard_map/ppermute | solution.py:339
  3.1 13.2 %collective-permute-start.2 = (bf16[32,1024]{1,0:T(8,128)(2,1)S(1)}, bf16[32,1024]{1,0:T(8,128)(2,1)S(1)}, u32[]{:S(2)}, u32[]{:S(2)}) collective-permute-start(bf16[32,1024]{1,0:T(8,128)(2,1)S(1)} %convolution_convert_fusion.1), channel_id=1, source_target_pairs={{0,2},{1,6},{2,10},{3,14},{4,3},{5,7},{6,11},{7,15},{8,0},{9,4},{1... | collective-permute-start | bytes 196616 | tf_op jit(solution)/shard_map/ppermute | solution.py:340
  13.4 2.9 %collective-permute-start.1 = (bf16[32,1024]{1,0:T(8,128)(2,1)S(1)}, bf16[32,1024]{1,0:T(8,128)(2,1)S(1)}, u32[]{:S(2)}, u32[]{:S(2)}) collective-permute-start(bf16[32,1024]{1,0:T(8,128)(2,1)S(1)} %collective-permute-done.refs_0_), channel_id=1, source_target_pairs={{0,1},{1,0},{2,3},{3,2},{4,5},{5,4},{6,7},{7,6},{8,9},{9,8},{10,11... | collective-permute-start | bytes 196616 | tf_op jit(solution)/shard_map/ppermute | solution.py:341
  16.3 1.3 %collective-permute-start.3 = (bf16[32,1024]{1,0:T(8,128)(2,1)S(1)}, bf16[32,1024]{1,0:T(8,128)(2,1)S(1)}, u32[]{:S(2)}, u32[]{:S(2)}) collective-permute-start(bf16[32,1024]{1,0:T(8,128)(2,1)S(1)} %collective-permute-done.2.refs_2_), channel_id=1, source_target_pairs={{0,1},{1,0},{2,3},{3,2},{4,5},{5,4},{6,7},{7,6},{8,9},{9,8},{10,11... | collective-permute-start | bytes 196616 | tf_op jit(solution)/shard_map/ppermute | solution.py:342
  17.6 1.6 %copy-start.5 = (bf16[1024,1024]{1,0:T(8,128)(2,1)S(1)}, bf16[1024,1024]{1,0:T(8,128)(2,1)}, u32[]{:S(2)}) copy-start(bf16[1024,1024]{1,0:T(8,128)(2,1)} %refs_4_.1) | copy-start | bytes 6291460
  19.6 6.9 %collective-permute-start.4 = (bf16[32,1024]{1,0:T(8,128)(2,1)S(1)}, bf16[32,1024]{1,0:T(8,128)(2,1)S(1)}, u32[]{:S(2)}, u32[]{:S(2)}) collective-permute-start(bf16[32,1024]{1,0:T(8,128)(2,1)S(1)} %get-tuple-element.17), channel_id=1, source_target_pairs={{0,12},{4,8},{8,4},{12,0},{1,13},{5,9},{9,5},{13,1},{2,14},{6,10},... | collective-permute-start | bytes 196616 | tf_op jit(solution)/shard_map/ppermute | solution.py:347
  20.0 7.8 %collective-permute-start.5 = (bf16[32,1024]{1,0:T(8,128)(2,1)S(1)}, bf16[32,1024]{1,0:T(8,128)(2,1)S(1)}, u32[]{:S(2)}, u32[]{:S(2)}) collective-permute-start(bf16[32,1024]{1,0:T(8,128)(2,1)S(1)} %get-tuple-element.19), channel_id=1, source_target_pairs={{0,8},{4,12},{8,0},{12,4},{1,9},{5,13},{9,1},{13,5},{2,10},{6,14},... | collective-permute-start | bytes 196616 | tf_op jit(solution)/shard_map/ppermute | solution.py:347
  21.4 6.5 %collective-permute-start.6 = (bf16[32,1024]{1,0:T(8,128)(2,1)S(1)}, bf16[32,1024]{1,0:T(8,128)(2,1)S(1)}, u32[]{:S(2)}, u32[]{:S(2)}) collective-permute-start(bf16[32,1024]{1,0:T(8,128)(2,1)S(1)} %get-tuple-element.18), channel_id=1, source_target_pairs={{0,4},{4,0},{8,12},{12,8},{1,5},{5,1},{9,13},{13,9},{2,6},{6,2},{1... | collective-permute-start | bytes 196616 | tf_op jit(solution)/shard_map/ppermute | solution.py:347
  28.1 4.7 %collective-permute-start.7 = (bf16[32,1152]{1,0:T(8,128)(2,1)S(1)}, bf16[32,1152]{1,0:T(8,128)(2,1)S(1)}, u32[]{:S(2)}, u32[]{:S(2)}) collective-permute-start(bf16[32,1152]{1,0:T(8,128)(2,1)S(1)} %pad_maximum_fusion.1), channel_id=1, source_target_pairs={{0,4},{4,0},{8,12},{12,8},{1,5},{5,1},{9,13},{13,9},{2,6},{6,2},{1... | collective-permute-start | bytes 221192 | tf_op jit(solution)/shard_map/ppermute | solution.py:366
  28.7 8.1 %collective-permute-start.8 = (bf16[32,1152]{1,0:T(8,128)(2,1)S(1)}, bf16[32,1152]{1,0:T(8,128)(2,1)S(1)}, u32[]{:S(2)}, u32[]{:S(2)}) collective-permute-start(bf16[32,1152]{1,0:T(8,128)(2,1)S(1)} %pad_maximum_fusion.1), channel_id=1, source_target_pairs={{0,8},{4,12},{8,0},{12,4},{1,9},{5,13},{9,1},{13,5},{2,10},{6,14},... | collective-permute-start | bytes 221192 | tf_op jit(solution)/shard_map/ppermute | solution.py:366
  30.1 6.7 %collective-permute-start.9 = (bf16[32,1152]{1,0:T(8,128)(2,1)S(1)}, bf16[32,1152]{1,0:T(8,128)(2,1)S(1)}, u32[]{:S(2)}, u32[]{:S(2)}) collective-permute-start(bf16[32,1152]{1,0:T(8,128)(2,1)S(1)} %pad_maximum_fusion.1), channel_id=1, source_target_pairs={{0,12},{4,8},{8,4},{12,0},{1,13},{5,9},{9,5},{13,1},{2,14},{6,10},... | collective-permute-start | bytes 221192 | tf_op jit(solution)/shard_map/ppermute | solution.py:366
  36.9 12.0 %collective-permute-start.10 = (bf16[64,1152]{1,0:T(8,128)(2,1)S(1)}, bf16[64,1152]{1,0:T(8,128)(2,1)S(1)}, u32[]{:S(2)}, u32[]{:S(2)}) collective-permute-start(bf16[64,1152]{1,0:T(8,128)(2,1)S(1)} %bitcast.74), channel_id=1, source_target_pairs={{0,16},{16,0},{1,17},{17,1},{2,18},{18,2},{3,19},{19,3},{4,20},{20... | collective-permute-start | bytes 442376 | tf_op jit(solution)/shard_map/ppermute | solution.py:372
  38.5 10.4 %collective-permute-start.11 = (bf16[64,1152]{1,0:T(8,128)(2,1)S(1)}, bf16[64,1152]{1,0:T(8,128)(2,1)S(1)}, u32[]{:S(2)}, u32[]{:S(2)}) collective-permute-start(bf16[64,1152]{1,0:T(8,128)(2,1)S(1)} %bitcast.63), channel_id=1, source_target_pairs={{0,2},{2,0},{1,3},{3,1},{4,6},{6,4},{5,7},{7,5},{8,10},{10,8},{9,1... | collective-permute-start | bytes 442376 | tf_op jit(solution)/shard_map/ppermute | solution.py:373
  40.4 8.5 %collective-permute-start.12 = (bf16[64,1152]{1,0:T(8,128)(2,1)S(1)}, bf16[64,1152]{1,0:T(8,128)(2,1)S(1)}, u32[]{:S(2)}, u32[]{:S(2)}) collective-permute-start(bf16[64,1152]{1,0:T(8,128)(2,1)S(1)} %bitcast.75), channel_id=1, source_target_pairs={{0,18},{2,16},{16,2},{18,0},{1,19},{3,17},{17,3},{19,1},{4,22},{6,... | collective-permute-start | bytes 442376 | tf_op jit(solution)/shard_map/ppermute | solution.py:371
  57.7 9.1 %collective-permute-start.13 = (bf16[2,128,2752]{1,2,0:T(8,128)(2,1)}, bf16[2,128,2752]{1,2,0:T(8,128)(2,1)}, u32[]{:S(2)}, u32[]{:S(2)}) collective-permute-start(bf16[2,128,2752]{1,2,0:T(8,128)(2,1)} %copy.11), channel_id=1, source_target_pairs={{0,1},{1,0},{2,3},{3,2},{4,5},{5,4},{6,7},{7,6},{8,9},{9,8},{10,11... | collective-permute-start | bytes 4227080 | tf_op jit(solution)/shard_map/ppermute | solution.py:384
  57.8 9.1 %collective-permute-start.14 = (f32[128,128]{1,0:T(8,128)S(1)}, f32[128,128]{1,0:T(8,128)S(1)}, u32[]{:S(2)}, u32[]{:S(2)}) collective-permute-start(f32[128,128]{1,0:T(8,128)S(1)} %pad_maximum_fusion.3), channel_id=1, source_target_pairs={{0,1},{1,0},{2,3},{3,2},{4,5},{5,4},{6,7},{7,6},{8,9},{9,8},{10,11... | collective-permute-start | bytes 196616 | tf_op jit(solution)/shard_map/ppermute | solution.py:381
  58.4 37.5 %copy-start.1 = (bf16[128,1024]{1,0:T(8,128)(2,1)S(1)}, bf16[128,1024]{1,0:T(8,128)(2,1)}, u32[]{:S(2)}) copy-start(bf16[128,1024]{1,0:T(8,128)(2,1)} %param.11) | copy-start | bytes 786436
  62.6 4.2 %copy-start.2 = (bf16[2752,2048]{1,0:T(8,128)(2,1)}, bf16[2752,2048]{1,0:T(8,128)(2,1)S(1)}, u32[]{:S(2)}) copy-start(bf16[2752,2048]{1,0:T(8,128)(2,1)S(1)} %keep_down.1.weight_ref) | copy-start | bytes 33816580
  68.6 4.2 %copy-start.3 = (bf16[2752,2048]{1,0:T(8,128)(2,1)S(1)}, bf16[2752,2048]{1,0:T(8,128)(2,1)}, u32[]{:S(2)}) copy-start(bf16[2752,2048]{1,0:T(8,128)(2,1)} %copy-done.2) | copy-start | bytes 33816580
  75.0 0.8 copy-start.4
  75.9 5.9 %collective-permute-start.15 = (bf16[64,1024]{1,0:T(8,128)(2,1)S(1)}, bf16[64,1024]{1,0:T(8,128)(2,1)S(1)}, u32[]{:S(2)}, u32[]{:S(2)}) collective-permute-start(bf16[64,1024]{1,0:T(8,128)(2,1)S(1)} %get-tuple-element.9), channel_id=1, source_target_pairs={{0,2},{2,0},{1,3},{3,1},{4,6},{6,4},{5,7},{7,5},{8,10},{10,8},{9,1... | collective-permute-start | bytes 393224 | tf_op jit(solution)/shard_map/ppermute | solution.py:390
  77.9 8.0 %collective-permute-start.16 = (bf16[64,1024]{1,0:T(8,128)(2,1)S(1)}, bf16[64,1024]{1,0:T(8,128)(2,1)S(1)}, u32[]{:S(2)}, u32[]{:S(2)}) collective-permute-start(bf16[64,1024]{1,0:T(8,128)(2,1)S(1)} %get-tuple-element.11), channel_id=1, source_target_pairs={{0,16},{16,0},{1,17},{17,1},{2,18},{18,2},{3,19},{19,3},{4,20},{20... | collective-permute-start | bytes 393224 | tf_op jit(solution)/shard_map/ppermute | solution.py:389
  79.5 6.4 %collective-permute-start.17 = (bf16[64,1024]{1,0:T(8,128)(2,1)S(1)}, bf16[64,1024]{1,0:T(8,128)(2,1)S(1)}, u32[]{:S(2)}, u32[]{:S(2)}) collective-permute-start(bf16[64,1024]{1,0:T(8,128)(2,1)S(1)} %get-tuple-element.10), channel_id=1, source_target_pairs={{0,18},{2,16},{16,2},{18,0},{1,19},{3,17},{17,3},{19,1},{4,22},{6,... | collective-permute-start | bytes 393224 | tf_op jit(solution)/shard_map/ppermute | solution.py:388
  86.9 6.2 %collective-permute-start.18 = (bf16[32,1024]{1,0:T(8,128)(2,1)S(1)}, bf16[32,1024]{1,0:T(8,128)(2,1)S(1)}, u32[]{:S(2)}, u32[]{:S(2)}) collective-permute-start(bf16[32,1024]{1,0:T(8,128)(2,1)S(1)} %get-tuple-element.14), channel_id=1, source_target_pairs={{0,12},{4,8},{8,4},{12,0},{1,13},{5,9},{9,5},{13,1},{2,14},{6,10},... | collective-permute-start | bytes 196616 | tf_op jit(solution)/shard_map/ppermute | solution.py:397
  88.8 5.9 %collective-permute-start.19 = (bf16[32,1024]{1,0:T(8,128)(2,1)S(1)}, bf16[32,1024]{1,0:T(8,128)(2,1)S(1)}, u32[]{:S(2)}, u32[]{:S(2)}) collective-permute-start(bf16[32,1024]{1,0:T(8,128)(2,1)S(1)} %get-tuple-element.16), channel_id=1, source_target_pairs={{0,8},{4,12},{8,0},{12,4},{1,9},{5,13},{9,1},{13,5},{2,10},{6,14},... | collective-permute-start | bytes 196616 | tf_op jit(solution)/shard_map/ppermute | solution.py:397
  89.7 5.0 %collective-permute-start.20 = (bf16[32,1024]{1,0:T(8,128)(2,1)S(1)}, bf16[32,1024]{1,0:T(8,128)(2,1)S(1)}, u32[]{:S(2)}, u32[]{:S(2)}) collective-permute-start(bf16[32,1024]{1,0:T(8,128)(2,1)S(1)} %get-tuple-element.15), channel_id=1, source_target_pairs={{0,4},{4,0},{8,12},{12,8},{1,5},{5,1},{9,13},{13,9},{2,6},{6,2},{1... | collective-permute-start | bytes 196616 | tf_op jit(solution)/shard_map/ppermute | solution.py:397

commit v3 on v1

--- a/solution.py
+++ b/solution.py
@@ -3,6 +3,8 @@
 import jax
 import jax.numpy as jnp
 from jax import lax
+from jax.experimental import pallas as pl
+from jax.experimental.pallas import tpu as pltpu
 from jax.sharding import PartitionSpec as P
 
 D = 4096
@@ -155,6 +157,337 @@
     ).astype(jnp.bfloat16)
 
 
+SWAP = [(0, 1), (1, 0)]
+CHUNK = 512
+STRIP = 688
+TILE = 16
+ON_CHIP = pl.BlockSpec(memory_space=pltpu.VMEM)
+SCALARS = pl.BlockSpec(memory_space=pltpu.SMEM)
+IN_HBM = pl.BlockSpec(memory_space=pltpu.HBM)
+ANYWHERE = pl.BlockSpec(memory_space=pl.ANY)
+GROUP, FLIP, SIDE, KIND = range(4)
+
+
+def crossed(bits, flip):
+    return [(i, i ^ flip) for i in range(1 << bits)]
+
+
+def call(kernel, name, outs, specs, args, scratch=(), flops=0, moved=0, limit=8 << 20):
+    return pl.pallas_call(
+        kernel,
+        out_shape=outs,
+        in_specs=specs,
+        out_specs=jax.tree.map(lambda _: ON_CHIP, outs),
+        scratch_shapes=list(scratch),
+        compiler_params=pltpu.CompilerParams(vmem_limit_bytes=limit),
+        cost_estimate=pl.CostEstimate(flops=flops, transcendentals=0, bytes_accessed=moved),
+        name=name,
+    )(*args)
+
+
+def array(*shape, dtype=jnp.bfloat16):
+    return jax.ShapeDtypeStruct(shape, dtype)
+
+
+def keep_kernel(ids_ref, after_ref, *refs):
+    count = (len(refs) - 1) // 2
+    weights, held, semaphores = refs[:count], refs[count : 2 * count], refs[-1]
+    copies = []
+    for n in reversed(range(count)):
+        source = weights[n].at[ids_ref[GROUP]] if n == 0 else weights[n]
+        copies.append(pltpu.make_async_copy(source, held[n], semaphores.at[n]))
+        copies[-1].start()
+    for copy in copies:
+        copy.wait()
+
+
+def keep_on_chip(ids, after, weights, name):
+    weights = [pltpu.with_memory_space_constraint(weight, pltpu.HBM) for weight in weights]
+    shapes = [weight.shape[1:] if n == 0 else weight.shape for n, weight in enumerate(weights)]
+    return call(
+        keep_kernel,
+        name,
+        [pltpu.VMEM(shape, jnp.bfloat16) for shape in shapes],
+        [SCALARS, ANYWHERE] + [IN_HBM] * len(weights),
+        [ids, after] + weights,
+        scratch=[pltpu.SemaphoreType.DMA((len(weights),))],
+        moved=sum(2 * a * b for a, b in shapes),
+        limit=1 << 20,
+    )
+
+
+def select_kernel(ids_ref, rows_ref, context_ref, residual_ref, picked_ref, rest_ref, pick_ref):
+    capacity = rows_ref.shape[1]
+    slots, tokens = pick_ref.shape
+    row = lax.broadcasted_iota(jnp.int32, (slots, tokens), 0)
+    token = lax.broadcasted_iota(jnp.int32, (slots, tokens), 1)
+    wanted = jnp.full((slots, tokens), -1, jnp.int32)
+    for e in range(2):
+        expert = 2 * ids_ref[KIND] + (ids_ref[GROUP] ^ e)
+        for s in range(capacity):
+            wanted = jnp.where(row == e * capacity + s, rows_ref[expert, s], wanted)
+    pick = jnp.where(wanted == token, 1.0, 0.0).astype(jnp.bfloat16)
+    pick_ref[...] = pick
+    picked_ref[...] = jnp.dot(pick, context_ref[...], preferred_element_type=jnp.float32).astype(jnp.bfloat16)
+    rest_ref[...] = jnp.dot(pick, residual_ref[...], preferred_element_type=jnp.float32)
+
+
+def project_kernel(ids_ref, *refs):
+    block_refs, weight_ref, out_ref, rows_ref = refs[:4], refs[4], refs[6], refs[7]
+    slots = block_refs[0].shape[0]
+    for u, block_ref in enumerate(block_refs):
+        rows_ref[u * slots : (u + 1) * slots, :] = block_ref[...]
+    product = jnp.dot(rows_ref[...], weight_ref[...], preferred_element_type=jnp.float32)
+    product = product.astype(jnp.bfloat16)
+    for u in range(len(block_refs)):
+        out_ref[ids_ref[FLIP] ^ u] = product[u * slots : (u + 1) * slots, :]
+
+
+def split_high_low(value):
+    high = value.astype(jnp.bfloat16).astype(jnp.float32)
+    return high, value - high
+
+
+def norm_kernel(ids_ref, rest_ref, partial_ref, one_ref, two_ref, three_ref, gain_ref, router_ref, _, out_ref):
+    slots, columns = rest_ref.shape
+    hidden = rest_ref[...] + partial_ref[0].astype(jnp.float32)
+    for got_ref in (three_ref, two_ref, one_ref):
+        hidden = hidden + got_ref[...].astype(jnp.float32)
+    gains = gain_ref[...].astype(jnp.float32)
+    gained = hidden * jnp.where(ids_ref[KIND] == 0, gains[0:1], gains[1:2])
+    out_ref[:, :columns] = gained.astype(jnp.bfloat16)
+    table = router_ref[...].astype(jnp.float32)
+    pieces = []
+    for e in range(2):
+        expert = 2 * ids_ref[KIND] + (ids_ref[GROUP] ^ e)
+        weights = table[0:1]
+        for k in range(1, table.shape[0]):
+            weights = jnp.where(expert == k, table[k : k + 1], weights)
+        half = slots // 2
+        pieces.append(jnp.sum(gained[e * half : (e + 1) * half] * weights, axis=1, keepdims=True))
+    logits = jnp.concatenate(pieces, axis=0)
+    squares = jnp.sum(hidden * hidden, axis=1, keepdims=True)
+    lane = lax.broadcasted_iota(jnp.int32, (slots, STAT_COLS), 1)
+    extra = jnp.where(lane == 4, ids_ref[KIND].astype(jnp.float32), 0.0)
+    for at, stat in enumerate(split_high_low(squares) + split_high_low(logits)):
+        extra = jnp.where(lane == at, stat, extra)
+    out_ref[:, columns:] = extra.astype(jnp.bfloat16)
+
+
+def arrange_kernel(zero_ref, one_ref, two_ref, three_ref, _, own_ref, given_ref):
+    half = zero_ref.shape[0] // 2
+    for v, ref in enumerate((zero_ref, one_ref, two_ref, three_ref)):
+        own_ref[v * half : (v + 1) * half, :] = ref[:half, :]
+        given_ref[v * half : (v + 1) * half, :] = ref[half:, :]
+
+
+def weight_times_rows(weight_ref, rows, out_ref):
+    units = weight_ref.shape[0]
+    for start in range(0, units, STRIP):
+        stop = min(start + STRIP, units)
+        out_ref[start:stop, :] = lax.dot_general(
+            weight_ref[start:stop, :], rows, (((1,), (1,)), ((), ())), preferred_element_type=jnp.float32
+        ).astype(jnp.bfloat16)
+
+
+def gate_kernel(ids_ref, own_ref, far_ref, side_own_ref, side_far_ref, weight_ref, out_ref, rows_ref):
+    half = own_ref.shape[0]
+    units, width = weight_ref.shape
+    columns = width // 2
+    for side in range(2):
+
+        @pl.when(ids_ref[SIDE] == side)
+        def _():
+            here, there = side * columns, (1 - side) * columns
+            rows_ref[:half, here : here + columns] = own_ref[:, :columns]
+            rows_ref[half:, here : here + columns] = far_ref[:, :columns]
+            rows_ref[:half, there : there + columns] = side_own_ref[:, :columns]
+            rows_ref[half:, there : there + columns] = side_far_ref[:, :columns]
+
+    weight_times_rows(weight_ref, rows_ref[...], out_ref)
+    tails = [ref[:, columns:].astype(jnp.float32) for ref in (own_ref, side_own_ref, far_ref, side_far_ref)]
+    stat = jnp.concatenate([tails[0] + tails[1], tails[2] + tails[3]], axis=0).T
+    squares = stat[0:1] + stat[1:2]
+    logits = stat[2:3] + stat[3:4]
+    at_row = lax.broadcasted_iota(jnp.int32, (TILE, 2 * half), 0)
+    extra = jnp.zeros((TILE, 2 * half), jnp.float32)
+    for at, piece in enumerate(split_high_low(squares) + split_high_low(logits)):
+        extra = jnp.where(at_row == at, piece, extra)
+    out_ref[units:, :] = extra.astype(jnp.bfloat16)
+
+
+def up_kernel(rows_ref, weight_ref, out_ref):
+    weight_times_rows(weight_ref, rows_ref[...], out_ref)
+
+
+def down_kernel(ids_ref, gate_ref, gate_other_ref, up_ref, up_other_ref, weight_ref, *refs):
+    out_refs, act_ref = refs[:4], refs[4]
+    units, width = weight_ref.shape
+    rows = act_ref.shape[1]
+    stat = gate_ref[units:, :].astype(jnp.float32) + gate_other_ref[units:, :].astype(jnp.float32)
+    inverse = lax.rsqrt((stat[0:1] + stat[1:2]) / D + 1e-05)
+    logits = (stat[2:3] + stat[3:4]) * inverse
+    score = 1.0 / (1.0 + jnp.exp(-logits))
+    score = jnp.broadcast_to(score, (rows, rows)).T[:, 0:1]
+    for start in range(0, units, STRIP):
+        stop = min(start + STRIP, units)
+        gate = gate_ref[start:stop, :].astype(jnp.float32) + gate_other_ref[start:stop, :].astype(jnp.float32)
+        up = up_ref[start:stop, :].astype(jnp.float32) + up_other_ref[start:stop, :].astype(jnp.float32)
+        gate, up = gate * inverse, up * inverse
+        act_ref[start:stop, :] = (gate / (1.0 + jnp.exp(-gate)) * up).astype(jnp.bfloat16)
+    columns = width // 2
+    half = rows // 2
+    for start in range(0, width, CHUNK):
+        value = lax.dot_general(
+            act_ref[...], weight_ref[:, start : start + CHUNK], (((0,), (0,)), ((), ())),
+            preferred_element_type=jnp.float32,
+        )
+        value = (value * score).astype(jnp.bfloat16)
+        quarter, at = divmod(start, columns)
+        for across in range(2):
+
+            @pl.when((ids_ref[SIDE] ^ quarter) == across)
+            def _():
+                out_refs[2 * across][:, at : at + CHUNK] = value[:half]
+                out_refs[2 * across + 1][:, at : at + CHUNK] = value[half:]
+
+
+def merge_kernel(ids_ref, own_ref, kept_ref, side_ref, far_ref, side_far_ref, *out_refs):
+    half, columns = kept_ref.shape
+    capacity = half // len(out_refs)
+    side = ids_ref[SIDE].astype(jnp.float32)
+    for v, out_ref in enumerate(out_refs):
+        span = slice(v * capacity, (v + 1) * capacity)
+        valid = own_ref[span, columns : columns + STAT_COLS].astype(jnp.float32)[:, 4:5] == side
+        for e, (mine, other) in enumerate(((kept_ref, side_ref), (far_ref, side_far_ref))):
+            chosen = jnp.where(valid, mine[span, :].astype(jnp.float32), other[span, :].astype(jnp.float32))
+            out_ref[e * capacity : (e + 1) * capacity, :] = chosen.astype(jnp.bfloat16)
+
+
+def scatter_kernel(pick_ref, zero_ref, one_ref, two_ref, three_ref, out_ref):
+    total = zero_ref[...].astype(jnp.float32)
+    for got_ref in (three_ref, two_ref, one_ref):
+        total = total + got_ref[...].astype(jnp.float32)
+    high, rest = split_high_low(total)
+    middle, low = split_high_low(rest)
+    result = 0.0
+    for piece in (low, middle, high):
+        result = result + lax.dot_general(
+            pick_ref[...], piece.astype(jnp.bfloat16), (((0,), (0,)), ((), ())),
+            preferred_element_type=jnp.float32,
+        )
+    out_ref[...] = result.astype(jnp.bfloat16)
+
+
+def paired_local(
+    residual,
+    context,
+    out_proj,
+    norm_gain,
+    router_weight,
+    block_modality,
+    expert_rows,
+    gate_weight,
+    up_weight,
+    down_weight,
+):
+    tokens, columns = residual.shape
+    experts, capacity = expert_rows.shape
+    slots = 2 * capacity
+    half = 4 * capacity
+    rows = 2 * half
+    units, width = down_weight.shape[1:]
+    assert block_modality.shape == (1,) and experts == 4 and gate_weight.shape[0] == 2
+    tok, side = lax.axis_index("tok"), lax.axis_index("mod")
+    corner = 2 * side + lax.axis_index("fsdp")
+    ids = jnp.stack([lax.axis_index("groups"), tok ^ corner, side, block_modality[0]])
+
+    picked, rest, pick = call(
+        select_kernel,
+        "select",
+        [array(slots, columns), array(slots, columns, dtype=jnp.float32), array(slots, tokens)],
+        [SCALARS, SCALARS, ON_CHIP, ON_CHIP],
+        [ids, expert_rows, context, residual],
+    )
+    plane = ("tok", "mod", "fsdp")
+    to_first = [(t * 4 + q, q * 4 + t) for t in range(4) for q in range(4)]
+    to_second = [(t * 4 + q, q * 4 + (t ^ 2)) for t in range(4) for q in range(4)]
+    near = lax.ppermute(picked, plane, to_first)
+    across = lax.ppermute(picked, plane, to_second)
+    near_core = lax.ppermute(near, "fsdp", SWAP)
+    across_core = lax.ppermute(across, "fsdp", SWAP)
+    gate_held, proj_held = keep_on_chip(ids, picked, [gate_weight.swapaxes(1, 2), out_proj], "keep_gate")
+    partial = call(
+        project_kernel,
+        "project",
+        array(4, slots, columns),
+        [SCALARS] + [ON_CHIP] * 6,
+        [ids, near, near_core, across, across_core, proj_held, gate_held],
+        scratch=[pltpu.VMEM((rows, columns), jnp.bfloat16)],
+    )
+    sums = [lax.ppermute(partial[v], "tok", crossed(2, v)) for v in (1, 2, 3)]
+    (up_held,) = keep_on_chip(ids, partial, [up_weight.swapaxes(1, 2)], "keep_up")
+    packed_columns = columns + STAT_COLS
+    packed = call(
+        norm_kernel,
+        "norm",
+        array(slots, packed_columns),
+        [SCALARS] + [ON_CHIP] * 8,
+        [ids, rest, partial, *sums, norm_gain, router_weight.T, up_held],
+    )
+    others = [lax.ppermute(packed, "tok", crossed(2, v)) for v in (1, 2, 3)]
+    (down_held,) = keep_on_chip(ids, packed, [down_weight], "keep_down")
+    own, given = call(
+        arrange_kernel,
+        "arrange",
+        [array(half, packed_columns)] * 2,
+        [ON_CHIP] * 5,
+        [packed, *others, down_held],
+    )
+    both_axes = ("groups", "mod")
+    side_far = lax.ppermute(given, both_axes, crossed(2, 3))
+    far = lax.ppermute(given, "groups", SWAP)
+    side_own = lax.ppermute(own, "mod", SWAP)
+
+    flops = 2 * rows * units * width
+    gate, gathered = call(
+        gate_kernel,
+        "gate",
+        [array(units + TILE, rows), array(rows, width)],
+        [SCALARS] + [ON_CHIP] * 5,
+        [ids, own, far, side_own, side_far, gate_held],
+        flops=flops,
+    )
+    up = call(
+        up_kernel, "up", array(units, rows), [ON_CHIP] * 2, [gathered, up_held], flops=flops
+    )
+    gate_other = lax.ppermute(gate, "fsdp", SWAP)
+    up_other = lax.ppermute(up, "fsdp", SWAP)
+    kept, to_far, to_side, to_side_far = call(
+        down_kernel,
+        "down",
+        [array(half, columns)] * 4,
+        [SCALARS] + [ON_CHIP] * 5,
+        [ids, gate, gate_other, up, up_other, down_held],
+        scratch=[pltpu.VMEM((units, rows), jnp.bfloat16)],
+        flops=flops,
+    )
+    from_side_far = lax.ppermute(to_side_far, both_axes, crossed(2, 3))
+    from_far = lax.ppermute(to_far, "groups", SWAP)
+    from_side = lax.ppermute(to_side, "mod", SWAP)
+    merged = call(
+        merge_kernel,
+        "merge",
+        [array(slots, columns)] * 4,
+        [SCALARS] + [ON_CHIP] * 5,
+        [ids, own, kept, from_side, from_far, from_side_far],
+    )
+    values = [merged[0]] + [lax.ppermute(merged[v], "tok", crossed(2, v)) for v in (1, 2, 3)]
+    return call(
+        scatter_kernel, "scatter", array(tokens, columns), [ON_CHIP] * 5, [pick, *values]
+    )
+
+
 def solution(mesh):
     placed = (
         P(("groups", "tok"), ("fsdp", "mod")),
@@ -169,8 +502,13 @@
         P("mod", "tok", "fsdp"),
     )
     sizes = dict(n_tok=mesh.shape["tok"], n_mod=mesh.shape["mod"], n_fsdp=mesh.shape["fsdp"])
+    paired = (
+        mesh.shape["groups"] == 2
+        and sizes == dict(n_tok=4, n_mod=2, n_fsdp=2)
+    )
+    body = paired_local if paired else functools.partial(local, **sizes)
     return jax.shard_map(
-        functools.partial(local, **sizes),
+        body,
         mesh=mesh,
         in_specs=placed,
         out_specs=P(("groups", "tok"), ("fsdp", "mod")),

time: 110 us -> 85 us (0.77)
  matrix products: 38 us -> 0 us
  Pallas kernels: 0 us -> 29.7 us
  blocking collectives: 26.9 us -> 0 us
  starting transfers between devices: 12.3 us -> 29 us
  waiting for transfers between devices: 26 us -> 22.6 us
  local copies, waits for them, and re-layouts: 4.53 us -> 2.6 us
    dot_general x7 -> x0, matrix products: 38 us -> none  [the longest x1 12.2 us: local(): jnp.einsum('esf,efd->esd', activation, down_weight, preferred_element_typ...]
    pallas_call x0 -> x12, Pallas kernels: none -> 29.7 us  [call(): pl.pallas_call(kernel, out_shape=outs, in_specs=specs, out_specs=jax.tree...]
    all_gather x2 -> x0, blocking collectives: 24.3 us -> none  [the longest x1 15.3 us: spread_context(): return lax.all_gather(swapped, ('mod', 'fsdp'), axis=0, tiled=False)]
    ppermute x13 -> x21, starting transfers between devices: 12.3 us -> 29 us  [the longest x3 5.4 us: paired_local(): sums = [lax.ppermute(partial[v], 'tok', crossed(2, v)) for v in (1, 2, 3)]]
    ppermute x13 -> x21, waiting for transfers between devices: 26 us -> 22.6 us  [the longest x1 4.66 us: paired_local(): across = lax.ppermute(picked, plane, to_second)]
    psum x1 -> x0, blocking collectives: 2.63 us -> none  [local(): stats = lax.psum(half_stats, 'fsdp')]
    unnamed x11 -> x10, local copies, waits for them, and re-layouts: 0.39 us -> 2.59 us
    dynamic_slice x2 -> x0, local copies, waits for them, and re-layouts: 1.78 us -> none  [the longest x1 1.09 us: local(): kept = lax.dynamic_index_in_dim(value, mod_index, 3, False)]
  transfers between devices with their start and end apart: 13 -> 21, of which waited for: 7 -> 10; matrix products, arithmetic and copies ran while one was open for 1% -> 0% of each run, Pallas kernels for 0% -> 21%
where the time goes in v3:
time: 85 us; the launch traced here: 84.8 us
  Pallas kernels  29.7 us (35%)
  starting transfers between devices  29 us (34%)
  waiting for transfers between devices  22.6 us (27%)
  local copies, waits for them, and re-layouts  2.6 us (3%)
    pallas_call x12, Pallas kernels, call(): pl.pallas_call(kernel, out_shape=outs, in_specs=specs, out_specs=jax.tree...  29.7 us
    ppermute x3, starting transfers between devices, paired_local(): sums = [lax.ppermute(partial[v], 'tok', crossed(2, v)) for v in (1, 2, 3)]  5.4 us
    ppermute x1, starting transfers between devices, paired_local(): side_far = lax.ppermute(given, both_axes, crossed(2, 3))  4.84 us
    ppermute x1, waiting for transfers between devices, paired_local(): across = lax.ppermute(picked, plane, to_second)  4.66 us
    ppermute x3, starting transfers between devices, paired_local(): lax.ppermute(merged[v], 'tok', crossed(2, v))  4.45 us
    ppermute x3, starting transfers between devices, paired_local(): others = [lax.ppermute(packed, 'tok', crossed(2, v)) for v in (1, 2, 3)]  4.44 us
    ppermute x1, waiting for transfers between devices, paired_local(): from_far = lax.ppermute(to_far, 'groups', SWAP)  4.17 us
    ppermute x3, waiting for transfers between devices, paired_local(): lax.ppermute(merged[v], 'tok', crossed(2, v))  3.88 us
  transfers between devices with their start and end apart: 21, of which 10 were waited for; matrix products, arithmetic and copies ran while one was open for 0% of the time, Pallas kernels for 21%

profile of v3, /device:TPU:0, one launch (start us, length us, event | category | flops | bytes accessed | tf_op | source)
XLA Modules:
  0.0 84.8 jit_solution(2959501338127761891)
XLA Ops:
  0.7 0.1 pad_add_fusion.ids_ref
  0.7 0.9 %copy-done = bf16[128,1024]{1,0:T(8,128)(2,1)S(1)} copy-done((bf16[128,1024]{1,0:T(8,128)(2,1)S(1)}, bf16[128,1024]{1,0:T(8,128)(2,1)}, u32[]{:S(2)}) %copy-start) | copy-done | bytes 262168
  1.7 0.9 %copy-done.1 = bf16[128,1024]{1,0:T(8,128)(2,1)S(1)} copy-done((bf16[128,1024]{1,0:T(8,128)(2,1)S(1)}, bf16[128,1024]{1,0:T(8,128)(2,1)}, u32[]{:S(2)}) %copy-start.1) | copy-done | bytes 262168
  2.6 0.7 copy-done.4
  3.3 0.7 select.1
  4.1 3.0 %collective-permute-start.2 = (bf16[32,1024]{1,0:T(8,128)(2,1)S(1)}, bf16[32,1024]{1,0:T(8,128)(2,1)S(1)}, u32[]{:S(2)}, u32[]{:S(2)}) collective-permute-start(bf16[32,1024]{1,0:T(8,128)(2,1)S(1)} %get-tuple-element.24.after_ref), channel_id=1, source_target_pairs={{0,2},{1,6},{2,10},{3,14},{4,3},{5,7},{6,11},{7,15},{8,0},{9,4},{1... | collective-permute-start | bytes 196616 | tf_op jit(solution)/shard_map/ppermute | solution.py:416
  7.1 0.7 collective-permute-start
  7.7 4.7 %collective-permute-done.2.refs_2_ = bf16[32,1024]{1,0:T(8,128)(2,1)S(1)} collective-permute-done((bf16[32,1024]{1,0:T(8,128)(2,1)S(1)}, bf16[32,1024]{1,0:T(8,128)(2,1)S(1)}, u32[]{:S(2)}, u32[]{:S(2)}) %collective-permute-start.2) | collective-permute-done | bytes 65568 | tf_op jit(solution)/shard_map/ppermute | solution.py:416
  12.4 1.4 %collective-permute-start.1 = (bf16[32,1024]{1,0:T(8,128)(2,1)S(1)}, bf16[32,1024]{1,0:T(8,128)(2,1)S(1)}, u32[]{:S(2)}, u32[]{:S(2)}) collective-permute-start(bf16[32,1024]{1,0:T(8,128)(2,1)S(1)} %collective-permute-done.refs_0_), channel_id=1, source_target_pairs={{0,1},{1,0},{2,3},{3,2},{4,5},{5,4},{6,7},{7,6},{8,9},{9,8},{10,11... | collective-permute-start | bytes 196616 | tf_op jit(solution)/shard_map/ppermute | solution.py:417
  13.8 5.4 %keep_gate.1 = (bf16[2752,2048]{1,0:T(8,128)(2,1)S(1)}, bf16[1024,1024]{1,0:T(8,128)(2,1)S(1)}) custom-call(s32[4]{0:T(128)S(1)} %pad_add_fusion.ids_ref, bf16[32,1024]{1,0:T(8,128)(2,1)S(1)} %get-tuple-element.24.after_ref, bf16[2,2752,2048]{2,1,0:T(8,128)(2,1)} %bitcast.13, bf16[1024,1024]{1,0:T(8,128)(2,1)} %refs_1_.1), custom_call_target="tpu_custom_call" | custom-call | bytes 13369344 | tf_op jit(solution)/shard_map/keep_gate/pallas_call | solution.py:176
  19.2 0.0 collective-permute-done.3.refs_3_
  19.2 1.0 %project.1.after_ref.partial_ref = bf16[4,32,1024]{2,1,0:T(8,128)(2,1)S(1)} custom-call(s32[4]{0:T(128)S(1)} %pad_add_fusion.ids_ref, bf16[32,1024]{1,0:T(8,128)(2,1)S(1)} %collective-permute-done.refs_0_, bf16[32,1024]{1,0:T(8,128)(2,1)S(1)} %collective-permute-done.1.refs_1_, bf16[32,1024]{1,0:T(8,128)(2,1)S(1)} %collective-permute-done.2.refs_2_, ...), custom_call_target="tpu_custom_call" | custom-call | tf_op jit(solution)/shard_map/project/pallas_call | solution.py:176
  20.2 4.8 %collective-permute-start.6 = (bf16[32,1024]{1,0:T(8,128)(2,1)S(1)}, bf16[32,1024]{1,0:T(8,128)(2,1)S(1)}, u32[]{:S(2)}, u32[]{:S(2)}) collective-permute-start(bf16[32,1024]{1,0:T(8,128)(2,1)S(1)} %get-tuple-element.39), channel_id=1, source_target_pairs={{0,12},{4,8},{8,4},{12,0},{1,13},{5,9},{9,5},{13,1},{2,14},{6,10},... | collective-permute-start | bytes 196616 | tf_op jit(solution)/shard_map/ppermute | solution.py:428
  25.0 0.0 collective-permute-start.5
  25.0 0.6 collective-permute-start.4
  25.6 4.8 %keep_up.1._.weight_ref = bf16[2752,2048]{1,0:T(8,128)(2,1)S(1)} custom-call(s32[4]{0:T(128)S(1)} %pad_add_fusion.ids_ref, bf16[4,32,1024]{2,1,0:T(8,128)(2,1)S(1)} %project.1.after_ref.partial_ref, bf16[2,2752,2048]{2,1,0:T(8,128)(2,1)} %bitcast.14), custom_call_target="tpu_custom_call" | custom-call | bytes 11272192 | tf_op jit(solution)/shard_map/keep_up/pallas_call | solution.py:176
  30.4 0.0 collective-permute-done.6.three_ref
  30.4 0.2 collective-permute-done.5.two_ref
  30.6 0.8 norm.1.after_ref.zero_ref
  31.3 3.7 %collective-permute-start.9 = (bf16[32,1152]{1,0:T(8,128)(2,1)S(1)}, bf16[32,1152]{1,0:T(8,128)(2,1)S(1)}, u32[]{:S(2)}, u32[]{:S(2)}) collective-permute-start(bf16[32,1152]{1,0:T(8,128)(2,1)S(1)} %norm.1.after_ref.zero_ref), channel_id=1, source_target_pairs={{0,12},{4,8},{8,4},{12,0},{1,13},{5,9},{9,5},{13,1},{2,14},{6,10},... | collective-permute-start | bytes 221192 | tf_op jit(solution)/shard_map/ppermute | solution.py:438
  35.0 0.0 collective-permute-start.8
  35.0 0.8 collective-permute-start.7
  35.8 4.8 %keep_down.1._.weight_ref = bf16[2752,2048]{1,0:T(8,128)(2,1)S(1)} custom-call(s32[4]{0:T(128)S(1)} %pad_add_fusion.ids_ref, bf16[32,1152]{1,0:T(8,128)(2,1)S(1)} %norm.1.after_ref.zero_ref, bf16[2,2752,2048]{2,1,0:T(8,128)(2,1)} %refs_0_.1), custom_call_target="tpu_custom_call" | custom-call | bytes 11272192 | tf_op jit(solution)/shard_map/keep_down/pallas_call | solution.py:176
  40.5 0.0 collective-permute-done.9.three_ref
  40.5 0.6 collective-permute-done.8.two_ref
  41.2 4.8 %collective-permute-start.12 = (bf16[64,1152]{1,0:T(8,128)(2,1)S(1)}, bf16[64,1152]{1,0:T(8,128)(2,1)S(1)}, u32[]{:S(2)}, u32[]{:S(2)}) collective-permute-start(bf16[64,1152]{1,0:T(8,128)(2,1)S(1)} %get-tuple-element.28), channel_id=1, source_target_pairs={{0,18},{2,16},{16,2},{18,0},{1,19},{3,17},{17,3},{19,1},{4,22},{6,... | collective-permute-start | bytes 442376 | tf_op jit(solution)/shard_map/ppermute | solution.py:448
  46.0 0.3 collective-permute-start.10
  46.3 0.3 collective-permute-start.11
  46.7 3.8 %collective-permute-done.12.side_far_ref = bf16[64,1152]{1,0:T(8,128)(2,1)S(1)} collective-permute-done((bf16[64,1152]{1,0:T(8,128)(2,1)S(1)}, bf16[64,1152]{1,0:T(8,128)(2,1)S(1)}, u32[]{:S(2)}, u32[]{:S(2)}) %collective-permute-start.12) | collective-permute-done | bytes 147488 | tf_op jit(solution)/shard_map/ppermute | solution.py:448
  50.4 1.2 %collective-permute-done.10.far_ref = bf16[64,1152]{1,0:T(8,128)(2,1)S(1)} collective-permute-done((bf16[64,1152]{1,0:T(8,128)(2,1)S(1)}, bf16[64,1152]{1,0:T(8,128)(2,1)S(1)}, u32[]{:S(2)}, u32[]{:S(2)}) %collective-permute-start.10) | collective-permute-done | bytes 147488 | tf_op jit(solution)/shard_map/ppermute | solution.py:449
  51.6 3.6 %gate.1 = (bf16[2768,128]{1,0:T(8,128)(2,1)S(1)}, bf16[128,2048]{1,0:T(8,128)(2,1)S(1)}) custom-call(s32[4]{0:T(128)S(1)} %pad_add_fusion.ids_ref, bf16[64,1152]{1,0:T(8,128)(2,1)S(1)} %get-tuple-element.27.own_ref, bf16[64,1152]{1,0:T(8,128)(2,1)S(1)} %collective-permute-done.10.far_ref, bf16[64,1152]{1,0:T(8,128)(2,1)S(1)} %collective-permute-done.11.side_own_ref, ...), custom_call_target="tpu_custom_call" | custom-call | flops 1442840576 | tf_op jit(solution)/shard_map/gate/pallas_call | solution.py:176
  55.3 0.1 collective-permute-start.13
  55.3 3.1 %up.1.up_ref = bf16[2752,128]{1,0:T(8,128)(2,1)S(1)} custom-call(bf16[128,2048]{1,0:T(8,128)(2,1)S(1)} %get-tuple-element.30.rows_ref, bf16[2752,2048]{1,0:T(8,128)(2,1)S(1)} %keep_up.1._.weight_ref), custom_call_target="tpu_custom_call" | custom-call | flops 1442840576 | tf_op jit(solution)/shard_map/up/pallas_call | solution.py:176
  58.4 0.6 collective-permute-start.14
  59.0 1.8 %collective-permute-done.14.up_other_ref = bf16[2752,128]{1,0:T(8,128)(2,1)S(1)} collective-permute-done((bf16[2752,128]{1,0:T(8,128)(2,1)S(1)}, bf16[2752,128]{1,0:T(8,128)(2,1)S(1)}, u32[]{:S(2)}, u32[]{:S(2)}) %collective-permute-start.14) | collective-permute-done | bytes 704544 | tf_op jit(solution)/shard_map/ppermute | solution.py:465
  60.8 3.8 %down.1 = (bf16[64,1024]{1,0:T(8,128)(2,1)S(1)}, bf16[64,1024]{1,0:T(8,128)(2,1)S(1)}, bf16[64,1024]{1,0:T(8,128)(2,1)S(1)}, bf16[64,1024]{1,0:T(8,128)(2,1)S(1)}) custom-call(s32[4]{0:T(128)S(1)} %pad_add_fusion.ids_ref, bf16[2768,128]{1,0:T(8,128)(2,1)S(1)} %get-tuple-element.29.gate_ref, bf16[2768,128]{1,0:T(8,128)(2,1)S(1)} %collective-permute-done.13.gate_other_ref, ...), custom_call_target="tpu_custom_call" | custom-call | flops 1442840576 | tf_op jit(solution)/shard_map/down/pallas_call | solution.py:176
  64.5 1.8 %collective-permute-start.15 = (bf16[64,1024]{1,0:T(8,128)(2,1)S(1)}, bf16[64,1024]{1,0:T(8,128)(2,1)S(1)}, u32[]{:S(2)}, u32[]{:S(2)}) collective-permute-start(bf16[64,1024]{1,0:T(8,128)(2,1)S(1)} %get-tuple-element.32), channel_id=1, source_target_pairs={{0,2},{2,0},{1,3},{3,1},{4,6},{6,4},{5,7},{7,5},{8,10},{10,8},{9,1... | collective-permute-start | bytes 393224 | tf_op jit(solution)/shard_map/ppermute | solution.py:477
  66.4 0.6 collective-permute-start.16
  66.9 1.2 %collective-permute-start.17 = (bf16[64,1024]{1,0:T(8,128)(2,1)S(1)}, bf16[64,1024]{1,0:T(8,128)(2,1)S(1)}, u32[]{:S(2)}, u32[]{:S(2)}) collective-permute-start(bf16[64,1024]{1,0:T(8,128)(2,1)S(1)} %get-tuple-element.34), channel_id=1, source_target_pairs={{0,18},{2,16},{16,2},{18,0},{1,19},{3,17},{17,3},{19,1},{4,22},{6,... | collective-permute-start | bytes 393224 | tf_op jit(solution)/shard_map/ppermute | solution.py:475
  68.1 2.4 %collective-permute-done.15.side_ref = bf16[64,1024]{1,0:T(8,128)(2,1)S(1)} collective-permute-done((bf16[64,1024]{1,0:T(8,128)(2,1)S(1)}, bf16[64,1024]{1,0:T(8,128)(2,1)S(1)}, u32[]{:S(2)}, u32[]{:S(2)}) %collective-permute-start.15) | collective-permute-done | bytes 131104 | tf_op jit(solution)/shard_map/ppermute | solution.py:477
  70.5 4.2 %collective-permute-done.16.far_ref = bf16[64,1024]{1,0:T(8,128)(2,1)S(1)} collective-permute-done((bf16[64,1024]{1,0:T(8,128)(2,1)S(1)}, bf16[64,1024]{1,0:T(8,128)(2,1)S(1)}, u32[]{:S(2)}, u32[]{:S(2)}) %collective-permute-start.16) | collective-permute-done | bytes 131104 | tf_op jit(solution)/shard_map/ppermute | solution.py:476
  74.6 0.7 merge.1
  75.3 0.3 collective-permute-start.18
  75.6 1.9 %collective-permute-start.19 = (bf16[32,1024]{1,0:T(8,128)(2,1)S(1)}, bf16[32,1024]{1,0:T(8,128)(2,1)S(1)}, u32[]{:S(2)}, u32[]{:S(2)}) collective-permute-start(bf16[32,1024]{1,0:T(8,128)(2,1)S(1)} %get-tuple-element.37), channel_id=1, source_target_pairs={{0,8},{4,12},{8,0},{12,4},{1,9},{5,13},{9,1},{13,5},{2,10},{6,14},... | collective-permute-start | bytes 196616 | tf_op jit(solution)/shard_map/ppermute | solution.py:485
  77.5 2.3 %collective-permute-start.20 = (bf16[32,1024]{1,0:T(8,128)(2,1)S(1)}, bf16[32,1024]{1,0:T(8,128)(2,1)S(1)}, u32[]{:S(2)}, u32[]{:S(2)}) collective-permute-start(bf16[32,1024]{1,0:T(8,128)(2,1)S(1)} %get-tuple-element.38), channel_id=1, source_target_pairs={{0,12},{4,8},{8,4},{12,0},{1,13},{5,9},{9,5},{13,1},{2,14},{6,10},... | collective-permute-start | bytes 196616 | tf_op jit(solution)/shard_map/ppermute | solution.py:485
  79.8 2.5 %collective-permute-done.19.two_ref = bf16[32,1024]{1,0:T(8,128)(2,1)S(1)} collective-permute-done((bf16[32,1024]{1,0:T(8,128)(2,1)S(1)}, bf16[32,1024]{1,0:T(8,128)(2,1)S(1)}, u32[]{:S(2)}, u32[]{:S(2)}) %collective-permute-start.19) | collective-permute-done | bytes 65568 | tf_op jit(solution)/shard_map/ppermute | solution.py:485
  82.3 1.3 %collective-permute-done.20.three_ref = bf16[32,1024]{1,0:T(8,128)(2,1)S(1)} collective-permute-done((bf16[32,1024]{1,0:T(8,128)(2,1)S(1)}, bf16[32,1024]{1,0:T(8,128)(2,1)S(1)}, u32[]{:S(2)}, u32[]{:S(2)}) %collective-permute-start.20) | collective-permute-done | bytes 65568 | tf_op jit(solution)/shard_map/ppermute | solution.py:485
  83.7 1.1 %scatter.1 = bf16[128,1024]{1,0:T(8,128)(2,1)} custom-call(bf16[32,128]{1,0:T(8,128)(2,1)S(1)} %get-tuple-element.22.pick_ref, bf16[32,1024]{1,0:T(8,128)(2,1)S(1)} %get-tuple-element.35.zero_ref, bf16[32,1024]{1,0:T(8,128)(2,1)S(1)} %collective-permute-done.18.one_ref, bf16[32,1024]{1,0:T(8,128)(2,1)S(1)} %collective-permute-done.19.two_ref, ...), custom_call_target="tpu_custom_call" | custom-call | tf_op jit(solution)/shard_map/scatter/pallas_call | solution.py:176
  (18 shorter events, 0.1 us)
Async XLA Ops:
  0.7 1.0 %copy-start = (bf16[128,1024]{1,0:T(8,128)(2,1)S(1)}, bf16[128,1024]{1,0:T(8,128)(2,1)}, u32[]{:S(2)}) copy-start(bf16[128,1024]{1,0:T(8,128)(2,1)} %context_ref.1) | copy-start | bytes 786436
  1.7 0.9 %copy-start.1 = (bf16[128,1024]{1,0:T(8,128)(2,1)S(1)}, bf16[128,1024]{1,0:T(8,128)(2,1)}, u32[]{:S(2)}) copy-start(bf16[128,1024]{1,0:T(8,128)(2,1)} %residual_ref.1) | copy-start | bytes 786436
  2.6 0.7 copy-start.4
  4.1 8.3 %collective-permute-start.2 = (bf16[32,1024]{1,0:T(8,128)(2,1)S(1)}, bf16[32,1024]{1,0:T(8,128)(2,1)S(1)}, u32[]{:S(2)}, u32[]{:S(2)}) collective-permute-start(bf16[32,1024]{1,0:T(8,128)(2,1)S(1)} %get-tuple-element.24.after_ref), channel_id=1, source_target_pairs={{0,2},{1,6},{2,10},{3,14},{4,3},{5,7},{6,11},{7,15},{8,0},{9,4},{1... | collective-permute-start | bytes 196616 | tf_op jit(solution)/shard_map/ppermute | solution.py:416
  7.1 5.3 %collective-permute-start = (bf16[32,1024]{1,0:T(8,128)(2,1)S(1)}, bf16[32,1024]{1,0:T(8,128)(2,1)S(1)}, u32[]{:S(2)}, u32[]{:S(2)}) collective-permute-start(bf16[32,1024]{1,0:T(8,128)(2,1)S(1)} %get-tuple-element.24.after_ref), channel_id=1, source_target_pairs={{0,0},{1,4},{2,8},{3,12},{4,1},{5,5},{6,9},{7,13},{8,2},{9,6},{10,... | collective-permute-start | bytes 196616 | tf_op jit(solution)/shard_map/ppermute | solution.py:415
  12.4 6.8 %collective-permute-start.3 = (bf16[32,1024]{1,0:T(8,128)(2,1)S(1)}, bf16[32,1024]{1,0:T(8,128)(2,1)S(1)}, u32[]{:S(2)}, u32[]{:S(2)}) collective-permute-start(bf16[32,1024]{1,0:T(8,128)(2,1)S(1)} %collective-permute-done.2.refs_2_), channel_id=1, source_target_pairs={{0,1},{1,0},{2,3},{3,2},{4,5},{5,4},{6,7},{7,6},{8,9},{9,8},{10,11... | collective-permute-start | bytes 196616 | tf_op jit(solution)/shard_map/ppermute | solution.py:418
  12.4 6.8 %collective-permute-start.1 = (bf16[32,1024]{1,0:T(8,128)(2,1)S(1)}, bf16[32,1024]{1,0:T(8,128)(2,1)S(1)}, u32[]{:S(2)}, u32[]{:S(2)}) collective-permute-start(bf16[32,1024]{1,0:T(8,128)(2,1)S(1)} %collective-permute-done.refs_0_), channel_id=1, source_target_pairs={{0,1},{1,0},{2,3},{3,2},{4,5},{5,4},{6,7},{7,6},{8,9},{9,8},{10,11... | collective-permute-start | bytes 196616 | tf_op jit(solution)/shard_map/ppermute | solution.py:417
  20.2 10.2 %collective-permute-start.6 = (bf16[32,1024]{1,0:T(8,128)(2,1)S(1)}, bf16[32,1024]{1,0:T(8,128)(2,1)S(1)}, u32[]{:S(2)}, u32[]{:S(2)}) collective-permute-start(bf16[32,1024]{1,0:T(8,128)(2,1)S(1)} %get-tuple-element.39), channel_id=1, source_target_pairs={{0,12},{4,8},{8,4},{12,0},{1,13},{5,9},{9,5},{13,1},{2,14},{6,10},... | collective-permute-start | bytes 196616 | tf_op jit(solution)/shard_map/ppermute | solution.py:428
  25.0 5.6 %collective-permute-start.5 = (bf16[32,1024]{1,0:T(8,128)(2,1)S(1)}, bf16[32,1024]{1,0:T(8,128)(2,1)S(1)}, u32[]{:S(2)}, u32[]{:S(2)}) collective-permute-start(bf16[32,1024]{1,0:T(8,128)(2,1)S(1)} %get-tuple-element.40), channel_id=1, source_target_pairs={{0,8},{4,12},{8,0},{12,4},{1,9},{5,13},{9,1},{13,5},{2,10},{6,14},... | collective-permute-start | bytes 196616 | tf_op jit(solution)/shard_map/ppermute | solution.py:428
  25.0 5.6 %collective-permute-start.4 = (bf16[32,1024]{1,0:T(8,128)(2,1)S(1)}, bf16[32,1024]{1,0:T(8,128)(2,1)S(1)}, u32[]{:S(2)}, u32[]{:S(2)}) collective-permute-start(bf16[32,1024]{1,0:T(8,128)(2,1)S(1)} %get-tuple-element.41), channel_id=1, source_target_pairs={{0,4},{4,0},{8,12},{12,8},{1,5},{5,1},{9,13},{13,9},{2,6},{6,2},{1... | collective-permute-start | bytes 196616 | tf_op jit(solution)/shard_map/ppermute | solution.py:428
  25.6 5.0 %copy-start.2 = (bf16[1024,4]{0,1:T(4,128)(2,1)S(1)}, bf16[1024,4]{0,1:T(4,128)(2,1)}, u32[]{:S(2)}) copy-start(bf16[1024,4]{0,1:T(4,128)(2,1)} %param.14) | copy-start | bytes 24580
  25.6 5.0 %copy-start.3 = (bf16[2,1024]{1,0:T(2,128)(2,1)S(1)}, bf16[2,1024]{1,0:T(2,128)(2,1)}, u32[]{:S(2)}) copy-start(bf16[2,1024]{1,0:T(2,128)(2,1)} %gain_ref.1) | copy-start | bytes 12292
  31.3 9.2 %collective-permute-start.9 = (bf16[32,1152]{1,0:T(8,128)(2,1)S(1)}, bf16[32,1152]{1,0:T(8,128)(2,1)S(1)}, u32[]{:S(2)}, u32[]{:S(2)}) collective-permute-start(bf16[32,1152]{1,0:T(8,128)(2,1)S(1)} %norm.1.after_ref.zero_ref), channel_id=1, source_target_pairs={{0,12},{4,8},{8,4},{12,0},{1,13},{5,9},{9,5},{13,1},{2,14},{6,10},... | collective-permute-start | bytes 221192 | tf_op jit(solution)/shard_map/ppermute | solution.py:438
  35.0 6.2 %collective-permute-start.8 = (bf16[32,1152]{1,0:T(8,128)(2,1)S(1)}, bf16[32,1152]{1,0:T(8,128)(2,1)S(1)}, u32[]{:S(2)}, u32[]{:S(2)}) collective-permute-start(bf16[32,1152]{1,0:T(8,128)(2,1)S(1)} %norm.1.after_ref.zero_ref), channel_id=1, source_target_pairs={{0,8},{4,12},{8,0},{12,4},{1,9},{5,13},{9,1},{13,5},{2,10},{6,14},... | collective-permute-start | bytes 221192 | tf_op jit(solution)/shard_map/ppermute | solution.py:438
  35.0 6.2 %collective-permute-start.7 = (bf16[32,1152]{1,0:T(8,128)(2,1)S(1)}, bf16[32,1152]{1,0:T(8,128)(2,1)S(1)}, u32[]{:S(2)}, u32[]{:S(2)}) collective-permute-start(bf16[32,1152]{1,0:T(8,128)(2,1)S(1)} %norm.1.after_ref.zero_ref), channel_id=1, source_target_pairs={{0,4},{4,0},{8,12},{12,8},{1,5},{5,1},{9,13},{13,9},{2,6},{6,2},{1... | collective-permute-start | bytes 221192 | tf_op jit(solution)/shard_map/ppermute | solution.py:438
  41.2 9.3 %collective-permute-start.12 = (bf16[64,1152]{1,0:T(8,128)(2,1)S(1)}, bf16[64,1152]{1,0:T(8,128)(2,1)S(1)}, u32[]{:S(2)}, u32[]{:S(2)}) collective-permute-start(bf16[64,1152]{1,0:T(8,128)(2,1)S(1)} %get-tuple-element.28), channel_id=1, source_target_pairs={{0,18},{2,16},{16,2},{18,0},{1,19},{3,17},{17,3},{19,1},{4,22},{6,... | collective-permute-start | bytes 442376 | tf_op jit(solution)/shard_map/ppermute | solution.py:448
  46.0 5.6 %collective-permute-start.10 = (bf16[64,1152]{1,0:T(8,128)(2,1)S(1)}, bf16[64,1152]{1,0:T(8,128)(2,1)S(1)}, u32[]{:S(2)}, u32[]{:S(2)}) collective-permute-start(bf16[64,1152]{1,0:T(8,128)(2,1)S(1)} %get-tuple-element.28), channel_id=1, source_target_pairs={{0,16},{16,0},{1,17},{17,1},{2,18},{18,2},{3,19},{19,3},{4,20},{20... | collective-permute-start | bytes 442376 | tf_op jit(solution)/shard_map/ppermute | solution.py:449
  46.3 5.3 %collective-permute-start.11 = (bf16[64,1152]{1,0:T(8,128)(2,1)S(1)}, bf16[64,1152]{1,0:T(8,128)(2,1)S(1)}, u32[]{:S(2)}, u32[]{:S(2)}) collective-permute-start(bf16[64,1152]{1,0:T(8,128)(2,1)S(1)} %get-tuple-element.27.own_ref), channel_id=1, source_target_pairs={{0,2},{2,0},{1,3},{3,1},{4,6},{6,4},{5,7},{7,5},{8,10},{10,8},{9,1... | collective-permute-start | bytes 442376 | tf_op jit(solution)/shard_map/ppermute | solution.py:450
  55.3 5.5 %collective-permute-start.13 = (bf16[2768,128]{1,0:T(8,128)(2,1)S(1)}, bf16[2768,128]{1,0:T(8,128)(2,1)S(1)}, u32[]{:S(2)}, u32[]{:S(2)}) collective-permute-start(bf16[2768,128]{1,0:T(8,128)(2,1)S(1)} %get-tuple-element.29.gate_ref), channel_id=1, source_target_pairs={{0,1},{1,0},{2,3},{3,2},{4,5},{5,4},{6,7},{7,6},{8,9},{9,8},{10,11... | collective-permute-start | bytes 2125832 | tf_op jit(solution)/shard_map/ppermute | solution.py:464
  58.4 2.4 %collective-permute-start.14 = (bf16[2752,128]{1,0:T(8,128)(2,1)S(1)}, bf16[2752,128]{1,0:T(8,128)(2,1)S(1)}, u32[]{:S(2)}, u32[]{:S(2)}) collective-permute-start(bf16[2752,128]{1,0:T(8,128)(2,1)S(1)} %up.1.up_ref), channel_id=1, source_target_pairs={{0,1},{1,0},{2,3},{3,2},{4,5},{5,4},{6,7},{7,6},{8,9},{9,8},{10,11... | collective-permute-start | bytes 2113544 | tf_op jit(solution)/shard_map/ppermute | solution.py:465
  64.5 5.9 %collective-permute-start.15 = (bf16[64,1024]{1,0:T(8,128)(2,1)S(1)}, bf16[64,1024]{1,0:T(8,128)(2,1)S(1)}, u32[]{:S(2)}, u32[]{:S(2)}) collective-permute-start(bf16[64,1024]{1,0:T(8,128)(2,1)S(1)} %get-tuple-element.32), channel_id=1, source_target_pairs={{0,2},{2,0},{1,3},{3,1},{4,6},{6,4},{5,7},{7,5},{8,10},{10,8},{9,1... | collective-permute-start | bytes 393224 | tf_op jit(solution)/shard_map/ppermute | solution.py:477
  66.4 8.3 %collective-permute-start.16 = (bf16[64,1024]{1,0:T(8,128)(2,1)S(1)}, bf16[64,1024]{1,0:T(8,128)(2,1)S(1)}, u32[]{:S(2)}, u32[]{:S(2)}) collective-permute-start(bf16[64,1024]{1,0:T(8,128)(2,1)S(1)} %get-tuple-element.33), channel_id=1, source_target_pairs={{0,16},{16,0},{1,17},{17,1},{2,18},{18,2},{3,19},{19,3},{4,20},{20... | collective-permute-start | bytes 393224 | tf_op jit(solution)/shard_map/ppermute | solution.py:476
  66.9 7.7 %collective-permute-start.17 = (bf16[64,1024]{1,0:T(8,128)(2,1)S(1)}, bf16[64,1024]{1,0:T(8,128)(2,1)S(1)}, u32[]{:S(2)}, u32[]{:S(2)}) collective-permute-start(bf16[64,1024]{1,0:T(8,128)(2,1)S(1)} %get-tuple-element.34), channel_id=1, source_target_pairs={{0,18},{2,16},{16,2},{18,0},{1,19},{3,17},{17,3},{19,1},{4,22},{6,... | collective-permute-start | bytes 393224 | tf_op jit(solution)/shard_map/ppermute | solution.py:475
  75.3 4.5 %collective-permute-start.18 = (bf16[32,1024]{1,0:T(8,128)(2,1)S(1)}, bf16[32,1024]{1,0:T(8,128)(2,1)S(1)}, u32[]{:S(2)}, u32[]{:S(2)}) collective-permute-start(bf16[32,1024]{1,0:T(8,128)(2,1)S(1)} %get-tuple-element.36), channel_id=1, source_target_pairs={{0,4},{4,0},{8,12},{12,8},{1,5},{5,1},{9,13},{13,9},{2,6},{6,2},{1... | collective-permute-start | bytes 196616 | tf_op jit(solution)/shard_map/ppermute | solution.py:485
  75.6 6.7 %collective-permute-start.19 = (bf16[32,1024]{1,0:T(8,128)(2,1)S(1)}, bf16[32,1024]{1,0:T(8,128)(2,1)S(1)}, u32[]{:S(2)}, u32[]{:S(2)}) collective-permute-start(bf16[32,1024]{1,0:T(8,128)(2,1)S(1)} %get-tuple-element.37), channel_id=1, source_target_pairs={{0,8},{4,12},{8,0},{12,4},{1,9},{5,13},{9,1},{13,5},{2,10},{6,14},... | collective-permute-start | bytes 196616 | tf_op jit(solution)/shard_map/ppermute | solution.py:485
  77.5 6.2 %collective-permute-start.20 = (bf16[32,1024]{1,0:T(8,128)(2,1)S(1)}, bf16[32,1024]{1,0:T(8,128)(2,1)S(1)}, u32[]{:S(2)}, u32[]{:S(2)}) collective-permute-start(bf16[32,1024]{1,0:T(8,128)(2,1)S(1)} %get-tuple-element.38), channel_id=1, source_target_pairs={{0,12},{4,8},{8,4},{12,0},{1,13},{5,9},{9,5},{13,1},{2,14},{6,10},... | collective-permute-start | bytes 196616 | tf_op jit(solution)/shard_map/ppermute | solution.py:485

commit v4 on v3

--- a/solution.py
+++ b/solution.py
@@ -165,7 +165,7 @@
 SCALARS = pl.BlockSpec(memory_space=pltpu.SMEM)
 IN_HBM = pl.BlockSpec(memory_space=pltpu.HBM)
 ANYWHERE = pl.BlockSpec(memory_space=pl.ANY)
-GROUP, FLIP, SIDE, KIND = range(4)
+GROUP, FLIP, SIDE = range(3)
 
 
 def crossed(bits, flip):
@@ -189,58 +189,82 @@
     return jax.ShapeDtypeStruct(shape, dtype)
 
 
-def keep_kernel(ids_ref, after_ref, *refs):
-    count = (len(refs) - 1) // 2
-    weights, held, semaphores = refs[:count], refs[count : 2 * count], refs[-1]
-    copies = []
-    for n in reversed(range(count)):
-        source = weights[n].at[ids_ref[GROUP]] if n == 0 else weights[n]
-        copies.append(pltpu.make_async_copy(source, held[n], semaphores.at[n]))
-        copies[-1].start()
-    for copy in copies:
-        copy.wait()
-
-
-def keep_on_chip(ids, after, weights, name):
-    weights = [pltpu.with_memory_space_constraint(weight, pltpu.HBM) for weight in weights]
-    shapes = [weight.shape[1:] if n == 0 else weight.shape for n, weight in enumerate(weights)]
+def keep_kernel(ids_ref, after_ref, weight_ref, held_ref, semaphore):
+    copy = pltpu.make_async_copy(weight_ref.at[ids_ref[GROUP]], held_ref, semaphore)
+    copy.start()
+    copy.wait()
+
+
+def in_hbm(value):
+    return pltpu.with_memory_space_constraint(value, pltpu.HBM)
+
+
+def keep_on_chip(ids, after, weight, name):
+    shape = weight.shape[1:]
     return call(
         keep_kernel,
         name,
-        [pltpu.VMEM(shape, jnp.bfloat16) for shape in shapes],
-        [SCALARS, ANYWHERE] + [IN_HBM] * len(weights),
-        [ids, after] + weights,
-        scratch=[pltpu.SemaphoreType.DMA((len(weights),))],
-        moved=sum(2 * a * b for a, b in shapes),
+        pltpu.VMEM(shape, jnp.bfloat16),
+        [SCALARS, ANYWHERE, IN_HBM],
+        [ids, after, in_hbm(weight)],
+        scratch=[pltpu.SemaphoreType.DMA(())],
+        moved=2 * shape[0] * shape[1],
         limit=1 << 20,
     )
 
 
-def select_kernel(ids_ref, rows_ref, context_ref, residual_ref, picked_ref, rest_ref, pick_ref):
+def select_kernel(ids_ref, kind_ref, rows_hbm, context_hbm, picked_ref, pick_ref, rows_ref, context_ref, semaphores):
+    rows_copy = pltpu.make_async_copy(rows_hbm, rows_ref, semaphores.at[0])
+    context_copy = pltpu.make_async_copy(context_hbm, context_ref, semaphores.at[1])
+    rows_copy.start()
+    context_copy.start()
+    rows_copy.wait()
     capacity = rows_ref.shape[1]
     slots, tokens = pick_ref.shape
     row = lax.broadcasted_iota(jnp.int32, (slots, tokens), 0)
     token = lax.broadcasted_iota(jnp.int32, (slots, tokens), 1)
     wanted = jnp.full((slots, tokens), -1, jnp.int32)
     for e in range(2):
-        expert = 2 * ids_ref[KIND] + (ids_ref[GROUP] ^ e)
+        expert = 2 * kind_ref[0] + (ids_ref[GROUP] ^ e)
         for s in range(capacity):
             wanted = jnp.where(row == e * capacity + s, rows_ref[expert, s], wanted)
     pick = jnp.where(wanted == token, 1.0, 0.0).astype(jnp.bfloat16)
     pick_ref[...] = pick
+    context_copy.wait()
     picked_ref[...] = jnp.dot(pick, context_ref[...], preferred_element_type=jnp.float32).astype(jnp.bfloat16)
-    rest_ref[...] = jnp.dot(pick, residual_ref[...], preferred_element_type=jnp.float32)
-
-
-def project_kernel(ids_ref, *refs):
-    block_refs, weight_ref, out_ref, rows_ref = refs[:4], refs[4], refs[6], refs[7]
-    slots = block_refs[0].shape[0]
-    for u, block_ref in enumerate(block_refs):
-        rows_ref[u * slots : (u + 1) * slots, :] = block_ref[...]
+
+
+def keep_gate_kernel(
+    ids_ref, pick_ref, residual_hbm, gate_ref, proj_ref, gate_held, proj_held, rest_ref, residual_ref, semaphores
+):
+    copies = [
+        pltpu.make_async_copy(residual_hbm, residual_ref, semaphores.at[0]),
+        pltpu.make_async_copy(proj_ref, proj_held, semaphores.at[1]),
+        pltpu.make_async_copy(gate_ref.at[ids_ref[GROUP]], gate_held, semaphores.at[2]),
+    ]
+    for copy in copies:
+        copy.start()
+    copies[0].wait()
+    rest_ref[...] = jnp.dot(pick_ref[...], residual_ref[...], preferred_element_type=jnp.float32)
+    for copy in copies[1:]:
+        copy.wait()
+
+
+def join_kernel(near_ref, across_ref, _, out_ref):
+    slots = near_ref.shape[0]
+    out_ref[:slots, :] = near_ref[...]
+    out_ref[slots:, :] = across_ref[...]
+
+
+def project_kernel(ids_ref, joined_ref, other_ref, weight_ref, out_ref, rows_ref):
+    pair = joined_ref.shape[0]
+    slots = pair // 2
+    rows_ref[:pair, :] = joined_ref[...]
+    rows_ref[pair:, :] = other_ref[...]
     product = jnp.dot(rows_ref[...], weight_ref[...], preferred_element_type=jnp.float32)
     product = product.astype(jnp.bfloat16)
-    for u in range(len(block_refs)):
-        out_ref[ids_ref[FLIP] ^ u] = product[u * slots : (u + 1) * slots, :]
+    for n, u in enumerate((0, 2, 1, 3)):
+        out_ref[ids_ref[FLIP] ^ u] = product[n * slots : (n + 1) * slots, :]
 
 
 def split_high_low(value):
@@ -248,18 +272,18 @@
     return high, value - high
 
 
-def norm_kernel(ids_ref, rest_ref, partial_ref, one_ref, two_ref, three_ref, gain_ref, router_ref, _, out_ref):
+def norm_kernel(ids_ref, kind_ref, rest_ref, partial_ref, one_ref, two_ref, three_ref, gain_ref, router_ref, _, out_ref):
     slots, columns = rest_ref.shape
     hidden = rest_ref[...] + partial_ref[0].astype(jnp.float32)
     for got_ref in (three_ref, two_ref, one_ref):
         hidden = hidden + got_ref[...].astype(jnp.float32)
     gains = gain_ref[...].astype(jnp.float32)
-    gained = hidden * jnp.where(ids_ref[KIND] == 0, gains[0:1], gains[1:2])
+    gained = hidden * jnp.where(kind_ref[0] == 0, gains[0:1], gains[1:2])
     out_ref[:, :columns] = gained.astype(jnp.bfloat16)
     table = router_ref[...].astype(jnp.float32)
     pieces = []
     for e in range(2):
-        expert = 2 * ids_ref[KIND] + (ids_ref[GROUP] ^ e)
+        expert = 2 * kind_ref[0] + (ids_ref[GROUP] ^ e)
         weights = table[0:1]
         for k in range(1, table.shape[0]):
             weights = jnp.where(expert == k, table[k : k + 1], weights)
@@ -268,7 +292,7 @@
     logits = jnp.concatenate(pieces, axis=0)
     squares = jnp.sum(hidden * hidden, axis=1, keepdims=True)
     lane = lax.broadcasted_iota(jnp.int32, (slots, STAT_COLS), 1)
-    extra = jnp.where(lane == 4, ids_ref[KIND].astype(jnp.float32), 0.0)
+    extra = jnp.where(lane == 4, kind_ref[0].astype(jnp.float32), 0.0)
     for at, stat in enumerate(split_high_low(squares) + split_high_low(logits)):
         extra = jnp.where(lane == at, stat, extra)
     out_ref[:, columns:] = extra.astype(jnp.bfloat16)
@@ -320,36 +344,54 @@
     weight_times_rows(weight_ref, rows_ref[...], out_ref)
 
 
-def down_kernel(ids_ref, gate_ref, gate_other_ref, up_ref, up_other_ref, weight_ref, *refs):
-    out_refs, act_ref = refs[:4], refs[4]
-    units, width = weight_ref.shape
-    rows = act_ref.shape[1]
+def silu_kernel(gate_ref, gate_other_ref, out_ref, stat_ref):
+    units = out_ref.shape[0]
     stat = gate_ref[units:, :].astype(jnp.float32) + gate_other_ref[units:, :].astype(jnp.float32)
     inverse = lax.rsqrt((stat[0:1] + stat[1:2]) / D + 1e-05)
     logits = (stat[2:3] + stat[3:4]) * inverse
     score = 1.0 / (1.0 + jnp.exp(-logits))
-    score = jnp.broadcast_to(score, (rows, rows)).T[:, 0:1]
+    at_row = lax.broadcasted_iota(jnp.int32, stat_ref.shape, 0)
+    stat_ref[...] = jnp.where(at_row == 0, inverse, score)
     for start in range(0, units, STRIP):
         stop = min(start + STRIP, units)
         gate = gate_ref[start:stop, :].astype(jnp.float32) + gate_other_ref[start:stop, :].astype(jnp.float32)
-        up = up_ref[start:stop, :].astype(jnp.float32) + up_other_ref[start:stop, :].astype(jnp.float32)
-        gate, up = gate * inverse, up * inverse
-        act_ref[start:stop, :] = (gate / (1.0 + jnp.exp(-gate)) * up).astype(jnp.bfloat16)
-    columns = width // 2
-    half = rows // 2
-    for start in range(0, width, CHUNK):
+        gate = gate * inverse
+        out_ref[start:stop, :] = gate / (1.0 + jnp.exp(-gate)) * inverse
+
+
+def scored_product(act_ref, weight_ref, stat_ref, quarter, span, out_refs):
+    rows = act_ref.shape[1]
+    columns = out_refs[0].shape[1]
+    score = jnp.broadcast_to(stat_ref[1:2, :], (rows, rows)).T[span, 0:1]
+    for start in range(0, columns, CHUNK):
+        at = pl.multiple_of(quarter * columns + start, CHUNK)
         value = lax.dot_general(
-            act_ref[...], weight_ref[:, start : start + CHUNK], (((0,), (0,)), ((), ())),
+            act_ref[:, span], weight_ref[:, pl.ds(at, CHUNK)], (((0,), (0,)), ((), ())),
             preferred_element_type=jnp.float32,
         )
         value = (value * score).astype(jnp.bfloat16)
-        quarter, at = divmod(start, columns)
-        for across in range(2):
-
-            @pl.when((ids_ref[SIDE] ^ quarter) == across)
-            def _():
-                out_refs[2 * across][:, at : at + CHUNK] = value[:half]
-                out_refs[2 * across + 1][:, at : at + CHUNK] = value[half:]
+        done = 0
+        for out_ref in out_refs:
+            out_ref[:, start : start + CHUNK] = value[done : done + out_ref.shape[0]]
+            done += out_ref.shape[0]
+
+
+def down_sent_kernel(
+    ids_ref, silu_ref, stat_ref, up_ref, up_other_ref, weight_ref, side_ref, side_far_ref, far_ref, act_ref
+):
+    units, rows = act_ref.shape
+    for start in range(0, units, STRIP):
+        stop = min(start + STRIP, units)
+        up = up_ref[start:stop, :].astype(jnp.float32) + up_other_ref[start:stop, :].astype(jnp.float32)
+        act_ref[start:stop, :] = (silu_ref[start:stop, :] * up).astype(jnp.bfloat16)
+    side = ids_ref[SIDE]
+    scored_product(act_ref, weight_ref, stat_ref, 1 - side, slice(0, rows), (side_ref, side_far_ref))
+    scored_product(act_ref, weight_ref, stat_ref, side, slice(rows // 2, rows), (far_ref,))
+
+
+def down_kept_kernel(ids_ref, act_ref, stat_ref, weight_ref, kept_ref):
+    rows = act_ref.shape[1]
+    scored_product(act_ref, weight_ref, stat_ref, ids_ref[SIDE], slice(0, rows // 2), (kept_ref,))
 
 
 def merge_kernel(ids_ref, own_ref, kept_ref, side_ref, far_ref, side_far_ref, *out_refs):
@@ -400,43 +442,61 @@
     assert block_modality.shape == (1,) and experts == 4 and gate_weight.shape[0] == 2
     tok, side = lax.axis_index("tok"), lax.axis_index("mod")
     corner = 2 * side + lax.axis_index("fsdp")
-    ids = jnp.stack([lax.axis_index("groups"), tok ^ corner, side, block_modality[0]])
-
-    picked, rest, pick = call(
+    ids = jnp.stack([lax.axis_index("groups"), tok ^ corner, side])
+
+    picked, pick = call(
         select_kernel,
         "select",
-        [array(slots, columns), array(slots, columns, dtype=jnp.float32), array(slots, tokens)],
-        [SCALARS, SCALARS, ON_CHIP, ON_CHIP],
-        [ids, expert_rows, context, residual],
+        [array(slots, columns), array(slots, tokens)],
+        [SCALARS] * 2 + [IN_HBM] * 2,
+        [ids, block_modality, in_hbm(expert_rows), in_hbm(context)],
+        scratch=[
+            pltpu.SMEM((experts, capacity), jnp.int32),
+            pltpu.VMEM((tokens, columns), jnp.bfloat16),
+            pltpu.SemaphoreType.DMA((2,)),
+        ],
     )
     plane = ("tok", "mod", "fsdp")
     to_first = [(t * 4 + q, q * 4 + t) for t in range(4) for q in range(4)]
     to_second = [(t * 4 + q, q * 4 + (t ^ 2)) for t in range(4) for q in range(4)]
     near = lax.ppermute(picked, plane, to_first)
     across = lax.ppermute(picked, plane, to_second)
-    near_core = lax.ppermute(near, "fsdp", SWAP)
-    across_core = lax.ppermute(across, "fsdp", SWAP)
-    gate_held, proj_held = keep_on_chip(ids, picked, [gate_weight.swapaxes(1, 2), out_proj], "keep_gate")
+    gate_held, proj_held, rest = call(
+        keep_gate_kernel,
+        "keep_gate",
+        [
+            pltpu.VMEM((units, width), jnp.bfloat16),
+            pltpu.VMEM(out_proj.shape, jnp.bfloat16),
+            array(slots, columns, dtype=jnp.float32),
+        ],
+        [SCALARS, ON_CHIP, IN_HBM, IN_HBM, IN_HBM],
+        [ids, pick, in_hbm(residual), in_hbm(gate_weight.swapaxes(1, 2)), in_hbm(out_proj)],
+        scratch=[pltpu.VMEM((tokens, columns), jnp.bfloat16), pltpu.SemaphoreType.DMA((3,))],
+        moved=2 * units * width,
+        limit=2 << 20,
+    )
+    joined = call(join_kernel, "join", array(half, columns), [ON_CHIP] * 3, [near, across, gate_held])
+    other = lax.ppermute(joined, "fsdp", SWAP)
     partial = call(
         project_kernel,
         "project",
         array(4, slots, columns),
-        [SCALARS] + [ON_CHIP] * 6,
-        [ids, near, near_core, across, across_core, proj_held, gate_held],
+        [SCALARS] + [ON_CHIP] * 3,
+        [ids, joined, other, proj_held],
         scratch=[pltpu.VMEM((rows, columns), jnp.bfloat16)],
     )
     sums = [lax.ppermute(partial[v], "tok", crossed(2, v)) for v in (1, 2, 3)]
-    (up_held,) = keep_on_chip(ids, partial, [up_weight.swapaxes(1, 2)], "keep_up")
+    up_held = keep_on_chip(ids, partial, up_weight.swapaxes(1, 2), "keep_up")
     packed_columns = columns + STAT_COLS
     packed = call(
         norm_kernel,
         "norm",
         array(slots, packed_columns),
-        [SCALARS] + [ON_CHIP] * 8,
-        [ids, rest, partial, *sums, norm_gain, router_weight.T, up_held],
+        [SCALARS, SCALARS] + [ON_CHIP] * 8,
+        [ids, block_modality, rest, partial, *sums, norm_gain, router_weight.T, up_held],
     )
     others = [lax.ppermute(packed, "tok", crossed(2, v)) for v in (1, 2, 3)]
-    (down_held,) = keep_on_chip(ids, packed, [down_weight], "keep_down")
+    down_held = keep_on_chip(ids, packed, down_weight, "keep_down")
     own, given = call(
         arrange_kernel,
         "arrange",
@@ -463,14 +523,29 @@
     )
     gate_other = lax.ppermute(gate, "fsdp", SWAP)
     up_other = lax.ppermute(up, "fsdp", SWAP)
-    kept, to_far, to_side, to_side_far = call(
-        down_kernel,
-        "down",
-        [array(half, columns)] * 4,
+    silu, stat = call(
+        silu_kernel,
+        "silu",
+        [array(units, rows, dtype=jnp.float32), array(8, rows, dtype=jnp.float32)],
+        [ON_CHIP] * 2,
+        [gate, gate_other],
+        moved=8 * units * rows,
+    )
+    to_side, to_side_far, to_far, act = call(
+        down_sent_kernel,
+        "down_sent",
+        [array(half, columns)] * 3 + [array(units, rows)],
         [SCALARS] + [ON_CHIP] * 5,
-        [ids, gate, gate_other, up, up_other, down_held],
-        scratch=[pltpu.VMEM((units, rows), jnp.bfloat16)],
-        flops=flops,
+        [ids, silu, stat, up, up_other, down_held],
+        flops=flops // 4 * 3,
+    )
+    kept = call(
+        down_kept_kernel,
+        "down_kept",
+        array(half, columns),
+        [SCALARS] + [ON_CHIP] * 3,
+        [ids, act, stat, down_held],
+        flops=flops // 4,
     )
     from_side_far = lax.ppermute(to_side_far, both_axes, crossed(2, 3))
     from_far = lax.ppermute(to_far, "groups", SWAP)

time: 85 us -> 79.5 us (0.935)
  waiting for transfers between devices: 22.6 us -> 17 us
  local copies, waits for them, and re-layouts: 2.6 us -> 0.02 us
  Pallas kernels: 29.7 us -> 32.1 us
    ppermute x1, waiting for transfers between devices: 4.66 us -> 0.01 us  [paired_local(): across = lax.ppermute(picked, plane, to_second)]
    ppermute x1, starting transfers between devices: 4.84 us -> 1.89 us  [paired_local(): side_far = lax.ppermute(given, both_axes, crossed(2, 3))]
    unnamed x10 -> x4, local copies, waits for them, and re-layouts: 2.59 us -> 0.01 us
    pallas_call x12 -> x15, Pallas kernels: 29.7 us -> 32.1 us  [call(): pl.pallas_call(kernel, out_shape=outs, in_specs=specs, out_specs=jax.tree...]
    ppermute x1, waiting for transfers between devices: 4.17 us -> 2.72 us  [paired_local(): from_far = lax.ppermute(to_far, 'groups', SWAP)]
    ppermute x1, waiting for transfers between devices: 2.37 us -> 1.16 us  [paired_local(): from_side = lax.ppermute(to_side, 'mod', SWAP)]
    ppermute x3, starting transfers between devices: 5.4 us -> 6.51 us  [paired_local(): sums = [lax.ppermute(partial[v], 'tok', crossed(2, v)) for v in (1, 2, 3)]]
    ppermute x2 -> x1, starting transfers between devices: 1.38 us -> 2.45 us  [paired_local(): other = lax.ppermute(joined, 'fsdp', SWAP)]
  transfers between devices with their start and end apart: 21 -> 20, of which waited for: 10 -> 12; matrix products, arithmetic and copies ran while one was open for 0% -> 0% of each run, Pallas kernels for 21% -> 26%
where the time goes in v4:
time: 79.5 us; the launch traced here: 79.3 us
  Pallas kernels  32.1 us (40%)
  starting transfers between devices  29.3 us (37%)
  waiting for transfers between devices  17 us (21%)
  between operations  0.83 us (1%)
    pallas_call x15, Pallas kernels, call(): pl.pallas_call(kernel, out_shape=outs, in_specs=specs, out_specs=jax.tree...  32.1 us
    ppermute x3, starting transfers between devices, paired_local(): sums = [lax.ppermute(partial[v], 'tok', crossed(2, v)) for v in (1, 2, 3)]  6.51 us
    ppermute x3, starting transfers between devices, paired_local(): others = [lax.ppermute(packed, 'tok', crossed(2, v)) for v in (1, 2, 3)]  4.45 us
    ppermute x3, starting transfers between devices, paired_local(): lax.ppermute(merged[v], 'tok', crossed(2, v))  4.44 us
    ppermute x3, waiting for transfers between devices, paired_local(): lax.ppermute(merged[v], 'tok', crossed(2, v))  4.08 us
    ppermute x1, waiting for transfers between devices, paired_local(): side_far = lax.ppermute(given, both_axes, crossed(2, 3))  4.04 us
    ppermute x1, starting transfers between devices, paired_local(): across = lax.ppermute(picked, plane, to_second)  2.99 us
    ppermute x1, waiting for transfers between devices, paired_local(): from_far = lax.ppermute(to_far, 'groups', SWAP)  2.72 us
  transfers between devices with their start and end apart: 20, of which 12 were waited for; matrix products, arithmetic and copies ran while one was open for 0% of the time, Pallas kernels for 26%

profile of v4, /device:TPU:0, one launch (start us, length us, event | category | flops | bytes accessed | tf_op | source)
XLA Modules:
  0.0 79.3 jit_solution(11145818505037147463)
XLA Ops:
  0.7 0.1 pad_add_fusion.ids_ref
  0.7 1.7 %select.1 = (bf16[32,1024]{1,0:T(8,128)(2,1)S(1)}, bf16[32,128]{1,0:T(8,128)(2,1)S(1)}) custom-call(s32[3]{0:T(128)S(1)} %pad_add_fusion.ids_ref, s32[1]{0:T(128)S(6)} %copy.11.kind_ref, s32[4,16]{1,0:T(4,128)} %rows_hbm.1, bf16[128,1024]{1,0:T(8,128)(2,1)} %context_hbm.1), custom_call_target="tpu_custom_call" | custom-call | tf_op jit(solution)/shard_map/select/pallas_call | solution.py:176
  2.4 3.0 %collective-permute-start.1 = (bf16[32,1024]{1,0:T(8,128)(2,1)S(1)}, bf16[32,1024]{1,0:T(8,128)(2,1)S(1)}, u32[]{:S(2)}, u32[]{:S(2)}) collective-permute-start(bf16[32,1024]{1,0:T(8,128)(2,1)S(1)} %get-tuple-element.26), channel_id=1, source_target_pairs={{0,2},{1,6},{2,10},{3,14},{4,3},{5,7},{6,11},{7,15},{8,0},{9,4},{1... | collective-permute-start | bytes 196616 | tf_op jit(solution)/shard_map/ppermute | solution.py:463
  5.4 0.7 collective-permute-start
  6.1 5.5 %keep_gate.1 = (bf16[2752,2048]{1,0:T(8,128)(2,1)S(1)}, bf16[1024,1024]{1,0:T(8,128)(2,1)S(1)}, f32[32,1024]{1,0:T(8,128)S(1)}) custom-call(s32[3]{0:T(128)S(1)} %pad_add_fusion.ids_ref, bf16[32,128]{1,0:T(8,128)(2,1)S(1)} %get-tuple-element.24.pick_ref, bf16[128,1024]{1,0:T(8,128)(2,1)} %residual_hbm.1, bf16[2,2752,2048]{2,1,0:T(8,128)(2,1)} %bitcast.13, ...), custom_call_target="tpu_custom_call" | custom-call | bytes 11272192 | tf_op jit(solution)/shard_map/keep_gate/pallas_call | solution.py:176
  11.6 0.0 collective-permute-done.1.across_ref
  11.6 2.4 %collective-permute-start.2 = (bf16[64,1024]{1,0:T(8,128)(2,1)S(1)}, bf16[64,1024]{1,0:T(8,128)(2,1)S(1)}, u32[]{:S(2)}, u32[]{:S(2)}) collective-permute-start(bf16[64,1024]{1,0:T(8,128)(2,1)S(1)} %join.1.joined_ref), channel_id=1, source_target_pairs={{0,1},{1,0},{2,3},{3,2},{4,5},{5,4},{6,7},{7,6},{8,9},{9,8},{10,11... | collective-permute-start | bytes 393224 | tf_op jit(solution)/shard_map/ppermute | solution.py:479
  14.1 1.0 %collective-permute-done.2.other_ref = bf16[64,1024]{1,0:T(8,128)(2,1)S(1)} collective-permute-done((bf16[64,1024]{1,0:T(8,128)(2,1)S(1)}, bf16[64,1024]{1,0:T(8,128)(2,1)S(1)}, u32[]{:S(2)}, u32[]{:S(2)}) %collective-permute-start.2) | collective-permute-done | bytes 131104 | tf_op jit(solution)/shard_map/ppermute | solution.py:479
  15.1 1.0 %project.1.after_ref.partial_ref = bf16[4,32,1024]{2,1,0:T(8,128)(2,1)S(1)} custom-call(s32[3]{0:T(128)S(1)} %pad_add_fusion.ids_ref, bf16[64,1024]{1,0:T(8,128)(2,1)S(1)} %join.1.joined_ref, bf16[64,1024]{1,0:T(8,128)(2,1)S(1)} %collective-permute-done.2.other_ref, bf16[1024,1024]{1,0:T(8,128)(2,1)S(1)} %get-tuple-element.28.weight_ref), custom_call_target="tpu_custom_call" | custom-call | tf_op jit(solution)/shard_map/project/pallas_call | solution.py:176
  16.1 5.9 %collective-permute-start.5 = (bf16[32,1024]{1,0:T(8,128)(2,1)S(1)}, bf16[32,1024]{1,0:T(8,128)(2,1)S(1)}, u32[]{:S(2)}, u32[]{:S(2)}) collective-permute-start(bf16[32,1024]{1,0:T(8,128)(2,1)S(1)} %get-tuple-element.43), channel_id=1, source_target_pairs={{0,12},{4,8},{8,4},{12,0},{1,13},{5,9},{9,5},{13,1},{2,14},{6,10},... | collective-permute-start | bytes 196616 | tf_op jit(solution)/shard_map/ppermute | solution.py:488
  21.9 0.0 collective-permute-start.4
  21.9 0.6 collective-permute-start.3
  22.6 4.8 %keep_up.1._.weight_ref = bf16[2752,2048]{1,0:T(8,128)(2,1)S(1)} custom-call(s32[3]{0:T(128)S(1)} %pad_add_fusion.ids_ref, bf16[4,32,1024]{2,1,0:T(8,128)(2,1)S(1)} %project.1.after_ref.partial_ref, bf16[2,2752,2048]{2,1,0:T(8,128)(2,1)} %bitcast.14), custom_call_target="tpu_custom_call" | custom-call | bytes 11272192 | tf_op jit(solution)/shard_map/keep_up/pallas_call | solution.py:176
  27.4 0.0 collective-permute-done.4.two_ref
  27.4 0.2 collective-permute-done.3.one_ref
  27.6 0.8 norm.1.after_ref.zero_ref
  28.4 3.6 %collective-permute-start.8 = (bf16[32,1152]{1,0:T(8,128)(2,1)S(1)}, bf16[32,1152]{1,0:T(8,128)(2,1)S(1)}, u32[]{:S(2)}, u32[]{:S(2)}) collective-permute-start(bf16[32,1152]{1,0:T(8,128)(2,1)S(1)} %norm.1.after_ref.zero_ref), channel_id=1, source_target_pairs={{0,12},{4,8},{8,4},{12,0},{1,13},{5,9},{9,5},{13,1},{2,14},{6,10},... | collective-permute-start | bytes 221192 | tf_op jit(solution)/shard_map/ppermute | solution.py:498
  32.0 0.0 collective-permute-start.7
  32.0 0.8 %collective-permute-start.6 = (bf16[32,1152]{1,0:T(8,128)(2,1)S(1)}, bf16[32,1152]{1,0:T(8,128)(2,1)S(1)}, u32[]{:S(2)}, u32[]{:S(2)}) collective-permute-start(bf16[32,1152]{1,0:T(8,128)(2,1)S(1)} %norm.1.after_ref.zero_ref), channel_id=1, source_target_pairs={{0,4},{4,0},{8,12},{12,8},{1,5},{5,1},{9,13},{13,9},{2,6},{6,2},{1... | collective-permute-start | bytes 221192 | tf_op jit(solution)/shard_map/ppermute | solution.py:498
  32.8 4.8 %keep_down.1._.weight_ref = bf16[2752,2048]{1,0:T(8,128)(2,1)S(1)} custom-call(s32[3]{0:T(128)S(1)} %pad_add_fusion.ids_ref, bf16[32,1152]{1,0:T(8,128)(2,1)S(1)} %norm.1.after_ref.zero_ref, bf16[2,2752,2048]{2,1,0:T(8,128)(2,1)} %weight_ref.1), custom_call_target="tpu_custom_call" | custom-call | bytes 11272192 | tf_op jit(solution)/shard_map/keep_down/pallas_call | solution.py:176
  37.6 0.3 collective-permute-done.7.two_ref
  37.8 0.1 collective-permute-done.6.one_ref
  37.9 1.9 %collective-permute-start.11 = (bf16[64,1152]{1,0:T(8,128)(2,1)S(1)}, bf16[64,1152]{1,0:T(8,128)(2,1)S(1)}, u32[]{:S(2)}, u32[]{:S(2)}) collective-permute-start(bf16[64,1152]{1,0:T(8,128)(2,1)S(1)} %get-tuple-element.30), channel_id=1, source_target_pairs={{0,18},{2,16},{16,2},{18,0},{1,19},{3,17},{17,3},{19,1},{4,22},{6,... | collective-permute-start | bytes 442376 | tf_op jit(solution)/shard_map/ppermute | solution.py:508
  39.8 0.5 collective-permute-start.9
  40.3 1.2 %collective-permute-start.10 = (bf16[64,1152]{1,0:T(8,128)(2,1)S(1)}, bf16[64,1152]{1,0:T(8,128)(2,1)S(1)}, u32[]{:S(2)}, u32[]{:S(2)}) collective-permute-start(bf16[64,1152]{1,0:T(8,128)(2,1)S(1)} %get-tuple-element.29.own_ref), channel_id=1, source_target_pairs={{0,2},{2,0},{1,3},{3,1},{4,6},{6,4},{5,7},{7,5},{8,10},{10,8},{9,1... | collective-permute-start | bytes 442376 | tf_op jit(solution)/shard_map/ppermute | solution.py:510
  41.5 4.0 %collective-permute-done.11.side_far_ref = bf16[64,1152]{1,0:T(8,128)(2,1)S(1)} collective-permute-done((bf16[64,1152]{1,0:T(8,128)(2,1)S(1)}, bf16[64,1152]{1,0:T(8,128)(2,1)S(1)}, u32[]{:S(2)}, u32[]{:S(2)}) %collective-permute-start.11) | collective-permute-done | bytes 147488 | tf_op jit(solution)/shard_map/ppermute | solution.py:508
  45.5 1.9 %collective-permute-done.9.far_ref = bf16[64,1152]{1,0:T(8,128)(2,1)S(1)} collective-permute-done((bf16[64,1152]{1,0:T(8,128)(2,1)S(1)}, bf16[64,1152]{1,0:T(8,128)(2,1)S(1)}, u32[]{:S(2)}, u32[]{:S(2)}) %collective-permute-start.9) | collective-permute-done | bytes 147488 | tf_op jit(solution)/shard_map/ppermute | solution.py:509
  47.4 0.3 collective-permute-done.10.side_own_ref
  47.7 3.7 %gate.1 = (bf16[2768,128]{1,0:T(8,128)(2,1)S(1)}, bf16[128,2048]{1,0:T(8,128)(2,1)S(1)}) custom-call(s32[3]{0:T(128)S(1)} %pad_add_fusion.ids_ref, bf16[64,1152]{1,0:T(8,128)(2,1)S(1)} %get-tuple-element.29.own_ref, bf16[64,1152]{1,0:T(8,128)(2,1)S(1)} %collective-permute-done.9.far_ref, bf16[64,1152]{1,0:T(8,128)(2,1)S(1)} %collective-permute-done.10.side_own_ref, ...), custom_call_target="tpu_custom_call" | custom-call | flops 1442840576 | tf_op jit(solution)/shard_map/gate/pallas_call | solution.py:176
  51.4 0.1 collective-permute-start.12
  51.5 3.1 %up.1.up_ref = bf16[2752,128]{1,0:T(8,128)(2,1)S(1)} custom-call(bf16[128,2048]{1,0:T(8,128)(2,1)S(1)} %get-tuple-element.34.rows_ref, bf16[2752,2048]{1,0:T(8,128)(2,1)S(1)} %keep_up.1._.weight_ref), custom_call_target="tpu_custom_call" | custom-call | flops 1442840576 | tf_op jit(solution)/shard_map/up/pallas_call | solution.py:176
  54.5 0.6 collective-permute-start.13
  55.1 0.5 silu.1
  55.6 1.3 %collective-permute-done.13.up_other_ref = bf16[2752,128]{1,0:T(8,128)(2,1)S(1)} collective-permute-done((bf16[2752,128]{1,0:T(8,128)(2,1)S(1)}, bf16[2752,128]{1,0:T(8,128)(2,1)S(1)}, u32[]{:S(2)}, u32[]{:S(2)}) %collective-permute-start.13) | collective-permute-done | bytes 704544 | tf_op jit(solution)/shard_map/ppermute | solution.py:525
  56.9 2.9 %down_sent.1 = (bf16[64,1024]{1,0:T(8,128)(2,1)S(1)}, bf16[64,1024]{1,0:T(8,128)(2,1)S(1)}, bf16[64,1024]{1,0:T(8,128)(2,1)S(1)}, bf16[2752,128]{1,0:T(8,128)(2,1)S(1)}) custom-call(s32[3]{0:T(128)S(1)} %pad_add_fusion.ids_ref, f32[2752,128]{1,0:T(8,128)S(1)} %get-tuple-element.32.silu_ref, f32[8,128]{1,0:T(8,128)S(1)} %get-tuple-element.33.stat_ref, ...), custom_call_target="tpu_custom_call" | custom-call | flops 1082130432 | tf_op jit(solution)/shard_map/down_sent/pallas_call | solution.py:176
  59.8 0.8 %collective-permute-start.14 = (bf16[64,1024]{1,0:T(8,128)(2,1)S(1)}, bf16[64,1024]{1,0:T(8,128)(2,1)S(1)}, u32[]{:S(2)}, u32[]{:S(2)}) collective-permute-start(bf16[64,1024]{1,0:T(8,128)(2,1)S(1)} %get-tuple-element.36), channel_id=1, source_target_pairs={{0,2},{2,0},{1,3},{3,1},{4,6},{6,4},{5,7},{7,5},{8,10},{10,8},{9,1... | collective-permute-start | bytes 393224 | tf_op jit(solution)/shard_map/ppermute | solution.py:552
  60.7 1.2 %collective-permute-start.15 = (bf16[64,1024]{1,0:T(8,128)(2,1)S(1)}, bf16[64,1024]{1,0:T(8,128)(2,1)S(1)}, u32[]{:S(2)}, u32[]{:S(2)}) collective-permute-start(bf16[64,1024]{1,0:T(8,128)(2,1)S(1)} %get-tuple-element.37), channel_id=1, source_target_pairs={{0,16},{16,0},{1,17},{17,1},{2,18},{18,2},{3,19},{19,3},{4,20},{20... | collective-permute-start | bytes 393224 | tf_op jit(solution)/shard_map/ppermute | solution.py:551
  61.9 1.5 %collective-permute-start.16 = (bf16[64,1024]{1,0:T(8,128)(2,1)S(1)}, bf16[64,1024]{1,0:T(8,128)(2,1)S(1)}, u32[]{:S(2)}, u32[]{:S(2)}) collective-permute-start(bf16[64,1024]{1,0:T(8,128)(2,1)S(1)} %get-tuple-element.38), channel_id=1, source_target_pairs={{0,18},{2,16},{16,2},{18,0},{1,19},{3,17},{17,3},{19,1},{4,22},{6,... | collective-permute-start | bytes 393224 | tf_op jit(solution)/shard_map/ppermute | solution.py:550
  63.4 1.7 %down_kept.1.kept_ref = bf16[64,1024]{1,0:T(8,128)(2,1)S(1)} custom-call(s32[3]{0:T(128)S(1)} %pad_add_fusion.ids_ref, bf16[2752,128]{1,0:T(8,128)(2,1)S(1)} %get-tuple-element.35.act_ref, f32[8,128]{1,0:T(8,128)S(1)} %get-tuple-element.33.stat_ref, bf16[2752,2048]{1,0:T(8,128)(2,1)S(1)} %keep_down.1._.weight_ref), custom_call_target="tpu_custom_call" | custom-call | flops 360710144 | tf_op jit(solution)/shard_map/down_kept/pallas_call | solution.py:176
  65.1 1.2 %collective-permute-done.14.side_ref = bf16[64,1024]{1,0:T(8,128)(2,1)S(1)} collective-permute-done((bf16[64,1024]{1,0:T(8,128)(2,1)S(1)}, bf16[64,1024]{1,0:T(8,128)(2,1)S(1)}, u32[]{:S(2)}, u32[]{:S(2)}) %collective-permute-start.14) | collective-permute-done | bytes 131104 | tf_op jit(solution)/shard_map/ppermute | solution.py:552
  66.2 2.7 %collective-permute-done.15.far_ref = bf16[64,1024]{1,0:T(8,128)(2,1)S(1)} collective-permute-done((bf16[64,1024]{1,0:T(8,128)(2,1)S(1)}, bf16[64,1024]{1,0:T(8,128)(2,1)S(1)}, u32[]{:S(2)}, u32[]{:S(2)}) %collective-permute-start.15) | collective-permute-done | bytes 131104 | tf_op jit(solution)/shard_map/ppermute | solution.py:551
  69.0 0.7 merge.1
  69.6 0.1 collective-permute-start.17
  69.7 2.3 %collective-permute-start.18 = (bf16[32,1024]{1,0:T(8,128)(2,1)S(1)}, bf16[32,1024]{1,0:T(8,128)(2,1)S(1)}, u32[]{:S(2)}, u32[]{:S(2)}) collective-permute-start(bf16[32,1024]{1,0:T(8,128)(2,1)S(1)} %get-tuple-element.41), channel_id=1, source_target_pairs={{0,8},{4,12},{8,0},{12,4},{1,9},{5,13},{9,1},{13,5},{2,10},{6,14},... | collective-permute-start | bytes 196616 | tf_op jit(solution)/shard_map/ppermute | solution.py:560
  72.0 2.1 %collective-permute-start.19 = (bf16[32,1024]{1,0:T(8,128)(2,1)S(1)}, bf16[32,1024]{1,0:T(8,128)(2,1)S(1)}, u32[]{:S(2)}, u32[]{:S(2)}) collective-permute-start(bf16[32,1024]{1,0:T(8,128)(2,1)S(1)} %get-tuple-element.42), channel_id=1, source_target_pairs={{0,12},{4,8},{8,4},{12,0},{1,13},{5,9},{9,5},{13,1},{2,14},{6,10},... | collective-permute-start | bytes 196616 | tf_op jit(solution)/shard_map/ppermute | solution.py:560
  74.1 1.4 %collective-permute-done.18.two_ref = bf16[32,1024]{1,0:T(8,128)(2,1)S(1)} collective-permute-done((bf16[32,1024]{1,0:T(8,128)(2,1)S(1)}, bf16[32,1024]{1,0:T(8,128)(2,1)S(1)}, u32[]{:S(2)}, u32[]{:S(2)}) %collective-permute-start.18) | collective-permute-done | bytes 65568 | tf_op jit(solution)/shard_map/ppermute | solution.py:560
  75.5 2.7 %collective-permute-done.19.three_ref = bf16[32,1024]{1,0:T(8,128)(2,1)S(1)} collective-permute-done((bf16[32,1024]{1,0:T(8,128)(2,1)S(1)}, bf16[32,1024]{1,0:T(8,128)(2,1)S(1)}, u32[]{:S(2)}, u32[]{:S(2)}) %collective-permute-start.19) | collective-permute-done | bytes 65568 | tf_op jit(solution)/shard_map/ppermute | solution.py:560
  78.2 1.1 %scatter.1 = bf16[128,1024]{1,0:T(8,128)(2,1)} custom-call(bf16[32,128]{1,0:T(8,128)(2,1)S(1)} %get-tuple-element.24.pick_ref, bf16[32,1024]{1,0:T(8,128)(2,1)S(1)} %get-tuple-element.39.zero_ref, bf16[32,1024]{1,0:T(8,128)(2,1)S(1)} %collective-permute-done.17.one_ref, bf16[32,1024]{1,0:T(8,128)(2,1)S(1)} %collective-permute-done.18.two_ref, ...), custom_call_target="tpu_custom_call" | custom-call | tf_op jit(solution)/shard_map/scatter/pallas_call | solution.py:176
  (13 shorter events, 0.1 us)
Async XLA Ops:
  2.4 9.2 %collective-permute-start.1 = (bf16[32,1024]{1,0:T(8,128)(2,1)S(1)}, bf16[32,1024]{1,0:T(8,128)(2,1)S(1)}, u32[]{:S(2)}, u32[]{:S(2)}) collective-permute-start(bf16[32,1024]{1,0:T(8,128)(2,1)S(1)} %get-tuple-element.26), channel_id=1, source_target_pairs={{0,2},{1,6},{2,10},{3,14},{4,3},{5,7},{6,11},{7,15},{8,0},{9,4},{1... | collective-permute-start | bytes 196616 | tf_op jit(solution)/shard_map/ppermute | solution.py:463
  5.4 6.2 %collective-permute-start = (bf16[32,1024]{1,0:T(8,128)(2,1)S(1)}, bf16[32,1024]{1,0:T(8,128)(2,1)S(1)}, u32[]{:S(2)}, u32[]{:S(2)}) collective-permute-start(bf16[32,1024]{1,0:T(8,128)(2,1)S(1)} %get-tuple-element.26), channel_id=1, source_target_pairs={{0,0},{1,4},{2,8},{3,12},{4,1},{5,5},{6,9},{7,13},{8,2},{9,6},{10,... | collective-permute-start | bytes 196616 | tf_op jit(solution)/shard_map/ppermute | solution.py:462
  11.6 3.4 %collective-permute-start.2 = (bf16[64,1024]{1,0:T(8,128)(2,1)S(1)}, bf16[64,1024]{1,0:T(8,128)(2,1)S(1)}, u32[]{:S(2)}, u32[]{:S(2)}) collective-permute-start(bf16[64,1024]{1,0:T(8,128)(2,1)S(1)} %join.1.joined_ref), channel_id=1, source_target_pairs={{0,1},{1,0},{2,3},{3,2},{4,5},{5,4},{6,7},{7,6},{8,9},{9,8},{10,11... | collective-permute-start | bytes 393224 | tf_op jit(solution)/shard_map/ppermute | solution.py:479
  16.1 11.3 %collective-permute-start.5 = (bf16[32,1024]{1,0:T(8,128)(2,1)S(1)}, bf16[32,1024]{1,0:T(8,128)(2,1)S(1)}, u32[]{:S(2)}, u32[]{:S(2)}) collective-permute-start(bf16[32,1024]{1,0:T(8,128)(2,1)S(1)} %get-tuple-element.43), channel_id=1, source_target_pairs={{0,12},{4,8},{8,4},{12,0},{1,13},{5,9},{9,5},{13,1},{2,14},{6,10},... | collective-permute-start | bytes 196616 | tf_op jit(solution)/shard_map/ppermute | solution.py:488
  21.9 5.4 %collective-permute-start.4 = (bf16[32,1024]{1,0:T(8,128)(2,1)S(1)}, bf16[32,1024]{1,0:T(8,128)(2,1)S(1)}, u32[]{:S(2)}, u32[]{:S(2)}) collective-permute-start(bf16[32,1024]{1,0:T(8,128)(2,1)S(1)} %get-tuple-element.44), channel_id=1, source_target_pairs={{0,8},{4,12},{8,0},{12,4},{1,9},{5,13},{9,1},{13,5},{2,10},{6,14},... | collective-permute-start | bytes 196616 | tf_op jit(solution)/shard_map/ppermute | solution.py:488
  21.9 5.7 %collective-permute-start.3 = (bf16[32,1024]{1,0:T(8,128)(2,1)S(1)}, bf16[32,1024]{1,0:T(8,128)(2,1)S(1)}, u32[]{:S(2)}, u32[]{:S(2)}) collective-permute-start(bf16[32,1024]{1,0:T(8,128)(2,1)S(1)} %get-tuple-element.45), channel_id=1, source_target_pairs={{0,4},{4,0},{8,12},{12,8},{1,5},{5,1},{9,13},{13,9},{2,6},{6,2},{1... | collective-permute-start | bytes 196616 | tf_op jit(solution)/shard_map/ppermute | solution.py:488
  22.6 5.0 %copy-start = (bf16[1024,4]{0,1:T(4,128)(2,1)S(1)}, bf16[1024,4]{0,1:T(4,128)(2,1)}, u32[]{:S(2)}) copy-start(bf16[1024,4]{0,1:T(4,128)(2,1)} %param.14) | copy-start | bytes 24580
  22.6 5.0 %copy-start.1 = (bf16[2,1024]{1,0:T(2,128)(2,1)S(1)}, bf16[2,1024]{1,0:T(2,128)(2,1)}, u32[]{:S(2)}) copy-start(bf16[2,1024]{1,0:T(2,128)(2,1)} %gain_ref.1) | copy-start | bytes 12292
  28.4 9.2 %collective-permute-start.8 = (bf16[32,1152]{1,0:T(8,128)(2,1)S(1)}, bf16[32,1152]{1,0:T(8,128)(2,1)S(1)}, u32[]{:S(2)}, u32[]{:S(2)}) collective-permute-start(bf16[32,1152]{1,0:T(8,128)(2,1)S(1)} %norm.1.after_ref.zero_ref), channel_id=1, source_target_pairs={{0,12},{4,8},{8,4},{12,0},{1,13},{5,9},{9,5},{13,1},{2,14},{6,10},... | collective-permute-start | bytes 221192 | tf_op jit(solution)/shard_map/ppermute | solution.py:498
  32.0 5.9 %collective-permute-start.7 = (bf16[32,1152]{1,0:T(8,128)(2,1)S(1)}, bf16[32,1152]{1,0:T(8,128)(2,1)S(1)}, u32[]{:S(2)}, u32[]{:S(2)}) collective-permute-start(bf16[32,1152]{1,0:T(8,128)(2,1)S(1)} %norm.1.after_ref.zero_ref), channel_id=1, source_target_pairs={{0,8},{4,12},{8,0},{12,4},{1,9},{5,13},{9,1},{13,5},{2,10},{6,14},... | collective-permute-start | bytes 221192 | tf_op jit(solution)/shard_map/ppermute | solution.py:498
  32.0 5.9 %collective-permute-start.6 = (bf16[32,1152]{1,0:T(8,128)(2,1)S(1)}, bf16[32,1152]{1,0:T(8,128)(2,1)S(1)}, u32[]{:S(2)}, u32[]{:S(2)}) collective-permute-start(bf16[32,1152]{1,0:T(8,128)(2,1)S(1)} %norm.1.after_ref.zero_ref), channel_id=1, source_target_pairs={{0,4},{4,0},{8,12},{12,8},{1,5},{5,1},{9,13},{13,9},{2,6},{6,2},{1... | collective-permute-start | bytes 221192 | tf_op jit(solution)/shard_map/ppermute | solution.py:498
  37.9 7.6 %collective-permute-start.11 = (bf16[64,1152]{1,0:T(8,128)(2,1)S(1)}, bf16[64,1152]{1,0:T(8,128)(2,1)S(1)}, u32[]{:S(2)}, u32[]{:S(2)}) collective-permute-start(bf16[64,1152]{1,0:T(8,128)(2,1)S(1)} %get-tuple-element.30), channel_id=1, source_target_pairs={{0,18},{2,16},{16,2},{18,0},{1,19},{3,17},{17,3},{19,1},{4,22},{6,... | collective-permute-start | bytes 442376 | tf_op jit(solution)/shard_map/ppermute | solution.py:508
  39.8 7.6 %collective-permute-start.9 = (bf16[64,1152]{1,0:T(8,128)(2,1)S(1)}, bf16[64,1152]{1,0:T(8,128)(2,1)S(1)}, u32[]{:S(2)}, u32[]{:S(2)}) collective-permute-start(bf16[64,1152]{1,0:T(8,128)(2,1)S(1)} %get-tuple-element.30), channel_id=1, source_target_pairs={{0,16},{16,0},{1,17},{17,1},{2,18},{18,2},{3,19},{19,3},{4,20},{20... | collective-permute-start | bytes 442376 | tf_op jit(solution)/shard_map/ppermute | solution.py:509
  40.3 7.4 %collective-permute-start.10 = (bf16[64,1152]{1,0:T(8,128)(2,1)S(1)}, bf16[64,1152]{1,0:T(8,128)(2,1)S(1)}, u32[]{:S(2)}, u32[]{:S(2)}) collective-permute-start(bf16[64,1152]{1,0:T(8,128)(2,1)S(1)} %get-tuple-element.29.own_ref), channel_id=1, source_target_pairs={{0,2},{2,0},{1,3},{3,1},{4,6},{6,4},{5,7},{7,5},{8,10},{10,8},{9,1... | collective-permute-start | bytes 442376 | tf_op jit(solution)/shard_map/ppermute | solution.py:510
  51.4 3.7 %collective-permute-start.12 = (bf16[2768,128]{1,0:T(8,128)(2,1)S(1)}, bf16[2768,128]{1,0:T(8,128)(2,1)S(1)}, u32[]{:S(2)}, u32[]{:S(2)}) collective-permute-start(bf16[2768,128]{1,0:T(8,128)(2,1)S(1)} %get-tuple-element.31.gate_ref), channel_id=1, source_target_pairs={{0,1},{1,0},{2,3},{3,2},{4,5},{5,4},{6,7},{7,6},{8,9},{9,8},{10,11... | collective-permute-start | bytes 2125832 | tf_op jit(solution)/shard_map/ppermute | solution.py:524
  54.5 2.4 %collective-permute-start.13 = (bf16[2752,128]{1,0:T(8,128)(2,1)S(1)}, bf16[2752,128]{1,0:T(8,128)(2,1)S(1)}, u32[]{:S(2)}, u32[]{:S(2)}) collective-permute-start(bf16[2752,128]{1,0:T(8,128)(2,1)S(1)} %up.1.up_ref), channel_id=1, source_target_pairs={{0,1},{1,0},{2,3},{3,2},{4,5},{5,4},{6,7},{7,6},{8,9},{9,8},{10,11... | collective-permute-start | bytes 2113544 | tf_op jit(solution)/shard_map/ppermute | solution.py:525
  59.8 6.4 %collective-permute-start.14 = (bf16[64,1024]{1,0:T(8,128)(2,1)S(1)}, bf16[64,1024]{1,0:T(8,128)(2,1)S(1)}, u32[]{:S(2)}, u32[]{:S(2)}) collective-permute-start(bf16[64,1024]{1,0:T(8,128)(2,1)S(1)} %get-tuple-element.36), channel_id=1, source_target_pairs={{0,2},{2,0},{1,3},{3,1},{4,6},{6,4},{5,7},{7,5},{8,10},{10,8},{9,1... | collective-permute-start | bytes 393224 | tf_op jit(solution)/shard_map/ppermute | solution.py:552
  60.7 8.3 %collective-permute-start.15 = (bf16[64,1024]{1,0:T(8,128)(2,1)S(1)}, bf16[64,1024]{1,0:T(8,128)(2,1)S(1)}, u32[]{:S(2)}, u32[]{:S(2)}) collective-permute-start(bf16[64,1024]{1,0:T(8,128)(2,1)S(1)} %get-tuple-element.37), channel_id=1, source_target_pairs={{0,16},{16,0},{1,17},{17,1},{2,18},{18,2},{3,19},{19,3},{4,20},{20... | collective-permute-start | bytes 393224 | tf_op jit(solution)/shard_map/ppermute | solution.py:551
  61.9 7.1 %collective-permute-start.16 = (bf16[64,1024]{1,0:T(8,128)(2,1)S(1)}, bf16[64,1024]{1,0:T(8,128)(2,1)S(1)}, u32[]{:S(2)}, u32[]{:S(2)}) collective-permute-start(bf16[64,1024]{1,0:T(8,128)(2,1)S(1)} %get-tuple-element.38), channel_id=1, source_target_pairs={{0,18},{2,16},{16,2},{18,0},{1,19},{3,17},{17,3},{19,1},{4,22},{6,... | collective-permute-start | bytes 393224 | tf_op jit(solution)/shard_map/ppermute | solution.py:550
  69.6 4.5 %collective-permute-start.17 = (bf16[32,1024]{1,0:T(8,128)(2,1)S(1)}, bf16[32,1024]{1,0:T(8,128)(2,1)S(1)}, u32[]{:S(2)}, u32[]{:S(2)}) collective-permute-start(bf16[32,1024]{1,0:T(8,128)(2,1)S(1)} %get-tuple-element.40), channel_id=1, source_target_pairs={{0,4},{4,0},{8,12},{12,8},{1,5},{5,1},{9,13},{13,9},{2,6},{6,2},{1... | collective-permute-start | bytes 196616 | tf_op jit(solution)/shard_map/ppermute | solution.py:560
  69.7 5.7 %collective-permute-start.18 = (bf16[32,1024]{1,0:T(8,128)(2,1)S(1)}, bf16[32,1024]{1,0:T(8,128)(2,1)S(1)}, u32[]{:S(2)}, u32[]{:S(2)}) collective-permute-start(bf16[32,1024]{1,0:T(8,128)(2,1)S(1)} %get-tuple-element.41), channel_id=1, source_target_pairs={{0,8},{4,12},{8,0},{12,4},{1,9},{5,13},{9,1},{13,5},{2,10},{6,14},... | collective-permute-start | bytes 196616 | tf_op jit(solution)/shard_map/ppermute | solution.py:560
  72.0 6.2 %collective-permute-start.19 = (bf16[32,1024]{1,0:T(8,128)(2,1)S(1)}, bf16[32,1024]{1,0:T(8,128)(2,1)S(1)}, u32[]{:S(2)}, u32[]{:S(2)}) collective-permute-start(bf16[32,1024]{1,0:T(8,128)(2,1)S(1)} %get-tuple-element.42), channel_id=1, source_target_pairs={{0,12},{4,8},{8,4},{12,0},{1,13},{5,9},{9,5},{13,1},{2,14},{6,10},... | collective-permute-start | bytes 196616 | tf_op jit(solution)/shard_map/ppermute | solution.py:560

commit v5 on v4

--- a/solution.py
+++ b/solution.py
@@ -158,7 +158,7 @@
 
 
 SWAP = [(0, 1), (1, 0)]
-CHUNK = 512
+CHUNK = 1024
 STRIP = 688
 TILE = 16
 ON_CHIP = pl.BlockSpec(memory_space=pltpu.VMEM)
@@ -189,26 +189,33 @@
     return jax.ShapeDtypeStruct(shape, dtype)
 
 
-def keep_kernel(ids_ref, after_ref, weight_ref, held_ref, semaphore):
-    copy = pltpu.make_async_copy(weight_ref.at[ids_ref[GROUP]], held_ref, semaphore)
-    copy.start()
-    copy.wait()
+def keep_kernel(spans, ids_ref, after_ref, *refs):
+    count = len(spans)
+    weights, held, semaphores = refs[:count], refs[count : 2 * count], refs[-1]
+    copies = [
+        pltpu.make_async_copy(weight.at[ids_ref[GROUP], a:b], to, semaphores.at[n])
+        for n, (weight, to, (a, b)) in enumerate(zip(weights, held, spans))
+    ]
+    for copy in copies:
+        copy.start()
+    for copy in copies:
+        copy.wait()
 
 
 def in_hbm(value):
     return pltpu.with_memory_space_constraint(value, pltpu.HBM)
 
 
-def keep_on_chip(ids, after, weight, name):
-    shape = weight.shape[1:]
+def keep_on_chip(ids, after, weights, spans, name):
+    width = weights[0].shape[2]
     return call(
-        keep_kernel,
+        functools.partial(keep_kernel, spans),
         name,
-        pltpu.VMEM(shape, jnp.bfloat16),
-        [SCALARS, ANYWHERE, IN_HBM],
-        [ids, after, in_hbm(weight)],
-        scratch=[pltpu.SemaphoreType.DMA(())],
-        moved=2 * shape[0] * shape[1],
+        [pltpu.VMEM((b - a, width), jnp.bfloat16) for a, b in spans],
+        [SCALARS, ANYWHERE] + [IN_HBM] * len(spans),
+        [ids, after] + [in_hbm(weight) for weight in weights],
+        scratch=[pltpu.SemaphoreType.DMA((len(spans),))],
+        moved=2 * width * sum(b - a for a, b in spans),
         limit=1 << 20,
     )
 
@@ -240,7 +247,7 @@
     copies = [
         pltpu.make_async_copy(residual_hbm, residual_ref, semaphores.at[0]),
         pltpu.make_async_copy(proj_ref, proj_held, semaphores.at[1]),
-        pltpu.make_async_copy(gate_ref.at[ids_ref[GROUP]], gate_held, semaphores.at[2]),
+        pltpu.make_async_copy(gate_ref.at[ids_ref[GROUP], : gate_held.shape[0]], gate_held, semaphores.at[2]),
     ]
     for copy in copies:
         copy.start()
@@ -305,19 +312,22 @@
         given_ref[v * half : (v + 1) * half, :] = ref[half:, :]
 
 
-def weight_times_rows(weight_ref, rows, out_ref):
-    units = weight_ref.shape[0]
-    for start in range(0, units, STRIP):
-        stop = min(start + STRIP, units)
-        out_ref[start:stop, :] = lax.dot_general(
-            weight_ref[start:stop, :], rows, (((1,), (1,)), ((), ())), preferred_element_type=jnp.float32
-        ).astype(jnp.bfloat16)
-
-
-def gate_kernel(ids_ref, own_ref, far_ref, side_own_ref, side_far_ref, weight_ref, out_ref, rows_ref):
+def weights_times_rows(weight_refs, rows, out_ref):
+    at = 0
+    for weight_ref in weight_refs:
+        for start in range(0, weight_ref.shape[0], STRIP):
+            stop = min(start + STRIP, weight_ref.shape[0])
+            out_ref[at : at + stop - start, :] = lax.dot_general(
+                weight_ref[start:stop, :], rows, (((1,), (1,)), ((), ())), preferred_element_type=jnp.float32
+            ).astype(jnp.bfloat16)
+            at += stop - start
+
+
+def gate_kernel(ids_ref, own_ref, far_ref, side_own_ref, side_far_ref, *refs):
+    weight_refs, out_ref, rows_ref = refs[:2], refs[-2], refs[-1]
     half = own_ref.shape[0]
-    units, width = weight_ref.shape
-    columns = width // 2
+    units = out_ref.shape[0] - TILE
+    columns = rows_ref.shape[1] // 2
     for side in range(2):
 
         @pl.when(ids_ref[SIDE] == side)
@@ -328,7 +338,7 @@
             rows_ref[:half, there : there + columns] = side_own_ref[:, :columns]
             rows_ref[half:, there : there + columns] = side_far_ref[:, :columns]
 
-    weight_times_rows(weight_ref, rows_ref[...], out_ref)
+    weights_times_rows(weight_refs, rows_ref[...], out_ref)
     tails = [ref[:, columns:].astype(jnp.float32) for ref in (own_ref, side_own_ref, far_ref, side_far_ref)]
     stat = jnp.concatenate([tails[0] + tails[1], tails[2] + tails[3]], axis=0).T
     squares = stat[0:1] + stat[1:2]
@@ -340,8 +350,9 @@
     out_ref[units:, :] = extra.astype(jnp.bfloat16)
 
 
-def up_kernel(rows_ref, weight_ref, out_ref):
-    weight_times_rows(weight_ref, rows_ref[...], out_ref)
+def up_kernel(rows_ref, *refs):
+    weight_refs, out_ref = refs[:-1], refs[-1]
+    weights_times_rows(weight_refs, rows_ref[...], out_ref)
 
 
 def silu_kernel(gate_ref, gate_other_ref, out_ref, stat_ref):
@@ -359,39 +370,29 @@
         out_ref[start:stop, :] = gate / (1.0 + jnp.exp(-gate)) * inverse
 
 
-def scored_product(act_ref, weight_ref, stat_ref, quarter, span, out_refs):
-    rows = act_ref.shape[1]
-    columns = out_refs[0].shape[1]
-    score = jnp.broadcast_to(stat_ref[1:2, :], (rows, rows)).T[span, 0:1]
-    for start in range(0, columns, CHUNK):
-        at = pl.multiple_of(quarter * columns + start, CHUNK)
-        value = lax.dot_general(
-            act_ref[:, span], weight_ref[:, pl.ds(at, CHUNK)], (((0,), (0,)), ((), ())),
-            preferred_element_type=jnp.float32,
-        )
-        value = (value * score).astype(jnp.bfloat16)
-        done = 0
-        for out_ref in out_refs:
-            out_ref[:, start : start + CHUNK] = value[done : done + out_ref.shape[0]]
-            done += out_ref.shape[0]
-
-
-def down_sent_kernel(
-    ids_ref, silu_ref, stat_ref, up_ref, up_other_ref, weight_ref, side_ref, side_far_ref, far_ref, act_ref
+def down_kernel(
+    ids_ref, silu_ref, stat_ref, up_ref, up_other_ref, weight_ref, kept_ref, far_ref, side_ref, side_far_ref, act_ref
 ):
     units, rows = act_ref.shape
     for start in range(0, units, STRIP):
         stop = min(start + STRIP, units)
         up = up_ref[start:stop, :].astype(jnp.float32) + up_other_ref[start:stop, :].astype(jnp.float32)
         act_ref[start:stop, :] = (silu_ref[start:stop, :] * up).astype(jnp.bfloat16)
-    side = ids_ref[SIDE]
-    scored_product(act_ref, weight_ref, stat_ref, 1 - side, slice(0, rows), (side_ref, side_far_ref))
-    scored_product(act_ref, weight_ref, stat_ref, side, slice(rows // 2, rows), (far_ref,))
-
-
-def down_kept_kernel(ids_ref, act_ref, stat_ref, weight_ref, kept_ref):
-    rows = act_ref.shape[1]
-    scored_product(act_ref, weight_ref, stat_ref, ids_ref[SIDE], slice(0, rows // 2), (kept_ref,))
+    half, columns = kept_ref.shape
+    score = jnp.broadcast_to(stat_ref[1:2, :], (rows, rows)).T[:, 0:1]
+    for start in range(0, 2 * columns, CHUNK):
+        value = lax.dot_general(
+            act_ref[...], weight_ref[:, start : start + CHUNK], (((0,), (0,)), ((), ())),
+            preferred_element_type=jnp.float32,
+        )
+        value = (value * score).astype(jnp.bfloat16)
+        quarter, at = divmod(start, columns)
+        for across, (own_out, far_out) in enumerate(((kept_ref, far_ref), (side_ref, side_far_ref))):
+
+            @pl.when((ids_ref[SIDE] ^ quarter) == across)
+            def _():
+                own_out[:, at : at + CHUNK] = value[:half]
+                far_out[:, at : at + CHUNK] = value[half:]
 
 
 def merge_kernel(ids_ref, own_ref, kept_ref, side_ref, far_ref, side_far_ref, *out_refs):
@@ -461,21 +462,22 @@
     to_second = [(t * 4 + q, q * 4 + (t ^ 2)) for t in range(4) for q in range(4)]
     near = lax.ppermute(picked, plane, to_first)
     across = lax.ppermute(picked, plane, to_second)
-    gate_held, proj_held, rest = call(
+    units_first = units // 2
+    gate_first, proj_held, rest = call(
         keep_gate_kernel,
         "keep_gate",
         [
-            pltpu.VMEM((units, width), jnp.bfloat16),
+            pltpu.VMEM((units_first, width), jnp.bfloat16),
             pltpu.VMEM(out_proj.shape, jnp.bfloat16),
             array(slots, columns, dtype=jnp.float32),
         ],
         [SCALARS, ON_CHIP, IN_HBM, IN_HBM, IN_HBM],
         [ids, pick, in_hbm(residual), in_hbm(gate_weight.swapaxes(1, 2)), in_hbm(out_proj)],
         scratch=[pltpu.VMEM((tokens, columns), jnp.bfloat16), pltpu.SemaphoreType.DMA((3,))],
-        moved=2 * units * width,
+        moved=units * width,
         limit=2 << 20,
     )
-    joined = call(join_kernel, "join", array(half, columns), [ON_CHIP] * 3, [near, across, gate_held])
+    joined = call(join_kernel, "join", array(half, columns), [ON_CHIP] * 3, [near, across, gate_first])
     other = lax.ppermute(joined, "fsdp", SWAP)
     partial = call(
         project_kernel,
@@ -486,40 +488,48 @@
         scratch=[pltpu.VMEM((rows, columns), jnp.bfloat16)],
     )
     sums = [lax.ppermute(partial[v], "tok", crossed(2, v)) for v in (1, 2, 3)]
-    up_held = keep_on_chip(ids, partial, up_weight.swapaxes(1, 2), "keep_up")
+    gate_second, up_first = keep_on_chip(
+        ids,
+        partial,
+        [gate_weight.swapaxes(1, 2), up_weight.swapaxes(1, 2)],
+        [(units_first, units), (0, units // 4)],
+        "keep_more",
+    )
     packed_columns = columns + STAT_COLS
     packed = call(
         norm_kernel,
         "norm",
         array(slots, packed_columns),
         [SCALARS, SCALARS] + [ON_CHIP] * 8,
-        [ids, block_modality, rest, partial, *sums, norm_gain, router_weight.T, up_held],
+        [ids, block_modality, rest, partial, *sums, norm_gain, router_weight.T, up_first],
     )
     others = [lax.ppermute(packed, "tok", crossed(2, v)) for v in (1, 2, 3)]
-    down_held = keep_on_chip(ids, packed, down_weight, "keep_down")
+    (up_second,) = keep_on_chip(ids, packed, [up_weight.swapaxes(1, 2)], [(units // 4, units)], "keep_up")
     own, given = call(
         arrange_kernel,
         "arrange",
         [array(half, packed_columns)] * 2,
         [ON_CHIP] * 5,
-        [packed, *others, down_held],
+        [packed, *others, up_second],
     )
     both_axes = ("groups", "mod")
     side_far = lax.ppermute(given, both_axes, crossed(2, 3))
     far = lax.ppermute(given, "groups", SWAP)
     side_own = lax.ppermute(own, "mod", SWAP)
+
+    (down_held,) = keep_on_chip(ids, own, [down_weight], [(0, units)], "keep_down")
 
     flops = 2 * rows * units * width
     gate, gathered = call(
         gate_kernel,
         "gate",
         [array(units + TILE, rows), array(rows, width)],
-        [SCALARS] + [ON_CHIP] * 5,
-        [ids, own, far, side_own, side_far, gate_held],
+        [SCALARS] + [ON_CHIP] * 7,
+        [ids, own, far, side_own, side_far, gate_first, gate_second, down_held],
         flops=flops,
     )
     up = call(
-        up_kernel, "up", array(units, rows), [ON_CHIP] * 2, [gathered, up_held], flops=flops
+        up_kernel, "up", array(units, rows), [ON_CHIP] * 3, [gathered, up_first, up_second], flops=flops
     )
     gate_other = lax.ppermute(gate, "fsdp", SWAP)
     up_other = lax.ppermute(up, "fsdp", SWAP)
@@ -531,21 +541,14 @@
         [gate, gate_other],
         moved=8 * units * rows,
     )
-    to_side, to_side_far, to_far, act = call(
-        down_sent_kernel,
-        "down_sent",
-        [array(half, columns)] * 3 + [array(units, rows)],
+    kept, to_far, to_side, to_side_far = call(
+        down_kernel,
+        "down",
+        [array(half, columns)] * 4,
         [SCALARS] + [ON_CHIP] * 5,
         [ids, silu, stat, up, up_other, down_held],
-        flops=flops // 4 * 3,
-    )
-    kept = call(
-        down_kept_kernel,
-        "down_kept",
-        array(half, columns),
-        [SCALARS] + [ON_CHIP] * 3,
-        [ids, act, stat, down_held],
-        flops=flops // 4,
+        scratch=[pltpu.VMEM((units, rows), jnp.bfloat16)],
+        flops=flops,
     )
     from_side_far = lax.ppermute(to_side_far, both_axes, crossed(2, 3))
     from_far = lax.ppermute(to_far, "groups", SWAP)

time: 79.5 us -> 77.6 us (0.976)
  starting transfers between devices: 29.3 us -> 28.5 us
    ppermute x1, waiting for transfers between devices: 4.04 us -> 0.01 us  [paired_local(): side_far = lax.ppermute(given, both_axes, crossed(2, 3))]
    ppermute x1, waiting for transfers between devices: 2.72 us -> 4.17 us  [paired_local(): from_far = lax.ppermute(to_far, 'groups', SWAP)]
    ppermute x1, waiting for transfers between devices: 1.16 us -> 2.42 us  [paired_local(): from_side = lax.ppermute(to_side, 'mod', SWAP)]
    ppermute x1, starting transfers between devices: 0.82 us -> 1.87 us  [paired_local(): from_side = lax.ppermute(to_side, 'mod', SWAP)]
    ppermute x1, starting transfers between devices: 1.16 us -> 0.14 us  [paired_local(): side_own = lax.ppermute(own, 'mod', SWAP)]
    ppermute x1, starting transfers between devices: 1.89 us -> 2.9 us  [paired_local(): side_far = lax.ppermute(given, both_axes, crossed(2, 3))]
  transfers between devices with their start and end apart: 20 -> 20, of which waited for: 12 -> 11; matrix products, arithmetic and copies ran while one was open for 0% -> 0% of each run, Pallas kernels for 26% -> 26%
where the time goes in v5:
time: 77.6 us; the launch traced here: 77.4 us
  Pallas kernels  31.7 us (41%)
  starting transfers between devices  28.5 us (37%)
  waiting for transfers between devices  16.3 us (21%)
  between operations  0.81 us (1%)
    pallas_call x15, Pallas kernels, call(): pl.pallas_call(kernel, out_shape=outs, in_specs=specs, out_specs=jax.tree...  31.7 us
    ppermute x3, starting transfers between devices, paired_local(): sums = [lax.ppermute(partial[v], 'tok', crossed(2, v)) for v in (1, 2, 3)]  6.51 us
    ppermute x3, starting transfers between devices, paired_local(): others = [lax.ppermute(packed, 'tok', crossed(2, v)) for v in (1, 2, 3)]  4.45 us
    ppermute x3, starting transfers between devices, paired_local(): lax.ppermute(merged[v], 'tok', crossed(2, v))  4.44 us
    ppermute x1, waiting for transfers between devices, paired_local(): from_far = lax.ppermute(to_far, 'groups', SWAP)  4.17 us
    ppermute x3, waiting for transfers between devices, paired_local(): lax.ppermute(merged[v], 'tok', crossed(2, v))  3.72 us
    ppermute x1, starting transfers between devices, paired_local(): across = lax.ppermute(picked, plane, to_second)  2.99 us
    ppermute x1, starting transfers between devices, paired_local(): side_far = lax.ppermute(given, both_axes, crossed(2, 3))  2.9 us
  transfers between devices with their start and end apart: 20, of which 11 were waited for; matrix products, arithmetic and copies ran while one was open for 0% of the time, Pallas kernels for 26%

profile of v5, /device:TPU:0, one launch (start us, length us, event | category | flops | bytes accessed | tf_op | source)
XLA Modules:
  0.0 77.4 jit_solution(12855795982997716523)
XLA Ops:
  0.7 0.1 pad_add_fusion.ids_ref
  0.7 1.7 %select.1 = (bf16[32,1024]{1,0:T(8,128)(2,1)S(1)}, bf16[32,128]{1,0:T(8,128)(2,1)S(1)}) custom-call(s32[3]{0:T(128)S(1)} %pad_add_fusion.ids_ref, s32[1]{0:T(128)S(6)} %copy.11.kind_ref, s32[4,16]{1,0:T(4,128)} %rows_hbm.1, bf16[128,1024]{1,0:T(8,128)(2,1)} %context_hbm.1), custom_call_target="tpu_custom_call" | custom-call | tf_op jit(solution)/shard_map/select/pallas_call | solution.py:176
  2.4 3.0 %collective-permute-start.1 = (bf16[32,1024]{1,0:T(8,128)(2,1)S(1)}, bf16[32,1024]{1,0:T(8,128)(2,1)S(1)}, u32[]{:S(2)}, u32[]{:S(2)}) collective-permute-start(bf16[32,1024]{1,0:T(8,128)(2,1)S(1)} %get-tuple-element.28), channel_id=1, source_target_pairs={{0,2},{1,6},{2,10},{3,14},{4,3},{5,7},{6,11},{7,15},{8,0},{9,4},{1... | collective-permute-start | bytes 196616 | tf_op jit(solution)/shard_map/ppermute | solution.py:464
  5.4 0.7 collective-permute-start
  6.1 3.9 %keep_gate.1 = (bf16[1376,2048]{1,0:T(8,128)(2,1)S(1)}, bf16[1024,1024]{1,0:T(8,128)(2,1)S(1)}, f32[32,1024]{1,0:T(8,128)S(1)}) custom-call(s32[3]{0:T(128)S(1)} %pad_add_fusion.ids_ref, bf16[32,128]{1,0:T(8,128)(2,1)S(1)} %get-tuple-element.26.pick_ref, bf16[128,1024]{1,0:T(8,128)(2,1)} %residual_hbm.1, bf16[2,2752,2048]{2,1,0:T(8,128)(2,1)} %bitcast.13, ...), custom_call_target="tpu_custom_call" | custom-call | bytes 5636096 | tf_op jit(solution)/shard_map/keep_gate/pallas_call | solution.py:176
  10.0 0.8 collective-permute-done.1.across_ref
  10.7 0.0 collective-permute-done.near_ref
  10.7 1.7 %collective-permute-start.2 = (bf16[64,1024]{1,0:T(8,128)(2,1)S(1)}, bf16[64,1024]{1,0:T(8,128)(2,1)S(1)}, u32[]{:S(2)}, u32[]{:S(2)}) collective-permute-start(bf16[64,1024]{1,0:T(8,128)(2,1)S(1)} %join.1.joined_ref), channel_id=1, source_target_pairs={{0,1},{1,0},{2,3},{3,2},{4,5},{5,4},{6,7},{7,6},{8,9},{9,8},{10,11... | collective-permute-start | bytes 393224 | tf_op jit(solution)/shard_map/ppermute | solution.py:481
  12.5 1.0 %collective-permute-done.2.other_ref = bf16[64,1024]{1,0:T(8,128)(2,1)S(1)} collective-permute-done((bf16[64,1024]{1,0:T(8,128)(2,1)S(1)}, bf16[64,1024]{1,0:T(8,128)(2,1)S(1)}, u32[]{:S(2)}, u32[]{:S(2)}) %collective-permute-start.2) | collective-permute-done | bytes 131104 | tf_op jit(solution)/shard_map/ppermute | solution.py:481
  13.4 1.0 %project.1.after_ref.partial_ref = bf16[4,32,1024]{2,1,0:T(8,128)(2,1)S(1)} custom-call(s32[3]{0:T(128)S(1)} %pad_add_fusion.ids_ref, bf16[64,1024]{1,0:T(8,128)(2,1)S(1)} %join.1.joined_ref, bf16[64,1024]{1,0:T(8,128)(2,1)S(1)} %collective-permute-done.2.other_ref, bf16[1024,1024]{1,0:T(8,128)(2,1)S(1)} %get-tuple-element.30.weight_ref), custom_call_target="tpu_custom_call" | custom-call | tf_op jit(solution)/shard_map/project/pallas_call | solution.py:176
  14.5 5.9 %collective-permute-start.5 = (bf16[32,1024]{1,0:T(8,128)(2,1)S(1)}, bf16[32,1024]{1,0:T(8,128)(2,1)S(1)}, u32[]{:S(2)}, u32[]{:S(2)}) collective-permute-start(bf16[32,1024]{1,0:T(8,128)(2,1)S(1)} %get-tuple-element.47), channel_id=1, source_target_pairs={{0,12},{4,8},{8,4},{12,0},{1,13},{5,9},{9,5},{13,1},{2,14},{6,10},... | collective-permute-start | bytes 196616 | tf_op jit(solution)/shard_map/ppermute | solution.py:490
  20.3 0.0 collective-permute-start.4
  20.3 0.6 collective-permute-start.3
  21.0 4.0 %keep_more.1 = (bf16[1376,2048]{1,0:T(8,128)(2,1)S(1)}, bf16[688,2048]{1,0:T(8,128)(2,1)S(1)}) custom-call(s32[3]{0:T(128)S(1)} %pad_add_fusion.ids_ref, bf16[4,32,1024]{2,1,0:T(8,128)(2,1)S(1)} %project.1.after_ref.partial_ref, bf16[2,2752,2048]{2,1,0:T(8,128)(2,1)} %bitcast.14, bf16[2,2752,2048]{2,1,0:T(8,128)(2,1)} %bitcast.15), custom_call_target="tpu_custom_call" | custom-call | bytes 8454144 | tf_op jit(solution)/shard_map/keep_more/pallas_call | solution.py:176
  25.0 0.0 collective-permute-done.5.three_ref
  25.0 0.6 collective-permute-done.4.two_ref
  25.7 0.3 collective-permute-done.3.one_ref
  26.0 0.8 norm.1.after_ref.zero_ref
  26.8 2.9 %collective-permute-start.8 = (bf16[32,1152]{1,0:T(8,128)(2,1)S(1)}, bf16[32,1152]{1,0:T(8,128)(2,1)S(1)}, u32[]{:S(2)}, u32[]{:S(2)}) collective-permute-start(bf16[32,1152]{1,0:T(8,128)(2,1)S(1)} %norm.1.after_ref.zero_ref), channel_id=1, source_target_pairs={{0,12},{4,8},{8,4},{12,0},{1,13},{5,9},{9,5},{13,1},{2,14},{6,10},... | collective-permute-start | bytes 221192 | tf_op jit(solution)/shard_map/ppermute | solution.py:506
  29.6 0.0 collective-permute-start.7
  29.6 1.6 %collective-permute-start.6 = (bf16[32,1152]{1,0:T(8,128)(2,1)S(1)}, bf16[32,1152]{1,0:T(8,128)(2,1)S(1)}, u32[]{:S(2)}, u32[]{:S(2)}) collective-permute-start(bf16[32,1152]{1,0:T(8,128)(2,1)S(1)} %norm.1.after_ref.zero_ref), channel_id=1, source_target_pairs={{0,4},{4,0},{8,12},{12,8},{1,5},{5,1},{9,13},{13,9},{2,6},{6,2},{1... | collective-permute-start | bytes 221192 | tf_op jit(solution)/shard_map/ppermute | solution.py:506
  31.2 4.0 %keep_up.1._.refs_1_ = bf16[2064,2048]{1,0:T(8,128)(2,1)S(1)} custom-call(s32[3]{0:T(128)S(1)} %pad_add_fusion.ids_ref, bf16[32,1152]{1,0:T(8,128)(2,1)S(1)} %norm.1.after_ref.zero_ref, bf16[2,2752,2048]{2,1,0:T(8,128)(2,1)} %bitcast.16), custom_call_target="tpu_custom_call" | custom-call | bytes 8454144 | tf_op jit(solution)/shard_map/keep_up/pallas_call | solution.py:176
  35.2 0.0 collective-permute-done.8.three_ref
  35.2 0.6 collective-permute-done.7.two_ref
  35.8 2.9 %collective-permute-start.11 = (bf16[64,1152]{1,0:T(8,128)(2,1)S(1)}, bf16[64,1152]{1,0:T(8,128)(2,1)S(1)}, u32[]{:S(2)}, u32[]{:S(2)}) collective-permute-start(bf16[64,1152]{1,0:T(8,128)(2,1)S(1)} %get-tuple-element.33), channel_id=1, source_target_pairs={{0,18},{2,16},{16,2},{18,0},{1,19},{3,17},{17,3},{19,1},{4,22},{6,... | collective-permute-start | bytes 442376 | tf_op jit(solution)/shard_map/ppermute | solution.py:516
  38.7 0.5 collective-permute-start.9
  39.2 0.1 collective-permute-start.10
  39.3 4.8 %keep_down.1.refs_2_.weight_ref = bf16[2752,2048]{1,0:T(8,128)(2,1)S(1)} custom-call(s32[3]{0:T(128)S(1)} %pad_add_fusion.ids_ref, bf16[64,1152]{1,0:T(8,128)(2,1)S(1)} %get-tuple-element.32.after_ref.own_ref, bf16[2,2752,2048]{2,1,0:T(8,128)(2,1)} %refs_0_.1), custom_call_target="tpu_custom_call" | custom-call | bytes 11272192 | tf_op jit(solution)/shard_map/keep_down/pallas_call | solution.py:176
  44.1 1.4 %collective-permute-done.9.far_ref = bf16[64,1152]{1,0:T(8,128)(2,1)S(1)} collective-permute-done((bf16[64,1152]{1,0:T(8,128)(2,1)S(1)}, bf16[64,1152]{1,0:T(8,128)(2,1)S(1)}, u32[]{:S(2)}, u32[]{:S(2)}) %collective-permute-start.9) | collective-permute-done | bytes 147488 | tf_op jit(solution)/shard_map/ppermute | solution.py:517
  45.5 3.6 %gate.1 = (bf16[2768,128]{1,0:T(8,128)(2,1)S(1)}, bf16[128,2048]{1,0:T(8,128)(2,1)S(1)}) custom-call(s32[3]{0:T(128)S(1)} %pad_add_fusion.ids_ref, bf16[64,1152]{1,0:T(8,128)(2,1)S(1)} %get-tuple-element.32.after_ref.own_ref, bf16[64,1152]{1,0:T(8,128)(2,1)S(1)} %collective-permute-done.9.far_ref, bf16[64,1152]{1,0:T(8,128)(2,1)S(1)} %collective-permute-done.10.side_own_ref, ...), custom_call_target="tpu_custom_call" | custom-call | flops 1442840576 | tf_op jit(solution)/shard_map/gate/pallas_call | solution.py:176
  49.1 0.1 collective-permute-start.12
  49.2 3.1 %up.1.up_ref = bf16[2752,128]{1,0:T(8,128)(2,1)S(1)} custom-call(bf16[128,2048]{1,0:T(8,128)(2,1)S(1)} %get-tuple-element.38.rows_ref, bf16[688,2048]{1,0:T(8,128)(2,1)S(1)} %get-tuple-element.31._.refs_0_, bf16[2064,2048]{1,0:T(8,128)(2,1)S(1)} %keep_up.1._.refs_1_), custom_call_target="tpu_custom_call" | custom-call | flops 1442840576 | tf_op jit(solution)/shard_map/up/pallas_call | solution.py:176
  52.3 0.6 collective-permute-start.13
  52.9 0.5 silu.1
  53.4 1.3 %collective-permute-done.13.up_other_ref = bf16[2752,128]{1,0:T(8,128)(2,1)S(1)} collective-permute-done((bf16[2752,128]{1,0:T(8,128)(2,1)S(1)}, bf16[2752,128]{1,0:T(8,128)(2,1)S(1)}, u32[]{:S(2)}, u32[]{:S(2)}) %collective-permute-start.13) | collective-permute-done | bytes 704544 | tf_op jit(solution)/shard_map/ppermute | solution.py:535
  54.7 2.6 %down.1 = (bf16[64,1024]{1,0:T(8,128)(2,1)S(1)}, bf16[64,1024]{1,0:T(8,128)(2,1)S(1)}, bf16[64,1024]{1,0:T(8,128)(2,1)S(1)}, bf16[64,1024]{1,0:T(8,128)(2,1)S(1)}) custom-call(s32[3]{0:T(128)S(1)} %pad_add_fusion.ids_ref, f32[2752,128]{1,0:T(8,128)S(1)} %get-tuple-element.36.silu_ref, f32[8,128]{1,0:T(8,128)S(1)} %get-tuple-element.37.stat_ref, ...), custom_call_target="tpu_custom_call" | custom-call | flops 1442840576 | tf_op jit(solution)/shard_map/down/pallas_call | solution.py:176
  57.3 1.9 %collective-permute-start.14 = (bf16[64,1024]{1,0:T(8,128)(2,1)S(1)}, bf16[64,1024]{1,0:T(8,128)(2,1)S(1)}, u32[]{:S(2)}, u32[]{:S(2)}) collective-permute-start(bf16[64,1024]{1,0:T(8,128)(2,1)S(1)} %get-tuple-element.40), channel_id=1, source_target_pairs={{0,2},{2,0},{1,3},{3,1},{4,6},{6,4},{5,7},{7,5},{8,10},{10,8},{9,1... | collective-permute-start | bytes 393224 | tf_op jit(solution)/shard_map/ppermute | solution.py:555
  59.1 0.6 collective-permute-start.15
  59.7 1.1 %collective-permute-start.16 = (bf16[64,1024]{1,0:T(8,128)(2,1)S(1)}, bf16[64,1024]{1,0:T(8,128)(2,1)S(1)}, u32[]{:S(2)}, u32[]{:S(2)}) collective-permute-start(bf16[64,1024]{1,0:T(8,128)(2,1)S(1)} %get-tuple-element.42), channel_id=1, source_target_pairs={{0,18},{2,16},{16,2},{18,0},{1,19},{3,17},{17,3},{19,1},{4,22},{6,... | collective-permute-start | bytes 393224 | tf_op jit(solution)/shard_map/ppermute | solution.py:553
  60.8 2.4 %collective-permute-done.14.side_ref = bf16[64,1024]{1,0:T(8,128)(2,1)S(1)} collective-permute-done((bf16[64,1024]{1,0:T(8,128)(2,1)S(1)}, bf16[64,1024]{1,0:T(8,128)(2,1)S(1)}, u32[]{:S(2)}, u32[]{:S(2)}) %collective-permute-start.14) | collective-permute-done | bytes 131104 | tf_op jit(solution)/shard_map/ppermute | solution.py:555
  63.3 4.2 %collective-permute-done.15.far_ref = bf16[64,1024]{1,0:T(8,128)(2,1)S(1)} collective-permute-done((bf16[64,1024]{1,0:T(8,128)(2,1)S(1)}, bf16[64,1024]{1,0:T(8,128)(2,1)S(1)}, u32[]{:S(2)}, u32[]{:S(2)}) %collective-permute-start.15) | collective-permute-done | bytes 131104 | tf_op jit(solution)/shard_map/ppermute | solution.py:554
  67.4 0.7 merge.1
  68.1 0.1 collective-permute-start.17
  68.2 1.9 %collective-permute-start.18 = (bf16[32,1024]{1,0:T(8,128)(2,1)S(1)}, bf16[32,1024]{1,0:T(8,128)(2,1)S(1)}, u32[]{:S(2)}, u32[]{:S(2)}) collective-permute-start(bf16[32,1024]{1,0:T(8,128)(2,1)S(1)} %get-tuple-element.45), channel_id=1, source_target_pairs={{0,8},{4,12},{8,0},{12,4},{1,9},{5,13},{9,1},{13,5},{2,10},{6,14},... | collective-permute-start | bytes 196616 | tf_op jit(solution)/shard_map/ppermute | solution.py:563
  70.1 2.5 %collective-permute-start.19 = (bf16[32,1024]{1,0:T(8,128)(2,1)S(1)}, bf16[32,1024]{1,0:T(8,128)(2,1)S(1)}, u32[]{:S(2)}, u32[]{:S(2)}) collective-permute-start(bf16[32,1024]{1,0:T(8,128)(2,1)S(1)} %get-tuple-element.46), channel_id=1, source_target_pairs={{0,12},{4,8},{8,4},{12,0},{1,13},{5,9},{9,5},{13,1},{2,14},{6,10},... | collective-permute-start | bytes 196616 | tf_op jit(solution)/shard_map/ppermute | solution.py:563
  72.6 1.0 %collective-permute-done.18.two_ref = bf16[32,1024]{1,0:T(8,128)(2,1)S(1)} collective-permute-done((bf16[32,1024]{1,0:T(8,128)(2,1)S(1)}, bf16[32,1024]{1,0:T(8,128)(2,1)S(1)}, u32[]{:S(2)}, u32[]{:S(2)}) %collective-permute-start.18) | collective-permute-done | bytes 65568 | tf_op jit(solution)/shard_map/ppermute | solution.py:563
  73.6 2.7 %collective-permute-done.19.three_ref = bf16[32,1024]{1,0:T(8,128)(2,1)S(1)} collective-permute-done((bf16[32,1024]{1,0:T(8,128)(2,1)S(1)}, bf16[32,1024]{1,0:T(8,128)(2,1)S(1)}, u32[]{:S(2)}, u32[]{:S(2)}) %collective-permute-start.19) | collective-permute-done | bytes 65568 | tf_op jit(solution)/shard_map/ppermute | solution.py:563
  76.3 1.1 %scatter.1 = bf16[128,1024]{1,0:T(8,128)(2,1)} custom-call(bf16[32,128]{1,0:T(8,128)(2,1)S(1)} %get-tuple-element.26.pick_ref, bf16[32,1024]{1,0:T(8,128)(2,1)S(1)} %get-tuple-element.43.zero_ref, bf16[32,1024]{1,0:T(8,128)(2,1)S(1)} %collective-permute-done.17.one_ref, bf16[32,1024]{1,0:T(8,128)(2,1)S(1)} %collective-permute-done.18.two_ref, ...), custom_call_target="tpu_custom_call" | custom-call | tf_op jit(solution)/shard_map/scatter/pallas_call | solution.py:176
  (13 shorter events, 0.1 us)
Async XLA Ops:
  2.4 8.3 %collective-permute-start.1 = (bf16[32,1024]{1,0:T(8,128)(2,1)S(1)}, bf16[32,1024]{1,0:T(8,128)(2,1)S(1)}, u32[]{:S(2)}, u32[]{:S(2)}) collective-permute-start(bf16[32,1024]{1,0:T(8,128)(2,1)S(1)} %get-tuple-element.28), channel_id=1, source_target_pairs={{0,2},{1,6},{2,10},{3,14},{4,3},{5,7},{6,11},{7,15},{8,0},{9,4},{1... | collective-permute-start | bytes 196616 | tf_op jit(solution)/shard_map/ppermute | solution.py:464
  5.4 5.3 %collective-permute-start = (bf16[32,1024]{1,0:T(8,128)(2,1)S(1)}, bf16[32,1024]{1,0:T(8,128)(2,1)S(1)}, u32[]{:S(2)}, u32[]{:S(2)}) collective-permute-start(bf16[32,1024]{1,0:T(8,128)(2,1)S(1)} %get-tuple-element.28), channel_id=1, source_target_pairs={{0,0},{1,4},{2,8},{3,12},{4,1},{5,5},{6,9},{7,13},{8,2},{9,6},{10,... | collective-permute-start | bytes 196616 | tf_op jit(solution)/shard_map/ppermute | solution.py:463
  10.7 2.7 %collective-permute-start.2 = (bf16[64,1024]{1,0:T(8,128)(2,1)S(1)}, bf16[64,1024]{1,0:T(8,128)(2,1)S(1)}, u32[]{:S(2)}, u32[]{:S(2)}) collective-permute-start(bf16[64,1024]{1,0:T(8,128)(2,1)S(1)} %join.1.joined_ref), channel_id=1, source_target_pairs={{0,1},{1,0},{2,3},{3,2},{4,5},{5,4},{6,7},{7,6},{8,9},{9,8},{10,11... | collective-permute-start | bytes 393224 | tf_op jit(solution)/shard_map/ppermute | solution.py:481
  14.5 10.6 %collective-permute-start.5 = (bf16[32,1024]{1,0:T(8,128)(2,1)S(1)}, bf16[32,1024]{1,0:T(8,128)(2,1)S(1)}, u32[]{:S(2)}, u32[]{:S(2)}) collective-permute-start(bf16[32,1024]{1,0:T(8,128)(2,1)S(1)} %get-tuple-element.47), channel_id=1, source_target_pairs={{0,12},{4,8},{8,4},{12,0},{1,13},{5,9},{9,5},{13,1},{2,14},{6,10},... | collective-permute-start | bytes 196616 | tf_op jit(solution)/shard_map/ppermute | solution.py:490
  20.3 5.3 %collective-permute-start.4 = (bf16[32,1024]{1,0:T(8,128)(2,1)S(1)}, bf16[32,1024]{1,0:T(8,128)(2,1)S(1)}, u32[]{:S(2)}, u32[]{:S(2)}) collective-permute-start(bf16[32,1024]{1,0:T(8,128)(2,1)S(1)} %get-tuple-element.48), channel_id=1, source_target_pairs={{0,8},{4,12},{8,0},{12,4},{1,9},{5,13},{9,1},{13,5},{2,10},{6,14},... | collective-permute-start | bytes 196616 | tf_op jit(solution)/shard_map/ppermute | solution.py:490
  20.3 5.7 %collective-permute-start.3 = (bf16[32,1024]{1,0:T(8,128)(2,1)S(1)}, bf16[32,1024]{1,0:T(8,128)(2,1)S(1)}, u32[]{:S(2)}, u32[]{:S(2)}) collective-permute-start(bf16[32,1024]{1,0:T(8,128)(2,1)S(1)} %get-tuple-element.49), channel_id=1, source_target_pairs={{0,4},{4,0},{8,12},{12,8},{1,5},{5,1},{9,13},{13,9},{2,6},{6,2},{1... | collective-permute-start | bytes 196616 | tf_op jit(solution)/shard_map/ppermute | solution.py:490
  21.0 5.0 %copy-start = (bf16[1024,4]{0,1:T(4,128)(2,1)S(1)}, bf16[1024,4]{0,1:T(4,128)(2,1)}, u32[]{:S(2)}) copy-start(bf16[1024,4]{0,1:T(4,128)(2,1)} %param.14) | copy-start | bytes 24580
  21.0 5.0 %copy-start.1 = (bf16[2,1024]{1,0:T(2,128)(2,1)S(1)}, bf16[2,1024]{1,0:T(2,128)(2,1)}, u32[]{:S(2)}) copy-start(bf16[2,1024]{1,0:T(2,128)(2,1)} %gain_ref.1) | copy-start | bytes 12292
  26.8 8.4 %collective-permute-start.8 = (bf16[32,1152]{1,0:T(8,128)(2,1)S(1)}, bf16[32,1152]{1,0:T(8,128)(2,1)S(1)}, u32[]{:S(2)}, u32[]{:S(2)}) collective-permute-start(bf16[32,1152]{1,0:T(8,128)(2,1)S(1)} %norm.1.after_ref.zero_ref), channel_id=1, source_target_pairs={{0,12},{4,8},{8,4},{12,0},{1,13},{5,9},{9,5},{13,1},{2,14},{6,10},... | collective-permute-start | bytes 221192 | tf_op jit(solution)/shard_map/ppermute | solution.py:506
  29.6 6.1 %collective-permute-start.7 = (bf16[32,1152]{1,0:T(8,128)(2,1)S(1)}, bf16[32,1152]{1,0:T(8,128)(2,1)S(1)}, u32[]{:S(2)}, u32[]{:S(2)}) collective-permute-start(bf16[32,1152]{1,0:T(8,128)(2,1)S(1)} %norm.1.after_ref.zero_ref), channel_id=1, source_target_pairs={{0,8},{4,12},{8,0},{12,4},{1,9},{5,13},{9,1},{13,5},{2,10},{6,14},... | collective-permute-start | bytes 221192 | tf_op jit(solution)/shard_map/ppermute | solution.py:506
  29.6 6.1 %collective-permute-start.6 = (bf16[32,1152]{1,0:T(8,128)(2,1)S(1)}, bf16[32,1152]{1,0:T(8,128)(2,1)S(1)}, u32[]{:S(2)}, u32[]{:S(2)}) collective-permute-start(bf16[32,1152]{1,0:T(8,128)(2,1)S(1)} %norm.1.after_ref.zero_ref), channel_id=1, source_target_pairs={{0,4},{4,0},{8,12},{12,8},{1,5},{5,1},{9,13},{13,9},{2,6},{6,2},{1... | collective-permute-start | bytes 221192 | tf_op jit(solution)/shard_map/ppermute | solution.py:506
  35.8 8.3 %collective-permute-start.11 = (bf16[64,1152]{1,0:T(8,128)(2,1)S(1)}, bf16[64,1152]{1,0:T(8,128)(2,1)S(1)}, u32[]{:S(2)}, u32[]{:S(2)}) collective-permute-start(bf16[64,1152]{1,0:T(8,128)(2,1)S(1)} %get-tuple-element.33), channel_id=1, source_target_pairs={{0,18},{2,16},{16,2},{18,0},{1,19},{3,17},{17,3},{19,1},{4,22},{6,... | collective-permute-start | bytes 442376 | tf_op jit(solution)/shard_map/ppermute | solution.py:516
  38.7 6.8 %collective-permute-start.9 = (bf16[64,1152]{1,0:T(8,128)(2,1)S(1)}, bf16[64,1152]{1,0:T(8,128)(2,1)S(1)}, u32[]{:S(2)}, u32[]{:S(2)}) collective-permute-start(bf16[64,1152]{1,0:T(8,128)(2,1)S(1)} %get-tuple-element.33), channel_id=1, source_target_pairs={{0,16},{16,0},{1,17},{17,1},{2,18},{18,2},{3,19},{19,3},{4,20},{20... | collective-permute-start | bytes 442376 | tf_op jit(solution)/shard_map/ppermute | solution.py:517
  39.2 6.3 %collective-permute-start.10 = (bf16[64,1152]{1,0:T(8,128)(2,1)S(1)}, bf16[64,1152]{1,0:T(8,128)(2,1)S(1)}, u32[]{:S(2)}, u32[]{:S(2)}) collective-permute-start(bf16[64,1152]{1,0:T(8,128)(2,1)S(1)} %get-tuple-element.32.after_ref.own_ref), channel_id=1, source_target_pairs={{0,2},{2,0},{1,3},{3,1},{4,6},{6,4},{5,7},{7,5},{8,10},{10,8},{9,1... | collective-permute-start | bytes 442376 | tf_op jit(solution)/shard_map/ppermute | solution.py:518
  49.1 3.7 %collective-permute-start.12 = (bf16[2768,128]{1,0:T(8,128)(2,1)S(1)}, bf16[2768,128]{1,0:T(8,128)(2,1)S(1)}, u32[]{:S(2)}, u32[]{:S(2)}) collective-permute-start(bf16[2768,128]{1,0:T(8,128)(2,1)S(1)} %get-tuple-element.35.gate_ref), channel_id=1, source_target_pairs={{0,1},{1,0},{2,3},{3,2},{4,5},{5,4},{6,7},{7,6},{8,9},{9,8},{10,11... | collective-permute-start | bytes 2125832 | tf_op jit(solution)/shard_map/ppermute | solution.py:534
  52.3 2.4 %collective-permute-start.13 = (bf16[2752,128]{1,0:T(8,128)(2,1)S(1)}, bf16[2752,128]{1,0:T(8,128)(2,1)S(1)}, u32[]{:S(2)}, u32[]{:S(2)}) collective-permute-start(bf16[2752,128]{1,0:T(8,128)(2,1)S(1)} %up.1.up_ref), channel_id=1, source_target_pairs={{0,1},{1,0},{2,3},{3,2},{4,5},{5,4},{6,7},{7,6},{8,9},{9,8},{10,11... | collective-permute-start | bytes 2113544 | tf_op jit(solution)/shard_map/ppermute | solution.py:535
  57.3 6.0 %collective-permute-start.14 = (bf16[64,1024]{1,0:T(8,128)(2,1)S(1)}, bf16[64,1024]{1,0:T(8,128)(2,1)S(1)}, u32[]{:S(2)}, u32[]{:S(2)}) collective-permute-start(bf16[64,1024]{1,0:T(8,128)(2,1)S(1)} %get-tuple-element.40), channel_id=1, source_target_pairs={{0,2},{2,0},{1,3},{3,1},{4,6},{6,4},{5,7},{7,5},{8,10},{10,8},{9,1... | collective-permute-start | bytes 393224 | tf_op jit(solution)/shard_map/ppermute | solution.py:555
  59.1 8.3 %collective-permute-start.15 = (bf16[64,1024]{1,0:T(8,128)(2,1)S(1)}, bf16[64,1024]{1,0:T(8,128)(2,1)S(1)}, u32[]{:S(2)}, u32[]{:S(2)}) collective-permute-start(bf16[64,1024]{1,0:T(8,128)(2,1)S(1)} %get-tuple-element.41), channel_id=1, source_target_pairs={{0,16},{16,0},{1,17},{17,1},{2,18},{18,2},{3,19},{19,3},{4,20},{20... | collective-permute-start | bytes 393224 | tf_op jit(solution)/shard_map/ppermute | solution.py:554
  59.7 7.7 %collective-permute-start.16 = (bf16[64,1024]{1,0:T(8,128)(2,1)S(1)}, bf16[64,1024]{1,0:T(8,128)(2,1)S(1)}, u32[]{:S(2)}, u32[]{:S(2)}) collective-permute-start(bf16[64,1024]{1,0:T(8,128)(2,1)S(1)} %get-tuple-element.42), channel_id=1, source_target_pairs={{0,18},{2,16},{16,2},{18,0},{1,19},{3,17},{17,3},{19,1},{4,22},{6,... | collective-permute-start | bytes 393224 | tf_op jit(solution)/shard_map/ppermute | solution.py:553
  68.1 4.5 %collective-permute-start.17 = (bf16[32,1024]{1,0:T(8,128)(2,1)S(1)}, bf16[32,1024]{1,0:T(8,128)(2,1)S(1)}, u32[]{:S(2)}, u32[]{:S(2)}) collective-permute-start(bf16[32,1024]{1,0:T(8,128)(2,1)S(1)} %get-tuple-element.44), channel_id=1, source_target_pairs={{0,4},{4,0},{8,12},{12,8},{1,5},{5,1},{9,13},{13,9},{2,6},{6,2},{1... | collective-permute-start | bytes 196616 | tf_op jit(solution)/shard_map/ppermute | solution.py:563
  68.2 5.4 %collective-permute-start.18 = (bf16[32,1024]{1,0:T(8,128)(2,1)S(1)}, bf16[32,1024]{1,0:T(8,128)(2,1)S(1)}, u32[]{:S(2)}, u32[]{:S(2)}) collective-permute-start(bf16[32,1024]{1,0:T(8,128)(2,1)S(1)} %get-tuple-element.45), channel_id=1, source_target_pairs={{0,8},{4,12},{8,0},{12,4},{1,9},{5,13},{9,1},{13,5},{2,10},{6,14},... | collective-permute-start | bytes 196616 | tf_op jit(solution)/shard_map/ppermute | solution.py:563
  70.1 6.2 %collective-permute-start.19 = (bf16[32,1024]{1,0:T(8,128)(2,1)S(1)}, bf16[32,1024]{1,0:T(8,128)(2,1)S(1)}, u32[]{:S(2)}, u32[]{:S(2)}) collective-permute-start(bf16[32,1024]{1,0:T(8,128)(2,1)S(1)} %get-tuple-element.46), channel_id=1, source_target_pairs={{0,12},{4,8},{8,4},{12,0},{1,13},{5,9},{9,5},{13,1},{2,14},{6,10},... | collective-permute-start | bytes 196616 | tf_op jit(solution)/shard_map/ppermute | solution.py:563

commit v6 on v5

--- a/solution.py
+++ b/solution.py
@@ -158,7 +158,6 @@
 
 
 SWAP = [(0, 1), (1, 0)]
-CHUNK = 1024
 STRIP = 688
 TILE = 16
 ON_CHIP = pl.BlockSpec(memory_space=pltpu.VMEM)
@@ -193,8 +192,8 @@
     count = len(spans)
     weights, held, semaphores = refs[:count], refs[count : 2 * count], refs[-1]
     copies = [
-        pltpu.make_async_copy(weight.at[ids_ref[GROUP], a:b], to, semaphores.at[n])
-        for n, (weight, to, (a, b)) in enumerate(zip(weights, held, spans))
+        pltpu.make_async_copy(weight.at[ids_ref[GROUP], a:b, c:d], to, semaphores.at[n])
+        for n, (weight, to, (a, b, c, d)) in enumerate(zip(weights, held, spans))
     ]
     for copy in copies:
         copy.start()
@@ -207,15 +206,14 @@
 
 
 def keep_on_chip(ids, after, weights, spans, name):
-    width = weights[0].shape[2]
     return call(
         functools.partial(keep_kernel, spans),
         name,
-        [pltpu.VMEM((b - a, width), jnp.bfloat16) for a, b in spans],
+        [pltpu.VMEM((b - a, d - c), jnp.bfloat16) for a, b, c, d in spans],
         [SCALARS, ANYWHERE] + [IN_HBM] * len(spans),
         [ids, after] + [in_hbm(weight) for weight in weights],
         scratch=[pltpu.SemaphoreType.DMA((len(spans),))],
-        moved=2 * width * sum(b - a for a, b in spans),
+        moved=sum(2 * (b - a) * (d - c) for a, b, c, d in spans),
         limit=1 << 20,
     )
 
@@ -305,11 +303,35 @@
     out_ref[:, columns:] = extra.astype(jnp.bfloat16)
 
 
-def arrange_kernel(zero_ref, one_ref, two_ref, three_ref, _, own_ref, given_ref):
-    half = zero_ref.shape[0] // 2
-    for v, ref in enumerate((zero_ref, one_ref, two_ref, three_ref)):
-        own_ref[v * half : (v + 1) * half, :] = ref[:half, :]
-        given_ref[v * half : (v + 1) * half, :] = ref[half:, :]
+def places(ids_ref, packed_refs, columns):
+    side = ids_ref[SIDE]
+    matches, found, before = [], [], 0
+    for v, ref in enumerate(packed_refs):
+        tail = ref[:, columns:].astype(jnp.float32)
+        lane = lax.broadcasted_iota(jnp.int32, tail.shape, 1)
+        kind = jnp.where(jnp.max(jnp.where(lane == 4, tail, 0.0)) > 0.5, 1, 0)
+        match = kind == side
+        place = jnp.minimum(jnp.where(match, before, v - before), len(packed_refs) - 2)
+        matches.append(match)
+        found.append(place)
+        before = before + jnp.where(match, 1, 0)
+    return matches, found
+
+
+def arrange_kernel(ids_ref, zero_ref, one_ref, two_ref, three_ref, _, *out_refs):
+    packed_refs = (zero_ref, one_ref, two_ref, three_ref)
+    capacity = zero_ref.shape[0] // 2
+    for out_ref in out_refs:
+        out_ref[...] = jnp.zeros(out_ref.shape, out_ref.dtype)
+    matches, found = places(ids_ref, packed_refs, zero_ref.shape[1] - STAT_COLS)
+    for ref, match, place in zip(packed_refs, matches, found):
+        span = pl.ds(pl.multiple_of(place * capacity, capacity), capacity)
+        for wanted, (own_ref, given_ref) in ((True, out_refs[:2]), (False, out_refs[2:])):
+
+            @pl.when(match == wanted)
+            def _():
+                own_ref[span, :] = ref[:capacity, :]
+                given_ref[span, :] = ref[capacity:, :]
 
 
 def weights_times_rows(weight_refs, rows, out_ref):
@@ -326,25 +348,28 @@
 def gate_kernel(ids_ref, own_ref, far_ref, side_own_ref, side_far_ref, *refs):
     weight_refs, out_ref, rows_ref = refs[:2], refs[-2], refs[-1]
     half = own_ref.shape[0]
+    rows = rows_ref.shape[0]
     units = out_ref.shape[0] - TILE
     columns = rows_ref.shape[1] // 2
+    rows_ref[2 * half :, :] = jnp.zeros((rows - 2 * half, 2 * columns), rows_ref.dtype)
     for side in range(2):
 
         @pl.when(ids_ref[SIDE] == side)
         def _():
             here, there = side * columns, (1 - side) * columns
             rows_ref[:half, here : here + columns] = own_ref[:, :columns]
-            rows_ref[half:, here : here + columns] = far_ref[:, :columns]
+            rows_ref[half : 2 * half, here : here + columns] = far_ref[:, :columns]
             rows_ref[:half, there : there + columns] = side_own_ref[:, :columns]
-            rows_ref[half:, there : there + columns] = side_far_ref[:, :columns]
+            rows_ref[half : 2 * half, there : there + columns] = side_far_ref[:, :columns]
 
     weights_times_rows(weight_refs, rows_ref[...], out_ref)
     tails = [ref[:, columns:].astype(jnp.float32) for ref in (own_ref, side_own_ref, far_ref, side_far_ref)]
-    stat = jnp.concatenate([tails[0] + tails[1], tails[2] + tails[3]], axis=0).T
+    unused = jnp.zeros((rows - 2 * half, STAT_COLS), jnp.float32)
+    stat = jnp.concatenate([tails[0] + tails[1], tails[2] + tails[3], unused], axis=0).T
     squares = stat[0:1] + stat[1:2]
     logits = stat[2:3] + stat[3:4]
-    at_row = lax.broadcasted_iota(jnp.int32, (TILE, 2 * half), 0)
-    extra = jnp.zeros((TILE, 2 * half), jnp.float32)
+    at_row = lax.broadcasted_iota(jnp.int32, (TILE, rows), 0)
+    extra = jnp.zeros((TILE, rows), jnp.float32)
     for at, piece in enumerate(split_high_low(squares) + split_high_low(logits)):
         extra = jnp.where(at_row == at, piece, extra)
     out_ref[units:, :] = extra.astype(jnp.bfloat16)
@@ -371,7 +396,8 @@
 
 
 def down_kernel(
-    ids_ref, silu_ref, stat_ref, up_ref, up_other_ref, weight_ref, kept_ref, far_ref, side_ref, side_far_ref, act_ref
+    ids_ref, silu_ref, stat_ref, up_ref, up_other_ref, first_ref, second_ref,
+    kept_ref, far_ref, side_ref, side_far_ref, act_ref,
 ):
     units, rows = act_ref.shape
     for start in range(0, units, STRIP):
@@ -380,10 +406,14 @@
         act_ref[start:stop, :] = (silu_ref[start:stop, :] * up).astype(jnp.bfloat16)
     half, columns = kept_ref.shape
     score = jnp.broadcast_to(stat_ref[1:2, :], (rows, rows)).T[:, 0:1]
-    for start in range(0, 2 * columns, CHUNK):
+    width_first = first_ref.shape[1]
+    for start, weight_ref, a, b in (
+        (0, first_ref, 0, columns),
+        (columns, first_ref, columns, width_first),
+        (width_first, second_ref, 0, 2 * columns - width_first),
+    ):
         value = lax.dot_general(
-            act_ref[...], weight_ref[:, start : start + CHUNK], (((0,), (0,)), ((), ())),
-            preferred_element_type=jnp.float32,
+            act_ref[...], weight_ref[:, a:b], (((0,), (0,)), ((), ())), preferred_element_type=jnp.float32
         )
         value = (value * score).astype(jnp.bfloat16)
         quarter, at = divmod(start, columns)
@@ -391,20 +421,22 @@
 
             @pl.when((ids_ref[SIDE] ^ quarter) == across)
             def _():
-                own_out[:, at : at + CHUNK] = value[:half]
-                far_out[:, at : at + CHUNK] = value[half:]
-
-
-def merge_kernel(ids_ref, own_ref, kept_ref, side_ref, far_ref, side_far_ref, *out_refs):
-    half, columns = kept_ref.shape
-    capacity = half // len(out_refs)
-    side = ids_ref[SIDE].astype(jnp.float32)
-    for v, out_ref in enumerate(out_refs):
-        span = slice(v * capacity, (v + 1) * capacity)
-        valid = own_ref[span, columns : columns + STAT_COLS].astype(jnp.float32)[:, 4:5] == side
-        for e, (mine, other) in enumerate(((kept_ref, side_ref), (far_ref, side_far_ref))):
-            chosen = jnp.where(valid, mine[span, :].astype(jnp.float32), other[span, :].astype(jnp.float32))
-            out_ref[e * capacity : (e + 1) * capacity, :] = chosen.astype(jnp.bfloat16)
+                own_out[:, at : at + b - a] = value[:half]
+                far_out[:, at : at + b - a] = value[half : 2 * half]
+
+
+def merge_kernel(ids_ref, zero_ref, one_ref, two_ref, three_ref, kept_ref, side_ref, far_ref, side_far_ref, *out_refs):
+    columns = kept_ref.shape[1]
+    capacity = zero_ref.shape[0] // 2
+    matches, found = places(ids_ref, (zero_ref, one_ref, two_ref, three_ref), columns)
+    for out_ref, match, place in zip(out_refs, matches, found):
+        span = pl.ds(pl.multiple_of(place * capacity, capacity), capacity)
+        for wanted, (first_ref, second_ref) in ((True, (kept_ref, far_ref)), (False, (side_ref, side_far_ref))):
+
+            @pl.when(match == wanted)
+            def _():
+                out_ref[:capacity, :] = first_ref[span, :]
+                out_ref[capacity:, :] = second_ref[span, :]
 
 
 def scatter_kernel(pick_ref, zero_ref, one_ref, two_ref, three_ref, out_ref):
@@ -492,7 +524,7 @@
         ids,
         partial,
         [gate_weight.swapaxes(1, 2), up_weight.swapaxes(1, 2)],
-        [(units_first, units), (0, units // 4)],
+        [(units_first, units, 0, width), (0, units // 4, 0, width)],
         "keep_more",
     )
     packed_columns = columns + STAT_COLS
@@ -504,20 +536,22 @@
         [ids, block_modality, rest, partial, *sums, norm_gain, router_weight.T, up_first],
     )
     others = [lax.ppermute(packed, "tok", crossed(2, v)) for v in (1, 2, 3)]
-    (up_second,) = keep_on_chip(ids, packed, [up_weight.swapaxes(1, 2)], [(units // 4, units)], "keep_up")
-    own, given = call(
+    (up_second,) = keep_on_chip(ids, packed, [up_weight.swapaxes(1, 2)], [(units // 4, units, 0, width)], "keep_up")
+    kept_slots = 3 * capacity
+    own, to_far_rows, to_side_rows, to_corner_rows = call(
         arrange_kernel,
         "arrange",
-        [array(half, packed_columns)] * 2,
-        [ON_CHIP] * 5,
-        [packed, *others, up_second],
+        [array(kept_slots, packed_columns)] * 4,
+        [SCALARS] + [ON_CHIP] * 5,
+        [ids, packed, *others, up_second],
     )
     both_axes = ("groups", "mod")
-    side_far = lax.ppermute(given, both_axes, crossed(2, 3))
-    far = lax.ppermute(given, "groups", SWAP)
-    side_own = lax.ppermute(own, "mod", SWAP)
-
-    (down_held,) = keep_on_chip(ids, own, [down_weight], [(0, units)], "keep_down")
+    side_far = lax.ppermute(to_corner_rows, both_axes, crossed(2, 3))
+    far = lax.ppermute(to_far_rows, "groups", SWAP)
+    side_own = lax.ppermute(to_side_rows, "mod", SWAP)
+
+    width_first = width // 4 * 3
+    (down_first,) = keep_on_chip(ids, own, [down_weight], [(0, units, 0, width_first)], "keep_down")
 
     flops = 2 * rows * units * width
     gate, gathered = call(
@@ -525,7 +559,7 @@
         "gate",
         [array(units + TILE, rows), array(rows, width)],
         [SCALARS] + [ON_CHIP] * 7,
-        [ids, own, far, side_own, side_far, gate_first, gate_second, down_held],
+        [ids, own, far, side_own, side_far, gate_first, gate_second, down_first],
         flops=flops,
     )
     up = call(
@@ -533,6 +567,7 @@
     )
     gate_other = lax.ppermute(gate, "fsdp", SWAP)
     up_other = lax.ppermute(up, "fsdp", SWAP)
+    (down_second,) = keep_on_chip(ids, up, [down_weight], [(0, units, width_first, width)], "keep_last")
     silu, stat = call(
         silu_kernel,
         "silu",
@@ -544,9 +579,9 @@
     kept, to_far, to_side, to_side_far = call(
         down_kernel,
         "down",
-        [array(half, columns)] * 4,
-        [SCALARS] + [ON_CHIP] * 5,
-        [ids, silu, stat, up, up_other, down_held],
+        [array(kept_slots, columns)] * 4,
+        [SCALARS] + [ON_CHIP] * 6,
+        [ids, silu, stat, up, up_other, down_first, down_second],
         scratch=[pltpu.VMEM((units, rows), jnp.bfloat16)],
         flops=flops,
     )
@@ -557,8 +592,8 @@
         merge_kernel,
         "merge",
         [array(slots, columns)] * 4,
-        [SCALARS] + [ON_CHIP] * 5,
-        [ids, own, kept, from_side, from_far, from_side_far],
+        [SCALARS] + [ON_CHIP] * 8,
+        [ids, packed, *others, kept, from_side, from_far, from_side_far],
     )
     values = [merged[0]] + [lax.ppermute(merged[v], "tok", crossed(2, v)) for v in (1, 2, 3)]
     return call(

time: 77.6 us -> 77.3 us (level)
  waiting for transfers between devices: 16.3 us -> 13.3 us
  Pallas kernels: 31.7 us -> 34.3 us
    pallas_call x15 -> x16, Pallas kernels: 31.7 us -> 34.3 us  [call(): pl.pallas_call(kernel, out_shape=outs, in_specs=specs, out_specs=jax.tree...]
    ppermute x1, waiting for transfers between devices: 4.17 us -> 1.78 us  [paired_local(): from_far = lax.ppermute(to_far, 'groups', SWAP)]
    ppermute x1, waiting for transfers between devices: 0.01 us -> 1.3 us  [paired_local(): from_side_far = lax.ppermute(to_side_far, both_axes, crossed(2, 3))]
    ppermute x1, waiting for transfers between devices: 1.27 us -> 0.01 us  [paired_local(): up_other = lax.ppermute(up, 'fsdp', SWAP)]
    ppermute x1, waiting for transfers between devices: 2.42 us -> 1.46 us  [paired_local(): from_side = lax.ppermute(to_side, 'mod', SWAP)]
    ppermute x1, starting transfers between devices: 0.6 us -> 1.52 us  [paired_local(): from_far = lax.ppermute(to_far, 'groups', SWAP)]
    ppermute x1, starting transfers between devices: 1.87 us -> 1.06 us  [paired_local(): from_side = lax.ppermute(to_side, 'mod', SWAP)]
  transfers between devices with their start and end apart: 20 -> 20, of which waited for: 11 -> 11; matrix products, arithmetic and copies ran while one was open for 0% -> 0% of each run, Pallas kernels for 26% -> 28%
where the time goes in v6:
time: 77.3 us; the launch traced here: 77 us
  Pallas kernels  34.3 us (44%)
  starting transfers between devices  28.5 us (37%)
  waiting for transfers between devices  13.3 us (17%)
  between operations  0.85 us (1%)
    pallas_call x16, Pallas kernels, call(): pl.pallas_call(kernel, out_shape=outs, in_specs=specs, out_specs=jax.tree...  34.3 us
    ppermute x3, starting transfers between devices, paired_local(): sums = [lax.ppermute(partial[v], 'tok', crossed(2, v)) for v in (1, 2, 3)]  6.51 us
    ppermute x3, starting transfers between devices, paired_local(): others = [lax.ppermute(packed, 'tok', crossed(2, v)) for v in (1, 2, 3)]  4.45 us
    ppermute x3, starting transfers between devices, paired_local(): lax.ppermute(merged[v], 'tok', crossed(2, v))  4.44 us
    ppermute x3, waiting for transfers between devices, paired_local(): lax.ppermute(merged[v], 'tok', crossed(2, v))  3.89 us
    ppermute x1, starting transfers between devices, paired_local(): across = lax.ppermute(picked, plane, to_second)  2.99 us
    ppermute x1, starting transfers between devices, paired_local(): side_own = lax.ppermute(to_side_rows, 'mod', SWAP)  1.89 us
    ppermute x1, waiting for transfers between devices, paired_local(): from_far = lax.ppermute(to_far, 'groups', SWAP)  1.78 us
  transfers between devices with their start and end apart: 20, of which 11 were waited for; matrix products, arithmetic and copies ran while one was open for 0% of the time, Pallas kernels for 28%

profile of v6, /device:TPU:0, one launch (start us, length us, event | category | flops | bytes accessed | tf_op | source)
XLA Modules:
  0.0 77.0 jit_solution(8345630023852303196)
XLA Ops:
  0.7 0.1 pad_add_fusion.ids_ref
  0.7 1.7 %select.1 = (bf16[32,1024]{1,0:T(8,128)(2,1)S(1)}, bf16[32,128]{1,0:T(8,128)(2,1)S(1)}) custom-call(s32[3]{0:T(128)S(1)} %pad_add_fusion.ids_ref, s32[1]{0:T(128)S(6)} %copy.11.kind_ref, s32[4,16]{1,0:T(4,128)} %rows_hbm.1, bf16[128,1024]{1,0:T(8,128)(2,1)} %context_hbm.1), custom_call_target="tpu_custom_call" | custom-call | tf_op jit(solution)/shard_map/select/pallas_call | solution.py:175
  2.4 3.0 %collective-permute-start.1 = (bf16[32,1024]{1,0:T(8,128)(2,1)S(1)}, bf16[32,1024]{1,0:T(8,128)(2,1)S(1)}, u32[]{:S(2)}, u32[]{:S(2)}) collective-permute-start(bf16[32,1024]{1,0:T(8,128)(2,1)S(1)} %get-tuple-element.30), channel_id=1, source_target_pairs={{0,2},{1,6},{2,10},{3,14},{4,3},{5,7},{6,11},{7,15},{8,0},{9,4},{1... | collective-permute-start | bytes 196616 | tf_op jit(solution)/shard_map/ppermute | solution.py:496
  5.4 0.7 collective-permute-start
  6.1 3.9 %keep_gate.1 = (bf16[1376,2048]{1,0:T(8,128)(2,1)S(1)}, bf16[1024,1024]{1,0:T(8,128)(2,1)S(1)}, f32[32,1024]{1,0:T(8,128)S(1)}) custom-call(s32[3]{0:T(128)S(1)} %pad_add_fusion.ids_ref, bf16[32,128]{1,0:T(8,128)(2,1)S(1)} %get-tuple-element.28.pick_ref, bf16[128,1024]{1,0:T(8,128)(2,1)} %residual_hbm.1, bf16[2,2752,2048]{2,1,0:T(8,128)(2,1)} %bitcast.13, ...), custom_call_target="tpu_custom_call" | custom-call | bytes 5636096 | tf_op jit(solution)/shard_map/keep_gate/pallas_call | solution.py:175
  10.0 0.8 collective-permute-done.1.across_ref
  10.7 0.0 collective-permute-done.near_ref
  10.7 1.7 %collective-permute-start.2 = (bf16[64,1024]{1,0:T(8,128)(2,1)S(1)}, bf16[64,1024]{1,0:T(8,128)(2,1)S(1)}, u32[]{:S(2)}, u32[]{:S(2)}) collective-permute-start(bf16[64,1024]{1,0:T(8,128)(2,1)S(1)} %join.1.joined_ref), channel_id=1, source_target_pairs={{0,1},{1,0},{2,3},{3,2},{4,5},{5,4},{6,7},{7,6},{8,9},{9,8},{10,11... | collective-permute-start | bytes 393224 | tf_op jit(solution)/shard_map/ppermute | solution.py:513
  12.5 1.0 %collective-permute-done.2.other_ref = bf16[64,1024]{1,0:T(8,128)(2,1)S(1)} collective-permute-done((bf16[64,1024]{1,0:T(8,128)(2,1)S(1)}, bf16[64,1024]{1,0:T(8,128)(2,1)S(1)}, u32[]{:S(2)}, u32[]{:S(2)}) %collective-permute-start.2) | collective-permute-done | bytes 131104 | tf_op jit(solution)/shard_map/ppermute | solution.py:513
  13.4 1.0 %project.1.after_ref.partial_ref = bf16[4,32,1024]{2,1,0:T(8,128)(2,1)S(1)} custom-call(s32[3]{0:T(128)S(1)} %pad_add_fusion.ids_ref, bf16[64,1024]{1,0:T(8,128)(2,1)S(1)} %join.1.joined_ref, bf16[64,1024]{1,0:T(8,128)(2,1)S(1)} %collective-permute-done.2.other_ref, bf16[1024,1024]{1,0:T(8,128)(2,1)S(1)} %get-tuple-element.32.weight_ref), custom_call_target="tpu_custom_call" | custom-call | tf_op jit(solution)/shard_map/project/pallas_call | solution.py:175
  14.5 5.9 %collective-permute-start.5 = (bf16[32,1024]{1,0:T(8,128)(2,1)S(1)}, bf16[32,1024]{1,0:T(8,128)(2,1)S(1)}, u32[]{:S(2)}, u32[]{:S(2)}) collective-permute-start(bf16[32,1024]{1,0:T(8,128)(2,1)S(1)} %get-tuple-element.51), channel_id=1, source_target_pairs={{0,12},{4,8},{8,4},{12,0},{1,13},{5,9},{9,5},{13,1},{2,14},{6,10},... | collective-permute-start | bytes 196616 | tf_op jit(solution)/shard_map/ppermute | solution.py:522
  20.3 0.0 collective-permute-start.4
  20.3 0.6 collective-permute-start.3
  21.0 4.0 %keep_more.1 = (bf16[1376,2048]{1,0:T(8,128)(2,1)S(1)}, bf16[688,2048]{1,0:T(8,128)(2,1)S(1)}) custom-call(s32[3]{0:T(128)S(1)} %pad_add_fusion.ids_ref, bf16[4,32,1024]{2,1,0:T(8,128)(2,1)S(1)} %project.1.after_ref.partial_ref, bf16[2,2752,2048]{2,1,0:T(8,128)(2,1)} %bitcast.14, bf16[2,2752,2048]{2,1,0:T(8,128)(2,1)} %bitcast.15), custom_call_target="tpu_custom_call" | custom-call | bytes 8454144 | tf_op jit(solution)/shard_map/keep_more/pallas_call | solution.py:175
  25.0 0.0 collective-permute-done.5.three_ref
  25.0 0.6 collective-permute-done.4.two_ref
  25.7 0.3 collective-permute-done.3.one_ref
  26.0 0.8 norm.1.after_ref.zero_ref
  26.8 2.9 %collective-permute-start.8 = (bf16[32,1152]{1,0:T(8,128)(2,1)S(1)}, bf16[32,1152]{1,0:T(8,128)(2,1)S(1)}, u32[]{:S(2)}, u32[]{:S(2)}) collective-permute-start(bf16[32,1152]{1,0:T(8,128)(2,1)S(1)} %norm.1.after_ref.zero_ref), channel_id=1, source_target_pairs={{0,12},{4,8},{8,4},{12,0},{1,13},{5,9},{9,5},{13,1},{2,14},{6,10},... | collective-permute-start | bytes 221192 | tf_op jit(solution)/shard_map/ppermute | solution.py:538
  29.6 1.6 %collective-permute-start.6 = (bf16[32,1152]{1,0:T(8,128)(2,1)S(1)}, bf16[32,1152]{1,0:T(8,128)(2,1)S(1)}, u32[]{:S(2)}, u32[]{:S(2)}) collective-permute-start(bf16[32,1152]{1,0:T(8,128)(2,1)S(1)} %norm.1.after_ref.zero_ref), channel_id=1, source_target_pairs={{0,4},{4,0},{8,12},{12,8},{1,5},{5,1},{9,13},{13,9},{2,6},{6,2},{1... | collective-permute-start | bytes 221192 | tf_op jit(solution)/shard_map/ppermute | solution.py:538
  31.2 4.0 %keep_up.1._.refs_1_ = bf16[2064,2048]{1,0:T(8,128)(2,1)S(1)} custom-call(s32[3]{0:T(128)S(1)} %pad_add_fusion.ids_ref, bf16[32,1152]{1,0:T(8,128)(2,1)S(1)} %norm.1.after_ref.zero_ref, bf16[2,2752,2048]{2,1,0:T(8,128)(2,1)} %bitcast.16), custom_call_target="tpu_custom_call" | custom-call | bytes 8454144 | tf_op jit(solution)/shard_map/keep_up/pallas_call | solution.py:175
  35.2 0.6 collective-permute-done.7.two_ref
  35.8 0.7 arrange.1
  36.5 1.6 %collective-permute-start.9 = (bf16[48,1152]{1,0:T(8,128)(2,1)S(1)}, bf16[48,1152]{1,0:T(8,128)(2,1)S(1)}, u32[]{:S(2)}, u32[]{:S(2)}) collective-permute-start(bf16[48,1152]{1,0:T(8,128)(2,1)S(1)} %get-tuple-element.35), channel_id=1, source_target_pairs={{0,16},{16,0},{1,17},{17,1},{2,18},{18,2},{3,19},{19,3},{4,20},{20... | collective-permute-start | bytes 331784 | tf_op jit(solution)/shard_map/ppermute | solution.py:550
  38.1 1.9 %collective-permute-start.10 = (bf16[48,1152]{1,0:T(8,128)(2,1)S(1)}, bf16[48,1152]{1,0:T(8,128)(2,1)S(1)}, u32[]{:S(2)}, u32[]{:S(2)}) collective-permute-start(bf16[48,1152]{1,0:T(8,128)(2,1)S(1)} %get-tuple-element.36), channel_id=1, source_target_pairs={{0,2},{2,0},{1,3},{3,1},{4,6},{6,4},{5,7},{7,5},{8,10},{10,8},{9,1... | collective-permute-start | bytes 331784 | tf_op jit(solution)/shard_map/ppermute | solution.py:551
  39.9 0.1 collective-permute-start.11
  40.0 4.0 %keep_down.1.refs_2_.first_ref = bf16[2752,1536]{1,0:T(8,128)(2,1)S(1)} custom-call(s32[3]{0:T(128)S(1)} %pad_add_fusion.ids_ref, bf16[48,1152]{1,0:T(8,128)(2,1)S(1)} %get-tuple-element.34.after_ref.own_ref, bf16[2,2752,2048]{2,1,0:T(8,128)(2,1)} %refs_0_.3), custom_call_target="tpu_custom_call" | custom-call | bytes 8454144 | tf_op jit(solution)/shard_map/keep_down/pallas_call | solution.py:175
  44.0 1.6 %collective-permute-done.11.side_far_ref = bf16[48,1152]{1,0:T(8,128)(2,1)S(1)} collective-permute-done((bf16[48,1152]{1,0:T(8,128)(2,1)S(1)}, bf16[48,1152]{1,0:T(8,128)(2,1)S(1)}, u32[]{:S(2)}, u32[]{:S(2)}) %collective-permute-start.11) | collective-permute-done | bytes 110624 | tf_op jit(solution)/shard_map/ppermute | solution.py:549
  45.6 3.6 %gate.1 = (bf16[2768,128]{1,0:T(8,128)(2,1)S(1)}, bf16[128,2048]{1,0:T(8,128)(2,1)S(1)}) custom-call(s32[3]{0:T(128)S(1)} %pad_add_fusion.ids_ref, bf16[48,1152]{1,0:T(8,128)(2,1)S(1)} %get-tuple-element.34.after_ref.own_ref, bf16[48,1152]{1,0:T(8,128)(2,1)S(1)} %collective-permute-done.9.far_ref, bf16[48,1152]{1,0:T(8,128)(2,1)S(1)} %collective-permute-done.10.side_own_ref, ...), custom_call_target="tpu_custom_call" | custom-call | flops 1442840576 | tf_op jit(solution)/shard_map/gate/pallas_call | solution.py:175
  49.2 0.1 collective-permute-start.12
  49.3 3.1 %up.1.after_ref.up_ref = bf16[2752,128]{1,0:T(8,128)(2,1)S(1)} custom-call(bf16[128,2048]{1,0:T(8,128)(2,1)S(1)} %get-tuple-element.42.rows_ref, bf16[688,2048]{1,0:T(8,128)(2,1)S(1)} %get-tuple-element.33._.refs_0_, bf16[2064,2048]{1,0:T(8,128)(2,1)S(1)} %keep_up.1._.refs_1_), custom_call_target="tpu_custom_call" | custom-call | flops 1442840576 | tf_op jit(solution)/shard_map/up/pallas_call | solution.py:175
  52.4 0.6 collective-permute-start.13
  52.9 2.3 %keep_last.1.second_ref = bf16[2752,512]{1,0:T(8,128)(2,1)S(1)} custom-call(s32[3]{0:T(128)S(1)} %pad_add_fusion.ids_ref, bf16[2752,128]{1,0:T(8,128)(2,1)S(1)} %up.1.after_ref.up_ref, bf16[2,2752,2048]{2,1,0:T(8,128)(2,1)} %refs_0_.3), custom_call_target="tpu_custom_call" | custom-call | bytes 2818048 | tf_op jit(solution)/shard_map/keep_last/pallas_call | solution.py:175
  55.3 0.5 silu.1
  55.8 2.9 %down.1 = (bf16[48,1024]{1,0:T(8,128)(2,1)S(1)}, bf16[48,1024]{1,0:T(8,128)(2,1)S(1)}, bf16[48,1024]{1,0:T(8,128)(2,1)S(1)}, bf16[48,1024]{1,0:T(8,128)(2,1)S(1)}) custom-call(s32[3]{0:T(128)S(1)} %pad_add_fusion.ids_ref, f32[2752,128]{1,0:T(8,128)S(1)} %get-tuple-element.40.silu_ref, f32[8,128]{1,0:T(8,128)S(1)} %get-tuple-element.41.stat_ref, ...), custom_call_target="tpu_custom_call" | custom-call | flops 1442840576 | tf_op jit(solution)/shard_map/down/pallas_call | solution.py:175
  58.7 1.1 %collective-permute-start.14 = (bf16[48,1024]{1,0:T(8,128)(2,1)S(1)}, bf16[48,1024]{1,0:T(8,128)(2,1)S(1)}, u32[]{:S(2)}, u32[]{:S(2)}) collective-permute-start(bf16[48,1024]{1,0:T(8,128)(2,1)S(1)} %get-tuple-element.44), channel_id=1, source_target_pairs={{0,2},{2,0},{1,3},{3,1},{4,6},{6,4},{5,7},{7,5},{8,10},{10,8},{9,1... | collective-permute-start | bytes 294920 | tf_op jit(solution)/shard_map/ppermute | solution.py:590
  59.8 1.5 %collective-permute-start.15 = (bf16[48,1024]{1,0:T(8,128)(2,1)S(1)}, bf16[48,1024]{1,0:T(8,128)(2,1)S(1)}, u32[]{:S(2)}, u32[]{:S(2)}) collective-permute-start(bf16[48,1024]{1,0:T(8,128)(2,1)S(1)} %get-tuple-element.45), channel_id=1, source_target_pairs={{0,16},{16,0},{1,17},{17,1},{2,18},{18,2},{3,19},{19,3},{4,20},{20... | collective-permute-start | bytes 294920 | tf_op jit(solution)/shard_map/ppermute | solution.py:589
  61.3 1.0 %collective-permute-start.16 = (bf16[48,1024]{1,0:T(8,128)(2,1)S(1)}, bf16[48,1024]{1,0:T(8,128)(2,1)S(1)}, u32[]{:S(2)}, u32[]{:S(2)}) collective-permute-start(bf16[48,1024]{1,0:T(8,128)(2,1)S(1)} %get-tuple-element.46), channel_id=1, source_target_pairs={{0,18},{2,16},{16,2},{18,0},{1,19},{3,17},{17,3},{19,1},{4,22},{6,... | collective-permute-start | bytes 294920 | tf_op jit(solution)/shard_map/ppermute | solution.py:588
  62.3 1.5 %collective-permute-done.14.side_ref = bf16[48,1024]{1,0:T(8,128)(2,1)S(1)} collective-permute-done((bf16[48,1024]{1,0:T(8,128)(2,1)S(1)}, bf16[48,1024]{1,0:T(8,128)(2,1)S(1)}, u32[]{:S(2)}, u32[]{:S(2)}) %collective-permute-start.14) | collective-permute-done | bytes 98336 | tf_op jit(solution)/shard_map/ppermute | solution.py:590
  63.8 1.8 %collective-permute-done.15.far_ref = bf16[48,1024]{1,0:T(8,128)(2,1)S(1)} collective-permute-done((bf16[48,1024]{1,0:T(8,128)(2,1)S(1)}, bf16[48,1024]{1,0:T(8,128)(2,1)S(1)}, u32[]{:S(2)}, u32[]{:S(2)}) %collective-permute-start.15) | collective-permute-done | bytes 98336 | tf_op jit(solution)/shard_map/ppermute | solution.py:589
  65.5 1.3 %collective-permute-done.16.side_far_ref = bf16[48,1024]{1,0:T(8,128)(2,1)S(1)} collective-permute-done((bf16[48,1024]{1,0:T(8,128)(2,1)S(1)}, bf16[48,1024]{1,0:T(8,128)(2,1)S(1)}, u32[]{:S(2)}, u32[]{:S(2)}) %collective-permute-start.16) | collective-permute-done | bytes 98336 | tf_op jit(solution)/shard_map/ppermute | solution.py:588
  66.8 0.7 merge.1
  67.6 0.1 collective-permute-start.17
  67.6 2.2 %collective-permute-start.18 = (bf16[32,1024]{1,0:T(8,128)(2,1)S(1)}, bf16[32,1024]{1,0:T(8,128)(2,1)S(1)}, u32[]{:S(2)}, u32[]{:S(2)}) collective-permute-start(bf16[32,1024]{1,0:T(8,128)(2,1)S(1)} %get-tuple-element.49), channel_id=1, source_target_pairs={{0,8},{4,12},{8,0},{12,4},{1,9},{5,13},{9,1},{13,5},{2,10},{6,14},... | collective-permute-start | bytes 196616 | tf_op jit(solution)/shard_map/ppermute | solution.py:598
  69.8 2.2 %collective-permute-start.19 = (bf16[32,1024]{1,0:T(8,128)(2,1)S(1)}, bf16[32,1024]{1,0:T(8,128)(2,1)S(1)}, u32[]{:S(2)}, u32[]{:S(2)}) collective-permute-start(bf16[32,1024]{1,0:T(8,128)(2,1)S(1)} %get-tuple-element.50), channel_id=1, source_target_pairs={{0,12},{4,8},{8,4},{12,0},{1,13},{5,9},{9,5},{13,1},{2,14},{6,10},... | collective-permute-start | bytes 196616 | tf_op jit(solution)/shard_map/ppermute | solution.py:598
  72.0 1.5 %collective-permute-done.18.two_ref = bf16[32,1024]{1,0:T(8,128)(2,1)S(1)} collective-permute-done((bf16[32,1024]{1,0:T(8,128)(2,1)S(1)}, bf16[32,1024]{1,0:T(8,128)(2,1)S(1)}, u32[]{:S(2)}, u32[]{:S(2)}) %collective-permute-start.18) | collective-permute-done | bytes 65568 | tf_op jit(solution)/shard_map/ppermute | solution.py:598
  73.5 2.4 %collective-permute-done.19.three_ref = bf16[32,1024]{1,0:T(8,128)(2,1)S(1)} collective-permute-done((bf16[32,1024]{1,0:T(8,128)(2,1)S(1)}, bf16[32,1024]{1,0:T(8,128)(2,1)S(1)}, u32[]{:S(2)}, u32[]{:S(2)}) %collective-permute-start.19) | collective-permute-done | bytes 65568 | tf_op jit(solution)/shard_map/ppermute | solution.py:598
  75.9 1.1 %scatter.1 = bf16[128,1024]{1,0:T(8,128)(2,1)} custom-call(bf16[32,128]{1,0:T(8,128)(2,1)S(1)} %get-tuple-element.28.pick_ref, bf16[32,1024]{1,0:T(8,128)(2,1)S(1)} %get-tuple-element.47.zero_ref, bf16[32,1024]{1,0:T(8,128)(2,1)S(1)} %collective-permute-done.17.one_ref, bf16[32,1024]{1,0:T(8,128)(2,1)S(1)} %collective-permute-done.18.two_ref, ...), custom_call_target="tpu_custom_call" | custom-call | tf_op jit(solution)/shard_map/scatter/pallas_call | solution.py:175
  (14 shorter events, 0.1 us)
Async XLA Ops:
  2.4 8.3 %collective-permute-start.1 = (bf16[32,1024]{1,0:T(8,128)(2,1)S(1)}, bf16[32,1024]{1,0:T(8,128)(2,1)S(1)}, u32[]{:S(2)}, u32[]{:S(2)}) collective-permute-start(bf16[32,1024]{1,0:T(8,128)(2,1)S(1)} %get-tuple-element.30), channel_id=1, source_target_pairs={{0,2},{1,6},{2,10},{3,14},{4,3},{5,7},{6,11},{7,15},{8,0},{9,4},{1... | collective-permute-start | bytes 196616 | tf_op jit(solution)/shard_map/ppermute | solution.py:496
  5.4 5.3 %collective-permute-start = (bf16[32,1024]{1,0:T(8,128)(2,1)S(1)}, bf16[32,1024]{1,0:T(8,128)(2,1)S(1)}, u32[]{:S(2)}, u32[]{:S(2)}) collective-permute-start(bf16[32,1024]{1,0:T(8,128)(2,1)S(1)} %get-tuple-element.30), channel_id=1, source_target_pairs={{0,0},{1,4},{2,8},{3,12},{4,1},{5,5},{6,9},{7,13},{8,2},{9,6},{10,... | collective-permute-start | bytes 196616 | tf_op jit(solution)/shard_map/ppermute | solution.py:495
  10.7 2.7 %collective-permute-start.2 = (bf16[64,1024]{1,0:T(8,128)(2,1)S(1)}, bf16[64,1024]{1,0:T(8,128)(2,1)S(1)}, u32[]{:S(2)}, u32[]{:S(2)}) collective-permute-start(bf16[64,1024]{1,0:T(8,128)(2,1)S(1)} %join.1.joined_ref), channel_id=1, source_target_pairs={{0,1},{1,0},{2,3},{3,2},{4,5},{5,4},{6,7},{7,6},{8,9},{9,8},{10,11... | collective-permute-start | bytes 393224 | tf_op jit(solution)/shard_map/ppermute | solution.py:513
  14.5 10.6 %collective-permute-start.5 = (bf16[32,1024]{1,0:T(8,128)(2,1)S(1)}, bf16[32,1024]{1,0:T(8,128)(2,1)S(1)}, u32[]{:S(2)}, u32[]{:S(2)}) collective-permute-start(bf16[32,1024]{1,0:T(8,128)(2,1)S(1)} %get-tuple-element.51), channel_id=1, source_target_pairs={{0,12},{4,8},{8,4},{12,0},{1,13},{5,9},{9,5},{13,1},{2,14},{6,10},... | collective-permute-start | bytes 196616 | tf_op jit(solution)/shard_map/ppermute | solution.py:522
  20.3 5.3 %collective-permute-start.4 = (bf16[32,1024]{1,0:T(8,128)(2,1)S(1)}, bf16[32,1024]{1,0:T(8,128)(2,1)S(1)}, u32[]{:S(2)}, u32[]{:S(2)}) collective-permute-start(bf16[32,1024]{1,0:T(8,128)(2,1)S(1)} %get-tuple-element.52), channel_id=1, source_target_pairs={{0,8},{4,12},{8,0},{12,4},{1,9},{5,13},{9,1},{13,5},{2,10},{6,14},... | collective-permute-start | bytes 196616 | tf_op jit(solution)/shard_map/ppermute | solution.py:522
  20.3 5.7 %collective-permute-start.3 = (bf16[32,1024]{1,0:T(8,128)(2,1)S(1)}, bf16[32,1024]{1,0:T(8,128)(2,1)S(1)}, u32[]{:S(2)}, u32[]{:S(2)}) collective-permute-start(bf16[32,1024]{1,0:T(8,128)(2,1)S(1)} %get-tuple-element.53), channel_id=1, source_target_pairs={{0,4},{4,0},{8,12},{12,8},{1,5},{5,1},{9,13},{13,9},{2,6},{6,2},{1... | collective-permute-start | bytes 196616 | tf_op jit(solution)/shard_map/ppermute | solution.py:522
  21.0 5.0 %copy-start = (bf16[1024,4]{0,1:T(4,128)(2,1)S(1)}, bf16[1024,4]{0,1:T(4,128)(2,1)}, u32[]{:S(2)}) copy-start(bf16[1024,4]{0,1:T(4,128)(2,1)} %param.14) | copy-start | bytes 24580
  21.0 5.0 %copy-start.1 = (bf16[2,1024]{1,0:T(2,128)(2,1)S(1)}, bf16[2,1024]{1,0:T(2,128)(2,1)}, u32[]{:S(2)}) copy-start(bf16[2,1024]{1,0:T(2,128)(2,1)} %gain_ref.1) | copy-start | bytes 12292
  26.8 8.4 %collective-permute-start.8 = (bf16[32,1152]{1,0:T(8,128)(2,1)S(1)}, bf16[32,1152]{1,0:T(8,128)(2,1)S(1)}, u32[]{:S(2)}, u32[]{:S(2)}) collective-permute-start(bf16[32,1152]{1,0:T(8,128)(2,1)S(1)} %norm.1.after_ref.zero_ref), channel_id=1, source_target_pairs={{0,12},{4,8},{8,4},{12,0},{1,13},{5,9},{9,5},{13,1},{2,14},{6,10},... | collective-permute-start | bytes 221192 | tf_op jit(solution)/shard_map/ppermute | solution.py:538
  29.6 6.1 %collective-permute-start.7 = (bf16[32,1152]{1,0:T(8,128)(2,1)S(1)}, bf16[32,1152]{1,0:T(8,128)(2,1)S(1)}, u32[]{:S(2)}, u32[]{:S(2)}) collective-permute-start(bf16[32,1152]{1,0:T(8,128)(2,1)S(1)} %norm.1.after_ref.zero_ref), channel_id=1, source_target_pairs={{0,8},{4,12},{8,0},{12,4},{1,9},{5,13},{9,1},{13,5},{2,10},{6,14},... | collective-permute-start | bytes 221192 | tf_op jit(solution)/shard_map/ppermute | solution.py:538
  29.6 6.1 %collective-permute-start.6 = (bf16[32,1152]{1,0:T(8,128)(2,1)S(1)}, bf16[32,1152]{1,0:T(8,128)(2,1)S(1)}, u32[]{:S(2)}, u32[]{:S(2)}) collective-permute-start(bf16[32,1152]{1,0:T(8,128)(2,1)S(1)} %norm.1.after_ref.zero_ref), channel_id=1, source_target_pairs={{0,4},{4,0},{8,12},{12,8},{1,5},{5,1},{9,13},{13,9},{2,6},{6,2},{1... | collective-permute-start | bytes 221192 | tf_op jit(solution)/shard_map/ppermute | solution.py:538
  36.5 7.5 %collective-permute-start.9 = (bf16[48,1152]{1,0:T(8,128)(2,1)S(1)}, bf16[48,1152]{1,0:T(8,128)(2,1)S(1)}, u32[]{:S(2)}, u32[]{:S(2)}) collective-permute-start(bf16[48,1152]{1,0:T(8,128)(2,1)S(1)} %get-tuple-element.35), channel_id=1, source_target_pairs={{0,16},{16,0},{1,17},{17,1},{2,18},{18,2},{3,19},{19,3},{4,20},{20... | collective-permute-start | bytes 331784 | tf_op jit(solution)/shard_map/ppermute | solution.py:550
  38.1 5.9 %collective-permute-start.10 = (bf16[48,1152]{1,0:T(8,128)(2,1)S(1)}, bf16[48,1152]{1,0:T(8,128)(2,1)S(1)}, u32[]{:S(2)}, u32[]{:S(2)}) collective-permute-start(bf16[48,1152]{1,0:T(8,128)(2,1)S(1)} %get-tuple-element.36), channel_id=1, source_target_pairs={{0,2},{2,0},{1,3},{3,1},{4,6},{6,4},{5,7},{7,5},{8,10},{10,8},{9,1... | collective-permute-start | bytes 331784 | tf_op jit(solution)/shard_map/ppermute | solution.py:551
  39.9 5.6 %collective-permute-start.11 = (bf16[48,1152]{1,0:T(8,128)(2,1)S(1)}, bf16[48,1152]{1,0:T(8,128)(2,1)S(1)}, u32[]{:S(2)}, u32[]{:S(2)}) collective-permute-start(bf16[48,1152]{1,0:T(8,128)(2,1)S(1)} %get-tuple-element.37), channel_id=1, source_target_pairs={{0,18},{2,16},{16,2},{18,0},{1,19},{3,17},{17,3},{19,1},{4,22},{6,... | collective-permute-start | bytes 331784 | tf_op jit(solution)/shard_map/ppermute | solution.py:549
  49.2 6.1 %collective-permute-start.12 = (bf16[2768,128]{1,0:T(8,128)(2,1)S(1)}, bf16[2768,128]{1,0:T(8,128)(2,1)S(1)}, u32[]{:S(2)}, u32[]{:S(2)}) collective-permute-start(bf16[2768,128]{1,0:T(8,128)(2,1)S(1)} %get-tuple-element.39.gate_ref), channel_id=1, source_target_pairs={{0,1},{1,0},{2,3},{3,2},{4,5},{5,4},{6,7},{7,6},{8,9},{9,8},{10,11... | collective-permute-start | bytes 2125832 | tf_op jit(solution)/shard_map/ppermute | solution.py:568
  52.4 3.4 %collective-permute-start.13 = (bf16[2752,128]{1,0:T(8,128)(2,1)S(1)}, bf16[2752,128]{1,0:T(8,128)(2,1)S(1)}, u32[]{:S(2)}, u32[]{:S(2)}) collective-permute-start(bf16[2752,128]{1,0:T(8,128)(2,1)S(1)} %up.1.after_ref.up_ref), channel_id=1, source_target_pairs={{0,1},{1,0},{2,3},{3,2},{4,5},{5,4},{6,7},{7,6},{8,9},{9,8},{10,11... | collective-permute-start | bytes 2113544 | tf_op jit(solution)/shard_map/ppermute | solution.py:569
  58.7 5.0 %collective-permute-start.14 = (bf16[48,1024]{1,0:T(8,128)(2,1)S(1)}, bf16[48,1024]{1,0:T(8,128)(2,1)S(1)}, u32[]{:S(2)}, u32[]{:S(2)}) collective-permute-start(bf16[48,1024]{1,0:T(8,128)(2,1)S(1)} %get-tuple-element.44), channel_id=1, source_target_pairs={{0,2},{2,0},{1,3},{3,1},{4,6},{6,4},{5,7},{7,5},{8,10},{10,8},{9,1... | collective-permute-start | bytes 294920 | tf_op jit(solution)/shard_map/ppermute | solution.py:590
  59.8 5.7 %collective-permute-start.15 = (bf16[48,1024]{1,0:T(8,128)(2,1)S(1)}, bf16[48,1024]{1,0:T(8,128)(2,1)S(1)}, u32[]{:S(2)}, u32[]{:S(2)}) collective-permute-start(bf16[48,1024]{1,0:T(8,128)(2,1)S(1)} %get-tuple-element.45), channel_id=1, source_target_pairs={{0,16},{16,0},{1,17},{17,1},{2,18},{18,2},{3,19},{19,3},{4,20},{20... | collective-permute-start | bytes 294920 | tf_op jit(solution)/shard_map/ppermute | solution.py:589
  61.3 5.5 %collective-permute-start.16 = (bf16[48,1024]{1,0:T(8,128)(2,1)S(1)}, bf16[48,1024]{1,0:T(8,128)(2,1)S(1)}, u32[]{:S(2)}, u32[]{:S(2)}) collective-permute-start(bf16[48,1024]{1,0:T(8,128)(2,1)S(1)} %get-tuple-element.46), channel_id=1, source_target_pairs={{0,18},{2,16},{16,2},{18,0},{1,19},{3,17},{17,3},{19,1},{4,22},{6,... | collective-permute-start | bytes 294920 | tf_op jit(solution)/shard_map/ppermute | solution.py:588
  67.6 4.5 %collective-permute-start.17 = (bf16[32,1024]{1,0:T(8,128)(2,1)S(1)}, bf16[32,1024]{1,0:T(8,128)(2,1)S(1)}, u32[]{:S(2)}, u32[]{:S(2)}) collective-permute-start(bf16[32,1024]{1,0:T(8,128)(2,1)S(1)} %get-tuple-element.48), channel_id=1, source_target_pairs={{0,4},{4,0},{8,12},{12,8},{1,5},{5,1},{9,13},{13,9},{2,6},{6,2},{1... | collective-permute-start | bytes 196616 | tf_op jit(solution)/shard_map/ppermute | solution.py:598
  67.6 5.9 %collective-permute-start.18 = (bf16[32,1024]{1,0:T(8,128)(2,1)S(1)}, bf16[32,1024]{1,0:T(8,128)(2,1)S(1)}, u32[]{:S(2)}, u32[]{:S(2)}) collective-permute-start(bf16[32,1024]{1,0:T(8,128)(2,1)S(1)} %get-tuple-element.49), channel_id=1, source_target_pairs={{0,8},{4,12},{8,0},{12,4},{1,9},{5,13},{9,1},{13,5},{2,10},{6,14},... | collective-permute-start | bytes 196616 | tf_op jit(solution)/shard_map/ppermute | solution.py:598
  69.8 6.1 %collective-permute-start.19 = (bf16[32,1024]{1,0:T(8,128)(2,1)S(1)}, bf16[32,1024]{1,0:T(8,128)(2,1)S(1)}, u32[]{:S(2)}, u32[]{:S(2)}) collective-permute-start(bf16[32,1024]{1,0:T(8,128)(2,1)S(1)} %get-tuple-element.50), channel_id=1, source_target_pairs={{0,12},{4,8},{8,4},{12,0},{1,13},{5,9},{9,5},{13,1},{2,14},{6,10},... | collective-permute-start | bytes 196616 | tf_op jit(solution)/shard_map/ppermute | solution.py:598

commit v7 on v6

--- a/solution.py
+++ b/solution.py
@@ -160,11 +160,10 @@
 SWAP = [(0, 1), (1, 0)]
 STRIP = 688
 TILE = 16
+SCALARS = pl.BlockSpec(memory_space=pltpu.SMEM)
 ON_CHIP = pl.BlockSpec(memory_space=pltpu.VMEM)
-SCALARS = pl.BlockSpec(memory_space=pltpu.SMEM)
 IN_HBM = pl.BlockSpec(memory_space=pltpu.HBM)
 ANYWHERE = pl.BlockSpec(memory_space=pl.ANY)
-GROUP, FLIP, SIDE = range(3)
 
 
 def crossed(bits, flip):
@@ -188,11 +187,11 @@
     return jax.ShapeDtypeStruct(shape, dtype)
 
 
-def keep_kernel(spans, ids_ref, after_ref, *refs):
+def keep_kernel(spans, after_ref, *refs):
     count = len(spans)
     weights, held, semaphores = refs[:count], refs[count : 2 * count], refs[-1]
     copies = [
-        pltpu.make_async_copy(weight.at[ids_ref[GROUP], a:b, c:d], to, semaphores.at[n])
+        pltpu.make_async_copy(weight.at[lax.axis_index("groups"), a:b, c:d], to, semaphores.at[n])
         for n, (weight, to, (a, b, c, d)) in enumerate(zip(weights, held, spans))
     ]
     for copy in copies:
@@ -205,32 +204,35 @@
     return pltpu.with_memory_space_constraint(value, pltpu.HBM)
 
 
-def keep_on_chip(ids, after, weights, spans, name):
+def keep_on_chip(after, weights, spans, name):
     return call(
         functools.partial(keep_kernel, spans),
         name,
         [pltpu.VMEM((b - a, d - c), jnp.bfloat16) for a, b, c, d in spans],
-        [SCALARS, ANYWHERE] + [IN_HBM] * len(spans),
-        [ids, after] + [in_hbm(weight) for weight in weights],
+        [ANYWHERE] + [IN_HBM] * len(spans),
+        [after] + [in_hbm(weight) for weight in weights],
         scratch=[pltpu.SemaphoreType.DMA((len(spans),))],
         moved=sum(2 * (b - a) * (d - c) for a, b, c, d in spans),
         limit=1 << 20,
     )
 
 
-def select_kernel(ids_ref, kind_ref, rows_hbm, context_hbm, picked_ref, pick_ref, rows_ref, context_ref, semaphores):
+def select_kernel(
+    kind_ref, rows_hbm, context_hbm, picked_ref, pick_ref, kind_out, rows_ref, context_ref, semaphores
+):
     rows_copy = pltpu.make_async_copy(rows_hbm, rows_ref, semaphores.at[0])
     context_copy = pltpu.make_async_copy(context_hbm, context_ref, semaphores.at[1])
     rows_copy.start()
     context_copy.start()
     rows_copy.wait()
+    kind_out[...] = jnp.full(kind_out.shape, kind_ref[0], jnp.int32).astype(jnp.float32)
     capacity = rows_ref.shape[1]
     slots, tokens = pick_ref.shape
     row = lax.broadcasted_iota(jnp.int32, (slots, tokens), 0)
     token = lax.broadcasted_iota(jnp.int32, (slots, tokens), 1)
     wanted = jnp.full((slots, tokens), -1, jnp.int32)
     for e in range(2):
-        expert = 2 * kind_ref[0] + (ids_ref[GROUP] ^ e)
+        expert = 2 * kind_ref[0] + (lax.axis_index("groups") ^ e)
         for s in range(capacity):
             wanted = jnp.where(row == e * capacity + s, rows_ref[expert, s], wanted)
     pick = jnp.where(wanted == token, 1.0, 0.0).astype(jnp.bfloat16)
@@ -240,12 +242,12 @@
 
 
 def keep_gate_kernel(
-    ids_ref, pick_ref, residual_hbm, gate_ref, proj_ref, gate_held, proj_held, rest_ref, residual_ref, semaphores
+    pick_ref, residual_hbm, gate_ref, proj_ref, gate_held, proj_held, rest_ref, residual_ref, semaphores
 ):
     copies = [
         pltpu.make_async_copy(residual_hbm, residual_ref, semaphores.at[0]),
         pltpu.make_async_copy(proj_ref, proj_held, semaphores.at[1]),
-        pltpu.make_async_copy(gate_ref.at[ids_ref[GROUP], : gate_held.shape[0]], gate_held, semaphores.at[2]),
+        pltpu.make_async_copy(gate_ref.at[lax.axis_index("groups"), : gate_held.shape[0]], gate_held, semaphores.at[2]),
     ]
     for copy in copies:
         copy.start()
@@ -261,15 +263,17 @@
     out_ref[slots:, :] = across_ref[...]
 
 
-def project_kernel(ids_ref, joined_ref, other_ref, weight_ref, out_ref, rows_ref):
+def project_kernel(joined_ref, other_ref, weight_ref, out_ref, rows_ref):
     pair = joined_ref.shape[0]
     slots = pair // 2
     rows_ref[:pair, :] = joined_ref[...]
     rows_ref[pair:, :] = other_ref[...]
     product = jnp.dot(rows_ref[...], weight_ref[...], preferred_element_type=jnp.float32)
     product = product.astype(jnp.bfloat16)
+    corner = 2 * lax.axis_index("mod") + lax.axis_index("fsdp")
+    flip = lax.axis_index("tok") ^ corner
     for n, u in enumerate((0, 2, 1, 3)):
-        out_ref[ids_ref[FLIP] ^ u] = product[n * slots : (n + 1) * slots, :]
+        out_ref[flip ^ u] = product[n * slots : (n + 1) * slots, :]
 
 
 def split_high_low(value):
@@ -277,39 +281,39 @@
     return high, value - high
 
 
-def norm_kernel(ids_ref, kind_ref, rest_ref, partial_ref, one_ref, two_ref, three_ref, gain_ref, router_ref, _, out_ref):
+def norm_kernel(kind_ref, rest_ref, partial_ref, one_ref, two_ref, three_ref, gain_ref, router_ref, _, out_ref):
     slots, columns = rest_ref.shape
     hidden = rest_ref[...] + partial_ref[0].astype(jnp.float32)
     for got_ref in (three_ref, two_ref, one_ref):
         hidden = hidden + got_ref[...].astype(jnp.float32)
+    kind = kind_ref[0:1, 0:1]
     gains = gain_ref[...].astype(jnp.float32)
-    gained = hidden * jnp.where(kind_ref[0] == 0, gains[0:1], gains[1:2])
+    gained = hidden * jnp.where(kind == 0.0, gains[0:1], gains[1:2])
     out_ref[:, :columns] = gained.astype(jnp.bfloat16)
     table = router_ref[...].astype(jnp.float32)
     pieces = []
     for e in range(2):
-        expert = 2 * kind_ref[0] + (ids_ref[GROUP] ^ e)
-        weights = table[0:1]
-        for k in range(1, table.shape[0]):
-            weights = jnp.where(expert == k, table[k : k + 1], weights)
+        second = (lax.axis_index("groups") ^ e) == 1
+        text = jnp.where(second, table[1:2], table[0:1])
+        image = jnp.where(second, table[3:4], table[2:3])
+        weights = jnp.where(kind == 0.0, text, image)
         half = slots // 2
         pieces.append(jnp.sum(gained[e * half : (e + 1) * half] * weights, axis=1, keepdims=True))
     logits = jnp.concatenate(pieces, axis=0)
     squares = jnp.sum(hidden * hidden, axis=1, keepdims=True)
     lane = lax.broadcasted_iota(jnp.int32, (slots, STAT_COLS), 1)
-    extra = jnp.where(lane == 4, kind_ref[0].astype(jnp.float32), 0.0)
+    extra = jnp.where(lane == 4, kind, 0.0)
     for at, stat in enumerate(split_high_low(squares) + split_high_low(logits)):
         extra = jnp.where(lane == at, stat, extra)
     out_ref[:, columns:] = extra.astype(jnp.bfloat16)
 
 
-def places(ids_ref, packed_refs, columns):
-    side = ids_ref[SIDE]
+def places(packed_refs, columns):
+    side = lax.axis_index("mod")
     matches, found, before = [], [], 0
     for v, ref in enumerate(packed_refs):
-        tail = ref[:, columns:].astype(jnp.float32)
-        lane = lax.broadcasted_iota(jnp.int32, tail.shape, 1)
-        kind = jnp.where(jnp.max(jnp.where(lane == 4, tail, 0.0)) > 0.5, 1, 0)
+        flag = ref[:TILE, columns:].astype(jnp.float32)[0, 4]
+        kind = jnp.where(flag > 0.5, 1, 0)
         match = kind == side
         place = jnp.minimum(jnp.where(match, before, v - before), len(packed_refs) - 2)
         matches.append(match)
@@ -318,12 +322,12 @@
     return matches, found
 
 
-def arrange_kernel(ids_ref, zero_ref, one_ref, two_ref, three_ref, _, *out_refs):
+def arrange_kernel(zero_ref, one_ref, two_ref, three_ref, _, *out_refs):
     packed_refs = (zero_ref, one_ref, two_ref, three_ref)
     capacity = zero_ref.shape[0] // 2
     for out_ref in out_refs:
         out_ref[...] = jnp.zeros(out_ref.shape, out_ref.dtype)
-    matches, found = places(ids_ref, packed_refs, zero_ref.shape[1] - STAT_COLS)
+    matches, found = places(packed_refs, zero_ref.shape[1] - STAT_COLS)
     for ref, match, place in zip(packed_refs, matches, found):
         span = pl.ds(pl.multiple_of(place * capacity, capacity), capacity)
         for wanted, (own_ref, given_ref) in ((True, out_refs[:2]), (False, out_refs[2:])):
@@ -345,7 +349,7 @@
             at += stop - start
 
 
-def gate_kernel(ids_ref, own_ref, far_ref, side_own_ref, side_far_ref, *refs):
+def gate_kernel(own_ref, far_ref, side_own_ref, side_far_ref, *refs):
     weight_refs, out_ref, rows_ref = refs[:2], refs[-2], refs[-1]
     half = own_ref.shape[0]
     rows = rows_ref.shape[0]
@@ -354,7 +358,7 @@
     rows_ref[2 * half :, :] = jnp.zeros((rows - 2 * half, 2 * columns), rows_ref.dtype)
     for side in range(2):
 
-        @pl.when(ids_ref[SIDE] == side)
+        @pl.when(lax.axis_index("mod") == side)
         def _():
             here, there = side * columns, (1 - side) * columns
             rows_ref[:half, here : here + columns] = own_ref[:, :columns]
@@ -396,7 +400,7 @@
 
 
 def down_kernel(
-    ids_ref, silu_ref, stat_ref, up_ref, up_other_ref, first_ref, second_ref,
+    silu_ref, stat_ref, up_ref, up_other_ref, first_ref, second_ref,
     kept_ref, far_ref, side_ref, side_far_ref, act_ref,
 ):
     units, rows = act_ref.shape
@@ -406,29 +410,28 @@
         act_ref[start:stop, :] = (silu_ref[start:stop, :] * up).astype(jnp.bfloat16)
     half, columns = kept_ref.shape
     score = jnp.broadcast_to(stat_ref[1:2, :], (rows, rows)).T[:, 0:1]
-    width_first = first_ref.shape[1]
-    for start, weight_ref, a, b in (
-        (0, first_ref, 0, columns),
-        (columns, first_ref, columns, width_first),
-        (width_first, second_ref, 0, 2 * columns - width_first),
-    ):
-        value = lax.dot_general(
-            act_ref[...], weight_ref[:, a:b], (((0,), (0,)), ((), ())), preferred_element_type=jnp.float32
+    first_units = first_ref.shape[0]
+    for quarter in range(2):
+        span = slice(quarter * columns, (quarter + 1) * columns)
+        value = sum(
+            lax.dot_general(
+                act_ref[a:b, :], weight_ref[:, span], (((0,), (0,)), ((), ())), preferred_element_type=jnp.float32
+            )
+            for a, b, weight_ref in ((0, first_units, first_ref), (first_units, units, second_ref))
         )
         value = (value * score).astype(jnp.bfloat16)
-        quarter, at = divmod(start, columns)
         for across, (own_out, far_out) in enumerate(((kept_ref, far_ref), (side_ref, side_far_ref))):
 
-            @pl.when((ids_ref[SIDE] ^ quarter) == across)
+            @pl.when((lax.axis_index("mod") ^ quarter) == across)
             def _():
-                own_out[:, at : at + b - a] = value[:half]
-                far_out[:, at : at + b - a] = value[half : 2 * half]
-
-
-def merge_kernel(ids_ref, zero_ref, one_ref, two_ref, three_ref, kept_ref, side_ref, far_ref, side_far_ref, *out_refs):
+                own_out[...] = value[:half]
+                far_out[...] = value[half : 2 * half]
+
+
+def merge_kernel(zero_ref, one_ref, two_ref, three_ref, kept_ref, side_ref, far_ref, side_far_ref, *out_refs):
     columns = kept_ref.shape[1]
     capacity = zero_ref.shape[0] // 2
-    matches, found = places(ids_ref, (zero_ref, one_ref, two_ref, three_ref), columns)
+    matches, found = places((zero_ref, one_ref, two_ref, three_ref), columns)
     for out_ref, match, place in zip(out_refs, matches, found):
         span = pl.ds(pl.multiple_of(place * capacity, capacity), capacity)
         for wanted, (first_ref, second_ref) in ((True, (kept_ref, far_ref)), (False, (side_ref, side_far_ref))):
@@ -473,16 +476,12 @@
     rows = 2 * half
     units, width = down_weight.shape[1:]
     assert block_modality.shape == (1,) and experts == 4 and gate_weight.shape[0] == 2
-    tok, side = lax.axis_index("tok"), lax.axis_index("mod")
-    corner = 2 * side + lax.axis_index("fsdp")
-    ids = jnp.stack([lax.axis_index("groups"), tok ^ corner, side])
-
-    picked, pick = call(
+    picked, pick, kind = call(
         select_kernel,
         "select",
-        [array(slots, columns), array(slots, tokens)],
-        [SCALARS] * 2 + [IN_HBM] * 2,
-        [ids, block_modality, in_hbm(expert_rows), in_hbm(context)],
+        [array(slots, columns), array(slots, tokens), array(8, STAT_COLS, dtype=jnp.float32)],
+        [SCALARS, IN_HBM, IN_HBM],
+        [block_modality, in_hbm(expert_rows), in_hbm(context)],
         scratch=[
             pltpu.SMEM((experts, capacity), jnp.int32),
             pltpu.VMEM((tokens, columns), jnp.bfloat16),
@@ -503,8 +502,8 @@
             pltpu.VMEM(out_proj.shape, jnp.bfloat16),
             array(slots, columns, dtype=jnp.float32),
         ],
-        [SCALARS, ON_CHIP, IN_HBM, IN_HBM, IN_HBM],
-        [ids, pick, in_hbm(residual), in_hbm(gate_weight.swapaxes(1, 2)), in_hbm(out_proj)],
+        [ON_CHIP, IN_HBM, IN_HBM, IN_HBM],
+        [pick, in_hbm(residual), in_hbm(gate_weight.swapaxes(1, 2)), in_hbm(out_proj)],
         scratch=[pltpu.VMEM((tokens, columns), jnp.bfloat16), pltpu.SemaphoreType.DMA((3,))],
         moved=units * width,
         limit=2 << 20,
@@ -515,13 +514,12 @@
         project_kernel,
         "project",
         array(4, slots, columns),
-        [SCALARS] + [ON_CHIP] * 3,
-        [ids, joined, other, proj_held],
+        [ON_CHIP] * 3,
+        [joined, other, proj_held],
         scratch=[pltpu.VMEM((rows, columns), jnp.bfloat16)],
     )
     sums = [lax.ppermute(partial[v], "tok", crossed(2, v)) for v in (1, 2, 3)]
     gate_second, up_first = keep_on_chip(
-        ids,
         partial,
         [gate_weight.swapaxes(1, 2), up_weight.swapaxes(1, 2)],
         [(units_first, units, 0, width), (0, units // 4, 0, width)],
@@ -532,34 +530,34 @@
         norm_kernel,
         "norm",
         array(slots, packed_columns),
-        [SCALARS, SCALARS] + [ON_CHIP] * 8,
-        [ids, block_modality, rest, partial, *sums, norm_gain, router_weight.T, up_first],
+        [ON_CHIP] * 9,
+        [kind, rest, partial, *sums, norm_gain, router_weight.T, up_first],
     )
     others = [lax.ppermute(packed, "tok", crossed(2, v)) for v in (1, 2, 3)]
-    (up_second,) = keep_on_chip(ids, packed, [up_weight.swapaxes(1, 2)], [(units // 4, units, 0, width)], "keep_up")
+    (up_second,) = keep_on_chip(packed, [up_weight.swapaxes(1, 2)], [(units // 4, units, 0, width)], "keep_up")
     kept_slots = 3 * capacity
     own, to_far_rows, to_side_rows, to_corner_rows = call(
         arrange_kernel,
         "arrange",
         [array(kept_slots, packed_columns)] * 4,
-        [SCALARS] + [ON_CHIP] * 5,
-        [ids, packed, *others, up_second],
+        [ON_CHIP] * 5,
+        [packed, *others, up_second],
     )
     both_axes = ("groups", "mod")
     side_far = lax.ppermute(to_corner_rows, both_axes, crossed(2, 3))
     far = lax.ppermute(to_far_rows, "groups", SWAP)
     side_own = lax.ppermute(to_side_rows, "mod", SWAP)
 
-    width_first = width // 4 * 3
-    (down_first,) = keep_on_chip(ids, own, [down_weight], [(0, units, 0, width_first)], "keep_down")
+    down_units = units // 4 * 3
+    (down_first,) = keep_on_chip(own, [down_weight], [(0, down_units, 0, width)], "keep_down")
 
     flops = 2 * rows * units * width
     gate, gathered = call(
         gate_kernel,
         "gate",
         [array(units + TILE, rows), array(rows, width)],
-        [SCALARS] + [ON_CHIP] * 7,
-        [ids, own, far, side_own, side_far, gate_first, gate_second, down_first],
+        [ON_CHIP] * 7,
+        [own, far, side_own, side_far, gate_first, gate_second, down_first],
         flops=flops,
     )
     up = call(
@@ -567,7 +565,7 @@
     )
     gate_other = lax.ppermute(gate, "fsdp", SWAP)
     up_other = lax.ppermute(up, "fsdp", SWAP)
-    (down_second,) = keep_on_chip(ids, up, [down_weight], [(0, units, width_first, width)], "keep_last")
+    (down_second,) = keep_on_chip(up, [down_weight], [(down_units, units, 0, width)], "keep_last")
     silu, stat = call(
         silu_kernel,
         "silu",
@@ -580,8 +578,8 @@
         down_kernel,
         "down",
         [array(kept_slots, columns)] * 4,
-        [SCALARS] + [ON_CHIP] * 6,
-        [ids, silu, stat, up, up_other, down_first, down_second],
+        [ON_CHIP] * 6,
+        [silu, stat, up, up_other, down_first, down_second],
         scratch=[pltpu.VMEM((units, rows), jnp.bfloat16)],
         flops=flops,
     )
@@ -592,8 +590,8 @@
         merge_kernel,
         "merge",
         [array(slots, columns)] * 4,
-        [SCALARS] + [ON_CHIP] * 8,
-        [ids, packed, *others, kept, from_side, from_far, from_side_far],
+        [ON_CHIP] * 8,
+        [packed, *others, kept, from_side, from_far, from_side_far],
     )
     values = [merged[0]] + [lax.ppermute(merged[v], "tok", crossed(2, v)) for v in (1, 2, 3)]
     return call(

time: 77.3 us -> 72.5 us (0.938)
  Pallas kernels: 34.3 us -> 27.7 us
  waiting for transfers between devices: 13.3 us -> 15.3 us
    pallas_call x16, Pallas kernels: 34.3 us -> 27.7 us  [call(): pl.pallas_call(kernel, out_shape=outs, in_specs=specs, out_specs=jax.tree...]
  transfers between devices with their start and end apart: 20 -> 20, of which waited for: 11 -> 12; matrix products, arithmetic and copies ran while one was open for 0% -> 0% of each run, Pallas kernels for 28% -> 26%
where the time goes in v7:
time: 72.5 us; the launch traced here: 72.2 us
  starting transfers between devices  28.4 us (39%)
  Pallas kernels  27.7 us (38%)
  waiting for transfers between devices  15.3 us (21%)
  between operations  0.83 us (1%)
    pallas_call x16, Pallas kernels, call(): pl.pallas_call(kernel, out_shape=outs, in_specs=specs, out_specs=jax.tree...  27.7 us
    ppermute x3, starting transfers between devices, paired_local(): sums = [lax.ppermute(partial[v], 'tok', crossed(2, v)) for v in (1, 2, 3)]  6.25 us
    ppermute x3, starting transfers between devices, paired_local(): lax.ppermute(merged[v], 'tok', crossed(2, v))  4.44 us
    ppermute x3, starting transfers between devices, paired_local(): others = [lax.ppermute(packed, 'tok', crossed(2, v)) for v in (1, 2, 3)]  4.42 us
    ppermute x3, waiting for transfers between devices, paired_local(): lax.ppermute(merged[v], 'tok', crossed(2, v))  3.61 us
    ppermute x1, starting transfers between devices, paired_local(): across = lax.ppermute(picked, plane, to_second)  2.99 us
    ppermute x1, starting transfers between devices, paired_local(): side_own = lax.ppermute(to_side_rows, 'mod', SWAP)  2.43 us
    ppermute x1, waiting for transfers between devices, paired_local(): side_far = lax.ppermute(to_corner_rows, both_axes, crossed(2, 3))  1.82 us
  transfers between devices with their start and end apart: 20, of which 12 were waited for; matrix products, arithmetic and copies ran while one was open for 0% of the time, Pallas kernels for 26%

profile of v7, /device:TPU:0, one launch (start us, length us, event | category | flops | bytes accessed | tf_op | source)
XLA Modules:
  0.0 72.2 jit_solution(18442201048690783084)
XLA Ops:
  0.7 1.1 %select.1 = (bf16[32,1024]{1,0:T(8,128)(2,1)S(1)}, bf16[32,128]{1,0:T(8,128)(2,1)S(1)}, f32[8,128]{1,0:T(8,128)S(1)}) custom-call(s32[1]{0:T(128)S(6)} %copy.11.kind_ref, s32[4,16]{1,0:T(4,128)} %rows_hbm.1, bf16[128,1024]{1,0:T(8,128)(2,1)} %context_hbm.1), custom_call_target="tpu_custom_call" | custom-call | tf_op jit(solution)/shard_map/select/pallas_call | solution.py:174
  1.8 3.0 %collective-permute-start.1 = (bf16[32,1024]{1,0:T(8,128)(2,1)S(1)}, bf16[32,1024]{1,0:T(8,128)(2,1)S(1)}, u32[]{:S(2)}, u32[]{:S(2)}) collective-permute-start(bf16[32,1024]{1,0:T(8,128)(2,1)S(1)} %get-tuple-element.32), channel_id=1, source_target_pairs={{0,2},{1,6},{2,10},{3,14},{4,3},{5,7},{6,11},{7,15},{8,0},{9,4},{1... | collective-permute-start | bytes 196616 | tf_op jit(solution)/shard_map/ppermute | solution.py:495
  4.8 0.7 collective-permute-start
  5.4 3.4 %keep_gate.1 = (bf16[1376,2048]{1,0:T(8,128)(2,1)S(1)}, bf16[1024,1024]{1,0:T(8,128)(2,1)S(1)}, f32[32,1024]{1,0:T(8,128)S(1)}) custom-call(bf16[32,128]{1,0:T(8,128)(2,1)S(1)} %get-tuple-element.29.pick_ref, bf16[128,1024]{1,0:T(8,128)(2,1)} %residual_hbm.1, bf16[2,2752,2048]{2,1,0:T(8,128)(2,1)} %bitcast.10, bf16[1024,1024]{1,0:T(8,128)(2,1)} %proj_ref.1), custom_call_target="tpu_custom_call" | custom-call | bytes 5636096 | tf_op jit(solution)/shard_map/keep_gate/pallas_call | solution.py:174
  8.8 1.3 %collective-permute-done.1.across_ref = bf16[32,1024]{1,0:T(8,128)(2,1)S(1)} collective-permute-done((bf16[32,1024]{1,0:T(8,128)(2,1)S(1)}, bf16[32,1024]{1,0:T(8,128)(2,1)S(1)}, u32[]{:S(2)}, u32[]{:S(2)}) %collective-permute-start.1) | collective-permute-done | bytes 65568 | tf_op jit(solution)/shard_map/ppermute | solution.py:495
  10.1 0.0 collective-permute-done.near_ref
  10.1 1.4 %collective-permute-start.2 = (bf16[64,1024]{1,0:T(8,128)(2,1)S(1)}, bf16[64,1024]{1,0:T(8,128)(2,1)S(1)}, u32[]{:S(2)}, u32[]{:S(2)}) collective-permute-start(bf16[64,1024]{1,0:T(8,128)(2,1)S(1)} %join.1.joined_ref), channel_id=1, source_target_pairs={{0,1},{1,0},{2,3},{3,2},{4,5},{5,4},{6,7},{7,6},{8,9},{9,8},{10,11... | collective-permute-start | bytes 393224 | tf_op jit(solution)/shard_map/ppermute | solution.py:512
  11.6 1.0 %collective-permute-done.2.other_ref = bf16[64,1024]{1,0:T(8,128)(2,1)S(1)} collective-permute-done((bf16[64,1024]{1,0:T(8,128)(2,1)S(1)}, bf16[64,1024]{1,0:T(8,128)(2,1)S(1)}, u32[]{:S(2)}, u32[]{:S(2)}) %collective-permute-start.2) | collective-permute-done | bytes 131104 | tf_op jit(solution)/shard_map/ppermute | solution.py:512
  12.6 0.5 project.1.after_ref.partial_ref
  13.1 5.6 %collective-permute-start.5 = (bf16[32,1024]{1,0:T(8,128)(2,1)S(1)}, bf16[32,1024]{1,0:T(8,128)(2,1)S(1)}, u32[]{:S(2)}, u32[]{:S(2)}) collective-permute-start(bf16[32,1024]{1,0:T(8,128)(2,1)S(1)} %get-tuple-element.53), channel_id=1, source_target_pairs={{0,12},{4,8},{8,4},{12,0},{1,13},{5,9},{9,5},{13,1},{2,14},{6,10},... | collective-permute-start | bytes 196616 | tf_op jit(solution)/shard_map/ppermute | solution.py:521
  18.7 0.6 collective-permute-start.3
  19.3 3.5 %keep_more.1 = (bf16[1376,2048]{1,0:T(8,128)(2,1)S(1)}, bf16[688,2048]{1,0:T(8,128)(2,1)S(1)}) custom-call(bf16[4,32,1024]{2,1,0:T(8,128)(2,1)S(1)} %project.1.after_ref.partial_ref, bf16[2,2752,2048]{2,1,0:T(8,128)(2,1)} %bitcast.11, bf16[2,2752,2048]{2,1,0:T(8,128)(2,1)} %bitcast.12), custom_call_target="tpu_custom_call" | custom-call | bytes 8454144 | tf_op jit(solution)/shard_map/keep_more/pallas_call | solution.py:174
  22.8 0.0 collective-permute-done.5.three_ref
  22.8 1.2 %collective-permute-done.4.two_ref = bf16[32,1024]{1,0:T(8,128)(2,1)S(1)} collective-permute-done((bf16[32,1024]{1,0:T(8,128)(2,1)S(1)}, bf16[32,1024]{1,0:T(8,128)(2,1)S(1)}, u32[]{:S(2)}, u32[]{:S(2)}) %collective-permute-start.4) | collective-permute-done | bytes 65568 | tf_op jit(solution)/shard_map/ppermute | solution.py:521
  24.0 0.3 collective-permute-done.3.one_ref
  24.3 0.2 norm.1.after_ref.zero_ref
  24.6 2.4 %collective-permute-start.8 = (bf16[32,1152]{1,0:T(8,128)(2,1)S(1)}, bf16[32,1152]{1,0:T(8,128)(2,1)S(1)}, u32[]{:S(2)}, u32[]{:S(2)}) collective-permute-start(bf16[32,1152]{1,0:T(8,128)(2,1)S(1)} %norm.1.after_ref.zero_ref), channel_id=1, source_target_pairs={{0,12},{4,8},{8,4},{12,0},{1,13},{5,9},{9,5},{13,1},{2,14},{6,10},... | collective-permute-start | bytes 221192 | tf_op jit(solution)/shard_map/ppermute | solution.py:536
  27.0 0.4 collective-permute-start.7
  27.4 1.6 %collective-permute-start.6 = (bf16[32,1152]{1,0:T(8,128)(2,1)S(1)}, bf16[32,1152]{1,0:T(8,128)(2,1)S(1)}, u32[]{:S(2)}, u32[]{:S(2)}) collective-permute-start(bf16[32,1152]{1,0:T(8,128)(2,1)S(1)} %norm.1.after_ref.zero_ref), channel_id=1, source_target_pairs={{0,4},{4,0},{8,12},{12,8},{1,5},{5,1},{9,13},{13,9},{2,6},{6,2},{1... | collective-permute-start | bytes 221192 | tf_op jit(solution)/shard_map/ppermute | solution.py:536
  29.0 3.4 %keep_up.1._.refs_1_ = bf16[2064,2048]{1,0:T(8,128)(2,1)S(1)} custom-call(bf16[32,1152]{1,0:T(8,128)(2,1)S(1)} %norm.1.after_ref.zero_ref, bf16[2,2752,2048]{2,1,0:T(8,128)(2,1)} %bitcast.13), custom_call_target="tpu_custom_call" | custom-call | bytes 8454144 | tf_op jit(solution)/shard_map/keep_up/pallas_call | solution.py:174
  32.4 1.1 %collective-permute-done.7.two_ref = bf16[32,1152]{1,0:T(8,128)(2,1)S(1)} collective-permute-done((bf16[32,1152]{1,0:T(8,128)(2,1)S(1)}, bf16[32,1152]{1,0:T(8,128)(2,1)S(1)}, u32[]{:S(2)}, u32[]{:S(2)}) %collective-permute-start.7) | collective-permute-done | bytes 73760 | tf_op jit(solution)/shard_map/ppermute | solution.py:536
  33.5 0.0 collective-permute-done.6.one_ref
  33.5 0.2 arrange.1
  33.7 1.6 %collective-permute-start.9 = (bf16[48,1152]{1,0:T(8,128)(2,1)S(1)}, bf16[48,1152]{1,0:T(8,128)(2,1)S(1)}, u32[]{:S(2)}, u32[]{:S(2)}) collective-permute-start(bf16[48,1152]{1,0:T(8,128)(2,1)S(1)} %get-tuple-element.37), channel_id=1, source_target_pairs={{0,16},{16,0},{1,17},{17,1},{2,18},{18,2},{3,19},{19,3},{4,20},{20... | collective-permute-start | bytes 331784 | tf_op jit(solution)/shard_map/ppermute | solution.py:548
  35.3 2.4 %collective-permute-start.10 = (bf16[48,1152]{1,0:T(8,128)(2,1)S(1)}, bf16[48,1152]{1,0:T(8,128)(2,1)S(1)}, u32[]{:S(2)}, u32[]{:S(2)}) collective-permute-start(bf16[48,1152]{1,0:T(8,128)(2,1)S(1)} %get-tuple-element.38), channel_id=1, source_target_pairs={{0,2},{2,0},{1,3},{3,1},{4,6},{6,4},{5,7},{7,5},{8,10},{10,8},{9,1... | collective-permute-start | bytes 331784 | tf_op jit(solution)/shard_map/ppermute | solution.py:549
  37.7 3.4 %keep_down.1.refs_2_.first_ref = bf16[2064,2048]{1,0:T(8,128)(2,1)S(1)} custom-call(bf16[48,1152]{1,0:T(8,128)(2,1)S(1)} %get-tuple-element.36.after_ref.own_ref, bf16[2,2752,2048]{2,1,0:T(8,128)(2,1)} %refs_0_.3), custom_call_target="tpu_custom_call" | custom-call | bytes 8454144 | tf_op jit(solution)/shard_map/keep_down/pallas_call | solution.py:174
  41.1 0.4 collective-permute-done.10.side_own_ref
  41.5 1.8 %collective-permute-done.11.side_far_ref = bf16[48,1152]{1,0:T(8,128)(2,1)S(1)} collective-permute-done((bf16[48,1152]{1,0:T(8,128)(2,1)S(1)}, bf16[48,1152]{1,0:T(8,128)(2,1)S(1)}, u32[]{:S(2)}, u32[]{:S(2)}) %collective-permute-start.11) | collective-permute-done | bytes 110624 | tf_op jit(solution)/shard_map/ppermute | solution.py:547
  43.4 3.1 %gate.1 = (bf16[2768,128]{1,0:T(8,128)(2,1)S(1)}, bf16[128,2048]{1,0:T(8,128)(2,1)S(1)}) custom-call(bf16[48,1152]{1,0:T(8,128)(2,1)S(1)} %get-tuple-element.36.after_ref.own_ref, bf16[48,1152]{1,0:T(8,128)(2,1)S(1)} %collective-permute-done.9.far_ref, bf16[48,1152]{1,0:T(8,128)(2,1)S(1)} %collective-permute-done.10.side_own_ref, ...), custom_call_target="tpu_custom_call" | custom-call | flops 1442840576 | tf_op jit(solution)/shard_map/gate/pallas_call | solution.py:174
  46.5 0.1 collective-permute-start.12
  46.6 3.1 %up.1.after_ref.up_ref = bf16[2752,128]{1,0:T(8,128)(2,1)S(1)} custom-call(bf16[128,2048]{1,0:T(8,128)(2,1)S(1)} %get-tuple-element.44.rows_ref, bf16[688,2048]{1,0:T(8,128)(2,1)S(1)} %get-tuple-element.35._.refs_0_, bf16[2064,2048]{1,0:T(8,128)(2,1)S(1)} %keep_up.1._.refs_1_), custom_call_target="tpu_custom_call" | custom-call | flops 1442840576 | tf_op jit(solution)/shard_map/up/pallas_call | solution.py:174
  49.6 0.6 collective-permute-start.13
  50.2 1.8 %keep_last.1.second_ref = bf16[688,2048]{1,0:T(8,128)(2,1)S(1)} custom-call(bf16[2752,128]{1,0:T(8,128)(2,1)S(1)} %up.1.after_ref.up_ref, bf16[2,2752,2048]{2,1,0:T(8,128)(2,1)} %refs_0_.3), custom_call_target="tpu_custom_call" | custom-call | bytes 2818048 | tf_op jit(solution)/shard_map/keep_last/pallas_call | solution.py:174
  52.0 0.5 silu.1
  52.5 2.3 %down.1 = (bf16[48,1024]{1,0:T(8,128)(2,1)S(1)}, bf16[48,1024]{1,0:T(8,128)(2,1)S(1)}, bf16[48,1024]{1,0:T(8,128)(2,1)S(1)}, bf16[48,1024]{1,0:T(8,128)(2,1)S(1)}) custom-call(f32[2752,128]{1,0:T(8,128)S(1)} %get-tuple-element.42.silu_ref, f32[8,128]{1,0:T(8,128)S(1)} %get-tuple-element.43.stat_ref, bf16[2752,128]{1,0:T(8,128)(2,1)S(1)} %up.1.after_ref.up_ref, ...), custom_call_target="tpu_custom_call" | custom-call | flops 1442840576 | tf_op jit(solution)/shard_map/down/pallas_call | solution.py:174
  54.8 1.0 %collective-permute-start.14 = (bf16[48,1024]{1,0:T(8,128)(2,1)S(1)}, bf16[48,1024]{1,0:T(8,128)(2,1)S(1)}, u32[]{:S(2)}, u32[]{:S(2)}) collective-permute-start(bf16[48,1024]{1,0:T(8,128)(2,1)S(1)} %get-tuple-element.46), channel_id=1, source_target_pairs={{0,2},{2,0},{1,3},{3,1},{4,6},{6,4},{5,7},{7,5},{8,10},{10,8},{9,1... | collective-permute-start | bytes 294920 | tf_op jit(solution)/shard_map/ppermute | solution.py:588
  55.9 1.5 %collective-permute-start.15 = (bf16[48,1024]{1,0:T(8,128)(2,1)S(1)}, bf16[48,1024]{1,0:T(8,128)(2,1)S(1)}, u32[]{:S(2)}, u32[]{:S(2)}) collective-permute-start(bf16[48,1024]{1,0:T(8,128)(2,1)S(1)} %get-tuple-element.47), channel_id=1, source_target_pairs={{0,16},{16,0},{1,17},{17,1},{2,18},{18,2},{3,19},{19,3},{4,20},{20... | collective-permute-start | bytes 294920 | tf_op jit(solution)/shard_map/ppermute | solution.py:587
  57.4 1.0 %collective-permute-start.16 = (bf16[48,1024]{1,0:T(8,128)(2,1)S(1)}, bf16[48,1024]{1,0:T(8,128)(2,1)S(1)}, u32[]{:S(2)}, u32[]{:S(2)}) collective-permute-start(bf16[48,1024]{1,0:T(8,128)(2,1)S(1)} %get-tuple-element.48), channel_id=1, source_target_pairs={{0,18},{2,16},{16,2},{18,0},{1,19},{3,17},{17,3},{19,1},{4,22},{6,... | collective-permute-start | bytes 294920 | tf_op jit(solution)/shard_map/ppermute | solution.py:586
  58.4 1.5 %collective-permute-done.14.side_ref = bf16[48,1024]{1,0:T(8,128)(2,1)S(1)} collective-permute-done((bf16[48,1024]{1,0:T(8,128)(2,1)S(1)}, bf16[48,1024]{1,0:T(8,128)(2,1)S(1)}, u32[]{:S(2)}, u32[]{:S(2)}) %collective-permute-start.14) | collective-permute-done | bytes 98336 | tf_op jit(solution)/shard_map/ppermute | solution.py:588
  59.8 1.8 %collective-permute-done.15.far_ref = bf16[48,1024]{1,0:T(8,128)(2,1)S(1)} collective-permute-done((bf16[48,1024]{1,0:T(8,128)(2,1)S(1)}, bf16[48,1024]{1,0:T(8,128)(2,1)S(1)}, u32[]{:S(2)}, u32[]{:S(2)}) %collective-permute-start.15) | collective-permute-done | bytes 98336 | tf_op jit(solution)/shard_map/ppermute | solution.py:587
  61.6 1.3 %collective-permute-done.16.side_far_ref = bf16[48,1024]{1,0:T(8,128)(2,1)S(1)} collective-permute-done((bf16[48,1024]{1,0:T(8,128)(2,1)S(1)}, bf16[48,1024]{1,0:T(8,128)(2,1)S(1)}, u32[]{:S(2)}, u32[]{:S(2)}) %collective-permute-start.16) | collective-permute-done | bytes 98336 | tf_op jit(solution)/shard_map/ppermute | solution.py:586
  62.9 0.2 merge.1
  63.1 0.1 collective-permute-start.17
  63.1 1.9 %collective-permute-start.18 = (bf16[32,1024]{1,0:T(8,128)(2,1)S(1)}, bf16[32,1024]{1,0:T(8,128)(2,1)S(1)}, u32[]{:S(2)}, u32[]{:S(2)}) collective-permute-start(bf16[32,1024]{1,0:T(8,128)(2,1)S(1)} %get-tuple-element.51), channel_id=1, source_target_pairs={{0,8},{4,12},{8,0},{12,4},{1,9},{5,13},{9,1},{13,5},{2,10},{6,14},... | collective-permute-start | bytes 196616 | tf_op jit(solution)/shard_map/ppermute | solution.py:596
  65.1 2.5 %collective-permute-start.19 = (bf16[32,1024]{1,0:T(8,128)(2,1)S(1)}, bf16[32,1024]{1,0:T(8,128)(2,1)S(1)}, u32[]{:S(2)}, u32[]{:S(2)}) collective-permute-start(bf16[32,1024]{1,0:T(8,128)(2,1)S(1)} %get-tuple-element.52), channel_id=1, source_target_pairs={{0,12},{4,8},{8,4},{12,0},{1,13},{5,9},{9,5},{13,1},{2,14},{6,10},... | collective-permute-start | bytes 196616 | tf_op jit(solution)/shard_map/ppermute | solution.py:596
  67.5 1.4 %collective-permute-done.18.two_ref = bf16[32,1024]{1,0:T(8,128)(2,1)S(1)} collective-permute-done((bf16[32,1024]{1,0:T(8,128)(2,1)S(1)}, bf16[32,1024]{1,0:T(8,128)(2,1)S(1)}, u32[]{:S(2)}, u32[]{:S(2)}) %collective-permute-start.18) | collective-permute-done | bytes 65568 | tf_op jit(solution)/shard_map/ppermute | solution.py:596
  68.9 2.2 %collective-permute-done.19.three_ref = bf16[32,1024]{1,0:T(8,128)(2,1)S(1)} collective-permute-done((bf16[32,1024]{1,0:T(8,128)(2,1)S(1)}, bf16[32,1024]{1,0:T(8,128)(2,1)S(1)}, u32[]{:S(2)}, u32[]{:S(2)}) %collective-permute-start.19) | collective-permute-done | bytes 65568 | tf_op jit(solution)/shard_map/ppermute | solution.py:596
  71.1 1.1 %scatter.1 = bf16[128,1024]{1,0:T(8,128)(2,1)} custom-call(bf16[32,128]{1,0:T(8,128)(2,1)S(1)} %get-tuple-element.29.pick_ref, bf16[32,1024]{1,0:T(8,128)(2,1)S(1)} %get-tuple-element.49.zero_ref, bf16[32,1024]{1,0:T(8,128)(2,1)S(1)} %collective-permute-done.17.one_ref, bf16[32,1024]{1,0:T(8,128)(2,1)S(1)} %collective-permute-done.18.two_ref, ...), custom_call_target="tpu_custom_call" | custom-call | tf_op jit(solution)/shard_map/scatter/pallas_call | solution.py:174
  (13 shorter events, 0.1 us)
Async XLA Ops:
  1.8 8.3 %collective-permute-start.1 = (bf16[32,1024]{1,0:T(8,128)(2,1)S(1)}, bf16[32,1024]{1,0:T(8,128)(2,1)S(1)}, u32[]{:S(2)}, u32[]{:S(2)}) collective-permute-start(bf16[32,1024]{1,0:T(8,128)(2,1)S(1)} %get-tuple-element.32), channel_id=1, source_target_pairs={{0,2},{1,6},{2,10},{3,14},{4,3},{5,7},{6,11},{7,15},{8,0},{9,4},{1... | collective-permute-start | bytes 196616 | tf_op jit(solution)/shard_map/ppermute | solution.py:495
  4.8 5.3 %collective-permute-start = (bf16[32,1024]{1,0:T(8,128)(2,1)S(1)}, bf16[32,1024]{1,0:T(8,128)(2,1)S(1)}, u32[]{:S(2)}, u32[]{:S(2)}) collective-permute-start(bf16[32,1024]{1,0:T(8,128)(2,1)S(1)} %get-tuple-element.32), channel_id=1, source_target_pairs={{0,0},{1,4},{2,8},{3,12},{4,1},{5,5},{6,9},{7,13},{8,2},{9,6},{10,... | collective-permute-start | bytes 196616 | tf_op jit(solution)/shard_map/ppermute | solution.py:494
  10.1 2.4 %collective-permute-start.2 = (bf16[64,1024]{1,0:T(8,128)(2,1)S(1)}, bf16[64,1024]{1,0:T(8,128)(2,1)S(1)}, u32[]{:S(2)}, u32[]{:S(2)}) collective-permute-start(bf16[64,1024]{1,0:T(8,128)(2,1)S(1)} %join.1.joined_ref), channel_id=1, source_target_pairs={{0,1},{1,0},{2,3},{3,2},{4,5},{5,4},{6,7},{7,6},{8,9},{9,8},{10,11... | collective-permute-start | bytes 393224 | tf_op jit(solution)/shard_map/ppermute | solution.py:512
  13.1 9.8 %collective-permute-start.5 = (bf16[32,1024]{1,0:T(8,128)(2,1)S(1)}, bf16[32,1024]{1,0:T(8,128)(2,1)S(1)}, u32[]{:S(2)}, u32[]{:S(2)}) collective-permute-start(bf16[32,1024]{1,0:T(8,128)(2,1)S(1)} %get-tuple-element.53), channel_id=1, source_target_pairs={{0,12},{4,8},{8,4},{12,0},{1,13},{5,9},{9,5},{13,1},{2,14},{6,10},... | collective-permute-start | bytes 196616 | tf_op jit(solution)/shard_map/ppermute | solution.py:521
  18.7 5.3 %collective-permute-start.4 = (bf16[32,1024]{1,0:T(8,128)(2,1)S(1)}, bf16[32,1024]{1,0:T(8,128)(2,1)S(1)}, u32[]{:S(2)}, u32[]{:S(2)}) collective-permute-start(bf16[32,1024]{1,0:T(8,128)(2,1)S(1)} %get-tuple-element.54), channel_id=1, source_target_pairs={{0,8},{4,12},{8,0},{12,4},{1,9},{5,13},{9,1},{13,5},{2,10},{6,14},... | collective-permute-start | bytes 196616 | tf_op jit(solution)/shard_map/ppermute | solution.py:521
  18.7 5.7 %collective-permute-start.3 = (bf16[32,1024]{1,0:T(8,128)(2,1)S(1)}, bf16[32,1024]{1,0:T(8,128)(2,1)S(1)}, u32[]{:S(2)}, u32[]{:S(2)}) collective-permute-start(bf16[32,1024]{1,0:T(8,128)(2,1)S(1)} %get-tuple-element.55), channel_id=1, source_target_pairs={{0,4},{4,0},{8,12},{12,8},{1,5},{5,1},{9,13},{13,9},{2,6},{6,2},{1... | collective-permute-start | bytes 196616 | tf_op jit(solution)/shard_map/ppermute | solution.py:521
  19.3 5.0 %copy-start = (bf16[1024,4]{0,1:T(4,128)(2,1)S(1)}, bf16[1024,4]{0,1:T(4,128)(2,1)}, u32[]{:S(2)}) copy-start(bf16[1024,4]{0,1:T(4,128)(2,1)} %param.14) | copy-start | bytes 24580
  19.3 5.0 %copy-start.1 = (bf16[2,1024]{1,0:T(2,128)(2,1)S(1)}, bf16[2,1024]{1,0:T(2,128)(2,1)}, u32[]{:S(2)}) copy-start(bf16[2,1024]{1,0:T(2,128)(2,1)} %gain_ref.1) | copy-start | bytes 12292
  24.6 7.8 %collective-permute-start.8 = (bf16[32,1152]{1,0:T(8,128)(2,1)S(1)}, bf16[32,1152]{1,0:T(8,128)(2,1)S(1)}, u32[]{:S(2)}, u32[]{:S(2)}) collective-permute-start(bf16[32,1152]{1,0:T(8,128)(2,1)S(1)} %norm.1.after_ref.zero_ref), channel_id=1, source_target_pairs={{0,12},{4,8},{8,4},{12,0},{1,13},{5,9},{9,5},{13,1},{2,14},{6,10},... | collective-permute-start | bytes 221192 | tf_op jit(solution)/shard_map/ppermute | solution.py:536
  27.0 6.5 %collective-permute-start.7 = (bf16[32,1152]{1,0:T(8,128)(2,1)S(1)}, bf16[32,1152]{1,0:T(8,128)(2,1)S(1)}, u32[]{:S(2)}, u32[]{:S(2)}) collective-permute-start(bf16[32,1152]{1,0:T(8,128)(2,1)S(1)} %norm.1.after_ref.zero_ref), channel_id=1, source_target_pairs={{0,8},{4,12},{8,0},{12,4},{1,9},{5,13},{9,1},{13,5},{2,10},{6,14},... | collective-permute-start | bytes 221192 | tf_op jit(solution)/shard_map/ppermute | solution.py:536
  27.4 6.1 %collective-permute-start.6 = (bf16[32,1152]{1,0:T(8,128)(2,1)S(1)}, bf16[32,1152]{1,0:T(8,128)(2,1)S(1)}, u32[]{:S(2)}, u32[]{:S(2)}) collective-permute-start(bf16[32,1152]{1,0:T(8,128)(2,1)S(1)} %norm.1.after_ref.zero_ref), channel_id=1, source_target_pairs={{0,4},{4,0},{8,12},{12,8},{1,5},{5,1},{9,13},{13,9},{2,6},{6,2},{1... | collective-permute-start | bytes 221192 | tf_op jit(solution)/shard_map/ppermute | solution.py:536
  33.7 7.4 %collective-permute-start.9 = (bf16[48,1152]{1,0:T(8,128)(2,1)S(1)}, bf16[48,1152]{1,0:T(8,128)(2,1)S(1)}, u32[]{:S(2)}, u32[]{:S(2)}) collective-permute-start(bf16[48,1152]{1,0:T(8,128)(2,1)S(1)} %get-tuple-element.37), channel_id=1, source_target_pairs={{0,16},{16,0},{1,17},{17,1},{2,18},{18,2},{3,19},{19,3},{4,20},{20... | collective-permute-start | bytes 331784 | tf_op jit(solution)/shard_map/ppermute | solution.py:548
  35.3 6.3 %collective-permute-start.10 = (bf16[48,1152]{1,0:T(8,128)(2,1)S(1)}, bf16[48,1152]{1,0:T(8,128)(2,1)S(1)}, u32[]{:S(2)}, u32[]{:S(2)}) collective-permute-start(bf16[48,1152]{1,0:T(8,128)(2,1)S(1)} %get-tuple-element.38), channel_id=1, source_target_pairs={{0,2},{2,0},{1,3},{3,1},{4,6},{6,4},{5,7},{7,5},{8,10},{10,8},{9,1... | collective-permute-start | bytes 331784 | tf_op jit(solution)/shard_map/ppermute | solution.py:549
  37.7 5.6 %collective-permute-start.11 = (bf16[48,1152]{1,0:T(8,128)(2,1)S(1)}, bf16[48,1152]{1,0:T(8,128)(2,1)S(1)}, u32[]{:S(2)}, u32[]{:S(2)}) collective-permute-start(bf16[48,1152]{1,0:T(8,128)(2,1)S(1)} %get-tuple-element.39), channel_id=1, source_target_pairs={{0,18},{2,16},{16,2},{18,0},{1,19},{3,17},{17,3},{19,1},{4,22},{6,... | collective-permute-start | bytes 331784 | tf_op jit(solution)/shard_map/ppermute | solution.py:547
  46.5 5.5 %collective-permute-start.12 = (bf16[2768,128]{1,0:T(8,128)(2,1)S(1)}, bf16[2768,128]{1,0:T(8,128)(2,1)S(1)}, u32[]{:S(2)}, u32[]{:S(2)}) collective-permute-start(bf16[2768,128]{1,0:T(8,128)(2,1)S(1)} %get-tuple-element.41.gate_ref), channel_id=1, source_target_pairs={{0,1},{1,0},{2,3},{3,2},{4,5},{5,4},{6,7},{7,6},{8,9},{9,8},{10,11... | collective-permute-start | bytes 2125832 | tf_op jit(solution)/shard_map/ppermute | solution.py:566
  49.6 2.9 %collective-permute-start.13 = (bf16[2752,128]{1,0:T(8,128)(2,1)S(1)}, bf16[2752,128]{1,0:T(8,128)(2,1)S(1)}, u32[]{:S(2)}, u32[]{:S(2)}) collective-permute-start(bf16[2752,128]{1,0:T(8,128)(2,1)S(1)} %up.1.after_ref.up_ref), channel_id=1, source_target_pairs={{0,1},{1,0},{2,3},{3,2},{4,5},{5,4},{6,7},{7,6},{8,9},{9,8},{10,11... | collective-permute-start | bytes 2113544 | tf_op jit(solution)/shard_map/ppermute | solution.py:567
  54.8 5.0 %collective-permute-start.14 = (bf16[48,1024]{1,0:T(8,128)(2,1)S(1)}, bf16[48,1024]{1,0:T(8,128)(2,1)S(1)}, u32[]{:S(2)}, u32[]{:S(2)}) collective-permute-start(bf16[48,1024]{1,0:T(8,128)(2,1)S(1)} %get-tuple-element.46), channel_id=1, source_target_pairs={{0,2},{2,0},{1,3},{3,1},{4,6},{6,4},{5,7},{7,5},{8,10},{10,8},{9,1... | collective-permute-start | bytes 294920 | tf_op jit(solution)/shard_map/ppermute | solution.py:588
  55.9 5.7 %collective-permute-start.15 = (bf16[48,1024]{1,0:T(8,128)(2,1)S(1)}, bf16[48,1024]{1,0:T(8,128)(2,1)S(1)}, u32[]{:S(2)}, u32[]{:S(2)}) collective-permute-start(bf16[48,1024]{1,0:T(8,128)(2,1)S(1)} %get-tuple-element.47), channel_id=1, source_target_pairs={{0,16},{16,0},{1,17},{17,1},{2,18},{18,2},{3,19},{19,3},{4,20},{20... | collective-permute-start | bytes 294920 | tf_op jit(solution)/shard_map/ppermute | solution.py:587
  57.4 5.5 %collective-permute-start.16 = (bf16[48,1024]{1,0:T(8,128)(2,1)S(1)}, bf16[48,1024]{1,0:T(8,128)(2,1)S(1)}, u32[]{:S(2)}, u32[]{:S(2)}) collective-permute-start(bf16[48,1024]{1,0:T(8,128)(2,1)S(1)} %get-tuple-element.48), channel_id=1, source_target_pairs={{0,18},{2,16},{16,2},{18,0},{1,19},{3,17},{17,3},{19,1},{4,22},{6,... | collective-permute-start | bytes 294920 | tf_op jit(solution)/shard_map/ppermute | solution.py:586
  63.1 4.5 %collective-permute-start.17 = (bf16[32,1024]{1,0:T(8,128)(2,1)S(1)}, bf16[32,1024]{1,0:T(8,128)(2,1)S(1)}, u32[]{:S(2)}, u32[]{:S(2)}) collective-permute-start(bf16[32,1024]{1,0:T(8,128)(2,1)S(1)} %get-tuple-element.50), channel_id=1, source_target_pairs={{0,4},{4,0},{8,12},{12,8},{1,5},{5,1},{9,13},{13,9},{2,6},{6,2},{1... | collective-permute-start | bytes 196616 | tf_op jit(solution)/shard_map/ppermute | solution.py:596
  63.1 5.8 %collective-permute-start.18 = (bf16[32,1024]{1,0:T(8,128)(2,1)S(1)}, bf16[32,1024]{1,0:T(8,128)(2,1)S(1)}, u32[]{:S(2)}, u32[]{:S(2)}) collective-permute-start(bf16[32,1024]{1,0:T(8,128)(2,1)S(1)} %get-tuple-element.51), channel_id=1, source_target_pairs={{0,8},{4,12},{8,0},{12,4},{1,9},{5,13},{9,1},{13,5},{2,10},{6,14},... | collective-permute-start | bytes 196616 | tf_op jit(solution)/shard_map/ppermute | solution.py:596
  65.1 6.1 %collective-permute-start.19 = (bf16[32,1024]{1,0:T(8,128)(2,1)S(1)}, bf16[32,1024]{1,0:T(8,128)(2,1)S(1)}, u32[]{:S(2)}, u32[]{:S(2)}) collective-permute-start(bf16[32,1024]{1,0:T(8,128)(2,1)S(1)} %get-tuple-element.52), channel_id=1, source_target_pairs={{0,12},{4,8},{8,4},{12,0},{1,13},{5,9},{9,5},{13,1},{2,14},{6,10},... | collective-permute-start | bytes 196616 | tf_op jit(solution)/shard_map/ppermute | solution.py:596

commit v8 on v7

--- a/solution.py
+++ b/solution.py
@@ -160,7 +160,6 @@
 SWAP = [(0, 1), (1, 0)]
 STRIP = 688
 TILE = 16
-SCALARS = pl.BlockSpec(memory_space=pltpu.SMEM)
 ON_CHIP = pl.BlockSpec(memory_space=pltpu.VMEM)
 IN_HBM = pl.BlockSpec(memory_space=pltpu.HBM)
 ANYWHERE = pl.BlockSpec(memory_space=pl.ANY)
@@ -191,8 +190,8 @@
     count = len(spans)
     weights, held, semaphores = refs[:count], refs[count : 2 * count], refs[-1]
     copies = [
-        pltpu.make_async_copy(weight.at[lax.axis_index("groups"), a:b, c:d], to, semaphores.at[n])
-        for n, (weight, to, (a, b, c, d)) in enumerate(zip(weights, held, spans))
+        pltpu.make_async_copy(weight.at[lax.axis_index("groups"), a:b], to, semaphores.at[n])
+        for n, (weight, to, (a, b)) in enumerate(zip(weights, held, spans))
     ]
     for copy in copies:
         copy.start()
@@ -208,31 +207,32 @@
     return call(
         functools.partial(keep_kernel, spans),
         name,
-        [pltpu.VMEM((b - a, d - c), jnp.bfloat16) for a, b, c, d in spans],
+        [pltpu.VMEM((b - a, weight.shape[2]), jnp.bfloat16) for weight, (a, b) in zip(weights, spans)],
         [ANYWHERE] + [IN_HBM] * len(spans),
         [after] + [in_hbm(weight) for weight in weights],
         scratch=[pltpu.SemaphoreType.DMA((len(spans),))],
-        moved=sum(2 * (b - a) * (d - c) for a, b, c, d in spans),
+        moved=sum(2 * (b - a) * weight.shape[2] for weight, (a, b) in zip(weights, spans)),
         limit=1 << 20,
     )
 
 
 def select_kernel(
-    kind_ref, rows_hbm, context_hbm, picked_ref, pick_ref, kind_out, rows_ref, context_ref, semaphores
+    rows_hbm, context_hbm, picked_ref, pick_ref, kind_ref, rows_ref, context_ref, semaphores
 ):
     rows_copy = pltpu.make_async_copy(rows_hbm, rows_ref, semaphores.at[0])
     context_copy = pltpu.make_async_copy(context_hbm, context_ref, semaphores.at[1])
     rows_copy.start()
     context_copy.start()
     rows_copy.wait()
-    kind_out[...] = jnp.full(kind_out.shape, kind_ref[0], jnp.int32).astype(jnp.float32)
+    kind = jnp.where(jnp.maximum(rows_ref[2, 0], rows_ref[3, 0]) >= 0, 1, 0)
+    kind_ref[...] = jnp.full(kind_ref.shape, kind, jnp.int32).astype(jnp.float32)
     capacity = rows_ref.shape[1]
     slots, tokens = pick_ref.shape
     row = lax.broadcasted_iota(jnp.int32, (slots, tokens), 0)
     token = lax.broadcasted_iota(jnp.int32, (slots, tokens), 1)
     wanted = jnp.full((slots, tokens), -1, jnp.int32)
     for e in range(2):
-        expert = 2 * kind_ref[0] + (lax.axis_index("groups") ^ e)
+        expert = 2 * kind + (lax.axis_index("groups") ^ e)
         for s in range(capacity):
             wanted = jnp.where(row == e * capacity + s, rows_ref[expert, s], wanted)
     pick = jnp.where(wanted == token, 1.0, 0.0).astype(jnp.bfloat16)
@@ -257,7 +257,7 @@
         copy.wait()
 
 
-def join_kernel(near_ref, across_ref, _, out_ref):
+def join_kernel(across_ref, near_ref, _, out_ref):
     slots = near_ref.shape[0]
     out_ref[:slots, :] = near_ref[...]
     out_ref[slots:, :] = across_ref[...]
@@ -281,7 +281,7 @@
     return high, value - high
 
 
-def norm_kernel(kind_ref, rest_ref, partial_ref, one_ref, two_ref, three_ref, gain_ref, router_ref, _, out_ref):
+def norm_kernel(kind_ref, rest_ref, partial_ref, three_ref, two_ref, one_ref, gain_ref, router_ref, _, out_ref):
     slots, columns = rest_ref.shape
     hidden = rest_ref[...] + partial_ref[0].astype(jnp.float32)
     for got_ref in (three_ref, two_ref, one_ref):
@@ -322,7 +322,7 @@
     return matches, found
 
 
-def arrange_kernel(zero_ref, one_ref, two_ref, three_ref, _, *out_refs):
+def arrange_kernel(zero_ref, three_ref, two_ref, one_ref, _, *out_refs):
     packed_refs = (zero_ref, one_ref, two_ref, three_ref)
     capacity = zero_ref.shape[0] // 2
     for out_ref in out_refs:
@@ -338,11 +338,11 @@
                 given_ref[span, :] = ref[capacity:, :]
 
 
-def weights_times_rows(weight_refs, rows, out_ref):
+def weights_times_rows(weight_refs, spans, rows, out_ref):
     at = 0
-    for weight_ref in weight_refs:
-        for start in range(0, weight_ref.shape[0], STRIP):
-            stop = min(start + STRIP, weight_ref.shape[0])
+    for weight_ref, (first, last) in zip(weight_refs, spans):
+        for start in range(first, last, STRIP):
+            stop = min(start + STRIP, last)
             out_ref[at : at + stop - start, :] = lax.dot_general(
                 weight_ref[start:stop, :], rows, (((1,), (1,)), ((), ())), preferred_element_type=jnp.float32
             ).astype(jnp.bfloat16)
@@ -366,7 +366,8 @@
             rows_ref[:half, there : there + columns] = side_own_ref[:, :columns]
             rows_ref[half : 2 * half, there : there + columns] = side_far_ref[:, :columns]
 
-    weights_times_rows(weight_refs, rows_ref[...], out_ref)
+    spans = [(0, ref.shape[0]) for ref in weight_refs]
+    weights_times_rows(weight_refs, spans, rows_ref[...], out_ref)
     tails = [ref[:, columns:].astype(jnp.float32) for ref in (own_ref, side_own_ref, far_ref, side_far_ref)]
     unused = jnp.zeros((rows - 2 * half, STAT_COLS), jnp.float32)
     stat = jnp.concatenate([tails[0] + tails[1], tails[2] + tails[3], unused], axis=0).T
@@ -379,9 +380,8 @@
     out_ref[units:, :] = extra.astype(jnp.bfloat16)
 
 
-def up_kernel(rows_ref, *refs):
-    weight_refs, out_ref = refs[:-1], refs[-1]
-    weights_times_rows(weight_refs, rows_ref[...], out_ref)
+def up_kernel(spans, rows_ref, *refs):
+    weights_times_rows(refs[:-1], spans, rows_ref[...], refs[-1])
 
 
 def silu_kernel(gate_ref, gate_other_ref, out_ref, stat_ref):
@@ -400,14 +400,18 @@
 
 
 def down_kernel(
-    silu_ref, stat_ref, up_ref, up_other_ref, first_ref, second_ref,
+    silu_ref, stat_ref, up_ref, up_late_ref, other_ref, other_late_ref, first_ref, second_ref,
     kept_ref, far_ref, side_ref, side_far_ref, act_ref,
 ):
     units, rows = act_ref.shape
-    for start in range(0, units, STRIP):
-        stop = min(start + STRIP, units)
-        up = up_ref[start:stop, :].astype(jnp.float32) + up_other_ref[start:stop, :].astype(jnp.float32)
-        act_ref[start:stop, :] = (silu_ref[start:stop, :] * up).astype(jnp.bfloat16)
+    at = 0
+    for mine_ref, got_ref in ((up_ref, other_ref), (up_late_ref, other_late_ref)):
+        for start in range(0, mine_ref.shape[0], STRIP):
+            stop = min(start + STRIP, mine_ref.shape[0])
+            up = mine_ref[start:stop, :].astype(jnp.float32) + got_ref[start:stop, :].astype(jnp.float32)
+            span = slice(at, at + stop - start)
+            act_ref[span, :] = (silu_ref[span, :] * up).astype(jnp.bfloat16)
+            at += stop - start
     half, columns = kept_ref.shape
     score = jnp.broadcast_to(stat_ref[1:2, :], (rows, rows)).T[:, 0:1]
     first_units = first_ref.shape[0]
@@ -446,10 +450,8 @@
     total = zero_ref[...].astype(jnp.float32)
     for got_ref in (three_ref, two_ref, one_ref):
         total = total + got_ref[...].astype(jnp.float32)
-    high, rest = split_high_low(total)
-    middle, low = split_high_low(rest)
     result = 0.0
-    for piece in (low, middle, high):
+    for piece in split_high_low(total)[::-1]:
         result = result + lax.dot_general(
             pick_ref[...], piece.astype(jnp.bfloat16), (((0,), (0,)), ((), ())),
             preferred_element_type=jnp.float32,
@@ -480,8 +482,8 @@
         select_kernel,
         "select",
         [array(slots, columns), array(slots, tokens), array(8, STAT_COLS, dtype=jnp.float32)],
-        [SCALARS, IN_HBM, IN_HBM],
-        [block_modality, in_hbm(expert_rows), in_hbm(context)],
+        [IN_HBM] * 2,
+        [in_hbm(expert_rows), in_hbm(context)],
         scratch=[
             pltpu.SMEM((experts, capacity), jnp.int32),
             pltpu.VMEM((tokens, columns), jnp.bfloat16),
@@ -491,14 +493,14 @@
     plane = ("tok", "mod", "fsdp")
     to_first = [(t * 4 + q, q * 4 + t) for t in range(4) for q in range(4)]
     to_second = [(t * 4 + q, q * 4 + (t ^ 2)) for t in range(4) for q in range(4)]
+    across = lax.ppermute(picked, plane, to_second)
     near = lax.ppermute(picked, plane, to_first)
-    across = lax.ppermute(picked, plane, to_second)
-    units_first = units // 2
+    gate_units, up_units, down_units = [round(units * part / TILE) * TILE for part in (0.58, 0.41, 0.24)]
     gate_first, proj_held, rest = call(
         keep_gate_kernel,
         "keep_gate",
         [
-            pltpu.VMEM((units_first, width), jnp.bfloat16),
+            pltpu.VMEM((gate_units, width), jnp.bfloat16),
             pltpu.VMEM(out_proj.shape, jnp.bfloat16),
             array(slots, columns, dtype=jnp.float32),
         ],
@@ -508,7 +510,7 @@
         moved=units * width,
         limit=2 << 20,
     )
-    joined = call(join_kernel, "join", array(half, columns), [ON_CHIP] * 3, [near, across, gate_first])
+    joined = call(join_kernel, "join", array(half, columns), [ON_CHIP] * 3, [across, near, gate_first])
     other = lax.ppermute(joined, "fsdp", SWAP)
     partial = call(
         project_kernel,
@@ -518,11 +520,11 @@
         [joined, other, proj_held],
         scratch=[pltpu.VMEM((rows, columns), jnp.bfloat16)],
     )
-    sums = [lax.ppermute(partial[v], "tok", crossed(2, v)) for v in (1, 2, 3)]
+    sums = [lax.ppermute(partial[v], "tok", crossed(2, v)) for v in (3, 2, 1)][::-1]
     gate_second, up_first = keep_on_chip(
         partial,
         [gate_weight.swapaxes(1, 2), up_weight.swapaxes(1, 2)],
-        [(units_first, units, 0, width), (0, units // 4, 0, width)],
+        [(gate_units, units), (0, up_units)],
         "keep_more",
     )
     packed_columns = columns + STAT_COLS
@@ -531,25 +533,29 @@
         "norm",
         array(slots, packed_columns),
         [ON_CHIP] * 9,
-        [kind, rest, partial, *sums, norm_gain, router_weight.T, up_first],
-    )
-    others = [lax.ppermute(packed, "tok", crossed(2, v)) for v in (1, 2, 3)]
-    (up_second,) = keep_on_chip(packed, [up_weight.swapaxes(1, 2)], [(units // 4, units, 0, width)], "keep_up")
+        [kind, rest, partial, *sums[::-1], norm_gain, router_weight.T, up_first],
+    )
+    others = [lax.ppermute(packed, "tok", crossed(2, v)) for v in (3, 2, 1)][::-1]
+    up_second, down_first = keep_on_chip(
+        packed,
+        [up_weight.swapaxes(1, 2), down_weight],
+        [(up_units, units), (0, down_units)],
+        "keep_up",
+    )
     kept_slots = 3 * capacity
     own, to_far_rows, to_side_rows, to_corner_rows = call(
         arrange_kernel,
         "arrange",
         [array(kept_slots, packed_columns)] * 4,
         [ON_CHIP] * 5,
-        [packed, *others, up_second],
+        [packed, *others[::-1], up_second],
     )
     both_axes = ("groups", "mod")
     side_far = lax.ppermute(to_corner_rows, both_axes, crossed(2, 3))
     far = lax.ppermute(to_far_rows, "groups", SWAP)
     side_own = lax.ppermute(to_side_rows, "mod", SWAP)
 
-    down_units = units // 4 * 3
-    (down_first,) = keep_on_chip(own, [down_weight], [(0, down_units, 0, width)], "keep_down")
+    (down_second,) = keep_on_chip(own, [down_weight], [(down_units, units)], "keep_down")
 
     flops = 2 * rows * units * width
     gate, gathered = call(
@@ -557,15 +563,27 @@
         "gate",
         [array(units + TILE, rows), array(rows, width)],
         [ON_CHIP] * 7,
-        [own, far, side_own, side_far, gate_first, gate_second, down_first],
+        [own, far, side_own, side_far, gate_first, gate_second, down_second],
         flops=flops,
     )
-    up = call(
-        up_kernel, "up", array(units, rows), [ON_CHIP] * 3, [gathered, up_first, up_second], flops=flops
-    )
+    late = units // 4 // TILE * TILE
+    up_rest = units - up_units
+    up_parts = [
+        call(
+            functools.partial(up_kernel, spans),
+            "up",
+            array(sum(b - a for a, b in spans), rows),
+            [ON_CHIP] * (1 + len(spans)),
+            [gathered, *weights],
+            flops=flops * sum(b - a for a, b in spans) // units,
+        )
+        for spans, weights in (
+            (((0, up_units), (0, up_rest - late)), (up_first, up_second)),
+            (((up_rest - late, up_rest),), (up_second,)),
+        )
+    ]
     gate_other = lax.ppermute(gate, "fsdp", SWAP)
-    up_other = lax.ppermute(up, "fsdp", SWAP)
-    (down_second,) = keep_on_chip(up, [down_weight], [(down_units, units, 0, width)], "keep_last")
+    up_others = [lax.ppermute(part, "fsdp", SWAP) for part in up_parts]
     silu, stat = call(
         silu_kernel,
         "silu",
@@ -578,8 +596,8 @@
         down_kernel,
         "down",
         [array(kept_slots, columns)] * 4,
-        [ON_CHIP] * 6,
-        [silu, stat, up, up_other, down_first, down_second],
+        [ON_CHIP] * 8,
+        [silu, stat, *up_parts, *up_others, down_first, down_second],
         scratch=[pltpu.VMEM((units, rows), jnp.bfloat16)],
         flops=flops,
     )

time: 72.5 us -> 71.7 us (0.989)
  Pallas kernels: 27.7 us -> 26.8 us
    ppermute x1, starting transfers between devices: 2.99 us -> 6.79 us  [paired_local(): across = lax.ppermute(picked, plane, to_second)]
    ppermute x7 -> x8, starting transfers between devices: 11.2 us -> 9.52 us  [the longest x3 4.45 us: paired_local(): lax.ppermute(partial[v], 'tok', crossed(2, v))]
    ppermute x1, waiting for transfers between devices: 1.29 us -> 2.79 us  [paired_local(): across = lax.ppermute(picked, plane, to_second)]
    ppermute x1, starting transfers between devices: 2.43 us -> 0.96 us  [paired_local(): side_own = lax.ppermute(to_side_rows, 'mod', SWAP)]
    ppermute x1, starting transfers between devices: 1.44 us -> 0.07 us  [paired_local(): other = lax.ppermute(joined, 'fsdp', SWAP)]
    ppermute x1, starting transfers between devices: 0.01 us -> 0.93 us  [paired_local(): side_far = lax.ppermute(to_corner_rows, both_axes, crossed(2, 3))]
    pallas_call x16, Pallas kernels: 27.7 us -> 26.8 us  [call(): pl.pallas_call(kernel, out_shape=outs, in_specs=specs, out_specs=jax.tree...]
    ppermute x1, waiting for transfers between devices: 1.76 us -> 1 us  [paired_local(): from_far = lax.ppermute(to_far, 'groups', SWAP)]
  transfers between devices with their start and end apart: 20 -> 21, of which waited for: 12 -> 11; matrix products, arithmetic and copies ran while one was open for 0% -> 0% of each run, Pallas kernels for 26% -> 26%
where the time goes in v8:
time: 71.7 us; the launch traced here: 71.5 us
  starting transfers between devices  28.7 us (40%)
  Pallas kernels  26.8 us (37%)
  waiting for transfers between devices  15.8 us (22%)
    pallas_call x16, Pallas kernels, call(): pl.pallas_call(kernel, out_shape=outs, in_specs=specs, out_specs=jax.tree...  26.8 us
    ppermute x1, starting transfers between devices, paired_local(): across = lax.ppermute(picked, plane, to_second)  6.79 us
    ppermute x3, starting transfers between devices, paired_local(): lax.ppermute(partial[v], 'tok', crossed(2, v))  4.45 us
    ppermute x3, starting transfers between devices, paired_local(): lax.ppermute(merged[v], 'tok', crossed(2, v))  4.44 us
    ppermute x3, starting transfers between devices, paired_local(): lax.ppermute(packed, 'tok', crossed(2, v))  4.42 us
    ppermute x3, waiting for transfers between devices, paired_local(): lax.ppermute(merged[v], 'tok', crossed(2, v))  3.85 us
    ppermute x1, waiting for transfers between devices, paired_local(): across = lax.ppermute(picked, plane, to_second)  2.79 us
    ppermute x1, waiting for transfers between devices, paired_local(): from_side = lax.ppermute(to_side, 'mod', SWAP)  1.9 us
  transfers between devices with their start and end apart: 21, of which 11 were waited for; matrix products, arithmetic and copies ran while one was open for 0% of the time, Pallas kernels for 26%

profile of v8, /device:TPU:0, one launch (start us, length us, event | category | flops | bytes accessed | tf_op | source)
XLA Modules:
  0.0 71.5 jit_solution(2103345766171005544)
XLA Ops:
  0.0 1.1 %select.1 = (bf16[32,1024]{1,0:T(8,128)(2,1)S(1)}, bf16[32,128]{1,0:T(8,128)(2,1)S(1)}, f32[8,128]{1,0:T(8,128)S(1)}) custom-call(s32[4,16]{1,0:T(4,128)} %rows_hbm.1, bf16[128,1024]{1,0:T(8,128)(2,1)} %context_hbm.1), custom_call_target="tpu_custom_call" | custom-call | tf_op jit(solution)/shard_map/select/pallas_call | solution.py:173
  1.1 0.7 collective-permute-start.1
  1.8 6.8 %collective-permute-start = (bf16[32,1024]{1,0:T(8,128)(2,1)S(1)}, bf16[32,1024]{1,0:T(8,128)(2,1)S(1)}, u32[]{:S(2)}, u32[]{:S(2)}) collective-permute-start(bf16[32,1024]{1,0:T(8,128)(2,1)S(1)} %get-tuple-element.34), channel_id=1, source_target_pairs={{0,2},{1,6},{2,10},{3,14},{4,3},{5,7},{6,11},{7,15},{8,0},{9,4},{1... | collective-permute-start | bytes 196616 | tf_op jit(solution)/shard_map/ppermute | solution.py:496
  8.6 3.6 %keep_gate.1 = (bf16[1600,2048]{1,0:T(8,128)(2,1)S(1)}, bf16[1024,1024]{1,0:T(8,128)(2,1)S(1)}, f32[32,1024]{1,0:T(8,128)S(1)}) custom-call(bf16[32,128]{1,0:T(8,128)(2,1)S(1)} %get-tuple-element.31.pick_ref, bf16[128,1024]{1,0:T(8,128)(2,1)} %residual_hbm.1, bf16[2,2752,2048]{2,1,0:T(8,128)(2,1)} %bitcast.10, bf16[1024,1024]{1,0:T(8,128)(2,1)} %proj_ref.1), custom_call_target="tpu_custom_call" | custom-call | bytes 5636096 | tf_op jit(solution)/shard_map/keep_gate/pallas_call | solution.py:173
  12.2 2.8 %collective-permute-done.across_ref = bf16[32,1024]{1,0:T(8,128)(2,1)S(1)} collective-permute-done((bf16[32,1024]{1,0:T(8,128)(2,1)S(1)}, bf16[32,1024]{1,0:T(8,128)(2,1)S(1)}, u32[]{:S(2)}, u32[]{:S(2)}) %collective-permute-start) | collective-permute-done | bytes 65568 | tf_op jit(solution)/shard_map/ppermute | solution.py:496
  15.0 0.1 collective-permute-start.2
  15.1 1.3 %collective-permute-done.2.other_ref = bf16[64,1024]{1,0:T(8,128)(2,1)S(1)} collective-permute-done((bf16[64,1024]{1,0:T(8,128)(2,1)S(1)}, bf16[64,1024]{1,0:T(8,128)(2,1)S(1)}, u32[]{:S(2)}, u32[]{:S(2)}) %collective-permute-start.2) | collective-permute-done | bytes 131104 | tf_op jit(solution)/shard_map/ppermute | solution.py:514
  16.5 0.4 project.1.after_ref.partial_ref
  16.9 0.3 collective-permute-start.5
  17.2 0.5 collective-permute-start.4
  17.7 3.7 %collective-permute-start.3 = (bf16[32,1024]{1,0:T(8,128)(2,1)S(1)}, bf16[32,1024]{1,0:T(8,128)(2,1)S(1)}, u32[]{:S(2)}, u32[]{:S(2)}) collective-permute-start(bf16[32,1024]{1,0:T(8,128)(2,1)S(1)} %get-tuple-element.59), channel_id=1, source_target_pairs={{0,12},{4,8},{8,4},{12,0},{1,13},{5,9},{9,5},{13,1},{2,14},{6,10},... | collective-permute-start | bytes 196616 | tf_op jit(solution)/shard_map/ppermute | solution.py:523
  21.4 3.8 %keep_more.1 = (bf16[1152,2048]{1,0:T(8,128)(2,1)S(1)}, bf16[1136,2048]{1,0:T(8,128)(2,1)S(1)}) custom-call(bf16[4,32,1024]{2,1,0:T(8,128)(2,1)S(1)} %project.1.after_ref.partial_ref, bf16[2,2752,2048]{2,1,0:T(8,128)(2,1)} %bitcast.11, bf16[2,2752,2048]{2,1,0:T(8,128)(2,1)} %bitcast.12), custom_call_target="tpu_custom_call" | custom-call | bytes 9371648 | tf_op jit(solution)/shard_map/keep_more/pallas_call | solution.py:173
  25.2 0.0 collective-permute-done.5.one_ref
  25.2 0.4 collective-permute-done.4.two_ref
  25.6 0.2 norm.1.after_ref.zero_ref
  25.9 1.9 %collective-permute-start.8 = (bf16[32,1152]{1,0:T(8,128)(2,1)S(1)}, bf16[32,1152]{1,0:T(8,128)(2,1)S(1)}, u32[]{:S(2)}, u32[]{:S(2)}) collective-permute-start(bf16[32,1152]{1,0:T(8,128)(2,1)S(1)} %norm.1.after_ref.zero_ref), channel_id=1, source_target_pairs={{0,12},{4,8},{8,4},{12,0},{1,13},{5,9},{9,5},{13,1},{2,14},{6,10},... | collective-permute-start | bytes 221192 | tf_op jit(solution)/shard_map/ppermute | solution.py:538
  27.8 0.8 %collective-permute-start.7 = (bf16[32,1152]{1,0:T(8,128)(2,1)S(1)}, bf16[32,1152]{1,0:T(8,128)(2,1)S(1)}, u32[]{:S(2)}, u32[]{:S(2)}) collective-permute-start(bf16[32,1152]{1,0:T(8,128)(2,1)S(1)} %norm.1.after_ref.zero_ref), channel_id=1, source_target_pairs={{0,8},{4,12},{8,0},{12,4},{1,9},{5,13},{9,1},{13,5},{2,10},{6,14},... | collective-permute-start | bytes 221192 | tf_op jit(solution)/shard_map/ppermute | solution.py:538
  28.6 1.7 %collective-permute-start.6 = (bf16[32,1152]{1,0:T(8,128)(2,1)S(1)}, bf16[32,1152]{1,0:T(8,128)(2,1)S(1)}, u32[]{:S(2)}, u32[]{:S(2)}) collective-permute-start(bf16[32,1152]{1,0:T(8,128)(2,1)S(1)} %norm.1.after_ref.zero_ref), channel_id=1, source_target_pairs={{0,4},{4,0},{8,12},{12,8},{1,5},{5,1},{9,13},{13,9},{2,6},{6,2},{1... | collective-permute-start | bytes 221192 | tf_op jit(solution)/shard_map/ppermute | solution.py:538
  30.3 3.7 %keep_up.1 = (bf16[1616,2048]{1,0:T(8,128)(2,1)S(1)}, bf16[656,2048]{1,0:T(8,128)(2,1)S(1)}) custom-call(bf16[32,1152]{1,0:T(8,128)(2,1)S(1)} %norm.1.after_ref.zero_ref, bf16[2,2752,2048]{2,1,0:T(8,128)(2,1)} %bitcast.13, bf16[2,2752,2048]{2,1,0:T(8,128)(2,1)} %refs_0_.1), custom_call_target="tpu_custom_call" | custom-call | bytes 9306112 | tf_op jit(solution)/shard_map/keep_up/pallas_call | solution.py:173
  34.0 0.8 %collective-permute-done.7.two_ref = bf16[32,1152]{1,0:T(8,128)(2,1)S(1)} collective-permute-done((bf16[32,1152]{1,0:T(8,128)(2,1)S(1)}, bf16[32,1152]{1,0:T(8,128)(2,1)S(1)}, u32[]{:S(2)}, u32[]{:S(2)}) %collective-permute-start.7) | collective-permute-done | bytes 73760 | tf_op jit(solution)/shard_map/ppermute | solution.py:538
  34.8 0.2 arrange.1
  34.9 1.7 %collective-permute-start.9 = (bf16[48,1152]{1,0:T(8,128)(2,1)S(1)}, bf16[48,1152]{1,0:T(8,128)(2,1)S(1)}, u32[]{:S(2)}, u32[]{:S(2)}) collective-permute-start(bf16[48,1152]{1,0:T(8,128)(2,1)S(1)} %get-tuple-element.40), channel_id=1, source_target_pairs={{0,16},{16,0},{1,17},{17,1},{2,18},{18,2},{3,19},{19,3},{4,20},{20... | collective-permute-start | bytes 331784 | tf_op jit(solution)/shard_map/ppermute | solution.py:555
  36.6 1.0 %collective-permute-start.10 = (bf16[48,1152]{1,0:T(8,128)(2,1)S(1)}, bf16[48,1152]{1,0:T(8,128)(2,1)S(1)}, u32[]{:S(2)}, u32[]{:S(2)}) collective-permute-start(bf16[48,1152]{1,0:T(8,128)(2,1)S(1)} %get-tuple-element.41), channel_id=1, source_target_pairs={{0,2},{2,0},{1,3},{3,1},{4,6},{6,4},{5,7},{7,5},{8,10},{10,8},{9,1... | collective-permute-start | bytes 331784 | tf_op jit(solution)/shard_map/ppermute | solution.py:556
  37.5 0.9 %collective-permute-start.11 = (bf16[48,1152]{1,0:T(8,128)(2,1)S(1)}, bf16[48,1152]{1,0:T(8,128)(2,1)S(1)}, u32[]{:S(2)}, u32[]{:S(2)}) collective-permute-start(bf16[48,1152]{1,0:T(8,128)(2,1)S(1)} %get-tuple-element.42), channel_id=1, source_target_pairs={{0,18},{2,16},{16,2},{18,0},{1,19},{3,17},{17,3},{19,1},{4,22},{6,... | collective-permute-start | bytes 331784 | tf_op jit(solution)/shard_map/ppermute | solution.py:554
  38.5 3.4 %keep_down.1.refs_2_.second_ref = bf16[2096,2048]{1,0:T(8,128)(2,1)S(1)} custom-call(bf16[48,1152]{1,0:T(8,128)(2,1)S(1)} %get-tuple-element.39.after_ref.own_ref, bf16[2,2752,2048]{2,1,0:T(8,128)(2,1)} %refs_0_.1), custom_call_target="tpu_custom_call" | custom-call | bytes 8585216 | tf_op jit(solution)/shard_map/keep_down/pallas_call | solution.py:173
  42.0 1.6 %collective-permute-done.11.side_far_ref = bf16[48,1152]{1,0:T(8,128)(2,1)S(1)} collective-permute-done((bf16[48,1152]{1,0:T(8,128)(2,1)S(1)}, bf16[48,1152]{1,0:T(8,128)(2,1)S(1)}, u32[]{:S(2)}, u32[]{:S(2)}) %collective-permute-start.11) | collective-permute-done | bytes 110624 | tf_op jit(solution)/shard_map/ppermute | solution.py:554
  43.6 3.1 %gate.1 = (bf16[2768,128]{1,0:T(8,128)(2,1)S(1)}, bf16[128,2048]{1,0:T(8,128)(2,1)S(1)}) custom-call(bf16[48,1152]{1,0:T(8,128)(2,1)S(1)} %get-tuple-element.39.after_ref.own_ref, bf16[48,1152]{1,0:T(8,128)(2,1)S(1)} %collective-permute-done.9.far_ref, bf16[48,1152]{1,0:T(8,128)(2,1)S(1)} %collective-permute-done.10.side_own_ref, ...), custom_call_target="tpu_custom_call" | custom-call | flops 1442840576 | tf_op jit(solution)/shard_map/gate/pallas_call | solution.py:173
  46.7 0.1 collective-permute-start.12
  46.8 2.3 %up.2.up_ref = bf16[2064,128]{1,0:T(8,128)(2,1)S(1)} custom-call(bf16[128,2048]{1,0:T(8,128)(2,1)S(1)} %get-tuple-element.47.rows_ref, bf16[1136,2048]{1,0:T(8,128)(2,1)S(1)} %get-tuple-element.37._.refs_0_, bf16[1616,2048]{1,0:T(8,128)(2,1)S(1)} %get-tuple-element.38._.refs_1_.refs_0_), custom_call_target="tpu_custom_call" | custom-call | flops 1082130432 | tf_op jit(solution)/shard_map/up/pallas_call | solution.py:173
  49.1 0.6 collective-permute-start.13
  49.7 0.9 %up.3.up_late_ref = bf16[688,128]{1,0:T(8,128)(2,1)S(1)} custom-call(bf16[128,2048]{1,0:T(8,128)(2,1)S(1)} %get-tuple-element.47.rows_ref, bf16[1616,2048]{1,0:T(8,128)(2,1)S(1)} %get-tuple-element.38._.refs_1_.refs_0_), custom_call_target="tpu_custom_call" | custom-call | flops 360710144 | tf_op jit(solution)/shard_map/up/pallas_call | solution.py:173
  50.6 0.1 collective-permute-start.14
  50.7 0.5 silu.1
  51.2 0.9 %collective-permute-done.14.other_late_ref = bf16[688,128]{1,0:T(8,128)(2,1)S(1)} collective-permute-done((bf16[688,128]{1,0:T(8,128)(2,1)S(1)}, bf16[688,128]{1,0:T(8,128)(2,1)S(1)}, u32[]{:S(2)}, u32[]{:S(2)}) %collective-permute-start.14) | collective-permute-done | bytes 176160 | tf_op jit(solution)/shard_map/ppermute | solution.py:586
  52.1 2.3 %down.1 = (bf16[48,1024]{1,0:T(8,128)(2,1)S(1)}, bf16[48,1024]{1,0:T(8,128)(2,1)S(1)}, bf16[48,1024]{1,0:T(8,128)(2,1)S(1)}, bf16[48,1024]{1,0:T(8,128)(2,1)S(1)}) custom-call(f32[2752,128]{1,0:T(8,128)S(1)} %get-tuple-element.45.silu_ref, f32[8,128]{1,0:T(8,128)S(1)} %get-tuple-element.46.stat_ref, bf16[2064,128]{1,0:T(8,128)(2,1)S(1)} %up.2.up_ref, ...), custom_call_target="tpu_custom_call" | custom-call | flops 1442840576 | tf_op jit(solution)/shard_map/down/pallas_call | solution.py:173
  54.3 0.8 %collective-permute-start.15 = (bf16[48,1024]{1,0:T(8,128)(2,1)S(1)}, bf16[48,1024]{1,0:T(8,128)(2,1)S(1)}, u32[]{:S(2)}, u32[]{:S(2)}) collective-permute-start(bf16[48,1024]{1,0:T(8,128)(2,1)S(1)} %get-tuple-element.50), channel_id=1, source_target_pairs={{0,2},{2,0},{1,3},{3,1},{4,6},{6,4},{5,7},{7,5},{8,10},{10,8},{9,1... | collective-permute-start | bytes 294920 | tf_op jit(solution)/shard_map/ppermute | solution.py:606
  55.1 1.4 %collective-permute-start.16 = (bf16[48,1024]{1,0:T(8,128)(2,1)S(1)}, bf16[48,1024]{1,0:T(8,128)(2,1)S(1)}, u32[]{:S(2)}, u32[]{:S(2)}) collective-permute-start(bf16[48,1024]{1,0:T(8,128)(2,1)S(1)} %get-tuple-element.51), channel_id=1, source_target_pairs={{0,16},{16,0},{1,17},{17,1},{2,18},{18,2},{3,19},{19,3},{4,20},{20... | collective-permute-start | bytes 294920 | tf_op jit(solution)/shard_map/ppermute | solution.py:605
  56.5 1.4 %collective-permute-start.17 = (bf16[48,1024]{1,0:T(8,128)(2,1)S(1)}, bf16[48,1024]{1,0:T(8,128)(2,1)S(1)}, u32[]{:S(2)}, u32[]{:S(2)}) collective-permute-start(bf16[48,1024]{1,0:T(8,128)(2,1)S(1)} %get-tuple-element.52), channel_id=1, source_target_pairs={{0,18},{2,16},{16,2},{18,0},{1,19},{3,17},{17,3},{19,1},{4,22},{6,... | collective-permute-start | bytes 294920 | tf_op jit(solution)/shard_map/ppermute | solution.py:604
  57.9 1.9 %collective-permute-done.15.side_ref = bf16[48,1024]{1,0:T(8,128)(2,1)S(1)} collective-permute-done((bf16[48,1024]{1,0:T(8,128)(2,1)S(1)}, bf16[48,1024]{1,0:T(8,128)(2,1)S(1)}, u32[]{:S(2)}, u32[]{:S(2)}) %collective-permute-start.15) | collective-permute-done | bytes 98336 | tf_op jit(solution)/shard_map/ppermute | solution.py:606
  59.8 1.0 %collective-permute-done.16.far_ref = bf16[48,1024]{1,0:T(8,128)(2,1)S(1)} collective-permute-done((bf16[48,1024]{1,0:T(8,128)(2,1)S(1)}, bf16[48,1024]{1,0:T(8,128)(2,1)S(1)}, u32[]{:S(2)}, u32[]{:S(2)}) %collective-permute-start.16) | collective-permute-done | bytes 98336 | tf_op jit(solution)/shard_map/ppermute | solution.py:605
  60.8 1.2 %collective-permute-done.17.side_far_ref = bf16[48,1024]{1,0:T(8,128)(2,1)S(1)} collective-permute-done((bf16[48,1024]{1,0:T(8,128)(2,1)S(1)}, bf16[48,1024]{1,0:T(8,128)(2,1)S(1)}, u32[]{:S(2)}, u32[]{:S(2)}) %collective-permute-start.17) | collective-permute-done | bytes 98336 | tf_op jit(solution)/shard_map/ppermute | solution.py:604
  62.0 0.2 merge.1
  62.2 0.1 collective-permute-start.18
  62.3 2.2 %collective-permute-start.19 = (bf16[32,1024]{1,0:T(8,128)(2,1)S(1)}, bf16[32,1024]{1,0:T(8,128)(2,1)S(1)}, u32[]{:S(2)}, u32[]{:S(2)}) collective-permute-start(bf16[32,1024]{1,0:T(8,128)(2,1)S(1)} %get-tuple-element.55), channel_id=1, source_target_pairs={{0,8},{4,12},{8,0},{12,4},{1,9},{5,13},{9,1},{13,5},{2,10},{6,14},... | collective-permute-start | bytes 196616 | tf_op jit(solution)/shard_map/ppermute | solution.py:614
  64.4 2.2 %collective-permute-start.20 = (bf16[32,1024]{1,0:T(8,128)(2,1)S(1)}, bf16[32,1024]{1,0:T(8,128)(2,1)S(1)}, u32[]{:S(2)}, u32[]{:S(2)}) collective-permute-start(bf16[32,1024]{1,0:T(8,128)(2,1)S(1)} %get-tuple-element.56), channel_id=1, source_target_pairs={{0,12},{4,8},{8,4},{12,0},{1,13},{5,9},{9,5},{13,1},{2,14},{6,10},... | collective-permute-start | bytes 196616 | tf_op jit(solution)/shard_map/ppermute | solution.py:614
  66.6 2.3 %collective-permute-done.19.two_ref = bf16[32,1024]{1,0:T(8,128)(2,1)S(1)} collective-permute-done((bf16[32,1024]{1,0:T(8,128)(2,1)S(1)}, bf16[32,1024]{1,0:T(8,128)(2,1)S(1)}, u32[]{:S(2)}, u32[]{:S(2)}) %collective-permute-start.19) | collective-permute-done | bytes 65568 | tf_op jit(solution)/shard_map/ppermute | solution.py:614
  68.9 1.6 %collective-permute-done.20.three_ref = bf16[32,1024]{1,0:T(8,128)(2,1)S(1)} collective-permute-done((bf16[32,1024]{1,0:T(8,128)(2,1)S(1)}, bf16[32,1024]{1,0:T(8,128)(2,1)S(1)}, u32[]{:S(2)}, u32[]{:S(2)}) %collective-permute-start.20) | collective-permute-done | bytes 65568 | tf_op jit(solution)/shard_map/ppermute | solution.py:614
  70.5 1.0 %scatter.1 = bf16[128,1024]{1,0:T(8,128)(2,1)} custom-call(bf16[32,128]{1,0:T(8,128)(2,1)S(1)} %get-tuple-element.31.pick_ref, bf16[32,1024]{1,0:T(8,128)(2,1)S(1)} %get-tuple-element.53.zero_ref, bf16[32,1024]{1,0:T(8,128)(2,1)S(1)} %collective-permute-done.18.one_ref, bf16[32,1024]{1,0:T(8,128)(2,1)S(1)} %collective-permute-done.19.two_ref, ...), custom_call_target="tpu_custom_call" | custom-call | tf_op jit(solution)/shard_map/scatter/pallas_call | solution.py:173
  (15 shorter events, 0.1 us)
Async XLA Ops:
  1.1 11.1 %collective-permute-start.1 = (bf16[32,1024]{1,0:T(8,128)(2,1)S(1)}, bf16[32,1024]{1,0:T(8,128)(2,1)S(1)}, u32[]{:S(2)}, u32[]{:S(2)}) collective-permute-start(bf16[32,1024]{1,0:T(8,128)(2,1)S(1)} %get-tuple-element.34), channel_id=1, source_target_pairs={{0,0},{1,4},{2,8},{3,12},{4,1},{5,5},{6,9},{7,13},{8,2},{9,6},{10,... | collective-permute-start | bytes 196616 | tf_op jit(solution)/shard_map/ppermute | solution.py:497
  1.8 13.2 %collective-permute-start = (bf16[32,1024]{1,0:T(8,128)(2,1)S(1)}, bf16[32,1024]{1,0:T(8,128)(2,1)S(1)}, u32[]{:S(2)}, u32[]{:S(2)}) collective-permute-start(bf16[32,1024]{1,0:T(8,128)(2,1)S(1)} %get-tuple-element.34), channel_id=1, source_target_pairs={{0,2},{1,6},{2,10},{3,14},{4,3},{5,7},{6,11},{7,15},{8,0},{9,4},{1... | collective-permute-start | bytes 196616 | tf_op jit(solution)/shard_map/ppermute | solution.py:496
  15.0 1.4 %collective-permute-start.2 = (bf16[64,1024]{1,0:T(8,128)(2,1)S(1)}, bf16[64,1024]{1,0:T(8,128)(2,1)S(1)}, u32[]{:S(2)}, u32[]{:S(2)}) collective-permute-start(bf16[64,1024]{1,0:T(8,128)(2,1)S(1)} %join.1.joined_ref), channel_id=1, source_target_pairs={{0,1},{1,0},{2,3},{3,2},{4,5},{5,4},{6,7},{7,6},{8,9},{9,8},{10,11... | collective-permute-start | bytes 393224 | tf_op jit(solution)/shard_map/ppermute | solution.py:514
  16.9 8.3 %collective-permute-start.5 = (bf16[32,1024]{1,0:T(8,128)(2,1)S(1)}, bf16[32,1024]{1,0:T(8,128)(2,1)S(1)}, u32[]{:S(2)}, u32[]{:S(2)}) collective-permute-start(bf16[32,1024]{1,0:T(8,128)(2,1)S(1)} %get-tuple-element.57), channel_id=1, source_target_pairs={{0,4},{4,0},{8,12},{12,8},{1,5},{5,1},{9,13},{13,9},{2,6},{6,2},{1... | collective-permute-start | bytes 196616 | tf_op jit(solution)/shard_map/ppermute | solution.py:523
  17.2 8.4 %collective-permute-start.4 = (bf16[32,1024]{1,0:T(8,128)(2,1)S(1)}, bf16[32,1024]{1,0:T(8,128)(2,1)S(1)}, u32[]{:S(2)}, u32[]{:S(2)}) collective-permute-start(bf16[32,1024]{1,0:T(8,128)(2,1)S(1)} %get-tuple-element.58), channel_id=1, source_target_pairs={{0,8},{4,12},{8,0},{12,4},{1,9},{5,13},{9,1},{13,5},{2,10},{6,14},... | collective-permute-start | bytes 196616 | tf_op jit(solution)/shard_map/ppermute | solution.py:523
  17.7 7.9 %collective-permute-start.3 = (bf16[32,1024]{1,0:T(8,128)(2,1)S(1)}, bf16[32,1024]{1,0:T(8,128)(2,1)S(1)}, u32[]{:S(2)}, u32[]{:S(2)}) collective-permute-start(bf16[32,1024]{1,0:T(8,128)(2,1)S(1)} %get-tuple-element.59), channel_id=1, source_target_pairs={{0,12},{4,8},{8,4},{12,0},{1,13},{5,9},{9,5},{13,1},{2,14},{6,10},... | collective-permute-start | bytes 196616 | tf_op jit(solution)/shard_map/ppermute | solution.py:523
  21.4 4.3 %copy-start = (bf16[1024,4]{0,1:T(4,128)(2,1)S(1)}, bf16[1024,4]{0,1:T(4,128)(2,1)}, u32[]{:S(2)}) copy-start(bf16[1024,4]{0,1:T(4,128)(2,1)} %param.14) | copy-start | bytes 24580
  21.4 4.3 %copy-start.1 = (bf16[2,1024]{1,0:T(2,128)(2,1)S(1)}, bf16[2,1024]{1,0:T(2,128)(2,1)}, u32[]{:S(2)}) copy-start(bf16[2,1024]{1,0:T(2,128)(2,1)} %gain_ref.1) | copy-start | bytes 12292
  25.9 8.1 %collective-permute-start.8 = (bf16[32,1152]{1,0:T(8,128)(2,1)S(1)}, bf16[32,1152]{1,0:T(8,128)(2,1)S(1)}, u32[]{:S(2)}, u32[]{:S(2)}) collective-permute-start(bf16[32,1152]{1,0:T(8,128)(2,1)S(1)} %norm.1.after_ref.zero_ref), channel_id=1, source_target_pairs={{0,12},{4,8},{8,4},{12,0},{1,13},{5,9},{9,5},{13,1},{2,14},{6,10},... | collective-permute-start | bytes 221192 | tf_op jit(solution)/shard_map/ppermute | solution.py:538
  27.8 6.9 %collective-permute-start.7 = (bf16[32,1152]{1,0:T(8,128)(2,1)S(1)}, bf16[32,1152]{1,0:T(8,128)(2,1)S(1)}, u32[]{:S(2)}, u32[]{:S(2)}) collective-permute-start(bf16[32,1152]{1,0:T(8,128)(2,1)S(1)} %norm.1.after_ref.zero_ref), channel_id=1, source_target_pairs={{0,8},{4,12},{8,0},{12,4},{1,9},{5,13},{9,1},{13,5},{2,10},{6,14},... | collective-permute-start | bytes 221192 | tf_op jit(solution)/shard_map/ppermute | solution.py:538
  28.6 6.1 %collective-permute-start.6 = (bf16[32,1152]{1,0:T(8,128)(2,1)S(1)}, bf16[32,1152]{1,0:T(8,128)(2,1)S(1)}, u32[]{:S(2)}, u32[]{:S(2)}) collective-permute-start(bf16[32,1152]{1,0:T(8,128)(2,1)S(1)} %norm.1.after_ref.zero_ref), channel_id=1, source_target_pairs={{0,4},{4,0},{8,12},{12,8},{1,5},{5,1},{9,13},{13,9},{2,6},{6,2},{1... | collective-permute-start | bytes 221192 | tf_op jit(solution)/shard_map/ppermute | solution.py:538
  34.9 7.0 %collective-permute-start.9 = (bf16[48,1152]{1,0:T(8,128)(2,1)S(1)}, bf16[48,1152]{1,0:T(8,128)(2,1)S(1)}, u32[]{:S(2)}, u32[]{:S(2)}) collective-permute-start(bf16[48,1152]{1,0:T(8,128)(2,1)S(1)} %get-tuple-element.40), channel_id=1, source_target_pairs={{0,16},{16,0},{1,17},{17,1},{2,18},{18,2},{3,19},{19,3},{4,20},{20... | collective-permute-start | bytes 331784 | tf_op jit(solution)/shard_map/ppermute | solution.py:555
  36.6 5.4 %collective-permute-start.10 = (bf16[48,1152]{1,0:T(8,128)(2,1)S(1)}, bf16[48,1152]{1,0:T(8,128)(2,1)S(1)}, u32[]{:S(2)}, u32[]{:S(2)}) collective-permute-start(bf16[48,1152]{1,0:T(8,128)(2,1)S(1)} %get-tuple-element.41), channel_id=1, source_target_pairs={{0,2},{2,0},{1,3},{3,1},{4,6},{6,4},{5,7},{7,5},{8,10},{10,8},{9,1... | collective-permute-start | bytes 331784 | tf_op jit(solution)/shard_map/ppermute | solution.py:556
  37.5 6.0 %collective-permute-start.11 = (bf16[48,1152]{1,0:T(8,128)(2,1)S(1)}, bf16[48,1152]{1,0:T(8,128)(2,1)S(1)}, u32[]{:S(2)}, u32[]{:S(2)}) collective-permute-start(bf16[48,1152]{1,0:T(8,128)(2,1)S(1)} %get-tuple-element.42), channel_id=1, source_target_pairs={{0,18},{2,16},{16,2},{18,0},{1,19},{3,17},{17,3},{19,1},{4,22},{6,... | collective-permute-start | bytes 331784 | tf_op jit(solution)/shard_map/ppermute | solution.py:554
  46.7 4.0 %collective-permute-start.12 = (bf16[2768,128]{1,0:T(8,128)(2,1)S(1)}, bf16[2768,128]{1,0:T(8,128)(2,1)S(1)}, u32[]{:S(2)}, u32[]{:S(2)}) collective-permute-start(bf16[2768,128]{1,0:T(8,128)(2,1)S(1)} %get-tuple-element.44.gate_ref), channel_id=1, source_target_pairs={{0,1},{1,0},{2,3},{3,2},{4,5},{5,4},{6,7},{7,6},{8,9},{9,8},{10,11... | collective-permute-start | bytes 2125832 | tf_op jit(solution)/shard_map/ppermute | solution.py:585
  49.1 2.9 %collective-permute-start.13 = (bf16[2064,128]{1,0:T(8,128)(2,1)S(1)}, bf16[2064,128]{1,0:T(8,128)(2,1)S(1)}, u32[]{:S(2)}, u32[]{:S(2)}) collective-permute-start(bf16[2064,128]{1,0:T(8,128)(2,1)S(1)} %up.2.up_ref), channel_id=1, source_target_pairs={{0,1},{1,0},{2,3},{3,2},{4,5},{5,4},{6,7},{7,6},{8,9},{9,8},{10,11... | collective-permute-start | bytes 1585160 | tf_op jit(solution)/shard_map/ppermute | solution.py:586
  50.6 1.5 %collective-permute-start.14 = (bf16[688,128]{1,0:T(8,128)(2,1)S(1)}, bf16[688,128]{1,0:T(8,128)(2,1)S(1)}, u32[]{:S(2)}, u32[]{:S(2)}) collective-permute-start(bf16[688,128]{1,0:T(8,128)(2,1)S(1)} %up.3.up_late_ref), channel_id=1, source_target_pairs={{0,1},{1,0},{2,3},{3,2},{4,5},{5,4},{6,7},{7,6},{8,9},{9,8},{10,11... | collective-permute-start | bytes 528392 | tf_op jit(solution)/shard_map/ppermute | solution.py:586
  54.3 5.5 %collective-permute-start.15 = (bf16[48,1024]{1,0:T(8,128)(2,1)S(1)}, bf16[48,1024]{1,0:T(8,128)(2,1)S(1)}, u32[]{:S(2)}, u32[]{:S(2)}) collective-permute-start(bf16[48,1024]{1,0:T(8,128)(2,1)S(1)} %get-tuple-element.50), channel_id=1, source_target_pairs={{0,2},{2,0},{1,3},{3,1},{4,6},{6,4},{5,7},{7,5},{8,10},{10,8},{9,1... | collective-permute-start | bytes 294920 | tf_op jit(solution)/shard_map/ppermute | solution.py:606
  55.1 5.7 %collective-permute-start.16 = (bf16[48,1024]{1,0:T(8,128)(2,1)S(1)}, bf16[48,1024]{1,0:T(8,128)(2,1)S(1)}, u32[]{:S(2)}, u32[]{:S(2)}) collective-permute-start(bf16[48,1024]{1,0:T(8,128)(2,1)S(1)} %get-tuple-element.51), channel_id=1, source_target_pairs={{0,16},{16,0},{1,17},{17,1},{2,18},{18,2},{3,19},{19,3},{4,20},{20... | collective-permute-start | bytes 294920 | tf_op jit(solution)/shard_map/ppermute | solution.py:605
  56.5 5.5 %collective-permute-start.17 = (bf16[48,1024]{1,0:T(8,128)(2,1)S(1)}, bf16[48,1024]{1,0:T(8,128)(2,1)S(1)}, u32[]{:S(2)}, u32[]{:S(2)}) collective-permute-start(bf16[48,1024]{1,0:T(8,128)(2,1)S(1)} %get-tuple-element.52), channel_id=1, source_target_pairs={{0,18},{2,16},{16,2},{18,0},{1,19},{3,17},{17,3},{19,1},{4,22},{6,... | collective-permute-start | bytes 294920 | tf_op jit(solution)/shard_map/ppermute | solution.py:604
  62.2 4.5 %collective-permute-start.18 = (bf16[32,1024]{1,0:T(8,128)(2,1)S(1)}, bf16[32,1024]{1,0:T(8,128)(2,1)S(1)}, u32[]{:S(2)}, u32[]{:S(2)}) collective-permute-start(bf16[32,1024]{1,0:T(8,128)(2,1)S(1)} %get-tuple-element.54), channel_id=1, source_target_pairs={{0,4},{4,0},{8,12},{12,8},{1,5},{5,1},{9,13},{13,9},{2,6},{6,2},{1... | collective-permute-start | bytes 196616 | tf_op jit(solution)/shard_map/ppermute | solution.py:614
  62.3 6.7 %collective-permute-start.19 = (bf16[32,1024]{1,0:T(8,128)(2,1)S(1)}, bf16[32,1024]{1,0:T(8,128)(2,1)S(1)}, u32[]{:S(2)}, u32[]{:S(2)}) collective-permute-start(bf16[32,1024]{1,0:T(8,128)(2,1)S(1)} %get-tuple-element.55), channel_id=1, source_target_pairs={{0,8},{4,12},{8,0},{12,4},{1,9},{5,13},{9,1},{13,5},{2,10},{6,14},... | collective-permute-start | bytes 196616 | tf_op jit(solution)/shard_map/ppermute | solution.py:614
  64.4 6.1 %collective-permute-start.20 = (bf16[32,1024]{1,0:T(8,128)(2,1)S(1)}, bf16[32,1024]{1,0:T(8,128)(2,1)S(1)}, u32[]{:S(2)}, u32[]{:S(2)}) collective-permute-start(bf16[32,1024]{1,0:T(8,128)(2,1)S(1)} %get-tuple-element.56), channel_id=1, source_target_pairs={{0,12},{4,8},{8,4},{12,0},{1,13},{5,9},{9,5},{13,1},{2,14},{6,10},... | collective-permute-start | bytes 196616 | tf_op jit(solution)/shard_map/ppermute | solution.py:614

commit v9 on v8

--- a/solution.py
+++ b/solution.py
@@ -257,7 +257,7 @@
         copy.wait()
 
 
-def join_kernel(across_ref, near_ref, _, out_ref):
+def join_kernel(near_ref, across_ref, _, out_ref):
     slots = near_ref.shape[0]
     out_ref[:slots, :] = near_ref[...]
     out_ref[slots:, :] = across_ref[...]
@@ -349,7 +349,7 @@
             at += stop - start
 
 
-def gate_kernel(own_ref, far_ref, side_own_ref, side_far_ref, *refs):
+def gate_kernel(side_far_ref, side_own_ref, far_ref, own_ref, *refs):
     weight_refs, out_ref, rows_ref = refs[:2], refs[-2], refs[-1]
     half = own_ref.shape[0]
     rows = rows_ref.shape[0]
@@ -432,7 +432,7 @@
                 far_out[...] = value[half : 2 * half]
 
 
-def merge_kernel(zero_ref, one_ref, two_ref, three_ref, kept_ref, side_ref, far_ref, side_far_ref, *out_refs):
+def merge_kernel(zero_ref, three_ref, two_ref, one_ref, side_far_ref, side_ref, far_ref, kept_ref, *out_refs):
     columns = kept_ref.shape[1]
     capacity = zero_ref.shape[0] // 2
     matches, found = places((zero_ref, one_ref, two_ref, three_ref), columns)
@@ -446,17 +446,27 @@
                 out_ref[capacity:, :] = second_ref[span, :]
 
 
-def scatter_kernel(pick_ref, zero_ref, one_ref, two_ref, three_ref, out_ref):
-    total = zero_ref[...].astype(jnp.float32)
-    for got_ref in (three_ref, two_ref, one_ref):
-        total = total + got_ref[...].astype(jnp.float32)
-    result = 0.0
-    for piece in split_high_low(total)[::-1]:
-        result = result + lax.dot_general(
-            pick_ref[...], piece.astype(jnp.bfloat16), (((0,), (0,)), ((), ())),
-            preferred_element_type=jnp.float32,
-        )
-    out_ref[...] = result.astype(jnp.bfloat16)
+def scatter_kernel(pick_ref, zero_ref, one_ref, two_ref, three_ref, out_hbm, out_ref, semaphores):
+    columns = out_ref.shape[1]
+    pieces = semaphores.shape[0]
+    width = columns // pieces
+    copies = []
+    for n in range(pieces):
+        span = slice(n * width, (n + 1) * width)
+        total = zero_ref[:, span].astype(jnp.float32)
+        for got_ref in (three_ref, two_ref, one_ref):
+            total = total + got_ref[:, span].astype(jnp.float32)
+        result = 0.0
+        for piece in split_high_low(total)[::-1]:
+            result = result + lax.dot_general(
+                pick_ref[...], piece.astype(jnp.bfloat16), (((0,), (0,)), ((), ())),
+                preferred_element_type=jnp.float32,
+            )
+        out_ref[:, span] = result.astype(jnp.bfloat16)
+        copies.append(pltpu.make_async_copy(out_ref.at[:, span], out_hbm.at[:, span], semaphores.at[n]))
+        copies[-1].start()
+    for copy in copies:
+        copy.wait()
 
 
 def paired_local(
@@ -510,7 +520,7 @@
         moved=units * width,
         limit=2 << 20,
     )
-    joined = call(join_kernel, "join", array(half, columns), [ON_CHIP] * 3, [across, near, gate_first])
+    joined = call(join_kernel, "join", array(half, columns), [ON_CHIP] * 3, [near, across, gate_first])
     other = lax.ppermute(joined, "fsdp", SWAP)
     partial = call(
         project_kernel,
@@ -563,7 +573,7 @@
         "gate",
         [array(units + TILE, rows), array(rows, width)],
         [ON_CHIP] * 7,
-        [own, far, side_own, side_far, gate_first, gate_second, down_second],
+        [side_far, side_own, far, own, gate_first, gate_second, down_second],
         flops=flops,
     )
     late = units // 4 // TILE * TILE
@@ -609,12 +619,18 @@
         "merge",
         [array(slots, columns)] * 4,
         [ON_CHIP] * 8,
-        [packed, *others, kept, from_side, from_far, from_side_far],
+        [packed, *others[::-1], from_side_far, from_side, from_far, kept],
     )
     values = [merged[0]] + [lax.ppermute(merged[v], "tok", crossed(2, v)) for v in (1, 2, 3)]
-    return call(
-        scatter_kernel, "scatter", array(tokens, columns), [ON_CHIP] * 5, [pick, *values]
-    )
+    return pl.pallas_call(
+        scatter_kernel,
+        out_shape=pltpu.HBM((tokens, columns), jnp.bfloat16),
+        in_specs=[ON_CHIP] * 5,
+        out_specs=IN_HBM,
+        scratch_shapes=[pltpu.VMEM((tokens, columns), jnp.bfloat16), pltpu.SemaphoreType.DMA((4,))],
+        compiler_params=pltpu.CompilerParams(vmem_limit_bytes=8 << 20),
+        name="scatter",
+    )(pick, *values)
 
 
 def solution(mesh):

time: 71.7 us -> 71.6 us (level)
    ppermute x1, starting transfers between devices: 6.79 us -> 2.99 us  [paired_local(): across = lax.ppermute(picked, plane, to_second)]
    ppermute x1, starting transfers between devices: 0.93 us -> 3.24 us  [paired_local(): side_far = lax.ppermute(to_corner_rows, both_axes, crossed(2, 3))]
    ppermute x3, starting transfers between devices: 4.45 us -> 6.44 us  [paired_local(): lax.ppermute(partial[v], 'tok', crossed(2, v))]
    ppermute x3, waiting for transfers between devices: 0.44 us -> 2.35 us  [paired_local(): lax.ppermute(partial[v], 'tok', crossed(2, v))]
    ppermute x1, waiting for transfers between devices: 2.79 us -> 1.03 us  [paired_local(): across = lax.ppermute(picked, plane, to_second)]
    ppermute x1, waiting for transfers between devices: 1.62 us -> 0.01 us  [paired_local(): side_far = lax.ppermute(to_corner_rows, both_axes, crossed(2, 3))]
    ppermute x1, waiting for transfers between devices: 1.24 us -> 2.62 us  [paired_local(): from_side_far = lax.ppermute(to_side_far, both_axes, crossed(2, 3))]
    ppermute x1, starting transfers between devices: 0.07 us -> 1.44 us  [paired_local(): other = lax.ppermute(joined, 'fsdp', SWAP)]
where the time goes in v9:
time: 71.6 us; the launch traced here: 71.4 us
  starting transfers between devices  28.6 us (40%)
  Pallas kernels  26.8 us (37%)
  waiting for transfers between devices  15.9 us (22%)
    pallas_call x15, Pallas kernels, call(): pl.pallas_call(kernel, out_shape=outs, in_specs=specs, out_specs=jax.tree...  25.8 us
    ppermute x3, starting transfers between devices, paired_local(): lax.ppermute(partial[v], 'tok', crossed(2, v))  6.44 us
    ppermute x3, waiting for transfers between devices, paired_local(): lax.ppermute(merged[v], 'tok', crossed(2, v))  4.96 us
    ppermute x3, starting transfers between devices, paired_local(): lax.ppermute(merged[v], 'tok', crossed(2, v))  4.45 us
    ppermute x3, starting transfers between devices, paired_local(): lax.ppermute(packed, 'tok', crossed(2, v))  4.42 us
    ppermute x1, starting transfers between devices, paired_local(): side_far = lax.ppermute(to_corner_rows, both_axes, crossed(2, 3))  3.24 us
    ppermute x1, starting transfers between devices, paired_local(): across = lax.ppermute(picked, plane, to_second)  2.99 us
    ppermute x1, waiting for transfers between devices, paired_local(): from_side_far = lax.ppermute(to_side_far, both_axes, crossed(2, 3))  2.62 us
  transfers between devices with their start and end apart: 21, of which 11 were waited for; matrix products, arithmetic and copies ran while one was open for 0% of the time, Pallas kernels for 26%

profile of v9, /device:TPU:0, one launch (start us, length us, event | category | flops | bytes accessed | tf_op | source)
XLA Modules:
  0.0 71.4 jit_solution(10006920578827876490)
XLA Ops:
  0.0 1.1 %select.1 = (bf16[32,1024]{1,0:T(8,128)(2,1)S(1)}, bf16[32,128]{1,0:T(8,128)(2,1)S(1)}, f32[8,128]{1,0:T(8,128)S(1)}) custom-call(s32[4,16]{1,0:T(4,128)} %rows_hbm.1, bf16[128,1024]{1,0:T(8,128)(2,1)} %context_hbm.1), custom_call_target="tpu_custom_call" | custom-call | tf_op jit(solution)/shard_map/select/pallas_call | solution.py:173
  1.1 3.0 %collective-permute-start.1 = (bf16[32,1024]{1,0:T(8,128)(2,1)S(1)}, bf16[32,1024]{1,0:T(8,128)(2,1)S(1)}, u32[]{:S(2)}, u32[]{:S(2)}) collective-permute-start(bf16[32,1024]{1,0:T(8,128)(2,1)S(1)} %get-tuple-element.34), channel_id=1, source_target_pairs={{0,2},{1,6},{2,10},{3,14},{4,3},{5,7},{6,11},{7,15},{8,0},{9,4},{1... | collective-permute-start | bytes 196616 | tf_op jit(solution)/shard_map/ppermute | solution.py:506
  4.1 0.7 collective-permute-start
  4.8 3.6 %keep_gate.1 = (bf16[1600,2048]{1,0:T(8,128)(2,1)S(1)}, bf16[1024,1024]{1,0:T(8,128)(2,1)S(1)}, f32[32,1024]{1,0:T(8,128)S(1)}) custom-call(bf16[32,128]{1,0:T(8,128)(2,1)S(1)} %get-tuple-element.31.pick_ref, bf16[128,1024]{1,0:T(8,128)(2,1)} %residual_hbm.1, bf16[2,2752,2048]{2,1,0:T(8,128)(2,1)} %bitcast.10, bf16[1024,1024]{1,0:T(8,128)(2,1)} %proj_ref.1), custom_call_target="tpu_custom_call" | custom-call | bytes 5636096 | tf_op jit(solution)/shard_map/keep_gate/pallas_call | solution.py:173
  8.4 1.0 %collective-permute-done.1.across_ref = bf16[32,1024]{1,0:T(8,128)(2,1)S(1)} collective-permute-done((bf16[32,1024]{1,0:T(8,128)(2,1)S(1)}, bf16[32,1024]{1,0:T(8,128)(2,1)S(1)}, u32[]{:S(2)}, u32[]{:S(2)}) %collective-permute-start.1) | collective-permute-done | bytes 65568 | tf_op jit(solution)/shard_map/ppermute | solution.py:506
  9.5 0.0 collective-permute-done.near_ref
  9.5 1.4 %collective-permute-start.2 = (bf16[64,1024]{1,0:T(8,128)(2,1)S(1)}, bf16[64,1024]{1,0:T(8,128)(2,1)S(1)}, u32[]{:S(2)}, u32[]{:S(2)}) collective-permute-start(bf16[64,1024]{1,0:T(8,128)(2,1)S(1)} %join.1.joined_ref), channel_id=1, source_target_pairs={{0,1},{1,0},{2,3},{3,2},{4,5},{5,4},{6,7},{7,6},{8,9},{9,8},{10,11... | collective-permute-start | bytes 393224 | tf_op jit(solution)/shard_map/ppermute | solution.py:524
  10.9 1.0 %collective-permute-done.2.other_ref = bf16[64,1024]{1,0:T(8,128)(2,1)S(1)} collective-permute-done((bf16[64,1024]{1,0:T(8,128)(2,1)S(1)}, bf16[64,1024]{1,0:T(8,128)(2,1)S(1)}, u32[]{:S(2)}, u32[]{:S(2)}) %collective-permute-start.2) | collective-permute-done | bytes 131104 | tf_op jit(solution)/shard_map/ppermute | solution.py:524
  11.9 0.4 project.1.after_ref.partial_ref
  12.4 2.0 %collective-permute-start.5 = (bf16[32,1024]{1,0:T(8,128)(2,1)S(1)}, bf16[32,1024]{1,0:T(8,128)(2,1)S(1)}, u32[]{:S(2)}, u32[]{:S(2)}) collective-permute-start(bf16[32,1024]{1,0:T(8,128)(2,1)S(1)} %get-tuple-element.57), channel_id=1, source_target_pairs={{0,4},{4,0},{8,12},{12,8},{1,5},{5,1},{9,13},{13,9},{2,6},{6,2},{1... | collective-permute-start | bytes 196616 | tf_op jit(solution)/shard_map/ppermute | solution.py:533
  14.4 4.4 %collective-permute-start.4 = (bf16[32,1024]{1,0:T(8,128)(2,1)S(1)}, bf16[32,1024]{1,0:T(8,128)(2,1)S(1)}, u32[]{:S(2)}, u32[]{:S(2)}) collective-permute-start(bf16[32,1024]{1,0:T(8,128)(2,1)S(1)} %get-tuple-element.58), channel_id=1, source_target_pairs={{0,8},{4,12},{8,0},{12,4},{1,9},{5,13},{9,1},{13,5},{2,10},{6,14},... | collective-permute-start | bytes 196616 | tf_op jit(solution)/shard_map/ppermute | solution.py:533
  18.8 3.8 %keep_more.1 = (bf16[1152,2048]{1,0:T(8,128)(2,1)S(1)}, bf16[1136,2048]{1,0:T(8,128)(2,1)S(1)}) custom-call(bf16[4,32,1024]{2,1,0:T(8,128)(2,1)S(1)} %project.1.after_ref.partial_ref, bf16[2,2752,2048]{2,1,0:T(8,128)(2,1)} %bitcast.11, bf16[2,2752,2048]{2,1,0:T(8,128)(2,1)} %bitcast.12), custom_call_target="tpu_custom_call" | custom-call | bytes 9371648 | tf_op jit(solution)/shard_map/keep_more/pallas_call | solution.py:173
  22.6 0.0 collective-permute-done.5.one_ref
  22.6 0.2 collective-permute-done.4.two_ref
  22.9 2.1 %collective-permute-done.3.three_ref = bf16[32,1024]{1,0:T(8,128)(2,1)S(1)} collective-permute-done((bf16[32,1024]{1,0:T(8,128)(2,1)S(1)}, bf16[32,1024]{1,0:T(8,128)(2,1)S(1)}, u32[]{:S(2)}, u32[]{:S(2)}) %collective-permute-start.3) | collective-permute-done | bytes 65568 | tf_op jit(solution)/shard_map/ppermute | solution.py:533
  25.0 0.2 norm.1.after_ref.zero_ref
  25.2 0.8 %collective-permute-start.8 = (bf16[32,1152]{1,0:T(8,128)(2,1)S(1)}, bf16[32,1152]{1,0:T(8,128)(2,1)S(1)}, u32[]{:S(2)}, u32[]{:S(2)}) collective-permute-start(bf16[32,1152]{1,0:T(8,128)(2,1)S(1)} %norm.1.after_ref.zero_ref), channel_id=1, source_target_pairs={{0,4},{4,0},{8,12},{12,8},{1,5},{5,1},{9,13},{13,9},{2,6},{6,2},{1... | collective-permute-start | bytes 221192 | tf_op jit(solution)/shard_map/ppermute | solution.py:548
  26.0 1.7 %collective-permute-start.7 = (bf16[32,1152]{1,0:T(8,128)(2,1)S(1)}, bf16[32,1152]{1,0:T(8,128)(2,1)S(1)}, u32[]{:S(2)}, u32[]{:S(2)}) collective-permute-start(bf16[32,1152]{1,0:T(8,128)(2,1)S(1)} %norm.1.after_ref.zero_ref), channel_id=1, source_target_pairs={{0,8},{4,12},{8,0},{12,4},{1,9},{5,13},{9,1},{13,5},{2,10},{6,14},... | collective-permute-start | bytes 221192 | tf_op jit(solution)/shard_map/ppermute | solution.py:548
  27.7 1.9 %collective-permute-start.6 = (bf16[32,1152]{1,0:T(8,128)(2,1)S(1)}, bf16[32,1152]{1,0:T(8,128)(2,1)S(1)}, u32[]{:S(2)}, u32[]{:S(2)}) collective-permute-start(bf16[32,1152]{1,0:T(8,128)(2,1)S(1)} %norm.1.after_ref.zero_ref), channel_id=1, source_target_pairs={{0,12},{4,8},{8,4},{12,0},{1,13},{5,9},{9,5},{13,1},{2,14},{6,10},... | collective-permute-start | bytes 221192 | tf_op jit(solution)/shard_map/ppermute | solution.py:548
  29.7 3.7 %keep_up.1 = (bf16[1616,2048]{1,0:T(8,128)(2,1)S(1)}, bf16[656,2048]{1,0:T(8,128)(2,1)S(1)}) custom-call(bf16[32,1152]{1,0:T(8,128)(2,1)S(1)} %norm.1.after_ref.zero_ref, bf16[2,2752,2048]{2,1,0:T(8,128)(2,1)} %bitcast.13, bf16[2,2752,2048]{2,1,0:T(8,128)(2,1)} %refs_0_.1), custom_call_target="tpu_custom_call" | custom-call | bytes 9306112 | tf_op jit(solution)/shard_map/keep_up/pallas_call | solution.py:173
  33.3 0.0 collective-permute-done.8.one_ref
  33.3 0.0 collective-permute-done.7.two_ref
  33.4 0.6 collective-permute-done.6.three_ref
  34.0 0.2 arrange.1
  34.2 3.2 %collective-permute-start.9 = (bf16[48,1152]{1,0:T(8,128)(2,1)S(1)}, bf16[48,1152]{1,0:T(8,128)(2,1)S(1)}, u32[]{:S(2)}, u32[]{:S(2)}) collective-permute-start(bf16[48,1152]{1,0:T(8,128)(2,1)S(1)} %get-tuple-element.39), channel_id=1, source_target_pairs={{0,18},{2,16},{16,2},{18,0},{1,19},{3,17},{17,3},{19,1},{4,22},{6,... | collective-permute-start | bytes 331784 | tf_op jit(solution)/shard_map/ppermute | solution.py:564
  37.4 0.6 collective-permute-start.11
  38.0 3.4 %keep_down.1.refs_2_.second_ref = bf16[2096,2048]{1,0:T(8,128)(2,1)S(1)} custom-call(bf16[48,1152]{1,0:T(8,128)(2,1)S(1)} %get-tuple-element.42.after_ref.own_ref, bf16[2,2752,2048]{2,1,0:T(8,128)(2,1)} %refs_0_.1), custom_call_target="tpu_custom_call" | custom-call | bytes 8585216 | tf_op jit(solution)/shard_map/keep_down/pallas_call | solution.py:173
  41.5 0.6 collective-permute-done.10.side_own_ref
  42.2 3.1 %gate.1 = (bf16[2768,128]{1,0:T(8,128)(2,1)S(1)}, bf16[128,2048]{1,0:T(8,128)(2,1)S(1)}) custom-call(bf16[48,1152]{1,0:T(8,128)(2,1)S(1)} %collective-permute-done.9.side_far_ref, bf16[48,1152]{1,0:T(8,128)(2,1)S(1)} %collective-permute-done.10.side_own_ref, bf16[48,1152]{1,0:T(8,128)(2,1)S(1)} %collective-permute-done.11.far_ref, ...), custom_call_target="tpu_custom_call" | custom-call | flops 1442840576 | tf_op jit(solution)/shard_map/gate/pallas_call | solution.py:173
  45.3 0.1 collective-permute-start.12
  45.3 2.3 %up.2.up_ref = bf16[2064,128]{1,0:T(8,128)(2,1)S(1)} custom-call(bf16[128,2048]{1,0:T(8,128)(2,1)S(1)} %get-tuple-element.47.rows_ref, bf16[1136,2048]{1,0:T(8,128)(2,1)S(1)} %get-tuple-element.37._.refs_0_, bf16[1616,2048]{1,0:T(8,128)(2,1)S(1)} %get-tuple-element.38._.refs_1_.refs_0_), custom_call_target="tpu_custom_call" | custom-call | flops 1082130432 | tf_op jit(solution)/shard_map/up/pallas_call | solution.py:173
  47.7 0.6 collective-permute-start.13
  48.3 0.9 %up.3.up_late_ref = bf16[688,128]{1,0:T(8,128)(2,1)S(1)} custom-call(bf16[128,2048]{1,0:T(8,128)(2,1)S(1)} %get-tuple-element.47.rows_ref, bf16[1616,2048]{1,0:T(8,128)(2,1)S(1)} %get-tuple-element.38._.refs_1_.refs_0_), custom_call_target="tpu_custom_call" | custom-call | flops 360710144 | tf_op jit(solution)/shard_map/up/pallas_call | solution.py:173
  49.2 0.1 collective-permute-start.14
  49.2 0.5 silu.1
  49.8 0.9 %collective-permute-done.14.other_late_ref = bf16[688,128]{1,0:T(8,128)(2,1)S(1)} collective-permute-done((bf16[688,128]{1,0:T(8,128)(2,1)S(1)}, bf16[688,128]{1,0:T(8,128)(2,1)S(1)}, u32[]{:S(2)}, u32[]{:S(2)}) %collective-permute-start.14) | collective-permute-done | bytes 176160 | tf_op jit(solution)/shard_map/ppermute | solution.py:596
  50.6 2.3 %down.1 = (bf16[48,1024]{1,0:T(8,128)(2,1)S(1)}, bf16[48,1024]{1,0:T(8,128)(2,1)S(1)}, bf16[48,1024]{1,0:T(8,128)(2,1)S(1)}, bf16[48,1024]{1,0:T(8,128)(2,1)S(1)}) custom-call(f32[2752,128]{1,0:T(8,128)S(1)} %get-tuple-element.45.silu_ref, f32[8,128]{1,0:T(8,128)S(1)} %get-tuple-element.46.stat_ref, bf16[2064,128]{1,0:T(8,128)(2,1)S(1)} %up.2.up_ref, ...), custom_call_target="tpu_custom_call" | custom-call | flops 1442840576 | tf_op jit(solution)/shard_map/down/pallas_call | solution.py:173
  52.9 2.3 %collective-permute-start.15 = (bf16[48,1024]{1,0:T(8,128)(2,1)S(1)}, bf16[48,1024]{1,0:T(8,128)(2,1)S(1)}, u32[]{:S(2)}, u32[]{:S(2)}) collective-permute-start(bf16[48,1024]{1,0:T(8,128)(2,1)S(1)} %get-tuple-element.49), channel_id=1, source_target_pairs={{0,18},{2,16},{16,2},{18,0},{1,19},{3,17},{17,3},{19,1},{4,22},{6,... | collective-permute-start | bytes 294920 | tf_op jit(solution)/shard_map/ppermute | solution.py:614
  55.2 1.3 %collective-permute-start.17 = (bf16[48,1024]{1,0:T(8,128)(2,1)S(1)}, bf16[48,1024]{1,0:T(8,128)(2,1)S(1)}, u32[]{:S(2)}, u32[]{:S(2)}) collective-permute-start(bf16[48,1024]{1,0:T(8,128)(2,1)S(1)} %get-tuple-element.51), channel_id=1, source_target_pairs={{0,16},{16,0},{1,17},{17,1},{2,18},{18,2},{3,19},{19,3},{4,20},{20... | collective-permute-start | bytes 294920 | tf_op jit(solution)/shard_map/ppermute | solution.py:615
  56.5 2.6 %collective-permute-done.15.side_far_ref = bf16[48,1024]{1,0:T(8,128)(2,1)S(1)} collective-permute-done((bf16[48,1024]{1,0:T(8,128)(2,1)S(1)}, bf16[48,1024]{1,0:T(8,128)(2,1)S(1)}, u32[]{:S(2)}, u32[]{:S(2)}) %collective-permute-start.15) | collective-permute-done | bytes 98336 | tf_op jit(solution)/shard_map/ppermute | solution.py:614
  59.1 1.1 %collective-permute-done.16.side_ref = bf16[48,1024]{1,0:T(8,128)(2,1)S(1)} collective-permute-done((bf16[48,1024]{1,0:T(8,128)(2,1)S(1)}, bf16[48,1024]{1,0:T(8,128)(2,1)S(1)}, u32[]{:S(2)}, u32[]{:S(2)}) %collective-permute-start.16) | collective-permute-done | bytes 98336 | tf_op jit(solution)/shard_map/ppermute | solution.py:616
  60.2 0.6 collective-permute-done.17.far_ref
  60.8 0.2 merge.1
  61.0 1.5 %collective-permute-start.18 = (bf16[32,1024]{1,0:T(8,128)(2,1)S(1)}, bf16[32,1024]{1,0:T(8,128)(2,1)S(1)}, u32[]{:S(2)}, u32[]{:S(2)}) collective-permute-start(bf16[32,1024]{1,0:T(8,128)(2,1)S(1)} %get-tuple-element.54), channel_id=1, source_target_pairs={{0,4},{4,0},{8,12},{12,8},{1,5},{5,1},{9,13},{13,9},{2,6},{6,2},{1... | collective-permute-start | bytes 196616 | tf_op jit(solution)/shard_map/ppermute | solution.py:624
  62.5 1.1 %collective-permute-start.19 = (bf16[32,1024]{1,0:T(8,128)(2,1)S(1)}, bf16[32,1024]{1,0:T(8,128)(2,1)S(1)}, u32[]{:S(2)}, u32[]{:S(2)}) collective-permute-start(bf16[32,1024]{1,0:T(8,128)(2,1)S(1)} %get-tuple-element.55), channel_id=1, source_target_pairs={{0,8},{4,12},{8,0},{12,4},{1,9},{5,13},{9,1},{13,5},{2,10},{6,14},... | collective-permute-start | bytes 196616 | tf_op jit(solution)/shard_map/ppermute | solution.py:624
  63.6 1.8 %collective-permute-start.20 = (bf16[32,1024]{1,0:T(8,128)(2,1)S(1)}, bf16[32,1024]{1,0:T(8,128)(2,1)S(1)}, u32[]{:S(2)}, u32[]{:S(2)}) collective-permute-start(bf16[32,1024]{1,0:T(8,128)(2,1)S(1)} %get-tuple-element.56), channel_id=1, source_target_pairs={{0,12},{4,8},{8,4},{12,0},{1,13},{5,9},{9,5},{13,1},{2,14},{6,10},... | collective-permute-start | bytes 196616 | tf_op jit(solution)/shard_map/ppermute | solution.py:624
  65.4 5.0 %collective-permute-done.19.two_ref = bf16[32,1024]{1,0:T(8,128)(2,1)S(1)} collective-permute-done((bf16[32,1024]{1,0:T(8,128)(2,1)S(1)}, bf16[32,1024]{1,0:T(8,128)(2,1)S(1)}, u32[]{:S(2)}, u32[]{:S(2)}) %collective-permute-start.19) | collective-permute-done | bytes 65568 | tf_op jit(solution)/shard_map/ppermute | solution.py:624
  70.4 1.0 %scatter.1 = bf16[128,1024]{1,0:T(8,128)(2,1)} custom-call(bf16[32,128]{1,0:T(8,128)(2,1)S(1)} %get-tuple-element.31.pick_ref, bf16[32,1024]{1,0:T(8,128)(2,1)S(1)} %get-tuple-element.53.zero_ref, bf16[32,1024]{1,0:T(8,128)(2,1)S(1)} %collective-permute-done.18.one_ref, bf16[32,1024]{1,0:T(8,128)(2,1)S(1)} %collective-permute-done.19.two_ref, ...), custom_call_target="tpu_custom_call" | custom-call | tf_op jit(solution)/shard_map/scatter/pallas_call | solution.py:625
  (15 shorter events, 0.1 us)
Async XLA Ops:
  1.1 8.3 %collective-permute-start.1 = (bf16[32,1024]{1,0:T(8,128)(2,1)S(1)}, bf16[32,1024]{1,0:T(8,128)(2,1)S(1)}, u32[]{:S(2)}, u32[]{:S(2)}) collective-permute-start(bf16[32,1024]{1,0:T(8,128)(2,1)S(1)} %get-tuple-element.34), channel_id=1, source_target_pairs={{0,2},{1,6},{2,10},{3,14},{4,3},{5,7},{6,11},{7,15},{8,0},{9,4},{1... | collective-permute-start | bytes 196616 | tf_op jit(solution)/shard_map/ppermute | solution.py:506
  4.1 5.3 %collective-permute-start = (bf16[32,1024]{1,0:T(8,128)(2,1)S(1)}, bf16[32,1024]{1,0:T(8,128)(2,1)S(1)}, u32[]{:S(2)}, u32[]{:S(2)}) collective-permute-start(bf16[32,1024]{1,0:T(8,128)(2,1)S(1)} %get-tuple-element.34), channel_id=1, source_target_pairs={{0,0},{1,4},{2,8},{3,12},{4,1},{5,5},{6,9},{7,13},{8,2},{9,6},{10,... | collective-permute-start | bytes 196616 | tf_op jit(solution)/shard_map/ppermute | solution.py:507
  9.5 2.4 %collective-permute-start.2 = (bf16[64,1024]{1,0:T(8,128)(2,1)S(1)}, bf16[64,1024]{1,0:T(8,128)(2,1)S(1)}, u32[]{:S(2)}, u32[]{:S(2)}) collective-permute-start(bf16[64,1024]{1,0:T(8,128)(2,1)S(1)} %join.1.joined_ref), channel_id=1, source_target_pairs={{0,1},{1,0},{2,3},{3,2},{4,5},{5,4},{6,7},{7,6},{8,9},{9,8},{10,11... | collective-permute-start | bytes 393224 | tf_op jit(solution)/shard_map/ppermute | solution.py:524
  12.4 10.2 %collective-permute-start.5 = (bf16[32,1024]{1,0:T(8,128)(2,1)S(1)}, bf16[32,1024]{1,0:T(8,128)(2,1)S(1)}, u32[]{:S(2)}, u32[]{:S(2)}) collective-permute-start(bf16[32,1024]{1,0:T(8,128)(2,1)S(1)} %get-tuple-element.57), channel_id=1, source_target_pairs={{0,4},{4,0},{8,12},{12,8},{1,5},{5,1},{9,13},{13,9},{2,6},{6,2},{1... | collective-permute-start | bytes 196616 | tf_op jit(solution)/shard_map/ppermute | solution.py:533
  14.4 8.4 %collective-permute-start.4 = (bf16[32,1024]{1,0:T(8,128)(2,1)S(1)}, bf16[32,1024]{1,0:T(8,128)(2,1)S(1)}, u32[]{:S(2)}, u32[]{:S(2)}) collective-permute-start(bf16[32,1024]{1,0:T(8,128)(2,1)S(1)} %get-tuple-element.58), channel_id=1, source_target_pairs={{0,8},{4,12},{8,0},{12,4},{1,9},{5,13},{9,1},{13,5},{2,10},{6,14},... | collective-permute-start | bytes 196616 | tf_op jit(solution)/shard_map/ppermute | solution.py:533
  18.8 6.2 %collective-permute-start.3 = (bf16[32,1024]{1,0:T(8,128)(2,1)S(1)}, bf16[32,1024]{1,0:T(8,128)(2,1)S(1)}, u32[]{:S(2)}, u32[]{:S(2)}) collective-permute-start(bf16[32,1024]{1,0:T(8,128)(2,1)S(1)} %get-tuple-element.59), channel_id=1, source_target_pairs={{0,12},{4,8},{8,4},{12,0},{1,13},{5,9},{9,5},{13,1},{2,14},{6,10},... | collective-permute-start | bytes 196616 | tf_op jit(solution)/shard_map/ppermute | solution.py:533
  18.8 6.2 %copy-start = (bf16[1024,4]{0,1:T(4,128)(2,1)S(1)}, bf16[1024,4]{0,1:T(4,128)(2,1)}, u32[]{:S(2)}) copy-start(bf16[1024,4]{0,1:T(4,128)(2,1)} %param.14) | copy-start | bytes 24580
  18.8 6.2 %copy-start.1 = (bf16[2,1024]{1,0:T(2,128)(2,1)S(1)}, bf16[2,1024]{1,0:T(2,128)(2,1)}, u32[]{:S(2)}) copy-start(bf16[2,1024]{1,0:T(2,128)(2,1)} %gain_ref.1) | copy-start | bytes 12292
  25.2 8.1 %collective-permute-start.8 = (bf16[32,1152]{1,0:T(8,128)(2,1)S(1)}, bf16[32,1152]{1,0:T(8,128)(2,1)S(1)}, u32[]{:S(2)}, u32[]{:S(2)}) collective-permute-start(bf16[32,1152]{1,0:T(8,128)(2,1)S(1)} %norm.1.after_ref.zero_ref), channel_id=1, source_target_pairs={{0,4},{4,0},{8,12},{12,8},{1,5},{5,1},{9,13},{13,9},{2,6},{6,2},{1... | collective-permute-start | bytes 221192 | tf_op jit(solution)/shard_map/ppermute | solution.py:548
  26.0 7.3 %collective-permute-start.7 = (bf16[32,1152]{1,0:T(8,128)(2,1)S(1)}, bf16[32,1152]{1,0:T(8,128)(2,1)S(1)}, u32[]{:S(2)}, u32[]{:S(2)}) collective-permute-start(bf16[32,1152]{1,0:T(8,128)(2,1)S(1)} %norm.1.after_ref.zero_ref), channel_id=1, source_target_pairs={{0,8},{4,12},{8,0},{12,4},{1,9},{5,13},{9,1},{13,5},{2,10},{6,14},... | collective-permute-start | bytes 221192 | tf_op jit(solution)/shard_map/ppermute | solution.py:548
  27.7 6.3 %collective-permute-start.6 = (bf16[32,1152]{1,0:T(8,128)(2,1)S(1)}, bf16[32,1152]{1,0:T(8,128)(2,1)S(1)}, u32[]{:S(2)}, u32[]{:S(2)}) collective-permute-start(bf16[32,1152]{1,0:T(8,128)(2,1)S(1)} %norm.1.after_ref.zero_ref), channel_id=1, source_target_pairs={{0,12},{4,8},{8,4},{12,0},{1,13},{5,9},{9,5},{13,1},{2,14},{6,10},... | collective-permute-start | bytes 221192 | tf_op jit(solution)/shard_map/ppermute | solution.py:548
  34.2 7.3 %collective-permute-start.9 = (bf16[48,1152]{1,0:T(8,128)(2,1)S(1)}, bf16[48,1152]{1,0:T(8,128)(2,1)S(1)}, u32[]{:S(2)}, u32[]{:S(2)}) collective-permute-start(bf16[48,1152]{1,0:T(8,128)(2,1)S(1)} %get-tuple-element.39), channel_id=1, source_target_pairs={{0,18},{2,16},{16,2},{18,0},{1,19},{3,17},{17,3},{19,1},{4,22},{6,... | collective-permute-start | bytes 331784 | tf_op jit(solution)/shard_map/ppermute | solution.py:564
  37.4 4.7 %collective-permute-start.10 = (bf16[48,1152]{1,0:T(8,128)(2,1)S(1)}, bf16[48,1152]{1,0:T(8,128)(2,1)S(1)}, u32[]{:S(2)}, u32[]{:S(2)}) collective-permute-start(bf16[48,1152]{1,0:T(8,128)(2,1)S(1)} %get-tuple-element.40), channel_id=1, source_target_pairs={{0,2},{2,0},{1,3},{3,1},{4,6},{6,4},{5,7},{7,5},{8,10},{10,8},{9,1... | collective-permute-start | bytes 331784 | tf_op jit(solution)/shard_map/ppermute | solution.py:566
  37.4 4.7 %collective-permute-start.11 = (bf16[48,1152]{1,0:T(8,128)(2,1)S(1)}, bf16[48,1152]{1,0:T(8,128)(2,1)S(1)}, u32[]{:S(2)}, u32[]{:S(2)}) collective-permute-start(bf16[48,1152]{1,0:T(8,128)(2,1)S(1)} %get-tuple-element.41), channel_id=1, source_target_pairs={{0,16},{16,0},{1,17},{17,1},{2,18},{18,2},{3,19},{19,3},{4,20},{20... | collective-permute-start | bytes 331784 | tf_op jit(solution)/shard_map/ppermute | solution.py:565
  45.3 4.0 %collective-permute-start.12 = (bf16[2768,128]{1,0:T(8,128)(2,1)S(1)}, bf16[2768,128]{1,0:T(8,128)(2,1)S(1)}, u32[]{:S(2)}, u32[]{:S(2)}) collective-permute-start(bf16[2768,128]{1,0:T(8,128)(2,1)S(1)} %get-tuple-element.44.gate_ref), channel_id=1, source_target_pairs={{0,1},{1,0},{2,3},{3,2},{4,5},{5,4},{6,7},{7,6},{8,9},{9,8},{10,11... | collective-permute-start | bytes 2125832 | tf_op jit(solution)/shard_map/ppermute | solution.py:595
  47.7 2.9 %collective-permute-start.13 = (bf16[2064,128]{1,0:T(8,128)(2,1)S(1)}, bf16[2064,128]{1,0:T(8,128)(2,1)S(1)}, u32[]{:S(2)}, u32[]{:S(2)}) collective-permute-start(bf16[2064,128]{1,0:T(8,128)(2,1)S(1)} %up.2.up_ref), channel_id=1, source_target_pairs={{0,1},{1,0},{2,3},{3,2},{4,5},{5,4},{6,7},{7,6},{8,9},{9,8},{10,11... | collective-permute-start | bytes 1585160 | tf_op jit(solution)/shard_map/ppermute | solution.py:596
  49.2 1.5 %collective-permute-start.14 = (bf16[688,128]{1,0:T(8,128)(2,1)S(1)}, bf16[688,128]{1,0:T(8,128)(2,1)S(1)}, u32[]{:S(2)}, u32[]{:S(2)}) collective-permute-start(bf16[688,128]{1,0:T(8,128)(2,1)S(1)} %up.3.up_late_ref), channel_id=1, source_target_pairs={{0,1},{1,0},{2,3},{3,2},{4,5},{5,4},{6,7},{7,6},{8,9},{9,8},{10,11... | collective-permute-start | bytes 528392 | tf_op jit(solution)/shard_map/ppermute | solution.py:596
  52.9 6.2 %collective-permute-start.15 = (bf16[48,1024]{1,0:T(8,128)(2,1)S(1)}, bf16[48,1024]{1,0:T(8,128)(2,1)S(1)}, u32[]{:S(2)}, u32[]{:S(2)}) collective-permute-start(bf16[48,1024]{1,0:T(8,128)(2,1)S(1)} %get-tuple-element.49), channel_id=1, source_target_pairs={{0,18},{2,16},{16,2},{18,0},{1,19},{3,17},{17,3},{19,1},{4,22},{6,... | collective-permute-start | bytes 294920 | tf_op jit(solution)/shard_map/ppermute | solution.py:614
  55.2 5.0 %collective-permute-start.16 = (bf16[48,1024]{1,0:T(8,128)(2,1)S(1)}, bf16[48,1024]{1,0:T(8,128)(2,1)S(1)}, u32[]{:S(2)}, u32[]{:S(2)}) collective-permute-start(bf16[48,1024]{1,0:T(8,128)(2,1)S(1)} %get-tuple-element.50), channel_id=1, source_target_pairs={{0,2},{2,0},{1,3},{3,1},{4,6},{6,4},{5,7},{7,5},{8,10},{10,8},{9,1... | collective-permute-start | bytes 294920 | tf_op jit(solution)/shard_map/ppermute | solution.py:616
  55.2 5.6 %collective-permute-start.17 = (bf16[48,1024]{1,0:T(8,128)(2,1)S(1)}, bf16[48,1024]{1,0:T(8,128)(2,1)S(1)}, u32[]{:S(2)}, u32[]{:S(2)}) collective-permute-start(bf16[48,1024]{1,0:T(8,128)(2,1)S(1)} %get-tuple-element.51), channel_id=1, source_target_pairs={{0,16},{16,0},{1,17},{17,1},{2,18},{18,2},{3,19},{19,3},{4,20},{20... | collective-permute-start | bytes 294920 | tf_op jit(solution)/shard_map/ppermute | solution.py:615
  61.0 4.5 %collective-permute-start.18 = (bf16[32,1024]{1,0:T(8,128)(2,1)S(1)}, bf16[32,1024]{1,0:T(8,128)(2,1)S(1)}, u32[]{:S(2)}, u32[]{:S(2)}) collective-permute-start(bf16[32,1024]{1,0:T(8,128)(2,1)S(1)} %get-tuple-element.54), channel_id=1, source_target_pairs={{0,4},{4,0},{8,12},{12,8},{1,5},{5,1},{9,13},{13,9},{2,6},{6,2},{1... | collective-permute-start | bytes 196616 | tf_op jit(solution)/shard_map/ppermute | solution.py:624
  62.5 7.9 %collective-permute-start.19 = (bf16[32,1024]{1,0:T(8,128)(2,1)S(1)}, bf16[32,1024]{1,0:T(8,128)(2,1)S(1)}, u32[]{:S(2)}, u32[]{:S(2)}) collective-permute-start(bf16[32,1024]{1,0:T(8,128)(2,1)S(1)} %get-tuple-element.55), channel_id=1, source_target_pairs={{0,8},{4,12},{8,0},{12,4},{1,9},{5,13},{9,1},{13,5},{2,10},{6,14},... | collective-permute-start | bytes 196616 | tf_op jit(solution)/shard_map/ppermute | solution.py:624
  63.6 6.8 %collective-permute-start.20 = (bf16[32,1024]{1,0:T(8,128)(2,1)S(1)}, bf16[32,1024]{1,0:T(8,128)(2,1)S(1)}, u32[]{:S(2)}, u32[]{:S(2)}) collective-permute-start(bf16[32,1024]{1,0:T(8,128)(2,1)S(1)} %get-tuple-element.56), channel_id=1, source_target_pairs={{0,12},{4,8},{8,4},{12,0},{1,13},{5,9},{9,5},{13,1},{2,14},{6,10},... | collective-permute-start | bytes 196616 | tf_op jit(solution)/shard_map/ppermute | solution.py:624

commit v10 on v9

--- a/solution.py
+++ b/solution.py
@@ -432,30 +432,34 @@
                 far_out[...] = value[half : 2 * half]
 
 
-def merge_kernel(zero_ref, three_ref, two_ref, one_ref, side_far_ref, side_ref, far_ref, kept_ref, *out_refs):
+def merge_kernel(zero_ref, three_ref, two_ref, one_ref, kept_ref, other_ref, *out_refs):
     columns = kept_ref.shape[1]
     capacity = zero_ref.shape[0] // 2
     matches, found = places((zero_ref, one_ref, two_ref, three_ref), columns)
     for out_ref, match, place in zip(out_refs, matches, found):
         span = pl.ds(pl.multiple_of(place * capacity, capacity), capacity)
-        for wanted, (first_ref, second_ref) in ((True, (kept_ref, far_ref)), (False, (side_ref, side_far_ref))):
+        for wanted, source_ref in ((True, kept_ref), (False, other_ref)):
 
             @pl.when(match == wanted)
             def _():
-                out_ref[:capacity, :] = first_ref[span, :]
-                out_ref[capacity:, :] = second_ref[span, :]
-
-
-def scatter_kernel(pick_ref, zero_ref, one_ref, two_ref, three_ref, out_hbm, out_ref, semaphores):
+                out_ref[...] = source_ref[span, :]
+
+
+def scatter_kernel(pick_ref, *refs):
+    halves, (out_hbm, out_ref, semaphores) = (refs[:4], refs[4:8]), refs[8:]
     columns = out_ref.shape[1]
     pieces = semaphores.shape[0]
     width = columns // pieces
     copies = []
     for n in range(pieces):
         span = slice(n * width, (n + 1) * width)
-        total = zero_ref[:, span].astype(jnp.float32)
-        for got_ref in (three_ref, two_ref, one_ref):
-            total = total + got_ref[:, span].astype(jnp.float32)
+        totals = []
+        for half in halves:
+            total = half[0][:, span].astype(jnp.float32)
+            for got_ref in half[1:]:
+                total = total + got_ref[:, span].astype(jnp.float32)
+            totals.append(total)
+        total = jnp.concatenate(totals, axis=0)
         result = 0.0
         for piece in split_high_low(total)[::-1]:
             result = result + lax.dot_general(
@@ -611,21 +615,23 @@
         scratch=[pltpu.VMEM((units, rows), jnp.bfloat16)],
         flops=flops,
     )
+    from_side = lax.ppermute(to_side, "mod", SWAP)
     from_side_far = lax.ppermute(to_side_far, both_axes, crossed(2, 3))
     from_far = lax.ppermute(to_far, "groups", SWAP)
-    from_side = lax.ppermute(to_side, "mod", SWAP)
-    merged = call(
-        merge_kernel,
-        "merge",
-        [array(slots, columns)] * 4,
-        [ON_CHIP] * 8,
-        [packed, *others[::-1], from_side_far, from_side, from_far, kept],
-    )
-    values = [merged[0]] + [lax.ppermute(merged[v], "tok", crossed(2, v)) for v in (1, 2, 3)]
+    values = []
+    for mine, got, name in ((kept, from_side, "merge_first"), (from_far, from_side_far, "merge_second")):
+        merged = call(
+            merge_kernel,
+            name,
+            [array(capacity, columns)] * 4,
+            [ON_CHIP] * 6,
+            [packed, *others[::-1], mine, got],
+        )
+        values += [merged[0]] + [lax.ppermute(merged[v], "tok", crossed(2, v)) for v in (1, 2, 3)]
     return pl.pallas_call(
         scatter_kernel,
         out_shape=pltpu.HBM((tokens, columns), jnp.bfloat16),
-        in_specs=[ON_CHIP] * 5,
+        in_specs=[ON_CHIP] * 9,
         out_specs=IN_HBM,
         scratch_shapes=[pltpu.VMEM((tokens, columns), jnp.bfloat16), pltpu.SemaphoreType.DMA((4,))],
         compiler_params=pltpu.CompilerParams(vmem_limit_bytes=8 << 20),

time: 71.6 us -> 72.3 us (level)
  starting transfers between devices: 28.6 us -> 33.1 us
  waiting for transfers between devices: 15.9 us -> 11.8 us
    ppermute x3 -> x6, starting transfers between devices: 4.45 us -> 8.9 us  [paired_local(): lax.ppermute(merged[v], 'tok', crossed(2, v))]
    ppermute x1, waiting for transfers between devices: 2.62 us -> 0.01 us  [paired_local(): from_side_far = lax.ppermute(to_side_far, both_axes, crossed(2, 3))]
    ppermute x1, starting transfers between devices: 0.01 us -> 2.1 us  [paired_local(): from_side = lax.ppermute(to_side, 'mod', SWAP)]
    ppermute x1, starting transfers between devices: 2.3 us -> 0.77 us  [paired_local(): from_side_far = lax.ppermute(to_side_far, both_axes, crossed(2, 3))]
    ppermute x3 -> x6, waiting for transfers between devices: 4.96 us -> 3.68 us  [paired_local(): lax.ppermute(merged[v], 'tok', crossed(2, v))]
    pallas_call x15 -> x16, Pallas kernels: 25.8 us -> 25.9 us  [call(): pl.pallas_call(kernel, out_shape=outs, in_specs=specs, out_specs=jax.tree...]
  transfers between devices with their start and end apart: 21 -> 24, of which waited for: 11 -> 10; matrix products, arithmetic and copies ran while one was open for 0% -> 0% of each run, Pallas kernels for 26% -> 26%
where the time goes in v10:
time: 72.3 us; the launch traced here: 72.1 us
  starting transfers between devices  33.1 us (46%)
  Pallas kernels  26.9 us (37%)
  waiting for transfers between devices  11.8 us (16%)
    pallas_call x16, Pallas kernels, call(): pl.pallas_call(kernel, out_shape=outs, in_specs=specs, out_specs=jax.tree...  25.9 us
    ppermute x6, starting transfers between devices, paired_local(): lax.ppermute(merged[v], 'tok', crossed(2, v))  8.9 us
    ppermute x3, starting transfers between devices, paired_local(): lax.ppermute(partial[v], 'tok', crossed(2, v))  6.44 us
    ppermute x3, starting transfers between devices, paired_local(): lax.ppermute(packed, 'tok', crossed(2, v))  4.42 us
    ppermute x6, waiting for transfers between devices, paired_local(): lax.ppermute(merged[v], 'tok', crossed(2, v))  3.68 us
    ppermute x1, starting transfers between devices, paired_local(): side_far = lax.ppermute(to_corner_rows, both_axes, crossed(2, 3))  3.24 us
    ppermute x1, starting transfers between devices, paired_local(): across = lax.ppermute(picked, plane, to_second)  2.99 us
    ppermute x3, waiting for transfers between devices, paired_local(): lax.ppermute(partial[v], 'tok', crossed(2, v))  2.35 us
  transfers between devices with their start and end apart: 24, of which 10 were waited for; matrix products, arithmetic and copies ran while one was open for 0% of the time, Pallas kernels for 26%

profile of v10, /device:TPU:0, one launch (start us, length us, event | category | flops | bytes accessed | tf_op | source)
XLA Modules:
  0.0 72.1 jit_solution(10606659407310724115)
XLA Ops:
  0.0 1.1 %select.1 = (bf16[32,1024]{1,0:T(8,128)(2,1)S(1)}, bf16[32,128]{1,0:T(8,128)(2,1)S(1)}, f32[8,128]{1,0:T(8,128)S(1)}) custom-call(s32[4,16]{1,0:T(4,128)} %rows_hbm.1, bf16[128,1024]{1,0:T(8,128)(2,1)} %context_hbm.1), custom_call_target="tpu_custom_call" | custom-call | tf_op jit(solution)/shard_map/select/pallas_call | solution.py:173
  1.1 3.0 %collective-permute-start.1 = (bf16[32,1024]{1,0:T(8,128)(2,1)S(1)}, bf16[32,1024]{1,0:T(8,128)(2,1)S(1)}, u32[]{:S(2)}, u32[]{:S(2)}) collective-permute-start(bf16[32,1024]{1,0:T(8,128)(2,1)S(1)} %get-tuple-element.38), channel_id=1, source_target_pairs={{0,2},{1,6},{2,10},{3,14},{4,3},{5,7},{6,11},{7,15},{8,0},{9,4},{1... | collective-permute-start | bytes 196616 | tf_op jit(solution)/shard_map/ppermute | solution.py:510
  4.1 0.7 collective-permute-start
  4.8 3.6 %keep_gate.1 = (bf16[1600,2048]{1,0:T(8,128)(2,1)S(1)}, bf16[1024,1024]{1,0:T(8,128)(2,1)S(1)}, f32[32,1024]{1,0:T(8,128)S(1)}) custom-call(bf16[32,128]{1,0:T(8,128)(2,1)S(1)} %get-tuple-element.35.pick_ref, bf16[128,1024]{1,0:T(8,128)(2,1)} %residual_hbm.1, bf16[2,2752,2048]{2,1,0:T(8,128)(2,1)} %bitcast.10, bf16[1024,1024]{1,0:T(8,128)(2,1)} %proj_ref.1), custom_call_target="tpu_custom_call" | custom-call | bytes 5636096 | tf_op jit(solution)/shard_map/keep_gate/pallas_call | solution.py:173
  8.4 1.0 %collective-permute-done.1.across_ref = bf16[32,1024]{1,0:T(8,128)(2,1)S(1)} collective-permute-done((bf16[32,1024]{1,0:T(8,128)(2,1)S(1)}, bf16[32,1024]{1,0:T(8,128)(2,1)S(1)}, u32[]{:S(2)}, u32[]{:S(2)}) %collective-permute-start.1) | collective-permute-done | bytes 65568 | tf_op jit(solution)/shard_map/ppermute | solution.py:510
  9.5 1.4 %collective-permute-start.2 = (bf16[64,1024]{1,0:T(8,128)(2,1)S(1)}, bf16[64,1024]{1,0:T(8,128)(2,1)S(1)}, u32[]{:S(2)}, u32[]{:S(2)}) collective-permute-start(bf16[64,1024]{1,0:T(8,128)(2,1)S(1)} %join.1.joined_ref), channel_id=1, source_target_pairs={{0,1},{1,0},{2,3},{3,2},{4,5},{5,4},{6,7},{7,6},{8,9},{9,8},{10,11... | collective-permute-start | bytes 393224 | tf_op jit(solution)/shard_map/ppermute | solution.py:528
  10.9 1.0 %collective-permute-done.2.other_ref = bf16[64,1024]{1,0:T(8,128)(2,1)S(1)} collective-permute-done((bf16[64,1024]{1,0:T(8,128)(2,1)S(1)}, bf16[64,1024]{1,0:T(8,128)(2,1)S(1)}, u32[]{:S(2)}, u32[]{:S(2)}) %collective-permute-start.2) | collective-permute-done | bytes 131104 | tf_op jit(solution)/shard_map/ppermute | solution.py:528
  11.9 0.4 project.1.after_ref.partial_ref
  12.4 2.0 %collective-permute-start.5 = (bf16[32,1024]{1,0:T(8,128)(2,1)S(1)}, bf16[32,1024]{1,0:T(8,128)(2,1)S(1)}, u32[]{:S(2)}, u32[]{:S(2)}) collective-permute-start(bf16[32,1024]{1,0:T(8,128)(2,1)S(1)} %get-tuple-element.65), channel_id=1, source_target_pairs={{0,4},{4,0},{8,12},{12,8},{1,5},{5,1},{9,13},{13,9},{2,6},{6,2},{1... | collective-permute-start | bytes 196616 | tf_op jit(solution)/shard_map/ppermute | solution.py:537
  14.4 4.4 %collective-permute-start.4 = (bf16[32,1024]{1,0:T(8,128)(2,1)S(1)}, bf16[32,1024]{1,0:T(8,128)(2,1)S(1)}, u32[]{:S(2)}, u32[]{:S(2)}) collective-permute-start(bf16[32,1024]{1,0:T(8,128)(2,1)S(1)} %get-tuple-element.66), channel_id=1, source_target_pairs={{0,8},{4,12},{8,0},{12,4},{1,9},{5,13},{9,1},{13,5},{2,10},{6,14},... | collective-permute-start | bytes 196616 | tf_op jit(solution)/shard_map/ppermute | solution.py:537
  18.8 3.8 %keep_more.1 = (bf16[1152,2048]{1,0:T(8,128)(2,1)S(1)}, bf16[1136,2048]{1,0:T(8,128)(2,1)S(1)}) custom-call(bf16[4,32,1024]{2,1,0:T(8,128)(2,1)S(1)} %project.1.after_ref.partial_ref, bf16[2,2752,2048]{2,1,0:T(8,128)(2,1)} %bitcast.11, bf16[2,2752,2048]{2,1,0:T(8,128)(2,1)} %bitcast.12), custom_call_target="tpu_custom_call" | custom-call | bytes 9371648 | tf_op jit(solution)/shard_map/keep_more/pallas_call | solution.py:173
  22.6 0.2 collective-permute-done.4.two_ref
  22.9 2.1 %collective-permute-done.3.three_ref = bf16[32,1024]{1,0:T(8,128)(2,1)S(1)} collective-permute-done((bf16[32,1024]{1,0:T(8,128)(2,1)S(1)}, bf16[32,1024]{1,0:T(8,128)(2,1)S(1)}, u32[]{:S(2)}, u32[]{:S(2)}) %collective-permute-start.3) | collective-permute-done | bytes 65568 | tf_op jit(solution)/shard_map/ppermute | solution.py:537
  25.0 0.2 norm.1.after_ref.zero_ref
  25.2 0.8 %collective-permute-start.8 = (bf16[32,1152]{1,0:T(8,128)(2,1)S(1)}, bf16[32,1152]{1,0:T(8,128)(2,1)S(1)}, u32[]{:S(2)}, u32[]{:S(2)}) collective-permute-start(bf16[32,1152]{1,0:T(8,128)(2,1)S(1)} %norm.1.after_ref.zero_ref), channel_id=1, source_target_pairs={{0,4},{4,0},{8,12},{12,8},{1,5},{5,1},{9,13},{13,9},{2,6},{6,2},{1... | collective-permute-start | bytes 221192 | tf_op jit(solution)/shard_map/ppermute | solution.py:552
  26.0 1.7 %collective-permute-start.7 = (bf16[32,1152]{1,0:T(8,128)(2,1)S(1)}, bf16[32,1152]{1,0:T(8,128)(2,1)S(1)}, u32[]{:S(2)}, u32[]{:S(2)}) collective-permute-start(bf16[32,1152]{1,0:T(8,128)(2,1)S(1)} %norm.1.after_ref.zero_ref), channel_id=1, source_target_pairs={{0,8},{4,12},{8,0},{12,4},{1,9},{5,13},{9,1},{13,5},{2,10},{6,14},... | collective-permute-start | bytes 221192 | tf_op jit(solution)/shard_map/ppermute | solution.py:552
  27.7 1.9 %collective-permute-start.6 = (bf16[32,1152]{1,0:T(8,128)(2,1)S(1)}, bf16[32,1152]{1,0:T(8,128)(2,1)S(1)}, u32[]{:S(2)}, u32[]{:S(2)}) collective-permute-start(bf16[32,1152]{1,0:T(8,128)(2,1)S(1)} %norm.1.after_ref.zero_ref), channel_id=1, source_target_pairs={{0,12},{4,8},{8,4},{12,0},{1,13},{5,9},{9,5},{13,1},{2,14},{6,10},... | collective-permute-start | bytes 221192 | tf_op jit(solution)/shard_map/ppermute | solution.py:552
  29.7 3.7 %keep_up.1 = (bf16[1616,2048]{1,0:T(8,128)(2,1)S(1)}, bf16[656,2048]{1,0:T(8,128)(2,1)S(1)}) custom-call(bf16[32,1152]{1,0:T(8,128)(2,1)S(1)} %norm.1.after_ref.zero_ref, bf16[2,2752,2048]{2,1,0:T(8,128)(2,1)} %bitcast.13, bf16[2,2752,2048]{2,1,0:T(8,128)(2,1)} %refs_0_.1), custom_call_target="tpu_custom_call" | custom-call | bytes 9306112 | tf_op jit(solution)/shard_map/keep_up/pallas_call | solution.py:173
  33.4 0.6 collective-permute-done.6.three_ref
  34.0 0.2 arrange.1
  34.2 3.2 %collective-permute-start.9 = (bf16[48,1152]{1,0:T(8,128)(2,1)S(1)}, bf16[48,1152]{1,0:T(8,128)(2,1)S(1)}, u32[]{:S(2)}, u32[]{:S(2)}) collective-permute-start(bf16[48,1152]{1,0:T(8,128)(2,1)S(1)} %get-tuple-element.43), channel_id=1, source_target_pairs={{0,18},{2,16},{16,2},{18,0},{1,19},{3,17},{17,3},{19,1},{4,22},{6,... | collective-permute-start | bytes 331784 | tf_op jit(solution)/shard_map/ppermute | solution.py:568
  37.4 0.6 collective-permute-start.11
  38.0 3.4 %keep_down.1.refs_2_.second_ref = bf16[2096,2048]{1,0:T(8,128)(2,1)S(1)} custom-call(bf16[48,1152]{1,0:T(8,128)(2,1)S(1)} %get-tuple-element.46.after_ref.own_ref, bf16[2,2752,2048]{2,1,0:T(8,128)(2,1)} %refs_0_.1), custom_call_target="tpu_custom_call" | custom-call | bytes 8585216 | tf_op jit(solution)/shard_map/keep_down/pallas_call | solution.py:173
  41.5 0.6 collective-permute-done.10.side_own_ref
  42.2 3.1 %gate.1 = (bf16[2768,128]{1,0:T(8,128)(2,1)S(1)}, bf16[128,2048]{1,0:T(8,128)(2,1)S(1)}) custom-call(bf16[48,1152]{1,0:T(8,128)(2,1)S(1)} %collective-permute-done.9.side_far_ref, bf16[48,1152]{1,0:T(8,128)(2,1)S(1)} %collective-permute-done.10.side_own_ref, bf16[48,1152]{1,0:T(8,128)(2,1)S(1)} %collective-permute-done.11.far_ref, ...), custom_call_target="tpu_custom_call" | custom-call | flops 1442840576 | tf_op jit(solution)/shard_map/gate/pallas_call | solution.py:173
  45.3 0.1 collective-permute-start.12
  45.3 2.3 %up.2.up_ref = bf16[2064,128]{1,0:T(8,128)(2,1)S(1)} custom-call(bf16[128,2048]{1,0:T(8,128)(2,1)S(1)} %get-tuple-element.51.rows_ref, bf16[1136,2048]{1,0:T(8,128)(2,1)S(1)} %get-tuple-element.41._.refs_0_, bf16[1616,2048]{1,0:T(8,128)(2,1)S(1)} %get-tuple-element.42._.refs_1_.refs_0_), custom_call_target="tpu_custom_call" | custom-call | flops 1082130432 | tf_op jit(solution)/shard_map/up/pallas_call | solution.py:173
  47.7 0.6 collective-permute-start.13
  48.3 0.9 %up.3.up_late_ref = bf16[688,128]{1,0:T(8,128)(2,1)S(1)} custom-call(bf16[128,2048]{1,0:T(8,128)(2,1)S(1)} %get-tuple-element.51.rows_ref, bf16[1616,2048]{1,0:T(8,128)(2,1)S(1)} %get-tuple-element.42._.refs_1_.refs_0_), custom_call_target="tpu_custom_call" | custom-call | flops 360710144 | tf_op jit(solution)/shard_map/up/pallas_call | solution.py:173
  49.2 0.1 collective-permute-start.14
  49.3 0.5 silu.1
  49.8 0.9 %collective-permute-done.14.other_late_ref = bf16[688,128]{1,0:T(8,128)(2,1)S(1)} collective-permute-done((bf16[688,128]{1,0:T(8,128)(2,1)S(1)}, bf16[688,128]{1,0:T(8,128)(2,1)S(1)}, u32[]{:S(2)}, u32[]{:S(2)}) %collective-permute-start.14) | collective-permute-done | bytes 176160 | tf_op jit(solution)/shard_map/ppermute | solution.py:600
  50.6 2.2 %down.1 = (bf16[48,1024]{1,0:T(8,128)(2,1)S(1)}, bf16[48,1024]{1,0:T(8,128)(2,1)S(1)}, bf16[48,1024]{1,0:T(8,128)(2,1)S(1)}, bf16[48,1024]{1,0:T(8,128)(2,1)S(1)}) custom-call(f32[2752,128]{1,0:T(8,128)S(1)} %get-tuple-element.49.silu_ref, f32[8,128]{1,0:T(8,128)S(1)} %get-tuple-element.50.stat_ref, bf16[2064,128]{1,0:T(8,128)(2,1)S(1)} %up.2.up_ref, ...), custom_call_target="tpu_custom_call" | custom-call | flops 1442840576 | tf_op jit(solution)/shard_map/down/pallas_call | solution.py:173
  52.9 2.1 %collective-permute-start.15 = (bf16[48,1024]{1,0:T(8,128)(2,1)S(1)}, bf16[48,1024]{1,0:T(8,128)(2,1)S(1)}, u32[]{:S(2)}, u32[]{:S(2)}) collective-permute-start(bf16[48,1024]{1,0:T(8,128)(2,1)S(1)} %get-tuple-element.54), channel_id=1, source_target_pairs={{0,2},{2,0},{1,3},{3,1},{4,6},{6,4},{5,7},{7,5},{8,10},{10,8},{9,1... | collective-permute-start | bytes 294920 | tf_op jit(solution)/shard_map/ppermute | solution.py:618
  55.0 0.8 %collective-permute-start.19 = (bf16[48,1024]{1,0:T(8,128)(2,1)S(1)}, bf16[48,1024]{1,0:T(8,128)(2,1)S(1)}, u32[]{:S(2)}, u32[]{:S(2)}) collective-permute-start(bf16[48,1024]{1,0:T(8,128)(2,1)S(1)} %get-tuple-element.59), channel_id=1, source_target_pairs={{0,16},{16,0},{1,17},{17,1},{2,18},{18,2},{3,19},{19,3},{4,20},{20... | collective-permute-start | bytes 294920 | tf_op jit(solution)/shard_map/ppermute | solution.py:620
  55.8 0.8 %collective-permute-start.20 = (bf16[48,1024]{1,0:T(8,128)(2,1)S(1)}, bf16[48,1024]{1,0:T(8,128)(2,1)S(1)}, u32[]{:S(2)}, u32[]{:S(2)}) collective-permute-start(bf16[48,1024]{1,0:T(8,128)(2,1)S(1)} %get-tuple-element.60), channel_id=1, source_target_pairs={{0,18},{2,16},{16,2},{18,0},{1,19},{3,17},{17,3},{19,1},{4,22},{6,... | collective-permute-start | bytes 294920 | tf_op jit(solution)/shard_map/ppermute | solution.py:619
  56.5 1.6 %collective-permute-done.15.other_ref = bf16[48,1024]{1,0:T(8,128)(2,1)S(1)} collective-permute-done((bf16[48,1024]{1,0:T(8,128)(2,1)S(1)}, bf16[48,1024]{1,0:T(8,128)(2,1)S(1)}, u32[]{:S(2)}, u32[]{:S(2)}) %collective-permute-start.15) | collective-permute-done | bytes 98336 | tf_op jit(solution)/shard_map/ppermute | solution.py:618
  58.2 0.1 merge_first.1
  58.3 1.4 %collective-permute-start.16 = (bf16[16,1024]{1,0:T(8,128)(2,1)S(1)}, bf16[16,1024]{1,0:T(8,128)(2,1)S(1)}, u32[]{:S(2)}, u32[]{:S(2)}) collective-permute-start(bf16[16,1024]{1,0:T(8,128)(2,1)S(1)} %get-tuple-element.56), channel_id=1, source_target_pairs={{0,4},{4,0},{8,12},{12,8},{1,5},{5,1},{9,13},{13,9},{2,6},{6,2},{1... | collective-permute-start | bytes 98312 | tf_op jit(solution)/shard_map/ppermute | solution.py:630
  59.7 1.0 %collective-permute-start.17 = (bf16[16,1024]{1,0:T(8,128)(2,1)S(1)}, bf16[16,1024]{1,0:T(8,128)(2,1)S(1)}, u32[]{:S(2)}, u32[]{:S(2)}) collective-permute-start(bf16[16,1024]{1,0:T(8,128)(2,1)S(1)} %get-tuple-element.57), channel_id=1, source_target_pairs={{0,8},{4,12},{8,0},{12,4},{1,9},{5,13},{9,1},{13,5},{2,10},{6,14},... | collective-permute-start | bytes 98312 | tf_op jit(solution)/shard_map/ppermute | solution.py:630
  60.7 2.0 %collective-permute-start.18 = (bf16[16,1024]{1,0:T(8,128)(2,1)S(1)}, bf16[16,1024]{1,0:T(8,128)(2,1)S(1)}, u32[]{:S(2)}, u32[]{:S(2)}) collective-permute-start(bf16[16,1024]{1,0:T(8,128)(2,1)S(1)} %get-tuple-element.58), channel_id=1, source_target_pairs={{0,12},{4,8},{8,4},{12,0},{1,13},{5,9},{9,5},{13,1},{2,14},{6,10},... | collective-permute-start | bytes 98312 | tf_op jit(solution)/shard_map/ppermute | solution.py:630
  62.8 0.2 merge_second.1
  62.9 0.5 collective-permute-start.21
  63.5 1.9 %collective-permute-start.22 = (bf16[16,1024]{1,0:T(8,128)(2,1)S(1)}, bf16[16,1024]{1,0:T(8,128)(2,1)S(1)}, u32[]{:S(2)}, u32[]{:S(2)}) collective-permute-start(bf16[16,1024]{1,0:T(8,128)(2,1)S(1)} %get-tuple-element.63), channel_id=1, source_target_pairs={{0,8},{4,12},{8,0},{12,4},{1,9},{5,13},{9,1},{13,5},{2,10},{6,14},... | collective-permute-start | bytes 98312 | tf_op jit(solution)/shard_map/ppermute | solution.py:630
  65.4 2.0 %collective-permute-start.23 = (bf16[16,1024]{1,0:T(8,128)(2,1)S(1)}, bf16[16,1024]{1,0:T(8,128)(2,1)S(1)}, u32[]{:S(2)}, u32[]{:S(2)}) collective-permute-start(bf16[16,1024]{1,0:T(8,128)(2,1)S(1)} %get-tuple-element.64), channel_id=1, source_target_pairs={{0,12},{4,8},{8,4},{12,0},{1,13},{5,9},{9,5},{13,1},{2,14},{6,10},... | collective-permute-start | bytes 98312 | tf_op jit(solution)/shard_map/ppermute | solution.py:630
  67.4 1.0 %collective-permute-done.22.refs_6_ = bf16[16,1024]{1,0:T(8,128)(2,1)S(1)} collective-permute-done((bf16[16,1024]{1,0:T(8,128)(2,1)S(1)}, bf16[16,1024]{1,0:T(8,128)(2,1)S(1)}, u32[]{:S(2)}, u32[]{:S(2)}) %collective-permute-start.22) | collective-permute-done | bytes 32800 | tf_op jit(solution)/shard_map/ppermute | solution.py:630
  68.4 2.7 %collective-permute-done.23.refs_7_ = bf16[16,1024]{1,0:T(8,128)(2,1)S(1)} collective-permute-done((bf16[16,1024]{1,0:T(8,128)(2,1)S(1)}, bf16[16,1024]{1,0:T(8,128)(2,1)S(1)}, u32[]{:S(2)}, u32[]{:S(2)}) %collective-permute-start.23) | collective-permute-done | bytes 32800 | tf_op jit(solution)/shard_map/ppermute | solution.py:630
  71.1 1.0 %scatter.1 = bf16[128,1024]{1,0:T(8,128)(2,1)} custom-call(bf16[32,128]{1,0:T(8,128)(2,1)S(1)} %get-tuple-element.35.pick_ref, bf16[16,1024]{1,0:T(8,128)(2,1)S(1)} %get-tuple-element.55.refs_0_, bf16[16,1024]{1,0:T(8,128)(2,1)S(1)} %collective-permute-done.16.refs_1_, bf16[16,1024]{1,0:T(8,128)(2,1)S(1)} %collective-permute-done.17.refs_2_, ...), custom_call_target="tpu_custom_call" | custom-call | tf_op jit(solution)/shard_map/scatter/pallas_call | solution.py:631
  (22 shorter events, 0.1 us)
Async XLA Ops:
  1.1 8.3 %collective-permute-start.1 = (bf16[32,1024]{1,0:T(8,128)(2,1)S(1)}, bf16[32,1024]{1,0:T(8,128)(2,1)S(1)}, u32[]{:S(2)}, u32[]{:S(2)}) collective-permute-start(bf16[32,1024]{1,0:T(8,128)(2,1)S(1)} %get-tuple-element.38), channel_id=1, source_target_pairs={{0,2},{1,6},{2,10},{3,14},{4,3},{5,7},{6,11},{7,15},{8,0},{9,4},{1... | collective-permute-start | bytes 196616 | tf_op jit(solution)/shard_map/ppermute | solution.py:510
  4.1 5.3 %collective-permute-start = (bf16[32,1024]{1,0:T(8,128)(2,1)S(1)}, bf16[32,1024]{1,0:T(8,128)(2,1)S(1)}, u32[]{:S(2)}, u32[]{:S(2)}) collective-permute-start(bf16[32,1024]{1,0:T(8,128)(2,1)S(1)} %get-tuple-element.38), channel_id=1, source_target_pairs={{0,0},{1,4},{2,8},{3,12},{4,1},{5,5},{6,9},{7,13},{8,2},{9,6},{10,... | collective-permute-start | bytes 196616 | tf_op jit(solution)/shard_map/ppermute | solution.py:511
  9.5 2.4 %collective-permute-start.2 = (bf16[64,1024]{1,0:T(8,128)(2,1)S(1)}, bf16[64,1024]{1,0:T(8,128)(2,1)S(1)}, u32[]{:S(2)}, u32[]{:S(2)}) collective-permute-start(bf16[64,1024]{1,0:T(8,128)(2,1)S(1)} %join.1.joined_ref), channel_id=1, source_target_pairs={{0,1},{1,0},{2,3},{3,2},{4,5},{5,4},{6,7},{7,6},{8,9},{9,8},{10,11... | collective-permute-start | bytes 393224 | tf_op jit(solution)/shard_map/ppermute | solution.py:528
  12.4 10.2 %collective-permute-start.5 = (bf16[32,1024]{1,0:T(8,128)(2,1)S(1)}, bf16[32,1024]{1,0:T(8,128)(2,1)S(1)}, u32[]{:S(2)}, u32[]{:S(2)}) collective-permute-start(bf16[32,1024]{1,0:T(8,128)(2,1)S(1)} %get-tuple-element.65), channel_id=1, source_target_pairs={{0,4},{4,0},{8,12},{12,8},{1,5},{5,1},{9,13},{13,9},{2,6},{6,2},{1... | collective-permute-start | bytes 196616 | tf_op jit(solution)/shard_map/ppermute | solution.py:537
  14.4 8.4 %collective-permute-start.4 = (bf16[32,1024]{1,0:T(8,128)(2,1)S(1)}, bf16[32,1024]{1,0:T(8,128)(2,1)S(1)}, u32[]{:S(2)}, u32[]{:S(2)}) collective-permute-start(bf16[32,1024]{1,0:T(8,128)(2,1)S(1)} %get-tuple-element.66), channel_id=1, source_target_pairs={{0,8},{4,12},{8,0},{12,4},{1,9},{5,13},{9,1},{13,5},{2,10},{6,14},... | collective-permute-start | bytes 196616 | tf_op jit(solution)/shard_map/ppermute | solution.py:537
  18.8 6.2 %collective-permute-start.3 = (bf16[32,1024]{1,0:T(8,128)(2,1)S(1)}, bf16[32,1024]{1,0:T(8,128)(2,1)S(1)}, u32[]{:S(2)}, u32[]{:S(2)}) collective-permute-start(bf16[32,1024]{1,0:T(8,128)(2,1)S(1)} %get-tuple-element.67), channel_id=1, source_target_pairs={{0,12},{4,8},{8,4},{12,0},{1,13},{5,9},{9,5},{13,1},{2,14},{6,10},... | collective-permute-start | bytes 196616 | tf_op jit(solution)/shard_map/ppermute | solution.py:537
  18.8 6.2 %copy-start = (bf16[1024,4]{0,1:T(4,128)(2,1)S(1)}, bf16[1024,4]{0,1:T(4,128)(2,1)}, u32[]{:S(2)}) copy-start(bf16[1024,4]{0,1:T(4,128)(2,1)} %param.14) | copy-start | bytes 24580
  18.8 6.2 %copy-start.1 = (bf16[2,1024]{1,0:T(2,128)(2,1)S(1)}, bf16[2,1024]{1,0:T(2,128)(2,1)}, u32[]{:S(2)}) copy-start(bf16[2,1024]{1,0:T(2,128)(2,1)} %gain_ref.1) | copy-start | bytes 12292
  25.2 8.1 %collective-permute-start.8 = (bf16[32,1152]{1,0:T(8,128)(2,1)S(1)}, bf16[32,1152]{1,0:T(8,128)(2,1)S(1)}, u32[]{:S(2)}, u32[]{:S(2)}) collective-permute-start(bf16[32,1152]{1,0:T(8,128)(2,1)S(1)} %norm.1.after_ref.zero_ref), channel_id=1, source_target_pairs={{0,4},{4,0},{8,12},{12,8},{1,5},{5,1},{9,13},{13,9},{2,6},{6,2},{1... | collective-permute-start | bytes 221192 | tf_op jit(solution)/shard_map/ppermute | solution.py:552
  26.0 7.3 %collective-permute-start.7 = (bf16[32,1152]{1,0:T(8,128)(2,1)S(1)}, bf16[32,1152]{1,0:T(8,128)(2,1)S(1)}, u32[]{:S(2)}, u32[]{:S(2)}) collective-permute-start(bf16[32,1152]{1,0:T(8,128)(2,1)S(1)} %norm.1.after_ref.zero_ref), channel_id=1, source_target_pairs={{0,8},{4,12},{8,0},{12,4},{1,9},{5,13},{9,1},{13,5},{2,10},{6,14},... | collective-permute-start | bytes 221192 | tf_op jit(solution)/shard_map/ppermute | solution.py:552
  27.7 6.3 %collective-permute-start.6 = (bf16[32,1152]{1,0:T(8,128)(2,1)S(1)}, bf16[32,1152]{1,0:T(8,128)(2,1)S(1)}, u32[]{:S(2)}, u32[]{:S(2)}) collective-permute-start(bf16[32,1152]{1,0:T(8,128)(2,1)S(1)} %norm.1.after_ref.zero_ref), channel_id=1, source_target_pairs={{0,12},{4,8},{8,4},{12,0},{1,13},{5,9},{9,5},{13,1},{2,14},{6,10},... | collective-permute-start | bytes 221192 | tf_op jit(solution)/shard_map/ppermute | solution.py:552
  34.2 7.3 %collective-permute-start.9 = (bf16[48,1152]{1,0:T(8,128)(2,1)S(1)}, bf16[48,1152]{1,0:T(8,128)(2,1)S(1)}, u32[]{:S(2)}, u32[]{:S(2)}) collective-permute-start(bf16[48,1152]{1,0:T(8,128)(2,1)S(1)} %get-tuple-element.43), channel_id=1, source_target_pairs={{0,18},{2,16},{16,2},{18,0},{1,19},{3,17},{17,3},{19,1},{4,22},{6,... | collective-permute-start | bytes 331784 | tf_op jit(solution)/shard_map/ppermute | solution.py:568
  37.4 4.7 %collective-permute-start.10 = (bf16[48,1152]{1,0:T(8,128)(2,1)S(1)}, bf16[48,1152]{1,0:T(8,128)(2,1)S(1)}, u32[]{:S(2)}, u32[]{:S(2)}) collective-permute-start(bf16[48,1152]{1,0:T(8,128)(2,1)S(1)} %get-tuple-element.44), channel_id=1, source_target_pairs={{0,2},{2,0},{1,3},{3,1},{4,6},{6,4},{5,7},{7,5},{8,10},{10,8},{9,1... | collective-permute-start | bytes 331784 | tf_op jit(solution)/shard_map/ppermute | solution.py:570
  37.4 4.7 %collective-permute-start.11 = (bf16[48,1152]{1,0:T(8,128)(2,1)S(1)}, bf16[48,1152]{1,0:T(8,128)(2,1)S(1)}, u32[]{:S(2)}, u32[]{:S(2)}) collective-permute-start(bf16[48,1152]{1,0:T(8,128)(2,1)S(1)} %get-tuple-element.45), channel_id=1, source_target_pairs={{0,16},{16,0},{1,17},{17,1},{2,18},{18,2},{3,19},{19,3},{4,20},{20... | collective-permute-start | bytes 331784 | tf_op jit(solution)/shard_map/ppermute | solution.py:569
  45.3 4.0 %collective-permute-start.12 = (bf16[2768,128]{1,0:T(8,128)(2,1)S(1)}, bf16[2768,128]{1,0:T(8,128)(2,1)S(1)}, u32[]{:S(2)}, u32[]{:S(2)}) collective-permute-start(bf16[2768,128]{1,0:T(8,128)(2,1)S(1)} %get-tuple-element.48.gate_ref), channel_id=1, source_target_pairs={{0,1},{1,0},{2,3},{3,2},{4,5},{5,4},{6,7},{7,6},{8,9},{9,8},{10,11... | collective-permute-start | bytes 2125832 | tf_op jit(solution)/shard_map/ppermute | solution.py:599
  47.7 3.0 %collective-permute-start.13 = (bf16[2064,128]{1,0:T(8,128)(2,1)S(1)}, bf16[2064,128]{1,0:T(8,128)(2,1)S(1)}, u32[]{:S(2)}, u32[]{:S(2)}) collective-permute-start(bf16[2064,128]{1,0:T(8,128)(2,1)S(1)} %up.2.up_ref), channel_id=1, source_target_pairs={{0,1},{1,0},{2,3},{3,2},{4,5},{5,4},{6,7},{7,6},{8,9},{9,8},{10,11... | collective-permute-start | bytes 1585160 | tf_op jit(solution)/shard_map/ppermute | solution.py:600
  49.2 1.5 %collective-permute-start.14 = (bf16[688,128]{1,0:T(8,128)(2,1)S(1)}, bf16[688,128]{1,0:T(8,128)(2,1)S(1)}, u32[]{:S(2)}, u32[]{:S(2)}) collective-permute-start(bf16[688,128]{1,0:T(8,128)(2,1)S(1)} %up.3.up_late_ref), channel_id=1, source_target_pairs={{0,1},{1,0},{2,3},{3,2},{4,5},{5,4},{6,7},{7,6},{8,9},{9,8},{10,11... | collective-permute-start | bytes 528392 | tf_op jit(solution)/shard_map/ppermute | solution.py:600
  52.9 5.3 %collective-permute-start.15 = (bf16[48,1024]{1,0:T(8,128)(2,1)S(1)}, bf16[48,1024]{1,0:T(8,128)(2,1)S(1)}, u32[]{:S(2)}, u32[]{:S(2)}) collective-permute-start(bf16[48,1024]{1,0:T(8,128)(2,1)S(1)} %get-tuple-element.54), channel_id=1, source_target_pairs={{0,2},{2,0},{1,3},{3,1},{4,6},{6,4},{5,7},{7,5},{8,10},{10,8},{9,1... | collective-permute-start | bytes 294920 | tf_op jit(solution)/shard_map/ppermute | solution.py:618
  55.0 7.8 %collective-permute-start.19 = (bf16[48,1024]{1,0:T(8,128)(2,1)S(1)}, bf16[48,1024]{1,0:T(8,128)(2,1)S(1)}, u32[]{:S(2)}, u32[]{:S(2)}) collective-permute-start(bf16[48,1024]{1,0:T(8,128)(2,1)S(1)} %get-tuple-element.59), channel_id=1, source_target_pairs={{0,16},{16,0},{1,17},{17,1},{2,18},{18,2},{3,19},{19,3},{4,20},{20... | collective-permute-start | bytes 294920 | tf_op jit(solution)/shard_map/ppermute | solution.py:620
  55.8 7.0 %collective-permute-start.20 = (bf16[48,1024]{1,0:T(8,128)(2,1)S(1)}, bf16[48,1024]{1,0:T(8,128)(2,1)S(1)}, u32[]{:S(2)}, u32[]{:S(2)}) collective-permute-start(bf16[48,1024]{1,0:T(8,128)(2,1)S(1)} %get-tuple-element.60), channel_id=1, source_target_pairs={{0,18},{2,16},{16,2},{18,0},{1,19},{3,17},{17,3},{19,1},{4,22},{6,... | collective-permute-start | bytes 294920 | tf_op jit(solution)/shard_map/ppermute | solution.py:619
  58.3 7.0 %collective-permute-start.16 = (bf16[16,1024]{1,0:T(8,128)(2,1)S(1)}, bf16[16,1024]{1,0:T(8,128)(2,1)S(1)}, u32[]{:S(2)}, u32[]{:S(2)}) collective-permute-start(bf16[16,1024]{1,0:T(8,128)(2,1)S(1)} %get-tuple-element.56), channel_id=1, source_target_pairs={{0,4},{4,0},{8,12},{12,8},{1,5},{5,1},{9,13},{13,9},{2,6},{6,2},{1... | collective-permute-start | bytes 98312 | tf_op jit(solution)/shard_map/ppermute | solution.py:630
  59.7 7.6 %collective-permute-start.17 = (bf16[16,1024]{1,0:T(8,128)(2,1)S(1)}, bf16[16,1024]{1,0:T(8,128)(2,1)S(1)}, u32[]{:S(2)}, u32[]{:S(2)}) collective-permute-start(bf16[16,1024]{1,0:T(8,128)(2,1)S(1)} %get-tuple-element.57), channel_id=1, source_target_pairs={{0,8},{4,12},{8,0},{12,4},{1,9},{5,13},{9,1},{13,5},{2,10},{6,14},... | collective-permute-start | bytes 98312 | tf_op jit(solution)/shard_map/ppermute | solution.py:630
  60.7 6.7 %collective-permute-start.18 = (bf16[16,1024]{1,0:T(8,128)(2,1)S(1)}, bf16[16,1024]{1,0:T(8,128)(2,1)S(1)}, u32[]{:S(2)}, u32[]{:S(2)}) collective-permute-start(bf16[16,1024]{1,0:T(8,128)(2,1)S(1)} %get-tuple-element.58), channel_id=1, source_target_pairs={{0,12},{4,8},{8,4},{12,0},{1,13},{5,9},{9,5},{13,1},{2,14},{6,10},... | collective-permute-start | bytes 98312 | tf_op jit(solution)/shard_map/ppermute | solution.py:630
  62.9 4.5 %collective-permute-start.21 = (bf16[16,1024]{1,0:T(8,128)(2,1)S(1)}, bf16[16,1024]{1,0:T(8,128)(2,1)S(1)}, u32[]{:S(2)}, u32[]{:S(2)}) collective-permute-start(bf16[16,1024]{1,0:T(8,128)(2,1)S(1)} %get-tuple-element.62), channel_id=1, source_target_pairs={{0,4},{4,0},{8,12},{12,8},{1,5},{5,1},{9,13},{13,9},{2,6},{6,2},{1... | collective-permute-start | bytes 98312 | tf_op jit(solution)/shard_map/ppermute | solution.py:630
  63.5 4.9 %collective-permute-start.22 = (bf16[16,1024]{1,0:T(8,128)(2,1)S(1)}, bf16[16,1024]{1,0:T(8,128)(2,1)S(1)}, u32[]{:S(2)}, u32[]{:S(2)}) collective-permute-start(bf16[16,1024]{1,0:T(8,128)(2,1)S(1)} %get-tuple-element.63), channel_id=1, source_target_pairs={{0,8},{4,12},{8,0},{12,4},{1,9},{5,13},{9,1},{13,5},{2,10},{6,14},... | collective-permute-start | bytes 98312 | tf_op jit(solution)/shard_map/ppermute | solution.py:630
  65.4 5.7 %collective-permute-start.23 = (bf16[16,1024]{1,0:T(8,128)(2,1)S(1)}, bf16[16,1024]{1,0:T(8,128)(2,1)S(1)}, u32[]{:S(2)}, u32[]{:S(2)}) collective-permute-start(bf16[16,1024]{1,0:T(8,128)(2,1)S(1)} %get-tuple-element.64), channel_id=1, source_target_pairs={{0,12},{4,8},{8,4},{12,0},{1,13},{5,9},{9,5},{13,1},{2,14},{6,10},... | collective-permute-start | bytes 98312 | tf_op jit(solution)/shard_map/ppermute | solution.py:630

commit v11 on v9

--- a/solution.py
+++ b/solution.py
@@ -432,7 +432,7 @@
                 far_out[...] = value[half : 2 * half]
 
 
-def merge_kernel(zero_ref, three_ref, two_ref, one_ref, side_far_ref, side_ref, far_ref, kept_ref, *out_refs):
+def merge_kernel(zero_ref, three_ref, two_ref, one_ref, kept_ref, side_ref, far_ref, side_far_ref, *out_refs):
     columns = kept_ref.shape[1]
     capacity = zero_ref.shape[0] // 2
     matches, found = places((zero_ref, one_ref, two_ref, three_ref), columns)
@@ -505,7 +505,7 @@
     to_second = [(t * 4 + q, q * 4 + (t ^ 2)) for t in range(4) for q in range(4)]
     across = lax.ppermute(picked, plane, to_second)
     near = lax.ppermute(picked, plane, to_first)
-    gate_units, up_units, down_units = [round(units * part / TILE) * TILE for part in (0.58, 0.41, 0.24)]
+    gate_units, up_units, down_units = [round(units * part / TILE) * TILE for part in (0.49, 0.45, 0.3)]
     gate_first, proj_held, rest = call(
         keep_gate_kernel,
         "keep_gate",
@@ -619,7 +619,7 @@
         "merge",
         [array(slots, columns)] * 4,
         [ON_CHIP] * 8,
-        [packed, *others[::-1], from_side_far, from_side, from_far, kept],
+        [packed, *others[::-1], kept, from_side, from_far, from_side_far],
     )
     values = [merged[0]] + [lax.ppermute(merged[v], "tok", crossed(2, v)) for v in (1, 2, 3)]
     return pl.pallas_call(

time: 71.6 us -> 71.8 us (level)
    ppermute x1, waiting for transfers between devices: 0.61 us -> 3.57 us  [paired_local(): from_far = lax.ppermute(to_far, 'groups', SWAP)]
    ppermute x1, waiting for transfers between devices: 2.62 us -> 0.01 us  [paired_local(): from_side_far = lax.ppermute(to_side_far, both_axes, crossed(2, 3))]
    ppermute x1, starting transfers between devices: 0.01 us -> 2.09 us  [paired_local(): from_side = lax.ppermute(to_side, 'mod', SWAP)]
    ppermute x1, starting transfers between devices: 2.3 us -> 0.88 us  [paired_local(): from_side_far = lax.ppermute(to_side_far, both_axes, crossed(2, 3))]
    ppermute x3, waiting for transfers between devices: 4.96 us -> 3.99 us  [paired_local(): lax.ppermute(merged[v], 'tok', crossed(2, v))]
where the time goes in v11:
time: 71.8 us; the launch traced here: 71.6 us
  starting transfers between devices  28.8 us (40%)
  Pallas kernels  26.9 us (37%)
  waiting for transfers between devices  15.7 us (22%)
    pallas_call x15, Pallas kernels, call(): pl.pallas_call(kernel, out_shape=outs, in_specs=specs, out_specs=jax.tree...  25.9 us
    ppermute x3, starting transfers between devices, paired_local(): lax.ppermute(partial[v], 'tok', crossed(2, v))  6.14 us
    ppermute x3, starting transfers between devices, paired_local(): lax.ppermute(merged[v], 'tok', crossed(2, v))  4.45 us
    ppermute x3, starting transfers between devices, paired_local(): lax.ppermute(packed, 'tok', crossed(2, v))  4.42 us
    ppermute x3, waiting for transfers between devices, paired_local(): lax.ppermute(merged[v], 'tok', crossed(2, v))  3.99 us
    ppermute x1, starting transfers between devices, paired_local(): side_far = lax.ppermute(to_corner_rows, both_axes, crossed(2, 3))  3.71 us
    ppermute x1, waiting for transfers between devices, paired_local(): from_far = lax.ppermute(to_far, 'groups', SWAP)  3.57 us
    ppermute x1, starting transfers between devices, paired_local(): across = lax.ppermute(picked, plane, to_second)  2.99 us
  transfers between devices with their start and end apart: 21, of which 11 were waited for; matrix products, arithmetic and copies ran while one was open for 0% of the time, Pallas kernels for 26%

profile of v11, /device:TPU:0, one launch (start us, length us, event | category | flops | bytes accessed | tf_op | source)
XLA Modules:
  0.0 71.6 jit_solution(18177185579266852252)
XLA Ops:
  0.0 1.1 %select.1 = (bf16[32,1024]{1,0:T(8,128)(2,1)S(1)}, bf16[32,128]{1,0:T(8,128)(2,1)S(1)}, f32[8,128]{1,0:T(8,128)S(1)}) custom-call(s32[4,16]{1,0:T(4,128)} %rows_hbm.1, bf16[128,1024]{1,0:T(8,128)(2,1)} %context_hbm.1), custom_call_target="tpu_custom_call" | custom-call | tf_op jit(solution)/shard_map/select/pallas_call | solution.py:173
  1.1 3.0 %collective-permute-start.1 = (bf16[32,1024]{1,0:T(8,128)(2,1)S(1)}, bf16[32,1024]{1,0:T(8,128)(2,1)S(1)}, u32[]{:S(2)}, u32[]{:S(2)}) collective-permute-start(bf16[32,1024]{1,0:T(8,128)(2,1)S(1)} %get-tuple-element.34), channel_id=1, source_target_pairs={{0,2},{1,6},{2,10},{3,14},{4,3},{5,7},{6,11},{7,15},{8,0},{9,4},{1... | collective-permute-start | bytes 196616 | tf_op jit(solution)/shard_map/ppermute | solution.py:506
  4.1 0.7 collective-permute-start
  4.8 3.3 %keep_gate.1 = (bf16[1344,2048]{1,0:T(8,128)(2,1)S(1)}, bf16[1024,1024]{1,0:T(8,128)(2,1)S(1)}, f32[32,1024]{1,0:T(8,128)S(1)}) custom-call(bf16[32,128]{1,0:T(8,128)(2,1)S(1)} %get-tuple-element.31.pick_ref, bf16[128,1024]{1,0:T(8,128)(2,1)} %residual_hbm.1, bf16[2,2752,2048]{2,1,0:T(8,128)(2,1)} %bitcast.10, bf16[1024,1024]{1,0:T(8,128)(2,1)} %proj_ref.1), custom_call_target="tpu_custom_call" | custom-call | bytes 5636096 | tf_op jit(solution)/shard_map/keep_gate/pallas_call | solution.py:173
  8.1 1.3 %collective-permute-done.1.across_ref = bf16[32,1024]{1,0:T(8,128)(2,1)S(1)} collective-permute-done((bf16[32,1024]{1,0:T(8,128)(2,1)S(1)}, bf16[32,1024]{1,0:T(8,128)(2,1)S(1)}, u32[]{:S(2)}, u32[]{:S(2)}) %collective-permute-start.1) | collective-permute-done | bytes 65568 | tf_op jit(solution)/shard_map/ppermute | solution.py:506
  9.5 0.0 collective-permute-done.near_ref
  9.5 1.4 %collective-permute-start.2 = (bf16[64,1024]{1,0:T(8,128)(2,1)S(1)}, bf16[64,1024]{1,0:T(8,128)(2,1)S(1)}, u32[]{:S(2)}, u32[]{:S(2)}) collective-permute-start(bf16[64,1024]{1,0:T(8,128)(2,1)S(1)} %join.1.joined_ref), channel_id=1, source_target_pairs={{0,1},{1,0},{2,3},{3,2},{4,5},{5,4},{6,7},{7,6},{8,9},{9,8},{10,11... | collective-permute-start | bytes 393224 | tf_op jit(solution)/shard_map/ppermute | solution.py:524
  10.9 1.0 %collective-permute-done.2.other_ref = bf16[64,1024]{1,0:T(8,128)(2,1)S(1)} collective-permute-done((bf16[64,1024]{1,0:T(8,128)(2,1)S(1)}, bf16[64,1024]{1,0:T(8,128)(2,1)S(1)}, u32[]{:S(2)}, u32[]{:S(2)}) %collective-permute-start.2) | collective-permute-done | bytes 131104 | tf_op jit(solution)/shard_map/ppermute | solution.py:524
  11.9 0.5 project.1.after_ref.partial_ref
  12.4 1.7 %collective-permute-start.5 = (bf16[32,1024]{1,0:T(8,128)(2,1)S(1)}, bf16[32,1024]{1,0:T(8,128)(2,1)S(1)}, u32[]{:S(2)}, u32[]{:S(2)}) collective-permute-start(bf16[32,1024]{1,0:T(8,128)(2,1)S(1)} %get-tuple-element.57), channel_id=1, source_target_pairs={{0,4},{4,0},{8,12},{12,8},{1,5},{5,1},{9,13},{13,9},{2,6},{6,2},{1... | collective-permute-start | bytes 196616 | tf_op jit(solution)/shard_map/ppermute | solution.py:533
  14.1 4.4 %collective-permute-start.4 = (bf16[32,1024]{1,0:T(8,128)(2,1)S(1)}, bf16[32,1024]{1,0:T(8,128)(2,1)S(1)}, u32[]{:S(2)}, u32[]{:S(2)}) collective-permute-start(bf16[32,1024]{1,0:T(8,128)(2,1)S(1)} %get-tuple-element.58), channel_id=1, source_target_pairs={{0,8},{4,12},{8,0},{12,4},{1,9},{5,13},{9,1},{13,5},{2,10},{6,14},... | collective-permute-start | bytes 196616 | tf_op jit(solution)/shard_map/ppermute | solution.py:533
  18.5 0.0 collective-permute-start.3
  18.5 4.2 %keep_more.1 = (bf16[1408,2048]{1,0:T(8,128)(2,1)S(1)}, bf16[1232,2048]{1,0:T(8,128)(2,1)S(1)}) custom-call(bf16[4,32,1024]{2,1,0:T(8,128)(2,1)S(1)} %project.1.after_ref.partial_ref, bf16[2,2752,2048]{2,1,0:T(8,128)(2,1)} %bitcast.11, bf16[2,2752,2048]{2,1,0:T(8,128)(2,1)} %bitcast.12), custom_call_target="tpu_custom_call" | custom-call | bytes 10813440 | tf_op jit(solution)/shard_map/keep_more/pallas_call | solution.py:173
  22.7 0.0 collective-permute-done.5.one_ref
  22.7 2.0 %collective-permute-done.3.three_ref = bf16[32,1024]{1,0:T(8,128)(2,1)S(1)} collective-permute-done((bf16[32,1024]{1,0:T(8,128)(2,1)S(1)}, bf16[32,1024]{1,0:T(8,128)(2,1)S(1)}, u32[]{:S(2)}, u32[]{:S(2)}) %collective-permute-start.3) | collective-permute-done | bytes 65568 | tf_op jit(solution)/shard_map/ppermute | solution.py:533
  24.7 0.2 norm.1.after_ref.zero_ref
  25.0 0.8 %collective-permute-start.8 = (bf16[32,1152]{1,0:T(8,128)(2,1)S(1)}, bf16[32,1152]{1,0:T(8,128)(2,1)S(1)}, u32[]{:S(2)}, u32[]{:S(2)}) collective-permute-start(bf16[32,1152]{1,0:T(8,128)(2,1)S(1)} %norm.1.after_ref.zero_ref), channel_id=1, source_target_pairs={{0,4},{4,0},{8,12},{12,8},{1,5},{5,1},{9,13},{13,9},{2,6},{6,2},{1... | collective-permute-start | bytes 221192 | tf_op jit(solution)/shard_map/ppermute | solution.py:548
  25.7 1.7 %collective-permute-start.7 = (bf16[32,1152]{1,0:T(8,128)(2,1)S(1)}, bf16[32,1152]{1,0:T(8,128)(2,1)S(1)}, u32[]{:S(2)}, u32[]{:S(2)}) collective-permute-start(bf16[32,1152]{1,0:T(8,128)(2,1)S(1)} %norm.1.after_ref.zero_ref), channel_id=1, source_target_pairs={{0,8},{4,12},{8,0},{12,4},{1,9},{5,13},{9,1},{13,5},{2,10},{6,14},... | collective-permute-start | bytes 221192 | tf_op jit(solution)/shard_map/ppermute | solution.py:548
  27.5 1.9 %collective-permute-start.6 = (bf16[32,1152]{1,0:T(8,128)(2,1)S(1)}, bf16[32,1152]{1,0:T(8,128)(2,1)S(1)}, u32[]{:S(2)}, u32[]{:S(2)}) collective-permute-start(bf16[32,1152]{1,0:T(8,128)(2,1)S(1)} %norm.1.after_ref.zero_ref), channel_id=1, source_target_pairs={{0,12},{4,8},{8,4},{12,0},{1,13},{5,9},{9,5},{13,1},{2,14},{6,10},... | collective-permute-start | bytes 221192 | tf_op jit(solution)/shard_map/ppermute | solution.py:548
  29.4 3.8 %keep_up.1 = (bf16[1520,2048]{1,0:T(8,128)(2,1)S(1)}, bf16[832,2048]{1,0:T(8,128)(2,1)S(1)}) custom-call(bf16[32,1152]{1,0:T(8,128)(2,1)S(1)} %norm.1.after_ref.zero_ref, bf16[2,2752,2048]{2,1,0:T(8,128)(2,1)} %bitcast.13, bf16[2,2752,2048]{2,1,0:T(8,128)(2,1)} %refs_0_.1), custom_call_target="tpu_custom_call" | custom-call | bytes 9633792 | tf_op jit(solution)/shard_map/keep_up/pallas_call | solution.py:173
  33.2 0.5 collective-permute-done.6.three_ref
  33.7 0.2 arrange.1
  33.9 3.7 %collective-permute-start.9 = (bf16[48,1152]{1,0:T(8,128)(2,1)S(1)}, bf16[48,1152]{1,0:T(8,128)(2,1)S(1)}, u32[]{:S(2)}, u32[]{:S(2)}) collective-permute-start(bf16[48,1152]{1,0:T(8,128)(2,1)S(1)} %get-tuple-element.39), channel_id=1, source_target_pairs={{0,18},{2,16},{16,2},{18,0},{1,19},{3,17},{17,3},{19,1},{4,22},{6,... | collective-permute-start | bytes 331784 | tf_op jit(solution)/shard_map/ppermute | solution.py:564
  37.6 0.6 collective-permute-start.11
  38.2 3.2 %keep_down.1.refs_2_.second_ref = bf16[1920,2048]{1,0:T(8,128)(2,1)S(1)} custom-call(bf16[48,1152]{1,0:T(8,128)(2,1)S(1)} %get-tuple-element.42.after_ref.own_ref, bf16[2,2752,2048]{2,1,0:T(8,128)(2,1)} %refs_0_.1), custom_call_target="tpu_custom_call" | custom-call | bytes 7864320 | tf_op jit(solution)/shard_map/keep_down/pallas_call | solution.py:173
  41.5 0.8 %collective-permute-done.10.side_own_ref = bf16[48,1152]{1,0:T(8,128)(2,1)S(1)} collective-permute-done((bf16[48,1152]{1,0:T(8,128)(2,1)S(1)}, bf16[48,1152]{1,0:T(8,128)(2,1)S(1)}, u32[]{:S(2)}, u32[]{:S(2)}) %collective-permute-start.10) | collective-permute-done | bytes 110624 | tf_op jit(solution)/shard_map/ppermute | solution.py:566
  42.4 3.2 %gate.1 = (bf16[2768,128]{1,0:T(8,128)(2,1)S(1)}, bf16[128,2048]{1,0:T(8,128)(2,1)S(1)}) custom-call(bf16[48,1152]{1,0:T(8,128)(2,1)S(1)} %collective-permute-done.9.side_far_ref, bf16[48,1152]{1,0:T(8,128)(2,1)S(1)} %collective-permute-done.10.side_own_ref, bf16[48,1152]{1,0:T(8,128)(2,1)S(1)} %collective-permute-done.11.far_ref, ...), custom_call_target="tpu_custom_call" | custom-call | flops 1442840576 | tf_op jit(solution)/shard_map/gate/pallas_call | solution.py:173
  45.6 0.1 collective-permute-start.12
  45.6 2.4 %up.2.up_ref = bf16[2064,128]{1,0:T(8,128)(2,1)S(1)} custom-call(bf16[128,2048]{1,0:T(8,128)(2,1)S(1)} %get-tuple-element.47.rows_ref, bf16[1232,2048]{1,0:T(8,128)(2,1)S(1)} %get-tuple-element.37._.refs_0_, bf16[1520,2048]{1,0:T(8,128)(2,1)S(1)} %get-tuple-element.38._.refs_1_.refs_0_), custom_call_target="tpu_custom_call" | custom-call | flops 1082130432 | tf_op jit(solution)/shard_map/up/pallas_call | solution.py:173
  48.0 0.6 collective-permute-start.13
  48.6 0.9 %up.3.up_late_ref = bf16[688,128]{1,0:T(8,128)(2,1)S(1)} custom-call(bf16[128,2048]{1,0:T(8,128)(2,1)S(1)} %get-tuple-element.47.rows_ref, bf16[1520,2048]{1,0:T(8,128)(2,1)S(1)} %get-tuple-element.38._.refs_1_.refs_0_), custom_call_target="tpu_custom_call" | custom-call | flops 360710144 | tf_op jit(solution)/shard_map/up/pallas_call | solution.py:173
  49.5 0.1 collective-permute-start.14
  49.5 0.5 silu.1
  50.1 0.9 %collective-permute-done.14.other_late_ref = bf16[688,128]{1,0:T(8,128)(2,1)S(1)} collective-permute-done((bf16[688,128]{1,0:T(8,128)(2,1)S(1)}, bf16[688,128]{1,0:T(8,128)(2,1)S(1)}, u32[]{:S(2)}, u32[]{:S(2)}) %collective-permute-start.14) | collective-permute-done | bytes 176160 | tf_op jit(solution)/shard_map/ppermute | solution.py:596
  50.9 2.2 %down.1 = (bf16[48,1024]{1,0:T(8,128)(2,1)S(1)}, bf16[48,1024]{1,0:T(8,128)(2,1)S(1)}, bf16[48,1024]{1,0:T(8,128)(2,1)S(1)}, bf16[48,1024]{1,0:T(8,128)(2,1)S(1)}) custom-call(f32[2752,128]{1,0:T(8,128)S(1)} %get-tuple-element.45.silu_ref, f32[8,128]{1,0:T(8,128)S(1)} %get-tuple-element.46.stat_ref, bf16[2064,128]{1,0:T(8,128)(2,1)S(1)} %up.2.up_ref, ...), custom_call_target="tpu_custom_call" | custom-call | flops 1442840576 | tf_op jit(solution)/shard_map/down/pallas_call | solution.py:173
  53.2 2.1 %collective-permute-start.15 = (bf16[48,1024]{1,0:T(8,128)(2,1)S(1)}, bf16[48,1024]{1,0:T(8,128)(2,1)S(1)}, u32[]{:S(2)}, u32[]{:S(2)}) collective-permute-start(bf16[48,1024]{1,0:T(8,128)(2,1)S(1)} %get-tuple-element.50), channel_id=1, source_target_pairs={{0,2},{2,0},{1,3},{3,1},{4,6},{6,4},{5,7},{7,5},{8,10},{10,8},{9,1... | collective-permute-start | bytes 294920 | tf_op jit(solution)/shard_map/ppermute | solution.py:616
  55.3 0.7 collective-permute-start.16
  55.9 0.9 %collective-permute-start.17 = (bf16[48,1024]{1,0:T(8,128)(2,1)S(1)}, bf16[48,1024]{1,0:T(8,128)(2,1)S(1)}, u32[]{:S(2)}, u32[]{:S(2)}) collective-permute-start(bf16[48,1024]{1,0:T(8,128)(2,1)S(1)} %get-tuple-element.52), channel_id=1, source_target_pairs={{0,18},{2,16},{16,2},{18,0},{1,19},{3,17},{17,3},{19,1},{4,22},{6,... | collective-permute-start | bytes 294920 | tf_op jit(solution)/shard_map/ppermute | solution.py:614
  56.8 1.6 %collective-permute-done.15.side_ref = bf16[48,1024]{1,0:T(8,128)(2,1)S(1)} collective-permute-done((bf16[48,1024]{1,0:T(8,128)(2,1)S(1)}, bf16[48,1024]{1,0:T(8,128)(2,1)S(1)}, u32[]{:S(2)}, u32[]{:S(2)}) %collective-permute-start.15) | collective-permute-done | bytes 98336 | tf_op jit(solution)/shard_map/ppermute | solution.py:616
  58.4 3.6 %collective-permute-done.16.far_ref = bf16[48,1024]{1,0:T(8,128)(2,1)S(1)} collective-permute-done((bf16[48,1024]{1,0:T(8,128)(2,1)S(1)}, bf16[48,1024]{1,0:T(8,128)(2,1)S(1)}, u32[]{:S(2)}, u32[]{:S(2)}) %collective-permute-start.16) | collective-permute-done | bytes 98336 | tf_op jit(solution)/shard_map/ppermute | solution.py:615
  62.0 0.2 merge.1
  62.2 1.4 %collective-permute-start.18 = (bf16[32,1024]{1,0:T(8,128)(2,1)S(1)}, bf16[32,1024]{1,0:T(8,128)(2,1)S(1)}, u32[]{:S(2)}, u32[]{:S(2)}) collective-permute-start(bf16[32,1024]{1,0:T(8,128)(2,1)S(1)} %get-tuple-element.54), channel_id=1, source_target_pairs={{0,4},{4,0},{8,12},{12,8},{1,5},{5,1},{9,13},{13,9},{2,6},{6,2},{1... | collective-permute-start | bytes 196616 | tf_op jit(solution)/shard_map/ppermute | solution.py:624
  63.6 0.9 %collective-permute-start.19 = (bf16[32,1024]{1,0:T(8,128)(2,1)S(1)}, bf16[32,1024]{1,0:T(8,128)(2,1)S(1)}, u32[]{:S(2)}, u32[]{:S(2)}) collective-permute-start(bf16[32,1024]{1,0:T(8,128)(2,1)S(1)} %get-tuple-element.55), channel_id=1, source_target_pairs={{0,8},{4,12},{8,0},{12,4},{1,9},{5,13},{9,1},{13,5},{2,10},{6,14},... | collective-permute-start | bytes 196616 | tf_op jit(solution)/shard_map/ppermute | solution.py:624
  64.5 2.2 %collective-permute-start.20 = (bf16[32,1024]{1,0:T(8,128)(2,1)S(1)}, bf16[32,1024]{1,0:T(8,128)(2,1)S(1)}, u32[]{:S(2)}, u32[]{:S(2)}) collective-permute-start(bf16[32,1024]{1,0:T(8,128)(2,1)S(1)} %get-tuple-element.56), channel_id=1, source_target_pairs={{0,12},{4,8},{8,4},{12,0},{1,13},{5,9},{9,5},{13,1},{2,14},{6,10},... | collective-permute-start | bytes 196616 | tf_op jit(solution)/shard_map/ppermute | solution.py:624
  66.6 1.1 %collective-permute-done.18.one_ref = bf16[32,1024]{1,0:T(8,128)(2,1)S(1)} collective-permute-done((bf16[32,1024]{1,0:T(8,128)(2,1)S(1)}, bf16[32,1024]{1,0:T(8,128)(2,1)S(1)}, u32[]{:S(2)}, u32[]{:S(2)}) %collective-permute-start.18) | collective-permute-done | bytes 65568 | tf_op jit(solution)/shard_map/ppermute | solution.py:624
  67.7 1.7 %collective-permute-done.19.two_ref = bf16[32,1024]{1,0:T(8,128)(2,1)S(1)} collective-permute-done((bf16[32,1024]{1,0:T(8,128)(2,1)S(1)}, bf16[32,1024]{1,0:T(8,128)(2,1)S(1)}, u32[]{:S(2)}, u32[]{:S(2)}) %collective-permute-start.19) | collective-permute-done | bytes 65568 | tf_op jit(solution)/shard_map/ppermute | solution.py:624
  69.5 1.2 %collective-permute-done.20.three_ref = bf16[32,1024]{1,0:T(8,128)(2,1)S(1)} collective-permute-done((bf16[32,1024]{1,0:T(8,128)(2,1)S(1)}, bf16[32,1024]{1,0:T(8,128)(2,1)S(1)}, u32[]{:S(2)}, u32[]{:S(2)}) %collective-permute-start.20) | collective-permute-done | bytes 65568 | tf_op jit(solution)/shard_map/ppermute | solution.py:624
  70.6 1.0 %scatter.1 = bf16[128,1024]{1,0:T(8,128)(2,1)} custom-call(bf16[32,128]{1,0:T(8,128)(2,1)S(1)} %get-tuple-element.31.pick_ref, bf16[32,1024]{1,0:T(8,128)(2,1)S(1)} %get-tuple-element.53.zero_ref, bf16[32,1024]{1,0:T(8,128)(2,1)S(1)} %collective-permute-done.18.one_ref, bf16[32,1024]{1,0:T(8,128)(2,1)S(1)} %collective-permute-done.19.two_ref, ...), custom_call_target="tpu_custom_call" | custom-call | tf_op jit(solution)/shard_map/scatter/pallas_call | solution.py:625
  (15 shorter events, 0.1 us)
Async XLA Ops:
  1.1 8.3 %collective-permute-start.1 = (bf16[32,1024]{1,0:T(8,128)(2,1)S(1)}, bf16[32,1024]{1,0:T(8,128)(2,1)S(1)}, u32[]{:S(2)}, u32[]{:S(2)}) collective-permute-start(bf16[32,1024]{1,0:T(8,128)(2,1)S(1)} %get-tuple-element.34), channel_id=1, source_target_pairs={{0,2},{1,6},{2,10},{3,14},{4,3},{5,7},{6,11},{7,15},{8,0},{9,4},{1... | collective-permute-start | bytes 196616 | tf_op jit(solution)/shard_map/ppermute | solution.py:506
  4.1 5.3 %collective-permute-start = (bf16[32,1024]{1,0:T(8,128)(2,1)S(1)}, bf16[32,1024]{1,0:T(8,128)(2,1)S(1)}, u32[]{:S(2)}, u32[]{:S(2)}) collective-permute-start(bf16[32,1024]{1,0:T(8,128)(2,1)S(1)} %get-tuple-element.34), channel_id=1, source_target_pairs={{0,0},{1,4},{2,8},{3,12},{4,1},{5,5},{6,9},{7,13},{8,2},{9,6},{10,... | collective-permute-start | bytes 196616 | tf_op jit(solution)/shard_map/ppermute | solution.py:507
  9.5 2.4 %collective-permute-start.2 = (bf16[64,1024]{1,0:T(8,128)(2,1)S(1)}, bf16[64,1024]{1,0:T(8,128)(2,1)S(1)}, u32[]{:S(2)}, u32[]{:S(2)}) collective-permute-start(bf16[64,1024]{1,0:T(8,128)(2,1)S(1)} %join.1.joined_ref), channel_id=1, source_target_pairs={{0,1},{1,0},{2,3},{3,2},{4,5},{5,4},{6,7},{7,6},{8,9},{9,8},{10,11... | collective-permute-start | bytes 393224 | tf_op jit(solution)/shard_map/ppermute | solution.py:524
  12.4 10.3 %collective-permute-start.5 = (bf16[32,1024]{1,0:T(8,128)(2,1)S(1)}, bf16[32,1024]{1,0:T(8,128)(2,1)S(1)}, u32[]{:S(2)}, u32[]{:S(2)}) collective-permute-start(bf16[32,1024]{1,0:T(8,128)(2,1)S(1)} %get-tuple-element.57), channel_id=1, source_target_pairs={{0,4},{4,0},{8,12},{12,8},{1,5},{5,1},{9,13},{13,9},{2,6},{6,2},{1... | collective-permute-start | bytes 196616 | tf_op jit(solution)/shard_map/ppermute | solution.py:533
  14.1 8.6 %collective-permute-start.4 = (bf16[32,1024]{1,0:T(8,128)(2,1)S(1)}, bf16[32,1024]{1,0:T(8,128)(2,1)S(1)}, u32[]{:S(2)}, u32[]{:S(2)}) collective-permute-start(bf16[32,1024]{1,0:T(8,128)(2,1)S(1)} %get-tuple-element.58), channel_id=1, source_target_pairs={{0,8},{4,12},{8,0},{12,4},{1,9},{5,13},{9,1},{13,5},{2,10},{6,14},... | collective-permute-start | bytes 196616 | tf_op jit(solution)/shard_map/ppermute | solution.py:533
  18.5 6.2 %collective-permute-start.3 = (bf16[32,1024]{1,0:T(8,128)(2,1)S(1)}, bf16[32,1024]{1,0:T(8,128)(2,1)S(1)}, u32[]{:S(2)}, u32[]{:S(2)}) collective-permute-start(bf16[32,1024]{1,0:T(8,128)(2,1)S(1)} %get-tuple-element.59), channel_id=1, source_target_pairs={{0,12},{4,8},{8,4},{12,0},{1,13},{5,9},{9,5},{13,1},{2,14},{6,10},... | collective-permute-start | bytes 196616 | tf_op jit(solution)/shard_map/ppermute | solution.py:533
  18.5 6.2 %copy-start = (bf16[1024,4]{0,1:T(4,128)(2,1)S(1)}, bf16[1024,4]{0,1:T(4,128)(2,1)}, u32[]{:S(2)}) copy-start(bf16[1024,4]{0,1:T(4,128)(2,1)} %param.14) | copy-start | bytes 24580
  18.5 6.2 %copy-start.1 = (bf16[2,1024]{1,0:T(2,128)(2,1)S(1)}, bf16[2,1024]{1,0:T(2,128)(2,1)}, u32[]{:S(2)}) copy-start(bf16[2,1024]{1,0:T(2,128)(2,1)} %gain_ref.1) | copy-start | bytes 12292
  25.0 8.2 %collective-permute-start.8 = (bf16[32,1152]{1,0:T(8,128)(2,1)S(1)}, bf16[32,1152]{1,0:T(8,128)(2,1)S(1)}, u32[]{:S(2)}, u32[]{:S(2)}) collective-permute-start(bf16[32,1152]{1,0:T(8,128)(2,1)S(1)} %norm.1.after_ref.zero_ref), channel_id=1, source_target_pairs={{0,4},{4,0},{8,12},{12,8},{1,5},{5,1},{9,13},{13,9},{2,6},{6,2},{1... | collective-permute-start | bytes 221192 | tf_op jit(solution)/shard_map/ppermute | solution.py:548
  25.7 7.4 %collective-permute-start.7 = (bf16[32,1152]{1,0:T(8,128)(2,1)S(1)}, bf16[32,1152]{1,0:T(8,128)(2,1)S(1)}, u32[]{:S(2)}, u32[]{:S(2)}) collective-permute-start(bf16[32,1152]{1,0:T(8,128)(2,1)S(1)} %norm.1.after_ref.zero_ref), channel_id=1, source_target_pairs={{0,8},{4,12},{8,0},{12,4},{1,9},{5,13},{9,1},{13,5},{2,10},{6,14},... | collective-permute-start | bytes 221192 | tf_op jit(solution)/shard_map/ppermute | solution.py:548
  27.5 6.3 %collective-permute-start.6 = (bf16[32,1152]{1,0:T(8,128)(2,1)S(1)}, bf16[32,1152]{1,0:T(8,128)(2,1)S(1)}, u32[]{:S(2)}, u32[]{:S(2)}) collective-permute-start(bf16[32,1152]{1,0:T(8,128)(2,1)S(1)} %norm.1.after_ref.zero_ref), channel_id=1, source_target_pairs={{0,12},{4,8},{8,4},{12,0},{1,13},{5,9},{9,5},{13,1},{2,14},{6,10},... | collective-permute-start | bytes 221192 | tf_op jit(solution)/shard_map/ppermute | solution.py:548
  33.9 7.6 %collective-permute-start.9 = (bf16[48,1152]{1,0:T(8,128)(2,1)S(1)}, bf16[48,1152]{1,0:T(8,128)(2,1)S(1)}, u32[]{:S(2)}, u32[]{:S(2)}) collective-permute-start(bf16[48,1152]{1,0:T(8,128)(2,1)S(1)} %get-tuple-element.39), channel_id=1, source_target_pairs={{0,18},{2,16},{16,2},{18,0},{1,19},{3,17},{17,3},{19,1},{4,22},{6,... | collective-permute-start | bytes 331784 | tf_op jit(solution)/shard_map/ppermute | solution.py:564
  37.6 4.7 %collective-permute-start.10 = (bf16[48,1152]{1,0:T(8,128)(2,1)S(1)}, bf16[48,1152]{1,0:T(8,128)(2,1)S(1)}, u32[]{:S(2)}, u32[]{:S(2)}) collective-permute-start(bf16[48,1152]{1,0:T(8,128)(2,1)S(1)} %get-tuple-element.40), channel_id=1, source_target_pairs={{0,2},{2,0},{1,3},{3,1},{4,6},{6,4},{5,7},{7,5},{8,10},{10,8},{9,1... | collective-permute-start | bytes 331784 | tf_op jit(solution)/shard_map/ppermute | solution.py:566
  37.6 4.7 %collective-permute-start.11 = (bf16[48,1152]{1,0:T(8,128)(2,1)S(1)}, bf16[48,1152]{1,0:T(8,128)(2,1)S(1)}, u32[]{:S(2)}, u32[]{:S(2)}) collective-permute-start(bf16[48,1152]{1,0:T(8,128)(2,1)S(1)} %get-tuple-element.41), channel_id=1, source_target_pairs={{0,16},{16,0},{1,17},{17,1},{2,18},{18,2},{3,19},{19,3},{4,20},{20... | collective-permute-start | bytes 331784 | tf_op jit(solution)/shard_map/ppermute | solution.py:565
  45.6 4.0 %collective-permute-start.12 = (bf16[2768,128]{1,0:T(8,128)(2,1)S(1)}, bf16[2768,128]{1,0:T(8,128)(2,1)S(1)}, u32[]{:S(2)}, u32[]{:S(2)}) collective-permute-start(bf16[2768,128]{1,0:T(8,128)(2,1)S(1)} %get-tuple-element.44.gate_ref), channel_id=1, source_target_pairs={{0,1},{1,0},{2,3},{3,2},{4,5},{5,4},{6,7},{7,6},{8,9},{9,8},{10,11... | collective-permute-start | bytes 2125832 | tf_op jit(solution)/shard_map/ppermute | solution.py:595
  48.0 2.9 %collective-permute-start.13 = (bf16[2064,128]{1,0:T(8,128)(2,1)S(1)}, bf16[2064,128]{1,0:T(8,128)(2,1)S(1)}, u32[]{:S(2)}, u32[]{:S(2)}) collective-permute-start(bf16[2064,128]{1,0:T(8,128)(2,1)S(1)} %up.2.up_ref), channel_id=1, source_target_pairs={{0,1},{1,0},{2,3},{3,2},{4,5},{5,4},{6,7},{7,6},{8,9},{9,8},{10,11... | collective-permute-start | bytes 1585160 | tf_op jit(solution)/shard_map/ppermute | solution.py:596
  49.5 1.5 %collective-permute-start.14 = (bf16[688,128]{1,0:T(8,128)(2,1)S(1)}, bf16[688,128]{1,0:T(8,128)(2,1)S(1)}, u32[]{:S(2)}, u32[]{:S(2)}) collective-permute-start(bf16[688,128]{1,0:T(8,128)(2,1)S(1)} %up.3.up_late_ref), channel_id=1, source_target_pairs={{0,1},{1,0},{2,3},{3,2},{4,5},{5,4},{6,7},{7,6},{8,9},{9,8},{10,11... | collective-permute-start | bytes 528392 | tf_op jit(solution)/shard_map/ppermute | solution.py:596
  53.2 5.3 %collective-permute-start.15 = (bf16[48,1024]{1,0:T(8,128)(2,1)S(1)}, bf16[48,1024]{1,0:T(8,128)(2,1)S(1)}, u32[]{:S(2)}, u32[]{:S(2)}) collective-permute-start(bf16[48,1024]{1,0:T(8,128)(2,1)S(1)} %get-tuple-element.50), channel_id=1, source_target_pairs={{0,2},{2,0},{1,3},{3,1},{4,6},{6,4},{5,7},{7,5},{8,10},{10,8},{9,1... | collective-permute-start | bytes 294920 | tf_op jit(solution)/shard_map/ppermute | solution.py:616
  55.3 6.7 %collective-permute-start.16 = (bf16[48,1024]{1,0:T(8,128)(2,1)S(1)}, bf16[48,1024]{1,0:T(8,128)(2,1)S(1)}, u32[]{:S(2)}, u32[]{:S(2)}) collective-permute-start(bf16[48,1024]{1,0:T(8,128)(2,1)S(1)} %get-tuple-element.51), channel_id=1, source_target_pairs={{0,16},{16,0},{1,17},{17,1},{2,18},{18,2},{3,19},{19,3},{4,20},{20... | collective-permute-start | bytes 294920 | tf_op jit(solution)/shard_map/ppermute | solution.py:615
  55.9 6.1 %collective-permute-start.17 = (bf16[48,1024]{1,0:T(8,128)(2,1)S(1)}, bf16[48,1024]{1,0:T(8,128)(2,1)S(1)}, u32[]{:S(2)}, u32[]{:S(2)}) collective-permute-start(bf16[48,1024]{1,0:T(8,128)(2,1)S(1)} %get-tuple-element.52), channel_id=1, source_target_pairs={{0,18},{2,16},{16,2},{18,0},{1,19},{3,17},{17,3},{19,1},{4,22},{6,... | collective-permute-start | bytes 294920 | tf_op jit(solution)/shard_map/ppermute | solution.py:614
  62.2 5.6 %collective-permute-start.18 = (bf16[32,1024]{1,0:T(8,128)(2,1)S(1)}, bf16[32,1024]{1,0:T(8,128)(2,1)S(1)}, u32[]{:S(2)}, u32[]{:S(2)}) collective-permute-start(bf16[32,1024]{1,0:T(8,128)(2,1)S(1)} %get-tuple-element.54), channel_id=1, source_target_pairs={{0,4},{4,0},{8,12},{12,8},{1,5},{5,1},{9,13},{13,9},{2,6},{6,2},{1... | collective-permute-start | bytes 196616 | tf_op jit(solution)/shard_map/ppermute | solution.py:624
  63.6 5.9 %collective-permute-start.19 = (bf16[32,1024]{1,0:T(8,128)(2,1)S(1)}, bf16[32,1024]{1,0:T(8,128)(2,1)S(1)}, u32[]{:S(2)}, u32[]{:S(2)}) collective-permute-start(bf16[32,1024]{1,0:T(8,128)(2,1)S(1)} %get-tuple-element.55), channel_id=1, source_target_pairs={{0,8},{4,12},{8,0},{12,4},{1,9},{5,13},{9,1},{13,5},{2,10},{6,14},... | collective-permute-start | bytes 196616 | tf_op jit(solution)/shard_map/ppermute | solution.py:624
  64.5 6.2 %collective-permute-start.20 = (bf16[32,1024]{1,0:T(8,128)(2,1)S(1)}, bf16[32,1024]{1,0:T(8,128)(2,1)S(1)}, u32[]{:S(2)}, u32[]{:S(2)}) collective-permute-start(bf16[32,1024]{1,0:T(8,128)(2,1)S(1)} %get-tuple-element.56), channel_id=1, source_target_pairs={{0,12},{4,8},{8,4},{12,0},{1,13},{5,9},{9,5},{13,1},{2,14},{6,10},... | collective-permute-start | bytes 196616 | tf_op jit(solution)/shard_map/ppermute | solution.py:624

commit v12 on v9

--- a/solution.py
+++ b/solution.py
@@ -216,6 +216,34 @@
     )
 
 
+def keep_on_core_kernel(core, span, after_ref, weight_ref, *refs):
+    held_ref, semaphore = refs[-2:]
+
+    @pl.when(lax.axis_index("fsdp") == core)
+    def _():
+        a, b = span
+        copy = pltpu.make_async_copy(weight_ref.at[lax.axis_index("groups"), a:b], held_ref, semaphore)
+        copy.start()
+        copy.wait()
+
+
+def keep_on_core(core, after, weight, span, held, name):
+    extra = [] if held is None else [held]
+    return pl.pallas_call(
+        functools.partial(keep_on_core_kernel, core, span),
+        out_shape=pltpu.VMEM((span[1] - span[0], weight.shape[2]), jnp.bfloat16),
+        in_specs=[ANYWHERE, IN_HBM] + [ON_CHIP] * len(extra),
+        out_specs=ON_CHIP,
+        input_output_aliases={2: 0} if extra else {},
+        scratch_shapes=[pltpu.SemaphoreType.DMA(())],
+        compiler_params=pltpu.CompilerParams(vmem_limit_bytes=1 << 20),
+        cost_estimate=pl.CostEstimate(
+            flops=0, transcendentals=0, bytes_accessed=2 * (span[1] - span[0]) * weight.shape[2]
+        ),
+        name=name,
+    )(after, in_hbm(weight), *extra)
+
+
 def select_kernel(
     rows_hbm, context_hbm, picked_ref, pick_ref, kind_ref, rows_ref, context_ref, semaphores
 ):
@@ -322,7 +350,7 @@
     return matches, found
 
 
-def arrange_kernel(zero_ref, three_ref, two_ref, one_ref, _, *out_refs):
+def arrange_kernel(zero_ref, three_ref, two_ref, one_ref, _, __, *out_refs):
     packed_refs = (zero_ref, one_ref, two_ref, three_ref)
     capacity = zero_ref.shape[0] // 2
     for out_ref in out_refs:
@@ -552,20 +580,21 @@
         [(up_units, units), (0, down_units)],
         "keep_up",
     )
+    down_early = keep_on_core(1, up_second, down_weight, (down_units, units), None, "keep_down_early")
     kept_slots = 3 * capacity
     own, to_far_rows, to_side_rows, to_corner_rows = call(
         arrange_kernel,
         "arrange",
         [array(kept_slots, packed_columns)] * 4,
-        [ON_CHIP] * 5,
-        [packed, *others[::-1], up_second],
+        [ON_CHIP] * 6,
+        [packed, *others[::-1], up_second, down_early],
     )
     both_axes = ("groups", "mod")
     side_far = lax.ppermute(to_corner_rows, both_axes, crossed(2, 3))
     far = lax.ppermute(to_far_rows, "groups", SWAP)
     side_own = lax.ppermute(to_side_rows, "mod", SWAP)
 
-    (down_second,) = keep_on_chip(own, [down_weight], [(down_units, units)], "keep_down")
+    down_second = keep_on_core(0, own, down_weight, (down_units, units), down_early, "keep_down")
 
     flops = 2 * rows * units * width
     gate, gathered = call(

time: 71.6 us -> 72.4 us (1.011)
    pallas_call x0 -> x2, Pallas kernels: none -> 3.47 us  [keep_on_core(): pl.pallas_call(functools.partial(keep_on_core_kernel, core, span), out_sh...]
    pallas_call x15 -> x14, Pallas kernels: 25.8 us -> 22.3 us  [call(): pl.pallas_call(kernel, out_shape=outs, in_specs=specs, out_specs=jax.tree...]
    ppermute x1, waiting for transfers between devices: 0.64 us -> 1.48 us  [paired_local(): side_own = lax.ppermute(to_side_rows, 'mod', SWAP)]
  transfers between devices with their start and end apart: 21 -> 21, of which waited for: 11 -> 14; matrix products, arithmetic and copies ran while one was open for 0% -> 0% of each run, Pallas kernels for 26% -> 25%
where the time goes in v12:
time: 72.4 us; the launch traced here: 72.2 us
  starting transfers between devices  28.6 us (40%)
  Pallas kernels  26.8 us (37%)
  waiting for transfers between devices  16.6 us (23%)
    pallas_call x14, Pallas kernels, call(): pl.pallas_call(kernel, out_shape=outs, in_specs=specs, out_specs=jax.tree...  22.3 us
    ppermute x3, starting transfers between devices, paired_local(): lax.ppermute(partial[v], 'tok', crossed(2, v))  6.44 us
    ppermute x3, starting transfers between devices, paired_local(): lax.ppermute(merged[v], 'tok', crossed(2, v))  4.45 us
    ppermute x3, starting transfers between devices, paired_local(): lax.ppermute(packed, 'tok', crossed(2, v))  4.42 us
    ppermute x3, waiting for transfers between devices, paired_local(): lax.ppermute(merged[v], 'tok', crossed(2, v))  4.33 us
    pallas_call x2, Pallas kernels, keep_on_core(): pl.pallas_call(functools.partial(keep_on_core_kernel, core, span), out_sh...  3.47 us
    ppermute x1, starting transfers between devices, paired_local(): side_far = lax.ppermute(to_corner_rows, both_axes, crossed(2, 3))  3.24 us
    ppermute x1, starting transfers between devices, paired_local(): across = lax.ppermute(picked, plane, to_second)  2.99 us
  transfers between devices with their start and end apart: 21, of which 14 were waited for; matrix products, arithmetic and copies ran while one was open for 0% of the time, Pallas kernels for 25%

profile of v12, /device:TPU:0, one launch (start us, length us, event | category | flops | bytes accessed | tf_op | source)
XLA Modules:
  0.0 72.2 jit_solution(275858746835701995)
XLA Ops:
  0.0 1.1 %select.1 = (bf16[32,1024]{1,0:T(8,128)(2,1)S(1)}, bf16[32,128]{1,0:T(8,128)(2,1)S(1)}, f32[8,128]{1,0:T(8,128)S(1)}) custom-call(s32[4,16]{1,0:T(4,128)} %rows_hbm.1, bf16[128,1024]{1,0:T(8,128)(2,1)} %context_hbm.1), custom_call_target="tpu_custom_call" | custom-call | tf_op jit(solution)/shard_map/select/pallas_call | solution.py:173
  1.1 3.0 %collective-permute-start.1 = (bf16[32,1024]{1,0:T(8,128)(2,1)S(1)}, bf16[32,1024]{1,0:T(8,128)(2,1)S(1)}, u32[]{:S(2)}, u32[]{:S(2)}) collective-permute-start(bf16[32,1024]{1,0:T(8,128)(2,1)S(1)} %get-tuple-element.34), channel_id=1, source_target_pairs={{0,2},{1,6},{2,10},{3,14},{4,3},{5,7},{6,11},{7,15},{8,0},{9,4},{1... | collective-permute-start | bytes 196616 | tf_op jit(solution)/shard_map/ppermute | solution.py:534
  4.1 0.7 collective-permute-start
  4.8 3.6 %keep_gate.1 = (bf16[1600,2048]{1,0:T(8,128)(2,1)S(1)}, bf16[1024,1024]{1,0:T(8,128)(2,1)S(1)}, f32[32,1024]{1,0:T(8,128)S(1)}) custom-call(bf16[32,128]{1,0:T(8,128)(2,1)S(1)} %get-tuple-element.31.pick_ref, bf16[128,1024]{1,0:T(8,128)(2,1)} %residual_hbm.1, bf16[2,2752,2048]{2,1,0:T(8,128)(2,1)} %bitcast.10, bf16[1024,1024]{1,0:T(8,128)(2,1)} %proj_ref.1), custom_call_target="tpu_custom_call" | custom-call | bytes 5636096 | tf_op jit(solution)/shard_map/keep_gate/pallas_call | solution.py:173
  8.4 1.0 %collective-permute-done.1.across_ref = bf16[32,1024]{1,0:T(8,128)(2,1)S(1)} collective-permute-done((bf16[32,1024]{1,0:T(8,128)(2,1)S(1)}, bf16[32,1024]{1,0:T(8,128)(2,1)S(1)}, u32[]{:S(2)}, u32[]{:S(2)}) %collective-permute-start.1) | collective-permute-done | bytes 65568 | tf_op jit(solution)/shard_map/ppermute | solution.py:534
  9.5 0.0 collective-permute-done.near_ref
  9.5 1.4 %collective-permute-start.2 = (bf16[64,1024]{1,0:T(8,128)(2,1)S(1)}, bf16[64,1024]{1,0:T(8,128)(2,1)S(1)}, u32[]{:S(2)}, u32[]{:S(2)}) collective-permute-start(bf16[64,1024]{1,0:T(8,128)(2,1)S(1)} %join.1.joined_ref), channel_id=1, source_target_pairs={{0,1},{1,0},{2,3},{3,2},{4,5},{5,4},{6,7},{7,6},{8,9},{9,8},{10,11... | collective-permute-start | bytes 393224 | tf_op jit(solution)/shard_map/ppermute | solution.py:552
  10.9 1.0 %collective-permute-done.2.other_ref = bf16[64,1024]{1,0:T(8,128)(2,1)S(1)} collective-permute-done((bf16[64,1024]{1,0:T(8,128)(2,1)S(1)}, bf16[64,1024]{1,0:T(8,128)(2,1)S(1)}, u32[]{:S(2)}, u32[]{:S(2)}) %collective-permute-start.2) | collective-permute-done | bytes 131104 | tf_op jit(solution)/shard_map/ppermute | solution.py:552
  11.9 0.4 project.1.after_ref.partial_ref
  12.4 2.0 %collective-permute-start.5 = (bf16[32,1024]{1,0:T(8,128)(2,1)S(1)}, bf16[32,1024]{1,0:T(8,128)(2,1)S(1)}, u32[]{:S(2)}, u32[]{:S(2)}) collective-permute-start(bf16[32,1024]{1,0:T(8,128)(2,1)S(1)} %get-tuple-element.57), channel_id=1, source_target_pairs={{0,4},{4,0},{8,12},{12,8},{1,5},{5,1},{9,13},{13,9},{2,6},{6,2},{1... | collective-permute-start | bytes 196616 | tf_op jit(solution)/shard_map/ppermute | solution.py:561
  14.4 4.4 %collective-permute-start.4 = (bf16[32,1024]{1,0:T(8,128)(2,1)S(1)}, bf16[32,1024]{1,0:T(8,128)(2,1)S(1)}, u32[]{:S(2)}, u32[]{:S(2)}) collective-permute-start(bf16[32,1024]{1,0:T(8,128)(2,1)S(1)} %get-tuple-element.58), channel_id=1, source_target_pairs={{0,8},{4,12},{8,0},{12,4},{1,9},{5,13},{9,1},{13,5},{2,10},{6,14},... | collective-permute-start | bytes 196616 | tf_op jit(solution)/shard_map/ppermute | solution.py:561
  18.8 3.8 %keep_more.1 = (bf16[1152,2048]{1,0:T(8,128)(2,1)S(1)}, bf16[1136,2048]{1,0:T(8,128)(2,1)S(1)}) custom-call(bf16[4,32,1024]{2,1,0:T(8,128)(2,1)S(1)} %project.1.after_ref.partial_ref, bf16[2,2752,2048]{2,1,0:T(8,128)(2,1)} %bitcast.11, bf16[2,2752,2048]{2,1,0:T(8,128)(2,1)} %bitcast.12), custom_call_target="tpu_custom_call" | custom-call | bytes 9371648 | tf_op jit(solution)/shard_map/keep_more/pallas_call | solution.py:173
  22.6 0.2 collective-permute-done.4.two_ref
  22.9 2.1 %collective-permute-done.3.three_ref = bf16[32,1024]{1,0:T(8,128)(2,1)S(1)} collective-permute-done((bf16[32,1024]{1,0:T(8,128)(2,1)S(1)}, bf16[32,1024]{1,0:T(8,128)(2,1)S(1)}, u32[]{:S(2)}, u32[]{:S(2)}) %collective-permute-start.3) | collective-permute-done | bytes 65568 | tf_op jit(solution)/shard_map/ppermute | solution.py:561
  25.0 0.2 norm.1.after_ref.zero_ref
  25.2 0.8 %collective-permute-start.8 = (bf16[32,1152]{1,0:T(8,128)(2,1)S(1)}, bf16[32,1152]{1,0:T(8,128)(2,1)S(1)}, u32[]{:S(2)}, u32[]{:S(2)}) collective-permute-start(bf16[32,1152]{1,0:T(8,128)(2,1)S(1)} %norm.1.after_ref.zero_ref), channel_id=1, source_target_pairs={{0,4},{4,0},{8,12},{12,8},{1,5},{5,1},{9,13},{13,9},{2,6},{6,2},{1... | collective-permute-start | bytes 221192 | tf_op jit(solution)/shard_map/ppermute | solution.py:576
  26.0 1.7 %collective-permute-start.7 = (bf16[32,1152]{1,0:T(8,128)(2,1)S(1)}, bf16[32,1152]{1,0:T(8,128)(2,1)S(1)}, u32[]{:S(2)}, u32[]{:S(2)}) collective-permute-start(bf16[32,1152]{1,0:T(8,128)(2,1)S(1)} %norm.1.after_ref.zero_ref), channel_id=1, source_target_pairs={{0,8},{4,12},{8,0},{12,4},{1,9},{5,13},{9,1},{13,5},{2,10},{6,14},... | collective-permute-start | bytes 221192 | tf_op jit(solution)/shard_map/ppermute | solution.py:576
  27.7 1.9 %collective-permute-start.6 = (bf16[32,1152]{1,0:T(8,128)(2,1)S(1)}, bf16[32,1152]{1,0:T(8,128)(2,1)S(1)}, u32[]{:S(2)}, u32[]{:S(2)}) collective-permute-start(bf16[32,1152]{1,0:T(8,128)(2,1)S(1)} %norm.1.after_ref.zero_ref), channel_id=1, source_target_pairs={{0,12},{4,8},{8,4},{12,0},{1,13},{5,9},{9,5},{13,1},{2,14},{6,10},... | collective-permute-start | bytes 221192 | tf_op jit(solution)/shard_map/ppermute | solution.py:576
  29.7 3.7 %keep_up.1 = (bf16[1616,2048]{1,0:T(8,128)(2,1)S(1)}, bf16[656,2048]{1,0:T(8,128)(2,1)S(1)}) custom-call(bf16[32,1152]{1,0:T(8,128)(2,1)S(1)} %norm.1.after_ref.zero_ref, bf16[2,2752,2048]{2,1,0:T(8,128)(2,1)} %bitcast.13, bf16[2,2752,2048]{2,1,0:T(8,128)(2,1)} %weight_ref.3), custom_call_target="tpu_custom_call" | custom-call | bytes 9306112 | tf_op jit(solution)/shard_map/keep_up/pallas_call | solution.py:173
  33.4 0.6 collective-permute-done.6.three_ref
  34.0 0.2 arrange.1
  34.2 3.2 %collective-permute-start.9 = (bf16[48,1152]{1,0:T(8,128)(2,1)S(1)}, bf16[48,1152]{1,0:T(8,128)(2,1)S(1)}, u32[]{:S(2)}, u32[]{:S(2)}) collective-permute-start(bf16[48,1152]{1,0:T(8,128)(2,1)S(1)} %get-tuple-element.39), channel_id=1, source_target_pairs={{0,18},{2,16},{16,2},{18,0},{1,19},{3,17},{17,3},{19,1},{4,22},{6,... | collective-permute-start | bytes 331784 | tf_op jit(solution)/shard_map/ppermute | solution.py:593
  37.4 0.6 collective-permute-start.11
  38.0 3.4 %keep_down.1.refs_2_.second_ref = bf16[2096,2048]{1,0:T(8,128)(2,1)S(1)} custom-call(bf16[48,1152]{1,0:T(8,128)(2,1)S(1)} %get-tuple-element.42.after_ref.own_ref, bf16[2,2752,2048]{2,1,0:T(8,128)(2,1)} %weight_ref.3, bf16[2096,2048]{1,0:T(8,128)(2,1)S(1)} %keep_down_early.1.__.refs_0_), custom_call_target="tpu_custom_call", output_to_operand_aliasing={{}: (2, {})} | custom-call | bytes 8585216 | tf_op jit(solution)/shard_map/keep_down/pallas_call | solution.py:232
  41.5 1.5 %collective-permute-done.10.side_own_ref = bf16[48,1152]{1,0:T(8,128)(2,1)S(1)} collective-permute-done((bf16[48,1152]{1,0:T(8,128)(2,1)S(1)}, bf16[48,1152]{1,0:T(8,128)(2,1)S(1)}, u32[]{:S(2)}, u32[]{:S(2)}) %collective-permute-start.10) | collective-permute-done | bytes 110624 | tf_op jit(solution)/shard_map/ppermute | solution.py:595
  43.0 0.6 collective-permute-done.11.far_ref
  43.5 3.1 %gate.1 = (bf16[2768,128]{1,0:T(8,128)(2,1)S(1)}, bf16[128,2048]{1,0:T(8,128)(2,1)S(1)}) custom-call(bf16[48,1152]{1,0:T(8,128)(2,1)S(1)} %collective-permute-done.9.side_far_ref, bf16[48,1152]{1,0:T(8,128)(2,1)S(1)} %collective-permute-done.10.side_own_ref, bf16[48,1152]{1,0:T(8,128)(2,1)S(1)} %collective-permute-done.11.far_ref, ...), custom_call_target="tpu_custom_call" | custom-call | flops 1442840576 | tf_op jit(solution)/shard_map/gate/pallas_call | solution.py:173
  46.7 0.1 collective-permute-start.12
  46.8 2.4 %up.2.up_ref = bf16[2064,128]{1,0:T(8,128)(2,1)S(1)} custom-call(bf16[128,2048]{1,0:T(8,128)(2,1)S(1)} %get-tuple-element.47.rows_ref, bf16[1136,2048]{1,0:T(8,128)(2,1)S(1)} %get-tuple-element.37._.refs_0_, bf16[1616,2048]{1,0:T(8,128)(2,1)S(1)} %get-tuple-element.38.after_ref._.refs_1_.refs_0_), custom_call_target="tpu_custom_call" | custom-call | flops 1082130432 | tf_op jit(solution)/shard_map/up/pallas_call | solution.py:173
  49.1 0.5 collective-permute-start.13
  49.7 0.9 %up.3.up_late_ref = bf16[688,128]{1,0:T(8,128)(2,1)S(1)} custom-call(bf16[128,2048]{1,0:T(8,128)(2,1)S(1)} %get-tuple-element.47.rows_ref, bf16[1616,2048]{1,0:T(8,128)(2,1)S(1)} %get-tuple-element.38.after_ref._.refs_1_.refs_0_), custom_call_target="tpu_custom_call" | custom-call | flops 360710144 | tf_op jit(solution)/shard_map/up/pallas_call | solution.py:173
  50.6 0.1 collective-permute-start.14
  50.7 0.5 silu.1
  51.2 0.8 %collective-permute-done.14.other_late_ref = bf16[688,128]{1,0:T(8,128)(2,1)S(1)} collective-permute-done((bf16[688,128]{1,0:T(8,128)(2,1)S(1)}, bf16[688,128]{1,0:T(8,128)(2,1)S(1)}, u32[]{:S(2)}, u32[]{:S(2)}) %collective-permute-start.14) | collective-permute-done | bytes 176160 | tf_op jit(solution)/shard_map/ppermute | solution.py:625
  52.0 2.2 %down.1 = (bf16[48,1024]{1,0:T(8,128)(2,1)S(1)}, bf16[48,1024]{1,0:T(8,128)(2,1)S(1)}, bf16[48,1024]{1,0:T(8,128)(2,1)S(1)}, bf16[48,1024]{1,0:T(8,128)(2,1)S(1)}) custom-call(f32[2752,128]{1,0:T(8,128)S(1)} %get-tuple-element.45.silu_ref, f32[8,128]{1,0:T(8,128)S(1)} %get-tuple-element.46.stat_ref, bf16[2064,128]{1,0:T(8,128)(2,1)S(1)} %up.2.up_ref, ...), custom_call_target="tpu_custom_call" | custom-call | flops 1442840576 | tf_op jit(solution)/shard_map/down/pallas_call | solution.py:173
  54.3 2.7 %collective-permute-start.15 = (bf16[48,1024]{1,0:T(8,128)(2,1)S(1)}, bf16[48,1024]{1,0:T(8,128)(2,1)S(1)}, u32[]{:S(2)}, u32[]{:S(2)}) collective-permute-start(bf16[48,1024]{1,0:T(8,128)(2,1)S(1)} %get-tuple-element.49), channel_id=1, source_target_pairs={{0,18},{2,16},{16,2},{18,0},{1,19},{3,17},{17,3},{19,1},{4,22},{6,... | collective-permute-start | bytes 294920 | tf_op jit(solution)/shard_map/ppermute | solution.py:643
  57.0 0.8 %collective-permute-start.17 = (bf16[48,1024]{1,0:T(8,128)(2,1)S(1)}, bf16[48,1024]{1,0:T(8,128)(2,1)S(1)}, u32[]{:S(2)}, u32[]{:S(2)}) collective-permute-start(bf16[48,1024]{1,0:T(8,128)(2,1)S(1)} %get-tuple-element.51), channel_id=1, source_target_pairs={{0,16},{16,0},{1,17},{17,1},{2,18},{18,2},{3,19},{19,3},{4,20},{20... | collective-permute-start | bytes 294920 | tf_op jit(solution)/shard_map/ppermute | solution.py:644
  57.8 2.9 %collective-permute-done.15.side_far_ref = bf16[48,1024]{1,0:T(8,128)(2,1)S(1)} collective-permute-done((bf16[48,1024]{1,0:T(8,128)(2,1)S(1)}, bf16[48,1024]{1,0:T(8,128)(2,1)S(1)}, u32[]{:S(2)}, u32[]{:S(2)}) %collective-permute-start.15) | collective-permute-done | bytes 98336 | tf_op jit(solution)/shard_map/ppermute | solution.py:643
  60.8 0.9 %collective-permute-done.16.side_ref = bf16[48,1024]{1,0:T(8,128)(2,1)S(1)} collective-permute-done((bf16[48,1024]{1,0:T(8,128)(2,1)S(1)}, bf16[48,1024]{1,0:T(8,128)(2,1)S(1)}, u32[]{:S(2)}, u32[]{:S(2)}) %collective-permute-start.16) | collective-permute-done | bytes 98336 | tf_op jit(solution)/shard_map/ppermute | solution.py:645
  61.6 0.6 collective-permute-done.17.far_ref
  62.2 0.2 merge.1
  62.4 0.8 %collective-permute-start.18 = (bf16[32,1024]{1,0:T(8,128)(2,1)S(1)}, bf16[32,1024]{1,0:T(8,128)(2,1)S(1)}, u32[]{:S(2)}, u32[]{:S(2)}) collective-permute-start(bf16[32,1024]{1,0:T(8,128)(2,1)S(1)} %get-tuple-element.54), channel_id=1, source_target_pairs={{0,4},{4,0},{8,12},{12,8},{1,5},{5,1},{9,13},{13,9},{2,6},{6,2},{1... | collective-permute-start | bytes 196616 | tf_op jit(solution)/shard_map/ppermute | solution.py:653
  63.2 1.8 %collective-permute-start.19 = (bf16[32,1024]{1,0:T(8,128)(2,1)S(1)}, bf16[32,1024]{1,0:T(8,128)(2,1)S(1)}, u32[]{:S(2)}, u32[]{:S(2)}) collective-permute-start(bf16[32,1024]{1,0:T(8,128)(2,1)S(1)} %get-tuple-element.55), channel_id=1, source_target_pairs={{0,8},{4,12},{8,0},{12,4},{1,9},{5,13},{9,1},{13,5},{2,10},{6,14},... | collective-permute-start | bytes 196616 | tf_op jit(solution)/shard_map/ppermute | solution.py:653
  65.0 1.8 %collective-permute-start.20 = (bf16[32,1024]{1,0:T(8,128)(2,1)S(1)}, bf16[32,1024]{1,0:T(8,128)(2,1)S(1)}, u32[]{:S(2)}, u32[]{:S(2)}) collective-permute-start(bf16[32,1024]{1,0:T(8,128)(2,1)S(1)} %get-tuple-element.56), channel_id=1, source_target_pairs={{0,12},{4,8},{8,4},{12,0},{1,13},{5,9},{9,5},{13,1},{2,14},{6,10},... | collective-permute-start | bytes 196616 | tf_op jit(solution)/shard_map/ppermute | solution.py:653
  66.8 0.5 collective-permute-done.18.one_ref
  67.4 2.8 %collective-permute-done.19.two_ref = bf16[32,1024]{1,0:T(8,128)(2,1)S(1)} collective-permute-done((bf16[32,1024]{1,0:T(8,128)(2,1)S(1)}, bf16[32,1024]{1,0:T(8,128)(2,1)S(1)}, u32[]{:S(2)}, u32[]{:S(2)}) %collective-permute-start.19) | collective-permute-done | bytes 65568 | tf_op jit(solution)/shard_map/ppermute | solution.py:653
  70.2 1.0 %collective-permute-done.20.three_ref = bf16[32,1024]{1,0:T(8,128)(2,1)S(1)} collective-permute-done((bf16[32,1024]{1,0:T(8,128)(2,1)S(1)}, bf16[32,1024]{1,0:T(8,128)(2,1)S(1)}, u32[]{:S(2)}, u32[]{:S(2)}) %collective-permute-start.20) | collective-permute-done | bytes 65568 | tf_op jit(solution)/shard_map/ppermute | solution.py:653
  71.2 1.0 %scatter.1 = bf16[128,1024]{1,0:T(8,128)(2,1)} custom-call(bf16[32,128]{1,0:T(8,128)(2,1)S(1)} %get-tuple-element.31.pick_ref, bf16[32,1024]{1,0:T(8,128)(2,1)S(1)} %get-tuple-element.53.zero_ref, bf16[32,1024]{1,0:T(8,128)(2,1)S(1)} %collective-permute-done.18.one_ref, bf16[32,1024]{1,0:T(8,128)(2,1)S(1)} %collective-permute-done.19.two_ref, ...), custom_call_target="tpu_custom_call" | custom-call | tf_op jit(solution)/shard_map/scatter/pallas_call | solution.py:654
  (16 shorter events, 0.1 us)
Async XLA Ops:
  1.1 8.3 %collective-permute-start.1 = (bf16[32,1024]{1,0:T(8,128)(2,1)S(1)}, bf16[32,1024]{1,0:T(8,128)(2,1)S(1)}, u32[]{:S(2)}, u32[]{:S(2)}) collective-permute-start(bf16[32,1024]{1,0:T(8,128)(2,1)S(1)} %get-tuple-element.34), channel_id=1, source_target_pairs={{0,2},{1,6},{2,10},{3,14},{4,3},{5,7},{6,11},{7,15},{8,0},{9,4},{1... | collective-permute-start | bytes 196616 | tf_op jit(solution)/shard_map/ppermute | solution.py:534
  4.1 5.3 %collective-permute-start = (bf16[32,1024]{1,0:T(8,128)(2,1)S(1)}, bf16[32,1024]{1,0:T(8,128)(2,1)S(1)}, u32[]{:S(2)}, u32[]{:S(2)}) collective-permute-start(bf16[32,1024]{1,0:T(8,128)(2,1)S(1)} %get-tuple-element.34), channel_id=1, source_target_pairs={{0,0},{1,4},{2,8},{3,12},{4,1},{5,5},{6,9},{7,13},{8,2},{9,6},{10,... | collective-permute-start | bytes 196616 | tf_op jit(solution)/shard_map/ppermute | solution.py:535
  9.5 2.4 %collective-permute-start.2 = (bf16[64,1024]{1,0:T(8,128)(2,1)S(1)}, bf16[64,1024]{1,0:T(8,128)(2,1)S(1)}, u32[]{:S(2)}, u32[]{:S(2)}) collective-permute-start(bf16[64,1024]{1,0:T(8,128)(2,1)S(1)} %join.1.joined_ref), channel_id=1, source_target_pairs={{0,1},{1,0},{2,3},{3,2},{4,5},{5,4},{6,7},{7,6},{8,9},{9,8},{10,11... | collective-permute-start | bytes 393224 | tf_op jit(solution)/shard_map/ppermute | solution.py:552
  12.4 10.2 %collective-permute-start.5 = (bf16[32,1024]{1,0:T(8,128)(2,1)S(1)}, bf16[32,1024]{1,0:T(8,128)(2,1)S(1)}, u32[]{:S(2)}, u32[]{:S(2)}) collective-permute-start(bf16[32,1024]{1,0:T(8,128)(2,1)S(1)} %get-tuple-element.57), channel_id=1, source_target_pairs={{0,4},{4,0},{8,12},{12,8},{1,5},{5,1},{9,13},{13,9},{2,6},{6,2},{1... | collective-permute-start | bytes 196616 | tf_op jit(solution)/shard_map/ppermute | solution.py:561
  14.4 8.4 %collective-permute-start.4 = (bf16[32,1024]{1,0:T(8,128)(2,1)S(1)}, bf16[32,1024]{1,0:T(8,128)(2,1)S(1)}, u32[]{:S(2)}, u32[]{:S(2)}) collective-permute-start(bf16[32,1024]{1,0:T(8,128)(2,1)S(1)} %get-tuple-element.58), channel_id=1, source_target_pairs={{0,8},{4,12},{8,0},{12,4},{1,9},{5,13},{9,1},{13,5},{2,10},{6,14},... | collective-permute-start | bytes 196616 | tf_op jit(solution)/shard_map/ppermute | solution.py:561
  18.8 6.2 %collective-permute-start.3 = (bf16[32,1024]{1,0:T(8,128)(2,1)S(1)}, bf16[32,1024]{1,0:T(8,128)(2,1)S(1)}, u32[]{:S(2)}, u32[]{:S(2)}) collective-permute-start(bf16[32,1024]{1,0:T(8,128)(2,1)S(1)} %get-tuple-element.59), channel_id=1, source_target_pairs={{0,12},{4,8},{8,4},{12,0},{1,13},{5,9},{9,5},{13,1},{2,14},{6,10},... | collective-permute-start | bytes 196616 | tf_op jit(solution)/shard_map/ppermute | solution.py:561
  18.8 6.2 %copy-start = (bf16[1024,4]{0,1:T(4,128)(2,1)S(1)}, bf16[1024,4]{0,1:T(4,128)(2,1)}, u32[]{:S(2)}) copy-start(bf16[1024,4]{0,1:T(4,128)(2,1)} %param.14) | copy-start | bytes 24580
  18.8 6.2 %copy-start.1 = (bf16[2,1024]{1,0:T(2,128)(2,1)S(1)}, bf16[2,1024]{1,0:T(2,128)(2,1)}, u32[]{:S(2)}) copy-start(bf16[2,1024]{1,0:T(2,128)(2,1)} %gain_ref.1) | copy-start | bytes 12292
  25.2 8.1 %collective-permute-start.8 = (bf16[32,1152]{1,0:T(8,128)(2,1)S(1)}, bf16[32,1152]{1,0:T(8,128)(2,1)S(1)}, u32[]{:S(2)}, u32[]{:S(2)}) collective-permute-start(bf16[32,1152]{1,0:T(8,128)(2,1)S(1)} %norm.1.after_ref.zero_ref), channel_id=1, source_target_pairs={{0,4},{4,0},{8,12},{12,8},{1,5},{5,1},{9,13},{13,9},{2,6},{6,2},{1... | collective-permute-start | bytes 221192 | tf_op jit(solution)/shard_map/ppermute | solution.py:576
  26.0 7.3 %collective-permute-start.7 = (bf16[32,1152]{1,0:T(8,128)(2,1)S(1)}, bf16[32,1152]{1,0:T(8,128)(2,1)S(1)}, u32[]{:S(2)}, u32[]{:S(2)}) collective-permute-start(bf16[32,1152]{1,0:T(8,128)(2,1)S(1)} %norm.1.after_ref.zero_ref), channel_id=1, source_target_pairs={{0,8},{4,12},{8,0},{12,4},{1,9},{5,13},{9,1},{13,5},{2,10},{6,14},... | collective-permute-start | bytes 221192 | tf_op jit(solution)/shard_map/ppermute | solution.py:576
  27.7 6.3 %collective-permute-start.6 = (bf16[32,1152]{1,0:T(8,128)(2,1)S(1)}, bf16[32,1152]{1,0:T(8,128)(2,1)S(1)}, u32[]{:S(2)}, u32[]{:S(2)}) collective-permute-start(bf16[32,1152]{1,0:T(8,128)(2,1)S(1)} %norm.1.after_ref.zero_ref), channel_id=1, source_target_pairs={{0,12},{4,8},{8,4},{12,0},{1,13},{5,9},{9,5},{13,1},{2,14},{6,10},... | collective-permute-start | bytes 221192 | tf_op jit(solution)/shard_map/ppermute | solution.py:576
  34.2 7.3 %collective-permute-start.9 = (bf16[48,1152]{1,0:T(8,128)(2,1)S(1)}, bf16[48,1152]{1,0:T(8,128)(2,1)S(1)}, u32[]{:S(2)}, u32[]{:S(2)}) collective-permute-start(bf16[48,1152]{1,0:T(8,128)(2,1)S(1)} %get-tuple-element.39), channel_id=1, source_target_pairs={{0,18},{2,16},{16,2},{18,0},{1,19},{3,17},{17,3},{19,1},{4,22},{6,... | collective-permute-start | bytes 331784 | tf_op jit(solution)/shard_map/ppermute | solution.py:593
  37.4 5.6 %collective-permute-start.10 = (bf16[48,1152]{1,0:T(8,128)(2,1)S(1)}, bf16[48,1152]{1,0:T(8,128)(2,1)S(1)}, u32[]{:S(2)}, u32[]{:S(2)}) collective-permute-start(bf16[48,1152]{1,0:T(8,128)(2,1)S(1)} %get-tuple-element.40), channel_id=1, source_target_pairs={{0,2},{2,0},{1,3},{3,1},{4,6},{6,4},{5,7},{7,5},{8,10},{10,8},{9,1... | collective-permute-start | bytes 331784 | tf_op jit(solution)/shard_map/ppermute | solution.py:595
  37.4 6.1 %collective-permute-start.11 = (bf16[48,1152]{1,0:T(8,128)(2,1)S(1)}, bf16[48,1152]{1,0:T(8,128)(2,1)S(1)}, u32[]{:S(2)}, u32[]{:S(2)}) collective-permute-start(bf16[48,1152]{1,0:T(8,128)(2,1)S(1)} %get-tuple-element.41), channel_id=1, source_target_pairs={{0,16},{16,0},{1,17},{17,1},{2,18},{18,2},{3,19},{19,3},{4,20},{20... | collective-permute-start | bytes 331784 | tf_op jit(solution)/shard_map/ppermute | solution.py:594
  46.7 4.0 %collective-permute-start.12 = (bf16[2768,128]{1,0:T(8,128)(2,1)S(1)}, bf16[2768,128]{1,0:T(8,128)(2,1)S(1)}, u32[]{:S(2)}, u32[]{:S(2)}) collective-permute-start(bf16[2768,128]{1,0:T(8,128)(2,1)S(1)} %get-tuple-element.44.gate_ref), channel_id=1, source_target_pairs={{0,1},{1,0},{2,3},{3,2},{4,5},{5,4},{6,7},{7,6},{8,9},{9,8},{10,11... | collective-permute-start | bytes 2125832 | tf_op jit(solution)/shard_map/ppermute | solution.py:624
  49.1 2.9 %collective-permute-start.13 = (bf16[2064,128]{1,0:T(8,128)(2,1)S(1)}, bf16[2064,128]{1,0:T(8,128)(2,1)S(1)}, u32[]{:S(2)}, u32[]{:S(2)}) collective-permute-start(bf16[2064,128]{1,0:T(8,128)(2,1)S(1)} %up.2.up_ref), channel_id=1, source_target_pairs={{0,1},{1,0},{2,3},{3,2},{4,5},{5,4},{6,7},{7,6},{8,9},{9,8},{10,11... | collective-permute-start | bytes 1585160 | tf_op jit(solution)/shard_map/ppermute | solution.py:625
  50.6 1.5 %collective-permute-start.14 = (bf16[688,128]{1,0:T(8,128)(2,1)S(1)}, bf16[688,128]{1,0:T(8,128)(2,1)S(1)}, u32[]{:S(2)}, u32[]{:S(2)}) collective-permute-start(bf16[688,128]{1,0:T(8,128)(2,1)S(1)} %up.3.up_late_ref), channel_id=1, source_target_pairs={{0,1},{1,0},{2,3},{3,2},{4,5},{5,4},{6,7},{7,6},{8,9},{9,8},{10,11... | collective-permute-start | bytes 528392 | tf_op jit(solution)/shard_map/ppermute | solution.py:625
  54.3 6.5 %collective-permute-start.15 = (bf16[48,1024]{1,0:T(8,128)(2,1)S(1)}, bf16[48,1024]{1,0:T(8,128)(2,1)S(1)}, u32[]{:S(2)}, u32[]{:S(2)}) collective-permute-start(bf16[48,1024]{1,0:T(8,128)(2,1)S(1)} %get-tuple-element.49), channel_id=1, source_target_pairs={{0,18},{2,16},{16,2},{18,0},{1,19},{3,17},{17,3},{19,1},{4,22},{6,... | collective-permute-start | bytes 294920 | tf_op jit(solution)/shard_map/ppermute | solution.py:643
  57.0 4.6 %collective-permute-start.16 = (bf16[48,1024]{1,0:T(8,128)(2,1)S(1)}, bf16[48,1024]{1,0:T(8,128)(2,1)S(1)}, u32[]{:S(2)}, u32[]{:S(2)}) collective-permute-start(bf16[48,1024]{1,0:T(8,128)(2,1)S(1)} %get-tuple-element.50), channel_id=1, source_target_pairs={{0,2},{2,0},{1,3},{3,1},{4,6},{6,4},{5,7},{7,5},{8,10},{10,8},{9,1... | collective-permute-start | bytes 294920 | tf_op jit(solution)/shard_map/ppermute | solution.py:645
  57.0 5.2 %collective-permute-start.17 = (bf16[48,1024]{1,0:T(8,128)(2,1)S(1)}, bf16[48,1024]{1,0:T(8,128)(2,1)S(1)}, u32[]{:S(2)}, u32[]{:S(2)}) collective-permute-start(bf16[48,1024]{1,0:T(8,128)(2,1)S(1)} %get-tuple-element.51), channel_id=1, source_target_pairs={{0,16},{16,0},{1,17},{17,1},{2,18},{18,2},{3,19},{19,3},{4,20},{20... | collective-permute-start | bytes 294920 | tf_op jit(solution)/shard_map/ppermute | solution.py:644
  62.4 5.0 %collective-permute-start.18 = (bf16[32,1024]{1,0:T(8,128)(2,1)S(1)}, bf16[32,1024]{1,0:T(8,128)(2,1)S(1)}, u32[]{:S(2)}, u32[]{:S(2)}) collective-permute-start(bf16[32,1024]{1,0:T(8,128)(2,1)S(1)} %get-tuple-element.54), channel_id=1, source_target_pairs={{0,4},{4,0},{8,12},{12,8},{1,5},{5,1},{9,13},{13,9},{2,6},{6,2},{1... | collective-permute-start | bytes 196616 | tf_op jit(solution)/shard_map/ppermute | solution.py:653
  63.2 7.0 %collective-permute-start.19 = (bf16[32,1024]{1,0:T(8,128)(2,1)S(1)}, bf16[32,1024]{1,0:T(8,128)(2,1)S(1)}, u32[]{:S(2)}, u32[]{:S(2)}) collective-permute-start(bf16[32,1024]{1,0:T(8,128)(2,1)S(1)} %get-tuple-element.55), channel_id=1, source_target_pairs={{0,8},{4,12},{8,0},{12,4},{1,9},{5,13},{9,1},{13,5},{2,10},{6,14},... | collective-permute-start | bytes 196616 | tf_op jit(solution)/shard_map/ppermute | solution.py:653
  65.0 6.2 %collective-permute-start.20 = (bf16[32,1024]{1,0:T(8,128)(2,1)S(1)}, bf16[32,1024]{1,0:T(8,128)(2,1)S(1)}, u32[]{:S(2)}, u32[]{:S(2)}) collective-permute-start(bf16[32,1024]{1,0:T(8,128)(2,1)S(1)} %get-tuple-element.56), channel_id=1, source_target_pairs={{0,12},{4,8},{8,4},{12,0},{1,13},{5,9},{9,5},{13,1},{2,14},{6,10},... | collective-permute-start | bytes 196616 | tf_op jit(solution)/shard_map/ppermute | solution.py:653

commit v13 on v11

--- a/solution.py
+++ b/solution.py
@@ -384,8 +384,9 @@
     weights_times_rows(refs[:-1], spans, rows_ref[...], refs[-1])
 
 
-def silu_kernel(gate_ref, gate_other_ref, out_ref, stat_ref):
-    units = out_ref.shape[0]
+def activation_kernel(gate_ref, gate_other_ref, up_ref, up_other_ref, act_ref, silu_ref, stat_ref):
+    early = act_ref.shape[0]
+    units = early + silu_ref.shape[0]
     stat = gate_ref[units:, :].astype(jnp.float32) + gate_other_ref[units:, :].astype(jnp.float32)
     inverse = lax.rsqrt((stat[0:1] + stat[1:2]) / D + 1e-05)
     logits = (stat[2:3] + stat[3:4]) * inverse
@@ -396,22 +397,25 @@
         stop = min(start + STRIP, units)
         gate = gate_ref[start:stop, :].astype(jnp.float32) + gate_other_ref[start:stop, :].astype(jnp.float32)
         gate = gate * inverse
-        out_ref[start:stop, :] = gate / (1.0 + jnp.exp(-gate)) * inverse
+        silu = gate / (1.0 + jnp.exp(-gate)) * inverse
+        inside = max(0, min(stop, early) - start)
+        if inside:
+            span = slice(start, start + inside)
+            up = up_ref[span, :].astype(jnp.float32) + up_other_ref[span, :].astype(jnp.float32)
+            act_ref[span, :] = (silu[:inside] * up).astype(jnp.bfloat16)
+        if start + inside < stop:
+            silu_ref[start + inside - early : stop - early, :] = silu[inside:]
 
 
 def down_kernel(
-    silu_ref, stat_ref, up_ref, up_late_ref, other_ref, other_late_ref, first_ref, second_ref,
+    act_early_ref, silu_ref, stat_ref, up_ref, other_ref, first_ref, second_ref,
     kept_ref, far_ref, side_ref, side_far_ref, act_ref,
 ):
     units, rows = act_ref.shape
-    at = 0
-    for mine_ref, got_ref in ((up_ref, other_ref), (up_late_ref, other_late_ref)):
-        for start in range(0, mine_ref.shape[0], STRIP):
-            stop = min(start + STRIP, mine_ref.shape[0])
-            up = mine_ref[start:stop, :].astype(jnp.float32) + got_ref[start:stop, :].astype(jnp.float32)
-            span = slice(at, at + stop - start)
-            act_ref[span, :] = (silu_ref[span, :] * up).astype(jnp.bfloat16)
-            at += stop - start
+    early = act_early_ref.shape[0]
+    act_ref[:early, :] = act_early_ref[...]
+    up = up_ref[...].astype(jnp.float32) + other_ref[...].astype(jnp.float32)
+    act_ref[early:, :] = (silu_ref[...] * up).astype(jnp.bfloat16)
     half, columns = kept_ref.shape
     score = jnp.broadcast_to(stat_ref[1:2, :], (rows, rows)).T[:, 0:1]
     first_units = first_ref.shape[0]
@@ -505,7 +509,7 @@
     to_second = [(t * 4 + q, q * 4 + (t ^ 2)) for t in range(4) for q in range(4)]
     across = lax.ppermute(picked, plane, to_second)
     near = lax.ppermute(picked, plane, to_first)
-    gate_units, up_units, down_units = [round(units * part / TILE) * TILE for part in (0.49, 0.45, 0.3)]
+    gate_units, up_units, down_units = [round(units * part / TILE) * TILE for part in (0.54, 0.44, 0.27)]
     gate_first, proj_held, rest = call(
         keep_gate_kernel,
         "keep_gate",
@@ -594,20 +598,24 @@
     ]
     gate_other = lax.ppermute(gate, "fsdp", SWAP)
     up_others = [lax.ppermute(part, "fsdp", SWAP) for part in up_parts]
-    silu, stat = call(
-        silu_kernel,
-        "silu",
-        [array(units, rows, dtype=jnp.float32), array(8, rows, dtype=jnp.float32)],
-        [ON_CHIP] * 2,
-        [gate, gate_other],
+    act_early, silu_late, stat = call(
+        activation_kernel,
+        "activation",
+        [
+            array(units - late, rows),
+            array(late, rows, dtype=jnp.float32),
+            array(8, rows, dtype=jnp.float32),
+        ],
+        [ON_CHIP] * 4,
+        [gate, gate_other, up_parts[0], up_others[0]],
         moved=8 * units * rows,
     )
     kept, to_far, to_side, to_side_far = call(
         down_kernel,
         "down",
         [array(kept_slots, columns)] * 4,
-        [ON_CHIP] * 8,
-        [silu, stat, *up_parts, *up_others, down_first, down_second],
+        [ON_CHIP] * 7,
+        [act_early, silu_late, stat, up_parts[1], up_others[1], down_first, down_second],
         scratch=[pltpu.VMEM((units, rows), jnp.bfloat16)],
         flops=flops,
     )

time: 71.8 us -> 71.5 us (level)
  transfers between devices with their start and end apart: 21 -> 21, of which waited for: 11 -> 12; matrix products, arithmetic and copies ran while one was open for 0% -> 0% of each run, Pallas kernels for 26% -> 26%
where the time goes in v13:
time: 71.5 us; the launch traced here: 71.4 us
  starting transfers between devices  28.6 us (40%)
  Pallas kernels  26.8 us (37%)
  waiting for transfers between devices  15.7 us (22%)
    pallas_call x15, Pallas kernels, call(): pl.pallas_call(kernel, out_shape=outs, in_specs=specs, out_specs=jax.tree...  25.8 us
    ppermute x3, starting transfers between devices, paired_local(): lax.ppermute(partial[v], 'tok', crossed(2, v))  6.31 us
    ppermute x3, starting transfers between devices, paired_local(): lax.ppermute(merged[v], 'tok', crossed(2, v))  4.45 us
    ppermute x3, starting transfers between devices, paired_local(): lax.ppermute(packed, 'tok', crossed(2, v))  4.42 us
    ppermute x3, waiting for transfers between devices, paired_local(): lax.ppermute(merged[v], 'tok', crossed(2, v))  4.13 us
    ppermute x1, waiting for transfers between devices, paired_local(): from_far = lax.ppermute(to_far, 'groups', SWAP)  3.57 us
    ppermute x1, starting transfers between devices, paired_local(): side_far = lax.ppermute(to_corner_rows, both_axes, crossed(2, 3))  3.38 us
    ppermute x1, starting transfers between devices, paired_local(): across = lax.ppermute(picked, plane, to_second)  2.99 us
  transfers between devices with their start and end apart: 21, of which 12 were waited for; matrix products, arithmetic and copies ran while one was open for 0% of the time, Pallas kernels for 26%

profile of v13, /device:TPU:0, one launch (start us, length us, event | category | flops | bytes accessed | tf_op | source)
XLA Modules:
  0.0 71.4 jit_solution(12150279617091364252)
XLA Ops:
  0.0 1.1 %select.1 = (bf16[32,1024]{1,0:T(8,128)(2,1)S(1)}, bf16[32,128]{1,0:T(8,128)(2,1)S(1)}, f32[8,128]{1,0:T(8,128)S(1)}) custom-call(s32[4,16]{1,0:T(4,128)} %rows_hbm.1, bf16[128,1024]{1,0:T(8,128)(2,1)} %context_hbm.1), custom_call_target="tpu_custom_call" | custom-call | tf_op jit(solution)/shard_map/select/pallas_call | solution.py:173
  1.1 3.0 %collective-permute-start.1 = (bf16[32,1024]{1,0:T(8,128)(2,1)S(1)}, bf16[32,1024]{1,0:T(8,128)(2,1)S(1)}, u32[]{:S(2)}, u32[]{:S(2)}) collective-permute-start(bf16[32,1024]{1,0:T(8,128)(2,1)S(1)} %get-tuple-element.35), channel_id=1, source_target_pairs={{0,2},{1,6},{2,10},{3,14},{4,3},{5,7},{6,11},{7,15},{8,0},{9,4},{1... | collective-permute-start | bytes 196616 | tf_op jit(solution)/shard_map/ppermute | solution.py:510
  4.1 0.7 collective-permute-start
  4.8 3.5 %keep_gate.1 = (bf16[1488,2048]{1,0:T(8,128)(2,1)S(1)}, bf16[1024,1024]{1,0:T(8,128)(2,1)S(1)}, f32[32,1024]{1,0:T(8,128)S(1)}) custom-call(bf16[32,128]{1,0:T(8,128)(2,1)S(1)} %get-tuple-element.32.pick_ref, bf16[128,1024]{1,0:T(8,128)(2,1)} %residual_hbm.1, bf16[2,2752,2048]{2,1,0:T(8,128)(2,1)} %bitcast.10, bf16[1024,1024]{1,0:T(8,128)(2,1)} %proj_ref.1), custom_call_target="tpu_custom_call" | custom-call | bytes 5636096 | tf_op jit(solution)/shard_map/keep_gate/pallas_call | solution.py:173
  8.3 1.2 %collective-permute-done.1.across_ref = bf16[32,1024]{1,0:T(8,128)(2,1)S(1)} collective-permute-done((bf16[32,1024]{1,0:T(8,128)(2,1)S(1)}, bf16[32,1024]{1,0:T(8,128)(2,1)S(1)}, u32[]{:S(2)}, u32[]{:S(2)}) %collective-permute-start.1) | collective-permute-done | bytes 65568 | tf_op jit(solution)/shard_map/ppermute | solution.py:510
  9.5 1.4 %collective-permute-start.2 = (bf16[64,1024]{1,0:T(8,128)(2,1)S(1)}, bf16[64,1024]{1,0:T(8,128)(2,1)S(1)}, u32[]{:S(2)}, u32[]{:S(2)}) collective-permute-start(bf16[64,1024]{1,0:T(8,128)(2,1)S(1)} %join.1.joined_ref), channel_id=1, source_target_pairs={{0,1},{1,0},{2,3},{3,2},{4,5},{5,4},{6,7},{7,6},{8,9},{9,8},{10,11... | collective-permute-start | bytes 393224 | tf_op jit(solution)/shard_map/ppermute | solution.py:528
  10.9 1.0 %collective-permute-done.2.other_ref = bf16[64,1024]{1,0:T(8,128)(2,1)S(1)} collective-permute-done((bf16[64,1024]{1,0:T(8,128)(2,1)S(1)}, bf16[64,1024]{1,0:T(8,128)(2,1)S(1)}, u32[]{:S(2)}, u32[]{:S(2)}) %collective-permute-start.2) | collective-permute-done | bytes 131104 | tf_op jit(solution)/shard_map/ppermute | solution.py:528
  11.9 0.5 project.1.after_ref.partial_ref
  12.4 1.9 %collective-permute-start.5 = (bf16[32,1024]{1,0:T(8,128)(2,1)S(1)}, bf16[32,1024]{1,0:T(8,128)(2,1)S(1)}, u32[]{:S(2)}, u32[]{:S(2)}) collective-permute-start(bf16[32,1024]{1,0:T(8,128)(2,1)S(1)} %get-tuple-element.59), channel_id=1, source_target_pairs={{0,4},{4,0},{8,12},{12,8},{1,5},{5,1},{9,13},{13,9},{2,6},{6,2},{1... | collective-permute-start | bytes 196616 | tf_op jit(solution)/shard_map/ppermute | solution.py:537
  14.3 4.4 %collective-permute-start.4 = (bf16[32,1024]{1,0:T(8,128)(2,1)S(1)}, bf16[32,1024]{1,0:T(8,128)(2,1)S(1)}, u32[]{:S(2)}, u32[]{:S(2)}) collective-permute-start(bf16[32,1024]{1,0:T(8,128)(2,1)S(1)} %get-tuple-element.60), channel_id=1, source_target_pairs={{0,8},{4,12},{8,0},{12,4},{1,9},{5,13},{9,1},{13,5},{2,10},{6,14},... | collective-permute-start | bytes 196616 | tf_op jit(solution)/shard_map/ppermute | solution.py:537
  18.7 4.0 %keep_more.1 = (bf16[1264,2048]{1,0:T(8,128)(2,1)S(1)}, bf16[1216,2048]{1,0:T(8,128)(2,1)S(1)}) custom-call(bf16[4,32,1024]{2,1,0:T(8,128)(2,1)S(1)} %project.1.after_ref.partial_ref, bf16[2,2752,2048]{2,1,0:T(8,128)(2,1)} %bitcast.11, bf16[2,2752,2048]{2,1,0:T(8,128)(2,1)} %bitcast.12), custom_call_target="tpu_custom_call" | custom-call | bytes 10158080 | tf_op jit(solution)/shard_map/keep_more/pallas_call | solution.py:173
  22.7 0.0 collective-permute-done.4.two_ref
  22.8 2.1 %collective-permute-done.3.three_ref = bf16[32,1024]{1,0:T(8,128)(2,1)S(1)} collective-permute-done((bf16[32,1024]{1,0:T(8,128)(2,1)S(1)}, bf16[32,1024]{1,0:T(8,128)(2,1)S(1)}, u32[]{:S(2)}, u32[]{:S(2)}) %collective-permute-start.3) | collective-permute-done | bytes 65568 | tf_op jit(solution)/shard_map/ppermute | solution.py:537
  24.9 0.2 norm.1.after_ref.zero_ref
  25.1 0.8 %collective-permute-start.8 = (bf16[32,1152]{1,0:T(8,128)(2,1)S(1)}, bf16[32,1152]{1,0:T(8,128)(2,1)S(1)}, u32[]{:S(2)}, u32[]{:S(2)}) collective-permute-start(bf16[32,1152]{1,0:T(8,128)(2,1)S(1)} %norm.1.after_ref.zero_ref), channel_id=1, source_target_pairs={{0,4},{4,0},{8,12},{12,8},{1,5},{5,1},{9,13},{13,9},{2,6},{6,2},{1... | collective-permute-start | bytes 221192 | tf_op jit(solution)/shard_map/ppermute | solution.py:552
  25.9 1.7 %collective-permute-start.7 = (bf16[32,1152]{1,0:T(8,128)(2,1)S(1)}, bf16[32,1152]{1,0:T(8,128)(2,1)S(1)}, u32[]{:S(2)}, u32[]{:S(2)}) collective-permute-start(bf16[32,1152]{1,0:T(8,128)(2,1)S(1)} %norm.1.after_ref.zero_ref), channel_id=1, source_target_pairs={{0,8},{4,12},{8,0},{12,4},{1,9},{5,13},{9,1},{13,5},{2,10},{6,14},... | collective-permute-start | bytes 221192 | tf_op jit(solution)/shard_map/ppermute | solution.py:552
  27.6 1.9 %collective-permute-start.6 = (bf16[32,1152]{1,0:T(8,128)(2,1)S(1)}, bf16[32,1152]{1,0:T(8,128)(2,1)S(1)}, u32[]{:S(2)}, u32[]{:S(2)}) collective-permute-start(bf16[32,1152]{1,0:T(8,128)(2,1)S(1)} %norm.1.after_ref.zero_ref), channel_id=1, source_target_pairs={{0,12},{4,8},{8,4},{12,0},{1,13},{5,9},{9,5},{13,1},{2,14},{6,10},... | collective-permute-start | bytes 221192 | tf_op jit(solution)/shard_map/ppermute | solution.py:552
  29.5 3.7 %keep_up.1 = (bf16[1536,2048]{1,0:T(8,128)(2,1)S(1)}, bf16[736,2048]{1,0:T(8,128)(2,1)S(1)}) custom-call(bf16[32,1152]{1,0:T(8,128)(2,1)S(1)} %norm.1.after_ref.zero_ref, bf16[2,2752,2048]{2,1,0:T(8,128)(2,1)} %bitcast.13, bf16[2,2752,2048]{2,1,0:T(8,128)(2,1)} %refs_0_.1), custom_call_target="tpu_custom_call" | custom-call | bytes 9306112 | tf_op jit(solution)/shard_map/keep_up/pallas_call | solution.py:173
  33.2 0.0 collective-permute-done.7.two_ref
  33.3 0.6 collective-permute-done.6.three_ref
  33.9 0.2 arrange.1
  34.1 3.4 %collective-permute-start.9 = (bf16[48,1152]{1,0:T(8,128)(2,1)S(1)}, bf16[48,1152]{1,0:T(8,128)(2,1)S(1)}, u32[]{:S(2)}, u32[]{:S(2)}) collective-permute-start(bf16[48,1152]{1,0:T(8,128)(2,1)S(1)} %get-tuple-element.40), channel_id=1, source_target_pairs={{0,18},{2,16},{16,2},{18,0},{1,19},{3,17},{17,3},{19,1},{4,22},{6,... | collective-permute-start | bytes 331784 | tf_op jit(solution)/shard_map/ppermute | solution.py:568
  37.4 0.6 collective-permute-start.11
  38.1 3.4 %keep_down.1.refs_2_.second_ref = bf16[2016,2048]{1,0:T(8,128)(2,1)S(1)} custom-call(bf16[48,1152]{1,0:T(8,128)(2,1)S(1)} %get-tuple-element.43.after_ref.own_ref, bf16[2,2752,2048]{2,1,0:T(8,128)(2,1)} %refs_0_.1), custom_call_target="tpu_custom_call" | custom-call | bytes 8257536 | tf_op jit(solution)/shard_map/keep_down/pallas_call | solution.py:173
  41.5 0.7 %collective-permute-done.10.side_own_ref = bf16[48,1152]{1,0:T(8,128)(2,1)S(1)} collective-permute-done((bf16[48,1152]{1,0:T(8,128)(2,1)S(1)}, bf16[48,1152]{1,0:T(8,128)(2,1)S(1)}, u32[]{:S(2)}, u32[]{:S(2)}) %collective-permute-start.10) | collective-permute-done | bytes 110624 | tf_op jit(solution)/shard_map/ppermute | solution.py:570
  42.2 3.1 %gate.1 = (bf16[2768,128]{1,0:T(8,128)(2,1)S(1)}, bf16[128,2048]{1,0:T(8,128)(2,1)S(1)}) custom-call(bf16[48,1152]{1,0:T(8,128)(2,1)S(1)} %collective-permute-done.9.side_far_ref, bf16[48,1152]{1,0:T(8,128)(2,1)S(1)} %collective-permute-done.10.side_own_ref, bf16[48,1152]{1,0:T(8,128)(2,1)S(1)} %collective-permute-done.11.far_ref, ...), custom_call_target="tpu_custom_call" | custom-call | flops 1442840576 | tf_op jit(solution)/shard_map/gate/pallas_call | solution.py:173
  45.3 0.1 collective-permute-start.12
  45.4 2.4 %up.2.up_ref = bf16[2064,128]{1,0:T(8,128)(2,1)S(1)} custom-call(bf16[128,2048]{1,0:T(8,128)(2,1)S(1)} %get-tuple-element.46.rows_ref, bf16[1216,2048]{1,0:T(8,128)(2,1)S(1)} %get-tuple-element.38._.refs_0_, bf16[1536,2048]{1,0:T(8,128)(2,1)S(1)} %get-tuple-element.39._.refs_1_.refs_0_), custom_call_target="tpu_custom_call" | custom-call | flops 1082130432 | tf_op jit(solution)/shard_map/up/pallas_call | solution.py:173
  47.8 0.6 collective-permute-start.13
  48.4 0.9 %up.3.up_ref = bf16[688,128]{1,0:T(8,128)(2,1)S(1)} custom-call(bf16[128,2048]{1,0:T(8,128)(2,1)S(1)} %get-tuple-element.46.rows_ref, bf16[1536,2048]{1,0:T(8,128)(2,1)S(1)} %get-tuple-element.39._.refs_1_.refs_0_), custom_call_target="tpu_custom_call" | custom-call | flops 360710144 | tf_op jit(solution)/shard_map/up/pallas_call | solution.py:173
  49.2 0.1 collective-permute-start.14
  49.3 0.6 collective-permute-done.13.up_other_ref
  49.9 0.7 activation.1
  50.6 0.2 collective-permute-done.14.other_ref
  50.7 2.0 %down.1 = (bf16[48,1024]{1,0:T(8,128)(2,1)S(1)}, bf16[48,1024]{1,0:T(8,128)(2,1)S(1)}, bf16[48,1024]{1,0:T(8,128)(2,1)S(1)}, bf16[48,1024]{1,0:T(8,128)(2,1)S(1)}) custom-call(bf16[2064,128]{1,0:T(8,128)(2,1)S(1)} %get-tuple-element.47.act_early_ref, f32[688,128]{1,0:T(8,128)S(1)} %get-tuple-element.48.silu_ref, f32[8,128]{1,0:T(8,128)S(1)} %get-tuple-element.49.stat_ref, ...), custom_call_target="tpu_custom_call" | custom-call | flops 1442840576 | tf_op jit(solution)/shard_map/down/pallas_call | solution.py:173
  52.8 2.1 %collective-permute-start.15 = (bf16[48,1024]{1,0:T(8,128)(2,1)S(1)}, bf16[48,1024]{1,0:T(8,128)(2,1)S(1)}, u32[]{:S(2)}, u32[]{:S(2)}) collective-permute-start(bf16[48,1024]{1,0:T(8,128)(2,1)S(1)} %get-tuple-element.52), channel_id=1, source_target_pairs={{0,2},{2,0},{1,3},{3,1},{4,6},{6,4},{5,7},{7,5},{8,10},{10,8},{9,1... | collective-permute-start | bytes 294920 | tf_op jit(solution)/shard_map/ppermute | solution.py:624
  54.8 0.7 collective-permute-start.16
  55.5 0.9 %collective-permute-start.17 = (bf16[48,1024]{1,0:T(8,128)(2,1)S(1)}, bf16[48,1024]{1,0:T(8,128)(2,1)S(1)}, u32[]{:S(2)}, u32[]{:S(2)}) collective-permute-start(bf16[48,1024]{1,0:T(8,128)(2,1)S(1)} %get-tuple-element.54), channel_id=1, source_target_pairs={{0,18},{2,16},{16,2},{18,0},{1,19},{3,17},{17,3},{19,1},{4,22},{6,... | collective-permute-start | bytes 294920 | tf_op jit(solution)/shard_map/ppermute | solution.py:622
  56.4 1.7 %collective-permute-done.15.side_ref = bf16[48,1024]{1,0:T(8,128)(2,1)S(1)} collective-permute-done((bf16[48,1024]{1,0:T(8,128)(2,1)S(1)}, bf16[48,1024]{1,0:T(8,128)(2,1)S(1)}, u32[]{:S(2)}, u32[]{:S(2)}) %collective-permute-start.15) | collective-permute-done | bytes 98336 | tf_op jit(solution)/shard_map/ppermute | solution.py:624
  58.0 3.6 %collective-permute-done.16.far_ref = bf16[48,1024]{1,0:T(8,128)(2,1)S(1)} collective-permute-done((bf16[48,1024]{1,0:T(8,128)(2,1)S(1)}, bf16[48,1024]{1,0:T(8,128)(2,1)S(1)}, u32[]{:S(2)}, u32[]{:S(2)}) %collective-permute-start.16) | collective-permute-done | bytes 98336 | tf_op jit(solution)/shard_map/ppermute | solution.py:623
  61.6 0.2 merge.1
  61.8 1.4 %collective-permute-start.18 = (bf16[32,1024]{1,0:T(8,128)(2,1)S(1)}, bf16[32,1024]{1,0:T(8,128)(2,1)S(1)}, u32[]{:S(2)}, u32[]{:S(2)}) collective-permute-start(bf16[32,1024]{1,0:T(8,128)(2,1)S(1)} %get-tuple-element.56), channel_id=1, source_target_pairs={{0,4},{4,0},{8,12},{12,8},{1,5},{5,1},{9,13},{13,9},{2,6},{6,2},{1... | collective-permute-start | bytes 196616 | tf_op jit(solution)/shard_map/ppermute | solution.py:632
  63.2 1.0 %collective-permute-start.19 = (bf16[32,1024]{1,0:T(8,128)(2,1)S(1)}, bf16[32,1024]{1,0:T(8,128)(2,1)S(1)}, u32[]{:S(2)}, u32[]{:S(2)}) collective-permute-start(bf16[32,1024]{1,0:T(8,128)(2,1)S(1)} %get-tuple-element.57), channel_id=1, source_target_pairs={{0,8},{4,12},{8,0},{12,4},{1,9},{5,13},{9,1},{13,5},{2,10},{6,14},... | collective-permute-start | bytes 196616 | tf_op jit(solution)/shard_map/ppermute | solution.py:632
  64.2 2.0 %collective-permute-start.20 = (bf16[32,1024]{1,0:T(8,128)(2,1)S(1)}, bf16[32,1024]{1,0:T(8,128)(2,1)S(1)}, u32[]{:S(2)}, u32[]{:S(2)}) collective-permute-start(bf16[32,1024]{1,0:T(8,128)(2,1)S(1)} %get-tuple-element.58), channel_id=1, source_target_pairs={{0,12},{4,8},{8,4},{12,0},{1,13},{5,9},{9,5},{13,1},{2,14},{6,10},... | collective-permute-start | bytes 196616 | tf_op jit(solution)/shard_map/ppermute | solution.py:632
  66.2 1.2 %collective-permute-done.18.one_ref = bf16[32,1024]{1,0:T(8,128)(2,1)S(1)} collective-permute-done((bf16[32,1024]{1,0:T(8,128)(2,1)S(1)}, bf16[32,1024]{1,0:T(8,128)(2,1)S(1)}, u32[]{:S(2)}, u32[]{:S(2)}) %collective-permute-start.18) | collective-permute-done | bytes 65568 | tf_op jit(solution)/shard_map/ppermute | solution.py:632
  67.4 1.6 %collective-permute-done.19.two_ref = bf16[32,1024]{1,0:T(8,128)(2,1)S(1)} collective-permute-done((bf16[32,1024]{1,0:T(8,128)(2,1)S(1)}, bf16[32,1024]{1,0:T(8,128)(2,1)S(1)}, u32[]{:S(2)}, u32[]{:S(2)}) %collective-permute-start.19) | collective-permute-done | bytes 65568 | tf_op jit(solution)/shard_map/ppermute | solution.py:632
  69.1 1.3 %collective-permute-done.20.three_ref = bf16[32,1024]{1,0:T(8,128)(2,1)S(1)} collective-permute-done((bf16[32,1024]{1,0:T(8,128)(2,1)S(1)}, bf16[32,1024]{1,0:T(8,128)(2,1)S(1)}, u32[]{:S(2)}, u32[]{:S(2)}) %collective-permute-start.20) | collective-permute-done | bytes 65568 | tf_op jit(solution)/shard_map/ppermute | solution.py:632
  70.4 1.0 %scatter.1 = bf16[128,1024]{1,0:T(8,128)(2,1)} custom-call(bf16[32,128]{1,0:T(8,128)(2,1)S(1)} %get-tuple-element.32.pick_ref, bf16[32,1024]{1,0:T(8,128)(2,1)S(1)} %get-tuple-element.55.zero_ref, bf16[32,1024]{1,0:T(8,128)(2,1)S(1)} %collective-permute-done.18.one_ref, bf16[32,1024]{1,0:T(8,128)(2,1)S(1)} %collective-permute-done.19.two_ref, ...), custom_call_target="tpu_custom_call" | custom-call | tf_op jit(solution)/shard_map/scatter/pallas_call | solution.py:633
  (15 shorter events, 0.1 us)
Async XLA Ops:
  1.1 8.3 %collective-permute-start.1 = (bf16[32,1024]{1,0:T(8,128)(2,1)S(1)}, bf16[32,1024]{1,0:T(8,128)(2,1)S(1)}, u32[]{:S(2)}, u32[]{:S(2)}) collective-permute-start(bf16[32,1024]{1,0:T(8,128)(2,1)S(1)} %get-tuple-element.35), channel_id=1, source_target_pairs={{0,2},{1,6},{2,10},{3,14},{4,3},{5,7},{6,11},{7,15},{8,0},{9,4},{1... | collective-permute-start | bytes 196616 | tf_op jit(solution)/shard_map/ppermute | solution.py:510
  4.1 5.3 %collective-permute-start = (bf16[32,1024]{1,0:T(8,128)(2,1)S(1)}, bf16[32,1024]{1,0:T(8,128)(2,1)S(1)}, u32[]{:S(2)}, u32[]{:S(2)}) collective-permute-start(bf16[32,1024]{1,0:T(8,128)(2,1)S(1)} %get-tuple-element.35), channel_id=1, source_target_pairs={{0,0},{1,4},{2,8},{3,12},{4,1},{5,5},{6,9},{7,13},{8,2},{9,6},{10,... | collective-permute-start | bytes 196616 | tf_op jit(solution)/shard_map/ppermute | solution.py:511
  9.5 2.4 %collective-permute-start.2 = (bf16[64,1024]{1,0:T(8,128)(2,1)S(1)}, bf16[64,1024]{1,0:T(8,128)(2,1)S(1)}, u32[]{:S(2)}, u32[]{:S(2)}) collective-permute-start(bf16[64,1024]{1,0:T(8,128)(2,1)S(1)} %join.1.joined_ref), channel_id=1, source_target_pairs={{0,1},{1,0},{2,3},{3,2},{4,5},{5,4},{6,7},{7,6},{8,9},{9,8},{10,11... | collective-permute-start | bytes 393224 | tf_op jit(solution)/shard_map/ppermute | solution.py:528
  12.4 10.3 %collective-permute-start.5 = (bf16[32,1024]{1,0:T(8,128)(2,1)S(1)}, bf16[32,1024]{1,0:T(8,128)(2,1)S(1)}, u32[]{:S(2)}, u32[]{:S(2)}) collective-permute-start(bf16[32,1024]{1,0:T(8,128)(2,1)S(1)} %get-tuple-element.59), channel_id=1, source_target_pairs={{0,4},{4,0},{8,12},{12,8},{1,5},{5,1},{9,13},{13,9},{2,6},{6,2},{1... | collective-permute-start | bytes 196616 | tf_op jit(solution)/shard_map/ppermute | solution.py:537
  14.3 8.4 %collective-permute-start.4 = (bf16[32,1024]{1,0:T(8,128)(2,1)S(1)}, bf16[32,1024]{1,0:T(8,128)(2,1)S(1)}, u32[]{:S(2)}, u32[]{:S(2)}) collective-permute-start(bf16[32,1024]{1,0:T(8,128)(2,1)S(1)} %get-tuple-element.60), channel_id=1, source_target_pairs={{0,8},{4,12},{8,0},{12,4},{1,9},{5,13},{9,1},{13,5},{2,10},{6,14},... | collective-permute-start | bytes 196616 | tf_op jit(solution)/shard_map/ppermute | solution.py:537
  18.7 6.2 %collective-permute-start.3 = (bf16[32,1024]{1,0:T(8,128)(2,1)S(1)}, bf16[32,1024]{1,0:T(8,128)(2,1)S(1)}, u32[]{:S(2)}, u32[]{:S(2)}) collective-permute-start(bf16[32,1024]{1,0:T(8,128)(2,1)S(1)} %get-tuple-element.61), channel_id=1, source_target_pairs={{0,12},{4,8},{8,4},{12,0},{1,13},{5,9},{9,5},{13,1},{2,14},{6,10},... | collective-permute-start | bytes 196616 | tf_op jit(solution)/shard_map/ppermute | solution.py:537
  18.7 6.2 %copy-start = (bf16[1024,4]{0,1:T(4,128)(2,1)S(1)}, bf16[1024,4]{0,1:T(4,128)(2,1)}, u32[]{:S(2)}) copy-start(bf16[1024,4]{0,1:T(4,128)(2,1)} %param.14) | copy-start | bytes 24580
  18.7 6.2 %copy-start.1 = (bf16[2,1024]{1,0:T(2,128)(2,1)S(1)}, bf16[2,1024]{1,0:T(2,128)(2,1)}, u32[]{:S(2)}) copy-start(bf16[2,1024]{1,0:T(2,128)(2,1)} %gain_ref.1) | copy-start | bytes 12292
  25.1 8.1 %collective-permute-start.8 = (bf16[32,1152]{1,0:T(8,128)(2,1)S(1)}, bf16[32,1152]{1,0:T(8,128)(2,1)S(1)}, u32[]{:S(2)}, u32[]{:S(2)}) collective-permute-start(bf16[32,1152]{1,0:T(8,128)(2,1)S(1)} %norm.1.after_ref.zero_ref), channel_id=1, source_target_pairs={{0,4},{4,0},{8,12},{12,8},{1,5},{5,1},{9,13},{13,9},{2,6},{6,2},{1... | collective-permute-start | bytes 221192 | tf_op jit(solution)/shard_map/ppermute | solution.py:552
  25.9 7.3 %collective-permute-start.7 = (bf16[32,1152]{1,0:T(8,128)(2,1)S(1)}, bf16[32,1152]{1,0:T(8,128)(2,1)S(1)}, u32[]{:S(2)}, u32[]{:S(2)}) collective-permute-start(bf16[32,1152]{1,0:T(8,128)(2,1)S(1)} %norm.1.after_ref.zero_ref), channel_id=1, source_target_pairs={{0,8},{4,12},{8,0},{12,4},{1,9},{5,13},{9,1},{13,5},{2,10},{6,14},... | collective-permute-start | bytes 221192 | tf_op jit(solution)/shard_map/ppermute | solution.py:552
  27.6 6.3 %collective-permute-start.6 = (bf16[32,1152]{1,0:T(8,128)(2,1)S(1)}, bf16[32,1152]{1,0:T(8,128)(2,1)S(1)}, u32[]{:S(2)}, u32[]{:S(2)}) collective-permute-start(bf16[32,1152]{1,0:T(8,128)(2,1)S(1)} %norm.1.after_ref.zero_ref), channel_id=1, source_target_pairs={{0,12},{4,8},{8,4},{12,0},{1,13},{5,9},{9,5},{13,1},{2,14},{6,10},... | collective-permute-start | bytes 221192 | tf_op jit(solution)/shard_map/ppermute | solution.py:552
  34.1 7.4 %collective-permute-start.9 = (bf16[48,1152]{1,0:T(8,128)(2,1)S(1)}, bf16[48,1152]{1,0:T(8,128)(2,1)S(1)}, u32[]{:S(2)}, u32[]{:S(2)}) collective-permute-start(bf16[48,1152]{1,0:T(8,128)(2,1)S(1)} %get-tuple-element.40), channel_id=1, source_target_pairs={{0,18},{2,16},{16,2},{18,0},{1,19},{3,17},{17,3},{19,1},{4,22},{6,... | collective-permute-start | bytes 331784 | tf_op jit(solution)/shard_map/ppermute | solution.py:568
  37.4 4.7 %collective-permute-start.10 = (bf16[48,1152]{1,0:T(8,128)(2,1)S(1)}, bf16[48,1152]{1,0:T(8,128)(2,1)S(1)}, u32[]{:S(2)}, u32[]{:S(2)}) collective-permute-start(bf16[48,1152]{1,0:T(8,128)(2,1)S(1)} %get-tuple-element.41), channel_id=1, source_target_pairs={{0,2},{2,0},{1,3},{3,1},{4,6},{6,4},{5,7},{7,5},{8,10},{10,8},{9,1... | collective-permute-start | bytes 331784 | tf_op jit(solution)/shard_map/ppermute | solution.py:570
  37.4 4.7 %collective-permute-start.11 = (bf16[48,1152]{1,0:T(8,128)(2,1)S(1)}, bf16[48,1152]{1,0:T(8,128)(2,1)S(1)}, u32[]{:S(2)}, u32[]{:S(2)}) collective-permute-start(bf16[48,1152]{1,0:T(8,128)(2,1)S(1)} %get-tuple-element.42), channel_id=1, source_target_pairs={{0,16},{16,0},{1,17},{17,1},{2,18},{18,2},{3,19},{19,3},{4,20},{20... | collective-permute-start | bytes 331784 | tf_op jit(solution)/shard_map/ppermute | solution.py:569
  45.3 4.6 %collective-permute-start.12 = (bf16[2768,128]{1,0:T(8,128)(2,1)S(1)}, bf16[2768,128]{1,0:T(8,128)(2,1)S(1)}, u32[]{:S(2)}, u32[]{:S(2)}) collective-permute-start(bf16[2768,128]{1,0:T(8,128)(2,1)S(1)} %get-tuple-element.45.gate_ref), channel_id=1, source_target_pairs={{0,1},{1,0},{2,3},{3,2},{4,5},{5,4},{6,7},{7,6},{8,9},{9,8},{10,11... | collective-permute-start | bytes 2125832 | tf_op jit(solution)/shard_map/ppermute | solution.py:599
  47.8 2.1 %collective-permute-start.13 = (bf16[2064,128]{1,0:T(8,128)(2,1)S(1)}, bf16[2064,128]{1,0:T(8,128)(2,1)S(1)}, u32[]{:S(2)}, u32[]{:S(2)}) collective-permute-start(bf16[2064,128]{1,0:T(8,128)(2,1)S(1)} %up.2.up_ref), channel_id=1, source_target_pairs={{0,1},{1,0},{2,3},{3,2},{4,5},{5,4},{6,7},{7,6},{8,9},{9,8},{10,11... | collective-permute-start | bytes 1585160 | tf_op jit(solution)/shard_map/ppermute | solution.py:600
  49.2 1.5 %collective-permute-start.14 = (bf16[688,128]{1,0:T(8,128)(2,1)S(1)}, bf16[688,128]{1,0:T(8,128)(2,1)S(1)}, u32[]{:S(2)}, u32[]{:S(2)}) collective-permute-start(bf16[688,128]{1,0:T(8,128)(2,1)S(1)} %up.3.up_ref), channel_id=1, source_target_pairs={{0,1},{1,0},{2,3},{3,2},{4,5},{5,4},{6,7},{7,6},{8,9},{9,8},{10,11... | collective-permute-start | bytes 528392 | tf_op jit(solution)/shard_map/ppermute | solution.py:600
  52.8 5.3 %collective-permute-start.15 = (bf16[48,1024]{1,0:T(8,128)(2,1)S(1)}, bf16[48,1024]{1,0:T(8,128)(2,1)S(1)}, u32[]{:S(2)}, u32[]{:S(2)}) collective-permute-start(bf16[48,1024]{1,0:T(8,128)(2,1)S(1)} %get-tuple-element.52), channel_id=1, source_target_pairs={{0,2},{2,0},{1,3},{3,1},{4,6},{6,4},{5,7},{7,5},{8,10},{10,8},{9,1... | collective-permute-start | bytes 294920 | tf_op jit(solution)/shard_map/ppermute | solution.py:624
  54.8 6.8 %collective-permute-start.16 = (bf16[48,1024]{1,0:T(8,128)(2,1)S(1)}, bf16[48,1024]{1,0:T(8,128)(2,1)S(1)}, u32[]{:S(2)}, u32[]{:S(2)}) collective-permute-start(bf16[48,1024]{1,0:T(8,128)(2,1)S(1)} %get-tuple-element.53), channel_id=1, source_target_pairs={{0,16},{16,0},{1,17},{17,1},{2,18},{18,2},{3,19},{19,3},{4,20},{20... | collective-permute-start | bytes 294920 | tf_op jit(solution)/shard_map/ppermute | solution.py:623
  55.5 6.1 %collective-permute-start.17 = (bf16[48,1024]{1,0:T(8,128)(2,1)S(1)}, bf16[48,1024]{1,0:T(8,128)(2,1)S(1)}, u32[]{:S(2)}, u32[]{:S(2)}) collective-permute-start(bf16[48,1024]{1,0:T(8,128)(2,1)S(1)} %get-tuple-element.54), channel_id=1, source_target_pairs={{0,18},{2,16},{16,2},{18,0},{1,19},{3,17},{17,3},{19,1},{4,22},{6,... | collective-permute-start | bytes 294920 | tf_op jit(solution)/shard_map/ppermute | solution.py:622
  61.8 5.7 %collective-permute-start.18 = (bf16[32,1024]{1,0:T(8,128)(2,1)S(1)}, bf16[32,1024]{1,0:T(8,128)(2,1)S(1)}, u32[]{:S(2)}, u32[]{:S(2)}) collective-permute-start(bf16[32,1024]{1,0:T(8,128)(2,1)S(1)} %get-tuple-element.56), channel_id=1, source_target_pairs={{0,4},{4,0},{8,12},{12,8},{1,5},{5,1},{9,13},{13,9},{2,6},{6,2},{1... | collective-permute-start | bytes 196616 | tf_op jit(solution)/shard_map/ppermute | solution.py:632
  63.2 5.9 %collective-permute-start.19 = (bf16[32,1024]{1,0:T(8,128)(2,1)S(1)}, bf16[32,1024]{1,0:T(8,128)(2,1)S(1)}, u32[]{:S(2)}, u32[]{:S(2)}) collective-permute-start(bf16[32,1024]{1,0:T(8,128)(2,1)S(1)} %get-tuple-element.57), channel_id=1, source_target_pairs={{0,8},{4,12},{8,0},{12,4},{1,9},{5,13},{9,1},{13,5},{2,10},{6,14},... | collective-permute-start | bytes 196616 | tf_op jit(solution)/shard_map/ppermute | solution.py:632
  64.2 6.2 %collective-permute-start.20 = (bf16[32,1024]{1,0:T(8,128)(2,1)S(1)}, bf16[32,1024]{1,0:T(8,128)(2,1)S(1)}, u32[]{:S(2)}, u32[]{:S(2)}) collective-permute-start(bf16[32,1024]{1,0:T(8,128)(2,1)S(1)} %get-tuple-element.58), channel_id=1, source_target_pairs={{0,12},{4,8},{8,4},{12,0},{1,13},{5,9},{9,5},{13,1},{2,14},{6,10},... | collective-permute-start | bytes 196616 | tf_op jit(solution)/shard_map/ppermute | solution.py:632

commit v14 on v13

--- a/solution.py
+++ b/solution.py
@@ -257,23 +257,21 @@
         copy.wait()
 
 
-def join_kernel(near_ref, across_ref, _, out_ref):
-    slots = near_ref.shape[0]
-    out_ref[:slots, :] = near_ref[...]
-    out_ref[slots:, :] = across_ref[...]
-
-
-def project_kernel(joined_ref, other_ref, weight_ref, out_ref, rows_ref):
-    pair = joined_ref.shape[0]
-    slots = pair // 2
-    rows_ref[:pair, :] = joined_ref[...]
-    rows_ref[pair:, :] = other_ref[...]
+def pass_kernel(rows_ref, _, out_ref):
+    out_ref[...] = rows_ref[...]
+
+
+def project_kernel(*refs):
+    block_refs, (weight_ref, out_ref, rows_ref) = refs[:4], refs[4:]
+    slots = block_refs[0].shape[0]
+    for u, block_ref in enumerate(block_refs):
+        rows_ref[u * slots : (u + 1) * slots, :] = block_ref[...]
     product = jnp.dot(rows_ref[...], weight_ref[...], preferred_element_type=jnp.float32)
     product = product.astype(jnp.bfloat16)
     corner = 2 * lax.axis_index("mod") + lax.axis_index("fsdp")
     flip = lax.axis_index("tok") ^ corner
-    for n, u in enumerate((0, 2, 1, 3)):
-        out_ref[flip ^ u] = product[n * slots : (n + 1) * slots, :]
+    for u in range(4):
+        out_ref[flip ^ u] = product[u * slots : (u + 1) * slots, :]
 
 
 def split_high_low(value):
@@ -504,11 +502,8 @@
             pltpu.SemaphoreType.DMA((2,)),
         ],
     )
-    plane = ("tok", "mod", "fsdp")
-    to_first = [(t * 4 + q, q * 4 + t) for t in range(4) for q in range(4)]
-    to_second = [(t * 4 + q, q * 4 + (t ^ 2)) for t in range(4) for q in range(4)]
-    across = lax.ppermute(picked, plane, to_second)
-    near = lax.ppermute(picked, plane, to_first)
+    turned = [(t * 4 + q, q * 4 + t) for t in range(4) for q in range(4)]
+    near = lax.ppermute(picked, ("tok", "mod", "fsdp"), turned)
     gate_units, up_units, down_units = [round(units * part / TILE) * TILE for part in (0.54, 0.44, 0.27)]
     gate_first, proj_held, rest = call(
         keep_gate_kernel,
@@ -524,14 +519,14 @@
         moved=units * width,
         limit=2 << 20,
     )
-    joined = call(join_kernel, "join", array(half, columns), [ON_CHIP] * 3, [near, across, gate_first])
-    other = lax.ppermute(joined, "fsdp", SWAP)
+    block = call(pass_kernel, "pass", array(slots, columns), [ON_CHIP] * 2, [near, gate_first])
+    plane = [lax.ppermute(block, ("mod", "fsdp"), crossed(2, u)) for u in (3, 2, 1)][::-1]
     partial = call(
         project_kernel,
         "project",
         array(4, slots, columns),
-        [ON_CHIP] * 3,
-        [joined, other, proj_held],
+        [ON_CHIP] * 5,
+        [block, *plane, proj_held],
         scratch=[pltpu.VMEM((rows, columns), jnp.bfloat16)],
     )
     sums = [lax.ppermute(partial[v], "tok", crossed(2, v)) for v in (3, 2, 1)][::-1]

time: 71.5 us -> 72.6 us (1.015)
  starting transfers between devices: 28.6 us -> 30.3 us
    ppermute x3 -> x4, starting transfers between devices: 5.09 us -> 9.14 us  [the longest x3 8.47 us: paired_local(): lax.ppermute(block, ('mod', 'fsdp'), crossed(2, u))]
    ppermute x3, waiting for transfers between devices: 2.14 us -> 0.25 us  [paired_local(): lax.ppermute(partial[v], 'tok', crossed(2, v))]
    ppermute x3, starting transfers between devices: 6.31 us -> 4.44 us  [paired_local(): lax.ppermute(partial[v], 'tok', crossed(2, v))]
    ppermute x3 -> x4, waiting for transfers between devices: 2.15 us -> 4 us  [the longest x3 4 us: paired_local(): lax.ppermute(block, ('mod', 'fsdp'), crossed(2, u))]
    ppermute x1, starting transfers between devices: 3.38 us -> 2.43 us  [paired_local(): side_far = lax.ppermute(to_corner_rows, both_axes, crossed(2, 3))]
  transfers between devices with their start and end apart: 21 -> 22, of which waited for: 12 -> 13; matrix products, arithmetic and copies ran while one was open for 0% -> 0% of each run, Pallas kernels for 26% -> 25%
where the time goes in v14:
time: 72.6 us; the launch traced here: 72.5 us
  starting transfers between devices  30.3 us (42%)
  Pallas kernels  26.8 us (37%)
  waiting for transfers between devices  15.2 us (21%)
    pallas_call x15, Pallas kernels, call(): pl.pallas_call(kernel, out_shape=outs, in_specs=specs, out_specs=jax.tree...  25.8 us
    ppermute x3, starting transfers between devices, paired_local(): lax.ppermute(block, ('mod', 'fsdp'), crossed(2, u))  8.47 us
    ppermute x3, starting transfers between devices, paired_local(): lax.ppermute(merged[v], 'tok', crossed(2, v))  4.45 us
    ppermute x3, starting transfers between devices, paired_local(): lax.ppermute(partial[v], 'tok', crossed(2, v))  4.44 us
    ppermute x3, starting transfers between devices, paired_local(): lax.ppermute(packed, 'tok', crossed(2, v))  4.42 us
    ppermute x3, waiting for transfers between devices, paired_local(): lax.ppermute(merged[v], 'tok', crossed(2, v))  4.01 us
    ppermute x3, waiting for transfers between devices, paired_local(): lax.ppermute(block, ('mod', 'fsdp'), crossed(2, u))  4 us
    ppermute x1, waiting for transfers between devices, paired_local(): from_far = lax.ppermute(to_far, 'groups', SWAP)  3.25 us
  transfers between devices with their start and end apart: 22, of which 13 were waited for; matrix products, arithmetic and copies ran while one was open for 0% of the time, Pallas kernels for 25%

profile of v14, /device:TPU:0, one launch (start us, length us, event | category | flops | bytes accessed | tf_op | source)
XLA Modules:
  0.0 72.5 jit_solution(542701179899141478)
XLA Ops:
  0.0 1.1 %select.1 = (bf16[32,1024]{1,0:T(8,128)(2,1)S(1)}, bf16[32,128]{1,0:T(8,128)(2,1)S(1)}, f32[8,128]{1,0:T(8,128)S(1)}) custom-call(s32[4,16]{1,0:T(4,128)} %rows_hbm.1, bf16[128,1024]{1,0:T(8,128)(2,1)} %context_hbm.1), custom_call_target="tpu_custom_call" | custom-call | tf_op jit(solution)/shard_map/select/pallas_call | solution.py:173
  1.1 0.7 collective-permute-start
  1.8 3.5 %keep_gate.1 = (bf16[1488,2048]{1,0:T(8,128)(2,1)S(1)}, bf16[1024,1024]{1,0:T(8,128)(2,1)S(1)}, f32[32,1024]{1,0:T(8,128)S(1)}) custom-call(bf16[32,128]{1,0:T(8,128)(2,1)S(1)} %get-tuple-element.32.pick_ref, bf16[128,1024]{1,0:T(8,128)(2,1)} %residual_hbm.1, bf16[2,2752,2048]{2,1,0:T(8,128)(2,1)} %bitcast.10, bf16[1024,1024]{1,0:T(8,128)(2,1)} %proj_ref.1), custom_call_target="tpu_custom_call" | custom-call | bytes 5636096 | tf_op jit(solution)/shard_map/keep_gate/pallas_call | solution.py:173
  5.3 7.5 %collective-permute-start.3 = (bf16[32,1024]{1,0:T(8,128)(2,1)S(1)}, bf16[32,1024]{1,0:T(8,128)(2,1)S(1)}, u32[]{:S(2)}, u32[]{:S(2)}) collective-permute-start(bf16[32,1024]{1,0:T(8,128)(2,1)S(1)} %pass.1.refs_0_), channel_id=1, source_target_pairs={{0,3},{1,2},{2,1},{3,0},{4,7},{5,6},{6,5},{7,4},{8,11},{9,10},{10,... | collective-permute-start | bytes 196616 | tf_op jit(solution)/shard_map/ppermute | solution.py:523
  12.9 0.9 %collective-permute-start.2 = (bf16[32,1024]{1,0:T(8,128)(2,1)S(1)}, bf16[32,1024]{1,0:T(8,128)(2,1)S(1)}, u32[]{:S(2)}, u32[]{:S(2)}) collective-permute-start(bf16[32,1024]{1,0:T(8,128)(2,1)S(1)} %pass.1.refs_0_), channel_id=1, source_target_pairs={{0,2},{1,3},{2,0},{3,1},{4,6},{5,7},{6,4},{7,5},{8,10},{9,11},{10,... | collective-permute-start | bytes 196616 | tf_op jit(solution)/shard_map/ppermute | solution.py:523
  13.8 1.3 %collective-permute-done.3.refs_3_ = bf16[32,1024]{1,0:T(8,128)(2,1)S(1)} collective-permute-done((bf16[32,1024]{1,0:T(8,128)(2,1)S(1)}, bf16[32,1024]{1,0:T(8,128)(2,1)S(1)}, u32[]{:S(2)}, u32[]{:S(2)}) %collective-permute-start.3) | collective-permute-done | bytes 65568 | tf_op jit(solution)/shard_map/ppermute | solution.py:523
  15.1 2.7 %collective-permute-done.2.refs_2_ = bf16[32,1024]{1,0:T(8,128)(2,1)S(1)} collective-permute-done((bf16[32,1024]{1,0:T(8,128)(2,1)S(1)}, bf16[32,1024]{1,0:T(8,128)(2,1)S(1)}, u32[]{:S(2)}, u32[]{:S(2)}) %collective-permute-start.2) | collective-permute-done | bytes 65568 | tf_op jit(solution)/shard_map/ppermute | solution.py:523
  17.8 0.5 project.1.after_ref.partial_ref
  18.4 2.5 %collective-permute-start.5 = (bf16[32,1024]{1,0:T(8,128)(2,1)S(1)}, bf16[32,1024]{1,0:T(8,128)(2,1)S(1)}, u32[]{:S(2)}, u32[]{:S(2)}) collective-permute-start(bf16[32,1024]{1,0:T(8,128)(2,1)S(1)} %get-tuple-element.60), channel_id=1, source_target_pairs={{0,8},{4,12},{8,0},{12,4},{1,9},{5,13},{9,1},{13,5},{2,10},{6,14},... | collective-permute-start | bytes 196616 | tf_op jit(solution)/shard_map/ppermute | solution.py:532
  20.9 1.9 %collective-permute-start.4 = (bf16[32,1024]{1,0:T(8,128)(2,1)S(1)}, bf16[32,1024]{1,0:T(8,128)(2,1)S(1)}, u32[]{:S(2)}, u32[]{:S(2)}) collective-permute-start(bf16[32,1024]{1,0:T(8,128)(2,1)S(1)} %get-tuple-element.61), channel_id=1, source_target_pairs={{0,12},{4,8},{8,4},{12,0},{1,13},{5,9},{9,5},{13,1},{2,14},{6,10},... | collective-permute-start | bytes 196616 | tf_op jit(solution)/shard_map/ppermute | solution.py:532
  22.8 4.0 %keep_more.1 = (bf16[1264,2048]{1,0:T(8,128)(2,1)S(1)}, bf16[1216,2048]{1,0:T(8,128)(2,1)S(1)}) custom-call(bf16[4,32,1024]{2,1,0:T(8,128)(2,1)S(1)} %project.1.after_ref.partial_ref, bf16[2,2752,2048]{2,1,0:T(8,128)(2,1)} %bitcast.11, bf16[2,2752,2048]{2,1,0:T(8,128)(2,1)} %bitcast.12), custom_call_target="tpu_custom_call" | custom-call | bytes 10158080 | tf_op jit(solution)/shard_map/keep_more/pallas_call | solution.py:173
  26.8 0.2 collective-permute-done.4.three_ref
  27.0 0.2 norm.1.after_ref.zero_ref
  27.3 1.3 %collective-permute-start.9 = (bf16[32,1152]{1,0:T(8,128)(2,1)S(1)}, bf16[32,1152]{1,0:T(8,128)(2,1)S(1)}, u32[]{:S(2)}, u32[]{:S(2)}) collective-permute-start(bf16[32,1152]{1,0:T(8,128)(2,1)S(1)} %norm.1.after_ref.zero_ref), channel_id=1, source_target_pairs={{0,4},{4,0},{8,12},{12,8},{1,5},{5,1},{9,13},{13,9},{2,6},{6,2},{1... | collective-permute-start | bytes 221192 | tf_op jit(solution)/shard_map/ppermute | solution.py:547
  28.6 1.2 %collective-permute-start.8 = (bf16[32,1152]{1,0:T(8,128)(2,1)S(1)}, bf16[32,1152]{1,0:T(8,128)(2,1)S(1)}, u32[]{:S(2)}, u32[]{:S(2)}) collective-permute-start(bf16[32,1152]{1,0:T(8,128)(2,1)S(1)} %norm.1.after_ref.zero_ref), channel_id=1, source_target_pairs={{0,8},{4,12},{8,0},{12,4},{1,9},{5,13},{9,1},{13,5},{2,10},{6,14},... | collective-permute-start | bytes 221192 | tf_op jit(solution)/shard_map/ppermute | solution.py:547
  29.8 1.9 %collective-permute-start.7 = (bf16[32,1152]{1,0:T(8,128)(2,1)S(1)}, bf16[32,1152]{1,0:T(8,128)(2,1)S(1)}, u32[]{:S(2)}, u32[]{:S(2)}) collective-permute-start(bf16[32,1152]{1,0:T(8,128)(2,1)S(1)} %norm.1.after_ref.zero_ref), channel_id=1, source_target_pairs={{0,12},{4,8},{8,4},{12,0},{1,13},{5,9},{9,5},{13,1},{2,14},{6,10},... | collective-permute-start | bytes 221192 | tf_op jit(solution)/shard_map/ppermute | solution.py:547
  31.7 3.7 %keep_up.1 = (bf16[1536,2048]{1,0:T(8,128)(2,1)S(1)}, bf16[736,2048]{1,0:T(8,128)(2,1)S(1)}) custom-call(bf16[32,1152]{1,0:T(8,128)(2,1)S(1)} %norm.1.after_ref.zero_ref, bf16[2,2752,2048]{2,1,0:T(8,128)(2,1)} %bitcast.13, bf16[2,2752,2048]{2,1,0:T(8,128)(2,1)} %refs_0_.1), custom_call_target="tpu_custom_call" | custom-call | bytes 9306112 | tf_op jit(solution)/shard_map/keep_up/pallas_call | solution.py:173
  35.4 0.6 collective-permute-done.7.three_ref
  36.0 0.2 arrange.1
  36.2 2.4 %collective-permute-start.10 = (bf16[48,1152]{1,0:T(8,128)(2,1)S(1)}, bf16[48,1152]{1,0:T(8,128)(2,1)S(1)}, u32[]{:S(2)}, u32[]{:S(2)}) collective-permute-start(bf16[48,1152]{1,0:T(8,128)(2,1)S(1)} %get-tuple-element.40), channel_id=1, source_target_pairs={{0,18},{2,16},{16,2},{18,0},{1,19},{3,17},{17,3},{19,1},{4,22},{6,... | collective-permute-start | bytes 331784 | tf_op jit(solution)/shard_map/ppermute | solution.py:563
  38.6 0.6 collective-permute-start.11
  39.3 0.5 collective-permute-start.12
  39.8 3.4 %keep_down.1.refs_2_.second_ref = bf16[2016,2048]{1,0:T(8,128)(2,1)S(1)} custom-call(bf16[48,1152]{1,0:T(8,128)(2,1)S(1)} %get-tuple-element.43.after_ref.own_ref, bf16[2,2752,2048]{2,1,0:T(8,128)(2,1)} %refs_0_.1), custom_call_target="tpu_custom_call" | custom-call | bytes 8257536 | tf_op jit(solution)/shard_map/keep_down/pallas_call | solution.py:173
  43.1 0.3 collective-permute-done.11.side_own_ref
  43.4 0.6 collective-permute-done.12.far_ref
  44.0 3.1 %gate.1 = (bf16[2768,128]{1,0:T(8,128)(2,1)S(1)}, bf16[128,2048]{1,0:T(8,128)(2,1)S(1)}) custom-call(bf16[48,1152]{1,0:T(8,128)(2,1)S(1)} %collective-permute-done.10.side_far_ref, bf16[48,1152]{1,0:T(8,128)(2,1)S(1)} %collective-permute-done.11.side_own_ref, bf16[48,1152]{1,0:T(8,128)(2,1)S(1)} %collective-permute-done.12.far_ref, ...), custom_call_target="tpu_custom_call" | custom-call | flops 1442840576 | tf_op jit(solution)/shard_map/gate/pallas_call | solution.py:173
  47.1 0.1 collective-permute-start.13
  47.2 2.4 %up.2.up_ref = bf16[2064,128]{1,0:T(8,128)(2,1)S(1)} custom-call(bf16[128,2048]{1,0:T(8,128)(2,1)S(1)} %get-tuple-element.46.rows_ref, bf16[1216,2048]{1,0:T(8,128)(2,1)S(1)} %get-tuple-element.38._.refs_0_, bf16[1536,2048]{1,0:T(8,128)(2,1)S(1)} %get-tuple-element.39._.refs_1_.refs_0_), custom_call_target="tpu_custom_call" | custom-call | flops 1082130432 | tf_op jit(solution)/shard_map/up/pallas_call | solution.py:173
  49.6 0.6 collective-permute-start.14
  50.2 0.9 %up.3.up_ref = bf16[688,128]{1,0:T(8,128)(2,1)S(1)} custom-call(bf16[128,2048]{1,0:T(8,128)(2,1)S(1)} %get-tuple-element.46.rows_ref, bf16[1536,2048]{1,0:T(8,128)(2,1)S(1)} %get-tuple-element.39._.refs_1_.refs_0_), custom_call_target="tpu_custom_call" | custom-call | flops 360710144 | tf_op jit(solution)/shard_map/up/pallas_call | solution.py:173
  51.1 0.1 collective-permute-start.15
  51.1 0.6 collective-permute-done.14.up_other_ref
  51.7 0.7 activation.1
  52.4 0.2 collective-permute-done.15.other_ref
  52.5 2.0 %down.1 = (bf16[48,1024]{1,0:T(8,128)(2,1)S(1)}, bf16[48,1024]{1,0:T(8,128)(2,1)S(1)}, bf16[48,1024]{1,0:T(8,128)(2,1)S(1)}, bf16[48,1024]{1,0:T(8,128)(2,1)S(1)}) custom-call(bf16[2064,128]{1,0:T(8,128)(2,1)S(1)} %get-tuple-element.47.act_early_ref, f32[688,128]{1,0:T(8,128)S(1)} %get-tuple-element.48.silu_ref, f32[8,128]{1,0:T(8,128)S(1)} %get-tuple-element.49.stat_ref, ...), custom_call_target="tpu_custom_call" | custom-call | flops 1442840576 | tf_op jit(solution)/shard_map/down/pallas_call | solution.py:173
  54.6 1.5 %collective-permute-start.16 = (bf16[48,1024]{1,0:T(8,128)(2,1)S(1)}, bf16[48,1024]{1,0:T(8,128)(2,1)S(1)}, u32[]{:S(2)}, u32[]{:S(2)}) collective-permute-start(bf16[48,1024]{1,0:T(8,128)(2,1)S(1)} %get-tuple-element.52), channel_id=1, source_target_pairs={{0,2},{2,0},{1,3},{3,1},{4,6},{6,4},{5,7},{7,5},{8,10},{10,8},{9,1... | collective-permute-start | bytes 294920 | tf_op jit(solution)/shard_map/ppermute | solution.py:619
  56.0 0.7 collective-permute-start.17
  56.7 1.4 %collective-permute-start.18 = (bf16[48,1024]{1,0:T(8,128)(2,1)S(1)}, bf16[48,1024]{1,0:T(8,128)(2,1)S(1)}, u32[]{:S(2)}, u32[]{:S(2)}) collective-permute-start(bf16[48,1024]{1,0:T(8,128)(2,1)S(1)} %get-tuple-element.54), channel_id=1, source_target_pairs={{0,18},{2,16},{16,2},{18,0},{1,19},{3,17},{17,3},{19,1},{4,22},{6,... | collective-permute-start | bytes 294920 | tf_op jit(solution)/shard_map/ppermute | solution.py:617
  58.1 1.4 %collective-permute-done.16.side_ref = bf16[48,1024]{1,0:T(8,128)(2,1)S(1)} collective-permute-done((bf16[48,1024]{1,0:T(8,128)(2,1)S(1)}, bf16[48,1024]{1,0:T(8,128)(2,1)S(1)}, u32[]{:S(2)}, u32[]{:S(2)}) %collective-permute-start.16) | collective-permute-done | bytes 98336 | tf_op jit(solution)/shard_map/ppermute | solution.py:619
  59.6 3.2 %collective-permute-done.17.far_ref = bf16[48,1024]{1,0:T(8,128)(2,1)S(1)} collective-permute-done((bf16[48,1024]{1,0:T(8,128)(2,1)S(1)}, bf16[48,1024]{1,0:T(8,128)(2,1)S(1)}, u32[]{:S(2)}, u32[]{:S(2)}) %collective-permute-start.17) | collective-permute-done | bytes 98336 | tf_op jit(solution)/shard_map/ppermute | solution.py:618
  62.8 0.2 merge.1
  63.0 1.4 %collective-permute-start.19 = (bf16[32,1024]{1,0:T(8,128)(2,1)S(1)}, bf16[32,1024]{1,0:T(8,128)(2,1)S(1)}, u32[]{:S(2)}, u32[]{:S(2)}) collective-permute-start(bf16[32,1024]{1,0:T(8,128)(2,1)S(1)} %get-tuple-element.56), channel_id=1, source_target_pairs={{0,4},{4,0},{8,12},{12,8},{1,5},{5,1},{9,13},{13,9},{2,6},{6,2},{1... | collective-permute-start | bytes 196616 | tf_op jit(solution)/shard_map/ppermute | solution.py:627
  64.4 0.9 %collective-permute-start.20 = (bf16[32,1024]{1,0:T(8,128)(2,1)S(1)}, bf16[32,1024]{1,0:T(8,128)(2,1)S(1)}, u32[]{:S(2)}, u32[]{:S(2)}) collective-permute-start(bf16[32,1024]{1,0:T(8,128)(2,1)S(1)} %get-tuple-element.57), channel_id=1, source_target_pairs={{0,8},{4,12},{8,0},{12,4},{1,9},{5,13},{9,1},{13,5},{2,10},{6,14},... | collective-permute-start | bytes 196616 | tf_op jit(solution)/shard_map/ppermute | solution.py:627
  65.3 2.2 %collective-permute-start.21 = (bf16[32,1024]{1,0:T(8,128)(2,1)S(1)}, bf16[32,1024]{1,0:T(8,128)(2,1)S(1)}, u32[]{:S(2)}, u32[]{:S(2)}) collective-permute-start(bf16[32,1024]{1,0:T(8,128)(2,1)S(1)} %get-tuple-element.58), channel_id=1, source_target_pairs={{0,12},{4,8},{8,4},{12,0},{1,13},{5,9},{9,5},{13,1},{2,14},{6,10},... | collective-permute-start | bytes 196616 | tf_op jit(solution)/shard_map/ppermute | solution.py:627
  67.5 1.0 %collective-permute-done.19.one_ref = bf16[32,1024]{1,0:T(8,128)(2,1)S(1)} collective-permute-done((bf16[32,1024]{1,0:T(8,128)(2,1)S(1)}, bf16[32,1024]{1,0:T(8,128)(2,1)S(1)}, u32[]{:S(2)}, u32[]{:S(2)}) %collective-permute-start.19) | collective-permute-done | bytes 65568 | tf_op jit(solution)/shard_map/ppermute | solution.py:627
  68.5 1.8 %collective-permute-done.20.two_ref = bf16[32,1024]{1,0:T(8,128)(2,1)S(1)} collective-permute-done((bf16[32,1024]{1,0:T(8,128)(2,1)S(1)}, bf16[32,1024]{1,0:T(8,128)(2,1)S(1)}, u32[]{:S(2)}, u32[]{:S(2)}) %collective-permute-start.20) | collective-permute-done | bytes 65568 | tf_op jit(solution)/shard_map/ppermute | solution.py:627
  70.3 1.2 %collective-permute-done.21.three_ref = bf16[32,1024]{1,0:T(8,128)(2,1)S(1)} collective-permute-done((bf16[32,1024]{1,0:T(8,128)(2,1)S(1)}, bf16[32,1024]{1,0:T(8,128)(2,1)S(1)}, u32[]{:S(2)}, u32[]{:S(2)}) %collective-permute-start.21) | collective-permute-done | bytes 65568 | tf_op jit(solution)/shard_map/ppermute | solution.py:627
  71.5 1.0 %scatter.1 = bf16[128,1024]{1,0:T(8,128)(2,1)} custom-call(bf16[32,128]{1,0:T(8,128)(2,1)S(1)} %get-tuple-element.32.pick_ref, bf16[32,1024]{1,0:T(8,128)(2,1)S(1)} %get-tuple-element.55.zero_ref, bf16[32,1024]{1,0:T(8,128)(2,1)S(1)} %collective-permute-done.19.one_ref, bf16[32,1024]{1,0:T(8,128)(2,1)S(1)} %collective-permute-done.20.two_ref, ...), custom_call_target="tpu_custom_call" | custom-call | tf_op jit(solution)/shard_map/scatter/pallas_call | solution.py:628
  (17 shorter events, 0.2 us)
Async XLA Ops:
  1.1 4.2 %collective-permute-start = (bf16[32,1024]{1,0:T(8,128)(2,1)S(1)}, bf16[32,1024]{1,0:T(8,128)(2,1)S(1)}, u32[]{:S(2)}, u32[]{:S(2)}) collective-permute-start(bf16[32,1024]{1,0:T(8,128)(2,1)S(1)} %get-tuple-element.35), channel_id=1, source_target_pairs={{0,0},{1,4},{2,8},{3,12},{4,1},{5,5},{6,9},{7,13},{8,2},{9,6},{10,... | collective-permute-start | bytes 196616 | tf_op jit(solution)/shard_map/ppermute | solution.py:506
  5.3 9.8 %collective-permute-start.3 = (bf16[32,1024]{1,0:T(8,128)(2,1)S(1)}, bf16[32,1024]{1,0:T(8,128)(2,1)S(1)}, u32[]{:S(2)}, u32[]{:S(2)}) collective-permute-start(bf16[32,1024]{1,0:T(8,128)(2,1)S(1)} %pass.1.refs_0_), channel_id=1, source_target_pairs={{0,3},{1,2},{2,1},{3,0},{4,7},{5,6},{6,5},{7,4},{8,11},{9,10},{10,... | collective-permute-start | bytes 196616 | tf_op jit(solution)/shard_map/ppermute | solution.py:523
  12.9 4.9 %collective-permute-start.2 = (bf16[32,1024]{1,0:T(8,128)(2,1)S(1)}, bf16[32,1024]{1,0:T(8,128)(2,1)S(1)}, u32[]{:S(2)}, u32[]{:S(2)}) collective-permute-start(bf16[32,1024]{1,0:T(8,128)(2,1)S(1)} %pass.1.refs_0_), channel_id=1, source_target_pairs={{0,2},{1,3},{2,0},{3,1},{4,6},{5,7},{6,4},{7,5},{8,10},{9,11},{10,... | collective-permute-start | bytes 196616 | tf_op jit(solution)/shard_map/ppermute | solution.py:523
  13.8 4.0 %collective-permute-start.1 = (bf16[32,1024]{1,0:T(8,128)(2,1)S(1)}, bf16[32,1024]{1,0:T(8,128)(2,1)S(1)}, u32[]{:S(2)}, u32[]{:S(2)}) collective-permute-start(bf16[32,1024]{1,0:T(8,128)(2,1)S(1)} %pass.1.refs_0_), channel_id=1, source_target_pairs={{0,1},{1,0},{2,3},{3,2},{4,5},{5,4},{6,7},{7,6},{8,9},{9,8},{10,11... | collective-permute-start | bytes 196616 | tf_op jit(solution)/shard_map/ppermute | solution.py:523
  18.3 8.5 %collective-permute-start.6 = (bf16[32,1024]{1,0:T(8,128)(2,1)S(1)}, bf16[32,1024]{1,0:T(8,128)(2,1)S(1)}, u32[]{:S(2)}, u32[]{:S(2)}) collective-permute-start(bf16[32,1024]{1,0:T(8,128)(2,1)S(1)} %get-tuple-element.59), channel_id=1, source_target_pairs={{0,4},{4,0},{8,12},{12,8},{1,5},{5,1},{9,13},{13,9},{2,6},{6,2},{1... | collective-permute-start | bytes 196616 | tf_op jit(solution)/shard_map/ppermute | solution.py:532
  18.4 8.4 %collective-permute-start.5 = (bf16[32,1024]{1,0:T(8,128)(2,1)S(1)}, bf16[32,1024]{1,0:T(8,128)(2,1)S(1)}, u32[]{:S(2)}, u32[]{:S(2)}) collective-permute-start(bf16[32,1024]{1,0:T(8,128)(2,1)S(1)} %get-tuple-element.60), channel_id=1, source_target_pairs={{0,8},{4,12},{8,0},{12,4},{1,9},{5,13},{9,1},{13,5},{2,10},{6,14},... | collective-permute-start | bytes 196616 | tf_op jit(solution)/shard_map/ppermute | solution.py:532
  20.9 6.2 %collective-permute-start.4 = (bf16[32,1024]{1,0:T(8,128)(2,1)S(1)}, bf16[32,1024]{1,0:T(8,128)(2,1)S(1)}, u32[]{:S(2)}, u32[]{:S(2)}) collective-permute-start(bf16[32,1024]{1,0:T(8,128)(2,1)S(1)} %get-tuple-element.61), channel_id=1, source_target_pairs={{0,12},{4,8},{8,4},{12,0},{1,13},{5,9},{9,5},{13,1},{2,14},{6,10},... | collective-permute-start | bytes 196616 | tf_op jit(solution)/shard_map/ppermute | solution.py:532
  22.8 4.3 %copy-start = (bf16[1024,4]{0,1:T(4,128)(2,1)S(1)}, bf16[1024,4]{0,1:T(4,128)(2,1)}, u32[]{:S(2)}) copy-start(bf16[1024,4]{0,1:T(4,128)(2,1)} %param.14) | copy-start | bytes 24580
  22.8 4.3 %copy-start.1 = (bf16[2,1024]{1,0:T(2,128)(2,1)S(1)}, bf16[2,1024]{1,0:T(2,128)(2,1)}, u32[]{:S(2)}) copy-start(bf16[2,1024]{1,0:T(2,128)(2,1)} %gain_ref.1) | copy-start | bytes 12292
  27.3 8.1 %collective-permute-start.9 = (bf16[32,1152]{1,0:T(8,128)(2,1)S(1)}, bf16[32,1152]{1,0:T(8,128)(2,1)S(1)}, u32[]{:S(2)}, u32[]{:S(2)}) collective-permute-start(bf16[32,1152]{1,0:T(8,128)(2,1)S(1)} %norm.1.after_ref.zero_ref), channel_id=1, source_target_pairs={{0,4},{4,0},{8,12},{12,8},{1,5},{5,1},{9,13},{13,9},{2,6},{6,2},{1... | collective-permute-start | bytes 221192 | tf_op jit(solution)/shard_map/ppermute | solution.py:547
  28.6 6.8 %collective-permute-start.8 = (bf16[32,1152]{1,0:T(8,128)(2,1)S(1)}, bf16[32,1152]{1,0:T(8,128)(2,1)S(1)}, u32[]{:S(2)}, u32[]{:S(2)}) collective-permute-start(bf16[32,1152]{1,0:T(8,128)(2,1)S(1)} %norm.1.after_ref.zero_ref), channel_id=1, source_target_pairs={{0,8},{4,12},{8,0},{12,4},{1,9},{5,13},{9,1},{13,5},{2,10},{6,14},... | collective-permute-start | bytes 221192 | tf_op jit(solution)/shard_map/ppermute | solution.py:547
  29.8 6.3 %collective-permute-start.7 = (bf16[32,1152]{1,0:T(8,128)(2,1)S(1)}, bf16[32,1152]{1,0:T(8,128)(2,1)S(1)}, u32[]{:S(2)}, u32[]{:S(2)}) collective-permute-start(bf16[32,1152]{1,0:T(8,128)(2,1)S(1)} %norm.1.after_ref.zero_ref), channel_id=1, source_target_pairs={{0,12},{4,8},{8,4},{12,0},{1,13},{5,9},{9,5},{13,1},{2,14},{6,10},... | collective-permute-start | bytes 221192 | tf_op jit(solution)/shard_map/ppermute | solution.py:547
  36.2 6.9 %collective-permute-start.10 = (bf16[48,1152]{1,0:T(8,128)(2,1)S(1)}, bf16[48,1152]{1,0:T(8,128)(2,1)S(1)}, u32[]{:S(2)}, u32[]{:S(2)}) collective-permute-start(bf16[48,1152]{1,0:T(8,128)(2,1)S(1)} %get-tuple-element.40), channel_id=1, source_target_pairs={{0,18},{2,16},{16,2},{18,0},{1,19},{3,17},{17,3},{19,1},{4,22},{6,... | collective-permute-start | bytes 331784 | tf_op jit(solution)/shard_map/ppermute | solution.py:563
  38.6 4.7 %collective-permute-start.11 = (bf16[48,1152]{1,0:T(8,128)(2,1)S(1)}, bf16[48,1152]{1,0:T(8,128)(2,1)S(1)}, u32[]{:S(2)}, u32[]{:S(2)}) collective-permute-start(bf16[48,1152]{1,0:T(8,128)(2,1)S(1)} %get-tuple-element.41), channel_id=1, source_target_pairs={{0,2},{2,0},{1,3},{3,1},{4,6},{6,4},{5,7},{7,5},{8,10},{10,8},{9,1... | collective-permute-start | bytes 331784 | tf_op jit(solution)/shard_map/ppermute | solution.py:565
  39.3 4.7 %collective-permute-start.12 = (bf16[48,1152]{1,0:T(8,128)(2,1)S(1)}, bf16[48,1152]{1,0:T(8,128)(2,1)S(1)}, u32[]{:S(2)}, u32[]{:S(2)}) collective-permute-start(bf16[48,1152]{1,0:T(8,128)(2,1)S(1)} %get-tuple-element.42), channel_id=1, source_target_pairs={{0,16},{16,0},{1,17},{17,1},{2,18},{18,2},{3,19},{19,3},{4,20},{20... | collective-permute-start | bytes 331784 | tf_op jit(solution)/shard_map/ppermute | solution.py:564
  47.1 4.6 %collective-permute-start.13 = (bf16[2768,128]{1,0:T(8,128)(2,1)S(1)}, bf16[2768,128]{1,0:T(8,128)(2,1)S(1)}, u32[]{:S(2)}, u32[]{:S(2)}) collective-permute-start(bf16[2768,128]{1,0:T(8,128)(2,1)S(1)} %get-tuple-element.45.gate_ref), channel_id=1, source_target_pairs={{0,1},{1,0},{2,3},{3,2},{4,5},{5,4},{6,7},{7,6},{8,9},{9,8},{10,11... | collective-permute-start | bytes 2125832 | tf_op jit(solution)/shard_map/ppermute | solution.py:594
  49.6 2.1 %collective-permute-start.14 = (bf16[2064,128]{1,0:T(8,128)(2,1)S(1)}, bf16[2064,128]{1,0:T(8,128)(2,1)S(1)}, u32[]{:S(2)}, u32[]{:S(2)}) collective-permute-start(bf16[2064,128]{1,0:T(8,128)(2,1)S(1)} %up.2.up_ref), channel_id=1, source_target_pairs={{0,1},{1,0},{2,3},{3,2},{4,5},{5,4},{6,7},{7,6},{8,9},{9,8},{10,11... | collective-permute-start | bytes 1585160 | tf_op jit(solution)/shard_map/ppermute | solution.py:595
  51.1 1.5 %collective-permute-start.15 = (bf16[688,128]{1,0:T(8,128)(2,1)S(1)}, bf16[688,128]{1,0:T(8,128)(2,1)S(1)}, u32[]{:S(2)}, u32[]{:S(2)}) collective-permute-start(bf16[688,128]{1,0:T(8,128)(2,1)S(1)} %up.3.up_ref), channel_id=1, source_target_pairs={{0,1},{1,0},{2,3},{3,2},{4,5},{5,4},{6,7},{7,6},{8,9},{9,8},{10,11... | collective-permute-start | bytes 528392 | tf_op jit(solution)/shard_map/ppermute | solution.py:595
  54.6 5.0 %collective-permute-start.16 = (bf16[48,1024]{1,0:T(8,128)(2,1)S(1)}, bf16[48,1024]{1,0:T(8,128)(2,1)S(1)}, u32[]{:S(2)}, u32[]{:S(2)}) collective-permute-start(bf16[48,1024]{1,0:T(8,128)(2,1)S(1)} %get-tuple-element.52), channel_id=1, source_target_pairs={{0,2},{2,0},{1,3},{3,1},{4,6},{6,4},{5,7},{7,5},{8,10},{10,8},{9,1... | collective-permute-start | bytes 294920 | tf_op jit(solution)/shard_map/ppermute | solution.py:619
  56.0 6.8 %collective-permute-start.17 = (bf16[48,1024]{1,0:T(8,128)(2,1)S(1)}, bf16[48,1024]{1,0:T(8,128)(2,1)S(1)}, u32[]{:S(2)}, u32[]{:S(2)}) collective-permute-start(bf16[48,1024]{1,0:T(8,128)(2,1)S(1)} %get-tuple-element.53), channel_id=1, source_target_pairs={{0,16},{16,0},{1,17},{17,1},{2,18},{18,2},{3,19},{19,3},{4,20},{20... | collective-permute-start | bytes 294920 | tf_op jit(solution)/shard_map/ppermute | solution.py:618
  56.7 6.1 %collective-permute-start.18 = (bf16[48,1024]{1,0:T(8,128)(2,1)S(1)}, bf16[48,1024]{1,0:T(8,128)(2,1)S(1)}, u32[]{:S(2)}, u32[]{:S(2)}) collective-permute-start(bf16[48,1024]{1,0:T(8,128)(2,1)S(1)} %get-tuple-element.54), channel_id=1, source_target_pairs={{0,18},{2,16},{16,2},{18,0},{1,19},{3,17},{17,3},{19,1},{4,22},{6,... | collective-permute-start | bytes 294920 | tf_op jit(solution)/shard_map/ppermute | solution.py:617
  63.0 5.5 %collective-permute-start.19 = (bf16[32,1024]{1,0:T(8,128)(2,1)S(1)}, bf16[32,1024]{1,0:T(8,128)(2,1)S(1)}, u32[]{:S(2)}, u32[]{:S(2)}) collective-permute-start(bf16[32,1024]{1,0:T(8,128)(2,1)S(1)} %get-tuple-element.56), channel_id=1, source_target_pairs={{0,4},{4,0},{8,12},{12,8},{1,5},{5,1},{9,13},{13,9},{2,6},{6,2},{1... | collective-permute-start | bytes 196616 | tf_op jit(solution)/shard_map/ppermute | solution.py:627
  64.4 5.9 %collective-permute-start.20 = (bf16[32,1024]{1,0:T(8,128)(2,1)S(1)}, bf16[32,1024]{1,0:T(8,128)(2,1)S(1)}, u32[]{:S(2)}, u32[]{:S(2)}) collective-permute-start(bf16[32,1024]{1,0:T(8,128)(2,1)S(1)} %get-tuple-element.57), channel_id=1, source_target_pairs={{0,8},{4,12},{8,0},{12,4},{1,9},{5,13},{9,1},{13,5},{2,10},{6,14},... | collective-permute-start | bytes 196616 | tf_op jit(solution)/shard_map/ppermute | solution.py:627
  65.3 6.2 %collective-permute-start.21 = (bf16[32,1024]{1,0:T(8,128)(2,1)S(1)}, bf16[32,1024]{1,0:T(8,128)(2,1)S(1)}, u32[]{:S(2)}, u32[]{:S(2)}) collective-permute-start(bf16[32,1024]{1,0:T(8,128)(2,1)S(1)} %get-tuple-element.58), channel_id=1, source_target_pairs={{0,12},{4,8},{8,4},{12,0},{1,13},{5,9},{9,5},{13,1},{2,14},{6,10},... | collective-permute-start | bytes 196616 | tf_op jit(solution)/shard_map/ppermute | solution.py:627

commit v15 on v14

--- a/solution.py
+++ b/solution.py
@@ -242,7 +242,7 @@
 
 
 def keep_gate_kernel(
-    pick_ref, residual_hbm, gate_ref, proj_ref, gate_held, proj_held, rest_ref, residual_ref, semaphores
+    _, pick_ref, residual_hbm, gate_ref, proj_ref, gate_held, proj_held, rest_ref, residual_ref, semaphores
 ):
     copies = [
         pltpu.make_async_copy(residual_hbm, residual_ref, semaphores.at[0]),
@@ -257,12 +257,8 @@
         copy.wait()
 
 
-def pass_kernel(rows_ref, _, out_ref):
-    out_ref[...] = rows_ref[...]
-
-
 def project_kernel(*refs):
-    block_refs, (weight_ref, out_ref, rows_ref) = refs[:4], refs[4:]
+    block_refs, weight_ref, (out_ref, rows_ref) = refs[:4], refs[4], refs[-2:]
     slots = block_refs[0].shape[0]
     for u, block_ref in enumerate(block_refs):
         rows_ref[u * slots : (u + 1) * slots, :] = block_ref[...]
@@ -513,20 +509,19 @@
             pltpu.VMEM(out_proj.shape, jnp.bfloat16),
             array(slots, columns, dtype=jnp.float32),
         ],
-        [ON_CHIP, IN_HBM, IN_HBM, IN_HBM],
-        [pick, in_hbm(residual), in_hbm(gate_weight.swapaxes(1, 2)), in_hbm(out_proj)],
+        [ANYWHERE, ON_CHIP, IN_HBM, IN_HBM, IN_HBM],
+        [near, pick, in_hbm(residual), in_hbm(gate_weight.swapaxes(1, 2)), in_hbm(out_proj)],
         scratch=[pltpu.VMEM((tokens, columns), jnp.bfloat16), pltpu.SemaphoreType.DMA((3,))],
         moved=units * width,
         limit=2 << 20,
     )
-    block = call(pass_kernel, "pass", array(slots, columns), [ON_CHIP] * 2, [near, gate_first])
-    plane = [lax.ppermute(block, ("mod", "fsdp"), crossed(2, u)) for u in (3, 2, 1)][::-1]
+    plane = [lax.ppermute(near, ("mod", "fsdp"), crossed(2, u)) for u in (3, 2, 1)][::-1]
     partial = call(
         project_kernel,
         "project",
         array(4, slots, columns),
-        [ON_CHIP] * 5,
-        [block, *plane, proj_held],
+        [ON_CHIP] * 6,
+        [near, *plane, proj_held, gate_first],
         scratch=[pltpu.VMEM((rows, columns), jnp.bfloat16)],
     )
     sums = [lax.ppermute(partial[v], "tok", crossed(2, v)) for v in (3, 2, 1)][::-1]

time: 72.6 us -> 72.6 us (level)
  waiting for transfers between devices: 15.2 us -> 11.6 us
  starting transfers between devices: 30.3 us -> 33.8 us
    ppermute x3, waiting for transfers between devices: 4 us -> 0.01 us  [paired_local(): lax.ppermute(near, ('mod', 'fsdp'), crossed(2, u))]
    ppermute x3, starting transfers between devices: 8.47 us -> 12 us  [paired_local(): lax.ppermute(near, ('mod', 'fsdp'), crossed(2, u))]
    ppermute x3, waiting for transfers between devices: 0.25 us -> 1.11 us  [paired_local(): lax.ppermute(partial[v], 'tok', crossed(2, v))]
    pallas_call x15 -> x14, Pallas kernels: 25.8 us -> 25.8 us  [call(): pl.pallas_call(kernel, out_shape=outs, in_specs=specs, out_specs=jax.tree...]
  transfers between devices with their start and end apart: 22 -> 22, of which waited for: 13 -> 10; matrix products, arithmetic and copies ran while one was open for 0% -> 0% of each run, Pallas kernels for 25% -> 26%
where the time goes in v15:
time: 72.6 us; the launch traced here: 72.4 us
  starting transfers between devices  33.8 us (47%)
  Pallas kernels  26.8 us (37%)
  waiting for transfers between devices  11.6 us (16%)
    pallas_call x14, Pallas kernels, call(): pl.pallas_call(kernel, out_shape=outs, in_specs=specs, out_specs=jax.tree...  25.8 us
    ppermute x3, starting transfers between devices, paired_local(): lax.ppermute(near, ('mod', 'fsdp'), crossed(2, u))  12 us
    ppermute x3, starting transfers between devices, paired_local(): lax.ppermute(partial[v], 'tok', crossed(2, v))  4.45 us
    ppermute x3, starting transfers between devices, paired_local(): lax.ppermute(merged[v], 'tok', crossed(2, v))  4.45 us
    ppermute x3, starting transfers between devices, paired_local(): lax.ppermute(packed, 'tok', crossed(2, v))  4.42 us
    ppermute x3, waiting for transfers between devices, paired_local(): lax.ppermute(merged[v], 'tok', crossed(2, v))  4.12 us
    ppermute x1, waiting for transfers between devices, paired_local(): from_far = lax.ppermute(to_far, 'groups', SWAP)  2.67 us
    ppermute x1, starting transfers between devices, paired_local(): side_far = lax.ppermute(to_corner_rows, both_axes, crossed(2, 3))  2.02 us
  transfers between devices with their start and end apart: 22, of which 10 were waited for; matrix products, arithmetic and copies ran while one was open for 0% of the time, Pallas kernels for 26%

profile of v15, /device:TPU:0, one launch (start us, length us, event | category | flops | bytes accessed | tf_op | source)
XLA Modules:
  0.0 72.4 jit_solution(14307495172283563026)
XLA Ops:
  0.0 1.1 %select.1 = (bf16[32,1024]{1,0:T(8,128)(2,1)S(1)}, bf16[32,128]{1,0:T(8,128)(2,1)S(1)}, f32[8,128]{1,0:T(8,128)S(1)}) custom-call(s32[4,16]{1,0:T(4,128)} %rows_hbm.1, bf16[128,1024]{1,0:T(8,128)(2,1)} %context_hbm.1), custom_call_target="tpu_custom_call" | custom-call | tf_op jit(solution)/shard_map/select/pallas_call | solution.py:173
  1.1 0.7 collective-permute-start
  1.8 10.3 %collective-permute-start.3 = (bf16[32,1024]{1,0:T(8,128)(2,1)S(1)}, bf16[32,1024]{1,0:T(8,128)(2,1)S(1)}, u32[]{:S(2)}, u32[]{:S(2)}) collective-permute-start(bf16[32,1024]{1,0:T(8,128)(2,1)S(1)} %collective-permute-done._.refs_0_), channel_id=1, source_target_pairs={{0,3},{1,2},{2,1},{3,0},{4,7},{5,6},{6,5},{7,4},{8,11},{9,10},{10,... | collective-permute-start | bytes 196616 | tf_op jit(solution)/shard_map/ppermute | solution.py:518
  12.1 1.6 %collective-permute-start.2 = (bf16[32,1024]{1,0:T(8,128)(2,1)S(1)}, bf16[32,1024]{1,0:T(8,128)(2,1)S(1)}, u32[]{:S(2)}, u32[]{:S(2)}) collective-permute-start(bf16[32,1024]{1,0:T(8,128)(2,1)S(1)} %collective-permute-done._.refs_0_), channel_id=1, source_target_pairs={{0,2},{1,3},{2,0},{3,1},{4,6},{5,7},{6,4},{7,5},{8,10},{9,11},{10,... | collective-permute-start | bytes 196616 | tf_op jit(solution)/shard_map/ppermute | solution.py:518
  13.7 0.1 collective-permute-start.1
  13.8 3.5 %keep_gate.1 = (bf16[1488,2048]{1,0:T(8,128)(2,1)S(1)}, bf16[1024,1024]{1,0:T(8,128)(2,1)S(1)}, f32[32,1024]{1,0:T(8,128)S(1)}) custom-call(bf16[32,1024]{1,0:T(8,128)(2,1)S(1)} %collective-permute-done._.refs_0_, bf16[32,128]{1,0:T(8,128)(2,1)S(1)} %get-tuple-element.32.pick_ref, bf16[128,1024]{1,0:T(8,128)(2,1)} %residual_hbm.1, ...), custom_call_target="tpu_custom_call" | custom-call | bytes 5636096 | tf_op jit(solution)/shard_map/keep_gate/pallas_call | solution.py:173
  17.3 0.5 project.1.after_ref.partial_ref
  17.8 0.3 collective-permute-start.6
  18.1 3.2 %collective-permute-start.5 = (bf16[32,1024]{1,0:T(8,128)(2,1)S(1)}, bf16[32,1024]{1,0:T(8,128)(2,1)S(1)}, u32[]{:S(2)}, u32[]{:S(2)}) collective-permute-start(bf16[32,1024]{1,0:T(8,128)(2,1)S(1)} %get-tuple-element.60), channel_id=1, source_target_pairs={{0,8},{4,12},{8,0},{12,4},{1,9},{5,13},{9,1},{13,5},{2,10},{6,14},... | collective-permute-start | bytes 196616 | tf_op jit(solution)/shard_map/ppermute | solution.py:527
  21.2 1.0 %collective-permute-start.4 = (bf16[32,1024]{1,0:T(8,128)(2,1)S(1)}, bf16[32,1024]{1,0:T(8,128)(2,1)S(1)}, u32[]{:S(2)}, u32[]{:S(2)}) collective-permute-start(bf16[32,1024]{1,0:T(8,128)(2,1)S(1)} %get-tuple-element.61), channel_id=1, source_target_pairs={{0,12},{4,8},{8,4},{12,0},{1,13},{5,9},{9,5},{13,1},{2,14},{6,10},... | collective-permute-start | bytes 196616 | tf_op jit(solution)/shard_map/ppermute | solution.py:527
  22.3 4.0 %keep_more.1 = (bf16[1264,2048]{1,0:T(8,128)(2,1)S(1)}, bf16[1216,2048]{1,0:T(8,128)(2,1)S(1)}) custom-call(bf16[4,32,1024]{2,1,0:T(8,128)(2,1)S(1)} %project.1.after_ref.partial_ref, bf16[2,2752,2048]{2,1,0:T(8,128)(2,1)} %bitcast.11, bf16[2,2752,2048]{2,1,0:T(8,128)(2,1)} %bitcast.12), custom_call_target="tpu_custom_call" | custom-call | bytes 10158080 | tf_op jit(solution)/shard_map/keep_more/pallas_call | solution.py:173
  26.3 1.1 %collective-permute-done.4.three_ref = bf16[32,1024]{1,0:T(8,128)(2,1)S(1)} collective-permute-done((bf16[32,1024]{1,0:T(8,128)(2,1)S(1)}, bf16[32,1024]{1,0:T(8,128)(2,1)S(1)}, u32[]{:S(2)}, u32[]{:S(2)}) %collective-permute-start.4) | collective-permute-done | bytes 65568 | tf_op jit(solution)/shard_map/ppermute | solution.py:527
  27.4 0.2 norm.1.after_ref.zero_ref
  27.7 0.9 %collective-permute-start.9 = (bf16[32,1152]{1,0:T(8,128)(2,1)S(1)}, bf16[32,1152]{1,0:T(8,128)(2,1)S(1)}, u32[]{:S(2)}, u32[]{:S(2)}) collective-permute-start(bf16[32,1152]{1,0:T(8,128)(2,1)S(1)} %norm.1.after_ref.zero_ref), channel_id=1, source_target_pairs={{0,4},{4,0},{8,12},{12,8},{1,5},{5,1},{9,13},{13,9},{2,6},{6,2},{1... | collective-permute-start | bytes 221192 | tf_op jit(solution)/shard_map/ppermute | solution.py:542
  28.5 1.5 %collective-permute-start.8 = (bf16[32,1152]{1,0:T(8,128)(2,1)S(1)}, bf16[32,1152]{1,0:T(8,128)(2,1)S(1)}, u32[]{:S(2)}, u32[]{:S(2)}) collective-permute-start(bf16[32,1152]{1,0:T(8,128)(2,1)S(1)} %norm.1.after_ref.zero_ref), channel_id=1, source_target_pairs={{0,8},{4,12},{8,0},{12,4},{1,9},{5,13},{9,1},{13,5},{2,10},{6,14},... | collective-permute-start | bytes 221192 | tf_op jit(solution)/shard_map/ppermute | solution.py:542
  30.0 2.1 %collective-permute-start.7 = (bf16[32,1152]{1,0:T(8,128)(2,1)S(1)}, bf16[32,1152]{1,0:T(8,128)(2,1)S(1)}, u32[]{:S(2)}, u32[]{:S(2)}) collective-permute-start(bf16[32,1152]{1,0:T(8,128)(2,1)S(1)} %norm.1.after_ref.zero_ref), channel_id=1, source_target_pairs={{0,12},{4,8},{8,4},{12,0},{1,13},{5,9},{9,5},{13,1},{2,14},{6,10},... | collective-permute-start | bytes 221192 | tf_op jit(solution)/shard_map/ppermute | solution.py:542
  32.1 3.7 %keep_up.1 = (bf16[1536,2048]{1,0:T(8,128)(2,1)S(1)}, bf16[736,2048]{1,0:T(8,128)(2,1)S(1)}) custom-call(bf16[32,1152]{1,0:T(8,128)(2,1)S(1)} %norm.1.after_ref.zero_ref, bf16[2,2752,2048]{2,1,0:T(8,128)(2,1)} %bitcast.13, bf16[2,2752,2048]{2,1,0:T(8,128)(2,1)} %refs_0_.1), custom_call_target="tpu_custom_call" | custom-call | bytes 9306112 | tf_op jit(solution)/shard_map/keep_up/pallas_call | solution.py:173
  35.8 0.5 collective-permute-done.7.three_ref
  36.3 0.2 arrange.1
  36.4 2.0 %collective-permute-start.10 = (bf16[48,1152]{1,0:T(8,128)(2,1)S(1)}, bf16[48,1152]{1,0:T(8,128)(2,1)S(1)}, u32[]{:S(2)}, u32[]{:S(2)}) collective-permute-start(bf16[48,1152]{1,0:T(8,128)(2,1)S(1)} %get-tuple-element.40), channel_id=1, source_target_pairs={{0,18},{2,16},{16,2},{18,0},{1,19},{3,17},{17,3},{19,1},{4,22},{6,... | collective-permute-start | bytes 331784 | tf_op jit(solution)/shard_map/ppermute | solution.py:558
  38.5 1.0 %collective-permute-start.11 = (bf16[48,1152]{1,0:T(8,128)(2,1)S(1)}, bf16[48,1152]{1,0:T(8,128)(2,1)S(1)}, u32[]{:S(2)}, u32[]{:S(2)}) collective-permute-start(bf16[48,1152]{1,0:T(8,128)(2,1)S(1)} %get-tuple-element.41), channel_id=1, source_target_pairs={{0,2},{2,0},{1,3},{3,1},{4,6},{6,4},{5,7},{7,5},{8,10},{10,8},{9,1... | collective-permute-start | bytes 331784 | tf_op jit(solution)/shard_map/ppermute | solution.py:560
  39.5 0.5 collective-permute-start.12
  40.0 3.4 %keep_down.1.refs_2_.second_ref = bf16[2016,2048]{1,0:T(8,128)(2,1)S(1)} custom-call(bf16[48,1152]{1,0:T(8,128)(2,1)S(1)} %get-tuple-element.43.after_ref.own_ref, bf16[2,2752,2048]{2,1,0:T(8,128)(2,1)} %refs_0_.1), custom_call_target="tpu_custom_call" | custom-call | bytes 8257536 | tf_op jit(solution)/shard_map/keep_down/pallas_call | solution.py:173
  43.4 0.0 collective-permute-done.11.side_own_ref
  43.4 0.8 %collective-permute-done.12.far_ref = bf16[48,1152]{1,0:T(8,128)(2,1)S(1)} collective-permute-done((bf16[48,1152]{1,0:T(8,128)(2,1)S(1)}, bf16[48,1152]{1,0:T(8,128)(2,1)S(1)}, u32[]{:S(2)}, u32[]{:S(2)}) %collective-permute-start.12) | collective-permute-done | bytes 110624 | tf_op jit(solution)/shard_map/ppermute | solution.py:559
  44.2 3.1 %gate.1 = (bf16[2768,128]{1,0:T(8,128)(2,1)S(1)}, bf16[128,2048]{1,0:T(8,128)(2,1)S(1)}) custom-call(bf16[48,1152]{1,0:T(8,128)(2,1)S(1)} %collective-permute-done.10.side_far_ref, bf16[48,1152]{1,0:T(8,128)(2,1)S(1)} %collective-permute-done.11.side_own_ref, bf16[48,1152]{1,0:T(8,128)(2,1)S(1)} %collective-permute-done.12.far_ref, ...), custom_call_target="tpu_custom_call" | custom-call | flops 1442840576 | tf_op jit(solution)/shard_map/gate/pallas_call | solution.py:173
  47.4 0.1 collective-permute-start.13
  47.4 2.4 %up.2.up_ref = bf16[2064,128]{1,0:T(8,128)(2,1)S(1)} custom-call(bf16[128,2048]{1,0:T(8,128)(2,1)S(1)} %get-tuple-element.46.rows_ref, bf16[1216,2048]{1,0:T(8,128)(2,1)S(1)} %get-tuple-element.38._.refs_0_, bf16[1536,2048]{1,0:T(8,128)(2,1)S(1)} %get-tuple-element.39._.refs_1_.refs_0_), custom_call_target="tpu_custom_call" | custom-call | flops 1082130432 | tf_op jit(solution)/shard_map/up/pallas_call | solution.py:173
  49.8 0.6 collective-permute-start.14
  50.4 0.9 %up.3.up_ref = bf16[688,128]{1,0:T(8,128)(2,1)S(1)} custom-call(bf16[128,2048]{1,0:T(8,128)(2,1)S(1)} %get-tuple-element.46.rows_ref, bf16[1536,2048]{1,0:T(8,128)(2,1)S(1)} %get-tuple-element.39._.refs_1_.refs_0_), custom_call_target="tpu_custom_call" | custom-call | flops 360710144 | tf_op jit(solution)/shard_map/up/pallas_call | solution.py:173
  51.3 0.1 collective-permute-start.15
  51.4 0.6 collective-permute-done.14.up_other_ref
  51.9 0.7 activation.1
  52.6 0.1 collective-permute-done.15.other_ref
  52.8 2.0 %down.1 = (bf16[48,1024]{1,0:T(8,128)(2,1)S(1)}, bf16[48,1024]{1,0:T(8,128)(2,1)S(1)}, bf16[48,1024]{1,0:T(8,128)(2,1)S(1)}, bf16[48,1024]{1,0:T(8,128)(2,1)S(1)}) custom-call(bf16[2064,128]{1,0:T(8,128)(2,1)S(1)} %get-tuple-element.47.act_early_ref, f32[688,128]{1,0:T(8,128)S(1)} %get-tuple-element.48.silu_ref, f32[8,128]{1,0:T(8,128)S(1)} %get-tuple-element.49.stat_ref, ...), custom_call_target="tpu_custom_call" | custom-call | flops 1442840576 | tf_op jit(solution)/shard_map/down/pallas_call | solution.py:173
  54.8 1.1 %collective-permute-start.16 = (bf16[48,1024]{1,0:T(8,128)(2,1)S(1)}, bf16[48,1024]{1,0:T(8,128)(2,1)S(1)}, u32[]{:S(2)}, u32[]{:S(2)}) collective-permute-start(bf16[48,1024]{1,0:T(8,128)(2,1)S(1)} %get-tuple-element.52), channel_id=1, source_target_pairs={{0,2},{2,0},{1,3},{3,1},{4,6},{6,4},{5,7},{7,5},{8,10},{10,8},{9,1... | collective-permute-start | bytes 294920 | tf_op jit(solution)/shard_map/ppermute | solution.py:614
  55.9 0.7 collective-permute-start.17
  56.6 1.8 %collective-permute-start.18 = (bf16[48,1024]{1,0:T(8,128)(2,1)S(1)}, bf16[48,1024]{1,0:T(8,128)(2,1)S(1)}, u32[]{:S(2)}, u32[]{:S(2)}) collective-permute-start(bf16[48,1024]{1,0:T(8,128)(2,1)S(1)} %get-tuple-element.54), channel_id=1, source_target_pairs={{0,18},{2,16},{16,2},{18,0},{1,19},{3,17},{17,3},{19,1},{4,22},{6,... | collective-permute-start | bytes 294920 | tf_op jit(solution)/shard_map/ppermute | solution.py:612
  58.4 1.6 %collective-permute-done.16.side_ref = bf16[48,1024]{1,0:T(8,128)(2,1)S(1)} collective-permute-done((bf16[48,1024]{1,0:T(8,128)(2,1)S(1)}, bf16[48,1024]{1,0:T(8,128)(2,1)S(1)}, u32[]{:S(2)}, u32[]{:S(2)}) %collective-permute-start.16) | collective-permute-done | bytes 98336 | tf_op jit(solution)/shard_map/ppermute | solution.py:614
  60.0 2.7 %collective-permute-done.17.far_ref = bf16[48,1024]{1,0:T(8,128)(2,1)S(1)} collective-permute-done((bf16[48,1024]{1,0:T(8,128)(2,1)S(1)}, bf16[48,1024]{1,0:T(8,128)(2,1)S(1)}, u32[]{:S(2)}, u32[]{:S(2)}) %collective-permute-start.17) | collective-permute-done | bytes 98336 | tf_op jit(solution)/shard_map/ppermute | solution.py:613
  62.7 0.2 merge.1
  62.8 1.3 %collective-permute-start.19 = (bf16[32,1024]{1,0:T(8,128)(2,1)S(1)}, bf16[32,1024]{1,0:T(8,128)(2,1)S(1)}, u32[]{:S(2)}, u32[]{:S(2)}) collective-permute-start(bf16[32,1024]{1,0:T(8,128)(2,1)S(1)} %get-tuple-element.56), channel_id=1, source_target_pairs={{0,4},{4,0},{8,12},{12,8},{1,5},{5,1},{9,13},{13,9},{2,6},{6,2},{1... | collective-permute-start | bytes 196616 | tf_op jit(solution)/shard_map/ppermute | solution.py:622
  64.1 1.1 %collective-permute-start.20 = (bf16[32,1024]{1,0:T(8,128)(2,1)S(1)}, bf16[32,1024]{1,0:T(8,128)(2,1)S(1)}, u32[]{:S(2)}, u32[]{:S(2)}) collective-permute-start(bf16[32,1024]{1,0:T(8,128)(2,1)S(1)} %get-tuple-element.57), channel_id=1, source_target_pairs={{0,8},{4,12},{8,0},{12,4},{1,9},{5,13},{9,1},{13,5},{2,10},{6,14},... | collective-permute-start | bytes 196616 | tf_op jit(solution)/shard_map/ppermute | solution.py:622
  65.2 2.0 %collective-permute-start.21 = (bf16[32,1024]{1,0:T(8,128)(2,1)S(1)}, bf16[32,1024]{1,0:T(8,128)(2,1)S(1)}, u32[]{:S(2)}, u32[]{:S(2)}) collective-permute-start(bf16[32,1024]{1,0:T(8,128)(2,1)S(1)} %get-tuple-element.58), channel_id=1, source_target_pairs={{0,12},{4,8},{8,4},{12,0},{1,13},{5,9},{9,5},{13,1},{2,14},{6,10},... | collective-permute-start | bytes 196616 | tf_op jit(solution)/shard_map/ppermute | solution.py:622
  67.3 0.5 collective-permute-done.19.one_ref
  67.8 2.5 %collective-permute-done.20.two_ref = bf16[32,1024]{1,0:T(8,128)(2,1)S(1)} collective-permute-done((bf16[32,1024]{1,0:T(8,128)(2,1)S(1)}, bf16[32,1024]{1,0:T(8,128)(2,1)S(1)}, u32[]{:S(2)}, u32[]{:S(2)}) %collective-permute-start.20) | collective-permute-done | bytes 65568 | tf_op jit(solution)/shard_map/ppermute | solution.py:622
  70.3 1.1 %collective-permute-done.21.three_ref = bf16[32,1024]{1,0:T(8,128)(2,1)S(1)} collective-permute-done((bf16[32,1024]{1,0:T(8,128)(2,1)S(1)}, bf16[32,1024]{1,0:T(8,128)(2,1)S(1)}, u32[]{:S(2)}, u32[]{:S(2)}) %collective-permute-start.21) | collective-permute-done | bytes 65568 | tf_op jit(solution)/shard_map/ppermute | solution.py:622
  71.4 1.0 %scatter.1 = bf16[128,1024]{1,0:T(8,128)(2,1)} custom-call(bf16[32,128]{1,0:T(8,128)(2,1)S(1)} %get-tuple-element.32.pick_ref, bf16[32,1024]{1,0:T(8,128)(2,1)S(1)} %get-tuple-element.55.zero_ref, bf16[32,1024]{1,0:T(8,128)(2,1)S(1)} %collective-permute-done.19.one_ref, bf16[32,1024]{1,0:T(8,128)(2,1)S(1)} %collective-permute-done.20.two_ref, ...), custom_call_target="tpu_custom_call" | custom-call | tf_op jit(solution)/shard_map/scatter/pallas_call | solution.py:623
  (16 shorter events, 0.1 us)
Async XLA Ops:
  1.1 0.7 collective-permute-start
  1.8 15.5 %collective-permute-start.3 = (bf16[32,1024]{1,0:T(8,128)(2,1)S(1)}, bf16[32,1024]{1,0:T(8,128)(2,1)S(1)}, u32[]{:S(2)}, u32[]{:S(2)}) collective-permute-start(bf16[32,1024]{1,0:T(8,128)(2,1)S(1)} %collective-permute-done._.refs_0_), channel_id=1, source_target_pairs={{0,3},{1,2},{2,1},{3,0},{4,7},{5,6},{6,5},{7,4},{8,11},{9,10},{10,... | collective-permute-start | bytes 196616 | tf_op jit(solution)/shard_map/ppermute | solution.py:518
  12.1 5.2 %collective-permute-start.2 = (bf16[32,1024]{1,0:T(8,128)(2,1)S(1)}, bf16[32,1024]{1,0:T(8,128)(2,1)S(1)}, u32[]{:S(2)}, u32[]{:S(2)}) collective-permute-start(bf16[32,1024]{1,0:T(8,128)(2,1)S(1)} %collective-permute-done._.refs_0_), channel_id=1, source_target_pairs={{0,2},{1,3},{2,0},{3,1},{4,6},{5,7},{6,4},{7,5},{8,10},{9,11},{10,... | collective-permute-start | bytes 196616 | tf_op jit(solution)/shard_map/ppermute | solution.py:518
  13.7 3.6 %collective-permute-start.1 = (bf16[32,1024]{1,0:T(8,128)(2,1)S(1)}, bf16[32,1024]{1,0:T(8,128)(2,1)S(1)}, u32[]{:S(2)}, u32[]{:S(2)}) collective-permute-start(bf16[32,1024]{1,0:T(8,128)(2,1)S(1)} %collective-permute-done._.refs_0_), channel_id=1, source_target_pairs={{0,1},{1,0},{2,3},{3,2},{4,5},{5,4},{6,7},{7,6},{8,9},{9,8},{10,11... | collective-permute-start | bytes 196616 | tf_op jit(solution)/shard_map/ppermute | solution.py:518
  17.8 8.5 %collective-permute-start.6 = (bf16[32,1024]{1,0:T(8,128)(2,1)S(1)}, bf16[32,1024]{1,0:T(8,128)(2,1)S(1)}, u32[]{:S(2)}, u32[]{:S(2)}) collective-permute-start(bf16[32,1024]{1,0:T(8,128)(2,1)S(1)} %get-tuple-element.59), channel_id=1, source_target_pairs={{0,4},{4,0},{8,12},{12,8},{1,5},{5,1},{9,13},{13,9},{2,6},{6,2},{1... | collective-permute-start | bytes 196616 | tf_op jit(solution)/shard_map/ppermute | solution.py:527
  18.1 8.2 %collective-permute-start.5 = (bf16[32,1024]{1,0:T(8,128)(2,1)S(1)}, bf16[32,1024]{1,0:T(8,128)(2,1)S(1)}, u32[]{:S(2)}, u32[]{:S(2)}) collective-permute-start(bf16[32,1024]{1,0:T(8,128)(2,1)S(1)} %get-tuple-element.60), channel_id=1, source_target_pairs={{0,8},{4,12},{8,0},{12,4},{1,9},{5,13},{9,1},{13,5},{2,10},{6,14},... | collective-permute-start | bytes 196616 | tf_op jit(solution)/shard_map/ppermute | solution.py:527
  21.2 6.2 %collective-permute-start.4 = (bf16[32,1024]{1,0:T(8,128)(2,1)S(1)}, bf16[32,1024]{1,0:T(8,128)(2,1)S(1)}, u32[]{:S(2)}, u32[]{:S(2)}) collective-permute-start(bf16[32,1024]{1,0:T(8,128)(2,1)S(1)} %get-tuple-element.61), channel_id=1, source_target_pairs={{0,12},{4,8},{8,4},{12,0},{1,13},{5,9},{9,5},{13,1},{2,14},{6,10},... | collective-permute-start | bytes 196616 | tf_op jit(solution)/shard_map/ppermute | solution.py:527
  22.3 5.1 %copy-start = (bf16[1024,4]{0,1:T(4,128)(2,1)S(1)}, bf16[1024,4]{0,1:T(4,128)(2,1)}, u32[]{:S(2)}) copy-start(bf16[1024,4]{0,1:T(4,128)(2,1)} %param.14) | copy-start | bytes 24580
  22.3 5.1 %copy-start.1 = (bf16[2,1024]{1,0:T(2,128)(2,1)S(1)}, bf16[2,1024]{1,0:T(2,128)(2,1)}, u32[]{:S(2)}) copy-start(bf16[2,1024]{1,0:T(2,128)(2,1)} %gain_ref.1) | copy-start | bytes 12292
  27.7 8.1 %collective-permute-start.9 = (bf16[32,1152]{1,0:T(8,128)(2,1)S(1)}, bf16[32,1152]{1,0:T(8,128)(2,1)S(1)}, u32[]{:S(2)}, u32[]{:S(2)}) collective-permute-start(bf16[32,1152]{1,0:T(8,128)(2,1)S(1)} %norm.1.after_ref.zero_ref), channel_id=1, source_target_pairs={{0,4},{4,0},{8,12},{12,8},{1,5},{5,1},{9,13},{13,9},{2,6},{6,2},{1... | collective-permute-start | bytes 221192 | tf_op jit(solution)/shard_map/ppermute | solution.py:542
  28.5 7.2 %collective-permute-start.8 = (bf16[32,1152]{1,0:T(8,128)(2,1)S(1)}, bf16[32,1152]{1,0:T(8,128)(2,1)S(1)}, u32[]{:S(2)}, u32[]{:S(2)}) collective-permute-start(bf16[32,1152]{1,0:T(8,128)(2,1)S(1)} %norm.1.after_ref.zero_ref), channel_id=1, source_target_pairs={{0,8},{4,12},{8,0},{12,4},{1,9},{5,13},{9,1},{13,5},{2,10},{6,14},... | collective-permute-start | bytes 221192 | tf_op jit(solution)/shard_map/ppermute | solution.py:542
  30.0 6.3 %collective-permute-start.7 = (bf16[32,1152]{1,0:T(8,128)(2,1)S(1)}, bf16[32,1152]{1,0:T(8,128)(2,1)S(1)}, u32[]{:S(2)}, u32[]{:S(2)}) collective-permute-start(bf16[32,1152]{1,0:T(8,128)(2,1)S(1)} %norm.1.after_ref.zero_ref), channel_id=1, source_target_pairs={{0,12},{4,8},{8,4},{12,0},{1,13},{5,9},{9,5},{13,1},{2,14},{6,10},... | collective-permute-start | bytes 221192 | tf_op jit(solution)/shard_map/ppermute | solution.py:542
  36.4 6.9 %collective-permute-start.10 = (bf16[48,1152]{1,0:T(8,128)(2,1)S(1)}, bf16[48,1152]{1,0:T(8,128)(2,1)S(1)}, u32[]{:S(2)}, u32[]{:S(2)}) collective-permute-start(bf16[48,1152]{1,0:T(8,128)(2,1)S(1)} %get-tuple-element.40), channel_id=1, source_target_pairs={{0,18},{2,16},{16,2},{18,0},{1,19},{3,17},{17,3},{19,1},{4,22},{6,... | collective-permute-start | bytes 331784 | tf_op jit(solution)/shard_map/ppermute | solution.py:558
  38.5 4.9 %collective-permute-start.11 = (bf16[48,1152]{1,0:T(8,128)(2,1)S(1)}, bf16[48,1152]{1,0:T(8,128)(2,1)S(1)}, u32[]{:S(2)}, u32[]{:S(2)}) collective-permute-start(bf16[48,1152]{1,0:T(8,128)(2,1)S(1)} %get-tuple-element.41), channel_id=1, source_target_pairs={{0,2},{2,0},{1,3},{3,1},{4,6},{6,4},{5,7},{7,5},{8,10},{10,8},{9,1... | collective-permute-start | bytes 331784 | tf_op jit(solution)/shard_map/ppermute | solution.py:560
  39.5 4.7 %collective-permute-start.12 = (bf16[48,1152]{1,0:T(8,128)(2,1)S(1)}, bf16[48,1152]{1,0:T(8,128)(2,1)S(1)}, u32[]{:S(2)}, u32[]{:S(2)}) collective-permute-start(bf16[48,1152]{1,0:T(8,128)(2,1)S(1)} %get-tuple-element.42), channel_id=1, source_target_pairs={{0,16},{16,0},{1,17},{17,1},{2,18},{18,2},{3,19},{19,3},{4,20},{20... | collective-permute-start | bytes 331784 | tf_op jit(solution)/shard_map/ppermute | solution.py:559
  47.4 4.6 %collective-permute-start.13 = (bf16[2768,128]{1,0:T(8,128)(2,1)S(1)}, bf16[2768,128]{1,0:T(8,128)(2,1)S(1)}, u32[]{:S(2)}, u32[]{:S(2)}) collective-permute-start(bf16[2768,128]{1,0:T(8,128)(2,1)S(1)} %get-tuple-element.45.gate_ref), channel_id=1, source_target_pairs={{0,1},{1,0},{2,3},{3,2},{4,5},{5,4},{6,7},{7,6},{8,9},{9,8},{10,11... | collective-permute-start | bytes 2125832 | tf_op jit(solution)/shard_map/ppermute | solution.py:589
  49.8 2.1 %collective-permute-start.14 = (bf16[2064,128]{1,0:T(8,128)(2,1)S(1)}, bf16[2064,128]{1,0:T(8,128)(2,1)S(1)}, u32[]{:S(2)}, u32[]{:S(2)}) collective-permute-start(bf16[2064,128]{1,0:T(8,128)(2,1)S(1)} %up.2.up_ref), channel_id=1, source_target_pairs={{0,1},{1,0},{2,3},{3,2},{4,5},{5,4},{6,7},{7,6},{8,9},{9,8},{10,11... | collective-permute-start | bytes 1585160 | tf_op jit(solution)/shard_map/ppermute | solution.py:590
  51.3 1.5 %collective-permute-start.15 = (bf16[688,128]{1,0:T(8,128)(2,1)S(1)}, bf16[688,128]{1,0:T(8,128)(2,1)S(1)}, u32[]{:S(2)}, u32[]{:S(2)}) collective-permute-start(bf16[688,128]{1,0:T(8,128)(2,1)S(1)} %up.3.up_ref), channel_id=1, source_target_pairs={{0,1},{1,0},{2,3},{3,2},{4,5},{5,4},{6,7},{7,6},{8,9},{9,8},{10,11... | collective-permute-start | bytes 528392 | tf_op jit(solution)/shard_map/ppermute | solution.py:590
  54.8 5.2 %collective-permute-start.16 = (bf16[48,1024]{1,0:T(8,128)(2,1)S(1)}, bf16[48,1024]{1,0:T(8,128)(2,1)S(1)}, u32[]{:S(2)}, u32[]{:S(2)}) collective-permute-start(bf16[48,1024]{1,0:T(8,128)(2,1)S(1)} %get-tuple-element.52), channel_id=1, source_target_pairs={{0,2},{2,0},{1,3},{3,1},{4,6},{6,4},{5,7},{7,5},{8,10},{10,8},{9,1... | collective-permute-start | bytes 294920 | tf_op jit(solution)/shard_map/ppermute | solution.py:614
  55.9 6.8 %collective-permute-start.17 = (bf16[48,1024]{1,0:T(8,128)(2,1)S(1)}, bf16[48,1024]{1,0:T(8,128)(2,1)S(1)}, u32[]{:S(2)}, u32[]{:S(2)}) collective-permute-start(bf16[48,1024]{1,0:T(8,128)(2,1)S(1)} %get-tuple-element.53), channel_id=1, source_target_pairs={{0,16},{16,0},{1,17},{17,1},{2,18},{18,2},{3,19},{19,3},{4,20},{20... | collective-permute-start | bytes 294920 | tf_op jit(solution)/shard_map/ppermute | solution.py:613
  56.6 6.1 %collective-permute-start.18 = (bf16[48,1024]{1,0:T(8,128)(2,1)S(1)}, bf16[48,1024]{1,0:T(8,128)(2,1)S(1)}, u32[]{:S(2)}, u32[]{:S(2)}) collective-permute-start(bf16[48,1024]{1,0:T(8,128)(2,1)S(1)} %get-tuple-element.54), channel_id=1, source_target_pairs={{0,18},{2,16},{16,2},{18,0},{1,19},{3,17},{17,3},{19,1},{4,22},{6,... | collective-permute-start | bytes 294920 | tf_op jit(solution)/shard_map/ppermute | solution.py:612
  62.8 5.0 %collective-permute-start.19 = (bf16[32,1024]{1,0:T(8,128)(2,1)S(1)}, bf16[32,1024]{1,0:T(8,128)(2,1)S(1)}, u32[]{:S(2)}, u32[]{:S(2)}) collective-permute-start(bf16[32,1024]{1,0:T(8,128)(2,1)S(1)} %get-tuple-element.56), channel_id=1, source_target_pairs={{0,4},{4,0},{8,12},{12,8},{1,5},{5,1},{9,13},{13,9},{2,6},{6,2},{1... | collective-permute-start | bytes 196616 | tf_op jit(solution)/shard_map/ppermute | solution.py:622
  64.1 6.2 %collective-permute-start.20 = (bf16[32,1024]{1,0:T(8,128)(2,1)S(1)}, bf16[32,1024]{1,0:T(8,128)(2,1)S(1)}, u32[]{:S(2)}, u32[]{:S(2)}) collective-permute-start(bf16[32,1024]{1,0:T(8,128)(2,1)S(1)} %get-tuple-element.57), channel_id=1, source_target_pairs={{0,8},{4,12},{8,0},{12,4},{1,9},{5,13},{9,1},{13,5},{2,10},{6,14},... | collective-permute-start | bytes 196616 | tf_op jit(solution)/shard_map/ppermute | solution.py:622
  65.2 6.2 %collective-permute-start.21 = (bf16[32,1024]{1,0:T(8,128)(2,1)S(1)}, bf16[32,1024]{1,0:T(8,128)(2,1)S(1)}, u32[]{:S(2)}, u32[]{:S(2)}) collective-permute-start(bf16[32,1024]{1,0:T(8,128)(2,1)S(1)} %get-tuple-element.58), channel_id=1, source_target_pairs={{0,12},{4,8},{8,4},{12,0},{1,13},{5,9},{9,5},{13,1},{2,14},{6,10},... | collective-permute-start | bytes 196616 | tf_op jit(solution)/shard_map/ppermute | solution.py:622

commit v16 on v15

--- a/solution.py
+++ b/solution.py
@@ -500,7 +500,7 @@
     )
     turned = [(t * 4 + q, q * 4 + t) for t in range(4) for q in range(4)]
     near = lax.ppermute(picked, ("tok", "mod", "fsdp"), turned)
-    gate_units, up_units, down_units = [round(units * part / TILE) * TILE for part in (0.54, 0.44, 0.27)]
+    gate_units, up_units, down_units = [round(units * part / TILE) * TILE for part in (0.3, 0.3, 0.25)]
     gate_first, proj_held, rest = call(
         keep_gate_kernel,
         "keep_gate",

time: 72.6 us -> 72.5 us (level)
  transfers between devices with their start and end apart: 22 -> 22, of which waited for: 10 -> 11; matrix products, arithmetic and copies ran while one was open for 0% -> 0% of each run, Pallas kernels for 26% -> 25%
where the time goes in v16:
time: 72.5 us; the launch traced here: 72.3 us
  starting transfers between devices  33.8 us (47%)
  Pallas kernels  26.8 us (37%)
  waiting for transfers between devices  11.6 us (16%)
    pallas_call x14, Pallas kernels, call(): pl.pallas_call(kernel, out_shape=outs, in_specs=specs, out_specs=jax.tree...  25.8 us
    ppermute x3, starting transfers between devices, paired_local(): lax.ppermute(near, ('mod', 'fsdp'), crossed(2, u))  12 us
    ppermute x3, starting transfers between devices, paired_local(): lax.ppermute(partial[v], 'tok', crossed(2, v))  4.45 us
    ppermute x3, starting transfers between devices, paired_local(): lax.ppermute(merged[v], 'tok', crossed(2, v))  4.45 us
    ppermute x3, starting transfers between devices, paired_local(): lax.ppermute(packed, 'tok', crossed(2, v))  4.42 us
    ppermute x3, waiting for transfers between devices, paired_local(): lax.ppermute(merged[v], 'tok', crossed(2, v))  4.32 us
    ppermute x1, waiting for transfers between devices, paired_local(): from_far = lax.ppermute(to_far, 'groups', SWAP)  2.23 us
    ppermute x1, starting transfers between devices, paired_local(): from_side_far = lax.ppermute(to_side_far, both_axes, crossed(2, 3))  1.94 us
  transfers between devices with their start and end apart: 22, of which 11 were waited for; matrix products, arithmetic and copies ran while one was open for 0% of the time, Pallas kernels for 25%

profile of v16, /device:TPU:0, one launch (start us, length us, event | category | flops | bytes accessed | tf_op | source)
XLA Modules:
  0.0 72.3 jit_solution(18144432513768300340)
XLA Ops:
  0.0 1.1 %select.1 = (bf16[32,1024]{1,0:T(8,128)(2,1)S(1)}, bf16[32,128]{1,0:T(8,128)(2,1)S(1)}, f32[8,128]{1,0:T(8,128)S(1)}) custom-call(s32[4,16]{1,0:T(4,128)} %rows_hbm.1, bf16[128,1024]{1,0:T(8,128)(2,1)} %context_hbm.1), custom_call_target="tpu_custom_call" | custom-call | tf_op jit(solution)/shard_map/select/pallas_call | solution.py:173
  1.1 0.7 collective-permute-start
  1.8 10.3 %collective-permute-start.3 = (bf16[32,1024]{1,0:T(8,128)(2,1)S(1)}, bf16[32,1024]{1,0:T(8,128)(2,1)S(1)}, u32[]{:S(2)}, u32[]{:S(2)}) collective-permute-start(bf16[32,1024]{1,0:T(8,128)(2,1)S(1)} %collective-permute-done._.refs_0_), channel_id=1, source_target_pairs={{0,3},{1,2},{2,1},{3,0},{4,7},{5,6},{6,5},{7,4},{8,11},{9,10},{10,... | collective-permute-start | bytes 196616 | tf_op jit(solution)/shard_map/ppermute | solution.py:518
  12.1 1.6 %collective-permute-start.2 = (bf16[32,1024]{1,0:T(8,128)(2,1)S(1)}, bf16[32,1024]{1,0:T(8,128)(2,1)S(1)}, u32[]{:S(2)}, u32[]{:S(2)}) collective-permute-start(bf16[32,1024]{1,0:T(8,128)(2,1)S(1)} %collective-permute-done._.refs_0_), channel_id=1, source_target_pairs={{0,2},{1,3},{2,0},{3,1},{4,6},{5,7},{6,4},{7,5},{8,10},{9,11},{10,... | collective-permute-start | bytes 196616 | tf_op jit(solution)/shard_map/ppermute | solution.py:518
  13.7 0.1 collective-permute-start.1
  13.8 2.7 %keep_gate.1 = (bf16[832,2048]{1,0:T(8,128)(2,1)S(1)}, bf16[1024,1024]{1,0:T(8,128)(2,1)S(1)}, f32[32,1024]{1,0:T(8,128)S(1)}) custom-call(bf16[32,1024]{1,0:T(8,128)(2,1)S(1)} %collective-permute-done._.refs_0_, bf16[32,128]{1,0:T(8,128)(2,1)S(1)} %get-tuple-element.32.pick_ref, bf16[128,1024]{1,0:T(8,128)(2,1)} %residual_hbm.1, ...), custom_call_target="tpu_custom_call" | custom-call | bytes 5636096 | tf_op jit(solution)/shard_map/keep_gate/pallas_call | solution.py:173
  16.5 0.3 collective-permute-done.2.refs_2_
  16.8 0.4 project.1.after_ref.partial_ref
  17.3 0.3 collective-permute-start.6
  17.6 3.2 %collective-permute-start.5 = (bf16[32,1024]{1,0:T(8,128)(2,1)S(1)}, bf16[32,1024]{1,0:T(8,128)(2,1)S(1)}, u32[]{:S(2)}, u32[]{:S(2)}) collective-permute-start(bf16[32,1024]{1,0:T(8,128)(2,1)S(1)} %get-tuple-element.60), channel_id=1, source_target_pairs={{0,8},{4,12},{8,0},{12,4},{1,9},{5,13},{9,1},{13,5},{2,10},{6,14},... | collective-permute-start | bytes 196616 | tf_op jit(solution)/shard_map/ppermute | solution.py:527
  20.8 1.0 %collective-permute-start.4 = (bf16[32,1024]{1,0:T(8,128)(2,1)S(1)}, bf16[32,1024]{1,0:T(8,128)(2,1)S(1)}, u32[]{:S(2)}, u32[]{:S(2)}) collective-permute-start(bf16[32,1024]{1,0:T(8,128)(2,1)S(1)} %get-tuple-element.61), channel_id=1, source_target_pairs={{0,12},{4,8},{8,4},{12,0},{1,13},{5,9},{9,5},{13,1},{2,14},{6,10},... | collective-permute-start | bytes 196616 | tf_op jit(solution)/shard_map/ppermute | solution.py:527
  21.8 4.2 %keep_more.1 = (bf16[1920,2048]{1,0:T(8,128)(2,1)S(1)}, bf16[832,2048]{1,0:T(8,128)(2,1)S(1)}) custom-call(bf16[4,32,1024]{2,1,0:T(8,128)(2,1)S(1)} %project.1.after_ref.partial_ref, bf16[2,2752,2048]{2,1,0:T(8,128)(2,1)} %bitcast.11, bf16[2,2752,2048]{2,1,0:T(8,128)(2,1)} %bitcast.12), custom_call_target="tpu_custom_call" | custom-call | bytes 11272192 | tf_op jit(solution)/shard_map/keep_more/pallas_call | solution.py:173
  26.1 0.9 %collective-permute-done.4.three_ref = bf16[32,1024]{1,0:T(8,128)(2,1)S(1)} collective-permute-done((bf16[32,1024]{1,0:T(8,128)(2,1)S(1)}, bf16[32,1024]{1,0:T(8,128)(2,1)S(1)}, u32[]{:S(2)}, u32[]{:S(2)}) %collective-permute-start.4) | collective-permute-done | bytes 65568 | tf_op jit(solution)/shard_map/ppermute | solution.py:527
  27.0 0.2 norm.1.after_ref.zero_ref
  27.2 0.9 %collective-permute-start.9 = (bf16[32,1152]{1,0:T(8,128)(2,1)S(1)}, bf16[32,1152]{1,0:T(8,128)(2,1)S(1)}, u32[]{:S(2)}, u32[]{:S(2)}) collective-permute-start(bf16[32,1152]{1,0:T(8,128)(2,1)S(1)} %norm.1.after_ref.zero_ref), channel_id=1, source_target_pairs={{0,4},{4,0},{8,12},{12,8},{1,5},{5,1},{9,13},{13,9},{2,6},{6,2},{1... | collective-permute-start | bytes 221192 | tf_op jit(solution)/shard_map/ppermute | solution.py:542
  28.1 1.7 %collective-permute-start.8 = (bf16[32,1152]{1,0:T(8,128)(2,1)S(1)}, bf16[32,1152]{1,0:T(8,128)(2,1)S(1)}, u32[]{:S(2)}, u32[]{:S(2)}) collective-permute-start(bf16[32,1152]{1,0:T(8,128)(2,1)S(1)} %norm.1.after_ref.zero_ref), channel_id=1, source_target_pairs={{0,8},{4,12},{8,0},{12,4},{1,9},{5,13},{9,1},{13,5},{2,10},{6,14},... | collective-permute-start | bytes 221192 | tf_op jit(solution)/shard_map/ppermute | solution.py:542
  29.8 1.9 %collective-permute-start.7 = (bf16[32,1152]{1,0:T(8,128)(2,1)S(1)}, bf16[32,1152]{1,0:T(8,128)(2,1)S(1)}, u32[]{:S(2)}, u32[]{:S(2)}) collective-permute-start(bf16[32,1152]{1,0:T(8,128)(2,1)S(1)} %norm.1.after_ref.zero_ref), channel_id=1, source_target_pairs={{0,12},{4,8},{8,4},{12,0},{1,13},{5,9},{9,5},{13,1},{2,14},{6,10},... | collective-permute-start | bytes 221192 | tf_op jit(solution)/shard_map/ppermute | solution.py:542
  31.6 4.0 %keep_up.1 = (bf16[1920,2048]{1,0:T(8,128)(2,1)S(1)}, bf16[688,2048]{1,0:T(8,128)(2,1)S(1)}) custom-call(bf16[32,1152]{1,0:T(8,128)(2,1)S(1)} %norm.1.after_ref.zero_ref, bf16[2,2752,2048]{2,1,0:T(8,128)(2,1)} %bitcast.13, bf16[2,2752,2048]{2,1,0:T(8,128)(2,1)} %refs_0_.1), custom_call_target="tpu_custom_call" | custom-call | bytes 10682368 | tf_op jit(solution)/shard_map/keep_up/pallas_call | solution.py:173
  35.7 0.3 collective-permute-done.7.three_ref
  36.0 0.2 arrange.1
  36.2 1.9 %collective-permute-start.10 = (bf16[48,1152]{1,0:T(8,128)(2,1)S(1)}, bf16[48,1152]{1,0:T(8,128)(2,1)S(1)}, u32[]{:S(2)}, u32[]{:S(2)}) collective-permute-start(bf16[48,1152]{1,0:T(8,128)(2,1)S(1)} %get-tuple-element.40), channel_id=1, source_target_pairs={{0,18},{2,16},{16,2},{18,0},{1,19},{3,17},{17,3},{19,1},{4,22},{6,... | collective-permute-start | bytes 331784 | tf_op jit(solution)/shard_map/ppermute | solution.py:558
  38.1 1.2 %collective-permute-start.11 = (bf16[48,1152]{1,0:T(8,128)(2,1)S(1)}, bf16[48,1152]{1,0:T(8,128)(2,1)S(1)}, u32[]{:S(2)}, u32[]{:S(2)}) collective-permute-start(bf16[48,1152]{1,0:T(8,128)(2,1)S(1)} %get-tuple-element.41), channel_id=1, source_target_pairs={{0,2},{2,0},{1,3},{3,1},{4,6},{6,4},{5,7},{7,5},{8,10},{10,8},{9,1... | collective-permute-start | bytes 331784 | tf_op jit(solution)/shard_map/ppermute | solution.py:560
  39.3 0.4 collective-permute-start.12
  39.8 3.4 %keep_down.1.refs_2_.second_ref = bf16[2064,2048]{1,0:T(8,128)(2,1)S(1)} custom-call(bf16[48,1152]{1,0:T(8,128)(2,1)S(1)} %get-tuple-element.43.after_ref.own_ref, bf16[2,2752,2048]{2,1,0:T(8,128)(2,1)} %refs_0_.1), custom_call_target="tpu_custom_call" | custom-call | bytes 8454144 | tf_op jit(solution)/shard_map/keep_down/pallas_call | solution.py:173
  43.2 0.1 collective-permute-done.11.side_own_ref
  43.2 0.8 %collective-permute-done.12.far_ref = bf16[48,1152]{1,0:T(8,128)(2,1)S(1)} collective-permute-done((bf16[48,1152]{1,0:T(8,128)(2,1)S(1)}, bf16[48,1152]{1,0:T(8,128)(2,1)S(1)}, u32[]{:S(2)}, u32[]{:S(2)}) %collective-permute-start.12) | collective-permute-done | bytes 110624 | tf_op jit(solution)/shard_map/ppermute | solution.py:559
  44.1 3.1 %gate.1 = (bf16[2768,128]{1,0:T(8,128)(2,1)S(1)}, bf16[128,2048]{1,0:T(8,128)(2,1)S(1)}) custom-call(bf16[48,1152]{1,0:T(8,128)(2,1)S(1)} %collective-permute-done.10.side_far_ref, bf16[48,1152]{1,0:T(8,128)(2,1)S(1)} %collective-permute-done.11.side_own_ref, bf16[48,1152]{1,0:T(8,128)(2,1)S(1)} %collective-permute-done.12.far_ref, ...), custom_call_target="tpu_custom_call" | custom-call | flops 1442840576 | tf_op jit(solution)/shard_map/gate/pallas_call | solution.py:173
  47.2 0.1 collective-permute-start.13
  47.3 2.4 %up.2.up_ref = bf16[2064,128]{1,0:T(8,128)(2,1)S(1)} custom-call(bf16[128,2048]{1,0:T(8,128)(2,1)S(1)} %get-tuple-element.46.rows_ref, bf16[832,2048]{1,0:T(8,128)(2,1)S(1)} %get-tuple-element.38._.refs_0_, bf16[1920,2048]{1,0:T(8,128)(2,1)S(1)} %get-tuple-element.39._.refs_1_.refs_0_), custom_call_target="tpu_custom_call" | custom-call | flops 1082130432 | tf_op jit(solution)/shard_map/up/pallas_call | solution.py:173
  49.6 0.6 collective-permute-start.14
  50.2 0.9 %up.3.up_ref = bf16[688,128]{1,0:T(8,128)(2,1)S(1)} custom-call(bf16[128,2048]{1,0:T(8,128)(2,1)S(1)} %get-tuple-element.46.rows_ref, bf16[1920,2048]{1,0:T(8,128)(2,1)S(1)} %get-tuple-element.39._.refs_1_.refs_0_), custom_call_target="tpu_custom_call" | custom-call | flops 360710144 | tf_op jit(solution)/shard_map/up/pallas_call | solution.py:173
  51.1 0.1 collective-permute-start.15
  51.2 0.6 collective-permute-done.14.up_other_ref
  51.8 0.7 activation.1
  52.4 0.2 collective-permute-done.15.other_ref
  52.6 2.2 %down.1 = (bf16[48,1024]{1,0:T(8,128)(2,1)S(1)}, bf16[48,1024]{1,0:T(8,128)(2,1)S(1)}, bf16[48,1024]{1,0:T(8,128)(2,1)S(1)}, bf16[48,1024]{1,0:T(8,128)(2,1)S(1)}) custom-call(bf16[2064,128]{1,0:T(8,128)(2,1)S(1)} %get-tuple-element.47.act_early_ref, f32[688,128]{1,0:T(8,128)S(1)} %get-tuple-element.48.silu_ref, f32[8,128]{1,0:T(8,128)S(1)} %get-tuple-element.49.stat_ref, ...), custom_call_target="tpu_custom_call" | custom-call | flops 1442840576 | tf_op jit(solution)/shard_map/down/pallas_call | solution.py:173
  54.8 0.9 %collective-permute-start.16 = (bf16[48,1024]{1,0:T(8,128)(2,1)S(1)}, bf16[48,1024]{1,0:T(8,128)(2,1)S(1)}, u32[]{:S(2)}, u32[]{:S(2)}) collective-permute-start(bf16[48,1024]{1,0:T(8,128)(2,1)S(1)} %get-tuple-element.52), channel_id=1, source_target_pairs={{0,2},{2,0},{1,3},{3,1},{4,6},{6,4},{5,7},{7,5},{8,10},{10,8},{9,1... | collective-permute-start | bytes 294920 | tf_op jit(solution)/shard_map/ppermute | solution.py:614
  55.6 0.7 %collective-permute-start.17 = (bf16[48,1024]{1,0:T(8,128)(2,1)S(1)}, bf16[48,1024]{1,0:T(8,128)(2,1)S(1)}, u32[]{:S(2)}, u32[]{:S(2)}) collective-permute-start(bf16[48,1024]{1,0:T(8,128)(2,1)S(1)} %get-tuple-element.53), channel_id=1, source_target_pairs={{0,16},{16,0},{1,17},{17,1},{2,18},{18,2},{3,19},{19,3},{4,20},{20... | collective-permute-start | bytes 294920 | tf_op jit(solution)/shard_map/ppermute | solution.py:613
  56.4 1.9 %collective-permute-start.18 = (bf16[48,1024]{1,0:T(8,128)(2,1)S(1)}, bf16[48,1024]{1,0:T(8,128)(2,1)S(1)}, u32[]{:S(2)}, u32[]{:S(2)}) collective-permute-start(bf16[48,1024]{1,0:T(8,128)(2,1)S(1)} %get-tuple-element.54), channel_id=1, source_target_pairs={{0,18},{2,16},{16,2},{18,0},{1,19},{3,17},{17,3},{19,1},{4,22},{6,... | collective-permute-start | bytes 294920 | tf_op jit(solution)/shard_map/ppermute | solution.py:612
  58.3 1.9 %collective-permute-done.16.side_ref = bf16[48,1024]{1,0:T(8,128)(2,1)S(1)} collective-permute-done((bf16[48,1024]{1,0:T(8,128)(2,1)S(1)}, bf16[48,1024]{1,0:T(8,128)(2,1)S(1)}, u32[]{:S(2)}, u32[]{:S(2)}) %collective-permute-start.16) | collective-permute-done | bytes 98336 | tf_op jit(solution)/shard_map/ppermute | solution.py:614
  60.2 2.2 %collective-permute-done.17.far_ref = bf16[48,1024]{1,0:T(8,128)(2,1)S(1)} collective-permute-done((bf16[48,1024]{1,0:T(8,128)(2,1)S(1)}, bf16[48,1024]{1,0:T(8,128)(2,1)S(1)}, u32[]{:S(2)}, u32[]{:S(2)}) %collective-permute-start.17) | collective-permute-done | bytes 98336 | tf_op jit(solution)/shard_map/ppermute | solution.py:613
  62.4 0.2 merge.1
  62.6 1.4 %collective-permute-start.19 = (bf16[32,1024]{1,0:T(8,128)(2,1)S(1)}, bf16[32,1024]{1,0:T(8,128)(2,1)S(1)}, u32[]{:S(2)}, u32[]{:S(2)}) collective-permute-start(bf16[32,1024]{1,0:T(8,128)(2,1)S(1)} %get-tuple-element.56), channel_id=1, source_target_pairs={{0,4},{4,0},{8,12},{12,8},{1,5},{5,1},{9,13},{13,9},{2,6},{6,2},{1... | collective-permute-start | bytes 196616 | tf_op jit(solution)/shard_map/ppermute | solution.py:622
  64.0 1.2 %collective-permute-start.20 = (bf16[32,1024]{1,0:T(8,128)(2,1)S(1)}, bf16[32,1024]{1,0:T(8,128)(2,1)S(1)}, u32[]{:S(2)}, u32[]{:S(2)}) collective-permute-start(bf16[32,1024]{1,0:T(8,128)(2,1)S(1)} %get-tuple-element.57), channel_id=1, source_target_pairs={{0,8},{4,12},{8,0},{12,4},{1,9},{5,13},{9,1},{13,5},{2,10},{6,14},... | collective-permute-start | bytes 196616 | tf_op jit(solution)/shard_map/ppermute | solution.py:622
  65.2 1.9 %collective-permute-start.21 = (bf16[32,1024]{1,0:T(8,128)(2,1)S(1)}, bf16[32,1024]{1,0:T(8,128)(2,1)S(1)}, u32[]{:S(2)}, u32[]{:S(2)}) collective-permute-start(bf16[32,1024]{1,0:T(8,128)(2,1)S(1)} %get-tuple-element.58), channel_id=1, source_target_pairs={{0,12},{4,8},{8,4},{12,0},{1,13},{5,9},{9,5},{13,1},{2,14},{6,10},... | collective-permute-start | bytes 196616 | tf_op jit(solution)/shard_map/ppermute | solution.py:622
  67.0 3.0 %collective-permute-done.20.two_ref = bf16[32,1024]{1,0:T(8,128)(2,1)S(1)} collective-permute-done((bf16[32,1024]{1,0:T(8,128)(2,1)S(1)}, bf16[32,1024]{1,0:T(8,128)(2,1)S(1)}, u32[]{:S(2)}, u32[]{:S(2)}) %collective-permute-start.20) | collective-permute-done | bytes 65568 | tf_op jit(solution)/shard_map/ppermute | solution.py:622
  70.0 1.3 %collective-permute-done.21.three_ref = bf16[32,1024]{1,0:T(8,128)(2,1)S(1)} collective-permute-done((bf16[32,1024]{1,0:T(8,128)(2,1)S(1)}, bf16[32,1024]{1,0:T(8,128)(2,1)S(1)}, u32[]{:S(2)}, u32[]{:S(2)}) %collective-permute-start.21) | collective-permute-done | bytes 65568 | tf_op jit(solution)/shard_map/ppermute | solution.py:622
  71.3 1.0 %scatter.1 = bf16[128,1024]{1,0:T(8,128)(2,1)} custom-call(bf16[32,128]{1,0:T(8,128)(2,1)S(1)} %get-tuple-element.32.pick_ref, bf16[32,1024]{1,0:T(8,128)(2,1)S(1)} %get-tuple-element.55.zero_ref, bf16[32,1024]{1,0:T(8,128)(2,1)S(1)} %collective-permute-done.19.one_ref, bf16[32,1024]{1,0:T(8,128)(2,1)S(1)} %collective-permute-done.20.two_ref, ...), custom_call_target="tpu_custom_call" | custom-call | tf_op jit(solution)/shard_map/scatter/pallas_call | solution.py:623
  (16 shorter events, 0.1 us)
Async XLA Ops:
  1.1 0.7 collective-permute-start
  1.8 14.7 %collective-permute-start.3 = (bf16[32,1024]{1,0:T(8,128)(2,1)S(1)}, bf16[32,1024]{1,0:T(8,128)(2,1)S(1)}, u32[]{:S(2)}, u32[]{:S(2)}) collective-permute-start(bf16[32,1024]{1,0:T(8,128)(2,1)S(1)} %collective-permute-done._.refs_0_), channel_id=1, source_target_pairs={{0,3},{1,2},{2,1},{3,0},{4,7},{5,6},{6,5},{7,4},{8,11},{9,10},{10,... | collective-permute-start | bytes 196616 | tf_op jit(solution)/shard_map/ppermute | solution.py:518
  12.1 4.7 %collective-permute-start.2 = (bf16[32,1024]{1,0:T(8,128)(2,1)S(1)}, bf16[32,1024]{1,0:T(8,128)(2,1)S(1)}, u32[]{:S(2)}, u32[]{:S(2)}) collective-permute-start(bf16[32,1024]{1,0:T(8,128)(2,1)S(1)} %collective-permute-done._.refs_0_), channel_id=1, source_target_pairs={{0,2},{1,3},{2,0},{3,1},{4,6},{5,7},{6,4},{7,5},{8,10},{9,11},{10,... | collective-permute-start | bytes 196616 | tf_op jit(solution)/shard_map/ppermute | solution.py:518
  13.7 3.1 %collective-permute-start.1 = (bf16[32,1024]{1,0:T(8,128)(2,1)S(1)}, bf16[32,1024]{1,0:T(8,128)(2,1)S(1)}, u32[]{:S(2)}, u32[]{:S(2)}) collective-permute-start(bf16[32,1024]{1,0:T(8,128)(2,1)S(1)} %collective-permute-done._.refs_0_), channel_id=1, source_target_pairs={{0,1},{1,0},{2,3},{3,2},{4,5},{5,4},{6,7},{7,6},{8,9},{9,8},{10,11... | collective-permute-start | bytes 196616 | tf_op jit(solution)/shard_map/ppermute | solution.py:518
  17.3 8.7 %collective-permute-start.6 = (bf16[32,1024]{1,0:T(8,128)(2,1)S(1)}, bf16[32,1024]{1,0:T(8,128)(2,1)S(1)}, u32[]{:S(2)}, u32[]{:S(2)}) collective-permute-start(bf16[32,1024]{1,0:T(8,128)(2,1)S(1)} %get-tuple-element.59), channel_id=1, source_target_pairs={{0,4},{4,0},{8,12},{12,8},{1,5},{5,1},{9,13},{13,9},{2,6},{6,2},{1... | collective-permute-start | bytes 196616 | tf_op jit(solution)/shard_map/ppermute | solution.py:527
  17.6 8.5 %collective-permute-start.5 = (bf16[32,1024]{1,0:T(8,128)(2,1)S(1)}, bf16[32,1024]{1,0:T(8,128)(2,1)S(1)}, u32[]{:S(2)}, u32[]{:S(2)}) collective-permute-start(bf16[32,1024]{1,0:T(8,128)(2,1)S(1)} %get-tuple-element.60), channel_id=1, source_target_pairs={{0,8},{4,12},{8,0},{12,4},{1,9},{5,13},{9,1},{13,5},{2,10},{6,14},... | collective-permute-start | bytes 196616 | tf_op jit(solution)/shard_map/ppermute | solution.py:527
  20.8 6.2 %collective-permute-start.4 = (bf16[32,1024]{1,0:T(8,128)(2,1)S(1)}, bf16[32,1024]{1,0:T(8,128)(2,1)S(1)}, u32[]{:S(2)}, u32[]{:S(2)}) collective-permute-start(bf16[32,1024]{1,0:T(8,128)(2,1)S(1)} %get-tuple-element.61), channel_id=1, source_target_pairs={{0,12},{4,8},{8,4},{12,0},{1,13},{5,9},{9,5},{13,1},{2,14},{6,10},... | collective-permute-start | bytes 196616 | tf_op jit(solution)/shard_map/ppermute | solution.py:527
  21.8 5.2 %copy-start = (bf16[1024,4]{0,1:T(4,128)(2,1)S(1)}, bf16[1024,4]{0,1:T(4,128)(2,1)}, u32[]{:S(2)}) copy-start(bf16[1024,4]{0,1:T(4,128)(2,1)} %param.14) | copy-start | bytes 24580
  21.8 5.2 %copy-start.1 = (bf16[2,1024]{1,0:T(2,128)(2,1)S(1)}, bf16[2,1024]{1,0:T(2,128)(2,1)}, u32[]{:S(2)}) copy-start(bf16[2,1024]{1,0:T(2,128)(2,1)} %gain_ref.1) | copy-start | bytes 12292
  27.2 8.5 %collective-permute-start.9 = (bf16[32,1152]{1,0:T(8,128)(2,1)S(1)}, bf16[32,1152]{1,0:T(8,128)(2,1)S(1)}, u32[]{:S(2)}, u32[]{:S(2)}) collective-permute-start(bf16[32,1152]{1,0:T(8,128)(2,1)S(1)} %norm.1.after_ref.zero_ref), channel_id=1, source_target_pairs={{0,4},{4,0},{8,12},{12,8},{1,5},{5,1},{9,13},{13,9},{2,6},{6,2},{1... | collective-permute-start | bytes 221192 | tf_op jit(solution)/shard_map/ppermute | solution.py:542
  28.1 7.6 %collective-permute-start.8 = (bf16[32,1152]{1,0:T(8,128)(2,1)S(1)}, bf16[32,1152]{1,0:T(8,128)(2,1)S(1)}, u32[]{:S(2)}, u32[]{:S(2)}) collective-permute-start(bf16[32,1152]{1,0:T(8,128)(2,1)S(1)} %norm.1.after_ref.zero_ref), channel_id=1, source_target_pairs={{0,8},{4,12},{8,0},{12,4},{1,9},{5,13},{9,1},{13,5},{2,10},{6,14},... | collective-permute-start | bytes 221192 | tf_op jit(solution)/shard_map/ppermute | solution.py:542
  29.8 6.3 %collective-permute-start.7 = (bf16[32,1152]{1,0:T(8,128)(2,1)S(1)}, bf16[32,1152]{1,0:T(8,128)(2,1)S(1)}, u32[]{:S(2)}, u32[]{:S(2)}) collective-permute-start(bf16[32,1152]{1,0:T(8,128)(2,1)S(1)} %norm.1.after_ref.zero_ref), channel_id=1, source_target_pairs={{0,12},{4,8},{8,4},{12,0},{1,13},{5,9},{9,5},{13,1},{2,14},{6,10},... | collective-permute-start | bytes 221192 | tf_op jit(solution)/shard_map/ppermute | solution.py:542
  36.2 7.0 %collective-permute-start.10 = (bf16[48,1152]{1,0:T(8,128)(2,1)S(1)}, bf16[48,1152]{1,0:T(8,128)(2,1)S(1)}, u32[]{:S(2)}, u32[]{:S(2)}) collective-permute-start(bf16[48,1152]{1,0:T(8,128)(2,1)S(1)} %get-tuple-element.40), channel_id=1, source_target_pairs={{0,18},{2,16},{16,2},{18,0},{1,19},{3,17},{17,3},{19,1},{4,22},{6,... | collective-permute-start | bytes 331784 | tf_op jit(solution)/shard_map/ppermute | solution.py:558
  38.1 5.1 %collective-permute-start.11 = (bf16[48,1152]{1,0:T(8,128)(2,1)S(1)}, bf16[48,1152]{1,0:T(8,128)(2,1)S(1)}, u32[]{:S(2)}, u32[]{:S(2)}) collective-permute-start(bf16[48,1152]{1,0:T(8,128)(2,1)S(1)} %get-tuple-element.41), channel_id=1, source_target_pairs={{0,2},{2,0},{1,3},{3,1},{4,6},{6,4},{5,7},{7,5},{8,10},{10,8},{9,1... | collective-permute-start | bytes 331784 | tf_op jit(solution)/shard_map/ppermute | solution.py:560
  39.3 4.7 %collective-permute-start.12 = (bf16[48,1152]{1,0:T(8,128)(2,1)S(1)}, bf16[48,1152]{1,0:T(8,128)(2,1)S(1)}, u32[]{:S(2)}, u32[]{:S(2)}) collective-permute-start(bf16[48,1152]{1,0:T(8,128)(2,1)S(1)} %get-tuple-element.42), channel_id=1, source_target_pairs={{0,16},{16,0},{1,17},{17,1},{2,18},{18,2},{3,19},{19,3},{4,20},{20... | collective-permute-start | bytes 331784 | tf_op jit(solution)/shard_map/ppermute | solution.py:559
  47.2 4.5 %collective-permute-start.13 = (bf16[2768,128]{1,0:T(8,128)(2,1)S(1)}, bf16[2768,128]{1,0:T(8,128)(2,1)S(1)}, u32[]{:S(2)}, u32[]{:S(2)}) collective-permute-start(bf16[2768,128]{1,0:T(8,128)(2,1)S(1)} %get-tuple-element.45.gate_ref), channel_id=1, source_target_pairs={{0,1},{1,0},{2,3},{3,2},{4,5},{5,4},{6,7},{7,6},{8,9},{9,8},{10,11... | collective-permute-start | bytes 2125832 | tf_op jit(solution)/shard_map/ppermute | solution.py:589
  49.6 2.1 %collective-permute-start.14 = (bf16[2064,128]{1,0:T(8,128)(2,1)S(1)}, bf16[2064,128]{1,0:T(8,128)(2,1)S(1)}, u32[]{:S(2)}, u32[]{:S(2)}) collective-permute-start(bf16[2064,128]{1,0:T(8,128)(2,1)S(1)} %up.2.up_ref), channel_id=1, source_target_pairs={{0,1},{1,0},{2,3},{3,2},{4,5},{5,4},{6,7},{7,6},{8,9},{9,8},{10,11... | collective-permute-start | bytes 1585160 | tf_op jit(solution)/shard_map/ppermute | solution.py:590
  51.1 1.5 %collective-permute-start.15 = (bf16[688,128]{1,0:T(8,128)(2,1)S(1)}, bf16[688,128]{1,0:T(8,128)(2,1)S(1)}, u32[]{:S(2)}, u32[]{:S(2)}) collective-permute-start(bf16[688,128]{1,0:T(8,128)(2,1)S(1)} %up.3.up_ref), channel_id=1, source_target_pairs={{0,1},{1,0},{2,3},{3,2},{4,5},{5,4},{6,7},{7,6},{8,9},{9,8},{10,11... | collective-permute-start | bytes 528392 | tf_op jit(solution)/shard_map/ppermute | solution.py:590
  54.8 5.4 %collective-permute-start.16 = (bf16[48,1024]{1,0:T(8,128)(2,1)S(1)}, bf16[48,1024]{1,0:T(8,128)(2,1)S(1)}, u32[]{:S(2)}, u32[]{:S(2)}) collective-permute-start(bf16[48,1024]{1,0:T(8,128)(2,1)S(1)} %get-tuple-element.52), channel_id=1, source_target_pairs={{0,2},{2,0},{1,3},{3,1},{4,6},{6,4},{5,7},{7,5},{8,10},{10,8},{9,1... | collective-permute-start | bytes 294920 | tf_op jit(solution)/shard_map/ppermute | solution.py:614
  55.6 6.8 %collective-permute-start.17 = (bf16[48,1024]{1,0:T(8,128)(2,1)S(1)}, bf16[48,1024]{1,0:T(8,128)(2,1)S(1)}, u32[]{:S(2)}, u32[]{:S(2)}) collective-permute-start(bf16[48,1024]{1,0:T(8,128)(2,1)S(1)} %get-tuple-element.53), channel_id=1, source_target_pairs={{0,16},{16,0},{1,17},{17,1},{2,18},{18,2},{3,19},{19,3},{4,20},{20... | collective-permute-start | bytes 294920 | tf_op jit(solution)/shard_map/ppermute | solution.py:613
  56.4 6.0 %collective-permute-start.18 = (bf16[48,1024]{1,0:T(8,128)(2,1)S(1)}, bf16[48,1024]{1,0:T(8,128)(2,1)S(1)}, u32[]{:S(2)}, u32[]{:S(2)}) collective-permute-start(bf16[48,1024]{1,0:T(8,128)(2,1)S(1)} %get-tuple-element.54), channel_id=1, source_target_pairs={{0,18},{2,16},{16,2},{18,0},{1,19},{3,17},{17,3},{19,1},{4,22},{6,... | collective-permute-start | bytes 294920 | tf_op jit(solution)/shard_map/ppermute | solution.py:612
  62.6 4.5 %collective-permute-start.19 = (bf16[32,1024]{1,0:T(8,128)(2,1)S(1)}, bf16[32,1024]{1,0:T(8,128)(2,1)S(1)}, u32[]{:S(2)}, u32[]{:S(2)}) collective-permute-start(bf16[32,1024]{1,0:T(8,128)(2,1)S(1)} %get-tuple-element.56), channel_id=1, source_target_pairs={{0,4},{4,0},{8,12},{12,8},{1,5},{5,1},{9,13},{13,9},{2,6},{6,2},{1... | collective-permute-start | bytes 196616 | tf_op jit(solution)/shard_map/ppermute | solution.py:622
  64.0 6.0 %collective-permute-start.20 = (bf16[32,1024]{1,0:T(8,128)(2,1)S(1)}, bf16[32,1024]{1,0:T(8,128)(2,1)S(1)}, u32[]{:S(2)}, u32[]{:S(2)}) collective-permute-start(bf16[32,1024]{1,0:T(8,128)(2,1)S(1)} %get-tuple-element.57), channel_id=1, source_target_pairs={{0,8},{4,12},{8,0},{12,4},{1,9},{5,13},{9,1},{13,5},{2,10},{6,14},... | collective-permute-start | bytes 196616 | tf_op jit(solution)/shard_map/ppermute | solution.py:622
  65.2 6.2 %collective-permute-start.21 = (bf16[32,1024]{1,0:T(8,128)(2,1)S(1)}, bf16[32,1024]{1,0:T(8,128)(2,1)S(1)}, u32[]{:S(2)}, u32[]{:S(2)}) collective-permute-start(bf16[32,1024]{1,0:T(8,128)(2,1)S(1)} %get-tuple-element.58), channel_id=1, source_target_pairs={{0,12},{4,8},{8,4},{12,0},{1,13},{5,9},{9,5},{13,1},{2,14},{6,10},... | collective-permute-start | bytes 196616 | tf_op jit(solution)/shard_map/ppermute | solution.py:622

commit v17 on v13

--- a/solution.py
+++ b/solution.py
@@ -450,16 +450,20 @@
                 out_ref[capacity:, :] = second_ref[span, :]
 
 
-def scatter_kernel(pick_ref, zero_ref, one_ref, two_ref, three_ref, out_hbm, out_ref, semaphores):
+def add_kernel(zero_ref, one_ref, two_ref, out_ref):
+    out_ref[...] = (
+        zero_ref[...].astype(jnp.float32) + one_ref[...].astype(jnp.float32) + two_ref[...].astype(jnp.float32)
+    )
+
+
+def scatter_kernel(pick_ref, sum_ref, three_ref, out_hbm, out_ref, semaphores):
     columns = out_ref.shape[1]
     pieces = semaphores.shape[0]
     width = columns // pieces
     copies = []
     for n in range(pieces):
         span = slice(n * width, (n + 1) * width)
-        total = zero_ref[:, span].astype(jnp.float32)
-        for got_ref in (three_ref, two_ref, one_ref):
-            total = total + got_ref[:, span].astype(jnp.float32)
+        total = sum_ref[:, span] + three_ref[:, span].astype(jnp.float32)
         result = 0.0
         for piece in split_high_low(total)[::-1]:
             result = result + lax.dot_general(
@@ -509,7 +513,7 @@
     to_second = [(t * 4 + q, q * 4 + (t ^ 2)) for t in range(4) for q in range(4)]
     across = lax.ppermute(picked, plane, to_second)
     near = lax.ppermute(picked, plane, to_first)
-    gate_units, up_units, down_units = [round(units * part / TILE) * TILE for part in (0.54, 0.44, 0.27)]
+    gate_units, up_units, down_units = [round(units * part / TILE) * TILE for part in (0.4, 0.37, 0.27)]
     gate_first, proj_held, rest = call(
         keep_gate_kernel,
         "keep_gate",
@@ -630,15 +634,16 @@
         [packed, *others[::-1], kept, from_side, from_far, from_side_far],
     )
     values = [merged[0]] + [lax.ppermute(merged[v], "tok", crossed(2, v)) for v in (1, 2, 3)]
+    begun = call(add_kernel, "add", array(slots, columns, dtype=jnp.float32), [ON_CHIP] * 3, values[:3])
     return pl.pallas_call(
         scatter_kernel,
         out_shape=pltpu.HBM((tokens, columns), jnp.bfloat16),
-        in_specs=[ON_CHIP] * 5,
+        in_specs=[ON_CHIP] * 3,
         out_specs=IN_HBM,
         scratch_shapes=[pltpu.VMEM((tokens, columns), jnp.bfloat16), pltpu.SemaphoreType.DMA((4,))],
         compiler_params=pltpu.CompilerParams(vmem_limit_bytes=8 << 20),
         name="scatter",
-    )(pick, *values)
+    )(pick, begun, values[3])
 
 
 def solution(mesh):

time: 71.5 us -> 71.5 us (level)
    pallas_call x15 -> x16, Pallas kernels: 25.8 us -> 25.6 us  [call(): pl.pallas_call(kernel, out_shape=outs, in_specs=specs, out_specs=jax.tree...]
where the time goes in v17:
time: 71.5 us; the launch traced here: 71.3 us
  starting transfers between devices  28.8 us (40%)
  Pallas kernels  26.6 us (37%)
  waiting for transfers between devices  15.6 us (22%)
    pallas_call x16, Pallas kernels, call(): pl.pallas_call(kernel, out_shape=outs, in_specs=specs, out_specs=jax.tree...  25.6 us
    ppermute x3, starting transfers between devices, paired_local(): lax.ppermute(partial[v], 'tok', crossed(2, v))  5.85 us
    ppermute x3, starting transfers between devices, paired_local(): lax.ppermute(merged[v], 'tok', crossed(2, v))  4.45 us
    ppermute x3, starting transfers between devices, paired_local(): lax.ppermute(packed, 'tok', crossed(2, v))  4.42 us
    ppermute x1, starting transfers between devices, paired_local(): side_far = lax.ppermute(to_corner_rows, both_axes, crossed(2, 3))  4.03 us
    ppermute x3, waiting for transfers between devices, paired_local(): lax.ppermute(merged[v], 'tok', crossed(2, v))  3.89 us
    ppermute x1, waiting for transfers between devices, paired_local(): from_far = lax.ppermute(to_far, 'groups', SWAP)  3.57 us
    ppermute x1, starting transfers between devices, paired_local(): across = lax.ppermute(picked, plane, to_second)  2.99 us
  transfers between devices with their start and end apart: 21, of which 12 were waited for; matrix products, arithmetic and copies ran while one was open for 0% of the time, Pallas kernels for 26%

profile of v17, /device:TPU:0, one launch (start us, length us, event | category | flops | bytes accessed | tf_op | source)
XLA Modules:
  0.0 71.3 jit_solution(15314387586724467239)
XLA Ops:
  0.0 1.1 %select.1 = (bf16[32,1024]{1,0:T(8,128)(2,1)S(1)}, bf16[32,128]{1,0:T(8,128)(2,1)S(1)}, f32[8,128]{1,0:T(8,128)S(1)}) custom-call(s32[4,16]{1,0:T(4,128)} %rows_hbm.1, bf16[128,1024]{1,0:T(8,128)(2,1)} %context_hbm.1), custom_call_target="tpu_custom_call" | custom-call | tf_op jit(solution)/shard_map/select/pallas_call | solution.py:173
  1.1 3.0 %collective-permute-start.1 = (bf16[32,1024]{1,0:T(8,128)(2,1)S(1)}, bf16[32,1024]{1,0:T(8,128)(2,1)S(1)}, u32[]{:S(2)}, u32[]{:S(2)}) collective-permute-start(bf16[32,1024]{1,0:T(8,128)(2,1)S(1)} %get-tuple-element.35), channel_id=1, source_target_pairs={{0,2},{1,6},{2,10},{3,14},{4,3},{5,7},{6,11},{7,15},{8,0},{9,4},{1... | collective-permute-start | bytes 196616 | tf_op jit(solution)/shard_map/ppermute | solution.py:514
  4.1 0.7 collective-permute-start
  4.8 3.0 %keep_gate.1 = (bf16[1104,2048]{1,0:T(8,128)(2,1)S(1)}, bf16[1024,1024]{1,0:T(8,128)(2,1)S(1)}, f32[32,1024]{1,0:T(8,128)S(1)}) custom-call(bf16[32,128]{1,0:T(8,128)(2,1)S(1)} %get-tuple-element.32.pick_ref, bf16[128,1024]{1,0:T(8,128)(2,1)} %residual_hbm.1, bf16[2,2752,2048]{2,1,0:T(8,128)(2,1)} %bitcast.10, bf16[1024,1024]{1,0:T(8,128)(2,1)} %proj_ref.1), custom_call_target="tpu_custom_call" | custom-call | bytes 5636096 | tf_op jit(solution)/shard_map/keep_gate/pallas_call | solution.py:173
  7.8 1.6 %collective-permute-done.1.across_ref = bf16[32,1024]{1,0:T(8,128)(2,1)S(1)} collective-permute-done((bf16[32,1024]{1,0:T(8,128)(2,1)S(1)}, bf16[32,1024]{1,0:T(8,128)(2,1)S(1)}, u32[]{:S(2)}, u32[]{:S(2)}) %collective-permute-start.1) | collective-permute-done | bytes 65568 | tf_op jit(solution)/shard_map/ppermute | solution.py:514
  9.5 1.4 %collective-permute-start.2 = (bf16[64,1024]{1,0:T(8,128)(2,1)S(1)}, bf16[64,1024]{1,0:T(8,128)(2,1)S(1)}, u32[]{:S(2)}, u32[]{:S(2)}) collective-permute-start(bf16[64,1024]{1,0:T(8,128)(2,1)S(1)} %join.1.joined_ref), channel_id=1, source_target_pairs={{0,1},{1,0},{2,3},{3,2},{4,5},{5,4},{6,7},{7,6},{8,9},{9,8},{10,11... | collective-permute-start | bytes 393224 | tf_op jit(solution)/shard_map/ppermute | solution.py:532
  10.9 1.0 %collective-permute-done.2.other_ref = bf16[64,1024]{1,0:T(8,128)(2,1)S(1)} collective-permute-done((bf16[64,1024]{1,0:T(8,128)(2,1)S(1)}, bf16[64,1024]{1,0:T(8,128)(2,1)S(1)}, u32[]{:S(2)}, u32[]{:S(2)}) %collective-permute-start.2) | collective-permute-done | bytes 131104 | tf_op jit(solution)/shard_map/ppermute | solution.py:532
  11.9 0.4 project.1.after_ref.partial_ref
  12.4 1.5 %collective-permute-start.5 = (bf16[32,1024]{1,0:T(8,128)(2,1)S(1)}, bf16[32,1024]{1,0:T(8,128)(2,1)S(1)}, u32[]{:S(2)}, u32[]{:S(2)}) collective-permute-start(bf16[32,1024]{1,0:T(8,128)(2,1)S(1)} %get-tuple-element.59), channel_id=1, source_target_pairs={{0,4},{4,0},{8,12},{12,8},{1,5},{5,1},{9,13},{13,9},{2,6},{6,2},{1... | collective-permute-start | bytes 196616 | tf_op jit(solution)/shard_map/ppermute | solution.py:541
  13.8 4.4 %collective-permute-start.4 = (bf16[32,1024]{1,0:T(8,128)(2,1)S(1)}, bf16[32,1024]{1,0:T(8,128)(2,1)S(1)}, u32[]{:S(2)}, u32[]{:S(2)}) collective-permute-start(bf16[32,1024]{1,0:T(8,128)(2,1)S(1)} %get-tuple-element.60), channel_id=1, source_target_pairs={{0,8},{4,12},{8,0},{12,4},{1,9},{5,13},{9,1},{13,5},{2,10},{6,14},... | collective-permute-start | bytes 196616 | tf_op jit(solution)/shard_map/ppermute | solution.py:541
  18.2 4.2 %keep_more.1 = (bf16[1648,2048]{1,0:T(8,128)(2,1)S(1)}, bf16[1024,2048]{1,0:T(8,128)(2,1)S(1)}) custom-call(bf16[4,32,1024]{2,1,0:T(8,128)(2,1)S(1)} %project.1.after_ref.partial_ref, bf16[2,2752,2048]{2,1,0:T(8,128)(2,1)} %bitcast.11, bf16[2,2752,2048]{2,1,0:T(8,128)(2,1)} %bitcast.12), custom_call_target="tpu_custom_call" | custom-call | bytes 10944512 | tf_op jit(solution)/shard_map/keep_more/pallas_call | solution.py:173
  22.4 0.0 collective-permute-done.4.two_ref
  22.4 2.0 %collective-permute-done.3.three_ref = bf16[32,1024]{1,0:T(8,128)(2,1)S(1)} collective-permute-done((bf16[32,1024]{1,0:T(8,128)(2,1)S(1)}, bf16[32,1024]{1,0:T(8,128)(2,1)S(1)}, u32[]{:S(2)}, u32[]{:S(2)}) %collective-permute-start.3) | collective-permute-done | bytes 65568 | tf_op jit(solution)/shard_map/ppermute | solution.py:541
  24.4 0.2 norm.1.after_ref.zero_ref
  24.6 0.8 %collective-permute-start.8 = (bf16[32,1152]{1,0:T(8,128)(2,1)S(1)}, bf16[32,1152]{1,0:T(8,128)(2,1)S(1)}, u32[]{:S(2)}, u32[]{:S(2)}) collective-permute-start(bf16[32,1152]{1,0:T(8,128)(2,1)S(1)} %norm.1.after_ref.zero_ref), channel_id=1, source_target_pairs={{0,4},{4,0},{8,12},{12,8},{1,5},{5,1},{9,13},{13,9},{2,6},{6,2},{1... | collective-permute-start | bytes 221192 | tf_op jit(solution)/shard_map/ppermute | solution.py:556
  25.4 1.7 %collective-permute-start.7 = (bf16[32,1152]{1,0:T(8,128)(2,1)S(1)}, bf16[32,1152]{1,0:T(8,128)(2,1)S(1)}, u32[]{:S(2)}, u32[]{:S(2)}) collective-permute-start(bf16[32,1152]{1,0:T(8,128)(2,1)S(1)} %norm.1.after_ref.zero_ref), channel_id=1, source_target_pairs={{0,8},{4,12},{8,0},{12,4},{1,9},{5,13},{9,1},{13,5},{2,10},{6,14},... | collective-permute-start | bytes 221192 | tf_op jit(solution)/shard_map/ppermute | solution.py:556
  27.2 1.9 %collective-permute-start.6 = (bf16[32,1152]{1,0:T(8,128)(2,1)S(1)}, bf16[32,1152]{1,0:T(8,128)(2,1)S(1)}, u32[]{:S(2)}, u32[]{:S(2)}) collective-permute-start(bf16[32,1152]{1,0:T(8,128)(2,1)S(1)} %norm.1.after_ref.zero_ref), channel_id=1, source_target_pairs={{0,12},{4,8},{8,4},{12,0},{1,13},{5,9},{9,5},{13,1},{2,14},{6,10},... | collective-permute-start | bytes 221192 | tf_op jit(solution)/shard_map/ppermute | solution.py:556
  29.1 3.9 %keep_up.1 = (bf16[1728,2048]{1,0:T(8,128)(2,1)S(1)}, bf16[736,2048]{1,0:T(8,128)(2,1)S(1)}) custom-call(bf16[32,1152]{1,0:T(8,128)(2,1)S(1)} %norm.1.after_ref.zero_ref, bf16[2,2752,2048]{2,1,0:T(8,128)(2,1)} %bitcast.13, bf16[2,2752,2048]{2,1,0:T(8,128)(2,1)} %refs_0_.1), custom_call_target="tpu_custom_call" | custom-call | bytes 10092544 | tf_op jit(solution)/shard_map/keep_up/pallas_call | solution.py:173
  33.0 0.0 collective-permute-done.8.one_ref
  33.0 0.4 collective-permute-done.6.three_ref
  33.4 0.2 arrange.1
  33.6 4.0 %collective-permute-start.9 = (bf16[48,1152]{1,0:T(8,128)(2,1)S(1)}, bf16[48,1152]{1,0:T(8,128)(2,1)S(1)}, u32[]{:S(2)}, u32[]{:S(2)}) collective-permute-start(bf16[48,1152]{1,0:T(8,128)(2,1)S(1)} %get-tuple-element.40), channel_id=1, source_target_pairs={{0,18},{2,16},{16,2},{18,0},{1,19},{3,17},{17,3},{19,1},{4,22},{6,... | collective-permute-start | bytes 331784 | tf_op jit(solution)/shard_map/ppermute | solution.py:572
  37.6 0.6 collective-permute-start.11
  38.3 3.4 %keep_down.1.refs_2_.second_ref = bf16[2016,2048]{1,0:T(8,128)(2,1)S(1)} custom-call(bf16[48,1152]{1,0:T(8,128)(2,1)S(1)} %get-tuple-element.43.after_ref.own_ref, bf16[2,2752,2048]{2,1,0:T(8,128)(2,1)} %refs_0_.1), custom_call_target="tpu_custom_call" | custom-call | bytes 8257536 | tf_op jit(solution)/shard_map/keep_down/pallas_call | solution.py:173
  41.6 0.7 %collective-permute-done.10.side_own_ref = bf16[48,1152]{1,0:T(8,128)(2,1)S(1)} collective-permute-done((bf16[48,1152]{1,0:T(8,128)(2,1)S(1)}, bf16[48,1152]{1,0:T(8,128)(2,1)S(1)}, u32[]{:S(2)}, u32[]{:S(2)}) %collective-permute-start.10) | collective-permute-done | bytes 110624 | tf_op jit(solution)/shard_map/ppermute | solution.py:574
  42.4 3.1 %gate.1 = (bf16[2768,128]{1,0:T(8,128)(2,1)S(1)}, bf16[128,2048]{1,0:T(8,128)(2,1)S(1)}) custom-call(bf16[48,1152]{1,0:T(8,128)(2,1)S(1)} %collective-permute-done.9.side_far_ref, bf16[48,1152]{1,0:T(8,128)(2,1)S(1)} %collective-permute-done.10.side_own_ref, bf16[48,1152]{1,0:T(8,128)(2,1)S(1)} %collective-permute-done.11.far_ref, ...), custom_call_target="tpu_custom_call" | custom-call | flops 1442840576 | tf_op jit(solution)/shard_map/gate/pallas_call | solution.py:173
  45.5 0.1 collective-permute-start.12
  45.6 2.3 %up.2.up_ref = bf16[2064,128]{1,0:T(8,128)(2,1)S(1)} custom-call(bf16[128,2048]{1,0:T(8,128)(2,1)S(1)} %get-tuple-element.46.rows_ref, bf16[1024,2048]{1,0:T(8,128)(2,1)S(1)} %get-tuple-element.38._.refs_0_, bf16[1728,2048]{1,0:T(8,128)(2,1)S(1)} %get-tuple-element.39._.refs_1_.refs_0_), custom_call_target="tpu_custom_call" | custom-call | flops 1082130432 | tf_op jit(solution)/shard_map/up/pallas_call | solution.py:173
  47.9 0.6 collective-permute-start.13
  48.5 0.9 %up.3.up_ref = bf16[688,128]{1,0:T(8,128)(2,1)S(1)} custom-call(bf16[128,2048]{1,0:T(8,128)(2,1)S(1)} %get-tuple-element.46.rows_ref, bf16[1728,2048]{1,0:T(8,128)(2,1)S(1)} %get-tuple-element.39._.refs_1_.refs_0_), custom_call_target="tpu_custom_call" | custom-call | flops 360710144 | tf_op jit(solution)/shard_map/up/pallas_call | solution.py:173
  49.4 0.1 collective-permute-start.14
  49.4 0.6 collective-permute-done.13.up_other_ref
  50.0 0.7 activation.1
  50.7 0.2 collective-permute-done.14.other_ref
  50.8 2.0 %down.1 = (bf16[48,1024]{1,0:T(8,128)(2,1)S(1)}, bf16[48,1024]{1,0:T(8,128)(2,1)S(1)}, bf16[48,1024]{1,0:T(8,128)(2,1)S(1)}, bf16[48,1024]{1,0:T(8,128)(2,1)S(1)}) custom-call(bf16[2064,128]{1,0:T(8,128)(2,1)S(1)} %get-tuple-element.47.act_early_ref, f32[688,128]{1,0:T(8,128)S(1)} %get-tuple-element.48.silu_ref, f32[8,128]{1,0:T(8,128)S(1)} %get-tuple-element.49.stat_ref, ...), custom_call_target="tpu_custom_call" | custom-call | flops 1442840576 | tf_op jit(solution)/shard_map/down/pallas_call | solution.py:173
  52.9 2.1 %collective-permute-start.15 = (bf16[48,1024]{1,0:T(8,128)(2,1)S(1)}, bf16[48,1024]{1,0:T(8,128)(2,1)S(1)}, u32[]{:S(2)}, u32[]{:S(2)}) collective-permute-start(bf16[48,1024]{1,0:T(8,128)(2,1)S(1)} %get-tuple-element.52), channel_id=1, source_target_pairs={{0,2},{2,0},{1,3},{3,1},{4,6},{6,4},{5,7},{7,5},{8,10},{10,8},{9,1... | collective-permute-start | bytes 294920 | tf_op jit(solution)/shard_map/ppermute | solution.py:628
  55.0 0.7 collective-permute-start.16
  55.7 0.9 %collective-permute-start.17 = (bf16[48,1024]{1,0:T(8,128)(2,1)S(1)}, bf16[48,1024]{1,0:T(8,128)(2,1)S(1)}, u32[]{:S(2)}, u32[]{:S(2)}) collective-permute-start(bf16[48,1024]{1,0:T(8,128)(2,1)S(1)} %get-tuple-element.54), channel_id=1, source_target_pairs={{0,18},{2,16},{16,2},{18,0},{1,19},{3,17},{17,3},{19,1},{4,22},{6,... | collective-permute-start | bytes 294920 | tf_op jit(solution)/shard_map/ppermute | solution.py:626
  56.5 1.6 %collective-permute-done.15.side_ref = bf16[48,1024]{1,0:T(8,128)(2,1)S(1)} collective-permute-done((bf16[48,1024]{1,0:T(8,128)(2,1)S(1)}, bf16[48,1024]{1,0:T(8,128)(2,1)S(1)}, u32[]{:S(2)}, u32[]{:S(2)}) %collective-permute-start.15) | collective-permute-done | bytes 98336 | tf_op jit(solution)/shard_map/ppermute | solution.py:628
  58.2 3.6 %collective-permute-done.16.far_ref = bf16[48,1024]{1,0:T(8,128)(2,1)S(1)} collective-permute-done((bf16[48,1024]{1,0:T(8,128)(2,1)S(1)}, bf16[48,1024]{1,0:T(8,128)(2,1)S(1)}, u32[]{:S(2)}, u32[]{:S(2)}) %collective-permute-start.16) | collective-permute-done | bytes 98336 | tf_op jit(solution)/shard_map/ppermute | solution.py:627
  61.7 0.2 merge.1
  61.9 1.4 %collective-permute-start.18 = (bf16[32,1024]{1,0:T(8,128)(2,1)S(1)}, bf16[32,1024]{1,0:T(8,128)(2,1)S(1)}, u32[]{:S(2)}, u32[]{:S(2)}) collective-permute-start(bf16[32,1024]{1,0:T(8,128)(2,1)S(1)} %get-tuple-element.56), channel_id=1, source_target_pairs={{0,4},{4,0},{8,12},{12,8},{1,5},{5,1},{9,13},{13,9},{2,6},{6,2},{1... | collective-permute-start | bytes 196616 | tf_op jit(solution)/shard_map/ppermute | solution.py:636
  63.3 0.8 %collective-permute-start.19 = (bf16[32,1024]{1,0:T(8,128)(2,1)S(1)}, bf16[32,1024]{1,0:T(8,128)(2,1)S(1)}, u32[]{:S(2)}, u32[]{:S(2)}) collective-permute-start(bf16[32,1024]{1,0:T(8,128)(2,1)S(1)} %get-tuple-element.57), channel_id=1, source_target_pairs={{0,8},{4,12},{8,0},{12,4},{1,9},{5,13},{9,1},{13,5},{2,10},{6,14},... | collective-permute-start | bytes 196616 | tf_op jit(solution)/shard_map/ppermute | solution.py:636
  64.1 2.3 %collective-permute-start.20 = (bf16[32,1024]{1,0:T(8,128)(2,1)S(1)}, bf16[32,1024]{1,0:T(8,128)(2,1)S(1)}, u32[]{:S(2)}, u32[]{:S(2)}) collective-permute-start(bf16[32,1024]{1,0:T(8,128)(2,1)S(1)} %get-tuple-element.58), channel_id=1, source_target_pairs={{0,12},{4,8},{8,4},{12,0},{1,13},{5,9},{9,5},{13,1},{2,14},{6,10},... | collective-permute-start | bytes 196616 | tf_op jit(solution)/shard_map/ppermute | solution.py:636
  66.4 1.2 %collective-permute-done.18.one_ref = bf16[32,1024]{1,0:T(8,128)(2,1)S(1)} collective-permute-done((bf16[32,1024]{1,0:T(8,128)(2,1)S(1)}, bf16[32,1024]{1,0:T(8,128)(2,1)S(1)}, u32[]{:S(2)}, u32[]{:S(2)}) %collective-permute-start.18) | collective-permute-done | bytes 65568 | tf_op jit(solution)/shard_map/ppermute | solution.py:636
  67.5 1.7 %collective-permute-done.19.two_ref = bf16[32,1024]{1,0:T(8,128)(2,1)S(1)} collective-permute-done((bf16[32,1024]{1,0:T(8,128)(2,1)S(1)}, bf16[32,1024]{1,0:T(8,128)(2,1)S(1)}, u32[]{:S(2)}, u32[]{:S(2)}) %collective-permute-start.19) | collective-permute-done | bytes 65568 | tf_op jit(solution)/shard_map/ppermute | solution.py:636
  69.2 1.1 %collective-permute-done.20.three_ref = bf16[32,1024]{1,0:T(8,128)(2,1)S(1)} collective-permute-done((bf16[32,1024]{1,0:T(8,128)(2,1)S(1)}, bf16[32,1024]{1,0:T(8,128)(2,1)S(1)}, u32[]{:S(2)}, u32[]{:S(2)}) %collective-permute-start.20) | collective-permute-done | bytes 65568 | tf_op jit(solution)/shard_map/ppermute | solution.py:636
  70.3 1.0 %scatter.1 = bf16[128,1024]{1,0:T(8,128)(2,1)} custom-call(bf16[32,128]{1,0:T(8,128)(2,1)S(1)} %get-tuple-element.32.pick_ref, f32[32,1024]{1,0:T(8,128)S(1)} %add.1.sum_ref, bf16[32,1024]{1,0:T(8,128)(2,1)S(1)} %collective-permute-done.20.three_ref), custom_call_target="tpu_custom_call" | custom-call | tf_op jit(solution)/shard_map/scatter/pallas_call | solution.py:638
  (16 shorter events, 0.1 us)
Async XLA Ops:
  1.1 8.3 %collective-permute-start.1 = (bf16[32,1024]{1,0:T(8,128)(2,1)S(1)}, bf16[32,1024]{1,0:T(8,128)(2,1)S(1)}, u32[]{:S(2)}, u32[]{:S(2)}) collective-permute-start(bf16[32,1024]{1,0:T(8,128)(2,1)S(1)} %get-tuple-element.35), channel_id=1, source_target_pairs={{0,2},{1,6},{2,10},{3,14},{4,3},{5,7},{6,11},{7,15},{8,0},{9,4},{1... | collective-permute-start | bytes 196616 | tf_op jit(solution)/shard_map/ppermute | solution.py:514
  4.1 5.3 %collective-permute-start = (bf16[32,1024]{1,0:T(8,128)(2,1)S(1)}, bf16[32,1024]{1,0:T(8,128)(2,1)S(1)}, u32[]{:S(2)}, u32[]{:S(2)}) collective-permute-start(bf16[32,1024]{1,0:T(8,128)(2,1)S(1)} %get-tuple-element.35), channel_id=1, source_target_pairs={{0,0},{1,4},{2,8},{3,12},{4,1},{5,5},{6,9},{7,13},{8,2},{9,6},{10,... | collective-permute-start | bytes 196616 | tf_op jit(solution)/shard_map/ppermute | solution.py:515
  9.5 2.4 %collective-permute-start.2 = (bf16[64,1024]{1,0:T(8,128)(2,1)S(1)}, bf16[64,1024]{1,0:T(8,128)(2,1)S(1)}, u32[]{:S(2)}, u32[]{:S(2)}) collective-permute-start(bf16[64,1024]{1,0:T(8,128)(2,1)S(1)} %join.1.joined_ref), channel_id=1, source_target_pairs={{0,1},{1,0},{2,3},{3,2},{4,5},{5,4},{6,7},{7,6},{8,9},{9,8},{10,11... | collective-permute-start | bytes 393224 | tf_op jit(solution)/shard_map/ppermute | solution.py:532
  12.4 10.0 %collective-permute-start.5 = (bf16[32,1024]{1,0:T(8,128)(2,1)S(1)}, bf16[32,1024]{1,0:T(8,128)(2,1)S(1)}, u32[]{:S(2)}, u32[]{:S(2)}) collective-permute-start(bf16[32,1024]{1,0:T(8,128)(2,1)S(1)} %get-tuple-element.59), channel_id=1, source_target_pairs={{0,4},{4,0},{8,12},{12,8},{1,5},{5,1},{9,13},{13,9},{2,6},{6,2},{1... | collective-permute-start | bytes 196616 | tf_op jit(solution)/shard_map/ppermute | solution.py:541
  13.8 8.6 %collective-permute-start.4 = (bf16[32,1024]{1,0:T(8,128)(2,1)S(1)}, bf16[32,1024]{1,0:T(8,128)(2,1)S(1)}, u32[]{:S(2)}, u32[]{:S(2)}) collective-permute-start(bf16[32,1024]{1,0:T(8,128)(2,1)S(1)} %get-tuple-element.60), channel_id=1, source_target_pairs={{0,8},{4,12},{8,0},{12,4},{1,9},{5,13},{9,1},{13,5},{2,10},{6,14},... | collective-permute-start | bytes 196616 | tf_op jit(solution)/shard_map/ppermute | solution.py:541
  18.2 6.2 %collective-permute-start.3 = (bf16[32,1024]{1,0:T(8,128)(2,1)S(1)}, bf16[32,1024]{1,0:T(8,128)(2,1)S(1)}, u32[]{:S(2)}, u32[]{:S(2)}) collective-permute-start(bf16[32,1024]{1,0:T(8,128)(2,1)S(1)} %get-tuple-element.61), channel_id=1, source_target_pairs={{0,12},{4,8},{8,4},{12,0},{1,13},{5,9},{9,5},{13,1},{2,14},{6,10},... | collective-permute-start | bytes 196616 | tf_op jit(solution)/shard_map/ppermute | solution.py:541
  18.2 6.2 %copy-start = (bf16[1024,4]{0,1:T(4,128)(2,1)S(1)}, bf16[1024,4]{0,1:T(4,128)(2,1)}, u32[]{:S(2)}) copy-start(bf16[1024,4]{0,1:T(4,128)(2,1)} %param.14) | copy-start | bytes 24580
  18.2 6.2 %copy-start.1 = (bf16[2,1024]{1,0:T(2,128)(2,1)S(1)}, bf16[2,1024]{1,0:T(2,128)(2,1)}, u32[]{:S(2)}) copy-start(bf16[2,1024]{1,0:T(2,128)(2,1)} %gain_ref.1) | copy-start | bytes 12292
  24.6 8.3 %collective-permute-start.8 = (bf16[32,1152]{1,0:T(8,128)(2,1)S(1)}, bf16[32,1152]{1,0:T(8,128)(2,1)S(1)}, u32[]{:S(2)}, u32[]{:S(2)}) collective-permute-start(bf16[32,1152]{1,0:T(8,128)(2,1)S(1)} %norm.1.after_ref.zero_ref), channel_id=1, source_target_pairs={{0,4},{4,0},{8,12},{12,8},{1,5},{5,1},{9,13},{13,9},{2,6},{6,2},{1... | collective-permute-start | bytes 221192 | tf_op jit(solution)/shard_map/ppermute | solution.py:556
  25.4 7.6 %collective-permute-start.7 = (bf16[32,1152]{1,0:T(8,128)(2,1)S(1)}, bf16[32,1152]{1,0:T(8,128)(2,1)S(1)}, u32[]{:S(2)}, u32[]{:S(2)}) collective-permute-start(bf16[32,1152]{1,0:T(8,128)(2,1)S(1)} %norm.1.after_ref.zero_ref), channel_id=1, source_target_pairs={{0,8},{4,12},{8,0},{12,4},{1,9},{5,13},{9,1},{13,5},{2,10},{6,14},... | collective-permute-start | bytes 221192 | tf_op jit(solution)/shard_map/ppermute | solution.py:556
  27.2 6.3 %collective-permute-start.6 = (bf16[32,1152]{1,0:T(8,128)(2,1)S(1)}, bf16[32,1152]{1,0:T(8,128)(2,1)S(1)}, u32[]{:S(2)}, u32[]{:S(2)}) collective-permute-start(bf16[32,1152]{1,0:T(8,128)(2,1)S(1)} %norm.1.after_ref.zero_ref), channel_id=1, source_target_pairs={{0,12},{4,8},{8,4},{12,0},{1,13},{5,9},{9,5},{13,1},{2,14},{6,10},... | collective-permute-start | bytes 221192 | tf_op jit(solution)/shard_map/ppermute | solution.py:556
  33.6 8.0 %collective-permute-start.9 = (bf16[48,1152]{1,0:T(8,128)(2,1)S(1)}, bf16[48,1152]{1,0:T(8,128)(2,1)S(1)}, u32[]{:S(2)}, u32[]{:S(2)}) collective-permute-start(bf16[48,1152]{1,0:T(8,128)(2,1)S(1)} %get-tuple-element.40), channel_id=1, source_target_pairs={{0,18},{2,16},{16,2},{18,0},{1,19},{3,17},{17,3},{19,1},{4,22},{6,... | collective-permute-start | bytes 331784 | tf_op jit(solution)/shard_map/ppermute | solution.py:572
  37.6 4.7 %collective-permute-start.10 = (bf16[48,1152]{1,0:T(8,128)(2,1)S(1)}, bf16[48,1152]{1,0:T(8,128)(2,1)S(1)}, u32[]{:S(2)}, u32[]{:S(2)}) collective-permute-start(bf16[48,1152]{1,0:T(8,128)(2,1)S(1)} %get-tuple-element.41), channel_id=1, source_target_pairs={{0,2},{2,0},{1,3},{3,1},{4,6},{6,4},{5,7},{7,5},{8,10},{10,8},{9,1... | collective-permute-start | bytes 331784 | tf_op jit(solution)/shard_map/ppermute | solution.py:574
  37.6 4.7 %collective-permute-start.11 = (bf16[48,1152]{1,0:T(8,128)(2,1)S(1)}, bf16[48,1152]{1,0:T(8,128)(2,1)S(1)}, u32[]{:S(2)}, u32[]{:S(2)}) collective-permute-start(bf16[48,1152]{1,0:T(8,128)(2,1)S(1)} %get-tuple-element.42), channel_id=1, source_target_pairs={{0,16},{16,0},{1,17},{17,1},{2,18},{18,2},{3,19},{19,3},{4,20},{20... | collective-permute-start | bytes 331784 | tf_op jit(solution)/shard_map/ppermute | solution.py:573
  45.5 4.5 %collective-permute-start.12 = (bf16[2768,128]{1,0:T(8,128)(2,1)S(1)}, bf16[2768,128]{1,0:T(8,128)(2,1)S(1)}, u32[]{:S(2)}, u32[]{:S(2)}) collective-permute-start(bf16[2768,128]{1,0:T(8,128)(2,1)S(1)} %get-tuple-element.45.gate_ref), channel_id=1, source_target_pairs={{0,1},{1,0},{2,3},{3,2},{4,5},{5,4},{6,7},{7,6},{8,9},{9,8},{10,11... | collective-permute-start | bytes 2125832 | tf_op jit(solution)/shard_map/ppermute | solution.py:603
  47.9 2.1 %collective-permute-start.13 = (bf16[2064,128]{1,0:T(8,128)(2,1)S(1)}, bf16[2064,128]{1,0:T(8,128)(2,1)S(1)}, u32[]{:S(2)}, u32[]{:S(2)}) collective-permute-start(bf16[2064,128]{1,0:T(8,128)(2,1)S(1)} %up.2.up_ref), channel_id=1, source_target_pairs={{0,1},{1,0},{2,3},{3,2},{4,5},{5,4},{6,7},{7,6},{8,9},{9,8},{10,11... | collective-permute-start | bytes 1585160 | tf_op jit(solution)/shard_map/ppermute | solution.py:604
  49.4 1.5 %collective-permute-start.14 = (bf16[688,128]{1,0:T(8,128)(2,1)S(1)}, bf16[688,128]{1,0:T(8,128)(2,1)S(1)}, u32[]{:S(2)}, u32[]{:S(2)}) collective-permute-start(bf16[688,128]{1,0:T(8,128)(2,1)S(1)} %up.3.up_ref), channel_id=1, source_target_pairs={{0,1},{1,0},{2,3},{3,2},{4,5},{5,4},{6,7},{7,6},{8,9},{9,8},{10,11... | collective-permute-start | bytes 528392 | tf_op jit(solution)/shard_map/ppermute | solution.py:604
  52.9 5.3 %collective-permute-start.15 = (bf16[48,1024]{1,0:T(8,128)(2,1)S(1)}, bf16[48,1024]{1,0:T(8,128)(2,1)S(1)}, u32[]{:S(2)}, u32[]{:S(2)}) collective-permute-start(bf16[48,1024]{1,0:T(8,128)(2,1)S(1)} %get-tuple-element.52), channel_id=1, source_target_pairs={{0,2},{2,0},{1,3},{3,1},{4,6},{6,4},{5,7},{7,5},{8,10},{10,8},{9,1... | collective-permute-start | bytes 294920 | tf_op jit(solution)/shard_map/ppermute | solution.py:628
  55.0 6.8 %collective-permute-start.16 = (bf16[48,1024]{1,0:T(8,128)(2,1)S(1)}, bf16[48,1024]{1,0:T(8,128)(2,1)S(1)}, u32[]{:S(2)}, u32[]{:S(2)}) collective-permute-start(bf16[48,1024]{1,0:T(8,128)(2,1)S(1)} %get-tuple-element.53), channel_id=1, source_target_pairs={{0,16},{16,0},{1,17},{17,1},{2,18},{18,2},{3,19},{19,3},{4,20},{20... | collective-permute-start | bytes 294920 | tf_op jit(solution)/shard_map/ppermute | solution.py:627
  55.7 6.1 %collective-permute-start.17 = (bf16[48,1024]{1,0:T(8,128)(2,1)S(1)}, bf16[48,1024]{1,0:T(8,128)(2,1)S(1)}, u32[]{:S(2)}, u32[]{:S(2)}) collective-permute-start(bf16[48,1024]{1,0:T(8,128)(2,1)S(1)} %get-tuple-element.54), channel_id=1, source_target_pairs={{0,18},{2,16},{16,2},{18,0},{1,19},{3,17},{17,3},{19,1},{4,22},{6,... | collective-permute-start | bytes 294920 | tf_op jit(solution)/shard_map/ppermute | solution.py:626
  61.9 5.6 %collective-permute-start.18 = (bf16[32,1024]{1,0:T(8,128)(2,1)S(1)}, bf16[32,1024]{1,0:T(8,128)(2,1)S(1)}, u32[]{:S(2)}, u32[]{:S(2)}) collective-permute-start(bf16[32,1024]{1,0:T(8,128)(2,1)S(1)} %get-tuple-element.56), channel_id=1, source_target_pairs={{0,4},{4,0},{8,12},{12,8},{1,5},{5,1},{9,13},{13,9},{2,6},{6,2},{1... | collective-permute-start | bytes 196616 | tf_op jit(solution)/shard_map/ppermute | solution.py:636
  63.3 5.9 %collective-permute-start.19 = (bf16[32,1024]{1,0:T(8,128)(2,1)S(1)}, bf16[32,1024]{1,0:T(8,128)(2,1)S(1)}, u32[]{:S(2)}, u32[]{:S(2)}) collective-permute-start(bf16[32,1024]{1,0:T(8,128)(2,1)S(1)} %get-tuple-element.57), channel_id=1, source_target_pairs={{0,8},{4,12},{8,0},{12,4},{1,9},{5,13},{9,1},{13,5},{2,10},{6,14},... | collective-permute-start | bytes 196616 | tf_op jit(solution)/shard_map/ppermute | solution.py:636
  64.1 6.2 %collective-permute-start.20 = (bf16[32,1024]{1,0:T(8,128)(2,1)S(1)}, bf16[32,1024]{1,0:T(8,128)(2,1)S(1)}, u32[]{:S(2)}, u32[]{:S(2)}) collective-permute-start(bf16[32,1024]{1,0:T(8,128)(2,1)S(1)} %get-tuple-element.58), channel_id=1, source_target_pairs={{0,12},{4,8},{8,4},{12,0},{1,13},{5,9},{9,5},{13,1},{2,14},{6,10},... | collective-permute-start | bytes 196616 | tf_op jit(solution)/shard_map/ppermute | solution.py:636

commit v18 on v17

--- a/solution.py
+++ b/solution.py
@@ -513,7 +513,7 @@
     to_second = [(t * 4 + q, q * 4 + (t ^ 2)) for t in range(4) for q in range(4)]
     across = lax.ppermute(picked, plane, to_second)
     near = lax.ppermute(picked, plane, to_first)
-    gate_units, up_units, down_units = [round(units * part / TILE) * TILE for part in (0.4, 0.37, 0.27)]
+    gate_units, up_units, down_units = [round(units * part / TILE) * TILE for part in (0.3, 0.32, 0.29)]
     gate_first, proj_held, rest = call(
         keep_gate_kernel,
         "keep_gate",

time: 71.5 us -> 71.6 us (level)
  transfers between devices with their start and end apart: 21 -> 21, of which waited for: 12 -> 13; matrix products, arithmetic and copies ran while one was open for 0% -> 0% of each run, Pallas kernels for 26% -> 26%
where the time goes in v18:
time: 71.6 us; the launch traced here: 71.4 us
  starting transfers between devices  28.6 us (40%)
  Pallas kernels  26.8 us (37%)
  waiting for transfers between devices  15.8 us (22%)
    pallas_call x16, Pallas kernels, call(): pl.pallas_call(kernel, out_shape=outs, in_specs=specs, out_specs=jax.tree...  25.8 us
    ppermute x3, starting transfers between devices, paired_local(): lax.ppermute(partial[v], 'tok', crossed(2, v))  5.54 us
    ppermute x3, starting transfers between devices, paired_local(): lax.ppermute(merged[v], 'tok', crossed(2, v))  4.45 us
    ppermute x3, starting transfers between devices, paired_local(): lax.ppermute(packed, 'tok', crossed(2, v))  4.42 us
    ppermute x1, starting transfers between devices, paired_local(): side_far = lax.ppermute(to_corner_rows, both_axes, crossed(2, 3))  4.11 us
    ppermute x3, waiting for transfers between devices, paired_local(): lax.ppermute(merged[v], 'tok', crossed(2, v))  3.88 us
    ppermute x1, waiting for transfers between devices, paired_local(): from_far = lax.ppermute(to_far, 'groups', SWAP)  3.57 us
    ppermute x1, starting transfers between devices, paired_local(): across = lax.ppermute(picked, plane, to_second)  2.99 us
  transfers between devices with their start and end apart: 21, of which 13 were waited for; matrix products, arithmetic and copies ran while one was open for 0% of the time, Pallas kernels for 26%

profile of v18, /device:TPU:0, one launch (start us, length us, event | category | flops | bytes accessed | tf_op | source)
XLA Modules:
  0.0 71.4 jit_solution(5283505809368079741)
XLA Ops:
  0.0 1.1 %select.1 = (bf16[32,1024]{1,0:T(8,128)(2,1)S(1)}, bf16[32,128]{1,0:T(8,128)(2,1)S(1)}, f32[8,128]{1,0:T(8,128)S(1)}) custom-call(s32[4,16]{1,0:T(4,128)} %rows_hbm.1, bf16[128,1024]{1,0:T(8,128)(2,1)} %context_hbm.1), custom_call_target="tpu_custom_call" | custom-call | tf_op jit(solution)/shard_map/select/pallas_call | solution.py:173
  1.1 3.0 %collective-permute-start.1 = (bf16[32,1024]{1,0:T(8,128)(2,1)S(1)}, bf16[32,1024]{1,0:T(8,128)(2,1)S(1)}, u32[]{:S(2)}, u32[]{:S(2)}) collective-permute-start(bf16[32,1024]{1,0:T(8,128)(2,1)S(1)} %get-tuple-element.35), channel_id=1, source_target_pairs={{0,2},{1,6},{2,10},{3,14},{4,3},{5,7},{6,11},{7,15},{8,0},{9,4},{1... | collective-permute-start | bytes 196616 | tf_op jit(solution)/shard_map/ppermute | solution.py:514
  4.1 0.7 collective-permute-start
  4.8 2.7 %keep_gate.1 = (bf16[832,2048]{1,0:T(8,128)(2,1)S(1)}, bf16[1024,1024]{1,0:T(8,128)(2,1)S(1)}, f32[32,1024]{1,0:T(8,128)S(1)}) custom-call(bf16[32,128]{1,0:T(8,128)(2,1)S(1)} %get-tuple-element.32.pick_ref, bf16[128,1024]{1,0:T(8,128)(2,1)} %residual_hbm.1, bf16[2,2752,2048]{2,1,0:T(8,128)(2,1)} %bitcast.10, bf16[1024,1024]{1,0:T(8,128)(2,1)} %proj_ref.1), custom_call_target="tpu_custom_call" | custom-call | bytes 5636096 | tf_op jit(solution)/shard_map/keep_gate/pallas_call | solution.py:173
  7.5 1.9 %collective-permute-done.1.across_ref = bf16[32,1024]{1,0:T(8,128)(2,1)S(1)} collective-permute-done((bf16[32,1024]{1,0:T(8,128)(2,1)S(1)}, bf16[32,1024]{1,0:T(8,128)(2,1)S(1)}, u32[]{:S(2)}, u32[]{:S(2)}) %collective-permute-start.1) | collective-permute-done | bytes 65568 | tf_op jit(solution)/shard_map/ppermute | solution.py:514
  9.5 1.4 %collective-permute-start.2 = (bf16[64,1024]{1,0:T(8,128)(2,1)S(1)}, bf16[64,1024]{1,0:T(8,128)(2,1)S(1)}, u32[]{:S(2)}, u32[]{:S(2)}) collective-permute-start(bf16[64,1024]{1,0:T(8,128)(2,1)S(1)} %join.1.joined_ref), channel_id=1, source_target_pairs={{0,1},{1,0},{2,3},{3,2},{4,5},{5,4},{6,7},{7,6},{8,9},{9,8},{10,11... | collective-permute-start | bytes 393224 | tf_op jit(solution)/shard_map/ppermute | solution.py:532
  10.9 1.0 %collective-permute-done.2.other_ref = bf16[64,1024]{1,0:T(8,128)(2,1)S(1)} collective-permute-done((bf16[64,1024]{1,0:T(8,128)(2,1)S(1)}, bf16[64,1024]{1,0:T(8,128)(2,1)S(1)}, u32[]{:S(2)}, u32[]{:S(2)}) %collective-permute-start.2) | collective-permute-done | bytes 131104 | tf_op jit(solution)/shard_map/ppermute | solution.py:532
  11.9 0.4 project.1.after_ref.partial_ref
  12.4 1.1 %collective-permute-start.5 = (bf16[32,1024]{1,0:T(8,128)(2,1)S(1)}, bf16[32,1024]{1,0:T(8,128)(2,1)S(1)}, u32[]{:S(2)}, u32[]{:S(2)}) collective-permute-start(bf16[32,1024]{1,0:T(8,128)(2,1)S(1)} %get-tuple-element.59), channel_id=1, source_target_pairs={{0,4},{4,0},{8,12},{12,8},{1,5},{5,1},{9,13},{13,9},{2,6},{6,2},{1... | collective-permute-start | bytes 196616 | tf_op jit(solution)/shard_map/ppermute | solution.py:541
  13.5 4.4 %collective-permute-start.4 = (bf16[32,1024]{1,0:T(8,128)(2,1)S(1)}, bf16[32,1024]{1,0:T(8,128)(2,1)S(1)}, u32[]{:S(2)}, u32[]{:S(2)}) collective-permute-start(bf16[32,1024]{1,0:T(8,128)(2,1)S(1)} %get-tuple-element.60), channel_id=1, source_target_pairs={{0,8},{4,12},{8,0},{12,4},{1,9},{5,13},{9,1},{13,5},{2,10},{6,14},... | collective-permute-start | bytes 196616 | tf_op jit(solution)/shard_map/ppermute | solution.py:541
  17.9 0.0 collective-permute-start.3
  17.9 4.3 %keep_more.1 = (bf16[1920,2048]{1,0:T(8,128)(2,1)S(1)}, bf16[880,2048]{1,0:T(8,128)(2,1)S(1)}) custom-call(bf16[4,32,1024]{2,1,0:T(8,128)(2,1)S(1)} %project.1.after_ref.partial_ref, bf16[2,2752,2048]{2,1,0:T(8,128)(2,1)} %bitcast.11, bf16[2,2752,2048]{2,1,0:T(8,128)(2,1)} %bitcast.12), custom_call_target="tpu_custom_call" | custom-call | bytes 11468800 | tf_op jit(solution)/shard_map/keep_more/pallas_call | solution.py:173
  22.2 0.4 collective-permute-done.4.two_ref
  22.7 1.4 %collective-permute-done.3.three_ref = bf16[32,1024]{1,0:T(8,128)(2,1)S(1)} collective-permute-done((bf16[32,1024]{1,0:T(8,128)(2,1)S(1)}, bf16[32,1024]{1,0:T(8,128)(2,1)S(1)}, u32[]{:S(2)}, u32[]{:S(2)}) %collective-permute-start.3) | collective-permute-done | bytes 65568 | tf_op jit(solution)/shard_map/ppermute | solution.py:541
  24.1 0.2 norm.1.after_ref.zero_ref
  24.3 0.9 %collective-permute-start.8 = (bf16[32,1152]{1,0:T(8,128)(2,1)S(1)}, bf16[32,1152]{1,0:T(8,128)(2,1)S(1)}, u32[]{:S(2)}, u32[]{:S(2)}) collective-permute-start(bf16[32,1152]{1,0:T(8,128)(2,1)S(1)} %norm.1.after_ref.zero_ref), channel_id=1, source_target_pairs={{0,4},{4,0},{8,12},{12,8},{1,5},{5,1},{9,13},{13,9},{2,6},{6,2},{1... | collective-permute-start | bytes 221192 | tf_op jit(solution)/shard_map/ppermute | solution.py:556
  25.2 1.9 %collective-permute-start.7 = (bf16[32,1152]{1,0:T(8,128)(2,1)S(1)}, bf16[32,1152]{1,0:T(8,128)(2,1)S(1)}, u32[]{:S(2)}, u32[]{:S(2)}) collective-permute-start(bf16[32,1152]{1,0:T(8,128)(2,1)S(1)} %norm.1.after_ref.zero_ref), channel_id=1, source_target_pairs={{0,8},{4,12},{8,0},{12,4},{1,9},{5,13},{9,1},{13,5},{2,10},{6,14},... | collective-permute-start | bytes 221192 | tf_op jit(solution)/shard_map/ppermute | solution.py:556
  27.1 1.7 %collective-permute-start.6 = (bf16[32,1152]{1,0:T(8,128)(2,1)S(1)}, bf16[32,1152]{1,0:T(8,128)(2,1)S(1)}, u32[]{:S(2)}, u32[]{:S(2)}) collective-permute-start(bf16[32,1152]{1,0:T(8,128)(2,1)S(1)} %norm.1.after_ref.zero_ref), channel_id=1, source_target_pairs={{0,12},{4,8},{8,4},{12,0},{1,13},{5,9},{9,5},{13,1},{2,14},{6,10},... | collective-permute-start | bytes 221192 | tf_op jit(solution)/shard_map/ppermute | solution.py:556
  28.8 4.1 %keep_up.1 = (bf16[1872,2048]{1,0:T(8,128)(2,1)S(1)}, bf16[800,2048]{1,0:T(8,128)(2,1)S(1)}) custom-call(bf16[32,1152]{1,0:T(8,128)(2,1)S(1)} %norm.1.after_ref.zero_ref, bf16[2,2752,2048]{2,1,0:T(8,128)(2,1)} %bitcast.13, bf16[2,2752,2048]{2,1,0:T(8,128)(2,1)} %refs_0_.1), custom_call_target="tpu_custom_call" | custom-call | bytes 10944512 | tf_op jit(solution)/shard_map/keep_up/pallas_call | solution.py:173
  32.9 0.4 collective-permute-done.6.three_ref
  33.3 0.2 arrange.1
  33.5 4.1 %collective-permute-start.9 = (bf16[48,1152]{1,0:T(8,128)(2,1)S(1)}, bf16[48,1152]{1,0:T(8,128)(2,1)S(1)}, u32[]{:S(2)}, u32[]{:S(2)}) collective-permute-start(bf16[48,1152]{1,0:T(8,128)(2,1)S(1)} %get-tuple-element.40), channel_id=1, source_target_pairs={{0,18},{2,16},{16,2},{18,0},{1,19},{3,17},{17,3},{19,1},{4,22},{6,... | collective-permute-start | bytes 331784 | tf_op jit(solution)/shard_map/ppermute | solution.py:572
  37.6 0.6 collective-permute-start.11
  38.3 3.3 %keep_down.1.refs_2_.second_ref = bf16[1952,2048]{1,0:T(8,128)(2,1)S(1)} custom-call(bf16[48,1152]{1,0:T(8,128)(2,1)S(1)} %get-tuple-element.43.after_ref.own_ref, bf16[2,2752,2048]{2,1,0:T(8,128)(2,1)} %refs_0_.1), custom_call_target="tpu_custom_call" | custom-call | bytes 7995392 | tf_op jit(solution)/shard_map/keep_down/pallas_call | solution.py:173
  41.5 0.8 %collective-permute-done.10.side_own_ref = bf16[48,1152]{1,0:T(8,128)(2,1)S(1)} collective-permute-done((bf16[48,1152]{1,0:T(8,128)(2,1)S(1)}, bf16[48,1152]{1,0:T(8,128)(2,1)S(1)}, u32[]{:S(2)}, u32[]{:S(2)}) %collective-permute-start.10) | collective-permute-done | bytes 110624 | tf_op jit(solution)/shard_map/ppermute | solution.py:574
  42.4 3.1 %gate.1 = (bf16[2768,128]{1,0:T(8,128)(2,1)S(1)}, bf16[128,2048]{1,0:T(8,128)(2,1)S(1)}) custom-call(bf16[48,1152]{1,0:T(8,128)(2,1)S(1)} %collective-permute-done.9.side_far_ref, bf16[48,1152]{1,0:T(8,128)(2,1)S(1)} %collective-permute-done.10.side_own_ref, bf16[48,1152]{1,0:T(8,128)(2,1)S(1)} %collective-permute-done.11.far_ref, ...), custom_call_target="tpu_custom_call" | custom-call | flops 1442840576 | tf_op jit(solution)/shard_map/gate/pallas_call | solution.py:173
  45.5 0.1 collective-permute-start.12
  45.5 2.3 %up.2.up_ref = bf16[2064,128]{1,0:T(8,128)(2,1)S(1)} custom-call(bf16[128,2048]{1,0:T(8,128)(2,1)S(1)} %get-tuple-element.46.rows_ref, bf16[880,2048]{1,0:T(8,128)(2,1)S(1)} %get-tuple-element.38._.refs_0_, bf16[1872,2048]{1,0:T(8,128)(2,1)S(1)} %get-tuple-element.39._.refs_1_.refs_0_), custom_call_target="tpu_custom_call" | custom-call | flops 1082130432 | tf_op jit(solution)/shard_map/up/pallas_call | solution.py:173
  47.9 0.6 collective-permute-start.13
  48.5 0.9 %up.3.up_ref = bf16[688,128]{1,0:T(8,128)(2,1)S(1)} custom-call(bf16[128,2048]{1,0:T(8,128)(2,1)S(1)} %get-tuple-element.46.rows_ref, bf16[1872,2048]{1,0:T(8,128)(2,1)S(1)} %get-tuple-element.39._.refs_1_.refs_0_), custom_call_target="tpu_custom_call" | custom-call | flops 360710144 | tf_op jit(solution)/shard_map/up/pallas_call | solution.py:173
  49.4 0.1 collective-permute-start.14
  49.4 0.6 collective-permute-done.13.up_other_ref
  50.0 0.7 activation.1
  50.7 0.2 collective-permute-done.14.other_ref
  50.8 2.2 %down.1 = (bf16[48,1024]{1,0:T(8,128)(2,1)S(1)}, bf16[48,1024]{1,0:T(8,128)(2,1)S(1)}, bf16[48,1024]{1,0:T(8,128)(2,1)S(1)}, bf16[48,1024]{1,0:T(8,128)(2,1)S(1)}) custom-call(bf16[2064,128]{1,0:T(8,128)(2,1)S(1)} %get-tuple-element.47.act_early_ref, f32[688,128]{1,0:T(8,128)S(1)} %get-tuple-element.48.silu_ref, f32[8,128]{1,0:T(8,128)S(1)} %get-tuple-element.49.stat_ref, ...), custom_call_target="tpu_custom_call" | custom-call | flops 1442840576 | tf_op jit(solution)/shard_map/down/pallas_call | solution.py:173
  53.0 2.1 %collective-permute-start.15 = (bf16[48,1024]{1,0:T(8,128)(2,1)S(1)}, bf16[48,1024]{1,0:T(8,128)(2,1)S(1)}, u32[]{:S(2)}, u32[]{:S(2)}) collective-permute-start(bf16[48,1024]{1,0:T(8,128)(2,1)S(1)} %get-tuple-element.52), channel_id=1, source_target_pairs={{0,2},{2,0},{1,3},{3,1},{4,6},{6,4},{5,7},{7,5},{8,10},{10,8},{9,1... | collective-permute-start | bytes 294920 | tf_op jit(solution)/shard_map/ppermute | solution.py:628
  55.1 0.6 collective-permute-start.16
  55.7 0.9 %collective-permute-start.17 = (bf16[48,1024]{1,0:T(8,128)(2,1)S(1)}, bf16[48,1024]{1,0:T(8,128)(2,1)S(1)}, u32[]{:S(2)}, u32[]{:S(2)}) collective-permute-start(bf16[48,1024]{1,0:T(8,128)(2,1)S(1)} %get-tuple-element.54), channel_id=1, source_target_pairs={{0,18},{2,16},{16,2},{18,0},{1,19},{3,17},{17,3},{19,1},{4,22},{6,... | collective-permute-start | bytes 294920 | tf_op jit(solution)/shard_map/ppermute | solution.py:626
  56.7 1.7 %collective-permute-done.15.side_ref = bf16[48,1024]{1,0:T(8,128)(2,1)S(1)} collective-permute-done((bf16[48,1024]{1,0:T(8,128)(2,1)S(1)}, bf16[48,1024]{1,0:T(8,128)(2,1)S(1)}, u32[]{:S(2)}, u32[]{:S(2)}) %collective-permute-start.15) | collective-permute-done | bytes 98336 | tf_op jit(solution)/shard_map/ppermute | solution.py:628
  58.3 3.6 %collective-permute-done.16.far_ref = bf16[48,1024]{1,0:T(8,128)(2,1)S(1)} collective-permute-done((bf16[48,1024]{1,0:T(8,128)(2,1)S(1)}, bf16[48,1024]{1,0:T(8,128)(2,1)S(1)}, u32[]{:S(2)}, u32[]{:S(2)}) %collective-permute-start.16) | collective-permute-done | bytes 98336 | tf_op jit(solution)/shard_map/ppermute | solution.py:627
  61.9 0.2 merge.1
  62.0 1.4 %collective-permute-start.18 = (bf16[32,1024]{1,0:T(8,128)(2,1)S(1)}, bf16[32,1024]{1,0:T(8,128)(2,1)S(1)}, u32[]{:S(2)}, u32[]{:S(2)}) collective-permute-start(bf16[32,1024]{1,0:T(8,128)(2,1)S(1)} %get-tuple-element.56), channel_id=1, source_target_pairs={{0,4},{4,0},{8,12},{12,8},{1,5},{5,1},{9,13},{13,9},{2,6},{6,2},{1... | collective-permute-start | bytes 196616 | tf_op jit(solution)/shard_map/ppermute | solution.py:636
  63.4 0.8 %collective-permute-start.19 = (bf16[32,1024]{1,0:T(8,128)(2,1)S(1)}, bf16[32,1024]{1,0:T(8,128)(2,1)S(1)}, u32[]{:S(2)}, u32[]{:S(2)}) collective-permute-start(bf16[32,1024]{1,0:T(8,128)(2,1)S(1)} %get-tuple-element.57), channel_id=1, source_target_pairs={{0,8},{4,12},{8,0},{12,4},{1,9},{5,13},{9,1},{13,5},{2,10},{6,14},... | collective-permute-start | bytes 196616 | tf_op jit(solution)/shard_map/ppermute | solution.py:636
  64.2 2.3 %collective-permute-start.20 = (bf16[32,1024]{1,0:T(8,128)(2,1)S(1)}, bf16[32,1024]{1,0:T(8,128)(2,1)S(1)}, u32[]{:S(2)}, u32[]{:S(2)}) collective-permute-start(bf16[32,1024]{1,0:T(8,128)(2,1)S(1)} %get-tuple-element.58), channel_id=1, source_target_pairs={{0,12},{4,8},{8,4},{12,0},{1,13},{5,9},{9,5},{13,1},{2,14},{6,10},... | collective-permute-start | bytes 196616 | tf_op jit(solution)/shard_map/ppermute | solution.py:636
  66.5 1.1 %collective-permute-done.18.one_ref = bf16[32,1024]{1,0:T(8,128)(2,1)S(1)} collective-permute-done((bf16[32,1024]{1,0:T(8,128)(2,1)S(1)}, bf16[32,1024]{1,0:T(8,128)(2,1)S(1)}, u32[]{:S(2)}, u32[]{:S(2)}) %collective-permute-start.18) | collective-permute-done | bytes 65568 | tf_op jit(solution)/shard_map/ppermute | solution.py:636
  67.6 1.7 %collective-permute-done.19.two_ref = bf16[32,1024]{1,0:T(8,128)(2,1)S(1)} collective-permute-done((bf16[32,1024]{1,0:T(8,128)(2,1)S(1)}, bf16[32,1024]{1,0:T(8,128)(2,1)S(1)}, u32[]{:S(2)}, u32[]{:S(2)}) %collective-permute-start.19) | collective-permute-done | bytes 65568 | tf_op jit(solution)/shard_map/ppermute | solution.py:636
  69.3 1.1 %collective-permute-done.20.three_ref = bf16[32,1024]{1,0:T(8,128)(2,1)S(1)} collective-permute-done((bf16[32,1024]{1,0:T(8,128)(2,1)S(1)}, bf16[32,1024]{1,0:T(8,128)(2,1)S(1)}, u32[]{:S(2)}, u32[]{:S(2)}) %collective-permute-start.20) | collective-permute-done | bytes 65568 | tf_op jit(solution)/shard_map/ppermute | solution.py:636
  70.4 1.0 %scatter.1 = bf16[128,1024]{1,0:T(8,128)(2,1)} custom-call(bf16[32,128]{1,0:T(8,128)(2,1)S(1)} %get-tuple-element.32.pick_ref, f32[32,1024]{1,0:T(8,128)S(1)} %add.1.sum_ref, bf16[32,1024]{1,0:T(8,128)(2,1)S(1)} %collective-permute-done.20.three_ref), custom_call_target="tpu_custom_call" | custom-call | tf_op jit(solution)/shard_map/scatter/pallas_call | solution.py:638
  (16 shorter events, 0.1 us)
Async XLA Ops:
  1.1 8.3 %collective-permute-start.1 = (bf16[32,1024]{1,0:T(8,128)(2,1)S(1)}, bf16[32,1024]{1,0:T(8,128)(2,1)S(1)}, u32[]{:S(2)}, u32[]{:S(2)}) collective-permute-start(bf16[32,1024]{1,0:T(8,128)(2,1)S(1)} %get-tuple-element.35), channel_id=1, source_target_pairs={{0,2},{1,6},{2,10},{3,14},{4,3},{5,7},{6,11},{7,15},{8,0},{9,4},{1... | collective-permute-start | bytes 196616 | tf_op jit(solution)/shard_map/ppermute | solution.py:514
  4.1 5.3 %collective-permute-start = (bf16[32,1024]{1,0:T(8,128)(2,1)S(1)}, bf16[32,1024]{1,0:T(8,128)(2,1)S(1)}, u32[]{:S(2)}, u32[]{:S(2)}) collective-permute-start(bf16[32,1024]{1,0:T(8,128)(2,1)S(1)} %get-tuple-element.35), channel_id=1, source_target_pairs={{0,0},{1,4},{2,8},{3,12},{4,1},{5,5},{6,9},{7,13},{8,2},{9,6},{10,... | collective-permute-start | bytes 196616 | tf_op jit(solution)/shard_map/ppermute | solution.py:515
  9.5 2.4 %collective-permute-start.2 = (bf16[64,1024]{1,0:T(8,128)(2,1)S(1)}, bf16[64,1024]{1,0:T(8,128)(2,1)S(1)}, u32[]{:S(2)}, u32[]{:S(2)}) collective-permute-start(bf16[64,1024]{1,0:T(8,128)(2,1)S(1)} %join.1.joined_ref), channel_id=1, source_target_pairs={{0,1},{1,0},{2,3},{3,2},{4,5},{5,4},{6,7},{7,6},{8,9},{9,8},{10,11... | collective-permute-start | bytes 393224 | tf_op jit(solution)/shard_map/ppermute | solution.py:532
  12.4 9.9 %collective-permute-start.5 = (bf16[32,1024]{1,0:T(8,128)(2,1)S(1)}, bf16[32,1024]{1,0:T(8,128)(2,1)S(1)}, u32[]{:S(2)}, u32[]{:S(2)}) collective-permute-start(bf16[32,1024]{1,0:T(8,128)(2,1)S(1)} %get-tuple-element.59), channel_id=1, source_target_pairs={{0,4},{4,0},{8,12},{12,8},{1,5},{5,1},{9,13},{13,9},{2,6},{6,2},{1... | collective-permute-start | bytes 196616 | tf_op jit(solution)/shard_map/ppermute | solution.py:541
  13.5 9.1 %collective-permute-start.4 = (bf16[32,1024]{1,0:T(8,128)(2,1)S(1)}, bf16[32,1024]{1,0:T(8,128)(2,1)S(1)}, u32[]{:S(2)}, u32[]{:S(2)}) collective-permute-start(bf16[32,1024]{1,0:T(8,128)(2,1)S(1)} %get-tuple-element.60), channel_id=1, source_target_pairs={{0,8},{4,12},{8,0},{12,4},{1,9},{5,13},{9,1},{13,5},{2,10},{6,14},... | collective-permute-start | bytes 196616 | tf_op jit(solution)/shard_map/ppermute | solution.py:541
  17.9 6.2 %collective-permute-start.3 = (bf16[32,1024]{1,0:T(8,128)(2,1)S(1)}, bf16[32,1024]{1,0:T(8,128)(2,1)S(1)}, u32[]{:S(2)}, u32[]{:S(2)}) collective-permute-start(bf16[32,1024]{1,0:T(8,128)(2,1)S(1)} %get-tuple-element.61), channel_id=1, source_target_pairs={{0,12},{4,8},{8,4},{12,0},{1,13},{5,9},{9,5},{13,1},{2,14},{6,10},... | collective-permute-start | bytes 196616 | tf_op jit(solution)/shard_map/ppermute | solution.py:541
  17.9 6.2 %copy-start = (bf16[1024,4]{0,1:T(4,128)(2,1)S(1)}, bf16[1024,4]{0,1:T(4,128)(2,1)}, u32[]{:S(2)}) copy-start(bf16[1024,4]{0,1:T(4,128)(2,1)} %param.14) | copy-start | bytes 24580
  17.9 6.2 %copy-start.1 = (bf16[2,1024]{1,0:T(2,128)(2,1)S(1)}, bf16[2,1024]{1,0:T(2,128)(2,1)}, u32[]{:S(2)}) copy-start(bf16[2,1024]{1,0:T(2,128)(2,1)} %gain_ref.1) | copy-start | bytes 12292
  24.3 8.6 %collective-permute-start.8 = (bf16[32,1152]{1,0:T(8,128)(2,1)S(1)}, bf16[32,1152]{1,0:T(8,128)(2,1)S(1)}, u32[]{:S(2)}, u32[]{:S(2)}) collective-permute-start(bf16[32,1152]{1,0:T(8,128)(2,1)S(1)} %norm.1.after_ref.zero_ref), channel_id=1, source_target_pairs={{0,4},{4,0},{8,12},{12,8},{1,5},{5,1},{9,13},{13,9},{2,6},{6,2},{1... | collective-permute-start | bytes 221192 | tf_op jit(solution)/shard_map/ppermute | solution.py:556
  25.2 7.7 %collective-permute-start.7 = (bf16[32,1152]{1,0:T(8,128)(2,1)S(1)}, bf16[32,1152]{1,0:T(8,128)(2,1)S(1)}, u32[]{:S(2)}, u32[]{:S(2)}) collective-permute-start(bf16[32,1152]{1,0:T(8,128)(2,1)S(1)} %norm.1.after_ref.zero_ref), channel_id=1, source_target_pairs={{0,8},{4,12},{8,0},{12,4},{1,9},{5,13},{9,1},{13,5},{2,10},{6,14},... | collective-permute-start | bytes 221192 | tf_op jit(solution)/shard_map/ppermute | solution.py:556
  27.1 6.3 %collective-permute-start.6 = (bf16[32,1152]{1,0:T(8,128)(2,1)S(1)}, bf16[32,1152]{1,0:T(8,128)(2,1)S(1)}, u32[]{:S(2)}, u32[]{:S(2)}) collective-permute-start(bf16[32,1152]{1,0:T(8,128)(2,1)S(1)} %norm.1.after_ref.zero_ref), channel_id=1, source_target_pairs={{0,12},{4,8},{8,4},{12,0},{1,13},{5,9},{9,5},{13,1},{2,14},{6,10},... | collective-permute-start | bytes 221192 | tf_op jit(solution)/shard_map/ppermute | solution.py:556
  33.5 8.0 %collective-permute-start.9 = (bf16[48,1152]{1,0:T(8,128)(2,1)S(1)}, bf16[48,1152]{1,0:T(8,128)(2,1)S(1)}, u32[]{:S(2)}, u32[]{:S(2)}) collective-permute-start(bf16[48,1152]{1,0:T(8,128)(2,1)S(1)} %get-tuple-element.40), channel_id=1, source_target_pairs={{0,18},{2,16},{16,2},{18,0},{1,19},{3,17},{17,3},{19,1},{4,22},{6,... | collective-permute-start | bytes 331784 | tf_op jit(solution)/shard_map/ppermute | solution.py:572
  37.6 4.7 %collective-permute-start.10 = (bf16[48,1152]{1,0:T(8,128)(2,1)S(1)}, bf16[48,1152]{1,0:T(8,128)(2,1)S(1)}, u32[]{:S(2)}, u32[]{:S(2)}) collective-permute-start(bf16[48,1152]{1,0:T(8,128)(2,1)S(1)} %get-tuple-element.41), channel_id=1, source_target_pairs={{0,2},{2,0},{1,3},{3,1},{4,6},{6,4},{5,7},{7,5},{8,10},{10,8},{9,1... | collective-permute-start | bytes 331784 | tf_op jit(solution)/shard_map/ppermute | solution.py:574
  37.6 4.7 %collective-permute-start.11 = (bf16[48,1152]{1,0:T(8,128)(2,1)S(1)}, bf16[48,1152]{1,0:T(8,128)(2,1)S(1)}, u32[]{:S(2)}, u32[]{:S(2)}) collective-permute-start(bf16[48,1152]{1,0:T(8,128)(2,1)S(1)} %get-tuple-element.42), channel_id=1, source_target_pairs={{0,16},{16,0},{1,17},{17,1},{2,18},{18,2},{3,19},{19,3},{4,20},{20... | collective-permute-start | bytes 331784 | tf_op jit(solution)/shard_map/ppermute | solution.py:573
  45.5 4.5 %collective-permute-start.12 = (bf16[2768,128]{1,0:T(8,128)(2,1)S(1)}, bf16[2768,128]{1,0:T(8,128)(2,1)S(1)}, u32[]{:S(2)}, u32[]{:S(2)}) collective-permute-start(bf16[2768,128]{1,0:T(8,128)(2,1)S(1)} %get-tuple-element.45.gate_ref), channel_id=1, source_target_pairs={{0,1},{1,0},{2,3},{3,2},{4,5},{5,4},{6,7},{7,6},{8,9},{9,8},{10,11... | collective-permute-start | bytes 2125832 | tf_op jit(solution)/shard_map/ppermute | solution.py:603
  47.9 2.1 %collective-permute-start.13 = (bf16[2064,128]{1,0:T(8,128)(2,1)S(1)}, bf16[2064,128]{1,0:T(8,128)(2,1)S(1)}, u32[]{:S(2)}, u32[]{:S(2)}) collective-permute-start(bf16[2064,128]{1,0:T(8,128)(2,1)S(1)} %up.2.up_ref), channel_id=1, source_target_pairs={{0,1},{1,0},{2,3},{3,2},{4,5},{5,4},{6,7},{7,6},{8,9},{9,8},{10,11... | collective-permute-start | bytes 1585160 | tf_op jit(solution)/shard_map/ppermute | solution.py:604
  49.4 1.5 %collective-permute-start.14 = (bf16[688,128]{1,0:T(8,128)(2,1)S(1)}, bf16[688,128]{1,0:T(8,128)(2,1)S(1)}, u32[]{:S(2)}, u32[]{:S(2)}) collective-permute-start(bf16[688,128]{1,0:T(8,128)(2,1)S(1)} %up.3.up_ref), channel_id=1, source_target_pairs={{0,1},{1,0},{2,3},{3,2},{4,5},{5,4},{6,7},{7,6},{8,9},{9,8},{10,11... | collective-permute-start | bytes 528392 | tf_op jit(solution)/shard_map/ppermute | solution.py:604
  53.0 5.3 %collective-permute-start.15 = (bf16[48,1024]{1,0:T(8,128)(2,1)S(1)}, bf16[48,1024]{1,0:T(8,128)(2,1)S(1)}, u32[]{:S(2)}, u32[]{:S(2)}) collective-permute-start(bf16[48,1024]{1,0:T(8,128)(2,1)S(1)} %get-tuple-element.52), channel_id=1, source_target_pairs={{0,2},{2,0},{1,3},{3,1},{4,6},{6,4},{5,7},{7,5},{8,10},{10,8},{9,1... | collective-permute-start | bytes 294920 | tf_op jit(solution)/shard_map/ppermute | solution.py:628
  55.1 6.8 %collective-permute-start.16 = (bf16[48,1024]{1,0:T(8,128)(2,1)S(1)}, bf16[48,1024]{1,0:T(8,128)(2,1)S(1)}, u32[]{:S(2)}, u32[]{:S(2)}) collective-permute-start(bf16[48,1024]{1,0:T(8,128)(2,1)S(1)} %get-tuple-element.53), channel_id=1, source_target_pairs={{0,16},{16,0},{1,17},{17,1},{2,18},{18,2},{3,19},{19,3},{4,20},{20... | collective-permute-start | bytes 294920 | tf_op jit(solution)/shard_map/ppermute | solution.py:627
  55.7 6.2 %collective-permute-start.17 = (bf16[48,1024]{1,0:T(8,128)(2,1)S(1)}, bf16[48,1024]{1,0:T(8,128)(2,1)S(1)}, u32[]{:S(2)}, u32[]{:S(2)}) collective-permute-start(bf16[48,1024]{1,0:T(8,128)(2,1)S(1)} %get-tuple-element.54), channel_id=1, source_target_pairs={{0,18},{2,16},{16,2},{18,0},{1,19},{3,17},{17,3},{19,1},{4,22},{6,... | collective-permute-start | bytes 294920 | tf_op jit(solution)/shard_map/ppermute | solution.py:626
  62.0 5.5 %collective-permute-start.18 = (bf16[32,1024]{1,0:T(8,128)(2,1)S(1)}, bf16[32,1024]{1,0:T(8,128)(2,1)S(1)}, u32[]{:S(2)}, u32[]{:S(2)}) collective-permute-start(bf16[32,1024]{1,0:T(8,128)(2,1)S(1)} %get-tuple-element.56), channel_id=1, source_target_pairs={{0,4},{4,0},{8,12},{12,8},{1,5},{5,1},{9,13},{13,9},{2,6},{6,2},{1... | collective-permute-start | bytes 196616 | tf_op jit(solution)/shard_map/ppermute | solution.py:636
  63.4 5.9 %collective-permute-start.19 = (bf16[32,1024]{1,0:T(8,128)(2,1)S(1)}, bf16[32,1024]{1,0:T(8,128)(2,1)S(1)}, u32[]{:S(2)}, u32[]{:S(2)}) collective-permute-start(bf16[32,1024]{1,0:T(8,128)(2,1)S(1)} %get-tuple-element.57), channel_id=1, source_target_pairs={{0,8},{4,12},{8,0},{12,4},{1,9},{5,13},{9,1},{13,5},{2,10},{6,14},... | collective-permute-start | bytes 196616 | tf_op jit(solution)/shard_map/ppermute | solution.py:636
  64.2 6.2 %collective-permute-start.20 = (bf16[32,1024]{1,0:T(8,128)(2,1)S(1)}, bf16[32,1024]{1,0:T(8,128)(2,1)S(1)}, u32[]{:S(2)}, u32[]{:S(2)}) collective-permute-start(bf16[32,1024]{1,0:T(8,128)(2,1)S(1)} %get-tuple-element.58), channel_id=1, source_target_pairs={{0,12},{4,8},{8,4},{12,0},{1,13},{5,9},{9,5},{13,1},{2,14},{6,10},... | collective-permute-start | bytes 196616 | tf_op jit(solution)/shard_map/ppermute | solution.py:636
